TPU v7x, 32 devices: a whole 2x2x4 slice. The times are simulated.
32 devices in a mesh: dp: 8 (over z, y), tensor: 4 (over x, core).
Axes of the slice: x: 2, y: 2, z: 4, core: 2. Of those that a mesh axis runs over, the one named last changes fastest.
Arguments:
- states: bfloat16 [32, 1024, 512], P(None, 'dp', 'tensor'), may hold values from -6 to 6
- timesteps: int32 [32], replicated, may hold values from 0 to 999
- lengths: int32 [32], replicated, may hold values from 1 to 1024, 20480 in all
- deal_order: int32 [32], replicated, may hold values from 0 to 31, each once
- w_qkv: bfloat16 [512, 3, 512], P('dp', None, 'tensor'), may hold values from -0.25 to 0.25
- w_out: bfloat16 [512, 512], P('tensor', 'dp'), may hold values from -2 to 2
- w_up: bfloat16 [512, 2048], P('dp', 'tensor'), may hold values from -0.25 to 0.25
- w_down: bfloat16 [2048, 512], P('tensor', 'dp'), may hold values from -0.125 to 0.125
- gain_attn: float32 [512], P(('dp', 'tensor')), may hold values from 0.25 to 1.75
- gain_ffn: float32 [512], P(('dp', 'tensor')), may hold values from 0.25 to 1.75
- out_grad: bfloat16 [32, 1024, 512], P(('dp', 'tensor')), may hold values from -6 to 6
Outputs:
- output: bfloat16 [32, 1024, 512], P(('dp', 'tensor'))
- states_grad: bfloat16 [32, 1024, 512], P(None, 'dp', 'tensor')
- w_qkv_grad: float32 [512, 3, 512], P('dp', None, 'tensor')
- w_out_grad: float32 [512, 512], P('tensor', 'dp')
- w_up_grad: float32 [512, 2048], P('dp', 'tensor')
- w_down_grad: float32 [2048, 512], P('tensor', 'dp')
- gain_attn_grad: float32 [512], P(('dp', 'tensor'))
- gain_ffn_grad: float32 [512], P(('dp', 'tensor'))
Inputs may be any that keep to these rules, and one draw needn't show every extreme that they name: `deal_order`: every sequence number appears in exactly one slot.
All inputs are finite; a program needn't handle non-finite values.
Results may differ from a plain program's by a relative error of at most 0.017.
Values may be sent and summed in bfloat16 or wider, within the bound.
No kernel may reach another device: no remote copies, remote signals or barrier semaphores. Data moves between devices by JAX's collectives and lax.ppermute only.
A program may use at most 128 MiB of HBM per device.

v0:
```python
import functools
import math

import jax
import jax.numpy as jnp
from jax import lax
from jax.experimental import pallas as pl
from jax.experimental.pallas import tpu as pltpu
from jax.sharding import PartitionSpec as P

HEAD_DIM = 64
PAIR = 2 * HEAD_DIM
ROWS = 256
KEYS = 256
BACK_KEYS = 512
SPARE = 8
SCORE_SCALE = 1.0 / math.sqrt(HEAD_DIM)
LOG2E = math.log2(math.e)
F32 = jnp.float32
BF16 = jnp.bfloat16
NN = (((1,), (0,)), ((), ()))
NT = (((1,), (1,)), ((), ()))
VMEM_LIMIT = 56 * 1024 * 1024


def mul(lhs, rhs, dims=NN):
    return lax.dot_general(lhs, rhs, dims, preferred_element_type=F32)


def join_tokens(ref):
    blocks, parts, tall, width = ref.shape
    tokens = tall - SPARE
    return jnp.concatenate(
        [ref[:, part, 0:tokens].reshape(blocks * tokens, width) for part in range(parts)], axis=-1
    ).astype(F32)


def norm_parts(values):
    center = values - jnp.mean(values, axis=-1, keepdims=True)
    spread = jnp.mean(center * center, axis=-1, keepdims=True)
    inverse = lax.rsqrt(spread + 1e-05)
    return center * inverse, inverse


def norm_back(grad, gain, unit, inverse):
    scaled = grad * gain
    mean_scaled = jnp.mean(scaled, axis=-1, keepdims=True)
    mean_along = jnp.mean(scaled * unit, axis=-1, keepdims=True)
    return inverse * (scaled - mean_scaled - unit * mean_along)


def cost(microseconds):
    return pl.CostEstimate(
        flops=int(microseconds * 1.15e9), bytes_accessed=1 << 20, transcendentals=0
    )


def params(**kwargs):
    return pltpu.CompilerParams(vmem_limit_bytes=VMEM_LIMIT, **kwargs)


def project_kernel(limit_ref, x_ref, clock_ref, gain_ref, *refs):
    w_refs, (mixed_ref, n_turn_ref, wide) = refs[:-3], refs[-3:]
    step = pl.program_id(0)

    @pl.when(step == 0)
    def _():
        for part, w_ref in enumerate(w_refs):
            width = w_ref.shape[1]
            columns = slice(part * width, (part + 1) * width)
            wide[:, columns] = w_ref[...]

    @pl.when(step * ROWS < limit_ref[0])
    def _():
        begin = join_tokens(x_ref) + clock_ref[...]
        unit, _ = norm_parts(begin)
        normed = (unit * gain_ref[...]).astype(BF16)
        n_turn_ref[...] = normed.T
        mixed_ref[...] = mul(normed, wide[...]).astype(BF16)

    @pl.when(step * ROWS >= limit_ref[0])
    def _():
        n_turn_ref[...] = jnp.zeros_like(n_turn_ref)
        mixed_ref[...] = jnp.zeros_like(mixed_ref)


def project(limit, x_blocks, clock, gain, w_parts):
    senders, feature_parts, tall, width = x_blocks.shape
    tokens = tall - SPARE
    length = senders * tokens
    features = feature_parts * width
    parts, columns = len(w_parts), w_parts[0].shape[1]
    take = ROWS // tokens
    return pl.pallas_call(
        project_kernel,
        grid_spec=pltpu.PrefetchScalarGridSpec(
            num_scalar_prefetch=1,
            grid=(length // ROWS,),
            in_specs=[
                pl.BlockSpec((take, feature_parts, tall, width), lambda i, *s: (i, 0, 0, 0)),
                pl.BlockSpec((1, features), lambda i, *s: (0, 0)),
                pl.BlockSpec((1, features), lambda i, *s: (0, 0)),
            ]
            + [pl.BlockSpec((features, columns), lambda i, *s: (0, 0))] * parts,
            out_specs=[
                pl.BlockSpec((ROWS, parts * columns), lambda i, *s: (i, 0)),
                pl.BlockSpec((features, ROWS), lambda i, *s: (0, i)),
                pl.BlockSpec((features, parts * columns), lambda i, *s: (0, 0)),
            ],
        ),
        out_shape=[
            jax.ShapeDtypeStruct((length, parts * columns), BF16),
            jax.ShapeDtypeStruct((features, length), BF16),
            jax.ShapeDtypeStruct((features, parts * columns), BF16),
        ],
        compiler_params=params(),
        cost_estimate=cost(5),
        name="project",
    )(limit, x_blocks, clock, gain, *w_parts)


def head_lanes(shape, head):
    lane = lax.broadcasted_iota(jnp.int32, shape, 1)
    return (lane >= head * HEAD_DIM) & (lane < (head + 1) * HEAD_DIM)


def spare_lane(shape, head):
    lane = lax.broadcasted_iota(jnp.int32, shape, 1)
    return lane == (1 - head) * HEAD_DIM


def masked_keys(keys, head, limit):
    row = lax.broadcasted_iota(jnp.int32, keys.shape, 0)
    spare = jnp.where(
        spare_lane(keys.shape, head) & (row >= limit), jnp.asarray(-1e30, F32), jnp.asarray(0.0, F32)
    )
    return jnp.where(head_lanes(keys.shape, head), keys.astype(F32), spare).astype(BF16)


def own_lanes(values, head):
    return jnp.where(head_lanes(values.shape, head), values.astype(F32), 0.0).astype(BF16)


def masked_queries(queries, head):
    spare = jnp.where(spare_lane(queries.shape, head), jnp.asarray(1.0, F32), jnp.asarray(0.0, F32))
    return jnp.where(head_lanes(queries.shape, head), queries.astype(F32), spare).astype(BF16)


def attend_kernel(limit_ref, q_ref, k_ref, v_ref, ctx_ref, turn_ref, lse_ref, keys_s, q_s, vt_s, sc_s):
    length = q_ref.shape[0]
    vt_s[...] = v_ref[...].astype(F32).T.astype(BF16)
    for head in range(2):
        keys_s[head] = masked_keys(k_ref[...], head, limit_ref[0])
        q_s[head] = masked_queries(q_ref[...], head)
    factor = SCORE_SCALE * LOG2E
    spans = [slice(at, at + KEYS) for at in range(0, length, KEYS)]
    outs = []
    for head in range(2):
        feats = slice(head * HEAD_DIM, (head + 1) * HEAD_DIM)
        peak = None
        for span in spans:
            scores = mul(keys_s[head, span], q_s[head], NT)
            sc_s[head, span] = scores
            high = jnp.max(scores, axis=0, keepdims=True)
            peak = high if peak is None else jnp.maximum(peak, high)
        peak = peak * factor
        total = jnp.zeros_like(peak)
        gathered = jnp.zeros((HEAD_DIM, length), F32)
        for span in spans:
            expo = jnp.exp2(sc_s[head, span] * factor - peak)
            total += jnp.sum(expo, axis=0, keepdims=True)
            gathered += mul(vt_s[feats, span], expo.astype(BF16))
        outs.append(gathered / total)
        lse_ref[0, head : head + 1, :] = peak + jnp.log2(total)
    both = jnp.concatenate(outs, axis=0)
    turn_ref[...] = both.astype(BF16)
    ctx_ref[...] = both.T.astype(BF16)


def attend(limit, mixed, pairs):
    length = mixed.shape[0]
    column = lambda c: pl.BlockSpec((length, PAIR), lambda i, s: (0, i * 3 + c))
    return pl.pallas_call(
        attend_kernel,
        grid_spec=pltpu.PrefetchScalarGridSpec(
            num_scalar_prefetch=1,
            grid=(pairs,),
            in_specs=[column(0), column(1), column(2)],
            out_specs=[
                pl.BlockSpec((length, PAIR), lambda i, s: (0, i)),
                pl.BlockSpec((PAIR, length), lambda i, s: (i, 0)),
                pl.BlockSpec((1, 2, length), lambda i, s: (i, 0, 0)),
            ],
            scratch_shapes=[
                pltpu.VMEM((2, length, PAIR), BF16),
                pltpu.VMEM((2, length, PAIR), BF16),
                pltpu.VMEM((PAIR, length), BF16),
                pltpu.VMEM((2, length, length), F32),
            ],
        ),
        out_shape=[
            jax.ShapeDtypeStruct((length, pairs * PAIR), BF16),
            jax.ShapeDtypeStruct((pairs * PAIR, length), BF16),
            jax.ShapeDtypeStruct((pairs, 2, length), F32),
        ],
        compiler_params=params(),
        cost_estimate=cost(15),
        name="attend",
    )(limit, mixed, mixed, mixed)


def gelu_both(values):
    root = math.sqrt(2.0 / math.pi)
    square = values * values
    tanh = jnp.tanh(root * values * (1.0 + 0.044715 * square))
    half = 0.5 + 0.5 * tanh
    slope = half + (0.5 * root) * values * (1.0 - tanh * tanh) * (1.0 + (3 * 0.044715) * square)
    return values * half, slope


def middle_kernel(
    groups, limit_ref, place_ref, x_ref, clock_ref, gain_ref, ctx_ref, og_ref, *refs
):
    weight_refs, refs = refs[:-14], refs[-14:]
    out_ref, cg_ref, mg_ref, gg_ref, send_ref, keep_ref = refs[:6]
    wide, units, active_s, ug_s, n_turn, fg_turn, ag_turn, ctx_s = refs[6:]
    step = pl.program_id(0)
    parts, _, hidden = active_s.shape
    blocks = pl.num_programs(0) - parts

    @pl.when(step == 0)
    def _():
        gg_ref[...] = jnp.zeros_like(gg_ref)
        each = len(weight_refs) // parts
        for part in range(parts):
            thin = slice(part * PAIR, (part + 1) * PAIR)
            thick = slice(part * 2 * hidden, (part + 1) * 2 * hidden)
            for at, w_ref in enumerate(weight_refs[part * each : (part + 1) * each]):
                if groups is None:
                    wide[:, thin] = w_ref[:, 0:PAIR]
                    units[:, thick] = w_ref[:, PAIR:]
                    continue
                count = groups // each
                rows = w_ref.shape[0] // count
                for group in range(count):
                    spot = place_ref[at * count + group] * rows
                    spot = pl.ds(pl.multiple_of(spot, rows), rows)
                    source = w_ref[group * rows : (group + 1) * rows]
                    wide[spot, thin] = source[:, 0:PAIR]
                    units[spot, thick] = source[:, PAIR:]

    dead = (step < blocks) & (step * ROWS >= limit_ref[0])

    @pl.when((step < blocks) & jnp.logical_not(dead))
    def _():
        spot = pl.ds(pl.multiple_of(step * ROWS, ROWS), ROWS)
        gain = gain_ref[...]
        live = step * ROWS + lax.broadcasted_iota(jnp.int32, (ROWS, 1), 0) < limit_ref[0]
        begin = join_tokens(x_ref) + clock_ref[...]
        middle = begin + mul(ctx_ref[...], wide[...], NT)
        unit, inverse = norm_parts(middle)
        normed = (unit * gain).astype(BF16)
        n_turn[:, spot] = normed.T
        res_grad = jnp.where(live, og_ref[0].astype(F32), 0.0)
        feed_grad = res_grad.astype(BF16)
        fg_turn[:, spot] = feed_grad.T
        feed = jnp.zeros_like(middle)
        two_grad = jnp.zeros_like(middle)
        for part in range(parts):
            up = slice(2 * part * hidden, (2 * part + 1) * hidden)
            down = slice((2 * part + 1) * hidden, (2 * part + 2) * hidden)
            upper = mul(normed, units[:, up])
            active, slope = gelu_both(upper)
            active = active.astype(BF16)
            active_s[part, spot] = active
            feed += mul(active, units[:, down], NT)
            upper_grad = (mul(feed_grad, units[:, down]) * slope).astype(BF16)
            ug_s[part, spot] = upper_grad
            two_grad += mul(upper_grad, units[:, up], NT)
        out_ref[0] = jnp.where(live, middle + feed, 0.0).astype(BF16)
        gg_ref[...] += jnp.sum(two_grad * unit, axis=0, keepdims=True)
        middle_grad = res_grad + norm_back(two_grad, gain, unit, inverse)
        mg_ref[...] = middle_grad
        att_grad = middle_grad.astype(BF16)
        ag_turn[:, spot] = att_grad.T
        cg_ref[...] = mul(att_grad, wide[...]).astype(BF16)
        for part in range(parts):
            ctx_s[part, spot] = ctx_ref[:, part * PAIR : (part + 1) * PAIR]

    @pl.when(dead)
    def _():
        spot = pl.ds(pl.multiple_of(step * ROWS, ROWS), ROWS)
        for ref in (out_ref, cg_ref, mg_ref):
            ref[...] = jnp.zeros_like(ref)
        for ref in (active_s, ug_s, ctx_s):
            ref[:, spot] = jnp.zeros((ref.shape[0], ROWS, ref.shape[2]), BF16)
        for ref in (n_turn, fg_turn, ag_turn):
            ref[:, spot] = jnp.zeros((ref.shape[0], ROWS), BF16)

    @pl.when(step >= blocks)
    def _():
        turn = step - blocks
        part = jnp.where(turn < 2, 3 - 2 * turn, 6 - 2 * turn)
        grads = (
            mul(ag_turn[...], ctx_s[part]).astype(BF16),
            mul(n_turn[...], ug_s[part]).astype(BF16),
            mul(fg_turn[...], active_s[part]).astype(BF16),
        )

        def into(ref):
            ref[0, :, 0:PAIR], ref[0, :, PAIR : PAIR + hidden], ref[0, :, PAIR + hidden :] = grads

        pl.when(turn < 2)(lambda: into(send_ref))
        pl.when(turn >= 2)(lambda: into(keep_ref))


def middle_block(limit, place, groups, x_blocks, clock, gain, ctx, w_parts, out_grad):
    senders, feature_parts, tall, width = x_blocks.shape
    tokens = tall - SPARE
    length = senders * tokens
    features = feature_parts * width
    parts = len(w_parts)
    weights = [w for part in w_parts for w in part]
    columns = weights[0].shape[1]
    hidden = (columns - PAIR) // 2
    take = ROWS // tokens
    blocks = length // ROWS
    row = lambda i: jnp.minimum(i, blocks - 1)
    whole = lambda array: pl.BlockSpec(
        array.shape, lambda i, *s: (0,) * array.ndim, pipeline_mode=pl.Buffered(1)
    )
    rows = lambda n: pl.BlockSpec((ROWS, n), lambda i, *s: (row(i), 0))
    one = pl.BlockSpec((1, ROWS, features), lambda i, *s: (0, row(i), 0))
    grads = lambda first: pl.BlockSpec(
        (1, features, columns), lambda i, *s: (jnp.clip(i - blocks - first, 0, 1), 0, 0)
    )
    grads_shape = jax.ShapeDtypeStruct((2, features, columns), BF16)
    return pl.pallas_call(
        functools.partial(middle_kernel, groups),
        grid_spec=pltpu.PrefetchScalarGridSpec(
            num_scalar_prefetch=2,
            grid=(blocks + parts,),
            in_specs=[
                pl.BlockSpec(
                    (take, feature_parts, tall, width), lambda i, *s: (row(i), 0, 0, 0)
                ),
                whole(clock),
                whole(gain),
                rows(features),
                one,
            ]
            + [whole(w) for w in weights],
            out_specs=[
                one, rows(features), rows(features),
                pl.BlockSpec((1, features), lambda i, *s: (0, 0)),
                grads(0), grads(2),
            ],
            scratch_shapes=[
                pltpu.VMEM((features, parts * PAIR), BF16),
                pltpu.VMEM((features, parts * 2 * hidden), BF16),
                pltpu.VMEM((parts, length, hidden), BF16),
                pltpu.VMEM((parts, length, hidden), BF16),
                pltpu.VMEM((features, length), BF16),
                pltpu.VMEM((features, length), BF16),
                pltpu.VMEM((features, length), BF16),
                pltpu.VMEM((parts, length, PAIR), BF16),
            ],
        ),
        out_shape=[
            jax.ShapeDtypeStruct((1, length, features), BF16),
            jax.ShapeDtypeStruct((length, features), BF16),
            jax.ShapeDtypeStruct((length, features), F32),
            jax.ShapeDtypeStruct((1, features), F32),
            grads_shape,
            grads_shape,
        ],
        compiler_params=params(),
        cost_estimate=cost(25),
        name="middle",
    )(limit, place, x_blocks, clock, gain, ctx, out_grad, *weights)


def attend_back_kernel(
    limit_ref, q_ref, k_ref, v_ref, turn_ref, lse_ref, cg_ref, n_turn_ref,
    dm_ref, wg_ref, keys_s, q_s, qz_s, do_s, kt_s, delta_s,
):
    limit = limit_ref[0]
    length = q_ref.shape[0]
    kt_s[...] = k_ref[...].astype(F32).T.astype(BF16)
    along = cg_ref[...].astype(F32).T * turn_ref[...].astype(F32)
    for head in range(2):
        feats = slice(head * HEAD_DIM, (head + 1) * HEAD_DIM)
        delta_s[head : head + 1, :] = jnp.sum(along[feats, :], axis=0, keepdims=True)
        keys_s[head] = masked_keys(k_ref[...], head, limit)
        q_s[head] = masked_queries(q_ref[...], head)
        qz_s[head] = own_lanes(q_ref[...], head)
        do_s[head] = own_lanes(cg_ref[...], head)
    factor = SCORE_SCALE * LOG2E
    turned = [jnp.zeros((HEAD_DIM, length), F32)] * 2
    for at in range(0, length, BACK_KEYS):
        span = slice(at, at + BACK_KEYS)
        key_grad = jnp.zeros((BACK_KEYS, PAIR), F32)
        value_grad = jnp.zeros((BACK_KEYS, PAIR), F32)
        for head in range(2):
            feats = slice(head * HEAD_DIM, (head + 1) * HEAD_DIM)
            scores = mul(keys_s[head, span], q_s[head], NT)
            prob = jnp.exp2(scores * factor - lse_ref[0, head : head + 1, :])
            prob_grad = mul(v_ref[span, :], do_s[head], NT)
            score_grad = (prob * (prob_grad - delta_s[head : head + 1, :])).astype(BF16)
            value_grad += mul(prob.astype(BF16), do_s[head])
            key_grad += mul(score_grad, qz_s[head])
            turned[head] += mul(kt_s[feats, span], score_grad)
        dm_ref[span, PAIR : 2 * PAIR] = (key_grad * SCORE_SCALE).astype(BF16)
        dm_ref[span, 2 * PAIR : 3 * PAIR] = value_grad.astype(BF16)
    query_grad = jnp.concatenate(turned, axis=0) * SCORE_SCALE
    dm_ref[:, 0:PAIR] = query_grad.T.astype(BF16)
    wg_ref[0] = mul(n_turn_ref[...], dm_ref[...]).astype(BF16)


def attend_back(limit, mixed, ctx_turn, lse, context_grad, n_turn, first):
    length = mixed.shape[0]
    features = n_turn.shape[0]
    pair = lambda i: first - 2 * i
    column = lambda c: pl.BlockSpec((length, PAIR), lambda i, s: (0, pair(i) * 3 + c))
    return pl.pallas_call(
        attend_back_kernel,
        grid_spec=pltpu.PrefetchScalarGridSpec(
            num_scalar_prefetch=1,
            grid=(2,),
            in_specs=[
                column(0), column(1), column(2),
                pl.BlockSpec((PAIR, length), lambda i, s: (pair(i), 0)),
                pl.BlockSpec((1, 2, length), lambda i, s: (pair(i), 0, 0)),
                pl.BlockSpec((length, PAIR), lambda i, s: (0, pair(i))),
                pl.BlockSpec((features, length), lambda i, s: (0, 0)),
            ],
            out_specs=[
                pl.BlockSpec((length, 3 * PAIR), lambda i, s: (0, i)),
                pl.BlockSpec((1, features, 3 * PAIR), lambda i, s: (i, 0, 0)),
            ],
            scratch_shapes=[
                pltpu.VMEM((2, length, PAIR), BF16),
                pltpu.VMEM((2, length, PAIR), BF16),
                pltpu.VMEM((2, length, PAIR), BF16),
                pltpu.VMEM((2, length, PAIR), BF16),
                pltpu.VMEM((PAIR, length), BF16),
                pltpu.VMEM((8, length), F32),
            ],
        ),
        out_shape=[
            jax.ShapeDtypeStruct((length, 2 * 3 * PAIR), BF16),
            jax.ShapeDtypeStruct((2, features, 3 * PAIR), BF16),
        ],
        compiler_params=params(),
        cost_estimate=cost(16),
        name="attend_back",
    )(limit, mixed, mixed, mixed, ctx_turn, lse, context_grad, n_turn)


def begin_kernel(
    limit_ref, x_ref, clock_ref, gain_ref, gg_two_ref, mg_ref, w_ref, odd_ref, even_ref, bg_ref, gg_s
):
    step = pl.program_id(0)
    _, parts, tall, width = bg_ref.shape
    tokens = tall - SPARE
    blocks = ROWS // tokens
    spot = pl.ds(step * blocks, blocks)

    @pl.when(step == 0)
    def _():
        gg_s[...] = jnp.zeros_like(gg_s)

    @pl.when(step * ROWS < limit_ref[0])
    def _():
        begin = join_tokens(x_ref) + clock_ref[...]
        unit, inverse = norm_parts(begin)
        one_grad = jnp.zeros_like(begin)
        for part, (d_ref, at) in enumerate(((even_ref, 1), (odd_ref, 1), (even_ref, 0), (odd_ref, 0))):
            columns = slice(part * 3 * PAIR, (part + 1) * 3 * PAIR)
            own = slice(at * 3 * PAIR, (at + 1) * 3 * PAIR)
            one_grad += mul(d_ref[:, own], w_ref[:, columns], NT)
        gg_s[...] += jnp.sum(one_grad * unit, axis=0, keepdims=True)
        total = (mg_ref[...] + norm_back(one_grad, gain_ref[...], unit, inverse)).astype(BF16)
        for part in range(parts):
            piece = total[:, part * width : (part + 1) * width]
            bg_ref[spot, part, 0:tokens] = piece.reshape(blocks, tokens, width)

    @pl.when(step * ROWS >= limit_ref[0])
    def _():
        bg_ref[spot] = jnp.zeros((blocks,) + bg_ref.shape[1:], BF16)

    @pl.when(step == pl.num_programs(0) - 1)
    def _():
        rows = []
        for ref in (gg_s, gg_two_ref):
            for part in range(parts):
                rows.append(ref[:, part * width : (part + 1) * width])
        bg_ref[:, :, tokens:tall] = jnp.broadcast_to(
            jnp.concatenate(rows, axis=0).astype(BF16), bg_ref.shape[:2] + (SPARE, width)
        )


def begin_block(limit, x_blocks, clock, gain, two_grad, w_wide, middle_grad, odd, even):
    senders, feature_parts, tall, width = x_blocks.shape
    tokens = tall - SPARE
    length = senders * tokens
    features = feature_parts * width
    take = ROWS // tokens
    whole = lambda array: pl.BlockSpec(array.shape, lambda i, s: (0,) * array.ndim)
    rows = lambda n: pl.BlockSpec((ROWS, n), lambda i, s: (i, 0))
    return pl.pallas_call(
        begin_kernel,
        grid_spec=pltpu.PrefetchScalarGridSpec(
            num_scalar_prefetch=1,
            grid=(length // ROWS,),
            in_specs=[
                pl.BlockSpec((take, feature_parts, tall, width), lambda i, s: (i, 0, 0, 0)),
                whole(clock), whole(gain), whole(two_grad), rows(features), whole(w_wide),
            ]
            + [rows(6 * PAIR)] * 2,
            out_specs=whole(x_blocks),
            scratch_shapes=[pltpu.VMEM((1, features), F32)],
        ),
        out_shape=jax.ShapeDtypeStruct(x_blocks.shape, BF16),
        compiler_params=params(),
        cost_estimate=cost(7),
        name="begin_back",
    )(limit, x_blocks, clock, gain, two_grad, middle_grad, w_wide, odd, even)


DIRECT = 8


def clock_rows(step_ids, features):
    half_width = features // 2
    ladder = jnp.arange(half_width, dtype=F32) / half_width
    rate_rows = jnp.exp(-math.log(10000.0) * ladder)
    angles = step_ids.astype(F32)[:, None] * rate_rows[None, :]
    return jnp.concatenate([jnp.sin(angles), jnp.cos(angles)], axis=-1)


def swap(value, apart):
    count = lax.axis_size("tensor")
    return lax.ppermute(value, "tensor", [(i, i ^ apart) for i in range(count)])


def along_dp(value, move):
    count = lax.axis_size("dp")
    return lax.ppermute(value, "dp", [(i, move(i)) for i in range(count)])


def across(value):
    return along_dp(value, lambda i: i ^ 1)


def ahead(value, step):
    count = lax.axis_size("dp") // 2
    return along_dp(value, lambda i: (i // 2 + step) % count * 2 + i % 2)


def places():
    count = lax.axis_size("dp") // 2
    own = lax.axis_index("dp")
    coarse = (own // 2 - jnp.arange(count, dtype=jnp.int32)) % count
    return jnp.concatenate([coarse * 2 + own % 2, coarse * 2 + 1 - own % 2])


def collect_pieces(shard, gate):
    count = lax.axis_size("dp") // 2
    mine = jnp.concatenate([shard] + [ahead(shard, step) for step in range(1, count)], axis=0)
    other = across(mine)
    far_mine = swap(after(mine, gate), 2)
    far_other = swap(other, 2)
    return (
        (mine, other),
        (swap(mine, 1), swap(other, 1)),
        (far_mine, far_other),
        (swap(far_mine, 1), swap(far_other, 1)),
    )


def collect_rows(shard):
    count = lax.axis_size("dp")
    rows = lax.all_to_all(
        jnp.broadcast_to(shard[None], (count,) + shard.shape), "dp", 0, 0, tiled=True
    )
    return rows.reshape(count * shard.shape[0], shard.shape[1])


def collect_columns(rows):
    far = swap(rows, 2)
    return rows, swap(rows, 1), far, swap(far, 1)


def add(*values):
    total = values[0].astype(F32)
    for value in values[1:]:
        total += value.astype(F32)
    return total.astype(BF16)


def fold_pair(values):
    own = lax.axis_index("dp") % 2
    pick = lambda value, which: lax.dynamic_index_in_dim(value, which, value.ndim - 3, keepdims=False)
    sent = add(*[pick(value, 1 - own) for value in values])
    return sent, lambda: [pick(value, own) for value in values] + [across(sent)]


def fold_far(values):
    sent = add(*[value[0] for value in values])
    return sent, lambda: [value[1] for value in values] + [swap(sent, 2)]


def fold_coarse(values):
    count = lax.axis_size("dp") // 2
    own = lax.axis_index("dp") // 2
    pick = lambda value, which: lax.dynamic_index_in_dim(value, which % count, 0, keepdims=False)
    value = add(*values)
    total = pick(value, own).astype(F32)
    for step in range(1, count):
        total += ahead(pick(value, own + step), step).astype(F32)
    return total


def grouped(value):
    count = lax.axis_size("dp")
    two, rows, columns = value.shape
    return value.reshape(two, count // 2, 2, rows // count, columns)


def exchange_rows(value):
    count = lax.axis_size("dp")
    groups = value.reshape(count, value.shape[0] // count, value.shape[1])
    return jnp.sum(lax.all_to_all(groups, "dp", 0, 0, tiled=True).astype(F32), axis=0)


def three_terms(values):
    terms = []
    for _ in range(3):
        term = lax.reduce_precision(values, 8, 7)
        terms.append(term.astype(BF16))
        values = values - term
    return terms


def after(value, *others):
    return lax.optimization_barrier((value,) + others)[0]


def on_device(
    states, timesteps, lengths, deal_order, w_qkv, w_out, w_up, w_down, gain_attn, gain_ffn, out_grad
):
    both = ("dp", "tensor")
    dp_count = lax.axis_size("dp")
    tensor_count = lax.axis_size("tensor")
    devices = dp_count * tensor_count
    total_seqs, tokens, width = states.shape
    assert tensor_count == 4 and total_seqs == devices
    features = width * tensor_count
    own = lax.axis_index("dp") * tensor_count + lax.axis_index("tensor")
    own_id = lax.dynamic_slice_in_dim(deal_order, own, 1)
    limit = lengths[own_id]
    clock = clock_rows(timesteps[own_id], features)
    per = gain_attn.shape[0]
    rows = w_qkv.shape[0]
    hidden = w_up.shape[1]

    rest = jnp.concatenate([w_out.T, w_up, w_down.T], axis=1)
    qkv_rows = collect_rows(w_qkv.reshape(rows, -1))
    qkv_parts = collect_columns(qkv_rows)

    direct = dp_count <= DIRECT
    rest = after(rest, qkv_rows)
    if direct:
        place, groups = places(), dp_count
        rest_parts = collect_pieces(rest, qkv_parts[2])
    else:
        place, groups = jnp.zeros((1,), jnp.int32), None
        rest_parts = [(part,) for part in collect_columns(collect_rows(rest))]

    spare = jnp.stack(three_terms(gain_attn) + three_terms(gain_ffn)).reshape(1, 6 * per)
    spare = jnp.pad(spare, ((0, SPARE - 1), (0, width - 6 * per)))
    arranged = jnp.concatenate(
        [states[deal_order], jnp.broadcast_to(spare[None], (devices, SPARE, width))], axis=1
    )
    x_blocks = lax.all_to_all(after(arranged, qkv_rows), both, 0, 0, tiled=True)
    gains = jnp.sum(x_blocks[:, tokens, : 6 * per].reshape(devices, 2, 3, per).astype(F32), axis=2)
    gain_one = gains[:, 0].reshape(1, features)
    gain_two = gains[:, 1].reshape(1, features)
    x_blocks = x_blocks.reshape(dp_count, tensor_count, tokens + SPARE, width)

    mixed, n_one_turn, qkv_wide = project(limit, x_blocks, clock, gain_one, qkv_parts)
    ctx, ctx_turn, lse = attend(limit, mixed, tensor_count)
    output, context_grad, middle_grad, two_grad, rest_send, rest_keep = middle_block(
        limit, place, groups, x_blocks, clock, gain_two, ctx, rest_parts, out_grad
    )
    rest_came = swap(rest_send, 1)

    back = functools.partial(attend_back, limit, mixed, ctx_turn, lse)
    context_grad = after(context_grad, rest_send)
    odd, qkv_send = back(context_grad, n_one_turn, 3)
    qkv_came = swap(qkv_send, 1)
    split = PAIR + hidden
    if direct:
        rest_values = [grouped(value) for value in (rest_keep, rest_came)]
        down_sent, down_rest = fold_pair([value[..., split:] for value in rest_values])
        up_sent, up_rest = fold_far([value[..., :split] for value in rest_values])
        even, qkv_keep = back(after(context_grad, odd, down_sent, up_sent), n_one_turn, 2)
        down_value, up_value = add(*down_rest()), add(*up_rest())
        down_sent, down_rest = fold_far([down_value])
        up_sent, up_rest = fold_pair([up_value])
        qkv_keep = after(qkv_keep, down_value, up_value)
        qkv_values = [grouped(value) for value in (qkv_keep, qkv_came)]
        qkv_sent, qkv_rest = fold_pair(qkv_values)
        middle_grad = after(middle_grad, down_sent, up_sent, qkv_sent)
        down_total = fold_coarse(down_rest())
        up_total = fold_coarse(up_rest())
        qkv_sent, qkv_rest = fold_far([add(*qkv_rest())])
        qkv_total = fold_coarse(qkv_rest())
    else:
        even, qkv_keep = back(after(context_grad, odd), n_one_turn, 2)
        rest_sent, rest_rest = fold_far([rest_keep, rest_came])
        rest_total = exchange_rows(add(*rest_rest()))
        up_total, down_total = rest_total[:, :split], rest_total[:, split:]
        qkv_sent, qkv_rest = fold_far([qkv_keep, qkv_came])
        qkv_total = exchange_rows(add(*qkv_rest()))
    begin_grad = begin_block(
        limit, x_blocks, clock, gain_one, two_grad, qkv_wide, middle_grad, odd, even
    )
    returned = lax.all_to_all(
        begin_grad.reshape(devices, tokens + SPARE, width), both, 0, 0, tiled=True
    )
    inverse = (
        jnp.zeros((total_seqs,), jnp.int32)
        .at[deal_order]
        .set(jnp.arange(total_seqs, dtype=jnp.int32))
    )
    states_grad = returned[:, :tokens][inverse]
    gain_grads = jnp.sum(returned[:, tokens:].astype(F32), axis=0).reshape(2, devices, per)
    gain_grads = lax.dynamic_index_in_dim(gain_grads, own, 1, keepdims=False)
    return (
        output,
        states_grad,
        qkv_total.reshape(w_qkv.shape),
        up_total[:, :PAIR].T,
        up_total[:, PAIR:],
        down_total.T,
        gain_grads[0],
        gain_grads[1],
    )


def solution(mesh):
    in_specs = (
        P(None, "dp", "tensor"),
        P(),
        P(),
        P(),
        P("dp", None, "tensor"),
        P("tensor", "dp"),
        P("dp", "tensor"),
        P("tensor", "dp"),
        P(("dp", "tensor")),
        P(("dp", "tensor")),
        P(("dp", "tensor"), None, None),
    )
    out_specs = (
        P(("dp", "tensor"), None, None),
        P(None, "dp", "tensor"),
        P("dp", None, "tensor"),
        P("tensor", "dp"),
        P("dp", "tensor"),
        P("tensor", "dp"),
        P(("dp", "tensor")),
        P(("dp", "tensor")),
    )
    return jax.shard_map(
        on_device, mesh=mesh, in_specs=in_specs, out_specs=out_specs, check_vma=False
    )
```

profile of v0, /device:TPU:0, one launch (start us, length us, event | category | flops | bytes accessed | tf_op | source)
XLA Modules:
  0.0 271.8 jit_solution(18206858540163598275)
XLA Ops:
  0.7 0.9 copy_bitcast_fusion.1
  1.6 0.8 broadcast_in_dim.30
  2.4 7.3 %all-to-all-start = ((bf16[8,64,384]{2,1,0:T(8,128)(2,1)}), bf16[8,64,384]{2,1,0:T(8,128)(2,1)S(1)}, u32[]{:S(2)}, u32[]{:S(2)}) async-start(bf16[8,64,384]{2,1,0:T(8,128)(2,1)} %broadcast_in_dim.30), calls=%async_computation | async-start | bytes 786432 | tf_op jit(solution)/shard_map/all_to_all | solution.py:584
  9.8 0.7 gather_fusion
  10.6 1.1 pad_maximum_fusion
  11.8 9.6 %all-to-all-done = bf16[8,64,384]{2,1,0:T(8,128)(2,1)S(1)} async-done(((bf16[8,64,384]{2,1,0:T(8,128)(2,1)}), bf16[8,64,384]{2,1,0:T(8,128)(2,1)S(1)}, u32[]{:S(2)}, u32[]{:S(2)}) %all-to-all-start) | async-done | bytes 393248 | tf_op jit(solution)/shard_map/all_to_all | solution.py:584
  21.3 3.6 %all-to-all-start.1 = ((bf16[32,136,128]{2,1,0:T(8,128)(2,1)}), bf16[32,136,128]{2,1,0:T(8,128)(2,1)S(1)}, u32[]{:S(2)}, u32[]{:S(2)}) async-start(bf16[32,136,128]{2,1,0:T(8,128)(2,1)} %pad_maximum_fusion), calls=%async_computation.1 | async-start | bytes 2228224 | tf_op jit(solution)/shard_map/all_to_all | solution.py:686
  25.1 3.7 %collective-permute-start.5 = (bf16[64,1152]{1,0:T(8,128)(2,1)S(1)}, bf16[64,1152]{1,0:T(8,128)(2,1)S(1)}, u32[]{:S(2)}, u32[]{:S(2)}) collective-permute-start(bf16[64,1152]{1,0:T(8,128)(2,1)S(1)} %pad_maximum_fusion.1), channel_id=1, source_target_pairs={{0,24},{4,28},{8,0},{12,4},{16,8},{20,12},{24,16},{28,20},{1,25},{... | collective-permute-start | bytes 442376 | tf_op jit(solution)/shard_map/ppermute | solution.py:549
  28.7 1.1 collective-permute-start.3
  29.8 27.4 %collective-permute-done.3 = bf16[64,1152]{1,0:T(8,128)(2,1)S(1)} collective-permute-done((bf16[64,1152]{1,0:T(8,128)(2,1)S(1)}, bf16[64,1152]{1,0:T(8,128)(2,1)S(1)}, u32[]{:S(2)}, u32[]{:S(2)}) %collective-permute-start.3) | collective-permute-done | bytes 147488 | tf_op jit(solution)/shard_map/ppermute | solution.py:549
  57.2 8.1 %collective-permute-done.4 = bf16[64,1152]{1,0:T(8,128)(2,1)S(1)} collective-permute-done((bf16[64,1152]{1,0:T(8,128)(2,1)S(1)}, bf16[64,1152]{1,0:T(8,128)(2,1)S(1)}, u32[]{:S(2)}, u32[]{:S(2)}) %collective-permute-start.4) | collective-permute-done | bytes 147488 | tf_op jit(solution)/shard_map/ppermute | solution.py:549
  65.3 1.5 collective-permute-start.6
  66.9 1.5 collective-permute-start.1
  68.3 0.6 dynamic_slice.79
  70.9 0.6 dynamic-slice.5
  72.2 5.1 %collective-permute-done.1.refs_2_ = bf16[512,384]{1,0:T(8,128)(2,1)} collective-permute-done((bf16[512,384]{1,0:T(8,128)(2,1)S(1)}, bf16[512,384]{1,0:T(8,128)(2,1)}, u32[]{:S(2)}, u32[]{:S(2)}) %collective-permute-start.1) | collective-permute-done | bytes 393248 | tf_op jit(solution)/shard_map/ppermute | solution.py:544
  77.3 1.5 collective-permute-start.9
  78.8 1.5 collective-permute-done.6.refs_1_
  80.4 1.5 collective-permute-start.10
  81.9 0.7 pad_add_fusion.place_ref
  82.5 0.6 dynamic-slice.4.limit_ref
  83.1 0.6 pad_maximum_fusion.2.clock_ref
  84.4 0.7 reshape_squeeze.8.gain_ref
  85.7 8.0 %collective-permute-done.9.refs_4_ = bf16[256,1152]{1,0:T(8,128)(2,1)} collective-permute-done((bf16[256,1152]{1,0:T(8,128)(2,1)S(1)}, bf16[256,1152]{1,0:T(8,128)(2,1)}, u32[]{:S(2)}, u32[]{:S(2)}) %collective-permute-start.9) | collective-permute-done | bytes 589856 | tf_op jit(solution)/shard_map/ppermute | solution.py:544
  93.7 10.0 %collective-permute-done.10.refs_5_ = bf16[256,1152]{1,0:T(8,128)(2,1)} collective-permute-done((bf16[256,1152]{1,0:T(8,128)(2,1)}, bf16[256,1152]{1,0:T(8,128)(2,1)}, u32[]{:S(2)}, u32[]{:S(2)}) %collective-permute-start.10) | collective-permute-done | bytes 589856 | tf_op jit(solution)/shard_map/ppermute | solution.py:544
  103.8 7.6 %project.1 = (bf16[1024,1536]{1,0:T(8,128)(2,1)}, bf16[512,1024]{1,0:T(8,128)(2,1)}, bf16[512,1536]{1,0:T(8,128)(2,1)}) custom-call(s32[1]{0:T(128)} %dynamic-slice.4.limit_ref, bf16[8,4,136,128]{3,2,1,0:T(8,128)(2,1)} %bitcast.130, f32[1,512]{1,0:T(1,128)} %pad_maximum_fusion.2.clock_ref, f32[1,512]{1,0:T(1,128)} %reshape_squeeze.8.gain_ref, ...), custom_call_target="tpu_custom_call" | custom-call | flops 5750000128 | bytes 1048576 | tf_op jit(solution)/shard_map/project/pallas_call | solution.py:94
  111.3 15.3 %attend.1 = (bf16[1024,512]{1,0:T(8,128)(2,1)}, bf16[512,1024]{1,0:T(8,128)(2,1)}, f32[4,2,1024]{2,1,0:T(2,128)}) custom-call(s32[1]{0:T(128)} %dynamic-slice.4.limit_ref, bf16[1024,1536]{1,0:T(8,128)(2,1)} %get-tuple-element.32.q_ref.k_ref.v_ref, bf16[1024,1536]{1,0:T(8,128)(2,1)} %get-tuple-element.32.q_ref.k_ref.v_ref, ...), custom_call_target="tpu_custom_call" | custom-call | flops 17250000896 | bytes 1048576 | tf_op jit(solution)/shard_map/attend/pallas_call | solution.py:183
  126.7 0.7 reshape_squeeze.7.gain_ref
  127.4 30.5 %middle.1 = (bf16[1,1024,512]{2,1,0:T(8,128)(2,1)}, bf16[1024,512]{1,0:T(8,128)(2,1)}, f32[1024,512]{1,0:T(8,128)}, f32[1,512]{1,0:T(1,128)}, bf16[2,512,1152]{2...) custom-call(s32[1]{0:T(128)} %dynamic-slice.4.limit_ref, s32[8]{0:T(128)} %pad_add_fusion.place_ref, ...), custom_call_target="tpu_custom_call" | custom-call | flops 28750000128 | bytes 1048576 | tf_op jit(solution)/shard_map/middle/pallas_call | solution.py:338
  158.4 0.9 scatter_custom_fusion
  159.3 1.3 slice.101
  160.7 16.0 %attend_back.2 = (bf16[1024,768]{1,0:T(8,128)(2,1)}, bf16[2,512,384]{2,1,0:T(8,128)(2,1)}) custom-call(s32[1]{0:T(128)} %dynamic-slice.4.limit_ref, bf16[1024,1536]{1,0:T(8,128)(2,1)} %get-tuple-element.32.q_ref.k_ref.v_ref, bf16[1024,1536]{1,0:T(8,128)(2,1)} %get-tuple-element.32.q_ref.k_ref.v_ref, bf16[1024,1536]{1,0:T(8,128)(2,1)} %get-tuple-element.32.q_ref.k_ref.v_ref, ...), custom_call_target="tpu_custom_call" | custom-call | flops 18400000000 | bytes 1048576 | tf_op jit(solution)/shard_map/attend_back/pallas_call | solution.py:425
  176.9 1.3 slice.102
  178.2 1.4 fusion.36
  179.8 0.6 collective-permute-start.14
  180.7 15.8 %attend_back.3 = (bf16[1024,768]{1,0:T(8,128)(2,1)}, bf16[2,512,384]{2,1,0:T(8,128)(2,1)}) custom-call(s32[1]{0:T(128)} %dynamic-slice.4.limit_ref, bf16[1024,1536]{1,0:T(8,128)(2,1)} %get-tuple-element.32.q_ref.k_ref.v_ref, bf16[1024,1536]{1,0:T(8,128)(2,1)} %get-tuple-element.32.q_ref.k_ref.v_ref, bf16[1024,1536]{1,0:T(8,128)(2,1)} %get-tuple-element.32.q_ref.k_ref.v_ref, ...), custom_call_target="tpu_custom_call" | custom-call | flops 18400000000 | bytes 1048576 | tf_op jit(solution)/shard_map/attend_back/pallas_call | solution.py:425
  196.7 0.7 slice_bitcast_fusion.1
  197.5 2.0 collective-permute-start.26
  199.7 0.8 dynamic-slice_bitcast_fusion
  200.5 1.5 collective-permute-start.22
  202.0 1.0 fusion.7
  202.9 8.0 %begin_back.1 = bf16[8,4,136,128]{3,2,1,0:T(8,128)(2,1)} custom-call(s32[1]{0:T(128)} %dynamic-slice.4.limit_ref, bf16[8,4,136,128]{3,2,1,0:T(8,128)(2,1)} %bitcast.132, f32[1,512]{1,0:T(1,128)} %pad_maximum_fusion.2.clock_ref, f32[1,512]{1,0:T(1,128)} %reshape_squeeze.8.gain_ref, f32[1,512]{1,0:T(1,128)} %get-tuple-element.37.gg_two_ref, ...), custom_call_target="tpu_custom_call" | custom-call | flops 8049999872 | bytes 1048576 | tf_op jit(solution)/shard_map/begin_back/pallas_call | solution.py:511
  210.9 2.7 all-to-all-start.2
  213.6 1.0 fusion.6
  214.7 0.7 copy-done.3
  215.4 1.8 collective-permute-start.27
  217.2 2.1 collective-permute-start.29
  219.3 0.9 collective-permute-start.28
  220.1 1.5 collective-permute-start.17
  221.7 16.4 %collective-permute-done.27 = bf16[64,512]{1,0:T(8,128)(2,1)S(1)} collective-permute-done((bf16[64,512]{1,0:T(8,128)(2,1)S(1)}, bf16[64,512]{1,0:T(8,128)(2,1)S(1)}, u32[]{:S(2)}, u32[]{:S(2)}) %collective-permute-start.27) | collective-permute-done | bytes 65568 | tf_op jit(solution)/shard_map/ppermute | solution.py:549
  238.1 8.8 %collective-permute-done.28 = bf16[64,512]{1,0:T(8,128)(2,1)S(1)} collective-permute-done((bf16[64,512]{1,0:T(8,128)(2,1)S(1)}, bf16[64,512]{1,0:T(8,128)(2,1)S(1)}, u32[]{:S(2)}, u32[]{:S(2)}) %collective-permute-start.28) | collective-permute-done | bytes 65568 | tf_op jit(solution)/shard_map/ppermute | solution.py:549
  246.9 1.5 fusion.13
  248.4 1.1 fusion.4
  249.6 3.8 %collective-permute-start.25 = (bf16[64,640]{1,0:T(8,128)(2,1)S(1)}, bf16[64,640]{1,0:T(8,128)(2,1)S(1)}, u32[]{:S(2)}, u32[]{:S(2)}) collective-permute-start(bf16[64,640]{1,0:T(8,128)(2,1)S(1)} %get-tuple-element.121), channel_id=1, source_target_pairs={{0,24},{4,28},{8,0},{12,4},{16,8},{20,12},{24,16},{28,20},{1,25},{... | collective-permute-start | bytes 245768 | tf_op jit(solution)/shard_map/ppermute | solution.py:549
  253.6 1.5 collective-permute-start.18
  255.1 1.6 collective-permute-done.23
  256.7 3.0 %collective-permute-done.24 = bf16[64,640]{1,0:T(8,128)(2,1)S(1)} collective-permute-done((bf16[64,640]{1,0:T(8,128)(2,1)S(1)}, bf16[64,640]{1,0:T(8,128)(2,1)S(1)}, u32[]{:S(2)}, u32[]{:S(2)}) %collective-permute-start.24) | collective-permute-done | bytes 81952 | tf_op jit(solution)/shard_map/ppermute | solution.py:549
  260.3 3.5 %collective-permute-start.21 = (bf16[64,384]{1,0:T(8,128)(2,1)S(1)}, bf16[64,384]{1,0:T(8,128)(2,1)S(1)}, u32[]{:S(2)}, u32[]{:S(2)}) collective-permute-start(bf16[64,384]{1,0:T(8,128)(2,1)S(1)} %get-tuple-element.127), channel_id=1, source_target_pairs={{0,24},{4,28},{8,0},{12,4},{16,8},{20,12},{24,16},{28,20},{1,25},{... | collective-permute-start | bytes 147464 | tf_op jit(solution)/shard_map/ppermute | solution.py:549
  263.8 0.7 collective-permute-start.20
  264.4 0.6 slice_bitcast_fusion.4
  265.0 0.7 slice.112
  265.9 2.8 %collective-permute-done.20 = bf16[64,384]{1,0:T(8,128)(2,1)S(1)} collective-permute-done((bf16[64,384]{1,0:T(8,128)(2,1)S(1)}, bf16[64,384]{1,0:T(8,128)(2,1)S(1)}, u32[]{:S(2)}, u32[]{:S(2)}) %collective-permute-start.20) | collective-permute-done | bytes 49184 | tf_op jit(solution)/shard_map/ppermute | solution.py:549
  268.8 0.7 copy_bitcast_fusion
  269.7 1.7 gather_fusion.1
  (109 shorter events, 5.2 us)
Async XLA Ops:
  0.6 9.2 %copy-start = (bf16[32,128,128]{2,1,0:T(8,128)(2,1)S(1)}, bf16[32,128,128]{2,1,0:T(8,128)(2,1)}, u32[]{:S(2)}) copy-start(bf16[32,128,128]{2,1,0:T(8,128)(2,1)} %param.11) | copy-start | bytes 3145732
  0.6 9.0 %copy-start.14 = (f32[16]{0:T(128)S(1)}, f32[16]{0:T(128)}, u32[]{:S(2)}) copy-start(f32[16]{0:T(128)} %param.20) | copy-start | bytes 196
  0.7 9.0 %copy-start.13 = (f32[16]{0:T(128)S(1)}, f32[16]{0:T(128)}, u32[]{:S(2)}) copy-start(f32[16]{0:T(128)} %param.19) | copy-start | bytes 196
  0.7 9.1 %copy-start.15 = (s32[32]{0:T(128)S(1)}, s32[32]{0:T(128)}, u32[]{:S(2)}) copy-start(s32[32]{0:T(128)} %param.14) | copy-start | bytes 388
  2.4 19.0 %all-to-all-start = ((bf16[8,64,384]{2,1,0:T(8,128)(2,1)}), bf16[8,64,384]{2,1,0:T(8,128)(2,1)S(1)}, u32[]{:S(2)}, u32[]{:S(2)}) async-start(bf16[8,64,384]{2,1,0:T(8,128)(2,1)} %broadcast_in_dim.30), calls=%async_computation | async-start | bytes 786432 | tf_op jit(solution)/shard_map/all_to_all | solution.py:584
  11.8 13.2 %copy-start.9 = (bf16[512,64]{0,1:T(8,128)(2,1)S(1)}, bf16[512,64]{0,1:T(8,128)(2,1)}, u32[]{:S(2)}) copy-start(bf16[512,64]{0,1:T(8,128)(2,1)} %param.18) | copy-start | bytes 196612
  11.8 13.2 %copy-start.10 = (bf16[64,512]{1,0:T(8,128)(2,1)S(1)}, bf16[64,512]{1,0:T(8,128)(2,1)}, u32[]{:S(2)}) copy-start(bf16[64,512]{1,0:T(8,128)(2,1)} %param.17) | copy-start | bytes 196612
  11.8 13.3 %copy-start.12 = (bf16[128,64]{0,1:T(8,128)(2,1)S(1)}, bf16[128,64]{0,1:T(8,128)(2,1)}, u32[]{:S(2)}) copy-start(bf16[128,64]{0,1:T(8,128)(2,1)} %param.16) | copy-start | bytes 49156
  21.3 62.4 %copy-start.8 = (bf16[8,64,384]{2,1,0:T(8,128)(2,1)}, bf16[8,64,384]{2,1,0:T(8,128)(2,1)S(1)}, u32[]{:S(2)}) copy-start(bf16[8,64,384]{2,1,0:T(8,128)(2,1)S(1)} %all-to-all-done) | copy-start | bytes 1179652
  21.3 62.9 %all-to-all-start.1 = ((bf16[32,136,128]{2,1,0:T(8,128)(2,1)}), bf16[32,136,128]{2,1,0:T(8,128)(2,1)S(1)}, u32[]{:S(2)}, u32[]{:S(2)}) async-start(bf16[32,136,128]{2,1,0:T(8,128)(2,1)} %pad_maximum_fusion), calls=%async_computation.1 | async-start | bytes 2228224 | tf_op jit(solution)/shard_map/all_to_all | solution.py:686
  25.0 45.9 %copy-start.16 = (s32[32]{0:T(128)S(1)}, s32[32]{0:T(128)}, u32[]{:S(2)}) copy-start(s32[32]{0:T(128)} %param.12) | copy-start | bytes 388
  25.0 57.5 %copy-start.17 = (s32[32]{0:T(128)S(1)}, s32[32]{0:T(128)}, u32[]{:S(2)}) copy-start(s32[32]{0:T(128)} %param.13) | copy-start | bytes 388
  25.1 40.2 %collective-permute-start.5 = (bf16[64,1152]{1,0:T(8,128)(2,1)S(1)}, bf16[64,1152]{1,0:T(8,128)(2,1)S(1)}, u32[]{:S(2)}, u32[]{:S(2)}) collective-permute-start(bf16[64,1152]{1,0:T(8,128)(2,1)S(1)} %pad_maximum_fusion.1), channel_id=1, source_target_pairs={{0,24},{4,28},{8,0},{12,4},{16,8},{20,12},{24,16},{28,20},{1,25},{... | collective-permute-start | bytes 442376 | tf_op jit(solution)/shard_map/ppermute | solution.py:549
  28.7 36.5 %collective-permute-start.4 = (bf16[64,1152]{1,0:T(8,128)(2,1)S(1)}, bf16[64,1152]{1,0:T(8,128)(2,1)S(1)}, u32[]{:S(2)}, u32[]{:S(2)}) collective-permute-start(bf16[64,1152]{1,0:T(8,128)(2,1)S(1)} %pad_maximum_fusion.1), channel_id=1, source_target_pairs={{0,16},{4,20},{8,24},{12,28},{16,0},{20,4},{24,8},{28,12},{1,17},{... | collective-permute-start | bytes 442376 | tf_op jit(solution)/shard_map/ppermute | solution.py:549
  28.7 28.4 %collective-permute-start.3 = (bf16[64,1152]{1,0:T(8,128)(2,1)S(1)}, bf16[64,1152]{1,0:T(8,128)(2,1)S(1)}, u32[]{:S(2)}, u32[]{:S(2)}) collective-permute-start(bf16[64,1152]{1,0:T(8,128)(2,1)S(1)} %pad_maximum_fusion.1), channel_id=1, source_target_pairs={{0,8},{4,12},{8,16},{12,20},{16,24},{20,28},{24,0},{28,4},{1,9},{5... | collective-permute-start | bytes 442376 | tf_op jit(solution)/shard_map/ppermute | solution.py:549
  65.3 46.0 %copy-start.11 = (bf16[256,1152]{1,0:T(8,128)(2,1)}, bf16[256,1152]{1,0:T(8,128)(2,1)S(1)}, u32[]{:S(2)}) copy-start(bf16[256,1152]{1,0:T(8,128)(2,1)S(1)} %constant_dynamic-update-slice_fusion.refs_0_) | copy-start | bytes 1769476
  65.3 15.0 %collective-permute-start.6 = (bf16[256,1152]{1,0:T(8,128)(2,1)S(1)}, bf16[256,1152]{1,0:T(8,128)(2,1)}, u32[]{:S(2)}, u32[]{:S(2)}) collective-permute-start(bf16[256,1152]{1,0:T(8,128)(2,1)S(1)} %constant_dynamic-update-slice_fusion.refs_0_), channel_id=1, source_target_pairs={{0,4},{4,0},{8,12},{12,8},{16,20},{20,16},{24,28},{28,24},{1,5},{5... | collective-permute-start | bytes 1769480 | tf_op jit(solution)/shard_map/ppermute | solution.py:549
  66.9 10.5 %collective-permute-start.1 = (bf16[512,384]{1,0:T(8,128)(2,1)S(1)}, bf16[512,384]{1,0:T(8,128)(2,1)}, u32[]{:S(2)}, u32[]{:S(2)}) collective-permute-start(bf16[512,384]{1,0:T(8,128)(2,1)S(1)} %bitcast.138), channel_id=1, source_target_pairs={{0,2},{1,3},{2,0},{3,1},{4,6},{5,7},{6,4},{7,5},{8,10},{9,11},{10,... | collective-permute-start | bytes 1179656 | tf_op jit(solution)/shard_map/ppermute | solution.py:544
  77.3 16.4 %collective-permute-start.9 = (bf16[256,1152]{1,0:T(8,128)(2,1)S(1)}, bf16[256,1152]{1,0:T(8,128)(2,1)}, u32[]{:S(2)}, u32[]{:S(2)}) collective-permute-start(bf16[256,1152]{1,0:T(8,128)(2,1)S(1)} %constant_dynamic-update-slice_fusion.refs_0_), channel_id=1, source_target_pairs={{0,2},{1,3},{2,0},{3,1},{4,6},{5,7},{6,4},{7,5},{8,10},{9,11},{10,... | collective-permute-start | bytes 1769480 | tf_op jit(solution)/shard_map/ppermute | solution.py:544
  80.4 23.4 %collective-permute-start.10 = (bf16[256,1152]{1,0:T(8,128)(2,1)}, bf16[256,1152]{1,0:T(8,128)(2,1)}, u32[]{:S(2)}, u32[]{:S(2)}) collective-permute-start(bf16[256,1152]{1,0:T(8,128)(2,1)} %collective-permute-done.6.refs_1_), channel_id=1, source_target_pairs={{0,2},{1,3},{2,0},{3,1},{4,6},{5,7},{6,4},{7,5},{8,10},{9,11},{10,... | collective-permute-start | bytes 1769480 | tf_op jit(solution)/shard_map/ppermute | solution.py:544
  83.7 1.9 collective-permute-start
  83.7 43.6 %collective-permute-start.7 = (bf16[256,1152]{1,0:T(8,128)(2,1)S(1)}, bf16[256,1152]{1,0:T(8,128)(2,1)}, u32[]{:S(2)}, u32[]{:S(2)}) collective-permute-start(bf16[256,1152]{1,0:T(8,128)(2,1)S(1)} %constant_dynamic-update-slice_fusion.refs_0_), channel_id=1, source_target_pairs={{0,1},{1,0},{2,3},{3,2},{4,5},{5,4},{6,7},{7,6},{8,9},{9,8},{10,11... | collective-permute-start | bytes 1769480 | tf_op jit(solution)/shard_map/ppermute | solution.py:544
  84.2 19.6 %collective-permute-start.2 = (bf16[512,384]{1,0:T(8,128)(2,1)}, bf16[512,384]{1,0:T(8,128)(2,1)}, u32[]{:S(2)}, u32[]{:S(2)}) collective-permute-start(bf16[512,384]{1,0:T(8,128)(2,1)} %collective-permute-done.1.refs_2_), channel_id=1, source_target_pairs={{0,1},{1,0},{2,3},{3,2},{4,5},{5,4},{6,7},{7,6},{8,9},{9,8},{10,11... | collective-permute-start | bytes 1179656 | tf_op jit(solution)/shard_map/ppermute | solution.py:544
  84.2 19.5 %copy-start.2 = (bf16[32,136,128]{2,1,0:T(8,128)(2,1)}, bf16[32,136,128]{2,1,0:T(8,128)(2,1)S(1)}, u32[]{:S(2)}) copy-start(bf16[32,136,128]{2,1,0:T(8,128)(2,1)S(1)} %all-to-all-done.1) | copy-start | bytes 3342340
  85.6 41.8 %collective-permute-start.8 = (bf16[256,1152]{1,0:T(8,128)(2,1)}, bf16[256,1152]{1,0:T(8,128)(2,1)}, u32[]{:S(2)}, u32[]{:S(2)}) collective-permute-start(bf16[256,1152]{1,0:T(8,128)(2,1)} %collective-permute-done.6.refs_1_), channel_id=1, source_target_pairs={{0,1},{1,0},{2,3},{3,2},{4,5},{5,4},{6,7},{7,6},{8,9},{9,8},{10,11... | collective-permute-start | bytes 1769480 | tf_op jit(solution)/shard_map/ppermute | solution.py:544
  93.7 33.6 %collective-permute-start.11 = (bf16[256,1152]{1,0:T(8,128)(2,1)}, bf16[256,1152]{1,0:T(8,128)(2,1)}, u32[]{:S(2)}, u32[]{:S(2)}) collective-permute-start(bf16[256,1152]{1,0:T(8,128)(2,1)} %collective-permute-done.9.refs_4_), channel_id=1, source_target_pairs={{0,1},{1,0},{2,3},{3,2},{4,5},{5,4},{6,7},{7,6},{8,9},{9,8},{10,11... | collective-permute-start | bytes 1769480 | tf_op jit(solution)/shard_map/ppermute | solution.py:544
  103.8 23.6 %collective-permute-start.12 = (bf16[256,1152]{1,0:T(8,128)(2,1)}, bf16[256,1152]{1,0:T(8,128)(2,1)}, u32[]{:S(2)}, u32[]{:S(2)}) collective-permute-start(bf16[256,1152]{1,0:T(8,128)(2,1)} %collective-permute-done.10.refs_5_), channel_id=1, source_target_pairs={{0,1},{1,0},{2,3},{3,2},{4,5},{5,4},{6,7},{7,6},{8,9},{9,8},{10,11... | collective-permute-start | bytes 1769480 | tf_op jit(solution)/shard_map/ppermute | solution.py:544
  157.9 19.0 %collective-permute-start.13 = (bf16[2,512,1152]{2,1,0:T(8,128)(2,1)}, bf16[2,512,1152]{2,1,0:T(8,128)(2,1)}, u32[]{:S(2)}, u32[]{:S(2)}) collective-permute-start(bf16[2,512,1152]{2,1,0:T(8,128)(2,1)} %get-tuple-element.40), channel_id=1, source_target_pairs={{0,1},{1,0},{2,3},{3,2},{4,5},{5,4},{6,7},{7,6},{8,9},{9,8},{10,11... | collective-permute-start | bytes 7077896 | tf_op jit(solution)/shard_map/ppermute | solution.py:544
  160.7 16.1 %copy-start.1 = (bf16[2,512,1152]{2,1,0:T(8,128)(2,1)S(1)}, bf16[2,512,1152]{2,1,0:T(8,128)(2,1)}, u32[]{:S(2)}) copy-start(bf16[2,512,1152]{2,1,0:T(8,128)(2,1)} %get-tuple-element.39) | copy-start | bytes 7077892
  176.7 25.3 %collective-permute-start.16 = (bf16[2,512,384]{2,1,0:T(8,128)(2,1)}, bf16[2,512,384]{2,1,0:T(8,128)(2,1)S(1)}, u32[]{:S(2)}, u32[]{:S(2)}) collective-permute-start(bf16[2,512,384]{2,1,0:T(8,128)(2,1)} %get-tuple-element.50), channel_id=1, source_target_pairs={{0,1},{1,0},{2,3},{3,2},{4,5},{5,4},{6,7},{7,6},{8,9},{9,8},{10,11... | collective-permute-start | bytes 2359304 | tf_op jit(solution)/shard_map/ppermute | solution.py:544
  179.8 16.7 %collective-permute-start.14 = (bf16[2,4,64,512]{3,2,1,0:T(8,128)(2,1)S(1)}, bf16[2,4,64,512]{3,2,1,0:T(8,128)(2,1)S(1)}, u32[]{:S(2)}, u32[]{:S(2)}) collective-permute-start(bf16[2,4,64,512]{3,2,1,0:T(8,128)(2,1)S(1)} %fusion.5), channel_id=1, source_target_pairs={{0,4},{4,0},{8,12},{12,8},{16,20},{20,16},{24,28},{28,24},{1,5},{5... | collective-permute-start | bytes 1572872 | tf_op jit(solution)/shard_map/ppermute | solution.py:549
  180.6 18.9 %collective-permute-start.15 = (bf16[4,2,64,640]{3,2,0,1:T(8,128)(2,1)S(1)}, bf16[4,2,64,640]{3,2,0,1:T(8,128)(2,1)S(1)}, u32[]{:S(2)}, u32[]{:S(2)}) collective-permute-start(bf16[4,2,64,640]{3,2,0,1:T(8,128)(2,1)S(1)} %fusion.3), channel_id=1, source_target_pairs={{0,2},{1,3},{2,0},{3,1},{4,6},{5,7},{6,4},{7,5},{8,10},{9,11},{10,... | collective-permute-start | bytes 1966088 | tf_op jit(solution)/shard_map/ppermute | solution.py:544
  197.5 16.2 %collective-permute-start.26 = (bf16[4,64,512]{2,1,0:T(8,128)(2,1)}, bf16[4,64,512]{2,1,0:T(8,128)(2,1)}, u32[]{:S(2)}, u32[]{:S(2)}) collective-permute-start(bf16[4,64,512]{2,1,0:T(8,128)(2,1)} %slice_bitcast_fusion.1), channel_id=1, source_target_pairs={{0,2},{1,3},{2,0},{3,1},{4,6},{5,7},{6,4},{7,5},{8,10},{9,11},{10,... | collective-permute-start | bytes 786440 | tf_op jit(solution)/shard_map/ppermute | solution.py:544
  199.5 2.5 copy-start.6
  200.5 47.9 %collective-permute-start.22 = (bf16[4,64,640]{2,1,0:T(8,128)(2,1)}, bf16[4,64,640]{2,1,0:T(8,128)(2,1)}, u32[]{:S(2)}, u32[]{:S(2)}) collective-permute-start(bf16[4,64,640]{2,1,0:T(8,128)(2,1)} %dynamic-slice_bitcast_fusion), channel_id=1, source_target_pairs={{0,4},{4,0},{8,12},{12,8},{16,20},{20,16},{24,28},{28,24},{1,5},{5... | collective-permute-start | bytes 983048 | tf_op jit(solution)/shard_map/ppermute | solution.py:549
  202.0 9.0 %copy-start.4 = (bf16[2,512,384]{2,1,0:T(8,128)(2,1)}, bf16[2,512,384]{2,1,0:T(8,128)(2,1)S(1)}, u32[]{:S(2)}) copy-start(bf16[2,512,384]{2,1,0:T(8,128)(2,1)S(1)} %collective-permute-done.16) | copy-start | bytes 2359300
  210.9 58.5 %all-to-all-start.2 = ((bf16[32,136,128]{2,1,0:T(8,128)(2,1)}), bf16[32,136,128]{2,1,0:T(8,128)(2,1)S(1)}, u32[]{:S(2)}, u32[]{:S(2)}) async-start(bf16[32,136,128]{2,1,0:T(8,128)(2,1)} %bitcast.133), calls=%async_computation.2 | async-start | bytes 2228224 | tf_op jit(solution)/shard_map/all_to_all | solution.py:730
  214.7 0.7 copy-start.3
  215.4 22.8 %collective-permute-start.27 = (bf16[64,512]{1,0:T(8,128)(2,1)S(1)}, bf16[64,512]{1,0:T(8,128)(2,1)S(1)}, u32[]{:S(2)}, u32[]{:S(2)}) collective-permute-start(bf16[64,512]{1,0:T(8,128)(2,1)S(1)} %get-tuple-element.123), channel_id=1, source_target_pairs={{0,8},{4,12},{8,16},{12,20},{16,24},{20,28},{24,0},{28,4},{1,9},{5... | collective-permute-start | bytes 196616 | tf_op jit(solution)/shard_map/ppermute | solution.py:549
  217.2 20.9 %collective-permute-start.29 = (bf16[64,512]{1,0:T(8,128)(2,1)S(1)}, bf16[64,512]{1,0:T(8,128)(2,1)S(1)}, u32[]{:S(2)}, u32[]{:S(2)}) collective-permute-start(bf16[64,512]{1,0:T(8,128)(2,1)S(1)} %get-tuple-element.124), channel_id=1, source_target_pairs={{0,24},{4,28},{8,0},{12,4},{16,8},{20,12},{24,16},{28,20},{1,25},{... | collective-permute-start | bytes 196616 | tf_op jit(solution)/shard_map/ppermute | solution.py:549
  219.3 27.6 %collective-permute-start.28 = (bf16[64,512]{1,0:T(8,128)(2,1)S(1)}, bf16[64,512]{1,0:T(8,128)(2,1)S(1)}, u32[]{:S(2)}, u32[]{:S(2)}) collective-permute-start(bf16[64,512]{1,0:T(8,128)(2,1)S(1)} %get-tuple-element.125), channel_id=1, source_target_pairs={{0,16},{4,20},{8,24},{12,28},{16,0},{20,4},{24,8},{28,12},{1,17},{... | collective-permute-start | bytes 196616 | tf_op jit(solution)/shard_map/ppermute | solution.py:549
  220.1 33.3 %copy-start.5 = (bf16[2,512,384]{2,1,0:T(8,128)(2,1)S(1)}, bf16[2,512,384]{2,1,0:T(8,128)(2,1)}, u32[]{:S(2)}) copy-start(bf16[2,512,384]{2,1,0:T(8,128)(2,1)} %copy-done.4) | copy-start | bytes 2359300
  220.1 33.3 %copy-start.7 = (bf16[2,512,384]{2,1,0:T(8,128)(2,1)S(1)}, bf16[2,512,384]{2,1,0:T(8,128)(2,1)}, u32[]{:S(2)}) copy-start(bf16[2,512,384]{2,1,0:T(8,128)(2,1)} %get-tuple-element.49) | copy-start | bytes 2359300
  220.1 33.3 %collective-permute-start.17 = (bf16[2,4,64,384]{3,2,1,0:T(8,128)(2,1)}, bf16[2,4,64,384]{3,2,1,0:T(8,128)(2,1)S(1)}, u32[]{:S(2)}, u32[]{:S(2)}) collective-permute-start(bf16[2,4,64,384]{3,2,1,0:T(8,128)(2,1)} %fusion.7), channel_id=1, source_target_pairs={{0,4},{4,0},{8,12},{12,8},{16,20},{20,16},{24,28},{28,24},{1,5},{5... | collective-permute-start | bytes 1179656 | tf_op jit(solution)/shard_map/ppermute | solution.py:549
  249.5 7.2 %collective-permute-start.23 = (bf16[64,640]{1,0:T(8,128)(2,1)S(1)}, bf16[64,640]{1,0:T(8,128)(2,1)S(1)}, u32[]{:S(2)}, u32[]{:S(2)}) collective-permute-start(bf16[64,640]{1,0:T(8,128)(2,1)S(1)} %get-tuple-element.120), channel_id=1, source_target_pairs={{0,8},{4,12},{8,16},{12,20},{16,24},{20,28},{24,0},{28,4},{1,9},{5... | collective-permute-start | bytes 245768 | tf_op jit(solution)/shard_map/ppermute | solution.py:549
  249.6 7.1 %collective-permute-start.25 = (bf16[64,640]{1,0:T(8,128)(2,1)S(1)}, bf16[64,640]{1,0:T(8,128)(2,1)S(1)}, u32[]{:S(2)}, u32[]{:S(2)}) collective-permute-start(bf16[64,640]{1,0:T(8,128)(2,1)S(1)} %get-tuple-element.121), channel_id=1, source_target_pairs={{0,24},{4,28},{8,0},{12,4},{16,8},{20,12},{24,16},{28,20},{1,25},{... | collective-permute-start | bytes 245768 | tf_op jit(solution)/shard_map/ppermute | solution.py:549
  253.4 6.3 %collective-permute-start.24 = (bf16[64,640]{1,0:T(8,128)(2,1)S(1)}, bf16[64,640]{1,0:T(8,128)(2,1)S(1)}, u32[]{:S(2)}, u32[]{:S(2)}) collective-permute-start(bf16[64,640]{1,0:T(8,128)(2,1)S(1)} %get-tuple-element.122), channel_id=1, source_target_pairs={{0,16},{4,20},{8,24},{12,28},{16,0},{20,4},{24,8},{28,12},{1,17},{... | collective-permute-start | bytes 245768 | tf_op jit(solution)/shard_map/ppermute | solution.py:549
  253.6 6.2 %collective-permute-start.18 = (bf16[4,64,384]{2,1,0:T(8,128)(2,1)S(1)}, bf16[4,64,384]{2,1,0:T(8,128)(2,1)S(1)}, u32[]{:S(2)}, u32[]{:S(2)}) collective-permute-start(bf16[4,64,384]{2,1,0:T(8,128)(2,1)S(1)} %slice_bitcast_fusion.2), channel_id=1, source_target_pairs={{0,2},{1,3},{2,0},{3,1},{4,6},{5,7},{6,4},{7,5},{8,10},{9,11},{10,... | collective-permute-start | bytes 589832 | tf_op jit(solution)/shard_map/ppermute | solution.py:544
  259.9 6.0 %collective-permute-start.19 = (bf16[64,384]{1,0:T(8,128)(2,1)S(1)}, bf16[64,384]{1,0:T(8,128)(2,1)S(1)}, u32[]{:S(2)}, u32[]{:S(2)}) collective-permute-start(bf16[64,384]{1,0:T(8,128)(2,1)S(1)} %get-tuple-element.126), channel_id=1, source_target_pairs={{0,8},{4,12},{8,16},{12,20},{16,24},{20,28},{24,0},{28,4},{1,9},{5... | collective-permute-start | bytes 147464 | tf_op jit(solution)/shard_map/ppermute | solution.py:549
  260.3 5.7 %collective-permute-start.21 = (bf16[64,384]{1,0:T(8,128)(2,1)S(1)}, bf16[64,384]{1,0:T(8,128)(2,1)S(1)}, u32[]{:S(2)}, u32[]{:S(2)}) collective-permute-start(bf16[64,384]{1,0:T(8,128)(2,1)S(1)} %get-tuple-element.127), channel_id=1, source_target_pairs={{0,24},{4,28},{8,0},{12,4},{16,8},{20,12},{24,16},{28,20},{1,25},{... | collective-permute-start | bytes 147464 | tf_op jit(solution)/shard_map/ppermute | solution.py:549
  263.8 5.0 %collective-permute-start.20 = (bf16[64,384]{1,0:T(8,128)(2,1)S(1)}, bf16[64,384]{1,0:T(8,128)(2,1)S(1)}, u32[]{:S(2)}, u32[]{:S(2)}) collective-permute-start(bf16[64,384]{1,0:T(8,128)(2,1)S(1)} %get-tuple-element.128), channel_id=1, source_target_pairs={{0,16},{4,20},{8,24},{12,28},{16,0},{20,4},{24,8},{28,12},{1,17},{... | collective-permute-start | bytes 147464 | tf_op jit(solution)/shard_map/ppermute | solution.py:549
where the time goes:
time: 272 us
  waiting for transfers between devices  103 us (38%)
  Pallas kernels  93.2 us (34%)
  starting transfers between devices  46.1 us (17%)
  local copies, waits for them, and re-layouts  17 us (6%)
  other arithmetic  8.83 us (3%)
  between operations  3.79 us (1%)
    ppermute x16, waiting for transfers between devices, along_dp(): return lax.ppermute(value, 'dp', [(i, move(i)) for i in range(count)])  69.8 us
    pallas_call x2, Pallas kernels, attend_back(): pl.pallas_call(attend_back_kernel, grid_spec=pltpu.PrefetchScalarGridSpec...  31.8 us
    pallas_call x1, Pallas kernels, middle_block(): pl.pallas_call(functools.partial(middle_kernel, groups), grid_spec=pltpu....  30.5 us
    ppermute x14, waiting for transfers between devices, swap(): return lax.ppermute(value, 'tensor', [(i, i ^ apart) for i in range(count)])  23.6 us
    ppermute x16, starting transfers between devices, along_dp(): return lax.ppermute(value, 'dp', [(i, move(i)) for i in range(count)])  23.1 us
    pallas_call x1, Pallas kernels, attend(): pl.pallas_call(attend_kernel, grid_spec=pltpu.PrefetchScalarGridSpec(num_...  15.3 us
    all_to_all x1, waiting for transfers between devices, collect_rows(): lax.all_to_all(jnp.broadcast_to(shard[None], (count,) + shard.shape), 'dp...  9.56 us
    ppermute x14, starting transfers between devices, swap(): return lax.ppermute(value, 'tensor', [(i, i ^ apart) for i in range(count)])  9.39 us
  transfers between devices with their start and end apart: 33, of which 14 were waited for; matrix products, arithmetic and copies ran while one was open for 8% of the time, Pallas kernels for 23%

commit v1 on v0

--- a/solution.py
+++ b/solution.py
@@ -211,19 +211,20 @@
 
 def gelu_both(values):
     root = math.sqrt(2.0 / math.pi)
-    square = values * values
-    tanh = jnp.tanh(root * values * (1.0 + 0.044715 * square))
+    scaled = root * values
+    inner = scaled * (1.0 + 0.044715 * (values * values))
+    tanh = jnp.tanh(inner)
     half = 0.5 + 0.5 * tanh
-    slope = half + (0.5 * root) * values * (1.0 - tanh * tanh) * (1.0 + (3 * 0.044715) * square)
+    slope = half + (1.0 - tanh * tanh) * (1.5 * inner - scaled)
     return values * half, slope
 
 
 def middle_kernel(
     groups, limit_ref, place_ref, x_ref, clock_ref, gain_ref, ctx_ref, og_ref, *refs
 ):
-    weight_refs, refs = refs[:-14], refs[-14:]
-    out_ref, cg_ref, mg_ref, gg_ref, send_ref, keep_ref = refs[:6]
-    wide, units, active_s, ug_s, n_turn, fg_turn, ag_turn, ctx_s = refs[6:]
+    weight_refs, refs = refs[:-16], refs[-16:]
+    out_ref, cg_ref, mg_ref, gg_ref, up_send, down_send, up_keep, down_keep = refs[:8]
+    wide, units, active_s, ug_s, n_turn, fg_turn, ag_turn, ctx_s = refs[8:]
     step = pl.program_id(0)
     parts, _, hidden = active_s.shape
     blocks = pl.num_programs(0) - parts
@@ -307,11 +308,11 @@
             mul(fg_turn[...], active_s[part]).astype(BF16),
         )
 
-        def into(ref):
-            ref[0, :, 0:PAIR], ref[0, :, PAIR : PAIR + hidden], ref[0, :, PAIR + hidden :] = grads
-
-        pl.when(turn < 2)(lambda: into(send_ref))
-        pl.when(turn >= 2)(lambda: into(keep_ref))
+        def into(up_ref, down_ref):
+            up_ref[0, :, 0:PAIR], up_ref[0, :, PAIR:], down_ref[0] = grads
+
+        pl.when(turn < 2)(lambda: into(up_send, down_send))
+        pl.when(turn >= 2)(lambda: into(up_keep, down_keep))
 
 
 def middle_block(limit, place, groups, x_blocks, clock, gain, ctx, w_parts, out_grad):
@@ -331,10 +332,11 @@
     )
     rows = lambda n: pl.BlockSpec((ROWS, n), lambda i, *s: (row(i), 0))
     one = pl.BlockSpec((1, ROWS, features), lambda i, *s: (0, row(i), 0))
-    grads = lambda first: pl.BlockSpec(
-        (1, features, columns), lambda i, *s: (jnp.clip(i - blocks - first, 0, 1), 0, 0)
-    )
-    grads_shape = jax.ShapeDtypeStruct((2, features, columns), BF16)
+    grads = lambda first, n: pl.BlockSpec(
+        (1, features, n), lambda i, *s: (jnp.clip(i - blocks - first, 0, 1), 0, 0)
+    )
+    up_shape = jax.ShapeDtypeStruct((2, features, PAIR + hidden), BF16)
+    down_shape = jax.ShapeDtypeStruct((2, features, hidden), BF16)
     return pl.pallas_call(
         functools.partial(middle_kernel, groups),
         grid_spec=pltpu.PrefetchScalarGridSpec(
@@ -353,7 +355,7 @@
             out_specs=[
                 one, rows(features), rows(features),
                 pl.BlockSpec((1, features), lambda i, *s: (0, 0)),
-                grads(0), grads(2),
+                grads(0, PAIR + hidden), grads(0, hidden), grads(2, PAIR + hidden), grads(2, hidden),
             ],
             scratch_shapes=[
                 pltpu.VMEM((features, parts * PAIR), BF16),
@@ -371,8 +373,7 @@
             jax.ShapeDtypeStruct((length, features), BF16),
             jax.ShapeDtypeStruct((length, features), F32),
             jax.ShapeDtypeStruct((1, features), F32),
-            grads_shape,
-            grads_shape,
+            up_shape, down_shape, up_shape, down_shape,
         ],
         compiler_params=params(),
         cost_estimate=cost(25),
@@ -568,15 +569,9 @@
 def collect_pieces(shard, gate):
     count = lax.axis_size("dp") // 2
     mine = jnp.concatenate([shard] + [ahead(shard, step) for step in range(1, count)], axis=0)
+    mine = after(mine, gate)
     other = across(mine)
-    far_mine = swap(after(mine, gate), 2)
-    far_other = swap(other, 2)
-    return (
-        (mine, other),
-        (swap(mine, 1), swap(other, 1)),
-        (far_mine, far_other),
-        (swap(far_mine, 1), swap(far_other, 1)),
-    )
+    return mine, other, swap(mine, 2), swap(other, 2)
 
 
 def collect_rows(shard):
@@ -670,10 +665,9 @@
     qkv_parts = collect_columns(qkv_rows)
 
     direct = dp_count <= DIRECT
-    rest = after(rest, qkv_rows)
     if direct:
         place, groups = places(), dp_count
-        rest_parts = collect_pieces(rest, qkv_parts[2])
+        pieces = collect_pieces(rest, qkv_parts[2])
     else:
         place, groups = jnp.zeros((1,), jnp.int32), None
         rest_parts = [(part,) for part in collect_columns(collect_rows(rest))]
@@ -690,28 +684,34 @@
     x_blocks = x_blocks.reshape(dp_count, tensor_count, tokens + SPARE, width)
 
     mixed, n_one_turn, qkv_wide = project(limit, x_blocks, clock, gain_one, qkv_parts)
+    if direct:
+        mine, other, far_mine, far_other = pieces
+        near_mine, near_other, last_mine = swap(mine, 1), swap(other, 1), swap(far_mine, 1)
+        mixed = after(mixed, near_mine, near_other, last_mine)
     ctx, ctx_turn, lse = attend(limit, mixed, tensor_count)
-    output, context_grad, middle_grad, two_grad, rest_send, rest_keep = middle_block(
+    if direct:
+        last_other = swap(after(far_other, ctx), 1)
+        rest_parts = (
+            (mine, other), (near_mine, near_other), (far_mine, far_other), (last_mine, last_other)
+        )
+    output, context_grad, middle_grad, two_grad, up_send, down_send, up_keep, down_keep = middle_block(
         limit, place, groups, x_blocks, clock, gain_two, ctx, rest_parts, out_grad
     )
-    rest_came = swap(rest_send, 1)
+    up_came, down_came = swap(up_send, 1), swap(down_send, 1)
 
     back = functools.partial(attend_back, limit, mixed, ctx_turn, lse)
-    context_grad = after(context_grad, rest_send)
+    context_grad = after(context_grad, up_send, down_send)
     odd, qkv_send = back(context_grad, n_one_turn, 3)
     qkv_came = swap(qkv_send, 1)
-    split = PAIR + hidden
     if direct:
-        rest_values = [grouped(value) for value in (rest_keep, rest_came)]
-        down_sent, down_rest = fold_pair([value[..., split:] for value in rest_values])
-        up_sent, up_rest = fold_far([value[..., :split] for value in rest_values])
+        down_sent, down_rest = fold_pair([grouped(value) for value in (down_keep, down_came)])
+        up_sent, up_rest = fold_far([grouped(value) for value in (up_keep, up_came)])
         even, qkv_keep = back(after(context_grad, odd, down_sent, up_sent), n_one_turn, 2)
         down_value, up_value = add(*down_rest()), add(*up_rest())
         down_sent, down_rest = fold_far([down_value])
         up_sent, up_rest = fold_pair([up_value])
         qkv_keep = after(qkv_keep, down_value, up_value)
-        qkv_values = [grouped(value) for value in (qkv_keep, qkv_came)]
-        qkv_sent, qkv_rest = fold_pair(qkv_values)
+        qkv_sent, qkv_rest = fold_pair([grouped(value) for value in (qkv_keep, qkv_came)])
         middle_grad = after(middle_grad, down_sent, up_sent, qkv_sent)
         down_total = fold_coarse(down_rest())
         up_total = fold_coarse(up_rest())
@@ -719,11 +719,10 @@
         qkv_total = fold_coarse(qkv_rest())
     else:
         even, qkv_keep = back(after(context_grad, odd), n_one_turn, 2)
-        rest_sent, rest_rest = fold_far([rest_keep, rest_came])
-        rest_total = exchange_rows(add(*rest_rest()))
-        up_total, down_total = rest_total[:, :split], rest_total[:, split:]
-        qkv_sent, qkv_rest = fold_far([qkv_keep, qkv_came])
-        qkv_total = exchange_rows(add(*qkv_rest()))
+        totals = []
+        for pair in ((up_keep, up_came), (down_keep, down_came), (qkv_keep, qkv_came)):
+            totals.append(exchange_rows(add(*fold_far(pair)[1]())))
+        up_total, down_total, qkv_total = totals
     begin_grad = begin_block(
         limit, x_blocks, clock, gain_one, two_grad, qkv_wide, middle_grad, odd, even
     )

time: 272 us -> 248 us (0.912)
  waiting for transfers between devices: 103 us -> 77.2 us
  starting transfers between devices: 46.1 us -> 54.6 us
  Pallas kernels: 93.2 us -> 88.3 us
  local copies, waits for them, and re-layouts: 17 us -> 14.1 us
    ppermute x14 -> x15, waiting for transfers between devices: 23.6 us -> 7.89 us  [swap(): return lax.ppermute(value, 'tensor', [(i, i ^ apart) for i in range(count)])]
    ppermute x16, waiting for transfers between devices: 69.8 us -> 59.8 us  [along_dp(): return lax.ppermute(value, 'dp', [(i, move(i)) for i in range(count)])]
    ppermute x14 -> x15, starting transfers between devices: 9.39 us -> 13.6 us  [swap(): return lax.ppermute(value, 'tensor', [(i, i ^ apart) for i in range(count)])]
    slice x4 -> x0, local copies, waits for them, and re-layouts: 4.16 us -> none  [the longest x2 2.62 us: on_device(): value[..., split:]]
    ppermute x16, starting transfers between devices: 23.1 us -> 26.9 us  [along_dp(): return lax.ppermute(value, 'dp', [(i, move(i)) for i in range(count)])]
    pallas_call x1, Pallas kernels: 30.5 us -> 27 us  [middle_block(): pl.pallas_call(functools.partial(middle_kernel, groups), grid_spec=pltpu....]
  transfers between devices with their start and end apart: 33 -> 34, of which waited for: 14 -> 13; matrix products, arithmetic and copies ran while one was open for 8% -> 7% of each run, Pallas kernels for 23% -> 25%
where the time goes in v1:
time: 248 us; the launch traced here: 247 us
  Pallas kernels  88.3 us (36%)
  waiting for transfers between devices  77.2 us (31%)
  starting transfers between devices  54.6 us (22%)
  local copies, waits for them, and re-layouts  14.1 us (6%)
  other arithmetic  8.89 us (4%)
  between operations  3.78 us (2%)
    ppermute x16, waiting for transfers between devices, along_dp(): return lax.ppermute(value, 'dp', [(i, move(i)) for i in range(count)])  59.8 us
    pallas_call x2, Pallas kernels, attend_back(): pl.pallas_call(attend_back_kernel, grid_spec=pltpu.PrefetchScalarGridSpec...  32 us
    pallas_call x1, Pallas kernels, middle_block(): pl.pallas_call(functools.partial(middle_kernel, groups), grid_spec=pltpu....  27 us
    ppermute x16, starting transfers between devices, along_dp(): return lax.ppermute(value, 'dp', [(i, move(i)) for i in range(count)])  26.9 us
    pallas_call x1, Pallas kernels, attend(): pl.pallas_call(attend_kernel, grid_spec=pltpu.PrefetchScalarGridSpec(num_...  15.2 us
    ppermute x15, starting transfers between devices, swap(): return lax.ppermute(value, 'tensor', [(i, i ^ apart) for i in range(count)])  13.6 us
    all_to_all x1, waiting for transfers between devices, collect_rows(): lax.all_to_all(jnp.broadcast_to(shard[None], (count,) + shard.shape), 'dp...  9.58 us
    ppermute x15, waiting for transfers between devices, swap(): return lax.ppermute(value, 'tensor', [(i, i ^ apart) for i in range(count)])  7.89 us
  transfers between devices with their start and end apart: 34, of which 13 were waited for; matrix products, arithmetic and copies ran while one was open for 7% of the time, Pallas kernels for 25%

profile of v1, /device:TPU:0, one launch (start us, length us, event | category | flops | bytes accessed | tf_op | source)
XLA Modules:
  0.0 247.0 jit_solution(9149817738214640564)
XLA Ops:
  0.7 0.9 copy_bitcast_fusion.1
  1.6 0.8 broadcast_in_dim.30
  2.4 7.3 %all-to-all-start = ((bf16[8,64,384]{2,1,0:T(8,128)(2,1)}), bf16[8,64,384]{2,1,0:T(8,128)(2,1)S(1)}, u32[]{:S(2)}, u32[]{:S(2)}) async-start(bf16[8,64,384]{2,1,0:T(8,128)(2,1)} %broadcast_in_dim.30), calls=%async_computation | async-start | bytes 786432 | tf_op jit(solution)/shard_map/all_to_all | solution.py:579
  9.8 0.7 gather_fusion
  10.6 1.1 pad_maximum_fusion
  11.7 9.6 %all-to-all-done = bf16[8,64,384]{2,1,0:T(8,128)(2,1)S(1)} async-done(((bf16[8,64,384]{2,1,0:T(8,128)(2,1)}), bf16[8,64,384]{2,1,0:T(8,128)(2,1)S(1)}, u32[]{:S(2)}, u32[]{:S(2)}) %all-to-all-start) | async-done | bytes 393248 | tf_op jit(solution)/shard_map/all_to_all | solution.py:579
  21.3 3.6 %all-to-all-start.1 = ((bf16[32,136,128]{2,1,0:T(8,128)(2,1)}), bf16[32,136,128]{2,1,0:T(8,128)(2,1)S(1)}, u32[]{:S(2)}, u32[]{:S(2)}) async-start(bf16[32,136,128]{2,1,0:T(8,128)(2,1)} %pad_maximum_fusion), calls=%async_computation.1 | async-start | bytes 2228224 | tf_op jit(solution)/shard_map/all_to_all | solution.py:680
  25.1 1.8 collective-permute-start.3
  26.9 2.4 collective-permute-start.4
  29.3 1.4 collective-permute-start.5
  30.7 1.5 collective-permute-start.1
  32.2 19.1 %collective-permute-done.3 = bf16[64,1152]{1,0:T(8,128)(2,1)S(1)} collective-permute-done((bf16[64,1152]{1,0:T(8,128)(2,1)S(1)}, bf16[64,1152]{1,0:T(8,128)(2,1)S(1)}, u32[]{:S(2)}, u32[]{:S(2)}) %collective-permute-start.3) | collective-permute-done | bytes 147488 | tf_op jit(solution)/shard_map/ppermute | solution.py:550
  51.2 11.3 %collective-permute-done.4 = bf16[64,1152]{1,0:T(8,128)(2,1)S(1)} collective-permute-done((bf16[64,1152]{1,0:T(8,128)(2,1)S(1)}, bf16[64,1152]{1,0:T(8,128)(2,1)S(1)}, u32[]{:S(2)}, u32[]{:S(2)}) %collective-permute-start.4) | collective-permute-done | bytes 147488 | tf_op jit(solution)/shard_map/ppermute | solution.py:550
  62.7 0.8 copy-done.16
  63.4 1.5 collective-permute-start.7
  64.9 1.5 collective-permute-start.9
  70.2 0.6 dynamic-slice.4.limit_ref
  70.8 0.6 pad_maximum_fusion.3.clock_ref
  72.0 6.0 %collective-permute-done.7.refs_1_ = bf16[256,1152]{1,0:T(8,128)(2,1)} collective-permute-done((bf16[256,1152]{1,0:T(8,128)(2,1)S(1)}, bf16[256,1152]{1,0:T(8,128)(2,1)}, u32[]{:S(2)}, u32[]{:S(2)}) %collective-permute-start.7) | collective-permute-done | bytes 589856 | tf_op jit(solution)/shard_map/ppermute | solution.py:550
  78.0 1.2 collective-permute-done.9.refs_4_
  79.4 0.7 reshape_squeeze.8.gain_ref
  80.1 1.5 collective-permute-start.11
  81.6 6.9 %project.1 = (bf16[1024,1536]{1,0:T(8,128)(2,1)}, bf16[512,1024]{1,0:T(8,128)(2,1)}, bf16[512,1536]{1,0:T(8,128)(2,1)}) custom-call(s32[1]{0:T(128)} %dynamic-slice.4.limit_ref, bf16[8,4,136,128]{3,2,1,0:T(8,128)(2,1)} %bitcast.125, f32[1,512]{1,0:T(1,128)} %pad_maximum_fusion.3.clock_ref, f32[1,512]{1,0:T(1,128)} %reshape_squeeze.8.gain_ref, ...), custom_call_target="tpu_custom_call" | custom-call | flops 5750000128 | bytes 1048576 | tf_op jit(solution)/shard_map/project/pallas_call | solution.py:94
  88.5 15.2 %attend.1 = (bf16[1024,512]{1,0:T(8,128)(2,1)}, bf16[512,1024]{1,0:T(8,128)(2,1)}, f32[4,2,1024]{2,1,0:T(2,128)}) custom-call(s32[1]{0:T(128)} %dynamic-slice.4.limit_ref, bf16[1024,1536]{1,0:T(8,128)(2,1)} %get-tuple-element.37.q_ref.k_ref.v_ref, bf16[1024,1536]{1,0:T(8,128)(2,1)} %get-tuple-element.37.q_ref.k_ref.v_ref, ...), custom_call_target="tpu_custom_call" | custom-call | flops 17250000896 | bytes 1048576 | tf_op jit(solution)/shard_map/attend/pallas_call | solution.py:183
  103.8 0.9 collective-permute-start.12
  105.4 0.7 reshape_squeeze.7.gain_ref
  106.5 0.8 copy-done.15
  107.4 27.0 %middle.1 = (bf16[1,1024,512]{2,1,0:T(8,128)(2,1)}, bf16[1024,512]{1,0:T(8,128)(2,1)}, f32[1024,512]{1,0:T(8,128)}, f32[1,512]{1,0:T(1,128)}, bf16[2,512,640]{2,...) custom-call(s32[1]{0:T(128)} %dynamic-slice.4.limit_ref, ...), custom_call_target="tpu_custom_call" | custom-call | flops 28750000128 | bytes 1048576 | tf_op jit(solution)/shard_map/middle/pallas_call | solution.py:340
  134.4 3.9 %collective-permute-start.13 = (bf16[2,512,512]{2,1,0:T(8,128)(2,1)}, bf16[2,512,512]{2,1,0:T(8,128)(2,1)S(1)}, u32[]{:S(2)}, u32[]{:S(2)}) collective-permute-start(bf16[2,512,512]{2,1,0:T(8,128)(2,1)} %get-tuple-element.44), channel_id=1, source_target_pairs={{0,1},{1,0},{2,3},{3,2},{4,5},{5,4},{6,7},{7,6},{8,9},{9,8},{10,11... | collective-permute-start | bytes 3145736 | tf_op jit(solution)/shard_map/ppermute | solution.py:545
  138.3 0.7 scatter_custom_fusion
  139.1 1.6 collective-permute-done.13
  140.8 2.0 fusion.4
  142.8 0.9 collective-permute-start.14
  143.7 16.2 %attend_back.2 = (bf16[1024,768]{1,0:T(8,128)(2,1)}, bf16[2,512,384]{2,1,0:T(8,128)(2,1)}) custom-call(s32[1]{0:T(128)} %dynamic-slice.4.limit_ref, bf16[1024,1536]{1,0:T(8,128)(2,1)} %get-tuple-element.37.q_ref.k_ref.v_ref, bf16[1024,1536]{1,0:T(8,128)(2,1)} %get-tuple-element.37.q_ref.k_ref.v_ref, bf16[1024,1536]{1,0:T(8,128)(2,1)} %get-tuple-element.37.q_ref.k_ref.v_ref, ...), custom_call_target="tpu_custom_call" | custom-call | flops 18400000000 | bytes 1048576 | tf_op jit(solution)/shard_map/attend_back/pallas_call | solution.py:426
  160.3 0.6 collective-permute-start.16
  161.6 1.0 collective-permute-start.27
  162.7 15.8 %attend_back.3 = (bf16[1024,768]{1,0:T(8,128)(2,1)}, bf16[2,512,384]{2,1,0:T(8,128)(2,1)}) custom-call(s32[1]{0:T(128)} %dynamic-slice.4.limit_ref, bf16[1024,1536]{1,0:T(8,128)(2,1)} %get-tuple-element.37.q_ref.k_ref.v_ref, bf16[1024,1536]{1,0:T(8,128)(2,1)} %get-tuple-element.37.q_ref.k_ref.v_ref, bf16[1024,1536]{1,0:T(8,128)(2,1)} %get-tuple-element.37.q_ref.k_ref.v_ref, ...), custom_call_target="tpu_custom_call" | custom-call | flops 18400000000 | bytes 1048576 | tf_op jit(solution)/shard_map/attend_back/pallas_call | solution.py:426
  178.5 4.6 %collective-permute-done.27 = bf16[4,64,512]{2,1,0:T(8,128)(2,1)S(1)} collective-permute-done((bf16[4,64,512]{2,1,0:T(8,128)(2,1)S(1)}, bf16[4,64,512]{2,1,0:T(8,128)(2,1)S(1)}, u32[]{:S(2)}, u32[]{:S(2)}) %collective-permute-start.27) | collective-permute-done | bytes 262176 | tf_op jit(solution)/shard_map/ppermute | solution.py:545
  183.1 0.7 dynamic-slice_bitcast_fusion.6
  183.8 3.4 %collective-permute-start.28 = (bf16[64,512]{1,0:T(8,128)(2,1)}, bf16[64,512]{1,0:T(8,128)(2,1)S(1)}, u32[]{:S(2)}, u32[]{:S(2)}) collective-permute-start(bf16[64,512]{1,0:T(8,128)(2,1)} %get-tuple-element.127), channel_id=1, source_target_pairs={{0,8},{4,12},{8,16},{12,20},{16,24},{20,28},{24,0},{28,4},{1,9},{5... | collective-permute-start | bytes 196616 | tf_op jit(solution)/shard_map/ppermute | solution.py:550
  187.2 1.4 collective-permute-start.29
  188.6 0.9 collective-permute-start.30
  189.7 0.8 dynamic-slice_bitcast_fusion
  190.5 1.6 collective-permute-start.23
  192.2 7.2 %begin_back.1 = bf16[8,4,136,128]{3,2,1,0:T(8,128)(2,1)} custom-call(s32[1]{0:T(128)} %dynamic-slice.4.limit_ref, bf16[8,4,136,128]{3,2,1,0:T(8,128)(2,1)} %bitcast.127, f32[1,512]{1,0:T(1,128)} %pad_maximum_fusion.3.clock_ref, f32[1,512]{1,0:T(1,128)} %reshape_squeeze.8.gain_ref, f32[1,512]{1,0:T(1,128)} %get-tuple-element.41.gg_two_ref, ...), custom_call_target="tpu_custom_call" | custom-call | flops 8049999872 | bytes 1048576 | tf_op jit(solution)/shard_map/begin_back/pallas_call | solution.py:512
  199.4 3.2 %all-to-all-start.2 = ((bf16[32,136,128]{2,1,0:T(8,128)(2,1)}), bf16[32,136,128]{2,1,0:T(8,128)(2,1)S(1)}, u32[]{:S(2)}, u32[]{:S(2)}) async-start(bf16[32,136,128]{2,1,0:T(8,128)(2,1)} %bitcast.128), calls=%async_computation.2 | async-start | bytes 2228224 | tf_op jit(solution)/shard_map/all_to_all | solution.py:729
  202.7 1.8 collective-permute-start.18
  204.6 1.6 fusion.12
  206.1 1.1 fusion.3
  207.3 1.5 collective-permute-start.24
  208.8 2.4 collective-permute-start.25
  211.2 1.4 collective-permute-start.26
  212.6 11.4 %collective-permute-done.18 = bf16[2,4,64,384]{3,2,1,0:T(8,128)(2,1)S(1)} collective-permute-done((bf16[2,4,64,384]{3,2,1,0:T(8,128)(2,1)S(1)}, bf16[2,4,64,384]{3,2,1,0:T(8,128)(2,1)S(1)}, u32[]{:S(2)}, u32[]{:S(2)}) %collective-permute-start.18) | collective-permute-done | bytes 393248 | tf_op jit(solution)/shard_map/ppermute | solution.py:550
  224.2 2.0 collective-permute-start.19
  226.2 1.3 collective-permute-done.24
  227.5 8.5 %collective-permute-done.25 = bf16[64,640]{1,0:T(8,128)(2,1)S(1)} collective-permute-done((bf16[64,640]{1,0:T(8,128)(2,1)S(1)}, bf16[64,640]{1,0:T(8,128)(2,1)S(1)}, u32[]{:S(2)}, u32[]{:S(2)}) %collective-permute-start.25) | collective-permute-done | bytes 81952 | tf_op jit(solution)/shard_map/ppermute | solution.py:550
  236.2 1.9 collective-permute-start.20
  238.1 1.3 collective-permute-start.21
  239.4 1.1 collective-permute-start.22
  240.5 0.6 slice_bitcast_fusion.4
  241.2 0.7 slice.98
  242.3 1.6 collective-permute-done.21
  244.0 0.7 copy_bitcast_fusion
  244.9 1.7 gather_fusion.1
  (109 shorter events, 6.7 us)
Async XLA Ops:
  0.6 9.2 %copy-start = (bf16[32,128,128]{2,1,0:T(8,128)(2,1)S(1)}, bf16[32,128,128]{2,1,0:T(8,128)(2,1)}, u32[]{:S(2)}) copy-start(bf16[32,128,128]{2,1,0:T(8,128)(2,1)} %param.11) | copy-start | bytes 3145732
  0.6 9.0 %copy-start.13 = (f32[16]{0:T(128)S(1)}, f32[16]{0:T(128)}, u32[]{:S(2)}) copy-start(f32[16]{0:T(128)} %param.19) | copy-start | bytes 196
  0.7 9.0 %copy-start.14 = (f32[16]{0:T(128)S(1)}, f32[16]{0:T(128)}, u32[]{:S(2)}) copy-start(f32[16]{0:T(128)} %param.20) | copy-start | bytes 196
  0.7 9.1 %copy-start.17 = (s32[32]{0:T(128)S(1)}, s32[32]{0:T(128)}, u32[]{:S(2)}) copy-start(s32[32]{0:T(128)} %param.14) | copy-start | bytes 388
  2.4 19.0 %all-to-all-start = ((bf16[8,64,384]{2,1,0:T(8,128)(2,1)}), bf16[8,64,384]{2,1,0:T(8,128)(2,1)S(1)}, u32[]{:S(2)}, u32[]{:S(2)}) async-start(bf16[8,64,384]{2,1,0:T(8,128)(2,1)} %broadcast_in_dim.30), calls=%async_computation | async-start | bytes 786432 | tf_op jit(solution)/shard_map/all_to_all | solution.py:579
  11.7 13.3 %copy-start.10 = (bf16[512,64]{0,1:T(8,128)(2,1)S(1)}, bf16[512,64]{0,1:T(8,128)(2,1)}, u32[]{:S(2)}) copy-start(bf16[512,64]{0,1:T(8,128)(2,1)} %param.18) | copy-start | bytes 196612
  11.7 13.3 %copy-start.11 = (bf16[64,512]{1,0:T(8,128)(2,1)S(1)}, bf16[64,512]{1,0:T(8,128)(2,1)}, u32[]{:S(2)}) copy-start(bf16[64,512]{1,0:T(8,128)(2,1)} %param.17) | copy-start | bytes 196612
  11.7 13.3 %copy-start.12 = (bf16[128,64]{0,1:T(8,128)(2,1)S(1)}, bf16[128,64]{0,1:T(8,128)(2,1)}, u32[]{:S(2)}) copy-start(bf16[128,64]{0,1:T(8,128)(2,1)} %param.16) | copy-start | bytes 49156
  21.3 50.1 %copy-start.9 = (bf16[8,64,384]{2,1,0:T(8,128)(2,1)}, bf16[8,64,384]{2,1,0:T(8,128)(2,1)S(1)}, u32[]{:S(2)}) copy-start(bf16[8,64,384]{2,1,0:T(8,128)(2,1)S(1)} %all-to-all-done) | copy-start | bytes 1179652
  21.3 57.8 %all-to-all-start.1 = ((bf16[32,136,128]{2,1,0:T(8,128)(2,1)}), bf16[32,136,128]{2,1,0:T(8,128)(2,1)S(1)}, u32[]{:S(2)}, u32[]{:S(2)}) async-start(bf16[32,136,128]{2,1,0:T(8,128)(2,1)} %pad_maximum_fusion), calls=%async_computation.1 | async-start | bytes 2228224 | tf_op jit(solution)/shard_map/all_to_all | solution.py:680
  25.0 44.0 %copy-start.18 = (s32[32]{0:T(128)S(1)}, s32[32]{0:T(128)}, u32[]{:S(2)}) copy-start(s32[32]{0:T(128)} %param.12) | copy-start | bytes 388
  25.0 45.2 %copy-start.19 = (s32[32]{0:T(128)S(1)}, s32[32]{0:T(128)}, u32[]{:S(2)}) copy-start(s32[32]{0:T(128)} %param.13) | copy-start | bytes 388
  25.1 26.2 %collective-permute-start.3 = (bf16[64,1152]{1,0:T(8,128)(2,1)S(1)}, bf16[64,1152]{1,0:T(8,128)(2,1)S(1)}, u32[]{:S(2)}, u32[]{:S(2)}) collective-permute-start(bf16[64,1152]{1,0:T(8,128)(2,1)S(1)} %pad_maximum_fusion.2), channel_id=1, source_target_pairs={{0,8},{4,12},{8,16},{12,20},{16,24},{20,28},{24,0},{28,4},{1,9},{5... | collective-permute-start | bytes 442376 | tf_op jit(solution)/shard_map/ppermute | solution.py:550
  26.9 35.7 %collective-permute-start.4 = (bf16[64,1152]{1,0:T(8,128)(2,1)S(1)}, bf16[64,1152]{1,0:T(8,128)(2,1)S(1)}, u32[]{:S(2)}, u32[]{:S(2)}) collective-permute-start(bf16[64,1152]{1,0:T(8,128)(2,1)S(1)} %pad_maximum_fusion.2), channel_id=1, source_target_pairs={{0,16},{4,20},{8,24},{12,28},{16,0},{20,4},{24,8},{28,12},{1,17},{... | collective-permute-start | bytes 442376 | tf_op jit(solution)/shard_map/ppermute | solution.py:550
  29.3 33.3 %collective-permute-start.5 = (bf16[64,1152]{1,0:T(8,128)(2,1)S(1)}, bf16[64,1152]{1,0:T(8,128)(2,1)S(1)}, u32[]{:S(2)}, u32[]{:S(2)}) collective-permute-start(bf16[64,1152]{1,0:T(8,128)(2,1)S(1)} %pad_maximum_fusion.2), channel_id=1, source_target_pairs={{0,24},{4,28},{8,0},{12,4},{16,8},{20,12},{24,16},{28,20},{1,25},{... | collective-permute-start | bytes 442376 | tf_op jit(solution)/shard_map/ppermute | solution.py:550
  30.7 31.9 %collective-permute-start.1 = (bf16[512,384]{1,0:T(8,128)(2,1)S(1)}, bf16[512,384]{1,0:T(8,128)(2,1)S(1)}, u32[]{:S(2)}, u32[]{:S(2)}) collective-permute-start(bf16[512,384]{1,0:T(8,128)(2,1)S(1)} %bitcast.137), channel_id=1, source_target_pairs={{0,2},{1,3},{2,0},{3,1},{4,6},{5,7},{6,4},{7,5},{8,10},{9,11},{10,... | collective-permute-start | bytes 1179656 | tf_op jit(solution)/shard_map/ppermute | solution.py:545
  62.6 25.9 %copy-start.8 = (bf16[256,1152]{1,0:T(8,128)(2,1)}, bf16[256,1152]{1,0:T(8,128)(2,1)S(1)}, u32[]{:S(2)}) copy-start(bf16[256,1152]{1,0:T(8,128)(2,1)S(1)} %pad_maximum_fusion.1.refs_0_) | copy-start | bytes 1769476
  62.6 0.8 copy-start.16
  63.4 14.5 %collective-permute-start.7 = (bf16[256,1152]{1,0:T(8,128)(2,1)S(1)}, bf16[256,1152]{1,0:T(8,128)(2,1)}, u32[]{:S(2)}, u32[]{:S(2)}) collective-permute-start(bf16[256,1152]{1,0:T(8,128)(2,1)S(1)} %pad_maximum_fusion.1.refs_0_), channel_id=1, source_target_pairs={{0,4},{4,0},{8,12},{12,8},{16,20},{20,16},{24,28},{28,24},{1,5},{5... | collective-permute-start | bytes 1769480 | tf_op jit(solution)/shard_map/ppermute | solution.py:550
  64.9 14.2 %collective-permute-start.9 = (bf16[256,1152]{1,0:T(8,128)(2,1)S(1)}, bf16[256,1152]{1,0:T(8,128)(2,1)}, u32[]{:S(2)}, u32[]{:S(2)}) collective-permute-start(bf16[256,1152]{1,0:T(8,128)(2,1)S(1)} %pad_maximum_fusion.1.refs_0_), channel_id=1, source_target_pairs={{0,2},{1,3},{2,0},{3,1},{4,6},{5,7},{6,4},{7,5},{8,10},{9,11},{10,... | collective-permute-start | bytes 1769480 | tf_op jit(solution)/shard_map/ppermute | solution.py:545
  71.4 8.7 %collective-permute-start = (bf16[512,384]{1,0:T(8,128)(2,1)S(1)}, bf16[512,384]{1,0:T(8,128)(2,1)}, u32[]{:S(2)}, u32[]{:S(2)}) collective-permute-start(bf16[512,384]{1,0:T(8,128)(2,1)S(1)} %bitcast.138), channel_id=1, source_target_pairs={{0,1},{1,0},{2,3},{3,2},{4,5},{5,4},{6,7},{7,6},{8,9},{9,8},{10,11... | collective-permute-start | bytes 1179656 | tf_op jit(solution)/shard_map/ppermute | solution.py:545
  71.4 17.1 %collective-permute-start.6 = (bf16[256,1152]{1,0:T(8,128)(2,1)S(1)}, bf16[256,1152]{1,0:T(8,128)(2,1)}, u32[]{:S(2)}, u32[]{:S(2)}) collective-permute-start(bf16[256,1152]{1,0:T(8,128)(2,1)S(1)} %pad_maximum_fusion.1.refs_0_), channel_id=1, source_target_pairs={{0,1},{1,0},{2,3},{3,2},{4,5},{5,4},{6,7},{7,6},{8,9},{9,8},{10,11... | collective-permute-start | bytes 1769480 | tf_op jit(solution)/shard_map/ppermute | solution.py:545
  72.0 9.6 %collective-permute-start.2 = (bf16[512,384]{1,0:T(8,128)(2,1)}, bf16[512,384]{1,0:T(8,128)(2,1)}, u32[]{:S(2)}, u32[]{:S(2)}) collective-permute-start(bf16[512,384]{1,0:T(8,128)(2,1)} %copy-done.16), channel_id=1, source_target_pairs={{0,1},{1,0},{2,3},{3,2},{4,5},{5,4},{6,7},{7,6},{8,9},{9,8},{10,11... | collective-permute-start | bytes 1179656 | tf_op jit(solution)/shard_map/ppermute | solution.py:545
  78.0 10.6 %collective-permute-start.8 = (bf16[256,1152]{1,0:T(8,128)(2,1)}, bf16[256,1152]{1,0:T(8,128)(2,1)}, u32[]{:S(2)}, u32[]{:S(2)}) collective-permute-start(bf16[256,1152]{1,0:T(8,128)(2,1)} %collective-permute-done.7.refs_1_), channel_id=1, source_target_pairs={{0,1},{1,0},{2,3},{3,2},{4,5},{5,4},{6,7},{7,6},{8,9},{9,8},{10,11... | collective-permute-start | bytes 1769480 | tf_op jit(solution)/shard_map/ppermute | solution.py:545
  79.1 9.4 %collective-permute-start.10 = (bf16[256,1152]{1,0:T(8,128)(2,1)}, bf16[256,1152]{1,0:T(8,128)(2,1)}, u32[]{:S(2)}, u32[]{:S(2)}) collective-permute-start(bf16[256,1152]{1,0:T(8,128)(2,1)} %collective-permute-done.9.refs_4_), channel_id=1, source_target_pairs={{0,1},{1,0},{2,3},{3,2},{4,5},{5,4},{6,7},{7,6},{8,9},{9,8},{10,11... | collective-permute-start | bytes 1769480 | tf_op jit(solution)/shard_map/ppermute | solution.py:545
  79.2 2.4 copy-start.2
  80.1 23.7 %collective-permute-start.11 = (bf16[256,1152]{1,0:T(8,128)(2,1)}, bf16[256,1152]{1,0:T(8,128)(2,1)}, u32[]{:S(2)}, u32[]{:S(2)}) collective-permute-start(bf16[256,1152]{1,0:T(8,128)(2,1)} %collective-permute-done.7.refs_1_), channel_id=1, source_target_pairs={{0,2},{1,3},{2,0},{3,1},{4,6},{5,7},{6,4},{7,5},{8,10},{9,11},{10,... | collective-permute-start | bytes 1769480 | tf_op jit(solution)/shard_map/ppermute | solution.py:545
  103.8 2.8 %collective-permute-start.12 = (bf16[256,1152]{1,0:T(8,128)(2,1)}, bf16[256,1152]{1,0:T(8,128)(2,1)S(1)}, u32[]{:S(2)}, u32[]{:S(2)}) collective-permute-start(bf16[256,1152]{1,0:T(8,128)(2,1)} %collective-permute-done.11.refs_5_), channel_id=1, source_target_pairs={{0,1},{1,0},{2,3},{3,2},{4,5},{5,4},{6,7},{7,6},{8,9},{9,8},{10,11... | collective-permute-start | bytes 1769480 | tf_op jit(solution)/shard_map/ppermute | solution.py:545
  106.5 0.8 copy-start.15
  134.4 6.4 %collective-permute-start.13 = (bf16[2,512,512]{2,1,0:T(8,128)(2,1)}, bf16[2,512,512]{2,1,0:T(8,128)(2,1)S(1)}, u32[]{:S(2)}, u32[]{:S(2)}) collective-permute-start(bf16[2,512,512]{2,1,0:T(8,128)(2,1)} %get-tuple-element.44), channel_id=1, source_target_pairs={{0,1},{1,0},{2,3},{3,2},{4,5},{5,4},{6,7},{7,6},{8,9},{9,8},{10,11... | collective-permute-start | bytes 3145736 | tf_op jit(solution)/shard_map/ppermute | solution.py:545
  139.0 20.9 %collective-permute-start.15 = (bf16[2,512,640]{2,1,0:T(8,128)(2,1)}, bf16[2,512,640]{2,1,0:T(8,128)(2,1)S(1)}, u32[]{:S(2)}, u32[]{:S(2)}) collective-permute-start(bf16[2,512,640]{2,1,0:T(8,128)(2,1)} %get-tuple-element.46), channel_id=1, source_target_pairs={{0,1},{1,0},{2,3},{3,2},{4,5},{5,4},{6,7},{7,6},{8,9},{9,8},{10,11... | collective-permute-start | bytes 3932168 | tf_op jit(solution)/shard_map/ppermute | solution.py:545
  142.8 18.1 %collective-permute-start.14 = (bf16[2,4,64,512]{3,2,1,0:T(8,128)(2,1)}, bf16[2,4,64,512]{3,2,1,0:T(8,128)(2,1)S(1)}, u32[]{:S(2)}, u32[]{:S(2)}) collective-permute-start(bf16[2,4,64,512]{3,2,1,0:T(8,128)(2,1)} %fusion.4), channel_id=1, source_target_pairs={{0,4},{4,0},{8,12},{12,8},{16,20},{20,16},{24,28},{28,24},{1,5},{5... | collective-permute-start | bytes 1572872 | tf_op jit(solution)/shard_map/ppermute | solution.py:550
  143.7 16.2 %copy-start.1 = (bf16[2,512,640]{2,1,0:T(8,128)(2,1)S(1)}, bf16[2,512,640]{2,1,0:T(8,128)(2,1)}, u32[]{:S(2)}) copy-start(bf16[2,512,640]{2,1,0:T(8,128)(2,1)} %get-tuple-element.45) | copy-start | bytes 3932164
  159.9 32.2 %collective-permute-start.17 = (bf16[2,512,384]{2,1,0:T(8,128)(2,1)}, bf16[2,512,384]{2,1,0:T(8,128)(2,1)S(1)}, u32[]{:S(2)}, u32[]{:S(2)}) collective-permute-start(bf16[2,512,384]{2,1,0:T(8,128)(2,1)} %get-tuple-element.56), channel_id=1, source_target_pairs={{0,1},{1,0},{2,3},{3,2},{4,5},{5,4},{6,7},{7,6},{8,9},{9,8},{10,11... | collective-permute-start | bytes 2359304 | tf_op jit(solution)/shard_map/ppermute | solution.py:545
  160.2 1.2 copy-start.3
  160.3 29.3 %collective-permute-start.16 = (bf16[4,2,64,640]{3,2,0,1:T(8,128)(2,1)S(1)}, bf16[4,2,64,640]{3,2,0,1:T(8,128)(2,1)S(1)}, u32[]{:S(2)}, u32[]{:S(2)}) collective-permute-start(bf16[4,2,64,640]{3,2,0,1:T(8,128)(2,1)S(1)} %copy.94), channel_id=1, source_target_pairs={{0,2},{1,3},{2,0},{3,1},{4,6},{5,7},{6,4},{7,5},{8,10},{9,11},{10,... | collective-permute-start | bytes 1966088 | tf_op jit(solution)/shard_map/ppermute | solution.py:545
  161.6 21.4 %collective-permute-start.27 = (bf16[4,64,512]{2,1,0:T(8,128)(2,1)S(1)}, bf16[4,64,512]{2,1,0:T(8,128)(2,1)S(1)}, u32[]{:S(2)}, u32[]{:S(2)}) collective-permute-start(bf16[4,64,512]{2,1,0:T(8,128)(2,1)S(1)} %slice_bitcast_fusion.1), channel_id=1, source_target_pairs={{0,2},{1,3},{2,0},{3,1},{4,6},{5,7},{6,4},{7,5},{8,10},{9,11},{10,... | collective-permute-start | bytes 786440 | tf_op jit(solution)/shard_map/ppermute | solution.py:545
  183.8 20.7 %collective-permute-start.28 = (bf16[64,512]{1,0:T(8,128)(2,1)}, bf16[64,512]{1,0:T(8,128)(2,1)S(1)}, u32[]{:S(2)}, u32[]{:S(2)}) collective-permute-start(bf16[64,512]{1,0:T(8,128)(2,1)} %get-tuple-element.127), channel_id=1, source_target_pairs={{0,8},{4,12},{8,16},{12,20},{16,24},{20,28},{24,0},{28,4},{1,9},{5... | collective-permute-start | bytes 196616 | tf_op jit(solution)/shard_map/ppermute | solution.py:550
  187.2 17.4 %collective-permute-start.29 = (bf16[64,512]{1,0:T(8,128)(2,1)}, bf16[64,512]{1,0:T(8,128)(2,1)}, u32[]{:S(2)}, u32[]{:S(2)}) collective-permute-start(bf16[64,512]{1,0:T(8,128)(2,1)} %get-tuple-element.129), channel_id=1, source_target_pairs={{0,16},{4,20},{8,24},{12,28},{16,0},{20,4},{24,8},{28,12},{1,17},{... | collective-permute-start | bytes 196616 | tf_op jit(solution)/shard_map/ppermute | solution.py:550
  188.6 15.9 %collective-permute-start.30 = (bf16[64,512]{1,0:T(8,128)(2,1)}, bf16[64,512]{1,0:T(8,128)(2,1)}, u32[]{:S(2)}, u32[]{:S(2)}) collective-permute-start(bf16[64,512]{1,0:T(8,128)(2,1)} %get-tuple-element.128), channel_id=1, source_target_pairs={{0,24},{4,28},{8,0},{12,4},{16,8},{20,12},{24,16},{28,20},{1,25},{... | collective-permute-start | bytes 196616 | tf_op jit(solution)/shard_map/ppermute | solution.py:550
  189.6 2.5 %copy-start.6 = (bf16[2,512,384]{2,1,0:T(8,128)(2,1)S(1)}, bf16[2,512,384]{2,1,0:T(8,128)(2,1)}, u32[]{:S(2)}) copy-start(bf16[2,512,384]{2,1,0:T(8,128)(2,1)} %get-tuple-element.55) | copy-start | bytes 2359300
  190.5 15.6 %collective-permute-start.23 = (bf16[4,64,640]{2,1,0:T(8,128)(2,1)}, bf16[4,64,640]{2,1,0:T(8,128)(2,1)}, u32[]{:S(2)}, u32[]{:S(2)}) collective-permute-start(bf16[4,64,640]{2,1,0:T(8,128)(2,1)} %dynamic-slice_bitcast_fusion), channel_id=1, source_target_pairs={{0,4},{4,0},{8,12},{12,8},{16,20},{20,16},{24,28},{28,24},{1,5},{5... | collective-permute-start | bytes 983048 | tf_op jit(solution)/shard_map/ppermute | solution.py:550
  192.1 7.3 %copy-start.4 = (bf16[2,512,384]{2,1,0:T(8,128)(2,1)}, bf16[2,512,384]{2,1,0:T(8,128)(2,1)S(1)}, u32[]{:S(2)}) copy-start(bf16[2,512,384]{2,1,0:T(8,128)(2,1)S(1)} %collective-permute-done.17) | copy-start | bytes 2359300
  199.4 45.2 %all-to-all-start.2 = ((bf16[32,136,128]{2,1,0:T(8,128)(2,1)}), bf16[32,136,128]{2,1,0:T(8,128)(2,1)S(1)}, u32[]{:S(2)}, u32[]{:S(2)}) async-start(bf16[32,136,128]{2,1,0:T(8,128)(2,1)} %bitcast.128), calls=%async_computation.2 | async-start | bytes 2228224 | tf_op jit(solution)/shard_map/all_to_all | solution.py:729
  202.7 21.3 %copy-start.5 = (bf16[2,512,384]{2,1,0:T(8,128)(2,1)S(1)}, bf16[2,512,384]{2,1,0:T(8,128)(2,1)}, u32[]{:S(2)}) copy-start(bf16[2,512,384]{2,1,0:T(8,128)(2,1)} %copy-done.4) | copy-start | bytes 2359300
  202.7 21.3 %copy-start.7 = (bf16[2,512,384]{2,1,0:T(8,128)(2,1)S(1)}, bf16[2,512,384]{2,1,0:T(8,128)(2,1)}, u32[]{:S(2)}) copy-start(bf16[2,512,384]{2,1,0:T(8,128)(2,1)} %get-tuple-element.55) | copy-start | bytes 2359300
  202.7 21.3 %collective-permute-start.18 = (bf16[2,4,64,384]{3,2,1,0:T(8,128)(2,1)S(1)}, bf16[2,4,64,384]{3,2,1,0:T(8,128)(2,1)S(1)}, u32[]{:S(2)}, u32[]{:S(2)}) collective-permute-start(bf16[2,4,64,384]{3,2,1,0:T(8,128)(2,1)S(1)} %fusion.6), channel_id=1, source_target_pairs={{0,4},{4,0},{8,12},{12,8},{16,20},{20,16},{24,28},{28,24},{1,5},{5... | collective-permute-start | bytes 1179656 | tf_op jit(solution)/shard_map/ppermute | solution.py:550
  207.3 20.3 %collective-permute-start.24 = (bf16[64,640]{1,0:T(8,128)(2,1)S(1)}, bf16[64,640]{1,0:T(8,128)(2,1)S(1)}, u32[]{:S(2)}, u32[]{:S(2)}) collective-permute-start(bf16[64,640]{1,0:T(8,128)(2,1)S(1)} %get-tuple-element.124), channel_id=1, source_target_pairs={{0,8},{4,12},{8,16},{12,20},{16,24},{20,28},{24,0},{28,4},{1,9},{5... | collective-permute-start | bytes 245768 | tf_op jit(solution)/shard_map/ppermute | solution.py:550
  208.8 27.3 %collective-permute-start.25 = (bf16[64,640]{1,0:T(8,128)(2,1)S(1)}, bf16[64,640]{1,0:T(8,128)(2,1)S(1)}, u32[]{:S(2)}, u32[]{:S(2)}) collective-permute-start(bf16[64,640]{1,0:T(8,128)(2,1)S(1)} %get-tuple-element.126), channel_id=1, source_target_pairs={{0,16},{4,20},{8,24},{12,28},{16,0},{20,4},{24,8},{28,12},{1,17},{... | collective-permute-start | bytes 245768 | tf_op jit(solution)/shard_map/ppermute | solution.py:550
  211.2 24.8 %collective-permute-start.26 = (bf16[64,640]{1,0:T(8,128)(2,1)S(1)}, bf16[64,640]{1,0:T(8,128)(2,1)S(1)}, u32[]{:S(2)}, u32[]{:S(2)}) collective-permute-start(bf16[64,640]{1,0:T(8,128)(2,1)S(1)} %get-tuple-element.125), channel_id=1, source_target_pairs={{0,24},{4,28},{8,0},{12,4},{16,8},{20,12},{24,16},{28,20},{1,25},{... | collective-permute-start | bytes 245768 | tf_op jit(solution)/shard_map/ppermute | solution.py:550
  224.2 11.9 %collective-permute-start.19 = (bf16[4,64,384]{2,1,0:T(8,128)(2,1)S(1)}, bf16[4,64,384]{2,1,0:T(8,128)(2,1)S(1)}, u32[]{:S(2)}, u32[]{:S(2)}) collective-permute-start(bf16[4,64,384]{2,1,0:T(8,128)(2,1)S(1)} %slice_bitcast_fusion.2), channel_id=1, source_target_pairs={{0,2},{1,3},{2,0},{3,1},{4,6},{5,7},{6,4},{7,5},{8,10},{9,11},{10,... | collective-permute-start | bytes 589832 | tf_op jit(solution)/shard_map/ppermute | solution.py:545
  236.2 6.1 %collective-permute-start.20 = (bf16[64,384]{1,0:T(8,128)(2,1)S(1)}, bf16[64,384]{1,0:T(8,128)(2,1)S(1)}, u32[]{:S(2)}, u32[]{:S(2)}) collective-permute-start(bf16[64,384]{1,0:T(8,128)(2,1)S(1)} %get-tuple-element.130), channel_id=1, source_target_pairs={{0,8},{4,12},{8,16},{12,20},{16,24},{20,28},{24,0},{28,4},{1,9},{5... | collective-permute-start | bytes 147464 | tf_op jit(solution)/shard_map/ppermute | solution.py:550
  238.1 5.8 %collective-permute-start.21 = (bf16[64,384]{1,0:T(8,128)(2,1)S(1)}, bf16[64,384]{1,0:T(8,128)(2,1)S(1)}, u32[]{:S(2)}, u32[]{:S(2)}) collective-permute-start(bf16[64,384]{1,0:T(8,128)(2,1)S(1)} %get-tuple-element.132), channel_id=1, source_target_pairs={{0,16},{4,20},{8,24},{12,28},{16,0},{20,4},{24,8},{28,12},{1,17},{... | collective-permute-start | bytes 147464 | tf_op jit(solution)/shard_map/ppermute | solution.py:550
  239.4 4.6 %collective-permute-start.22 = (bf16[64,384]{1,0:T(8,128)(2,1)S(1)}, bf16[64,384]{1,0:T(8,128)(2,1)S(1)}, u32[]{:S(2)}, u32[]{:S(2)}) collective-permute-start(bf16[64,384]{1,0:T(8,128)(2,1)S(1)} %get-tuple-element.131), channel_id=1, source_target_pairs={{0,24},{4,28},{8,0},{12,4},{16,8},{20,12},{24,16},{28,20},{1,25},{... | collective-permute-start | bytes 147464 | tf_op jit(solution)/shard_map/ppermute | solution.py:550

commit v2 on v1

--- a/solution.py
+++ b/solution.py
@@ -35,6 +35,18 @@
     ).astype(F32)
 
 
+def place_rows(groups, place_ref, first, source, targets):
+    if groups is None:
+        for target, columns, own in targets:
+            target[:, columns] = source[:, own]
+        return
+    rows = source.shape[0] // groups
+    for group in range(groups):
+        spot = pl.ds(pl.multiple_of(place_ref[first + group] * rows, rows), rows)
+        for target, columns, own in targets:
+            target[spot, columns] = source[group * rows : (group + 1) * rows, own]
+
+
 def norm_parts(values):
     center = values - jnp.mean(values, axis=-1, keepdims=True)
     spread = jnp.mean(center * center, axis=-1, keepdims=True)
@@ -59,7 +71,7 @@
     return pltpu.CompilerParams(vmem_limit_bytes=VMEM_LIMIT, **kwargs)
 
 
-def project_kernel(limit_ref, x_ref, clock_ref, gain_ref, *refs):
+def project_kernel(groups, limit_ref, place_ref, x_ref, clock_ref, gain_ref, *refs):
     w_refs, (mixed_ref, n_turn_ref, wide) = refs[:-3], refs[-3:]
     step = pl.program_id(0)
 
@@ -68,7 +80,7 @@
         for part, w_ref in enumerate(w_refs):
             width = w_ref.shape[1]
             columns = slice(part * width, (part + 1) * width)
-            wide[:, columns] = w_ref[...]
+            place_rows(groups, place_ref, 0, w_ref, [(wide, columns, slice(0, width))])
 
     @pl.when(step * ROWS < limit_ref[0])
     def _():
@@ -84,7 +96,7 @@
         mixed_ref[...] = jnp.zeros_like(mixed_ref)
 
 
-def project(limit, x_blocks, clock, gain, w_parts):
+def project(limit, place, groups, x_blocks, clock, gain, w_parts):
     senders, feature_parts, tall, width = x_blocks.shape
     tokens = tall - SPARE
     length = senders * tokens
@@ -92,9 +104,9 @@
     parts, columns = len(w_parts), w_parts[0].shape[1]
     take = ROWS // tokens
     return pl.pallas_call(
-        project_kernel,
+        functools.partial(project_kernel, groups),
         grid_spec=pltpu.PrefetchScalarGridSpec(
-            num_scalar_prefetch=1,
+            num_scalar_prefetch=2,
             grid=(length // ROWS,),
             in_specs=[
                 pl.BlockSpec((take, feature_parts, tall, width), lambda i, *s: (i, 0, 0, 0)),
@@ -116,7 +128,7 @@
         compiler_params=params(),
         cost_estimate=cost(5),
         name="project",
-    )(limit, x_blocks, clock, gain, *w_parts)
+    )(limit, place, x_blocks, clock, gain, *w_parts)
 
 
 def head_lanes(shape, head):
@@ -237,18 +249,11 @@
             thin = slice(part * PAIR, (part + 1) * PAIR)
             thick = slice(part * 2 * hidden, (part + 1) * 2 * hidden)
             for at, w_ref in enumerate(weight_refs[part * each : (part + 1) * each]):
-                if groups is None:
-                    wide[:, thin] = w_ref[:, 0:PAIR]
-                    units[:, thick] = w_ref[:, PAIR:]
-                    continue
-                count = groups // each
-                rows = w_ref.shape[0] // count
-                for group in range(count):
-                    spot = place_ref[at * count + group] * rows
-                    spot = pl.ds(pl.multiple_of(spot, rows), rows)
-                    source = w_ref[group * rows : (group + 1) * rows]
-                    wide[spot, thin] = source[:, 0:PAIR]
-                    units[spot, thick] = source[:, PAIR:]
+                targets = [
+                    (wide, thin, slice(0, PAIR)), (units, thick, slice(PAIR, PAIR + 2 * hidden))
+                ]
+                count = None if groups is None else groups // each
+                place_rows(count, place_ref, at * (count or 0), w_ref, targets)
 
     dead = (step < blocks) & (step * ROWS >= limit_ref[0])
 
@@ -383,7 +388,7 @@
 
 def attend_back_kernel(
     limit_ref, q_ref, k_ref, v_ref, turn_ref, lse_ref, cg_ref, n_turn_ref,
-    dm_ref, wg_ref, keys_s, q_s, qz_s, do_s, kt_s, delta_s,
+    dm_ref, first_ref, second_ref, keys_s, q_s, qz_s, do_s, kt_s, delta_s,
 ):
     limit = limit_ref[0]
     length = q_ref.shape[0]
@@ -415,13 +420,21 @@
         dm_ref[span, 2 * PAIR : 3 * PAIR] = value_grad.astype(BF16)
     query_grad = jnp.concatenate(turned, axis=0) * SCORE_SCALE
     dm_ref[:, 0:PAIR] = query_grad.T.astype(BF16)
-    wg_ref[0] = mul(n_turn_ref[...], dm_ref[...]).astype(BF16)
+    grad = mul(n_turn_ref[...], dm_ref[...]).astype(BF16)
+
+    @pl.when(pl.program_id(0) == 0)
+    def _():
+        first_ref[...] = grad
+
+    @pl.when(pl.program_id(0) == 1)
+    def _():
+        second_ref[...] = grad
 
 
 def attend_back(limit, mixed, ctx_turn, lse, context_grad, n_turn, first):
     length = mixed.shape[0]
     features = n_turn.shape[0]
-    pair = lambda i: first - 2 * i
+    pair = lambda i: first - i
     column = lambda c: pl.BlockSpec((length, PAIR), lambda i, s: (0, pair(i) * 3 + c))
     return pl.pallas_call(
         attend_back_kernel,
@@ -437,7 +450,8 @@
             ],
             out_specs=[
                 pl.BlockSpec((length, 3 * PAIR), lambda i, s: (0, i)),
-                pl.BlockSpec((1, features, 3 * PAIR), lambda i, s: (i, 0, 0)),
+                pl.BlockSpec((features, 3 * PAIR), lambda i, s: (0, 0)),
+                pl.BlockSpec((features, 3 * PAIR), lambda i, s: (0, 0)),
             ],
             scratch_shapes=[
                 pltpu.VMEM((2, length, PAIR), BF16),
@@ -450,7 +464,8 @@
         ),
         out_shape=[
             jax.ShapeDtypeStruct((length, 2 * 3 * PAIR), BF16),
-            jax.ShapeDtypeStruct((2, features, 3 * PAIR), BF16),
+            jax.ShapeDtypeStruct((features, 3 * PAIR), BF16),
+            jax.ShapeDtypeStruct((features, 3 * PAIR), BF16),
         ],
         compiler_params=params(),
         cost_estimate=cost(16),
@@ -459,7 +474,7 @@
 
 
 def begin_kernel(
-    limit_ref, x_ref, clock_ref, gain_ref, gg_two_ref, mg_ref, w_ref, odd_ref, even_ref, bg_ref, gg_s
+    limit_ref, x_ref, clock_ref, gain_ref, gg_two_ref, mg_ref, w_ref, high_ref, low_ref, bg_ref, gg_s
 ):
     step = pl.program_id(0)
     _, parts, tall, width = bg_ref.shape
@@ -476,7 +491,7 @@
         begin = join_tokens(x_ref) + clock_ref[...]
         unit, inverse = norm_parts(begin)
         one_grad = jnp.zeros_like(begin)
-        for part, (d_ref, at) in enumerate(((even_ref, 1), (odd_ref, 1), (even_ref, 0), (odd_ref, 0))):
+        for part, (d_ref, at) in enumerate(((low_ref, 1), (low_ref, 0), (high_ref, 1), (high_ref, 0))):
             columns = slice(part * 3 * PAIR, (part + 1) * 3 * PAIR)
             own = slice(at * 3 * PAIR, (at + 1) * 3 * PAIR)
             one_grad += mul(d_ref[:, own], w_ref[:, columns], NT)
@@ -501,7 +516,7 @@
         )
 
 
-def begin_block(limit, x_blocks, clock, gain, two_grad, w_wide, middle_grad, odd, even):
+def begin_block(limit, x_blocks, clock, gain, two_grad, w_wide, middle_grad, high, low):
     senders, feature_parts, tall, width = x_blocks.shape
     tokens = tall - SPARE
     length = senders * tokens
@@ -526,7 +541,7 @@
         compiler_params=params(),
         cost_estimate=cost(7),
         name="begin_back",
-    )(limit, x_blocks, clock, gain, two_grad, middle_grad, w_wide, odd, even)
+    )(limit, x_blocks, clock, gain, two_grad, middle_grad, w_wide, high, low)
 
 
 DIRECT = 8
@@ -566,12 +581,9 @@
     return jnp.concatenate([coarse * 2 + own % 2, coarse * 2 + 1 - own % 2])
 
 
-def collect_pieces(shard, gate):
+def collect_coarse(shard):
     count = lax.axis_size("dp") // 2
-    mine = jnp.concatenate([shard] + [ahead(shard, step) for step in range(1, count)], axis=0)
-    mine = after(mine, gate)
-    other = across(mine)
-    return mine, other, swap(mine, 2), swap(other, 2)
+    return jnp.concatenate([shard] + [ahead(shard, step) for step in range(1, count)], axis=0)
 
 
 def collect_rows(shard):
@@ -611,10 +623,16 @@
     own = lax.axis_index("dp") // 2
     pick = lambda value, which: lax.dynamic_index_in_dim(value, which % count, 0, keepdims=False)
     value = add(*values)
-    total = pick(value, own).astype(F32)
-    for step in range(1, count):
-        total += ahead(pick(value, own + step), step).astype(F32)
-    return total
+    came = [ahead(pick(value, own + step), step) for step in range(1, count)]
+
+    def finish(*others):
+        pieces = lax.optimization_barrier((*came, *others))[: count - 1]
+        total = pick(value, own).astype(F32)
+        for piece in pieces:
+            total += piece.astype(F32)
+        return total
+
+    return value, finish
 
 
 def grouped(value):
@@ -661,15 +679,20 @@
     hidden = w_up.shape[1]
 
     rest = jnp.concatenate([w_out.T, w_up, w_down.T], axis=1)
-    qkv_rows = collect_rows(w_qkv.reshape(rows, -1))
-    qkv_parts = collect_columns(qkv_rows)
-
+    qkv = w_qkv.reshape(rows, -1)
     direct = dp_count <= DIRECT
     if direct:
         place, groups = places(), dp_count
-        pieces = collect_pieces(rest, qkv_parts[2])
+        first = collect_coarse(jnp.concatenate([qkv, rest], axis=1))
+        qkv_rows = first[:, : qkv.shape[1]]
+        qkv_parts = collect_columns(jnp.concatenate([qkv_rows, across(qkv_rows)], axis=0))
+        mine = after(first[:, qkv.shape[1] :], qkv_parts[2])
+        other = across(mine)
+        far_mine, far_other = swap(mine, 2), swap(other, 2)
     else:
         place, groups = jnp.zeros((1,), jnp.int32), None
+        first = collect_rows(qkv)
+        qkv_parts = collect_columns(first)
         rest_parts = [(part,) for part in collect_columns(collect_rows(rest))]
 
     spare = jnp.stack(three_terms(gain_attn) + three_terms(gain_ffn)).reshape(1, 6 * per)
@@ -677,15 +700,16 @@
     arranged = jnp.concatenate(
         [states[deal_order], jnp.broadcast_to(spare[None], (devices, SPARE, width))], axis=1
     )
-    x_blocks = lax.all_to_all(after(arranged, qkv_rows), both, 0, 0, tiled=True)
+    x_blocks = lax.all_to_all(after(arranged, first), both, 0, 0, tiled=True)
     gains = jnp.sum(x_blocks[:, tokens, : 6 * per].reshape(devices, 2, 3, per).astype(F32), axis=2)
     gain_one = gains[:, 0].reshape(1, features)
     gain_two = gains[:, 1].reshape(1, features)
     x_blocks = x_blocks.reshape(dp_count, tensor_count, tokens + SPARE, width)
 
-    mixed, n_one_turn, qkv_wide = project(limit, x_blocks, clock, gain_one, qkv_parts)
+    mixed, n_one_turn, qkv_wide = project(
+        limit, place, groups, x_blocks, clock, gain_one, qkv_parts
+    )
     if direct:
-        mine, other, far_mine, far_other = pieces
         near_mine, near_other, last_mine = swap(mine, 1), swap(other, 1), swap(far_mine, 1)
         mixed = after(mixed, near_mine, near_other, last_mine)
     ctx, ctx_turn, lse = attend(limit, mixed, tensor_count)
@@ -701,31 +725,36 @@
 
     back = functools.partial(attend_back, limit, mixed, ctx_turn, lse)
     context_grad = after(context_grad, up_send, down_send)
-    odd, qkv_send = back(context_grad, n_one_turn, 3)
-    qkv_came = swap(qkv_send, 1)
+    high, three, two = back(context_grad, n_one_turn, 3)
+    came_three = swap(three, 1)
+    far = add(two, came_three)
+    came_far = swap(far, 2)
+    context_grad = after(context_grad, high, far)
     if direct:
         down_sent, down_rest = fold_pair([grouped(value) for value in (down_keep, down_came)])
         up_sent, up_rest = fold_far([grouped(value) for value in (up_keep, up_came)])
-        even, qkv_keep = back(after(context_grad, odd, down_sent, up_sent), n_one_turn, 2)
-        down_value, up_value = add(*down_rest()), add(*up_rest())
-        down_sent, down_rest = fold_far([down_value])
-        up_sent, up_rest = fold_pair([up_value])
-        qkv_keep = after(qkv_keep, down_value, up_value)
-        qkv_sent, qkv_rest = fold_pair([grouped(value) for value in (qkv_keep, qkv_came)])
-        middle_grad = after(middle_grad, down_sent, up_sent, qkv_sent)
-        down_total = fold_coarse(down_rest())
-        up_total = fold_coarse(up_rest())
-        qkv_sent, qkv_rest = fold_far([add(*qkv_rest())])
-        qkv_total = fold_coarse(qkv_rest())
+        context_grad = after(context_grad, down_sent, up_sent)
+    low, one, own_part = back(context_grad, n_one_turn, 1)
+    came_one = swap(one, 1)
+    if direct:
+        down_sent, down_rest = fold_far([add(*[after(value, low) for value in down_rest()])])
+        up_sent, up_rest = fold_pair([add(*[after(value, low) for value in up_rest()])])
+        middle_grad = after(middle_grad, down_sent, up_sent, came_far)
+    begin_grad = begin_block(
+        limit, x_blocks, clock, gain_one, two_grad, qkv_wide, middle_grad, high, low
+    )
+    near = (own_part, came_one, came_far)
+    if direct:
+        down_value, down_finish = fold_coarse(down_rest())
+        up_value, up_finish = fold_coarse(up_rest())
+        begin_grad = after(begin_grad, down_value, up_value)
+        near = [grouped(after(value, up_value)[None])[0] for value in near]
+        qkv_value, qkv_finish = fold_coarse(fold_pair(near)[1]())
+        down_total, up_total, qkv_total = down_finish(qkv_value), up_finish(qkv_value), qkv_finish()
     else:
-        even, qkv_keep = back(after(context_grad, odd), n_one_turn, 2)
-        totals = []
-        for pair in ((up_keep, up_came), (down_keep, down_came), (qkv_keep, qkv_came)):
-            totals.append(exchange_rows(add(*fold_far(pair)[1]())))
-        up_total, down_total, qkv_total = totals
-    begin_grad = begin_block(
-        limit, x_blocks, clock, gain_one, two_grad, qkv_wide, middle_grad, odd, even
-    )
+        up_total = exchange_rows(add(*fold_far([up_keep, up_came])[1]()))
+        down_total = exchange_rows(add(*fold_far([down_keep, down_came])[1]()))
+        qkv_total = exchange_rows(add(*near))
     returned = lax.all_to_all(
         begin_grad.reshape(devices, tokens + SPARE, width), both, 0, 0, tiled=True
     )

time: 248 us -> 268 us (1.081)
  waiting for transfers between devices: 77.2 us -> 88.5 us
  Pallas kernels: 88.3 us -> 94.9 us
  other arithmetic: 8.89 us -> 13.1 us
    ppermute x15 -> x16, waiting for transfers between devices: 7.89 us -> 40.3 us  [swap(): return lax.ppermute(value, 'tensor', [(i, i ^ apart) for i in range(count)])]
    ppermute x16 -> x17, waiting for transfers between devices: 59.8 us -> 48.2 us  [along_dp(): return lax.ppermute(value, 'dp', [(i, move(i)) for i in range(count)])]
    all_to_all x2 -> x1, waiting for transfers between devices: 9.58 us -> 0.01 us  [on_device(): x_blocks = lax.all_to_all(after(arranged, first), both, 0, 0, tiled=True)]
    ppermute x16 -> x17, starting transfers between devices: 26.9 us -> 32.3 us  [along_dp(): return lax.ppermute(value, 'dp', [(i, move(i)) for i in range(count)])]
    pallas_call x1, Pallas kernels: 27 us -> 30.5 us  [middle_block(): pl.pallas_call(functools.partial(middle_kernel, groups), grid_spec=pltpu....]
    ppermute x15 -> x16, starting transfers between devices: 13.6 us -> 10.4 us  [swap(): return lax.ppermute(value, 'tensor', [(i, i ^ apart) for i in range(count)])]
    all_to_all x2 -> x1, starting transfers between devices: 10.9 us -> 7.97 us  [on_device(): x_blocks = lax.all_to_all(after(arranged, first), both, 0, 0, tiled=True)]
  transfers between devices with their start and end apart: 34 -> 35, of which waited for: 13 -> 15; matrix products, arithmetic and copies ran while one was open for 7% -> 7% of each run, Pallas kernels for 25% -> 24%
where the time goes in v2:
time: 268 us
  Pallas kernels  94.9 us (35%)
  waiting for transfers between devices  88.5 us (33%)
  starting transfers between devices  55.4 us (21%)
  other arithmetic  13.1 us (5%)
  local copies, waits for them, and re-layouts  11.9 us (4%)
  between operations  3.74 us (1%)
    ppermute x17, waiting for transfers between devices, along_dp(): return lax.ppermute(value, 'dp', [(i, move(i)) for i in range(count)])  48.2 us
    ppermute x16, waiting for transfers between devices, swap(): return lax.ppermute(value, 'tensor', [(i, i ^ apart) for i in range(count)])  40.3 us
    pallas_call x2, Pallas kernels, attend_back(): pl.pallas_call(attend_back_kernel, grid_spec=pltpu.PrefetchScalarGridSpec...  33 us
    ppermute x17, starting transfers between devices, along_dp(): return lax.ppermute(value, 'dp', [(i, move(i)) for i in range(count)])  32.3 us
    pallas_call x1, Pallas kernels, middle_block(): pl.pallas_call(functools.partial(middle_kernel, groups), grid_spec=pltpu....  30.5 us
    pallas_call x1, Pallas kernels, attend(): pl.pallas_call(attend_kernel, grid_spec=pltpu.PrefetchScalarGridSpec(num_...  15.2 us
    ppermute x16, starting transfers between devices, swap(): return lax.ppermute(value, 'tensor', [(i, i ^ apart) for i in range(count)])  10.4 us
    pallas_call x1, Pallas kernels, project(): pl.pallas_call(functools.partial(project_kernel, groups), grid_spec=pltpu...  8.21 us
  transfers between devices with their start and end apart: 35, of which 15 were waited for; matrix products, arithmetic and copies ran while one was open for 7% of the time, Pallas kernels for 24%

profile of v2, /device:TPU:0, one launch (start us, length us, event | category | flops | bytes accessed | tf_op | source)
XLA Modules:
  0.0 267.6 jit_solution(17966963035144061565)
XLA Ops:
  0.6 0.9 copy_bitcast_fusion.1
  1.5 0.9 pad_maximum_fusion.3
  2.4 3.1 %collective-permute-start = (bf16[64,1536]{1,0:T(8,128)(2,1)S(1)}, bf16[64,1536]{1,0:T(8,128)(2,1)S(1)}, u32[]{:S(2)}, u32[]{:S(2)}) collective-permute-start(bf16[64,1536]{1,0:T(8,128)(2,1)S(1)} %pad_maximum_fusion.3), channel_id=1, source_target_pairs={{0,8},{4,12},{8,16},{12,20},{16,24},{20,28},{24,0},{28,4},{1,9},{5... | collective-permute-start | bytes 589832 | tf_op jit(solution)/shard_map/ppermute | solution.py:565
  5.5 2.6 collective-permute-start.1
  8.1 1.3 collective-permute-start.2
  9.4 0.7 compare_select_fusion.1
  10.1 0.7 fusion.17
  10.9 0.7 gather_fusion
  11.7 1.1 pad_maximum_fusion
  13.4 7.6 %collective-permute-done.1 = bf16[64,1536]{1,0:T(8,128)(2,1)S(1)} collective-permute-done((bf16[64,1536]{1,0:T(8,128)(2,1)S(1)}, bf16[64,1536]{1,0:T(8,128)(2,1)S(1)}, u32[]{:S(2)}, u32[]{:S(2)}) %collective-permute-start.1) | collective-permute-done | bytes 196640 | tf_op jit(solution)/shard_map/ppermute | solution.py:565
  21.0 1.0 pad_maximum_fusion.1
  22.0 8.0 %all-to-all-start = ((bf16[32,136,128]{2,1,0:T(8,128)(2,1)}), bf16[32,136,128]{2,1,0:T(8,128)(2,1)S(1)}, u32[]{:S(2)}, u32[]{:S(2)}) async-start(bf16[32,136,128]{2,1,0:T(8,128)(2,1)} %pad_maximum_fusion), calls=%async_computation | async-start | bytes 2228224 | tf_op jit(solution)/shard_map/all_to_all | solution.py:703
  30.0 1.8 collective-permute-start.3
  31.9 13.6 %collective-permute-done.3 = bf16[256,384]{1,0:T(8,128)(2,1)S(1)} collective-permute-done((bf16[256,384]{1,0:T(8,128)(2,1)S(1)}, bf16[256,384]{1,0:T(8,128)(2,1)S(1)}, u32[]{:S(2)}, u32[]{:S(2)}) %collective-permute-start.3) | collective-permute-done | bytes 196640 | tf_op jit(solution)/shard_map/ppermute | solution.py:565
  45.5 2.1 collective-permute-start.5
  47.6 11.0 %collective-permute-done.5.refs_2_ = bf16[512,384]{1,0:T(8,128)(2,1)S(1)} collective-permute-done((bf16[512,384]{1,0:T(8,128)(2,1)S(1)}, bf16[512,384]{1,0:T(8,128)(2,1)S(1)}, u32[]{:S(2)}, u32[]{:S(2)}) %collective-permute-start.5) | collective-permute-done | bytes 393248 | tf_op jit(solution)/shard_map/ppermute | solution.py:560
  58.7 0.7 collective-permute-start.8
  59.5 1.6 collective-permute-start.10
  64.8 0.6 dynamic-slice.4.limit_ref
  67.2 6.5 %collective-permute-done.8.refs_1_ = bf16[256,1152]{1,0:T(8,128)(2,1)S(1)} collective-permute-done((bf16[256,1152]{1,0:T(8,128)(2,1)S(1)}, bf16[256,1152]{1,0:T(8,128)(2,1)S(1)}, u32[]{:S(2)}, u32[]{:S(2)}) %collective-permute-start.8) | collective-permute-done | bytes 589856 | tf_op jit(solution)/shard_map/ppermute | solution.py:565
  73.7 0.9 collective-permute-done.10.refs_4_
  74.8 0.7 reshape_squeeze.8.gain_ref
  75.5 1.1 collective-permute-start.12
  76.6 8.2 %project.1 = (bf16[1024,1536]{1,0:T(8,128)(2,1)}, bf16[512,1024]{1,0:T(8,128)(2,1)}, bf16[512,1536]{1,0:T(8,128)(2,1)}) custom-call(s32[1]{0:T(128)} %dynamic-slice.4.limit_ref, s32[8]{0:T(128)} %pad_add_fusion.place_ref, bf16[8,4,136,128]{3,2,1,0:T(8,128)(2,1)} %bitcast.120, f32[1,512]{1,0:T(1,128)} %pad_maximum_fusion.4.clock_ref, ...), custom_call_target="tpu_custom_call" | custom-call | flops 5750000128 | bytes 1048576 | tf_op jit(solution)/shard_map/project/pallas_call | solution.py:106
  84.9 15.2 %attend.1 = (bf16[1024,512]{1,0:T(8,128)(2,1)}, bf16[512,1024]{1,0:T(8,128)(2,1)}, f32[4,2,1024]{2,1,0:T(2,128)}) custom-call(s32[1]{0:T(128)} %dynamic-slice.4.limit_ref, bf16[1024,1536]{1,0:T(8,128)(2,1)} %get-tuple-element.58.q_ref.k_ref.v_ref, bf16[1024,1536]{1,0:T(8,128)(2,1)} %get-tuple-element.58.q_ref.k_ref.v_ref, ...), custom_call_target="tpu_custom_call" | custom-call | flops 17250000896 | bytes 1048576 | tf_op jit(solution)/shard_map/attend/pallas_call | solution.py:195
  100.3 0.7 reshape_squeeze.7.gain_ref
  100.9 1.5 collective-permute-done.13.refs_7_
  102.4 0.8 copy-done.12
  103.2 30.5 %middle.1 = (bf16[1,1024,512]{2,1,0:T(8,128)(2,1)}, bf16[1024,512]{1,0:T(8,128)(2,1)}, f32[1024,512]{1,0:T(8,128)}, f32[1,512]{1,0:T(1,128)}, bf16[2,512,640]{2,...) custom-call(s32[1]{0:T(128)} %dynamic-slice.4.limit_ref, ...), custom_call_target="tpu_custom_call" | custom-call | flops 28750000128 | bytes 1048576 | tf_op jit(solution)/shard_map/middle/pallas_call | solution.py:345
  134.2 16.6 %attend_back.2 = (bf16[1024,768]{1,0:T(8,128)(2,1)}, bf16[512,384]{1,0:T(8,128)(2,1)}, bf16[512,384]{1,0:T(8,128)(2,1)}) custom-call(s32[1]{0:T(128)} %dynamic-slice.4.limit_ref, bf16[1024,1536]{1,0:T(8,128)(2,1)} %get-tuple-element.58.q_ref.k_ref.v_ref, bf16[1024,1536]{1,0:T(8,128)(2,1)} %get-tuple-element.58.q_ref.k_ref.v_ref, ...), custom_call_target="tpu_custom_call" | custom-call | flops 18400000000 | bytes 1048576 | tf_op jit(solution)/shard_map/attend_back/pallas_call | solution.py:439
  151.1 1.9 collective-permute-done.14
  153.0 2.0 add_convert_fusion.4
  155.0 1.3 fusion.1
  156.3 1.1 dynamic-slice_bitcast_fusion
  157.6 16.4 %attend_back.3 = (bf16[1024,768]{1,0:T(8,128)(2,1)}, bf16[512,384]{1,0:T(8,128)(2,1)}, bf16[512,384]{1,0:T(8,128)(2,1)}) custom-call(s32[1]{0:T(128)} %dynamic-slice.4.limit_ref, bf16[1024,1536]{1,0:T(8,128)(2,1)} %get-tuple-element.58.q_ref.k_ref.v_ref, bf16[1024,1536]{1,0:T(8,128)(2,1)} %get-tuple-element.58.q_ref.k_ref.v_ref, ...), custom_call_target="tpu_custom_call" | custom-call | flops 18400000000 | bytes 1048576 | tf_op jit(solution)/shard_map/attend_back/pallas_call | solution.py:439
  174.1 1.9 collective-permute-start.18
  176.6 1.9 collective-permute-start.19
  178.6 18.8 %collective-permute-done.20 = bf16[4,64,512]{2,1,0:T(8,128)(2,1)S(1)} collective-permute-done((bf16[4,64,512]{2,1,0:T(8,128)(2,1)S(1)}, bf16[4,64,512]{2,1,0:T(8,128)(2,1)S(1)}, u32[]{:S(2)}, u32[]{:S(2)}) %collective-permute-start.20) | collective-permute-done | bytes 262176 | tf_op jit(solution)/shard_map/ppermute | solution.py:560
  197.7 2.1 collective-permute-start.21
  199.8 5.1 %collective-permute-done.19 = bf16[512,384]{1,0:T(8,128)(2,1)S(1)} collective-permute-done((bf16[512,384]{1,0:T(8,128)(2,1)S(1)}, bf16[512,384]{1,0:T(8,128)(2,1)S(1)}, u32[]{:S(2)}, u32[]{:S(2)}) %collective-permute-start.19) | collective-permute-done | bytes 393248 | tf_op jit(solution)/shard_map/ppermute | solution.py:560
  205.0 8.0 %begin_back.1 = bf16[8,4,136,128]{3,2,1,0:T(8,128)(2,1)} custom-call(s32[1]{0:T(128)} %dynamic-slice.4.limit_ref, bf16[8,4,136,128]{3,2,1,0:T(8,128)(2,1)} %bitcast.122, f32[1,512]{1,0:T(1,128)} %pad_maximum_fusion.4.clock_ref, f32[1,512]{1,0:T(1,128)} %reshape_squeeze.8.gain_ref, f32[1,512]{1,0:T(1,128)} %get-tuple-element.62.gg_two_ref, ...), custom_call_target="tpu_custom_call" | custom-call | flops 8049999872 | bytes 1048576 | tf_op jit(solution)/shard_map/begin_back/pallas_call | solution.py:527
  213.1 4.6 %all-to-all-start.1 = ((bf16[32,136,128]{2,1,0:T(8,128)(2,1)}), bf16[32,136,128]{2,1,0:T(8,128)(2,1)S(1)}, u32[]{:S(2)}, u32[]{:S(2)}) async-start(bf16[32,136,128]{2,1,0:T(8,128)(2,1)} %bitcast.123), calls=%async_computation.1 | async-start | bytes 2228224 | tf_op jit(solution)/shard_map/all_to_all | solution.py:758
  218.0 0.7 scatter_custom_fusion
  218.8 1.1 collective-permute-done.22
  219.8 1.0 fusion.4
  220.8 1.8 collective-permute-start.23
  222.7 1.5 collective-permute-start.30
  224.2 2.4 collective-permute-start.31
  226.7 1.4 collective-permute-start.32
  228.1 0.7 collective-permute-start.27
  228.8 13.4 %collective-permute-done.30 = bf16[64,512]{1,0:T(8,128)(2,1)S(1)} collective-permute-done((bf16[64,512]{1,0:T(8,128)(2,1)S(1)}, bf16[64,512]{1,0:T(8,128)(2,1)S(1)}, u32[]{:S(2)}, u32[]{:S(2)}) %collective-permute-start.30) | collective-permute-done | bytes 65568 | tf_op jit(solution)/shard_map/ppermute | solution.py:565
  242.2 7.9 %collective-permute-start.28 = (bf16[64,640]{1,0:T(8,128)(2,1)S(1)}, bf16[64,640]{1,0:T(8,128)(2,1)S(1)}, u32[]{:S(2)}, u32[]{:S(2)}) collective-permute-start(bf16[64,640]{1,0:T(8,128)(2,1)S(1)} %get-tuple-element.165), channel_id=1, source_target_pairs={{0,16},{4,20},{8,24},{12,28},{16,0},{20,4},{24,8},{28,12},{1,17},{... | collective-permute-start | bytes 245768 | tf_op jit(solution)/shard_map/ppermute | solution.py:565
  250.6 1.0 fusion.3
  251.6 1.6 collective-permute-done.31
  253.2 3.5 %collective-permute-done.28 = bf16[64,640]{1,0:T(8,128)(2,1)S(1)} collective-permute-done((bf16[64,640]{1,0:T(8,128)(2,1)S(1)}, bf16[64,640]{1,0:T(8,128)(2,1)S(1)}, u32[]{:S(2)}, u32[]{:S(2)}) %collective-permute-start.28) | collective-permute-done | bytes 81952 | tf_op jit(solution)/shard_map/ppermute | solution.py:565
  256.7 1.9 collective-permute-start.24
  258.6 1.3 collective-permute-start.25
  259.9 1.1 collective-permute-start.26
  261.1 0.7 fusion.9
  261.8 0.6 slice_bitcast_fusion.2
  262.4 0.7 slice.99
  263.1 1.4 collective-permute-done.25
  264.5 0.7 copy_bitcast_fusion
  265.4 1.7 gather_fusion.1
  (110 shorter events, 7.9 us)
Async XLA Ops:
  0.6 10.3 %copy-start = (bf16[32,128,128]{2,1,0:T(8,128)(2,1)S(1)}, bf16[32,128,128]{2,1,0:T(8,128)(2,1)}, u32[]{:S(2)}) copy-start(bf16[32,128,128]{2,1,0:T(8,128)(2,1)} %param.11) | copy-start | bytes 3145732
  2.4 11.0 %collective-permute-start = (bf16[64,1536]{1,0:T(8,128)(2,1)S(1)}, bf16[64,1536]{1,0:T(8,128)(2,1)S(1)}, u32[]{:S(2)}, u32[]{:S(2)}) collective-permute-start(bf16[64,1536]{1,0:T(8,128)(2,1)S(1)} %pad_maximum_fusion.3), channel_id=1, source_target_pairs={{0,8},{4,12},{8,16},{12,20},{16,24},{20,28},{24,0},{28,4},{1,9},{5... | collective-permute-start | bytes 589832 | tf_op jit(solution)/shard_map/ppermute | solution.py:565
  5.5 15.5 %collective-permute-start.1 = (bf16[64,1536]{1,0:T(8,128)(2,1)S(1)}, bf16[64,1536]{1,0:T(8,128)(2,1)S(1)}, u32[]{:S(2)}, u32[]{:S(2)}) collective-permute-start(bf16[64,1536]{1,0:T(8,128)(2,1)S(1)} %pad_maximum_fusion.3), channel_id=1, source_target_pairs={{0,16},{4,20},{8,24},{12,28},{16,0},{20,4},{24,8},{28,12},{1,17},{... | collective-permute-start | bytes 589832 | tf_op jit(solution)/shard_map/ppermute | solution.py:565
  8.1 12.9 %collective-permute-start.2 = (bf16[64,1536]{1,0:T(8,128)(2,1)S(1)}, bf16[64,1536]{1,0:T(8,128)(2,1)}, u32[]{:S(2)}, u32[]{:S(2)}) collective-permute-start(bf16[64,1536]{1,0:T(8,128)(2,1)S(1)} %pad_maximum_fusion.3), channel_id=1, source_target_pairs={{0,24},{4,28},{8,0},{12,4},{16,8},{20,12},{24,16},{28,20},{1,25},{... | collective-permute-start | bytes 589832 | tf_op jit(solution)/shard_map/ppermute | solution.py:565
  11.7 9.3 %copy-start.8 = (bf16[512,64]{0,1:T(8,128)(2,1)S(1)}, bf16[512,64]{0,1:T(8,128)(2,1)}, u32[]{:S(2)}) copy-start(bf16[512,64]{0,1:T(8,128)(2,1)} %param.18) | copy-start | bytes 196612
  11.7 9.3 %copy-start.9 = (bf16[64,512]{1,0:T(8,128)(2,1)S(1)}, bf16[64,512]{1,0:T(8,128)(2,1)}, u32[]{:S(2)}) copy-start(bf16[64,512]{1,0:T(8,128)(2,1)} %param.17) | copy-start | bytes 196612
  11.7 9.3 %copy-start.10 = (bf16[128,64]{0,1:T(8,128)(2,1)S(1)}, bf16[128,64]{0,1:T(8,128)(2,1)}, u32[]{:S(2)}) copy-start(bf16[128,64]{0,1:T(8,128)(2,1)} %param.16) | copy-start | bytes 49156
  22.0 52.5 %all-to-all-start = ((bf16[32,136,128]{2,1,0:T(8,128)(2,1)}), bf16[32,136,128]{2,1,0:T(8,128)(2,1)S(1)}, u32[]{:S(2)}, u32[]{:S(2)}) async-start(bf16[32,136,128]{2,1,0:T(8,128)(2,1)} %pad_maximum_fusion), calls=%async_computation | async-start | bytes 2228224 | tf_op jit(solution)/shard_map/all_to_all | solution.py:703
  30.0 31.0 %copy-start.14 = (s32[32]{0:T(128)S(1)}, s32[32]{0:T(128)}, u32[]{:S(2)}) copy-start(s32[32]{0:T(128)} %param.14) | copy-start | bytes 388
  30.0 33.6 %copy-start.15 = (s32[32]{0:T(128)S(1)}, s32[32]{0:T(128)}, u32[]{:S(2)}) copy-start(s32[32]{0:T(128)} %param.12) | copy-start | bytes 388
  30.0 34.8 %copy-start.16 = (s32[32]{0:T(128)S(1)}, s32[32]{0:T(128)}, u32[]{:S(2)}) copy-start(s32[32]{0:T(128)} %param.13) | copy-start | bytes 388
  30.0 15.4 %collective-permute-start.3 = (bf16[256,384]{1,0:T(8,128)(2,1)S(1)}, bf16[256,384]{1,0:T(8,128)(2,1)S(1)}, u32[]{:S(2)}, u32[]{:S(2)}) collective-permute-start(bf16[256,384]{1,0:T(8,128)(2,1)S(1)} %slice.91), channel_id=1, source_target_pairs={{0,4},{4,0},{8,12},{12,8},{16,20},{20,16},{24,28},{28,24},{1,5},{5... | collective-permute-start | bytes 589832 | tf_op jit(solution)/shard_map/ppermute | solution.py:565
  45.5 13.2 %copy-start.6 = (bf16[512,384]{1,0:T(8,128)(2,1)}, bf16[512,384]{1,0:T(8,128)(2,1)S(1)}, u32[]{:S(2)}) copy-start(bf16[512,384]{1,0:T(8,128)(2,1)S(1)} %pad_maximum_fusion.2.refs_0_) | copy-start | bytes 1179652
  45.5 13.2 %collective-permute-start.5 = (bf16[512,384]{1,0:T(8,128)(2,1)S(1)}, bf16[512,384]{1,0:T(8,128)(2,1)S(1)}, u32[]{:S(2)}, u32[]{:S(2)}) collective-permute-start(bf16[512,384]{1,0:T(8,128)(2,1)S(1)} %pad_maximum_fusion.2.refs_0_), channel_id=1, source_target_pairs={{0,2},{1,3},{2,0},{3,1},{4,6},{5,7},{6,4},{7,5},{8,10},{9,11},{10,... | collective-permute-start | bytes 1179656 | tf_op jit(solution)/shard_map/ppermute | solution.py:560
  47.6 37.2 %copy-start.4 = (bf16[256,1152]{1,0:T(8,128)(2,1)}, bf16[256,1152]{1,0:T(8,128)(2,1)S(1)}, u32[]{:S(2)}) copy-start(bf16[256,1152]{1,0:T(8,128)(2,1)S(1)} %slice.92.refs_0_) | copy-start | bytes 1769476
  58.7 0.8 copy-start.13
  58.7 15.0 %collective-permute-start.8 = (bf16[256,1152]{1,0:T(8,128)(2,1)S(1)}, bf16[256,1152]{1,0:T(8,128)(2,1)S(1)}, u32[]{:S(2)}, u32[]{:S(2)}) collective-permute-start(bf16[256,1152]{1,0:T(8,128)(2,1)S(1)} %slice.92.refs_0_), channel_id=1, source_target_pairs={{0,4},{4,0},{8,12},{12,8},{16,20},{20,16},{24,28},{28,24},{1,5},{5... | collective-permute-start | bytes 1769480 | tf_op jit(solution)/shard_map/ppermute | solution.py:565
  59.5 15.1 %collective-permute-start.10 = (bf16[256,1152]{1,0:T(8,128)(2,1)S(1)}, bf16[256,1152]{1,0:T(8,128)(2,1)}, u32[]{:S(2)}, u32[]{:S(2)}) collective-permute-start(bf16[256,1152]{1,0:T(8,128)(2,1)S(1)} %slice.92.refs_0_), channel_id=1, source_target_pairs={{0,2},{1,3},{2,0},{3,1},{4,6},{5,7},{6,4},{7,5},{8,10},{9,11},{10,... | collective-permute-start | bytes 1769480 | tf_op jit(solution)/shard_map/ppermute | solution.py:560
  66.6 8.8 %collective-permute-start.4 = (bf16[512,384]{1,0:T(8,128)(2,1)}, bf16[512,384]{1,0:T(8,128)(2,1)}, u32[]{:S(2)}, u32[]{:S(2)}) collective-permute-start(bf16[512,384]{1,0:T(8,128)(2,1)} %copy-done.6), channel_id=1, source_target_pairs={{0,1},{1,0},{2,3},{3,2},{4,5},{5,4},{6,7},{7,6},{8,9},{9,8},{10,11... | collective-permute-start | bytes 1179656 | tf_op jit(solution)/shard_map/ppermute | solution.py:560
  66.6 18.2 %collective-permute-start.7 = (bf16[256,1152]{1,0:T(8,128)(2,1)S(1)}, bf16[256,1152]{1,0:T(8,128)(2,1)}, u32[]{:S(2)}, u32[]{:S(2)}) collective-permute-start(bf16[256,1152]{1,0:T(8,128)(2,1)S(1)} %slice.92.refs_0_), channel_id=1, source_target_pairs={{0,1},{1,0},{2,3},{3,2},{4,5},{5,4},{6,7},{7,6},{8,9},{9,8},{10,11... | collective-permute-start | bytes 1769480 | tf_op jit(solution)/shard_map/ppermute | solution.py:560
  67.2 9.4 %collective-permute-start.6 = (bf16[512,384]{1,0:T(8,128)(2,1)}, bf16[512,384]{1,0:T(8,128)(2,1)}, u32[]{:S(2)}, u32[]{:S(2)}) collective-permute-start(bf16[512,384]{1,0:T(8,128)(2,1)} %copy-done.13), channel_id=1, source_target_pairs={{0,1},{1,0},{2,3},{3,2},{4,5},{5,4},{6,7},{7,6},{8,9},{9,8},{10,11... | collective-permute-start | bytes 1179656 | tf_op jit(solution)/shard_map/ppermute | solution.py:560
  73.7 11.2 %copy-start.11 = (bf16[256,1152]{1,0:T(8,128)(2,1)}, bf16[256,1152]{1,0:T(8,128)(2,1)S(1)}, u32[]{:S(2)}) copy-start(bf16[256,1152]{1,0:T(8,128)(2,1)S(1)} %collective-permute-done.8.refs_1_) | copy-start | bytes 1769476
  73.7 11.2 %collective-permute-start.9 = (bf16[256,1152]{1,0:T(8,128)(2,1)S(1)}, bf16[256,1152]{1,0:T(8,128)(2,1)}, u32[]{:S(2)}, u32[]{:S(2)}) collective-permute-start(bf16[256,1152]{1,0:T(8,128)(2,1)S(1)} %collective-permute-done.8.refs_1_), channel_id=1, source_target_pairs={{0,1},{1,0},{2,3},{3,2},{4,5},{5,4},{6,7},{7,6},{8,9},{9,8},{10,11... | collective-permute-start | bytes 1769480 | tf_op jit(solution)/shard_map/ppermute | solution.py:560
  74.5 10.3 %collective-permute-start.11 = (bf16[256,1152]{1,0:T(8,128)(2,1)}, bf16[256,1152]{1,0:T(8,128)(2,1)}, u32[]{:S(2)}, u32[]{:S(2)}) collective-permute-start(bf16[256,1152]{1,0:T(8,128)(2,1)} %collective-permute-done.10.refs_4_), channel_id=1, source_target_pairs={{0,1},{1,0},{2,3},{3,2},{4,5},{5,4},{6,7},{7,6},{8,9},{9,8},{10,11... | collective-permute-start | bytes 1769480 | tf_op jit(solution)/shard_map/ppermute | solution.py:560
  74.5 2.1 copy-start.2
  75.5 24.6 %collective-permute-start.12 = (bf16[256,1152]{1,0:T(8,128)(2,1)S(1)}, bf16[256,1152]{1,0:T(8,128)(2,1)}, u32[]{:S(2)}, u32[]{:S(2)}) collective-permute-start(bf16[256,1152]{1,0:T(8,128)(2,1)S(1)} %collective-permute-done.8.refs_1_), channel_id=1, source_target_pairs={{0,2},{1,3},{2,0},{3,1},{4,6},{5,7},{6,4},{7,5},{8,10},{9,11},{10,... | collective-permute-start | bytes 1769480 | tf_op jit(solution)/shard_map/ppermute | solution.py:560
  100.1 2.3 collective-permute-start.13
  102.4 0.8 copy-start.12
  133.7 23.8 %collective-permute-start.16 = (bf16[2,512,640]{2,1,0:T(8,128)(2,1)}, bf16[2,512,640]{2,1,0:T(8,128)(2,1)S(1)}, u32[]{:S(2)}, u32[]{:S(2)}) collective-permute-start(bf16[2,512,640]{2,1,0:T(8,128)(2,1)} %get-tuple-element.68), channel_id=1, source_target_pairs={{0,1},{1,0},{2,3},{3,2},{4,5},{5,4},{6,7},{7,6},{8,9},{9,8},{10,11... | collective-permute-start | bytes 3932168 | tf_op jit(solution)/shard_map/ppermute | solution.py:560
  133.7 21.2 %collective-permute-start.15 = (bf16[2,512,512]{2,1,0:T(8,128)(2,1)}, bf16[2,512,512]{2,1,0:T(8,128)(2,1)}, u32[]{:S(2)}, u32[]{:S(2)}) collective-permute-start(bf16[2,512,512]{2,1,0:T(8,128)(2,1)} %get-tuple-element.69), channel_id=1, source_target_pairs={{0,1},{1,0},{2,3},{3,2},{4,5},{5,4},{6,7},{7,6},{8,9},{9,8},{10,11... | collective-permute-start | bytes 3145736 | tf_op jit(solution)/shard_map/ppermute | solution.py:560
  134.2 16.8 %copy-start.3 = (bf16[2,512,512]{2,1,0:T(8,128)(2,1)S(1)}, bf16[2,512,512]{2,1,0:T(8,128)(2,1)}, u32[]{:S(2)}) copy-start(bf16[2,512,512]{2,1,0:T(8,128)(2,1)} %get-tuple-element.64) | copy-start | bytes 3145732
  150.9 2.1 collective-permute-start.14
  155.0 2.5 copy-start.1
  156.2 19.8 %collective-permute-start.17 = (bf16[2,4,64,512]{3,2,1,0:T(8,128)(2,1)S(1)}, bf16[2,4,64,512]{3,2,1,0:T(8,128)(2,1)S(1)}, u32[]{:S(2)}, u32[]{:S(2)}) collective-permute-start(bf16[2,4,64,512]{3,2,1,0:T(8,128)(2,1)S(1)} %fusion.1), channel_id=1, source_target_pairs={{0,4},{4,0},{8,12},{12,8},{16,20},{20,16},{24,28},{28,24},{1,5},{5... | collective-permute-start | bytes 1572872 | tf_op jit(solution)/shard_map/ppermute | solution.py:565
  174.1 2.5 copy-start.7
  174.1 23.3 %collective-permute-start.18 = (bf16[4,2,64,640]{3,2,0,1:T(8,128)(2,1)S(1)}, bf16[4,2,64,640]{3,2,0,1:T(8,128)(2,1)S(1)}, u32[]{:S(2)}, u32[]{:S(2)}) collective-permute-start(bf16[4,2,64,640]{3,2,0,1:T(8,128)(2,1)S(1)} %copy.99), channel_id=1, source_target_pairs={{0,2},{1,3},{2,0},{3,1},{4,6},{5,7},{6,4},{7,5},{8,10},{9,11},{10,... | collective-permute-start | bytes 1966088 | tf_op jit(solution)/shard_map/ppermute | solution.py:560
  176.3 21.1 %collective-permute-start.20 = (bf16[4,64,512]{2,1,0:T(8,128)(2,1)S(1)}, bf16[4,64,512]{2,1,0:T(8,128)(2,1)S(1)}, u32[]{:S(2)}, u32[]{:S(2)}) collective-permute-start(bf16[4,64,512]{2,1,0:T(8,128)(2,1)S(1)} %slice_bitcast_fusion.1), channel_id=1, source_target_pairs={{0,2},{1,3},{2,0},{3,1},{4,6},{5,7},{6,4},{7,5},{8,10},{9,11},{10,... | collective-permute-start | bytes 786440 | tf_op jit(solution)/shard_map/ppermute | solution.py:560
  176.6 28.4 %collective-permute-start.19 = (bf16[512,384]{1,0:T(8,128)(2,1)S(1)}, bf16[512,384]{1,0:T(8,128)(2,1)S(1)}, u32[]{:S(2)}, u32[]{:S(2)}) collective-permute-start(bf16[512,384]{1,0:T(8,128)(2,1)S(1)} %copy-done.7), channel_id=1, source_target_pairs={{0,2},{1,3},{2,0},{3,1},{4,6},{5,7},{6,4},{7,5},{8,10},{9,11},{10,... | collective-permute-start | bytes 1179656 | tf_op jit(solution)/shard_map/ppermute | solution.py:560
  197.7 15.2 %collective-permute-start.21 = (bf16[4,64,640]{2,1,0:T(8,128)(2,1)S(1)}, bf16[4,64,640]{2,1,0:T(8,128)(2,1)S(1)}, u32[]{:S(2)}, u32[]{:S(2)}) collective-permute-start(bf16[4,64,640]{2,1,0:T(8,128)(2,1)S(1)} %dynamic-slice_bitcast_fusion.2), channel_id=1, source_target_pairs={{0,4},{4,0},{8,12},{12,8},{16,20},{20,16},{24,28},{28,24},{1,5},{5... | collective-permute-start | bytes 983048 | tf_op jit(solution)/shard_map/ppermute | solution.py:565
  213.0 6.9 %copy-start.5 = (bf16[512,384]{1,0:T(8,128)(2,1)S(1)}, bf16[512,384]{1,0:T(8,128)(2,1)}, u32[]{:S(2)}) copy-start(bf16[512,384]{1,0:T(8,128)(2,1)} %get-tuple-element.89) | copy-start | bytes 1179652
  213.1 52.1 %all-to-all-start.1 = ((bf16[32,136,128]{2,1,0:T(8,128)(2,1)}), bf16[32,136,128]{2,1,0:T(8,128)(2,1)S(1)}, u32[]{:S(2)}, u32[]{:S(2)}) async-start(bf16[32,136,128]{2,1,0:T(8,128)(2,1)} %bitcast.123), calls=%async_computation.1 | async-start | bytes 2228224 | tf_op jit(solution)/shard_map/all_to_all | solution.py:758
  217.7 2.1 collective-permute-start.22
  220.8 29.3 %collective-permute-start.23 = (bf16[4,64,384]{2,1,0:T(8,128)(2,1)S(1)}, bf16[4,64,384]{2,1,0:T(8,128)(2,1)S(1)}, u32[]{:S(2)}, u32[]{:S(2)}) collective-permute-start(bf16[4,64,384]{2,1,0:T(8,128)(2,1)S(1)} %fusion.4), channel_id=1, source_target_pairs={{0,4},{4,0},{8,12},{12,8},{16,20},{20,16},{24,28},{28,24},{1,5},{5... | collective-permute-start | bytes 589832 | tf_op jit(solution)/shard_map/ppermute | solution.py:565
  222.7 19.5 %collective-permute-start.30 = (bf16[64,512]{1,0:T(8,128)(2,1)S(1)}, bf16[64,512]{1,0:T(8,128)(2,1)S(1)}, u32[]{:S(2)}, u32[]{:S(2)}) collective-permute-start(bf16[64,512]{1,0:T(8,128)(2,1)S(1)} %get-tuple-element.169), channel_id=1, source_target_pairs={{0,8},{4,12},{8,16},{12,20},{16,24},{20,28},{24,0},{28,4},{1,9},{5... | collective-permute-start | bytes 196616 | tf_op jit(solution)/shard_map/ppermute | solution.py:565
  224.2 29.0 %collective-permute-start.31 = (bf16[64,512]{1,0:T(8,128)(2,1)S(1)}, bf16[64,512]{1,0:T(8,128)(2,1)S(1)}, u32[]{:S(2)}, u32[]{:S(2)}) collective-permute-start(bf16[64,512]{1,0:T(8,128)(2,1)S(1)} %get-tuple-element.168), channel_id=1, source_target_pairs={{0,16},{4,20},{8,24},{12,28},{16,0},{20,4},{24,8},{28,12},{1,17},{... | collective-permute-start | bytes 196616 | tf_op jit(solution)/shard_map/ppermute | solution.py:565
  226.7 26.6 %collective-permute-start.32 = (bf16[64,512]{1,0:T(8,128)(2,1)S(1)}, bf16[64,512]{1,0:T(8,128)(2,1)S(1)}, u32[]{:S(2)}, u32[]{:S(2)}) collective-permute-start(bf16[64,512]{1,0:T(8,128)(2,1)S(1)} %get-tuple-element.167), channel_id=1, source_target_pairs={{0,24},{4,28},{8,0},{12,4},{16,8},{20,12},{24,16},{28,20},{1,25},{... | collective-permute-start | bytes 196616 | tf_op jit(solution)/shard_map/ppermute | solution.py:565
  228.1 25.2 %collective-permute-start.27 = (bf16[64,640]{1,0:T(8,128)(2,1)S(1)}, bf16[64,640]{1,0:T(8,128)(2,1)S(1)}, u32[]{:S(2)}, u32[]{:S(2)}) collective-permute-start(bf16[64,640]{1,0:T(8,128)(2,1)S(1)} %get-tuple-element.166), channel_id=1, source_target_pairs={{0,8},{4,12},{8,16},{12,20},{16,24},{20,28},{24,0},{28,4},{1,9},{5... | collective-permute-start | bytes 245768 | tf_op jit(solution)/shard_map/ppermute | solution.py:565
  242.2 14.5 %collective-permute-start.28 = (bf16[64,640]{1,0:T(8,128)(2,1)S(1)}, bf16[64,640]{1,0:T(8,128)(2,1)S(1)}, u32[]{:S(2)}, u32[]{:S(2)}) collective-permute-start(bf16[64,640]{1,0:T(8,128)(2,1)S(1)} %get-tuple-element.165), channel_id=1, source_target_pairs={{0,16},{4,20},{8,24},{12,28},{16,0},{20,4},{24,8},{28,12},{1,17},{... | collective-permute-start | bytes 245768 | tf_op jit(solution)/shard_map/ppermute | solution.py:565
  250.1 6.6 %collective-permute-start.29 = (bf16[64,640]{1,0:T(8,128)(2,1)S(1)}, bf16[64,640]{1,0:T(8,128)(2,1)S(1)}, u32[]{:S(2)}, u32[]{:S(2)}) collective-permute-start(bf16[64,640]{1,0:T(8,128)(2,1)S(1)} %get-tuple-element.164), channel_id=1, source_target_pairs={{0,24},{4,28},{8,0},{12,4},{16,8},{20,12},{24,16},{28,20},{1,25},{... | collective-permute-start | bytes 245768 | tf_op jit(solution)/shard_map/ppermute | solution.py:565
  256.7 6.4 %collective-permute-start.24 = (bf16[64,384]{1,0:T(8,128)(2,1)S(1)}, bf16[64,384]{1,0:T(8,128)(2,1)S(1)}, u32[]{:S(2)}, u32[]{:S(2)}) collective-permute-start(bf16[64,384]{1,0:T(8,128)(2,1)S(1)} %get-tuple-element.172), channel_id=1, source_target_pairs={{0,8},{4,12},{8,16},{12,20},{16,24},{20,28},{24,0},{28,4},{1,9},{5... | collective-permute-start | bytes 147464 | tf_op jit(solution)/shard_map/ppermute | solution.py:565
  258.6 5.8 %collective-permute-start.25 = (bf16[64,384]{1,0:T(8,128)(2,1)S(1)}, bf16[64,384]{1,0:T(8,128)(2,1)S(1)}, u32[]{:S(2)}, u32[]{:S(2)}) collective-permute-start(bf16[64,384]{1,0:T(8,128)(2,1)S(1)} %get-tuple-element.171), channel_id=1, source_target_pairs={{0,16},{4,20},{8,24},{12,28},{16,0},{20,4},{24,8},{28,12},{1,17},{... | collective-permute-start | bytes 147464 | tf_op jit(solution)/shard_map/ppermute | solution.py:565
  259.9 4.6 %collective-permute-start.26 = (bf16[64,384]{1,0:T(8,128)(2,1)S(1)}, bf16[64,384]{1,0:T(8,128)(2,1)S(1)}, u32[]{:S(2)}, u32[]{:S(2)}) collective-permute-start(bf16[64,384]{1,0:T(8,128)(2,1)S(1)} %get-tuple-element.170), channel_id=1, source_target_pairs={{0,24},{4,28},{8,0},{12,4},{16,8},{20,12},{24,16},{28,20},{1,25},{... | collective-permute-start | bytes 147464 | tf_op jit(solution)/shard_map/ppermute | solution.py:565

commit v3 on v2

--- a/solution.py
+++ b/solution.py
@@ -656,6 +656,10 @@
     return terms
 
 
+def together(*values):
+    return lax.optimization_barrier(values)
+
+
 def after(value, *others):
     return lax.optimization_barrier((value,) + others)[0]
 
@@ -687,8 +691,7 @@
         qkv_rows = first[:, : qkv.shape[1]]
         qkv_parts = collect_columns(jnp.concatenate([qkv_rows, across(qkv_rows)], axis=0))
         mine = after(first[:, qkv.shape[1] :], qkv_parts[2])
-        other = across(mine)
-        far_mine, far_other = swap(mine, 2), swap(other, 2)
+        other, far_mine = across(mine), swap(mine, 2)
     else:
         place, groups = jnp.zeros((1,), jnp.int32), None
         first = collect_rows(qkv)
@@ -697,10 +700,14 @@
 
     spare = jnp.stack(three_terms(gain_attn) + three_terms(gain_ffn)).reshape(1, 6 * per)
     spare = jnp.pad(spare, ((0, SPARE - 1), (0, width - 6 * per)))
+    by_tensor = deal_order.reshape(dp_count, tensor_count).T.reshape(devices)
     arranged = jnp.concatenate(
-        [states[deal_order], jnp.broadcast_to(spare[None], (devices, SPARE, width))], axis=1
-    )
-    x_blocks = lax.all_to_all(after(arranged, first), both, 0, 0, tiled=True)
+        [states[by_tensor], jnp.broadcast_to(spare[None], (devices, SPARE, width))], axis=1
+    )
+    arranged = lax.all_to_all(arranged, "tensor", 0, 0, tiled=True)
+    arranged = arranged.reshape(tensor_count, dp_count, tokens + SPARE, width).swapaxes(0, 1)
+    x_blocks = lax.all_to_all(after(arranged, first), "dp", 0, 0, tiled=True)
+    x_blocks = x_blocks.reshape(devices, tokens + SPARE, width)
     gains = jnp.sum(x_blocks[:, tokens, : 6 * per].reshape(devices, 2, 3, per).astype(F32), axis=2)
     gain_one = gains[:, 0].reshape(1, features)
     gain_two = gains[:, 1].reshape(1, features)
@@ -710,11 +717,15 @@
         limit, place, groups, x_blocks, clock, gain_one, qkv_parts
     )
     if direct:
-        near_mine, near_other, last_mine = swap(mine, 1), swap(other, 1), swap(far_mine, 1)
-        mixed = after(mixed, near_mine, near_other, last_mine)
+        mixed, other, far_mine = together(mixed, other, far_mine)
+        near_mine, near_other = swap(after(mine, mixed), 1), swap(other, 1)
+        last_mine, far_other = swap(far_mine, 1), swap(other, 2)
     ctx, ctx_turn, lse = attend(limit, mixed, tensor_count)
     if direct:
-        last_other = swap(after(far_other, ctx), 1)
+        ctx, near_mine, near_other, last_mine, far_other = together(
+            ctx, near_mine, near_other, last_mine, far_other
+        )
+        last_other = swap(far_other, 1)
         rest_parts = (
             (mine, other), (near_mine, near_other), (far_mine, far_other), (last_mine, last_other)
         )
@@ -724,37 +735,43 @@
     up_came, down_came = swap(up_send, 1), swap(down_send, 1)
 
     back = functools.partial(attend_back, limit, mixed, ctx_turn, lse)
-    context_grad = after(context_grad, up_send, down_send)
-    high, three, two = back(context_grad, n_one_turn, 3)
-    came_three = swap(three, 1)
-    far = add(two, came_three)
-    came_far = swap(far, 2)
-    context_grad = after(context_grad, high, far)
     if direct:
         down_sent, down_rest = fold_pair([grouped(value) for value in (down_keep, down_came)])
         up_sent, up_rest = fold_far([grouped(value) for value in (up_keep, up_came)])
         context_grad = after(context_grad, down_sent, up_sent)
-    low, one, own_part = back(context_grad, n_one_turn, 1)
+    high, three, two = back(context_grad, n_one_turn, 3)
+    if direct:
+        *down_rest, down_came = down_rest()
+        *up_rest, up_came = up_rest()
+        high, three, two, down_came, up_came = together(high, three, two, down_came, up_came)
+        down_sent, down_rest = fold_far([add(*down_rest, down_came)])
+        up_sent, up_rest = fold_pair([add(*up_rest, up_came)])
+        context_grad = after(context_grad, down_sent, up_sent)
+    far = add(two, swap(three, 1))
+    came_far = swap(far, 2)
+    low, one, own_part = back(after(context_grad, high, far), n_one_turn, 1)
+    if direct:
+        *down_rest, down_came = down_rest()
+        *up_rest, up_came = up_rest()
+        low, one, own_part, down_came, up_came, came_far = together(
+            low, one, own_part, down_came, up_came, came_far
+        )
+        down_value, down_finish = fold_coarse([*down_rest, down_came])
+        up_value, up_finish = fold_coarse([*up_rest, up_came])
+        middle_grad = after(middle_grad, down_value, up_value)
     came_one = swap(one, 1)
-    if direct:
-        down_sent, down_rest = fold_far([add(*[after(value, low) for value in down_rest()])])
-        up_sent, up_rest = fold_pair([add(*[after(value, low) for value in up_rest()])])
-        middle_grad = after(middle_grad, down_sent, up_sent, came_far)
     begin_grad = begin_block(
         limit, x_blocks, clock, gain_one, two_grad, qkv_wide, middle_grad, high, low
     )
-    near = (own_part, came_one, came_far)
     if direct:
-        down_value, down_finish = fold_coarse(down_rest())
-        up_value, up_finish = fold_coarse(up_rest())
-        begin_grad = after(begin_grad, down_value, up_value)
-        near = [grouped(after(value, up_value)[None])[0] for value in near]
+        begin_grad, came_one = together(begin_grad, came_one)
+        near = [grouped(value[None])[0] for value in (own_part, came_one, came_far)]
         qkv_value, qkv_finish = fold_coarse(fold_pair(near)[1]())
         down_total, up_total, qkv_total = down_finish(qkv_value), up_finish(qkv_value), qkv_finish()
     else:
         up_total = exchange_rows(add(*fold_far([up_keep, up_came])[1]()))
         down_total = exchange_rows(add(*fold_far([down_keep, down_came])[1]()))
-        qkv_total = exchange_rows(add(*near))
+        qkv_total = exchange_rows(add(own_part, came_one, came_far))
     returned = lax.all_to_all(
         begin_grad.reshape(devices, tokens + SPARE, width), both, 0, 0, tiled=True
     )

time: 268 us -> 244 us (0.910)
  waiting for transfers between devices: 88.5 us -> 59.6 us
  starting transfers between devices: 55.4 us -> 60.1 us
    ppermute x16, waiting for transfers between devices: 40.3 us -> 9.25 us  [swap(): return lax.ppermute(value, 'tensor', [(i, i ^ apart) for i in range(count)])]
    all_to_all x1 -> x2, starting transfers between devices: 7.97 us -> 12.4 us  [the longest x1 8.09 us: on_device(): x_blocks = lax.all_to_all(after(arranged, first), 'dp', 0, 0, tiled=True)]
    convert_element_type x9 -> x8, other arithmetic: 6.06 us -> 3.83 us  [add(): return total.astype(BF16)]
  transfers between devices with their start and end apart: 35 -> 36, of which waited for: 15 -> 12; matrix products, arithmetic and copies ran while one was open for 7% -> 6% of each run, Pallas kernels for 24% -> 27%
where the time goes in v3:
time: 244 us; the launch traced here: 243 us
  Pallas kernels  94.9 us (39%)
  starting transfers between devices  60.1 us (25%)
  waiting for transfers between devices  59.6 us (24%)
  local copies, waits for them, and re-layouts  13.4 us (5%)
  other arithmetic  10.9 us (4%)
  between operations  3.73 us (2%)
    ppermute x17, waiting for transfers between devices, along_dp(): return lax.ppermute(value, 'dp', [(i, move(i)) for i in range(count)])  50.3 us
    ppermute x17, starting transfers between devices, along_dp(): return lax.ppermute(value, 'dp', [(i, move(i)) for i in range(count)])  33.7 us
    pallas_call x2, Pallas kernels, attend_back(): pl.pallas_call(attend_back_kernel, grid_spec=pltpu.PrefetchScalarGridSpec...  33 us
    pallas_call x1, Pallas kernels, middle_block(): pl.pallas_call(functools.partial(middle_kernel, groups), grid_spec=pltpu....  30.5 us
    pallas_call x1, Pallas kernels, attend(): pl.pallas_call(attend_kernel, grid_spec=pltpu.PrefetchScalarGridSpec(num_...  15.2 us
    ppermute x16, waiting for transfers between devices, swap(): return lax.ppermute(value, 'tensor', [(i, i ^ apart) for i in range(count)])  9.25 us
    ppermute x16, starting transfers between devices, swap(): return lax.ppermute(value, 'tensor', [(i, i ^ apart) for i in range(count)])  8.51 us
    pallas_call x1, Pallas kernels, project(): pl.pallas_call(functools.partial(project_kernel, groups), grid_spec=pltpu...  8.21 us
  transfers between devices with their start and end apart: 36, of which 12 were waited for; matrix products, arithmetic and copies ran while one was open for 6% of the time, Pallas kernels for 27%

profile of v3, /device:TPU:0, one launch (start us, length us, event | category | flops | bytes accessed | tf_op | source)
XLA Modules:
  0.0 242.6 jit_solution(1984512082745436525)
XLA Ops:
  0.6 0.8 fusion.19
  1.5 0.7 reshape.155
  2.5 0.7 gather_fusion
  3.3 1.1 pad_maximum_fusion
  4.4 4.4 %all-to-all-start = ((bf16[32,136,128]{2,1,0:T(8,128)(2,1)}), bf16[32,136,128]{2,1,0:T(8,128)(2,1)S(1)}, u32[]{:S(2)}, u32[]{:S(2)}) async-start(bf16[32,136,128]{2,1,0:T(8,128)(2,1)} %pad_maximum_fusion), calls=%async_computation | async-start | bytes 2228224 | tf_op jit(solution)/shard_map/all_to_all | solution.py:707
  8.8 2.4 collective-permute-start
  11.2 2.6 %collective-permute-start.1 = (bf16[64,1536]{1,0:T(8,128)(2,1)S(1)}, bf16[64,1536]{1,0:T(8,128)(2,1)S(1)}, u32[]{:S(2)}, u32[]{:S(2)}) collective-permute-start(bf16[64,1536]{1,0:T(8,128)(2,1)S(1)} %pad_maximum_fusion.3), channel_id=1, source_target_pairs={{0,16},{4,20},{8,24},{12,28},{16,0},{20,4},{24,8},{28,12},{1,17},{... | collective-permute-start | bytes 589832 | tf_op jit(solution)/shard_map/ppermute | solution.py:565
  13.8 1.3 collective-permute-start.2
  15.2 4.0 %collective-permute-done = bf16[64,1536]{1,0:T(8,128)(2,1)S(1)} collective-permute-done((bf16[64,1536]{1,0:T(8,128)(2,1)S(1)}, bf16[64,1536]{1,0:T(8,128)(2,1)S(1)}, u32[]{:S(2)}, u32[]{:S(2)}) %collective-permute-start) | collective-permute-done | bytes 196640 | tf_op jit(solution)/shard_map/ppermute | solution.py:565
  19.2 8.2 %collective-permute-done.1 = bf16[64,1536]{1,0:T(8,128)(2,1)S(1)} collective-permute-done((bf16[64,1536]{1,0:T(8,128)(2,1)S(1)}, bf16[64,1536]{1,0:T(8,128)(2,1)S(1)}, u32[]{:S(2)}, u32[]{:S(2)}) %collective-permute-start.1) | collective-permute-done | bytes 196640 | tf_op jit(solution)/shard_map/ppermute | solution.py:565
  27.4 1.2 copy.85
  28.6 8.1 %all-to-all-start.1 = ((bf16[8,4,136,128]{3,2,1,0:T(8,128)(2,1)}), bf16[8,4,136,128]{3,2,1,0:T(8,128)(2,1)S(1)}, u32[]{:S(2)}, u32[]{:S(2)}) async-start(bf16[8,4,136,128]{3,2,1,0:T(8,128)(2,1)} %bitcast.127), calls=%async_computation.1 | async-start | bytes 2228224 | tf_op jit(solution)/shard_map/all_to_all | solution.py:709
  36.7 2.1 collective-permute-start.3
  38.8 13.3 %collective-permute-done.3 = bf16[256,384]{1,0:T(8,128)(2,1)S(1)} collective-permute-done((bf16[256,384]{1,0:T(8,128)(2,1)S(1)}, bf16[256,384]{1,0:T(8,128)(2,1)S(1)}, u32[]{:S(2)}, u32[]{:S(2)}) %collective-permute-start.3) | collective-permute-done | bytes 196640 | tf_op jit(solution)/shard_map/ppermute | solution.py:565
  52.1 0.8 pad_maximum_fusion.2.refs_0_
  52.9 1.6 collective-permute-start.5
  57.0 0.6 dynamic-slice.5
  58.9 2.8 %collective-permute-done.5.refs_2_ = bf16[512,384]{1,0:T(8,128)(2,1)} collective-permute-done((bf16[512,384]{1,0:T(8,128)(2,1)}, bf16[512,384]{1,0:T(8,128)(2,1)}, u32[]{:S(2)}, u32[]{:S(2)}) %collective-permute-start.5) | collective-permute-done | bytes 393248 | tf_op jit(solution)/shard_map/ppermute | solution.py:560
  61.7 0.6 pad_add_fusion.place_ref
  63.0 2.6 %collective-permute-start.7 = (bf16[256,1152]{1,0:T(8,128)(2,1)S(1)}, bf16[256,1152]{1,0:T(8,128)(2,1)S(1)}, u32[]{:S(2)}, u32[]{:S(2)}) collective-permute-start(bf16[256,1152]{1,0:T(8,128)(2,1)S(1)} %slice.92.refs_0_), channel_id=1, source_target_pairs={{0,4},{4,0},{8,12},{12,8},{16,20},{20,16},{24,28},{28,24},{1,5},{5... | collective-permute-start | bytes 1769480 | tf_op jit(solution)/shard_map/ppermute | solution.py:565
  65.6 1.2 collective-permute-start.8
  67.1 0.7 reshape_squeeze.8.gain_ref
  67.9 8.2 %project.1 = (bf16[1024,1536]{1,0:T(8,128)(2,1)}, bf16[512,1024]{1,0:T(8,128)(2,1)}, bf16[512,1536]{1,0:T(8,128)(2,1)}) custom-call(s32[1]{0:T(128)} %dynamic-slice.4.limit_ref, s32[8]{0:T(128)} %pad_add_fusion.place_ref, bf16[8,4,136,128]{3,2,1,0:T(8,128)(2,1)} %copy-done.2, f32[1,512]{1,0:T(1,128)} %pad_maximum_fusion.4.clock_ref, ...), custom_call_target="tpu_custom_call" | custom-call | flops 5750000128 | bytes 1048576 | tf_op jit(solution)/shard_map/project/pallas_call | solution.py:106
  76.1 3.5 %collective-permute-done.7.refs_1_ = bf16[256,1152]{1,0:T(8,128)(2,1)S(1)} collective-permute-done((bf16[256,1152]{1,0:T(8,128)(2,1)S(1)}, bf16[256,1152]{1,0:T(8,128)(2,1)S(1)}, u32[]{:S(2)}, u32[]{:S(2)}) %collective-permute-start.7) | collective-permute-done | bytes 589856 | tf_op jit(solution)/shard_map/ppermute | solution.py:565
  79.6 1.6 collective-permute-done.8.refs_4_
  81.2 1.2 collective-permute-start.12
  82.9 15.2 %attend.1 = (bf16[1024,512]{1,0:T(8,128)(2,1)}, bf16[512,1024]{1,0:T(8,128)(2,1)}, f32[4,2,1024]{2,1,0:T(2,128)}) custom-call(s32[1]{0:T(128)} %dynamic-slice.4.limit_ref, bf16[1024,1536]{1,0:T(8,128)(2,1)} %get-tuple-element.68.q_ref.k_ref.v_ref, bf16[1024,1536]{1,0:T(8,128)(2,1)} %get-tuple-element.68.q_ref.k_ref.v_ref, ...), custom_call_target="tpu_custom_call" | custom-call | flops 17250000896 | bytes 1048576 | tf_op jit(solution)/shard_map/attend/pallas_call | solution.py:195
  98.5 0.7 copy-done.14
  99.3 0.7 reshape_squeeze.7.gain_ref
  100.5 0.8 copy-done.16
  101.3 30.5 %middle.1 = (bf16[1,1024,512]{2,1,0:T(8,128)(2,1)}, bf16[1024,512]{1,0:T(8,128)(2,1)}, f32[1024,512]{1,0:T(8,128)}, f32[1,512]{1,0:T(1,128)}, bf16[2,512,640]{2,...) custom-call(s32[1]{0:T(128)} %dynamic-slice.4.limit_ref, ...), custom_call_target="tpu_custom_call" | custom-call | flops 28750000128 | bytes 1048576 | tf_op jit(solution)/shard_map/middle/pallas_call | solution.py:345
  132.4 4.2 %collective-permute-done.14 = bf16[2,512,512]{2,1,0:T(8,128)(2,1)S(1)} collective-permute-done((bf16[2,512,512]{2,1,0:T(8,128)(2,1)}, bf16[2,512,512]{2,1,0:T(8,128)(2,1)S(1)}, u32[]{:S(2)}, u32[]{:S(2)}) %collective-permute-start.14) | collective-permute-done | bytes 1048608 | tf_op jit(solution)/shard_map/ppermute | solution.py:560
  136.6 1.2 fusion.3
  138.1 1.6 convert_add_fusion
  139.7 0.9 collective-permute-start.17
  140.6 16.5 %attend_back.2 = (bf16[1024,768]{1,0:T(8,128)(2,1)}, bf16[512,384]{1,0:T(8,128)(2,1)}, bf16[512,384]{1,0:T(8,128)(2,1)}) custom-call(s32[1]{0:T(128)} %dynamic-slice.4.limit_ref, bf16[1024,1536]{1,0:T(8,128)(2,1)} %get-tuple-element.68.q_ref.k_ref.v_ref, bf16[1024,1536]{1,0:T(8,128)(2,1)} %get-tuple-element.68.q_ref.k_ref.v_ref, ...), custom_call_target="tpu_custom_call" | custom-call | flops 18400000000 | bytes 1048576 | tf_op jit(solution)/shard_map/attend_back/pallas_call | solution.py:439
  157.5 1.9 collective-permute-start.20
  159.6 1.3 collective-permute-start.19
  161.0 0.9 collective-permute-start.21
  161.8 16.4 %attend_back.3 = (bf16[1024,768]{1,0:T(8,128)(2,1)}, bf16[512,384]{1,0:T(8,128)(2,1)}, bf16[512,384]{1,0:T(8,128)(2,1)}) custom-call(s32[1]{0:T(128)} %dynamic-slice.4.limit_ref, bf16[1024,1536]{1,0:T(8,128)(2,1)} %get-tuple-element.68.q_ref.k_ref.v_ref, bf16[1024,1536]{1,0:T(8,128)(2,1)} %get-tuple-element.68.q_ref.k_ref.v_ref, ...), custom_call_target="tpu_custom_call" | custom-call | flops 18400000000 | bytes 1048576 | tf_op jit(solution)/shard_map/attend_back/pallas_call | solution.py:439
  178.5 0.8 copy-done.17
  179.3 8.0 %begin_back.1 = bf16[8,4,136,128]{3,2,1,0:T(8,128)(2,1)} custom-call(s32[1]{0:T(128)} %dynamic-slice.4.limit_ref, bf16[8,4,136,128]{3,2,1,0:T(8,128)(2,1)} %copy-done.2, f32[1,512]{1,0:T(1,128)} %pad_maximum_fusion.4.clock_ref, f32[1,512]{1,0:T(1,128)} %reshape_squeeze.8.gain_ref, f32[1,512]{1,0:T(1,128)} %get-tuple-element.79.gg_two_ref, ...), custom_call_target="tpu_custom_call" | custom-call | flops 8049999872 | bytes 1048576 | tf_op jit(solution)/shard_map/begin_back/pallas_call | solution.py:527
  187.3 5.4 %all-to-all-start.2 = ((bf16[32,136,128]{2,1,0:T(8,128)(2,1)}), bf16[32,136,128]{2,1,0:T(8,128)(2,1)S(1)}, u32[]{:S(2)}, u32[]{:S(2)}) async-start(bf16[32,136,128]{2,1,0:T(8,128)(2,1)} %bitcast.132), calls=%async_computation.2 | async-start | bytes 2228224 | tf_op jit(solution)/shard_map/all_to_all | solution.py:775
  192.7 0.7 scatter_custom_fusion
  193.5 1.0 fusion.6
  194.5 1.8 collective-permute-start.23
  196.3 1.5 collective-permute-start.30
  197.8 2.4 %collective-permute-start.31 = (bf16[64,512]{1,0:T(8,128)(2,1)S(1)}, bf16[64,512]{1,0:T(8,128)(2,1)S(1)}, u32[]{:S(2)}, u32[]{:S(2)}) collective-permute-start(bf16[64,512]{1,0:T(8,128)(2,1)S(1)} %get-tuple-element.166), channel_id=1, source_target_pairs={{0,16},{4,20},{8,24},{12,28},{16,0},{20,4},{24,8},{28,12},{1,17},{... | collective-permute-start | bytes 196616 | tf_op jit(solution)/shard_map/ppermute | solution.py:565
  200.3 1.4 collective-permute-start.32
  201.7 0.7 collective-permute-start.27
  202.4 14.8 %collective-permute-done.30 = bf16[64,512]{1,0:T(8,128)(2,1)S(1)} collective-permute-done((bf16[64,512]{1,0:T(8,128)(2,1)S(1)}, bf16[64,512]{1,0:T(8,128)(2,1)S(1)}, u32[]{:S(2)}, u32[]{:S(2)}) %collective-permute-start.30) | collective-permute-done | bytes 65568 | tf_op jit(solution)/shard_map/ppermute | solution.py:565
  217.2 7.9 %collective-permute-start.28 = (bf16[64,640]{1,0:T(8,128)(2,1)S(1)}, bf16[64,640]{1,0:T(8,128)(2,1)S(1)}, u32[]{:S(2)}, u32[]{:S(2)}) collective-permute-start(bf16[64,640]{1,0:T(8,128)(2,1)S(1)} %get-tuple-element.163), channel_id=1, source_target_pairs={{0,16},{4,20},{8,24},{12,28},{16,0},{20,4},{24,8},{28,12},{1,17},{... | collective-permute-start | bytes 245768 | tf_op jit(solution)/shard_map/ppermute | solution.py:565
  225.6 1.0 fusion.5
  226.6 1.6 collective-permute-done.31
  228.3 3.5 %collective-permute-done.28 = bf16[64,640]{1,0:T(8,128)(2,1)S(1)} collective-permute-done((bf16[64,640]{1,0:T(8,128)(2,1)S(1)}, bf16[64,640]{1,0:T(8,128)(2,1)S(1)}, u32[]{:S(2)}, u32[]{:S(2)}) %collective-permute-start.28) | collective-permute-done | bytes 81952 | tf_op jit(solution)/shard_map/ppermute | solution.py:565
  231.7 1.9 collective-permute-start.24
  233.6 1.3 collective-permute-start.25
  234.9 1.1 collective-permute-start.26
  236.1 0.7 fusion.11
  236.8 0.6 slice_bitcast_fusion.2
  237.4 0.7 slice.99
  238.1 1.4 collective-permute-done.25
  239.5 0.7 copy_bitcast_fusion.1
  240.4 1.7 gather_fusion.1
  (118 shorter events, 7.2 us)
Async XLA Ops:
  0.6 1.8 copy-start
  4.4 4.4 %copy-start.10 = (bf16[64,3,128]{2,0,1:T(8,128)(2,1)S(1)}, bf16[64,3,128]{2,0,1:T(8,128)(2,1)}, u32[]{:S(2)}) copy-start(bf16[64,3,128]{2,0,1:T(8,128)(2,1)} %param.15) | copy-start | bytes 147460
  4.4 4.4 %copy-start.7 = (bf16[512,64]{0,1:T(8,128)(2,1)S(1)}, bf16[512,64]{0,1:T(8,128)(2,1)}, u32[]{:S(2)}) copy-start(bf16[512,64]{0,1:T(8,128)(2,1)} %param.18) | copy-start | bytes 196612
  4.4 4.4 %copy-start.8 = (bf16[64,512]{1,0:T(8,128)(2,1)S(1)}, bf16[64,512]{1,0:T(8,128)(2,1)}, u32[]{:S(2)}) copy-start(bf16[64,512]{1,0:T(8,128)(2,1)} %param.17) | copy-start | bytes 196612
  4.4 4.4 %copy-start.9 = (bf16[128,64]{0,1:T(8,128)(2,1)S(1)}, bf16[128,64]{0,1:T(8,128)(2,1)}, u32[]{:S(2)}) copy-start(bf16[128,64]{0,1:T(8,128)(2,1)} %param.16) | copy-start | bytes 49156
  4.4 23.0 %all-to-all-start = ((bf16[32,136,128]{2,1,0:T(8,128)(2,1)}), bf16[32,136,128]{2,1,0:T(8,128)(2,1)S(1)}, u32[]{:S(2)}, u32[]{:S(2)}) async-start(bf16[32,136,128]{2,1,0:T(8,128)(2,1)} %pad_maximum_fusion), calls=%async_computation | async-start | bytes 2228224 | tf_op jit(solution)/shard_map/all_to_all | solution.py:707
  8.8 10.3 %collective-permute-start = (bf16[64,1536]{1,0:T(8,128)(2,1)S(1)}, bf16[64,1536]{1,0:T(8,128)(2,1)S(1)}, u32[]{:S(2)}, u32[]{:S(2)}) collective-permute-start(bf16[64,1536]{1,0:T(8,128)(2,1)S(1)} %pad_maximum_fusion.3), channel_id=1, source_target_pairs={{0,8},{4,12},{8,16},{12,20},{16,24},{20,28},{24,0},{28,4},{1,9},{5... | collective-permute-start | bytes 589832 | tf_op jit(solution)/shard_map/ppermute | solution.py:565
  11.2 16.1 %collective-permute-start.1 = (bf16[64,1536]{1,0:T(8,128)(2,1)S(1)}, bf16[64,1536]{1,0:T(8,128)(2,1)S(1)}, u32[]{:S(2)}, u32[]{:S(2)}) collective-permute-start(bf16[64,1536]{1,0:T(8,128)(2,1)S(1)} %pad_maximum_fusion.3), channel_id=1, source_target_pairs={{0,16},{4,20},{8,24},{12,28},{16,0},{20,4},{24,8},{28,12},{1,17},{... | collective-permute-start | bytes 589832 | tf_op jit(solution)/shard_map/ppermute | solution.py:565
  13.8 13.5 %collective-permute-start.2 = (bf16[64,1536]{1,0:T(8,128)(2,1)S(1)}, bf16[64,1536]{1,0:T(8,128)(2,1)S(1)}, u32[]{:S(2)}, u32[]{:S(2)}) collective-permute-start(bf16[64,1536]{1,0:T(8,128)(2,1)S(1)} %pad_maximum_fusion.3), channel_id=1, source_target_pairs={{0,24},{4,28},{8,0},{12,4},{16,8},{20,12},{24,16},{28,20},{1,25},{... | collective-permute-start | bytes 589832 | tf_op jit(solution)/shard_map/ppermute | solution.py:565
  28.6 25.9 %copy-start.11 = (s32[32]{0:T(128)S(1)}, s32[32]{0:T(128)}, u32[]{:S(2)}) copy-start(s32[32]{0:T(128)} %param.14) | copy-start | bytes 388
  28.6 28.4 %copy-start.18 = (s32[32]{0:T(128)S(1)}, s32[32]{0:T(128)}, u32[]{:S(2)}) copy-start(s32[32]{0:T(128)} %param.12) | copy-start | bytes 388
  28.6 33.8 %copy-start.19 = (s32[32]{0:T(128)S(1)}, s32[32]{0:T(128)}, u32[]{:S(2)}) copy-start(s32[32]{0:T(128)} %param.13) | copy-start | bytes 388
  28.6 38.3 %all-to-all-start.1 = ((bf16[8,4,136,128]{3,2,1,0:T(8,128)(2,1)}), bf16[8,4,136,128]{3,2,1,0:T(8,128)(2,1)S(1)}, u32[]{:S(2)}, u32[]{:S(2)}) async-start(bf16[8,4,136,128]{3,2,1,0:T(8,128)(2,1)} %bitcast.127), calls=%async_computation.1 | async-start | bytes 2228224 | tf_op jit(solution)/shard_map/all_to_all | solution.py:709
  36.7 15.4 %collective-permute-start.3 = (bf16[256,384]{1,0:T(8,128)(2,1)S(1)}, bf16[256,384]{1,0:T(8,128)(2,1)S(1)}, u32[]{:S(2)}, u32[]{:S(2)}) collective-permute-start(bf16[256,384]{1,0:T(8,128)(2,1)S(1)} %slice.91), channel_id=1, source_target_pairs={{0,4},{4,0},{8,12},{12,8},{16,20},{20,16},{24,28},{28,24},{1,5},{5... | collective-permute-start | bytes 589832 | tf_op jit(solution)/shard_map/ppermute | solution.py:565
  52.9 8.9 %collective-permute-start.5 = (bf16[512,384]{1,0:T(8,128)(2,1)}, bf16[512,384]{1,0:T(8,128)(2,1)}, u32[]{:S(2)}, u32[]{:S(2)}) collective-permute-start(bf16[512,384]{1,0:T(8,128)(2,1)} %pad_maximum_fusion.2.refs_0_), channel_id=1, source_target_pairs={{0,2},{1,3},{2,0},{3,1},{4,6},{5,7},{6,4},{7,5},{8,10},{9,11},{10,... | collective-permute-start | bytes 1179656 | tf_op jit(solution)/shard_map/ppermute | solution.py:560
  58.9 8.9 %collective-permute-start.4 = (bf16[512,384]{1,0:T(8,128)(2,1)}, bf16[512,384]{1,0:T(8,128)(2,1)}, u32[]{:S(2)}, u32[]{:S(2)}) collective-permute-start(bf16[512,384]{1,0:T(8,128)(2,1)} %pad_maximum_fusion.2.refs_0_), channel_id=1, source_target_pairs={{0,1},{1,0},{2,3},{3,2},{4,5},{5,4},{6,7},{7,6},{8,9},{9,8},{10,11... | collective-permute-start | bytes 1179656 | tf_op jit(solution)/shard_map/ppermute | solution.py:560
  61.7 6.1 %collective-permute-start.6 = (bf16[512,384]{1,0:T(8,128)(2,1)}, bf16[512,384]{1,0:T(8,128)(2,1)}, u32[]{:S(2)}, u32[]{:S(2)}) collective-permute-start(bf16[512,384]{1,0:T(8,128)(2,1)} %collective-permute-done.5.refs_2_), channel_id=1, source_target_pairs={{0,1},{1,0},{2,3},{3,2},{4,5},{5,4},{6,7},{7,6},{8,9},{9,8},{10,11... | collective-permute-start | bytes 1179656 | tf_op jit(solution)/shard_map/ppermute | solution.py:560
  63.0 19.4 %copy-start.4 = (bf16[256,1152]{1,0:T(8,128)(2,1)}, bf16[256,1152]{1,0:T(8,128)(2,1)S(1)}, u32[]{:S(2)}) copy-start(bf16[256,1152]{1,0:T(8,128)(2,1)S(1)} %slice.92.refs_0_) | copy-start | bytes 1769476
  63.0 16.6 %collective-permute-start.7 = (bf16[256,1152]{1,0:T(8,128)(2,1)S(1)}, bf16[256,1152]{1,0:T(8,128)(2,1)S(1)}, u32[]{:S(2)}, u32[]{:S(2)}) collective-permute-start(bf16[256,1152]{1,0:T(8,128)(2,1)S(1)} %slice.92.refs_0_), channel_id=1, source_target_pairs={{0,4},{4,0},{8,12},{12,8},{16,20},{20,16},{24,28},{28,24},{1,5},{5... | collective-permute-start | bytes 1769480 | tf_op jit(solution)/shard_map/ppermute | solution.py:565
  65.6 15.6 %collective-permute-start.8 = (bf16[256,1152]{1,0:T(8,128)(2,1)S(1)}, bf16[256,1152]{1,0:T(8,128)(2,1)}, u32[]{:S(2)}, u32[]{:S(2)}) collective-permute-start(bf16[256,1152]{1,0:T(8,128)(2,1)S(1)} %slice.92.refs_0_), channel_id=1, source_target_pairs={{0,2},{1,3},{2,0},{3,1},{4,6},{5,7},{6,4},{7,5},{8,10},{9,11},{10,... | collective-permute-start | bytes 1769480 | tf_op jit(solution)/shard_map/ppermute | solution.py:560
  66.8 1.0 copy-start.2
  79.6 18.6 %copy-start.12 = (bf16[256,1152]{1,0:T(8,128)(2,1)}, bf16[256,1152]{1,0:T(8,128)(2,1)S(1)}, u32[]{:S(2)}) copy-start(bf16[256,1152]{1,0:T(8,128)(2,1)S(1)} %collective-permute-done.7.refs_1_) | copy-start | bytes 1769476
  81.2 17.0 %collective-permute-start.10 = (bf16[256,1152]{1,0:T(8,128)(2,1)S(1)}, bf16[256,1152]{1,0:T(8,128)(2,1)S(1)}, u32[]{:S(2)}, u32[]{:S(2)}) collective-permute-start(bf16[256,1152]{1,0:T(8,128)(2,1)S(1)} %collective-permute-done.7.refs_1_), channel_id=1, source_target_pairs={{0,1},{1,0},{2,3},{3,2},{4,5},{5,4},{6,7},{7,6},{8,9},{9,8},{10,11... | collective-permute-start | bytes 1769480 | tf_op jit(solution)/shard_map/ppermute | solution.py:560
  81.2 17.1 %collective-permute-start.12 = (bf16[256,1152]{1,0:T(8,128)(2,1)S(1)}, bf16[256,1152]{1,0:T(8,128)(2,1)}, u32[]{:S(2)}, u32[]{:S(2)}) collective-permute-start(bf16[256,1152]{1,0:T(8,128)(2,1)S(1)} %collective-permute-done.7.refs_1_), channel_id=1, source_target_pairs={{0,2},{1,3},{2,0},{3,1},{4,6},{5,7},{6,4},{7,5},{8,10},{9,11},{10,... | collective-permute-start | bytes 1769480 | tf_op jit(solution)/shard_map/ppermute | solution.py:560
  82.4 15.8 %collective-permute-start.9 = (bf16[256,1152]{1,0:T(8,128)(2,1)S(1)}, bf16[256,1152]{1,0:T(8,128)(2,1)S(1)}, u32[]{:S(2)}, u32[]{:S(2)}) collective-permute-start(bf16[256,1152]{1,0:T(8,128)(2,1)S(1)} %slice.92.refs_0_), channel_id=1, source_target_pairs={{0,1},{1,0},{2,3},{3,2},{4,5},{5,4},{6,7},{7,6},{8,9},{9,8},{10,11... | collective-permute-start | bytes 1769480 | tf_op jit(solution)/shard_map/ppermute | solution.py:560
  82.6 15.6 %collective-permute-start.11 = (bf16[256,1152]{1,0:T(8,128)(2,1)}, bf16[256,1152]{1,0:T(8,128)(2,1)S(1)}, u32[]{:S(2)}, u32[]{:S(2)}) collective-permute-start(bf16[256,1152]{1,0:T(8,128)(2,1)} %collective-permute-done.8.refs_4_), channel_id=1, source_target_pairs={{0,1},{1,0},{2,3},{3,2},{4,5},{5,4},{6,7},{7,6},{8,9},{9,8},{10,11... | collective-permute-start | bytes 1769480 | tf_op jit(solution)/shard_map/ppermute | solution.py:560
  98.2 1.0 copy-start.14
  98.2 2.3 copy-start.13
  98.2 1.0 copy-start.15
  98.2 2.3 collective-permute-start.13
  100.5 0.8 copy-start.16
  131.8 6.3 %copy-start.1 = (bf16[2,512,640]{2,1,0:T(8,128)(2,1)S(1)}, bf16[2,512,640]{2,1,0:T(8,128)(2,1)}, u32[]{:S(2)}) copy-start(bf16[2,512,640]{2,1,0:T(8,128)(2,1)} %get-tuple-element.86) | copy-start | bytes 3932164
  131.8 6.3 %collective-permute-start.15 = (bf16[2,512,640]{2,1,0:T(8,128)(2,1)}, bf16[2,512,640]{2,1,0:T(8,128)(2,1)}, u32[]{:S(2)}, u32[]{:S(2)}) collective-permute-start(bf16[2,512,640]{2,1,0:T(8,128)(2,1)} %get-tuple-element.87), channel_id=1, source_target_pairs={{0,1},{1,0},{2,3},{3,2},{4,5},{5,4},{6,7},{7,6},{8,9},{9,8},{10,11... | collective-permute-start | bytes 3932168 | tf_op jit(solution)/shard_map/ppermute | solution.py:560
  132.1 4.5 %collective-permute-start.14 = (bf16[2,512,512]{2,1,0:T(8,128)(2,1)}, bf16[2,512,512]{2,1,0:T(8,128)(2,1)S(1)}, u32[]{:S(2)}, u32[]{:S(2)}) collective-permute-start(bf16[2,512,512]{2,1,0:T(8,128)(2,1)} %get-tuple-element.82), channel_id=1, source_target_pairs={{0,1},{1,0},{2,3},{3,2},{4,5},{5,4},{6,7},{7,6},{8,9},{9,8},{10,11... | collective-permute-start | bytes 3145736 | tf_op jit(solution)/shard_map/ppermute | solution.py:560
  137.8 19.4 %collective-permute-start.16 = (bf16[2,4,64,512]{3,2,1,0:T(8,128)(2,1)S(1)}, bf16[2,4,64,512]{3,2,1,0:T(8,128)(2,1)S(1)}, u32[]{:S(2)}, u32[]{:S(2)}) collective-permute-start(bf16[2,4,64,512]{3,2,1,0:T(8,128)(2,1)S(1)} %fusion.3), channel_id=1, source_target_pairs={{0,4},{4,0},{8,12},{12,8},{16,20},{20,16},{24,28},{28,24},{1,5},{5... | collective-permute-start | bytes 1572872 | tf_op jit(solution)/shard_map/ppermute | solution.py:565
  139.7 17.4 %collective-permute-start.17 = (bf16[4,2,64,640]{3,2,0,1:T(8,128)(2,1)S(1)}, bf16[4,2,64,640]{3,2,0,1:T(8,128)(2,1)S(1)}, u32[]{:S(2)}, u32[]{:S(2)}) collective-permute-start(bf16[4,2,64,640]{3,2,0,1:T(8,128)(2,1)S(1)} %copy.57), channel_id=1, source_target_pairs={{0,2},{1,3},{2,0},{3,1},{4,6},{5,7},{6,4},{7,5},{8,10},{9,11},{10,... | collective-permute-start | bytes 1966088 | tf_op jit(solution)/shard_map/ppermute | solution.py:560
  157.2 3.7 %collective-permute-start.18 = (bf16[512,384]{1,0:T(8,128)(2,1)}, bf16[512,384]{1,0:T(8,128)(2,1)S(1)}, u32[]{:S(2)}, u32[]{:S(2)}) collective-permute-start(bf16[512,384]{1,0:T(8,128)(2,1)} %get-tuple-element.98), channel_id=1, source_target_pairs={{0,1},{1,0},{2,3},{3,2},{4,5},{5,4},{6,7},{7,6},{8,9},{9,8},{10,11... | collective-permute-start | bytes 1179656 | tf_op jit(solution)/shard_map/ppermute | solution.py:560
  157.3 2.1 copy-start.3
  157.4 3.4 %copy-start.6 = (bf16[512,384]{1,0:T(8,128)(2,1)S(1)}, bf16[512,384]{1,0:T(8,128)(2,1)}, u32[]{:S(2)}) copy-start(bf16[512,384]{1,0:T(8,128)(2,1)} %get-tuple-element.97) | copy-start | bytes 1179652
  157.5 20.8 %collective-permute-start.20 = (bf16[4,64,640]{2,1,0:T(8,128)(2,1)S(1)}, bf16[4,64,640]{2,1,0:T(8,128)(2,1)S(1)}, u32[]{:S(2)}, u32[]{:S(2)}) collective-permute-start(bf16[4,64,640]{2,1,0:T(8,128)(2,1)S(1)} %dynamic-slice_bitcast_fusion), channel_id=1, source_target_pairs={{0,4},{4,0},{8,12},{12,8},{16,20},{20,16},{24,28},{28,24},{1,5},{5... | collective-permute-start | bytes 983048 | tf_op jit(solution)/shard_map/ppermute | solution.py:565
  159.6 18.7 %collective-permute-start.19 = (bf16[4,64,512]{2,1,0:T(8,128)(2,1)S(1)}, bf16[4,64,512]{2,1,0:T(8,128)(2,1)S(1)}, u32[]{:S(2)}, u32[]{:S(2)}) collective-permute-start(bf16[4,64,512]{2,1,0:T(8,128)(2,1)S(1)} %slice_bitcast_fusion), channel_id=1, source_target_pairs={{0,2},{1,3},{2,0},{3,1},{4,6},{5,7},{6,4},{7,5},{8,10},{9,11},{10,... | collective-permute-start | bytes 786440 | tf_op jit(solution)/shard_map/ppermute | solution.py:560
  161.0 17.3 %collective-permute-start.21 = (bf16[512,384]{1,0:T(8,128)(2,1)S(1)}, bf16[512,384]{1,0:T(8,128)(2,1)S(1)}, u32[]{:S(2)}, u32[]{:S(2)}) collective-permute-start(bf16[512,384]{1,0:T(8,128)(2,1)S(1)} %add_convert_fusion.2), channel_id=1, source_target_pairs={{0,2},{1,3},{2,0},{3,1},{4,6},{5,7},{6,4},{7,5},{8,10},{9,11},{10,... | collective-permute-start | bytes 1179656 | tf_op jit(solution)/shard_map/ppermute | solution.py:560
  178.3 1.0 copy-start.17
  179.3 8.0 %collective-permute-start.22 = (bf16[512,384]{1,0:T(8,128)(2,1)S(1)}, bf16[512,384]{1,0:T(8,128)(2,1)}, u32[]{:S(2)}, u32[]{:S(2)}) collective-permute-start(bf16[512,384]{1,0:T(8,128)(2,1)S(1)} %copy-done.17), channel_id=1, source_target_pairs={{0,1},{1,0},{2,3},{3,2},{4,5},{5,4},{6,7},{7,6},{8,9},{9,8},{10,11... | collective-permute-start | bytes 1179656 | tf_op jit(solution)/shard_map/ppermute | solution.py:560
  187.3 6.2 %copy-start.5 = (bf16[512,384]{1,0:T(8,128)(2,1)S(1)}, bf16[512,384]{1,0:T(8,128)(2,1)}, u32[]{:S(2)}) copy-start(bf16[512,384]{1,0:T(8,128)(2,1)} %get-tuple-element.110) | copy-start | bytes 1179652
  187.3 52.9 %all-to-all-start.2 = ((bf16[32,136,128]{2,1,0:T(8,128)(2,1)}), bf16[32,136,128]{2,1,0:T(8,128)(2,1)S(1)}, u32[]{:S(2)}, u32[]{:S(2)}) async-start(bf16[32,136,128]{2,1,0:T(8,128)(2,1)} %bitcast.132), calls=%async_computation.2 | async-start | bytes 2228224 | tf_op jit(solution)/shard_map/all_to_all | solution.py:775
  194.5 30.7 %collective-permute-start.23 = (bf16[4,64,384]{2,1,0:T(8,128)(2,1)S(1)}, bf16[4,64,384]{2,1,0:T(8,128)(2,1)S(1)}, u32[]{:S(2)}, u32[]{:S(2)}) collective-permute-start(bf16[4,64,384]{2,1,0:T(8,128)(2,1)S(1)} %fusion.6), channel_id=1, source_target_pairs={{0,4},{4,0},{8,12},{12,8},{16,20},{20,16},{24,28},{28,24},{1,5},{5... | collective-permute-start | bytes 589832 | tf_op jit(solution)/shard_map/ppermute | solution.py:565
  196.3 20.9 %collective-permute-start.30 = (bf16[64,512]{1,0:T(8,128)(2,1)S(1)}, bf16[64,512]{1,0:T(8,128)(2,1)S(1)}, u32[]{:S(2)}, u32[]{:S(2)}) collective-permute-start(bf16[64,512]{1,0:T(8,128)(2,1)S(1)} %get-tuple-element.167), channel_id=1, source_target_pairs={{0,8},{4,12},{8,16},{12,20},{16,24},{20,28},{24,0},{28,4},{1,9},{5... | collective-permute-start | bytes 196616 | tf_op jit(solution)/shard_map/ppermute | solution.py:565
  197.8 30.4 %collective-permute-start.31 = (bf16[64,512]{1,0:T(8,128)(2,1)S(1)}, bf16[64,512]{1,0:T(8,128)(2,1)S(1)}, u32[]{:S(2)}, u32[]{:S(2)}) collective-permute-start(bf16[64,512]{1,0:T(8,128)(2,1)S(1)} %get-tuple-element.166), channel_id=1, source_target_pairs={{0,16},{4,20},{8,24},{12,28},{16,0},{20,4},{24,8},{28,12},{1,17},{... | collective-permute-start | bytes 196616 | tf_op jit(solution)/shard_map/ppermute | solution.py:565
  200.3 28.0 %collective-permute-start.32 = (bf16[64,512]{1,0:T(8,128)(2,1)S(1)}, bf16[64,512]{1,0:T(8,128)(2,1)S(1)}, u32[]{:S(2)}, u32[]{:S(2)}) collective-permute-start(bf16[64,512]{1,0:T(8,128)(2,1)S(1)} %get-tuple-element.165), channel_id=1, source_target_pairs={{0,24},{4,28},{8,0},{12,4},{16,8},{20,12},{24,16},{28,20},{1,25},{... | collective-permute-start | bytes 196616 | tf_op jit(solution)/shard_map/ppermute | solution.py:565
  201.7 26.5 %collective-permute-start.27 = (bf16[64,640]{1,0:T(8,128)(2,1)S(1)}, bf16[64,640]{1,0:T(8,128)(2,1)S(1)}, u32[]{:S(2)}, u32[]{:S(2)}) collective-permute-start(bf16[64,640]{1,0:T(8,128)(2,1)S(1)} %get-tuple-element.164), channel_id=1, source_target_pairs={{0,8},{4,12},{8,16},{12,20},{16,24},{20,28},{24,0},{28,4},{1,9},{5... | collective-permute-start | bytes 245768 | tf_op jit(solution)/shard_map/ppermute | solution.py:565
  217.2 14.5 %collective-permute-start.28 = (bf16[64,640]{1,0:T(8,128)(2,1)S(1)}, bf16[64,640]{1,0:T(8,128)(2,1)S(1)}, u32[]{:S(2)}, u32[]{:S(2)}) collective-permute-start(bf16[64,640]{1,0:T(8,128)(2,1)S(1)} %get-tuple-element.163), channel_id=1, source_target_pairs={{0,16},{4,20},{8,24},{12,28},{16,0},{20,4},{24,8},{28,12},{1,17},{... | collective-permute-start | bytes 245768 | tf_op jit(solution)/shard_map/ppermute | solution.py:565
  225.1 6.6 %collective-permute-start.29 = (bf16[64,640]{1,0:T(8,128)(2,1)S(1)}, bf16[64,640]{1,0:T(8,128)(2,1)S(1)}, u32[]{:S(2)}, u32[]{:S(2)}) collective-permute-start(bf16[64,640]{1,0:T(8,128)(2,1)S(1)} %get-tuple-element.162), channel_id=1, source_target_pairs={{0,24},{4,28},{8,0},{12,4},{16,8},{20,12},{24,16},{28,20},{1,25},{... | collective-permute-start | bytes 245768 | tf_op jit(solution)/shard_map/ppermute | solution.py:565
  231.7 6.4 %collective-permute-start.24 = (bf16[64,384]{1,0:T(8,128)(2,1)S(1)}, bf16[64,384]{1,0:T(8,128)(2,1)S(1)}, u32[]{:S(2)}, u32[]{:S(2)}) collective-permute-start(bf16[64,384]{1,0:T(8,128)(2,1)S(1)} %get-tuple-element.170), channel_id=1, source_target_pairs={{0,8},{4,12},{8,16},{12,20},{16,24},{20,28},{24,0},{28,4},{1,9},{5... | collective-permute-start | bytes 147464 | tf_op jit(solution)/shard_map/ppermute | solution.py:565
  233.6 5.8 %collective-permute-start.25 = (bf16[64,384]{1,0:T(8,128)(2,1)S(1)}, bf16[64,384]{1,0:T(8,128)(2,1)S(1)}, u32[]{:S(2)}, u32[]{:S(2)}) collective-permute-start(bf16[64,384]{1,0:T(8,128)(2,1)S(1)} %get-tuple-element.169), channel_id=1, source_target_pairs={{0,16},{4,20},{8,24},{12,28},{16,0},{20,4},{24,8},{28,12},{1,17},{... | collective-permute-start | bytes 147464 | tf_op jit(solution)/shard_map/ppermute | solution.py:565
  234.9 4.6 %collective-permute-start.26 = (bf16[64,384]{1,0:T(8,128)(2,1)S(1)}, bf16[64,384]{1,0:T(8,128)(2,1)S(1)}, u32[]{:S(2)}, u32[]{:S(2)}) collective-permute-start(bf16[64,384]{1,0:T(8,128)(2,1)S(1)} %get-tuple-element.168), channel_id=1, source_target_pairs={{0,24},{4,28},{8,0},{12,4},{16,8},{20,12},{24,16},{28,20},{1,25},{... | collective-permute-start | bytes 147464 | tf_op jit(solution)/shard_map/ppermute | solution.py:565

commit v4 on v3

--- a/solution.py
+++ b/solution.py
@@ -10,7 +10,7 @@
 
 HEAD_DIM = 64
 PAIR = 2 * HEAD_DIM
-ROWS = 256
+ROWS = 512
 KEYS = 256
 BACK_KEYS = 512
 SPARE = 8
@@ -20,7 +20,7 @@
 BF16 = jnp.bfloat16
 NN = (((1,), (0,)), ((), ()))
 NT = (((1,), (1,)), ((), ()))
-VMEM_LIMIT = 56 * 1024 * 1024
+MIB = 1024 * 1024
 
 
 def mul(lhs, rhs, dims=NN):
@@ -67,8 +67,8 @@
     )
 
 
-def params(**kwargs):
-    return pltpu.CompilerParams(vmem_limit_bytes=VMEM_LIMIT, **kwargs)
+def params(mebibytes):
+    return pltpu.CompilerParams(vmem_limit_bytes=mebibytes * MIB)
 
 
 def project_kernel(groups, limit_ref, place_ref, x_ref, clock_ref, gain_ref, *refs):
@@ -125,7 +125,7 @@
             jax.ShapeDtypeStruct((features, length), BF16),
             jax.ShapeDtypeStruct((features, parts * columns), BF16),
         ],
-        compiler_params=params(),
+        compiler_params=params(20),
         cost_estimate=cost(5),
         name="project",
     )(limit, place, x_blocks, clock, gain, *w_parts)
@@ -215,7 +215,7 @@
             jax.ShapeDtypeStruct((pairs * PAIR, length), BF16),
             jax.ShapeDtypeStruct((pairs, 2, length), F32),
         ],
-        compiler_params=params(),
+        compiler_params=params(28),
         cost_estimate=cost(15),
         name="attend",
     )(limit, mixed, mixed, mixed)
@@ -380,7 +380,7 @@
             jax.ShapeDtypeStruct((1, features), F32),
             up_shape, down_shape, up_shape, down_shape,
         ],
-        compiler_params=params(),
+        compiler_params=params(40),
         cost_estimate=cost(25),
         name="middle",
     )(limit, place, x_blocks, clock, gain, ctx, out_grad, *weights)
@@ -467,7 +467,7 @@
             jax.ShapeDtypeStruct((features, 3 * PAIR), BF16),
             jax.ShapeDtypeStruct((features, 3 * PAIR), BF16),
         ],
-        compiler_params=params(),
+        compiler_params=params(28),
         cost_estimate=cost(16),
         name="attend_back",
     )(limit, mixed, mixed, mixed, ctx_turn, lse, context_grad, n_turn)
@@ -538,7 +538,7 @@
             scratch_shapes=[pltpu.VMEM((1, features), F32)],
         ),
         out_shape=jax.ShapeDtypeStruct(x_blocks.shape, BF16),
-        compiler_params=params(),
+        compiler_params=params(20),
         cost_estimate=cost(7),
         name="begin_back",
     )(limit, x_blocks, clock, gain, two_grad, middle_grad, w_wide, high, low)
@@ -689,9 +689,10 @@
         place, groups = places(), dp_count
         first = collect_coarse(jnp.concatenate([qkv, rest], axis=1))
         qkv_rows = first[:, : qkv.shape[1]]
-        qkv_parts = collect_columns(jnp.concatenate([qkv_rows, across(qkv_rows)], axis=0))
-        mine = after(first[:, qkv.shape[1] :], qkv_parts[2])
-        other, far_mine = across(mine), swap(mine, 2)
+        qkv_other = across(qkv_rows)
+        qkv_parts = collect_columns(jnp.concatenate([qkv_rows, qkv_other], axis=0))
+        mine = after(first[:, qkv.shape[1] :], qkv_other)
+        other, far_mine = across(mine), swap(after(mine, qkv_parts[2]), 2)
     else:
         place, groups = jnp.zeros((1,), jnp.int32), None
         first = collect_rows(qkv)
@@ -717,15 +718,15 @@
         limit, place, groups, x_blocks, clock, gain_one, qkv_parts
     )
     if direct:
-        mixed, other, far_mine = together(mixed, other, far_mine)
+        mixed, other = together(mixed, other)
         near_mine, near_other = swap(after(mine, mixed), 1), swap(other, 1)
-        last_mine, far_other = swap(far_mine, 1), swap(other, 2)
+        far_other = swap(other, 2)
     ctx, ctx_turn, lse = attend(limit, mixed, tensor_count)
     if direct:
-        ctx, near_mine, near_other, last_mine, far_other = together(
-            ctx, near_mine, near_other, last_mine, far_other
+        ctx, near_mine, near_other, far_mine, far_other = together(
+            ctx, near_mine, near_other, far_mine, far_other
         )
-        last_other = swap(far_other, 1)
+        last_mine, last_other = swap(far_mine, 1), swap(far_other, 1)
         rest_parts = (
             (mine, other), (near_mine, near_other), (far_mine, far_other), (last_mine, last_other)
         )
@@ -756,9 +757,9 @@
         low, one, own_part, down_came, up_came, came_far = together(
             low, one, own_part, down_came, up_came, came_far
         )
-        down_value, down_finish = fold_coarse([*down_rest, down_came])
-        up_value, up_finish = fold_coarse([*up_rest, up_came])
-        middle_grad = after(middle_grad, down_value, up_value)
+        rest_sum = [add(*up_rest, up_came), add(*down_rest, down_came)]
+        rest_value, rest_finish = fold_coarse([jnp.concatenate(rest_sum, axis=-1)])
+        middle_grad = after(middle_grad, rest_value)
     came_one = swap(one, 1)
     begin_grad = begin_block(
         limit, x_blocks, clock, gain_one, two_grad, qkv_wide, middle_grad, high, low
@@ -767,7 +768,8 @@
         begin_grad, came_one = together(begin_grad, came_one)
         near = [grouped(value[None])[0] for value in (own_part, came_one, came_far)]
         qkv_value, qkv_finish = fold_coarse(fold_pair(near)[1]())
-        down_total, up_total, qkv_total = down_finish(qkv_value), up_finish(qkv_value), qkv_finish()
+        rest_total, qkv_total = rest_finish(qkv_value), qkv_finish()
+        up_total, down_total = rest_total[:, : PAIR + hidden], rest_total[:, PAIR + hidden :]
     else:
         up_total = exchange_rows(add(*fold_far([up_keep, up_came])[1]()))
         down_total = exchange_rows(add(*fold_far([down_keep, down_came])[1]()))
@@ -780,7 +782,7 @@
         .at[deal_order]
         .set(jnp.arange(total_seqs, dtype=jnp.int32))
     )
-    states_grad = returned[:, :tokens][inverse]
+    states_grad = returned[inverse][:, :tokens]
     gain_grads = jnp.sum(returned[:, tokens:].astype(F32), axis=0).reshape(2, devices, per)
     gain_grads = lax.dynamic_index_in_dim(gain_grads, own, 1, keepdims=False)
     return (

time: 244 us -> 247 us (1.012)
  local copies, waits for them, and re-layouts: 13.4 us -> 30.1 us
  Pallas kernels: 94.9 us -> 79 us
  waiting for transfers between devices: 59.6 us -> 71.7 us
  starting transfers between devices: 60.1 us -> 52.4 us
    unnamed x41 -> x87, local copies, waits for them, and re-layouts: 2.54 us -> 19.3 us
    ppermute x17 -> x14, waiting for transfers between devices: 50.3 us -> 61.5 us  [along_dp(): return lax.ppermute(value, 'dp', [(i, move(i)) for i in range(count)])]
    ppermute x17 -> x14, starting transfers between devices: 33.7 us -> 26.2 us  [along_dp(): return lax.ppermute(value, 'dp', [(i, move(i)) for i in range(count)])]
    pallas_call x2, Pallas kernels: 33 us -> 28.1 us  [attend_back(): pl.pallas_call(attend_back_kernel, grid_spec=pltpu.PrefetchScalarGridSpec...]
    pallas_call x1, Pallas kernels: 30.5 us -> 25.9 us  [middle_block(): pl.pallas_call(functools.partial(middle_kernel, groups), grid_spec=pltpu....]
    pallas_call x1, Pallas kernels: 8.21 us -> 5.2 us  [project(): pl.pallas_call(functools.partial(project_kernel, groups), grid_spec=pltpu...]
    pallas_call x1, Pallas kernels: 8.01 us -> 5.05 us  [begin_block(): pl.pallas_call(begin_kernel, grid_spec=pltpu.PrefetchScalarGridSpec(num_s...]
  transfers between devices with their start and end apart: 36 -> 33, of which waited for: 12 -> 14; matrix products, arithmetic and copies ran while one was open for 6% -> 5% of each run, Pallas kernels for 27% -> 22%
where the time goes in v4:
time: 247 us; the launch traced here: 246 us
  Pallas kernels  79 us (32%)
  waiting for transfers between devices  71.7 us (29%)
  starting transfers between devices  52.4 us (21%)
  local copies, waits for them, and re-layouts  30.1 us (12%)
  other arithmetic  9.13 us (4%)
  between operations  3.81 us (2%)
    ppermute x14, waiting for transfers between devices, along_dp(): return lax.ppermute(value, 'dp', [(i, move(i)) for i in range(count)])  61.5 us
    pallas_call x2, Pallas kernels, attend_back(): pl.pallas_call(attend_back_kernel, grid_spec=pltpu.PrefetchScalarGridSpec...  28.1 us
    ppermute x14, starting transfers between devices, along_dp(): return lax.ppermute(value, 'dp', [(i, move(i)) for i in range(count)])  26.2 us
    pallas_call x1, Pallas kernels, middle_block(): pl.pallas_call(functools.partial(middle_kernel, groups), grid_spec=pltpu....  25.9 us
    unnamed x87, local copies, waits for them, and re-layouts  19.3 us
    pallas_call x1, Pallas kernels, attend(): pl.pallas_call(attend_kernel, grid_spec=pltpu.PrefetchScalarGridSpec(num_...  14.7 us
    ppermute x16, waiting for transfers between devices, swap(): return lax.ppermute(value, 'tensor', [(i, i ^ apart) for i in range(count)])  10.2 us
    ppermute x16, starting transfers between devices, swap(): return lax.ppermute(value, 'tensor', [(i, i ^ apart) for i in range(count)])  8.75 us
  transfers between devices with their start and end apart: 33, of which 14 were waited for; matrix products, arithmetic and copies ran while one was open for 5% of the time, Pallas kernels for 22%

profile of v4, /device:TPU:0, one launch (start us, length us, event | category | flops | bytes accessed | tf_op | source)
XLA Modules:
  0.0 246.2 jit_solution(9388841211075225442)
XLA Ops:
  3.3 1.1 pad_maximum_fusion
  4.4 4.4 %all-to-all-start = ((bf16[32,136,128]{2,1,0:T(8,128)(2,1)}), bf16[32,136,128]{2,1,0:T(8,128)(2,1)S(1)}, u32[]{:S(2)}, u32[]{:S(2)}) async-start(bf16[32,136,128]{2,1,0:T(8,128)(2,1)} %pad_maximum_fusion), calls=%async_computation | async-start | bytes 2228224 | tf_op jit(solution)/shard_map/all_to_all | solution.py:708
  8.8 2.4 collective-permute-start
  11.2 2.6 %collective-permute-start.1 = (bf16[64,1536]{1,0:T(8,128)(2,1)S(1)}, bf16[64,1536]{1,0:T(8,128)(2,1)S(1)}, u32[]{:S(2)}, u32[]{:S(2)}) collective-permute-start(bf16[64,1536]{1,0:T(8,128)(2,1)S(1)} %pad_maximum_fusion.4), channel_id=1, source_target_pairs={{0,16},{4,20},{8,24},{12,28},{16,0},{20,4},{24,8},{28,12},{1,17},{... | collective-permute-start | bytes 589832 | tf_op jit(solution)/shard_map/ppermute | solution.py:565
  13.8 1.3 collective-permute-start.2
  15.1 4.0 %collective-permute-done = bf16[64,1536]{1,0:T(8,128)(2,1)S(1)} collective-permute-done((bf16[64,1536]{1,0:T(8,128)(2,1)S(1)}, bf16[64,1536]{1,0:T(8,128)(2,1)S(1)}, u32[]{:S(2)}, u32[]{:S(2)}) %collective-permute-start) | collective-permute-done | bytes 196640 | tf_op jit(solution)/shard_map/ppermute | solution.py:565
  19.1 8.2 %collective-permute-done.1 = bf16[64,1536]{1,0:T(8,128)(2,1)S(1)} collective-permute-done((bf16[64,1536]{1,0:T(8,128)(2,1)S(1)}, bf16[64,1536]{1,0:T(8,128)(2,1)S(1)}, u32[]{:S(2)}, u32[]{:S(2)}) %collective-permute-start.1) | collective-permute-done | bytes 196640 | tf_op jit(solution)/shard_map/ppermute | solution.py:565
  27.4 1.2 copy.85
  28.6 8.1 %all-to-all-start.1 = ((bf16[8,4,136,128]{3,2,1,0:T(8,128)(2,1)}), bf16[8,4,136,128]{3,2,1,0:T(8,128)(2,1)S(1)}, u32[]{:S(2)}, u32[]{:S(2)}) async-start(bf16[8,4,136,128]{3,2,1,0:T(8,128)(2,1)} %bitcast.120), calls=%async_computation.1 | async-start | bytes 2228224 | tf_op jit(solution)/shard_map/all_to_all | solution.py:710
  36.7 2.1 collective-permute-start.3
  38.8 13.3 %collective-permute-done.3 = bf16[256,384]{1,0:T(8,128)(2,1)S(1)} collective-permute-done((bf16[256,384]{1,0:T(8,128)(2,1)S(1)}, bf16[256,384]{1,0:T(8,128)(2,1)S(1)}, u32[]{:S(2)}, u32[]{:S(2)}) %collective-permute-start.3) | collective-permute-done | bytes 196640 | tf_op jit(solution)/shard_map/ppermute | solution.py:565
  52.1 1.6 collective-permute-start.5
  57.8 3.1 %collective-permute-done.5.refs_2_ = bf16[512,384]{1,0:T(8,128)(2,1)} collective-permute-done((bf16[512,384]{1,0:T(8,128)(2,1)S(1)}, bf16[512,384]{1,0:T(8,128)(2,1)}, u32[]{:S(2)}, u32[]{:S(2)}) %collective-permute-start.5) | collective-permute-done | bytes 393248 | tf_op jit(solution)/shard_map/ppermute | solution.py:560
  61.5 1.1 slice.99.refs_0_
  62.7 2.6 %collective-permute-start.7 = (bf16[256,1152]{1,0:T(8,128)(2,1)S(1)}, bf16[256,1152]{1,0:T(8,128)(2,1)}, u32[]{:S(2)}, u32[]{:S(2)}) collective-permute-start(bf16[256,1152]{1,0:T(8,128)(2,1)S(1)} %slice.99.refs_0_), channel_id=1, source_target_pairs={{0,4},{4,0},{8,12},{12,8},{16,20},{20,16},{24,28},{28,24},{1,5},{5... | collective-permute-start | bytes 1769480 | tf_op jit(solution)/shard_map/ppermute | solution.py:565
  65.3 1.2 collective-permute-start.10
  66.8 5.2 %project.1 = (bf16[1024,1536]{1,0:T(8,128)(2,1)S(1)}, bf16[512,1024]{1,0:T(8,128)(2,1)S(1)}, bf16[512,1536]{1,0:T(8,128)(2,1)S(1)}) custom-call(s32[1]{0:T(128)} %dynamic-slice.4.limit_ref, s32[8]{0:T(128)S(1)} %pad_add_fusion.place_ref, bf16[8,4,136,128]{3,2,1,0:T(8,128)(2,1)S(1)} %all-to-all-done.1.x_ref, f32[1,512]{1,0:T(1,128)S(1)} %pad_maximum_fusion.5.clock_ref, ...), custom_call_target="tpu_custom_call" | custom-call | flops 5750000128 | bytes 1048576 | tf_op jit(solution)/shard_map/project/pallas_call | solution.py:106
  72.0 1.1 copy-done.17
  73.2 1.0 copy-done.19
  74.2 5.2 %collective-permute-done.7.refs_1_ = bf16[256,1152]{1,0:T(8,128)(2,1)} collective-permute-done((bf16[256,1152]{1,0:T(8,128)(2,1)S(1)}, bf16[256,1152]{1,0:T(8,128)(2,1)}, u32[]{:S(2)}, u32[]{:S(2)}) %collective-permute-start.7) | collective-permute-done | bytes 589856 | tf_op jit(solution)/shard_map/ppermute | solution.py:565
  79.4 1.2 collective-permute-start.11
  81.1 14.7 %attend.1 = (bf16[1024,512]{1,0:T(8,128)(2,1)S(1)}, bf16[512,1024]{1,0:T(8,128)(2,1)S(1)}, f32[4,2,1024]{2,1,0:T(2,128)S(1)}) custom-call(s32[1]{0:T(128)} %dynamic-slice.4.limit_ref, bf16[1024,1536]{1,0:T(8,128)(2,1)S(1)} %get-tuple-element.65.q_ref.k_ref.v_ref, bf16[1024,1536]{1,0:T(8,128)(2,1)S(1)} %get-tuple-element.65.q_ref.k_ref.v_ref, ...), custom_call_target="tpu_custom_call" | custom-call | flops 17250000896 | bytes 1048576 | tf_op jit(solution)/shard_map/attend/pallas_call | solution.py:195
  95.9 1.0 copy-done.21
  96.8 1.0 copy-done.23
  97.8 0.9 copy-done.10
  98.7 0.9 copy-done.8
  100.1 0.8 copy-done.6
  101.1 1.5 collective-permute-done.12.refs_6_
  103.4 1.1 copy-done.4
  104.5 1.2 copy-done.5
  105.7 1.1 copy-done.7
  106.8 1.1 copy-done.9
  107.8 1.1 copy-done.11
  108.9 1.1 copy-done.13
  110.0 1.2 copy-done.24
  111.2 25.9 %middle.1 = (bf16[1,1024,512]{2,1,0:T(8,128)(2,1)}, bf16[1024,512]{1,0:T(8,128)(2,1)S(1)}, f32[1024,512]{1,0:T(8,128)}, f32[1,512]{1,0:T(1,128)S(1)}, bf16[2,512...) custom-call(s32[1]{0:T(128)} %dynamic-slice.4.limit_ref, ...), custom_call_target="tpu_custom_call" | custom-call | flops 28750000128 | bytes 1048576 | tf_op jit(solution)/shard_map/middle/pallas_call | solution.py:345
  137.1 1.0 copy-done.1
  138.1 1.0 copy-done.25
  140.3 3.7 %collective-permute-done.15 = bf16[2,512,512]{2,1,0:T(8,128)(2,1)} collective-permute-done((bf16[2,512,512]{2,1,0:T(8,128)(2,1)}, bf16[2,512,512]{2,1,0:T(8,128)(2,1)}, u32[]{:S(2)}, u32[]{:S(2)}) %collective-permute-start.15) | collective-permute-done | bytes 1048608 | tf_op jit(solution)/shard_map/ppermute | solution.py:560
  144.0 1.4 fusion.3
  145.4 1.8 collective-permute-start.16
  147.3 1.7 convert_add_fusion
  149.1 0.9 collective-permute-start.17
  150.4 14.1 %attend_back.2 = (bf16[1024,768]{1,0:T(8,128)(2,1)S(1)}, bf16[512,384]{1,0:T(8,128)(2,1)S(1)}, bf16[512,384]{1,0:T(8,128)(2,1)S(1)}) custom-call(s32[1]{0:T(128)} %dynamic-slice.4.limit_ref, bf16[1024,1536]{1,0:T(8,128)(2,1)S(1)} %copy-done.15, bf16[1024,1536]{1,0:T(8,128)(2,1)S(1)} %copy-done.15, bf16[1024,1536]{1,0:T(8,128)(2,1)S(1)} %copy-done.15, ...), custom_call_target="tpu_custom_call" | custom-call | flops 18400000000 | bytes 1048576 | tf_op jit(solution)/shard_map/attend_back/pallas_call | solution.py:439
  164.5 1.1 collective-permute-done.17
  166.9 1.3 fusion.1
  168.2 0.9 collective-permute-start.19
  169.2 1.3 collective-permute-start.21
  170.4 14.1 %attend_back.3 = (bf16[1024,768]{1,0:T(8,128)(2,1)S(1)}, bf16[512,384]{1,0:T(8,128)(2,1)S(1)}, bf16[512,384]{1,0:T(8,128)(2,1)S(1)}) custom-call(s32[1]{0:T(128)} %dynamic-slice.4.limit_ref, bf16[1024,1536]{1,0:T(8,128)(2,1)S(1)} %copy-done.15, bf16[1024,1536]{1,0:T(8,128)(2,1)S(1)} %copy-done.15, bf16[1024,1536]{1,0:T(8,128)(2,1)S(1)} %copy-done.15, ...), custom_call_target="tpu_custom_call" | custom-call | flops 18400000000 | bytes 1048576 | tf_op jit(solution)/shard_map/attend_back/pallas_call | solution.py:439
  185.4 5.0 %begin_back.1 = bf16[8,4,136,128]{3,2,1,0:T(8,128)(2,1)} custom-call(s32[1]{0:T(128)} %dynamic-slice.4.limit_ref, bf16[8,4,136,128]{3,2,1,0:T(8,128)(2,1)S(1)} %all-to-all-done.1.x_ref, f32[1,512]{1,0:T(1,128)S(1)} %pad_maximum_fusion.5.clock_ref, f32[1,512]{1,0:T(1,128)S(1)} %reshape_squeeze.8.gain_ref, f32[1,512]{1,0:T(1,128)S(1)} %get-tuple-element.76.gg_two_ref, ...), custom_call_target="tpu_custom_call" | custom-call | flops 8049999872 | bytes 1048576 | tf_op jit(solution)/shard_map/begin_back/pallas_call | solution.py:527
  191.2 5.0 %all-to-all-start.2 = ((bf16[32,136,128]{2,1,0:T(8,128)(2,1)}), bf16[32,136,128]{2,1,0:T(8,128)(2,1)S(1)}, u32[]{:S(2)}, u32[]{:S(2)}) async-start(bf16[32,136,128]{2,1,0:T(8,128)(2,1)} %bitcast.26), calls=%async_computation.2 | async-start | bytes 2228224 | tf_op jit(solution)/shard_map/all_to_all | solution.py:777
  196.4 1.2 fusion.4
  197.6 1.8 collective-permute-start.23
  199.5 1.5 collective-permute-start.27
  201.0 2.4 collective-permute-start.28
  203.5 1.4 collective-permute-start.29
  204.9 6.8 %collective-permute-done.23 = bf16[4,64,384]{2,1,0:T(8,128)(2,1)S(1)} collective-permute-done((bf16[4,64,384]{2,1,0:T(8,128)(2,1)S(1)}, bf16[4,64,384]{2,1,0:T(8,128)(2,1)S(1)}, u32[]{:S(2)}, u32[]{:S(2)}) %collective-permute-start.23) | collective-permute-done | bytes 196640 | tf_op jit(solution)/shard_map/ppermute | solution.py:565
  211.8 10.7 %collective-permute-done.27 = bf16[64,1152]{1,0:T(8,128)(2,1)S(1)} collective-permute-done((bf16[64,1152]{1,0:T(8,128)(2,1)S(1)}, bf16[64,1152]{1,0:T(8,128)(2,1)S(1)}, u32[]{:S(2)}, u32[]{:S(2)}) %collective-permute-start.27) | collective-permute-done | bytes 147488 | tf_op jit(solution)/shard_map/ppermute | solution.py:565
  222.5 11.3 %collective-permute-done.28 = bf16[64,1152]{1,0:T(8,128)(2,1)S(1)} collective-permute-done((bf16[64,1152]{1,0:T(8,128)(2,1)S(1)}, bf16[64,1152]{1,0:T(8,128)(2,1)S(1)}, u32[]{:S(2)}, u32[]{:S(2)}) %collective-permute-start.28) | collective-permute-done | bytes 147488 | tf_op jit(solution)/shard_map/ppermute | solution.py:565
  233.8 3.3 %collective-permute-start.24 = (bf16[64,384]{1,0:T(8,128)(2,1)S(1)}, bf16[64,384]{1,0:T(8,128)(2,1)S(1)}, u32[]{:S(2)}, u32[]{:S(2)}) collective-permute-start(bf16[64,384]{1,0:T(8,128)(2,1)S(1)} %get-tuple-element.163), channel_id=1, source_target_pairs={{0,8},{4,12},{8,16},{12,20},{16,24},{20,28},{24,0},{28,4},{1,9},{5... | collective-permute-start | bytes 147464 | tf_op jit(solution)/shard_map/ppermute | solution.py:565
  237.1 1.3 collective-permute-start.25
  238.4 1.1 collective-permute-start.26
  241.0 1.7 collective-permute-done.25
  244.4 1.1 slice.104
  (156 shorter events, 15.9 us)
Async XLA Ops:
  0.6 1.8 copy-start
  4.4 4.4 %copy-start.39 = (bf16[64,3,128]{2,0,1:T(8,128)(2,1)S(1)}, bf16[64,3,128]{2,0,1:T(8,128)(2,1)}, u32[]{:S(2)}) copy-start(bf16[64,3,128]{2,0,1:T(8,128)(2,1)} %param.15) | copy-start | bytes 147460
  4.4 4.4 %copy-start.36 = (bf16[512,64]{0,1:T(8,128)(2,1)S(1)}, bf16[512,64]{0,1:T(8,128)(2,1)}, u32[]{:S(2)}) copy-start(bf16[512,64]{0,1:T(8,128)(2,1)} %param.18) | copy-start | bytes 196612
  4.4 4.4 %copy-start.37 = (bf16[64,512]{1,0:T(8,128)(2,1)S(1)}, bf16[64,512]{1,0:T(8,128)(2,1)}, u32[]{:S(2)}) copy-start(bf16[64,512]{1,0:T(8,128)(2,1)} %param.17) | copy-start | bytes 196612
  4.4 4.4 %copy-start.38 = (bf16[128,64]{0,1:T(8,128)(2,1)S(1)}, bf16[128,64]{0,1:T(8,128)(2,1)}, u32[]{:S(2)}) copy-start(bf16[128,64]{0,1:T(8,128)(2,1)} %param.16) | copy-start | bytes 49156
  4.4 23.0 %all-to-all-start = ((bf16[32,136,128]{2,1,0:T(8,128)(2,1)}), bf16[32,136,128]{2,1,0:T(8,128)(2,1)S(1)}, u32[]{:S(2)}, u32[]{:S(2)}) async-start(bf16[32,136,128]{2,1,0:T(8,128)(2,1)} %pad_maximum_fusion), calls=%async_computation | async-start | bytes 2228224 | tf_op jit(solution)/shard_map/all_to_all | solution.py:708
  8.8 10.3 %collective-permute-start = (bf16[64,1536]{1,0:T(8,128)(2,1)S(1)}, bf16[64,1536]{1,0:T(8,128)(2,1)S(1)}, u32[]{:S(2)}, u32[]{:S(2)}) collective-permute-start(bf16[64,1536]{1,0:T(8,128)(2,1)S(1)} %pad_maximum_fusion.4), channel_id=1, source_target_pairs={{0,8},{4,12},{8,16},{12,20},{16,24},{20,28},{24,0},{28,4},{1,9},{5... | collective-permute-start | bytes 589832 | tf_op jit(solution)/shard_map/ppermute | solution.py:565
  11.2 16.1 %collective-permute-start.1 = (bf16[64,1536]{1,0:T(8,128)(2,1)S(1)}, bf16[64,1536]{1,0:T(8,128)(2,1)S(1)}, u32[]{:S(2)}, u32[]{:S(2)}) collective-permute-start(bf16[64,1536]{1,0:T(8,128)(2,1)S(1)} %pad_maximum_fusion.4), channel_id=1, source_target_pairs={{0,16},{4,20},{8,24},{12,28},{16,0},{20,4},{24,8},{28,12},{1,17},{... | collective-permute-start | bytes 589832 | tf_op jit(solution)/shard_map/ppermute | solution.py:565
  13.8 13.5 %collective-permute-start.2 = (bf16[64,1536]{1,0:T(8,128)(2,1)S(1)}, bf16[64,1536]{1,0:T(8,128)(2,1)S(1)}, u32[]{:S(2)}, u32[]{:S(2)}) collective-permute-start(bf16[64,1536]{1,0:T(8,128)(2,1)S(1)} %pad_maximum_fusion.4), channel_id=1, source_target_pairs={{0,24},{4,28},{8,0},{12,4},{16,8},{20,12},{24,16},{28,20},{1,25},{... | collective-permute-start | bytes 589832 | tf_op jit(solution)/shard_map/ppermute | solution.py:565
  27.4 11.4 %copy-start.27 = (bf16[256,1536]{1,0:T(8,128)(2,1)}, bf16[256,1536]{1,0:T(8,128)(2,1)S(1)}, u32[]{:S(2)}) copy-start(bf16[256,1536]{1,0:T(8,128)(2,1)S(1)} %pad_maximum_fusion.2) | copy-start | bytes 2359300
  28.6 25.2 %copy-start.40 = (s32[32]{0:T(128)S(1)}, s32[32]{0:T(128)}, u32[]{:S(2)}) copy-start(s32[32]{0:T(128)} %param.14) | copy-start | bytes 388
  28.6 27.7 %copy-start.41 = (s32[32]{0:T(128)S(1)}, s32[32]{0:T(128)}, u32[]{:S(2)}) copy-start(s32[32]{0:T(128)} %param.12) | copy-start | bytes 388
  28.6 32.4 %copy-start.42 = (s32[32]{0:T(128)S(1)}, s32[32]{0:T(128)}, u32[]{:S(2)}) copy-start(s32[32]{0:T(128)} %param.13) | copy-start | bytes 388
  28.6 37.9 %all-to-all-start.1 = ((bf16[8,4,136,128]{3,2,1,0:T(8,128)(2,1)}), bf16[8,4,136,128]{3,2,1,0:T(8,128)(2,1)S(1)}, u32[]{:S(2)}, u32[]{:S(2)}) async-start(bf16[8,4,136,128]{3,2,1,0:T(8,128)(2,1)} %bitcast.120), calls=%async_computation.1 | async-start | bytes 2228224 | tf_op jit(solution)/shard_map/all_to_all | solution.py:710
  36.7 15.4 %collective-permute-start.3 = (bf16[256,384]{1,0:T(8,128)(2,1)S(1)}, bf16[256,384]{1,0:T(8,128)(2,1)S(1)}, u32[]{:S(2)}, u32[]{:S(2)}) collective-permute-start(bf16[256,384]{1,0:T(8,128)(2,1)S(1)} %slice.98), channel_id=1, source_target_pairs={{0,4},{4,0},{8,12},{12,8},{16,20},{20,16},{24,28},{28,24},{1,5},{5... | collective-permute-start | bytes 589832 | tf_op jit(solution)/shard_map/ppermute | solution.py:565
  52.1 8.7 %collective-permute-start.5 = (bf16[512,384]{1,0:T(8,128)(2,1)S(1)}, bf16[512,384]{1,0:T(8,128)(2,1)}, u32[]{:S(2)}, u32[]{:S(2)}) collective-permute-start(bf16[512,384]{1,0:T(8,128)(2,1)S(1)} %pad_maximum_fusion.3.refs_0_), channel_id=1, source_target_pairs={{0,2},{1,3},{2,0},{3,1},{4,6},{5,7},{6,4},{7,5},{8,10},{9,11},{10,... | collective-permute-start | bytes 1179656 | tf_op jit(solution)/shard_map/ppermute | solution.py:560
  57.7 9.1 %collective-permute-start.4 = (bf16[512,384]{1,0:T(8,128)(2,1)S(1)}, bf16[512,384]{1,0:T(8,128)(2,1)}, u32[]{:S(2)}, u32[]{:S(2)}) collective-permute-start(bf16[512,384]{1,0:T(8,128)(2,1)S(1)} %pad_maximum_fusion.3.refs_0_), channel_id=1, source_target_pairs={{0,1},{1,0},{2,3},{3,2},{4,5},{5,4},{6,7},{7,6},{8,9},{9,8},{10,11... | collective-permute-start | bytes 1179656 | tf_op jit(solution)/shard_map/ppermute | solution.py:560
  60.9 5.9 %collective-permute-start.6 = (bf16[512,384]{1,0:T(8,128)(2,1)}, bf16[512,384]{1,0:T(8,128)(2,1)}, u32[]{:S(2)}, u32[]{:S(2)}) collective-permute-start(bf16[512,384]{1,0:T(8,128)(2,1)} %collective-permute-done.5.refs_2_), channel_id=1, source_target_pairs={{0,1},{1,0},{2,3},{3,2},{4,5},{5,4},{6,7},{7,6},{8,9},{9,8},{10,11... | collective-permute-start | bytes 1179656 | tf_op jit(solution)/shard_map/ppermute | solution.py:560
  62.7 18.0 %copy-start.3 = (bf16[256,1152]{1,0:T(8,128)(2,1)}, bf16[256,1152]{1,0:T(8,128)(2,1)S(1)}, u32[]{:S(2)}) copy-start(bf16[256,1152]{1,0:T(8,128)(2,1)S(1)} %slice.99.refs_0_) | copy-start | bytes 1769476
  62.7 16.7 %collective-permute-start.7 = (bf16[256,1152]{1,0:T(8,128)(2,1)S(1)}, bf16[256,1152]{1,0:T(8,128)(2,1)}, u32[]{:S(2)}, u32[]{:S(2)}) collective-permute-start(bf16[256,1152]{1,0:T(8,128)(2,1)S(1)} %slice.99.refs_0_), channel_id=1, source_target_pairs={{0,4},{4,0},{8,12},{12,8},{16,20},{20,16},{24,28},{28,24},{1,5},{5... | collective-permute-start | bytes 1769480 | tf_op jit(solution)/shard_map/ppermute | solution.py:565
  65.3 32.6 %collective-permute-start.10 = (bf16[256,1152]{1,0:T(8,128)(2,1)S(1)}, bf16[256,1152]{1,0:T(8,128)(2,1)}, u32[]{:S(2)}, u32[]{:S(2)}) collective-permute-start(bf16[256,1152]{1,0:T(8,128)(2,1)S(1)} %slice.99.refs_0_), channel_id=1, source_target_pairs={{0,2},{1,3},{2,0},{3,1},{4,6},{5,7},{6,4},{7,5},{8,10},{9,11},{10,... | collective-permute-start | bytes 1769480 | tf_op jit(solution)/shard_map/ppermute | solution.py:560
  72.0 1.1 copy-start.17
  74.2 21.7 %copy-start.14 = (bf16[1024,1536]{1,0:T(8,128)(2,1)}, bf16[1024,1536]{1,0:T(8,128)(2,1)S(1)}, u32[]{:S(2)}) copy-start(bf16[1024,1536]{1,0:T(8,128)(2,1)S(1)} %get-tuple-element.65.q_ref.k_ref.v_ref) | copy-start | bytes 9437188
  79.4 19.3 %collective-permute-start.11 = (bf16[256,1152]{1,0:T(8,128)(2,1)}, bf16[256,1152]{1,0:T(8,128)(2,1)S(1)}, u32[]{:S(2)}, u32[]{:S(2)}) collective-permute-start(bf16[256,1152]{1,0:T(8,128)(2,1)} %collective-permute-done.7.refs_1_), channel_id=1, source_target_pairs={{0,2},{1,3},{2,0},{3,1},{4,6},{5,7},{6,4},{7,5},{8,10},{9,11},{10,... | collective-permute-start | bytes 1769480 | tf_op jit(solution)/shard_map/ppermute | solution.py:560
  80.6 18.1 %collective-permute-start.9 = (bf16[256,1152]{1,0:T(8,128)(2,1)}, bf16[256,1152]{1,0:T(8,128)(2,1)S(1)}, u32[]{:S(2)}, u32[]{:S(2)}) collective-permute-start(bf16[256,1152]{1,0:T(8,128)(2,1)} %collective-permute-done.7.refs_1_), channel_id=1, source_target_pairs={{0,1},{1,0},{2,3},{3,2},{4,5},{5,4},{6,7},{7,6},{8,9},{9,8},{10,11... | collective-permute-start | bytes 1769480 | tf_op jit(solution)/shard_map/ppermute | solution.py:560
  80.6 17.2 %collective-permute-start.8 = (bf16[256,1152]{1,0:T(8,128)(2,1)S(1)}, bf16[256,1152]{1,0:T(8,128)(2,1)S(1)}, u32[]{:S(2)}, u32[]{:S(2)}) collective-permute-start(bf16[256,1152]{1,0:T(8,128)(2,1)S(1)} %slice.99.refs_0_), channel_id=1, source_target_pairs={{0,1},{1,0},{2,3},{3,2},{4,5},{5,4},{6,7},{7,6},{8,9},{9,8},{10,11... | collective-permute-start | bytes 1769480 | tf_op jit(solution)/shard_map/ppermute | solution.py:560
  99.6 3.0 %collective-permute-start.12 = (bf16[256,1152]{1,0:T(8,128)(2,1)}, bf16[256,1152]{1,0:T(8,128)(2,1)S(1)}, u32[]{:S(2)}, u32[]{:S(2)}) collective-permute-start(bf16[256,1152]{1,0:T(8,128)(2,1)} %collective-permute-done.10.refs_4_), channel_id=1, source_target_pairs={{0,1},{1,0},{2,3},{3,2},{4,5},{5,4},{6,7},{7,6},{8,9},{9,8},{10,11... | collective-permute-start | bytes 1769480 | tf_op jit(solution)/shard_map/ppermute | solution.py:560
  99.6 3.8 %collective-permute-start.13 = (bf16[256,1152]{1,0:T(8,128)(2,1)S(1)}, bf16[256,1152]{1,0:T(8,128)(2,1)}, u32[]{:S(2)}, u32[]{:S(2)}) collective-permute-start(bf16[256,1152]{1,0:T(8,128)(2,1)S(1)} %collective-permute-done.11.refs_5_), channel_id=1, source_target_pairs={{0,1},{1,0},{2,3},{3,2},{4,5},{5,4},{6,7},{7,6},{8,9},{9,8},{10,11... | collective-permute-start | bytes 1769480 | tf_op jit(solution)/shard_map/ppermute | solution.py:560
  103.4 1.1 copy-start.4
  104.5 1.2 copy-start.5
  105.7 1.1 copy-start.7
  106.8 1.1 copy-start.9
  110.0 1.2 copy-start.24
  139.1 8.1 %collective-permute-start.14 = (bf16[2,512,640]{2,1,0:T(8,128)(2,1)}, bf16[2,512,640]{2,1,0:T(8,128)(2,1)}, u32[]{:S(2)}, u32[]{:S(2)}) collective-permute-start(bf16[2,512,640]{2,1,0:T(8,128)(2,1)} %get-tuple-element.79), channel_id=1, source_target_pairs={{0,1},{1,0},{2,3},{3,2},{4,5},{5,4},{6,7},{7,6},{8,9},{9,8},{10,11... | collective-permute-start | bytes 3932168 | tf_op jit(solution)/shard_map/ppermute | solution.py:560
  139.3 4.7 %collective-permute-start.15 = (bf16[2,512,512]{2,1,0:T(8,128)(2,1)}, bf16[2,512,512]{2,1,0:T(8,128)(2,1)}, u32[]{:S(2)}, u32[]{:S(2)}) collective-permute-start(bf16[2,512,512]{2,1,0:T(8,128)(2,1)} %get-tuple-element.84), channel_id=1, source_target_pairs={{0,1},{1,0},{2,3},{3,2},{4,5},{5,4},{6,7},{7,6},{8,9},{9,8},{10,11... | collective-permute-start | bytes 3145736 | tf_op jit(solution)/shard_map/ppermute | solution.py:560
  144.0 6.0 %copy-start.26 = (bf16[1024,512]{1,0:T(8,128)(2,1)S(1)}, bf16[1024,512]{1,0:T(8,128)(2,1)}, u32[]{:S(2)}) copy-start(bf16[1024,512]{1,0:T(8,128)(2,1)} %copy-done.25) | copy-start | bytes 3145732
  145.4 19.1 %collective-permute-start.16 = (bf16[2,4,64,512]{3,2,1,0:T(8,128)(2,1)S(1)}, bf16[2,4,64,512]{3,2,1,0:T(8,128)(2,1)S(1)}, u32[]{:S(2)}, u32[]{:S(2)}) collective-permute-start(bf16[2,4,64,512]{3,2,1,0:T(8,128)(2,1)S(1)} %fusion.3), channel_id=1, source_target_pairs={{0,4},{4,0},{8,12},{12,8},{16,20},{20,16},{24,28},{28,24},{1,5},{5... | collective-permute-start | bytes 1572872 | tf_op jit(solution)/shard_map/ppermute | solution.py:565
  147.3 2.7 %copy-start.15 = (bf16[1024,1536]{1,0:T(8,128)(2,1)S(1)}, bf16[1024,1536]{1,0:T(8,128)(2,1)}, u32[]{:S(2)}) copy-start(bf16[1024,1536]{1,0:T(8,128)(2,1)} %copy-done.14) | copy-start | bytes 9437188
  147.3 2.7 %copy-start.22 = (bf16[512,1024]{1,0:T(8,128)(2,1)S(1)}, bf16[512,1024]{1,0:T(8,128)(2,1)}, u32[]{:S(2)}) copy-start(bf16[512,1024]{1,0:T(8,128)(2,1)} %copy-done.21) | copy-start | bytes 3145732
  149.0 1.4 copy-start.20
  149.1 16.6 %collective-permute-start.17 = (bf16[4,2,64,640]{3,2,0,1:T(8,128)(2,1)S(1)}, bf16[4,2,64,640]{3,2,0,1:T(8,128)(2,1)S(1)}, u32[]{:S(2)}, u32[]{:S(2)}) collective-permute-start(bf16[4,2,64,640]{3,2,0,1:T(8,128)(2,1)S(1)} %copy.55), channel_id=1, source_target_pairs={{0,2},{1,3},{2,0},{3,1},{4,6},{5,7},{6,4},{7,5},{8,10},{9,11},{10,... | collective-permute-start | bytes 1966088 | tf_op jit(solution)/shard_map/ppermute | solution.py:560
  165.6 3.4 %collective-permute-start.18 = (bf16[512,384]{1,0:T(8,128)(2,1)S(1)}, bf16[512,384]{1,0:T(8,128)(2,1)S(1)}, u32[]{:S(2)}, u32[]{:S(2)}) collective-permute-start(bf16[512,384]{1,0:T(8,128)(2,1)S(1)} %get-tuple-element.95), channel_id=1, source_target_pairs={{0,1},{1,0},{2,3},{3,2},{4,5},{5,4},{6,7},{7,6},{8,9},{9,8},{10,11... | collective-permute-start | bytes 1179656 | tf_op jit(solution)/shard_map/ppermute | solution.py:560
  165.6 1.2 copy-start.2
  165.9 18.7 %collective-permute-start.20 = (bf16[4,64,640]{2,1,0:T(8,128)(2,1)S(1)}, bf16[4,64,640]{2,1,0:T(8,128)(2,1)S(1)}, u32[]{:S(2)}, u32[]{:S(2)}) collective-permute-start(bf16[4,64,640]{2,1,0:T(8,128)(2,1)S(1)} %dynamic-slice_bitcast_fusion), channel_id=1, source_target_pairs={{0,4},{4,0},{8,12},{12,8},{16,20},{20,16},{24,28},{28,24},{1,5},{5... | collective-permute-start | bytes 983048 | tf_op jit(solution)/shard_map/ppermute | solution.py:565
  168.1 16.4 %copy-start.28 = (bf16[2,4,64,512]{3,2,1,0:T(8,128)(2,1)}, bf16[2,4,64,512]{3,2,1,0:T(8,128)(2,1)S(1)}, u32[]{:S(2)}) copy-start(bf16[2,4,64,512]{3,2,1,0:T(8,128)(2,1)S(1)} %fusion.1) | copy-start | bytes 1572868
  168.2 16.4 %collective-permute-start.19 = (bf16[4,64,512]{2,1,0:T(8,128)(2,1)S(1)}, bf16[4,64,512]{2,1,0:T(8,128)(2,1)S(1)}, u32[]{:S(2)}, u32[]{:S(2)}) collective-permute-start(bf16[4,64,512]{2,1,0:T(8,128)(2,1)S(1)} %slice_bitcast_fusion.1), channel_id=1, source_target_pairs={{0,2},{1,3},{2,0},{3,1},{4,6},{5,7},{6,4},{7,5},{8,10},{9,11},{10,... | collective-permute-start | bytes 786440 | tf_op jit(solution)/shard_map/ppermute | solution.py:560
  169.1 16.2 %copy-start.16 = (f32[1024,512]{1,0:T(8,128)S(1)}, f32[1024,512]{1,0:T(8,128)}, u32[]{:S(2)}) copy-start(f32[1024,512]{1,0:T(8,128)} %get-tuple-element.102.mg_ref) | copy-start | bytes 6291460
  169.2 16.2 %copy-start.18 = (bf16[512,1536]{1,0:T(8,128)(2,1)S(1)}, bf16[512,1536]{1,0:T(8,128)(2,1)}, u32[]{:S(2)}) copy-start(bf16[512,1536]{1,0:T(8,128)(2,1)} %copy-done.17) | copy-start | bytes 4718596
  169.2 16.2 %collective-permute-start.21 = (bf16[512,384]{1,0:T(8,128)(2,1)S(1)}, bf16[512,384]{1,0:T(8,128)(2,1)S(1)}, u32[]{:S(2)}, u32[]{:S(2)}) collective-permute-start(bf16[512,384]{1,0:T(8,128)(2,1)S(1)} %add_convert_fusion.2), channel_id=1, source_target_pairs={{0,2},{1,3},{2,0},{3,1},{4,6},{5,7},{6,4},{7,5},{8,10},{9,11},{10,... | collective-permute-start | bytes 1179656 | tf_op jit(solution)/shard_map/ppermute | solution.py:560
  184.6 5.9 %copy-start.35 = (bf16[4,64,512]{2,1,0:T(8,128)(2,1)}, bf16[4,64,512]{2,1,0:T(8,128)(2,1)S(1)}, u32[]{:S(2)}) copy-start(bf16[4,64,512]{2,1,0:T(8,128)(2,1)S(1)} %collective-permute-done.19) | copy-start | bytes 786436
  184.6 5.9 %copy-start.33 = (bf16[4,64,640]{2,1,0:T(8,128)(2,1)}, bf16[4,64,640]{2,1,0:T(8,128)(2,1)S(1)}, u32[]{:S(2)}) copy-start(bf16[4,64,640]{2,1,0:T(8,128)(2,1)S(1)} %collective-permute-done.20) | copy-start | bytes 983044
  185.4 5.1 %copy-start.29 = (bf16[512,384]{1,0:T(8,128)(2,1)}, bf16[512,384]{1,0:T(8,128)(2,1)S(1)}, u32[]{:S(2)}) copy-start(bf16[512,384]{1,0:T(8,128)(2,1)S(1)} %collective-permute-done.21) | copy-start | bytes 1179652
  185.4 5.1 %collective-permute-start.22 = (bf16[512,384]{1,0:T(8,128)(2,1)S(1)}, bf16[512,384]{1,0:T(8,128)(2,1)S(1)}, u32[]{:S(2)}, u32[]{:S(2)}) collective-permute-start(bf16[512,384]{1,0:T(8,128)(2,1)S(1)} %get-tuple-element.105), channel_id=1, source_target_pairs={{0,1},{1,0},{2,3},{3,2},{4,5},{5,4},{6,7},{7,6},{8,9},{9,8},{10,11... | collective-permute-start | bytes 1179656 | tf_op jit(solution)/shard_map/ppermute | solution.py:560
  191.2 5.0 %copy-start.34 = (bf16[4,64,640]{2,1,0:T(8,128)(2,1)S(1)}, bf16[4,64,640]{2,1,0:T(8,128)(2,1)}, u32[]{:S(2)}) copy-start(bf16[4,64,640]{2,1,0:T(8,128)(2,1)} %copy-done.33) | copy-start | bytes 983044
  191.2 52.4 %all-to-all-start.2 = ((bf16[32,136,128]{2,1,0:T(8,128)(2,1)}), bf16[32,136,128]{2,1,0:T(8,128)(2,1)S(1)}, u32[]{:S(2)}, u32[]{:S(2)}) async-start(bf16[32,136,128]{2,1,0:T(8,128)(2,1)} %bitcast.26), calls=%async_computation.2 | async-start | bytes 2228224 | tf_op jit(solution)/shard_map/all_to_all | solution.py:777
  196.2 1.3 copy-start.30
  196.2 1.3 copy-start.32
  197.6 14.0 %collective-permute-start.23 = (bf16[4,64,384]{2,1,0:T(8,128)(2,1)S(1)}, bf16[4,64,384]{2,1,0:T(8,128)(2,1)S(1)}, u32[]{:S(2)}, u32[]{:S(2)}) collective-permute-start(bf16[4,64,384]{2,1,0:T(8,128)(2,1)S(1)} %fusion.8), channel_id=1, source_target_pairs={{0,4},{4,0},{8,12},{12,8},{16,20},{20,16},{24,28},{28,24},{1,5},{5... | collective-permute-start | bytes 589832 | tf_op jit(solution)/shard_map/ppermute | solution.py:565
  199.5 23.0 %collective-permute-start.27 = (bf16[64,1152]{1,0:T(8,128)(2,1)S(1)}, bf16[64,1152]{1,0:T(8,128)(2,1)S(1)}, u32[]{:S(2)}, u32[]{:S(2)}) collective-permute-start(bf16[64,1152]{1,0:T(8,128)(2,1)S(1)} %get-tuple-element.157), channel_id=1, source_target_pairs={{0,8},{4,12},{8,16},{12,20},{16,24},{20,28},{24,0},{28,4},{1,9},{5... | collective-permute-start | bytes 442376 | tf_op jit(solution)/shard_map/ppermute | solution.py:565
  201.0 32.8 %collective-permute-start.28 = (bf16[64,1152]{1,0:T(8,128)(2,1)S(1)}, bf16[64,1152]{1,0:T(8,128)(2,1)S(1)}, u32[]{:S(2)}, u32[]{:S(2)}) collective-permute-start(bf16[64,1152]{1,0:T(8,128)(2,1)S(1)} %get-tuple-element.158), channel_id=1, source_target_pairs={{0,16},{4,20},{8,24},{12,28},{16,0},{20,4},{24,8},{28,12},{1,17},{... | collective-permute-start | bytes 442376 | tf_op jit(solution)/shard_map/ppermute | solution.py:565
  203.5 30.4 %collective-permute-start.29 = (bf16[64,1152]{1,0:T(8,128)(2,1)S(1)}, bf16[64,1152]{1,0:T(8,128)(2,1)S(1)}, u32[]{:S(2)}, u32[]{:S(2)}) collective-permute-start(bf16[64,1152]{1,0:T(8,128)(2,1)S(1)} %get-tuple-element.156), channel_id=1, source_target_pairs={{0,24},{4,28},{8,0},{12,4},{16,8},{20,12},{24,16},{28,20},{1,25},{... | collective-permute-start | bytes 442376 | tf_op jit(solution)/shard_map/ppermute | solution.py:565
  233.8 7.2 %collective-permute-start.24 = (bf16[64,384]{1,0:T(8,128)(2,1)S(1)}, bf16[64,384]{1,0:T(8,128)(2,1)S(1)}, u32[]{:S(2)}, u32[]{:S(2)}) collective-permute-start(bf16[64,384]{1,0:T(8,128)(2,1)S(1)} %get-tuple-element.163), channel_id=1, source_target_pairs={{0,8},{4,12},{8,16},{12,20},{16,24},{20,28},{24,0},{28,4},{1,9},{5... | collective-permute-start | bytes 147464 | tf_op jit(solution)/shard_map/ppermute | solution.py:565
  237.1 5.5 %collective-permute-start.25 = (bf16[64,384]{1,0:T(8,128)(2,1)S(1)}, bf16[64,384]{1,0:T(8,128)(2,1)S(1)}, u32[]{:S(2)}, u32[]{:S(2)}) collective-permute-start(bf16[64,384]{1,0:T(8,128)(2,1)S(1)} %get-tuple-element.162), channel_id=1, source_target_pairs={{0,16},{4,20},{8,24},{12,28},{16,0},{20,4},{24,8},{28,12},{1,17},{... | collective-permute-start | bytes 147464 | tf_op jit(solution)/shard_map/ppermute | solution.py:565
  238.4 4.5 %collective-permute-start.26 = (bf16[64,384]{1,0:T(8,128)(2,1)S(1)}, bf16[64,384]{1,0:T(8,128)(2,1)S(1)}, u32[]{:S(2)}, u32[]{:S(2)}) collective-permute-start(bf16[64,384]{1,0:T(8,128)(2,1)S(1)} %get-tuple-element.161), channel_id=1, source_target_pairs={{0,24},{4,28},{8,0},{12,4},{16,8},{20,12},{24,16},{28,20},{1,25},{... | collective-permute-start | bytes 147464 | tf_op jit(solution)/shard_map/ppermute | solution.py:565
  (12 other events, 11.3 us)

commit v5 on v4

--- a/solution.py
+++ b/solution.py
@@ -234,26 +234,47 @@
 def middle_kernel(
     groups, limit_ref, place_ref, x_ref, clock_ref, gain_ref, ctx_ref, og_ref, *refs
 ):
-    weight_refs, refs = refs[:-16], refs[-16:]
+    weight_refs, refs = refs[:-17], refs[-17:]
     out_ref, cg_ref, mg_ref, gg_ref, up_send, down_send, up_keep, down_keep = refs[:8]
-    wide, units, active_s, ug_s, n_turn, fg_turn, ag_turn, ctx_s = refs[8:]
+    wide, units, active_s, ug_s, n_turn, fg_turn, ag_turn, ctx_s, sems = refs[8:]
     step = pl.program_id(0)
     parts, _, hidden = active_s.shape
     blocks = pl.num_programs(0) - parts
+    each = len(weight_refs) // parts
+
+    def fetch(part, kind):
+        target, wide_, own = (
+            (wide, PAIR, slice(0, PAIR)),
+            (units, 2 * hidden, slice(PAIR, PAIR + 2 * hidden)),
+        )[kind]
+        columns = slice(part * wide_, (part + 1) * wide_)
+        copies = []
+        for at, w_ref in enumerate(weight_refs[part * each : (part + 1) * each]):
+            count = 1 if groups is None else groups // each
+            rows = w_ref.shape[0] // count
+            for group in range(count):
+                index = at * count + group
+                spot = pl.ds(0, rows)
+                if groups is not None:
+                    spot = pl.ds(pl.multiple_of(place_ref[index] * rows, rows), rows)
+                copies.append(
+                    pltpu.make_async_copy(
+                        w_ref.at[pl.ds(group * rows, rows), own],
+                        target.at[spot, columns],
+                        sems.at[kind, part, index],
+                    )
+                )
+        return copies
 
     @pl.when(step == 0)
     def _():
         gg_ref[...] = jnp.zeros_like(gg_ref)
-        each = len(weight_refs) // parts
         for part in range(parts):
-            thin = slice(part * PAIR, (part + 1) * PAIR)
-            thick = slice(part * 2 * hidden, (part + 1) * 2 * hidden)
-            for at, w_ref in enumerate(weight_refs[part * each : (part + 1) * each]):
-                targets = [
-                    (wide, thin, slice(0, PAIR)), (units, thick, slice(PAIR, PAIR + 2 * hidden))
-                ]
-                count = None if groups is None else groups // each
-                place_rows(count, place_ref, at * (count or 0), w_ref, targets)
+            for copy in fetch(part, 0) + fetch(part, 1):
+                copy.start()
+        for part in range(parts):
+            for copy in fetch(part, 0) + fetch(part, 1):
+                copy.wait()
 
     dead = (step < blocks) & (step * ROWS >= limit_ref[0])
 
@@ -356,7 +377,7 @@
                 rows(features),
                 one,
             ]
-            + [whole(w) for w in weights],
+            + [pl.BlockSpec(memory_space=pltpu.HBM)] * len(weights),
             out_specs=[
                 one, rows(features), rows(features),
                 pl.BlockSpec((1, features), lambda i, *s: (0, 0)),
@@ -371,6 +392,7 @@
                 pltpu.VMEM((features, length), BF16),
                 pltpu.VMEM((features, length), BF16),
                 pltpu.VMEM((parts, length, PAIR), BF16),
+                pltpu.SemaphoreType.DMA((2, parts, groups or 1)),
             ],
         ),
         out_shape=[
@@ -600,10 +622,7 @@
 
 
 def add(*values):
-    total = values[0].astype(F32)
-    for value in values[1:]:
-        total += value.astype(F32)
-    return total.astype(BF16)
+    return add_wide(*values).astype(BF16)
 
 
 def fold_pair(values):
@@ -624,15 +643,14 @@
     pick = lambda value, which: lax.dynamic_index_in_dim(value, which % count, 0, keepdims=False)
     value = add(*values)
     came = [ahead(pick(value, own + step), step) for step in range(1, count)]
-
-    def finish(*others):
-        pieces = lax.optimization_barrier((*came, *others))[: count - 1]
-        total = pick(value, own).astype(F32)
-        for piece in pieces:
-            total += piece.astype(F32)
-        return total
-
-    return value, finish
+    return value, [pick(value, own)] + came
+
+
+def add_wide(*values):
+    total = values[0].astype(F32)
+    for value in values[1:]:
+        total += value.astype(F32)
+    return total
 
 
 def grouped(value):
@@ -737,29 +755,28 @@
 
     back = functools.partial(attend_back, limit, mixed, ctx_turn, lse)
     if direct:
-        down_sent, down_rest = fold_pair([grouped(value) for value in (down_keep, down_came)])
-        up_sent, up_rest = fold_far([grouped(value) for value in (up_keep, up_came)])
+        down_sent, down_rest = fold_far([grouped(value) for value in (down_keep, down_came)])
+        up_sent, up_rest = fold_pair([grouped(value) for value in (up_keep, up_came)])
         context_grad = after(context_grad, down_sent, up_sent)
     high, three, two = back(context_grad, n_one_turn, 3)
     if direct:
         *down_rest, down_came = down_rest()
         *up_rest, up_came = up_rest()
         high, three, two, down_came, up_came = together(high, three, two, down_came, up_came)
-        down_sent, down_rest = fold_far([add(*down_rest, down_came)])
-        up_sent, up_rest = fold_pair([add(*up_rest, up_came)])
-        context_grad = after(context_grad, down_sent, up_sent)
+        down_value, down_pieces = fold_coarse([*down_rest, down_came])
+        up_sent, up_rest = fold_far([add(*up_rest, up_came)])
+        context_grad = after(context_grad, down_value, up_sent)
     far = add(two, swap(three, 1))
     came_far = swap(far, 2)
     low, one, own_part = back(after(context_grad, high, far), n_one_turn, 1)
     if direct:
-        *down_rest, down_came = down_rest()
         *up_rest, up_came = up_rest()
-        low, one, own_part, down_came, up_came, came_far = together(
-            low, one, own_part, down_came, up_came, came_far
+        low, one, own_part, up_came, came_far, *down_pieces = together(
+            low, one, own_part, up_came, came_far, *down_pieces
         )
-        rest_sum = [add(*up_rest, up_came), add(*down_rest, down_came)]
-        rest_value, rest_finish = fold_coarse([jnp.concatenate(rest_sum, axis=-1)])
-        middle_grad = after(middle_grad, rest_value)
+        up_value, up_pieces = fold_coarse([*up_rest, up_came])
+        down_sent, down_rest = fold_pair([add_wide(*down_pieces)[..., None, :, :, :]])
+        middle_grad = after(middle_grad, up_value, down_sent)
     came_one = swap(one, 1)
     begin_grad = begin_block(
         limit, x_blocks, clock, gain_one, two_grad, qkv_wide, middle_grad, high, low
@@ -767,9 +784,11 @@
     if direct:
         begin_grad, came_one = together(begin_grad, came_one)
         near = [grouped(value[None])[0] for value in (own_part, came_one, came_far)]
-        qkv_value, qkv_finish = fold_coarse(fold_pair(near)[1]())
-        rest_total, qkv_total = rest_finish(qkv_value), qkv_finish()
-        up_total, down_total = rest_total[:, : PAIR + hidden], rest_total[:, PAIR + hidden :]
+        qkv_value, qkv_pieces = fold_coarse(fold_pair(near)[1]())
+        *up_pieces, down_came, _ = together(*up_pieces, down_rest()[-1], qkv_value)
+        up_total = add_wide(*up_pieces)
+        down_total = add_wide(*down_rest()[:-1], down_came)[0]
+        qkv_total = add_wide(*qkv_pieces)
     else:
         up_total = exchange_rows(add(*fold_far([up_keep, up_came])[1]()))
         down_total = exchange_rows(add(*fold_far([down_keep, down_came])[1]()))

time: 247 us -> 243 us (0.984)
  starting transfers between devices: 52.4 us -> 62.1 us
  waiting for transfers between devices: 71.7 us -> 63.6 us
  Pallas kernels: 79 us -> 71.1 us
    ppermute x16, starting transfers between devices: 8.75 us -> 15.6 us  [swap(): return lax.ppermute(value, 'tensor', [(i, i ^ apart) for i in range(count)])]
    pallas_call x1, Pallas kernels: 25.9 us -> 20.5 us  [middle_block(): pl.pallas_call(functools.partial(middle_kernel, groups), grid_spec=pltpu....]
    ppermute x14 -> x17, waiting for transfers between devices: 61.5 us -> 56.3 us  [along_dp(): return lax.ppermute(value, 'dp', [(i, move(i)) for i in range(count)])]
    ppermute x14 -> x17, starting transfers between devices: 26.2 us -> 31 us  [along_dp(): return lax.ppermute(value, 'dp', [(i, move(i)) for i in range(count)])]
    ppermute x16, waiting for transfers between devices: 10.2 us -> 7.31 us  [swap(): return lax.ppermute(value, 'tensor', [(i, i ^ apart) for i in range(count)])]
    convert_element_type x8 -> x7, other arithmetic: 4.43 us -> 4.97 us  [add(): return add_wide(*values).astype(BF16)]
    unnamed x87 -> x73, local copies, waits for them, and re-layouts: 19.3 us -> 19.3 us
  transfers between devices with their start and end apart: 33 -> 36, of which waited for: 14 -> 14; matrix products, arithmetic and copies ran while one was open for 5% -> 6% of each run, Pallas kernels for 22% -> 21%
where the time goes in v5:
time: 243 us; the launch traced here: 242 us
  Pallas kernels  71.1 us (29%)
  waiting for transfers between devices  63.6 us (26%)
  starting transfers between devices  62.1 us (26%)
  local copies, waits for them, and re-layouts  30.8 us (13%)
  other arithmetic  10.6 us (4%)
  between operations  3.76 us (2%)
    ppermute x17, waiting for transfers between devices, along_dp(): return lax.ppermute(value, 'dp', [(i, move(i)) for i in range(count)])  56.3 us
    ppermute x17, starting transfers between devices, along_dp(): return lax.ppermute(value, 'dp', [(i, move(i)) for i in range(count)])  31 us
    pallas_call x2, Pallas kernels, attend_back(): pl.pallas_call(attend_back_kernel, grid_spec=pltpu.PrefetchScalarGridSpec...  28.3 us
    pallas_call x1, Pallas kernels, middle_block(): pl.pallas_call(functools.partial(middle_kernel, groups), grid_spec=pltpu....  20.5 us
    unnamed x73, local copies, waits for them, and re-layouts  19.3 us
    ppermute x16, starting transfers between devices, swap(): return lax.ppermute(value, 'tensor', [(i, i ^ apart) for i in range(count)])  15.6 us
    pallas_call x1, Pallas kernels, attend(): pl.pallas_call(attend_kernel, grid_spec=pltpu.PrefetchScalarGridSpec(num_...  14.7 us
    all_to_all x1, starting transfers between devices, on_device(): x_blocks = lax.all_to_all(after(arranged, first), 'dp', 0, 0, tiled=True)  8.09 us
  transfers between devices with their start and end apart: 36, of which 14 were waited for; matrix products, arithmetic and copies ran while one was open for 6% of the time, Pallas kernels for 21%

profile of v5, /device:TPU:0, one launch (start us, length us, event | category | flops | bytes accessed | tf_op | source)
XLA Modules:
  0.0 241.8 jit_solution(12571807873294983992)
XLA Ops:
  3.3 1.1 pad_maximum_fusion
  4.4 4.4 %all-to-all-start = ((bf16[32,136,128]{2,1,0:T(8,128)(2,1)}), bf16[32,136,128]{2,1,0:T(8,128)(2,1)S(1)}, u32[]{:S(2)}, u32[]{:S(2)}) async-start(bf16[32,136,128]{2,1,0:T(8,128)(2,1)} %pad_maximum_fusion), calls=%async_computation | async-start | bytes 2228224 | tf_op jit(solution)/shard_map/all_to_all | solution.py:726
  8.8 2.4 collective-permute-start
  11.2 2.6 %collective-permute-start.1 = (bf16[64,1536]{1,0:T(8,128)(2,1)S(1)}, bf16[64,1536]{1,0:T(8,128)(2,1)S(1)}, u32[]{:S(2)}, u32[]{:S(2)}) collective-permute-start(bf16[64,1536]{1,0:T(8,128)(2,1)S(1)} %pad_maximum_fusion.3), channel_id=1, source_target_pairs={{0,16},{4,20},{8,24},{12,28},{16,0},{20,4},{24,8},{28,12},{1,17},{... | collective-permute-start | bytes 589832 | tf_op jit(solution)/shard_map/ppermute | solution.py:587
  13.8 1.3 collective-permute-start.2
  15.1 4.0 %collective-permute-done = bf16[64,1536]{1,0:T(8,128)(2,1)S(1)} collective-permute-done((bf16[64,1536]{1,0:T(8,128)(2,1)S(1)}, bf16[64,1536]{1,0:T(8,128)(2,1)S(1)}, u32[]{:S(2)}, u32[]{:S(2)}) %collective-permute-start) | collective-permute-done | bytes 196640 | tf_op jit(solution)/shard_map/ppermute | solution.py:587
  19.1 8.2 %collective-permute-done.1 = bf16[64,1536]{1,0:T(8,128)(2,1)S(1)} collective-permute-done((bf16[64,1536]{1,0:T(8,128)(2,1)S(1)}, bf16[64,1536]{1,0:T(8,128)(2,1)S(1)}, u32[]{:S(2)}, u32[]{:S(2)}) %collective-permute-start.1) | collective-permute-done | bytes 196640 | tf_op jit(solution)/shard_map/ppermute | solution.py:587
  27.4 1.2 copy.68
  28.6 8.1 %all-to-all-start.1 = ((bf16[8,4,136,128]{3,2,1,0:T(8,128)(2,1)}), bf16[8,4,136,128]{3,2,1,0:T(8,128)(2,1)S(1)}, u32[]{:S(2)}, u32[]{:S(2)}) async-start(bf16[8,4,136,128]{3,2,1,0:T(8,128)(2,1)} %bitcast.118), calls=%async_computation.1 | async-start | bytes 2228224 | tf_op jit(solution)/shard_map/all_to_all | solution.py:728
  36.7 2.1 collective-permute-start.3
  38.8 13.3 %collective-permute-done.3 = bf16[256,384]{1,0:T(8,128)(2,1)S(1)} collective-permute-done((bf16[256,384]{1,0:T(8,128)(2,1)S(1)}, bf16[256,384]{1,0:T(8,128)(2,1)S(1)}, u32[]{:S(2)}, u32[]{:S(2)}) %collective-permute-start.3) | collective-permute-done | bytes 196640 | tf_op jit(solution)/shard_map/ppermute | solution.py:587
  52.1 1.6 collective-permute-start.5
  57.8 3.1 %collective-permute-done.5.refs_2_ = bf16[512,384]{1,0:T(8,128)(2,1)} collective-permute-done((bf16[512,384]{1,0:T(8,128)(2,1)S(1)}, bf16[512,384]{1,0:T(8,128)(2,1)}, u32[]{:S(2)}, u32[]{:S(2)}) %collective-permute-start.5) | collective-permute-done | bytes 393248 | tf_op jit(solution)/shard_map/ppermute | solution.py:582
  61.5 1.1 slice.92.refs_0_
  62.7 2.6 %collective-permute-start.7 = (bf16[256,1152]{1,0:T(8,128)(2,1)S(1)}, bf16[256,1152]{1,0:T(8,128)(2,1)}, u32[]{:S(2)}, u32[]{:S(2)}) collective-permute-start(bf16[256,1152]{1,0:T(8,128)(2,1)S(1)} %slice.92.refs_0_), channel_id=1, source_target_pairs={{0,4},{4,0},{8,12},{12,8},{16,20},{20,16},{24,28},{28,24},{1,5},{5... | collective-permute-start | bytes 1769480 | tf_op jit(solution)/shard_map/ppermute | solution.py:587
  65.3 1.2 collective-permute-start.10
  66.8 4.1 %project.1 = (bf16[1024,1536]{1,0:T(8,128)(2,1)S(1)}, bf16[512,1024]{1,0:T(8,128)(2,1)S(1)}, bf16[512,1536]{1,0:T(8,128)(2,1)S(1)}) custom-call(s32[1]{0:T(128)} %dynamic-slice.9.limit_ref, s32[8]{0:T(128)S(1)} %pad_add_fusion.place_ref, bf16[8,4,136,128]{3,2,1,0:T(8,128)(2,1)S(1)} %all-to-all-done.1.x_ref, f32[1,512]{1,0:T(1,128)S(1)} %pad_maximum_fusion.4.clock_ref, ...), custom_call_target="tpu_custom_call" | custom-call | flops 5750000128 | bytes 1048576 | tf_op jit(solution)/shard_map/project/pallas_call | solution.py:106
  70.9 1.1 copy-done.16
  72.1 1.0 copy-done.18
  73.1 6.3 %collective-permute-done.7.refs_1_ = bf16[256,1152]{1,0:T(8,128)(2,1)} collective-permute-done((bf16[256,1152]{1,0:T(8,128)(2,1)S(1)}, bf16[256,1152]{1,0:T(8,128)(2,1)}, u32[]{:S(2)}, u32[]{:S(2)}) %collective-permute-start.7) | collective-permute-done | bytes 589856 | tf_op jit(solution)/shard_map/ppermute | solution.py:587
  79.4 1.2 collective-permute-start.11
  81.1 14.7 %attend.1 = (bf16[1024,512]{1,0:T(8,128)(2,1)S(1)}, bf16[512,1024]{1,0:T(8,128)(2,1)S(1)}, f32[4,2,1024]{2,1,0:T(2,128)S(1)}) custom-call(s32[1]{0:T(128)} %dynamic-slice.9.limit_ref, bf16[1024,1536]{1,0:T(8,128)(2,1)S(1)} %get-tuple-element.67.q_ref.k_ref.v_ref, bf16[1024,1536]{1,0:T(8,128)(2,1)S(1)} %get-tuple-element.67.q_ref.k_ref.v_ref, ...), custom_call_target="tpu_custom_call" | custom-call | flops 17250000896 | bytes 1048576 | tf_op jit(solution)/shard_map/attend/pallas_call | solution.py:195
  95.9 1.0 copy-done.20
  101.1 1.5 collective-permute-done.12.refs_6_
  103.5 1.1 copy-done.3
  104.5 1.2 copy-done.4
  105.7 1.1 copy-done.6
  106.8 1.1 copy-done.8
  107.9 1.1 copy-done.10
  108.9 1.1 copy-done.12
  110.0 1.2 copy-done.23
  111.2 20.5 %middle.1 = (bf16[1,1024,512]{2,1,0:T(8,128)(2,1)}, bf16[1024,512]{1,0:T(8,128)(2,1)S(1)}, f32[1024,512]{1,0:T(8,128)}, f32[1,512]{1,0:T(1,128)S(1)}, bf16[2,512...) custom-call(s32[1]{0:T(128)} %dynamic-slice.9.limit_ref, ...), custom_call_target="tpu_custom_call" | custom-call | flops 28750000128 | bytes 1048576 | tf_op jit(solution)/shard_map/middle/pallas_call | solution.py:366
  132.7 1.0 copy-done.24
  133.7 6.2 %collective-permute-start.15 = (bf16[2,512,512]{2,1,0:T(8,128)(2,1)}, bf16[2,512,512]{2,1,0:T(8,128)(2,1)}, u32[]{:S(2)}, u32[]{:S(2)}) collective-permute-start(bf16[2,512,512]{2,1,0:T(8,128)(2,1)} %get-tuple-element.86), channel_id=1, source_target_pairs={{0,1},{1,0},{2,3},{3,2},{4,5},{5,4},{6,7},{7,6},{8,9},{9,8},{10,11... | collective-permute-start | bytes 3145736 | tf_op jit(solution)/shard_map/ppermute | solution.py:582
  140.0 2.6 %collective-permute-done.15 = bf16[2,512,512]{2,1,0:T(8,128)(2,1)} collective-permute-done((bf16[2,512,512]{2,1,0:T(8,128)(2,1)}, bf16[2,512,512]{2,1,0:T(8,128)(2,1)}, u32[]{:S(2)}, u32[]{:S(2)}) %collective-permute-start.15) | collective-permute-done | bytes 1048608 | tf_op jit(solution)/shard_map/ppermute | solution.py:582
  142.6 2.0 convert_add_fusion
  144.6 1.1 collective-permute-start.16
  145.6 1.2 fusion.1
  146.9 1.1 collective-permute-start.17
  148.0 1.2 copy-done.25
  149.2 14.0 %attend_back.2 = (bf16[1024,768]{1,0:T(8,128)(2,1)S(1)}, bf16[512,384]{1,0:T(8,128)(2,1)S(1)}, bf16[512,384]{1,0:T(8,128)(2,1)S(1)}) custom-call(s32[1]{0:T(128)} %dynamic-slice.9.limit_ref, bf16[1024,1536]{1,0:T(8,128)(2,1)S(1)} %copy-done.14, bf16[1024,1536]{1,0:T(8,128)(2,1)S(1)} %copy-done.14, bf16[1024,1536]{1,0:T(8,128)(2,1)S(1)} %copy-done.14, ...), custom_call_target="tpu_custom_call" | custom-call | flops 18400000000 | bytes 1048576 | tf_op jit(solution)/shard_map/attend_back/pallas_call | solution.py:461
  163.5 1.3 fusion
  164.8 1.9 collective-permute-start.19
  167.4 4.2 %collective-permute-start.22 = (bf16[2,64,512]{2,1,0:T(8,128)(2,1)S(1)}, bf16[2,64,512]{2,1,0:T(8,128)(2,1)S(1)}, u32[]{:S(2)}, u32[]{:S(2)}) collective-permute-start(bf16[2,64,512]{2,1,0:T(8,128)(2,1)S(1)} %get-tuple-element.161), channel_id=1, source_target_pairs={{0,16},{4,20},{8,24},{12,28},{16,0},{20,4},{24,8},{28,12},{1,17},{... | collective-permute-start | bytes 393224 | tf_op jit(solution)/shard_map/ppermute | solution.py:587
  171.7 2.1 collective-permute-start.23
  173.9 1.2 collective-permute-start.20
  175.1 14.2 %attend_back.3 = (bf16[1024,768]{1,0:T(8,128)(2,1)S(1)}, bf16[512,384]{1,0:T(8,128)(2,1)S(1)}, bf16[512,384]{1,0:T(8,128)(2,1)S(1)}) custom-call(s32[1]{0:T(128)} %dynamic-slice.9.limit_ref, bf16[1024,1536]{1,0:T(8,128)(2,1)S(1)} %copy-done.14, bf16[1024,1536]{1,0:T(8,128)(2,1)S(1)} %copy-done.14, bf16[1024,1536]{1,0:T(8,128)(2,1)S(1)} %copy-done.14, ...), custom_call_target="tpu_custom_call" | custom-call | flops 18400000000 | bytes 1048576 | tf_op jit(solution)/shard_map/attend_back/pallas_call | solution.py:461
  190.9 3.4 %begin_back.1 = bf16[8,4,136,128]{3,2,1,0:T(8,128)(2,1)} custom-call(s32[1]{0:T(128)} %dynamic-slice.9.limit_ref, bf16[8,4,136,128]{3,2,1,0:T(8,128)(2,1)S(1)} %all-to-all-done.1.x_ref, f32[1,512]{1,0:T(1,128)S(1)} %pad_maximum_fusion.4.clock_ref, f32[1,512]{1,0:T(1,128)S(1)} %reshape_squeeze.8.gain_ref, f32[1,512]{1,0:T(1,128)S(1)} %get-tuple-element.78.gg_two_ref, ...), custom_call_target="tpu_custom_call" | custom-call | flops 8049999872 | bytes 1048576 | tf_op jit(solution)/shard_map/begin_back/pallas_call | solution.py:549
  194.4 3.0 %all-to-all-start.2 = ((bf16[32,136,128]{2,1,0:T(8,128)(2,1)}), bf16[32,136,128]{2,1,0:T(8,128)(2,1)S(1)}, u32[]{:S(2)}, u32[]{:S(2)}) async-start(bf16[32,136,128]{2,1,0:T(8,128)(2,1)} %bitcast.28), calls=%async_computation.2 | async-start | bytes 2228224 | tf_op jit(solution)/shard_map/all_to_all | solution.py:796
  198.1 1.0 fusion.4
  199.1 2.2 collective-permute-start.25
  201.5 1.6 collective-permute-start.29
  203.1 2.4 collective-permute-start.30
  205.5 1.4 collective-permute-start.31
  206.9 6.1 %collective-permute-done.25 = bf16[4,64,384]{2,1,0:T(8,128)(2,1)S(1)} collective-permute-done((bf16[4,64,384]{2,1,0:T(8,128)(2,1)S(1)}, bf16[4,64,384]{2,1,0:T(8,128)(2,1)S(1)}, u32[]{:S(2)}, u32[]{:S(2)}) %collective-permute-start.25) | collective-permute-done | bytes 196640 | tf_op jit(solution)/shard_map/ppermute | solution.py:587
  213.1 1.0 fusion.3
  214.1 1.2 collective-permute-done.32
  215.3 6.9 %collective-permute-done.29 = bf16[64,640]{1,0:T(8,128)(2,1)S(1)} collective-permute-done((bf16[64,640]{1,0:T(8,128)(2,1)S(1)}, bf16[64,640]{1,0:T(8,128)(2,1)S(1)}, u32[]{:S(2)}, u32[]{:S(2)}) %collective-permute-start.29) | collective-permute-done | bytes 81952 | tf_op jit(solution)/shard_map/ppermute | solution.py:587
  222.2 8.5 %collective-permute-done.30 = bf16[64,640]{1,0:T(8,128)(2,1)S(1)} collective-permute-done((bf16[64,640]{1,0:T(8,128)(2,1)S(1)}, bf16[64,640]{1,0:T(8,128)(2,1)S(1)}, u32[]{:S(2)}, u32[]{:S(2)}) %collective-permute-start.30) | collective-permute-done | bytes 81952 | tf_op jit(solution)/shard_map/ppermute | solution.py:587
  230.8 1.9 collective-permute-start.26
  232.7 1.5 collective-permute-start.27
  234.2 1.0 collective-permute-start.28
  237.1 1.4 collective-permute-done.27
  240.1 1.1 slice.97
  (149 shorter events, 19.1 us)
Async XLA Ops:
  0.6 1.8 copy-start
  4.4 4.4 %copy-start.32 = (bf16[64,3,128]{2,0,1:T(8,128)(2,1)S(1)}, bf16[64,3,128]{2,0,1:T(8,128)(2,1)}, u32[]{:S(2)}) copy-start(bf16[64,3,128]{2,0,1:T(8,128)(2,1)} %param.15) | copy-start | bytes 147460
  4.4 4.4 %copy-start.29 = (bf16[512,64]{0,1:T(8,128)(2,1)S(1)}, bf16[512,64]{0,1:T(8,128)(2,1)}, u32[]{:S(2)}) copy-start(bf16[512,64]{0,1:T(8,128)(2,1)} %param.18) | copy-start | bytes 196612
  4.4 4.4 %copy-start.30 = (bf16[64,512]{1,0:T(8,128)(2,1)S(1)}, bf16[64,512]{1,0:T(8,128)(2,1)}, u32[]{:S(2)}) copy-start(bf16[64,512]{1,0:T(8,128)(2,1)} %param.17) | copy-start | bytes 196612
  4.4 4.4 %copy-start.31 = (bf16[128,64]{0,1:T(8,128)(2,1)S(1)}, bf16[128,64]{0,1:T(8,128)(2,1)}, u32[]{:S(2)}) copy-start(bf16[128,64]{0,1:T(8,128)(2,1)} %param.16) | copy-start | bytes 49156
  4.4 23.0 %all-to-all-start = ((bf16[32,136,128]{2,1,0:T(8,128)(2,1)}), bf16[32,136,128]{2,1,0:T(8,128)(2,1)S(1)}, u32[]{:S(2)}, u32[]{:S(2)}) async-start(bf16[32,136,128]{2,1,0:T(8,128)(2,1)} %pad_maximum_fusion), calls=%async_computation | async-start | bytes 2228224 | tf_op jit(solution)/shard_map/all_to_all | solution.py:726
  8.8 10.3 %collective-permute-start = (bf16[64,1536]{1,0:T(8,128)(2,1)S(1)}, bf16[64,1536]{1,0:T(8,128)(2,1)S(1)}, u32[]{:S(2)}, u32[]{:S(2)}) collective-permute-start(bf16[64,1536]{1,0:T(8,128)(2,1)S(1)} %pad_maximum_fusion.3), channel_id=1, source_target_pairs={{0,8},{4,12},{8,16},{12,20},{16,24},{20,28},{24,0},{28,4},{1,9},{5... | collective-permute-start | bytes 589832 | tf_op jit(solution)/shard_map/ppermute | solution.py:587
  11.2 16.1 %collective-permute-start.1 = (bf16[64,1536]{1,0:T(8,128)(2,1)S(1)}, bf16[64,1536]{1,0:T(8,128)(2,1)S(1)}, u32[]{:S(2)}, u32[]{:S(2)}) collective-permute-start(bf16[64,1536]{1,0:T(8,128)(2,1)S(1)} %pad_maximum_fusion.3), channel_id=1, source_target_pairs={{0,16},{4,20},{8,24},{12,28},{16,0},{20,4},{24,8},{28,12},{1,17},{... | collective-permute-start | bytes 589832 | tf_op jit(solution)/shard_map/ppermute | solution.py:587
  13.8 13.5 %collective-permute-start.2 = (bf16[64,1536]{1,0:T(8,128)(2,1)S(1)}, bf16[64,1536]{1,0:T(8,128)(2,1)S(1)}, u32[]{:S(2)}, u32[]{:S(2)}) collective-permute-start(bf16[64,1536]{1,0:T(8,128)(2,1)S(1)} %pad_maximum_fusion.3), channel_id=1, source_target_pairs={{0,24},{4,28},{8,0},{12,4},{16,8},{20,12},{24,16},{28,20},{1,25},{... | collective-permute-start | bytes 589832 | tf_op jit(solution)/shard_map/ppermute | solution.py:587
  27.4 11.4 %copy-start.26 = (bf16[256,1536]{1,0:T(8,128)(2,1)}, bf16[256,1536]{1,0:T(8,128)(2,1)S(1)}, u32[]{:S(2)}) copy-start(bf16[256,1536]{1,0:T(8,128)(2,1)S(1)} %pad_maximum_fusion.1) | copy-start | bytes 2359300
  28.6 25.2 %copy-start.33 = (s32[32]{0:T(128)S(1)}, s32[32]{0:T(128)}, u32[]{:S(2)}) copy-start(s32[32]{0:T(128)} %param.14) | copy-start | bytes 388
  28.6 27.7 %copy-start.34 = (s32[32]{0:T(128)S(1)}, s32[32]{0:T(128)}, u32[]{:S(2)}) copy-start(s32[32]{0:T(128)} %param.12) | copy-start | bytes 388
  28.6 32.4 %copy-start.35 = (s32[32]{0:T(128)S(1)}, s32[32]{0:T(128)}, u32[]{:S(2)}) copy-start(s32[32]{0:T(128)} %param.13) | copy-start | bytes 388
  28.6 37.9 %all-to-all-start.1 = ((bf16[8,4,136,128]{3,2,1,0:T(8,128)(2,1)}), bf16[8,4,136,128]{3,2,1,0:T(8,128)(2,1)S(1)}, u32[]{:S(2)}, u32[]{:S(2)}) async-start(bf16[8,4,136,128]{3,2,1,0:T(8,128)(2,1)} %bitcast.118), calls=%async_computation.1 | async-start | bytes 2228224 | tf_op jit(solution)/shard_map/all_to_all | solution.py:728
  36.7 15.4 %collective-permute-start.3 = (bf16[256,384]{1,0:T(8,128)(2,1)S(1)}, bf16[256,384]{1,0:T(8,128)(2,1)S(1)}, u32[]{:S(2)}, u32[]{:S(2)}) collective-permute-start(bf16[256,384]{1,0:T(8,128)(2,1)S(1)} %slice.91), channel_id=1, source_target_pairs={{0,4},{4,0},{8,12},{12,8},{16,20},{20,16},{24,28},{28,24},{1,5},{5... | collective-permute-start | bytes 589832 | tf_op jit(solution)/shard_map/ppermute | solution.py:587
  52.1 8.7 %collective-permute-start.5 = (bf16[512,384]{1,0:T(8,128)(2,1)S(1)}, bf16[512,384]{1,0:T(8,128)(2,1)}, u32[]{:S(2)}, u32[]{:S(2)}) collective-permute-start(bf16[512,384]{1,0:T(8,128)(2,1)S(1)} %pad_maximum_fusion.2.refs_0_), channel_id=1, source_target_pairs={{0,2},{1,3},{2,0},{3,1},{4,6},{5,7},{6,4},{7,5},{8,10},{9,11},{10,... | collective-permute-start | bytes 1179656 | tf_op jit(solution)/shard_map/ppermute | solution.py:582
  57.7 9.1 %collective-permute-start.4 = (bf16[512,384]{1,0:T(8,128)(2,1)S(1)}, bf16[512,384]{1,0:T(8,128)(2,1)}, u32[]{:S(2)}, u32[]{:S(2)}) collective-permute-start(bf16[512,384]{1,0:T(8,128)(2,1)S(1)} %pad_maximum_fusion.2.refs_0_), channel_id=1, source_target_pairs={{0,1},{1,0},{2,3},{3,2},{4,5},{5,4},{6,7},{7,6},{8,9},{9,8},{10,11... | collective-permute-start | bytes 1179656 | tf_op jit(solution)/shard_map/ppermute | solution.py:582
  60.9 5.9 %collective-permute-start.6 = (bf16[512,384]{1,0:T(8,128)(2,1)}, bf16[512,384]{1,0:T(8,128)(2,1)}, u32[]{:S(2)}, u32[]{:S(2)}) collective-permute-start(bf16[512,384]{1,0:T(8,128)(2,1)} %collective-permute-done.5.refs_2_), channel_id=1, source_target_pairs={{0,1},{1,0},{2,3},{3,2},{4,5},{5,4},{6,7},{7,6},{8,9},{9,8},{10,11... | collective-permute-start | bytes 1179656 | tf_op jit(solution)/shard_map/ppermute | solution.py:582
  62.7 18.0 %copy-start.2 = (bf16[256,1152]{1,0:T(8,128)(2,1)}, bf16[256,1152]{1,0:T(8,128)(2,1)S(1)}, u32[]{:S(2)}) copy-start(bf16[256,1152]{1,0:T(8,128)(2,1)S(1)} %slice.92.refs_0_) | copy-start | bytes 1769476
  62.7 16.7 %collective-permute-start.7 = (bf16[256,1152]{1,0:T(8,128)(2,1)S(1)}, bf16[256,1152]{1,0:T(8,128)(2,1)}, u32[]{:S(2)}, u32[]{:S(2)}) collective-permute-start(bf16[256,1152]{1,0:T(8,128)(2,1)S(1)} %slice.92.refs_0_), channel_id=1, source_target_pairs={{0,4},{4,0},{8,12},{12,8},{16,20},{20,16},{24,28},{28,24},{1,5},{5... | collective-permute-start | bytes 1769480 | tf_op jit(solution)/shard_map/ppermute | solution.py:587
  65.3 32.6 %collective-permute-start.10 = (bf16[256,1152]{1,0:T(8,128)(2,1)S(1)}, bf16[256,1152]{1,0:T(8,128)(2,1)}, u32[]{:S(2)}, u32[]{:S(2)}) collective-permute-start(bf16[256,1152]{1,0:T(8,128)(2,1)S(1)} %slice.92.refs_0_), channel_id=1, source_target_pairs={{0,2},{1,3},{2,0},{3,1},{4,6},{5,7},{6,4},{7,5},{8,10},{9,11},{10,... | collective-permute-start | bytes 1769480 | tf_op jit(solution)/shard_map/ppermute | solution.py:582
  70.9 1.1 copy-start.16
  73.1 22.8 %copy-start.13 = (bf16[1024,1536]{1,0:T(8,128)(2,1)}, bf16[1024,1536]{1,0:T(8,128)(2,1)S(1)}, u32[]{:S(2)}) copy-start(bf16[1024,1536]{1,0:T(8,128)(2,1)S(1)} %get-tuple-element.67.q_ref.k_ref.v_ref) | copy-start | bytes 9437188
  79.4 19.3 %collective-permute-start.11 = (bf16[256,1152]{1,0:T(8,128)(2,1)}, bf16[256,1152]{1,0:T(8,128)(2,1)S(1)}, u32[]{:S(2)}, u32[]{:S(2)}) collective-permute-start(bf16[256,1152]{1,0:T(8,128)(2,1)} %collective-permute-done.7.refs_1_), channel_id=1, source_target_pairs={{0,2},{1,3},{2,0},{3,1},{4,6},{5,7},{6,4},{7,5},{8,10},{9,11},{10,... | collective-permute-start | bytes 1769480 | tf_op jit(solution)/shard_map/ppermute | solution.py:582
  80.6 18.1 %collective-permute-start.9 = (bf16[256,1152]{1,0:T(8,128)(2,1)}, bf16[256,1152]{1,0:T(8,128)(2,1)S(1)}, u32[]{:S(2)}, u32[]{:S(2)}) collective-permute-start(bf16[256,1152]{1,0:T(8,128)(2,1)} %collective-permute-done.7.refs_1_), channel_id=1, source_target_pairs={{0,1},{1,0},{2,3},{3,2},{4,5},{5,4},{6,7},{7,6},{8,9},{9,8},{10,11... | collective-permute-start | bytes 1769480 | tf_op jit(solution)/shard_map/ppermute | solution.py:582
  80.6 17.2 %collective-permute-start.8 = (bf16[256,1152]{1,0:T(8,128)(2,1)S(1)}, bf16[256,1152]{1,0:T(8,128)(2,1)S(1)}, u32[]{:S(2)}, u32[]{:S(2)}) collective-permute-start(bf16[256,1152]{1,0:T(8,128)(2,1)S(1)} %slice.92.refs_0_), channel_id=1, source_target_pairs={{0,1},{1,0},{2,3},{3,2},{4,5},{5,4},{6,7},{7,6},{8,9},{9,8},{10,11... | collective-permute-start | bytes 1769480 | tf_op jit(solution)/shard_map/ppermute | solution.py:582
  99.6 3.0 %collective-permute-start.12 = (bf16[256,1152]{1,0:T(8,128)(2,1)}, bf16[256,1152]{1,0:T(8,128)(2,1)S(1)}, u32[]{:S(2)}, u32[]{:S(2)}) collective-permute-start(bf16[256,1152]{1,0:T(8,128)(2,1)} %collective-permute-done.10.refs_4_), channel_id=1, source_target_pairs={{0,1},{1,0},{2,3},{3,2},{4,5},{5,4},{6,7},{7,6},{8,9},{9,8},{10,11... | collective-permute-start | bytes 1769480 | tf_op jit(solution)/shard_map/ppermute | solution.py:582
  99.6 3.8 %collective-permute-start.13 = (bf16[256,1152]{1,0:T(8,128)(2,1)S(1)}, bf16[256,1152]{1,0:T(8,128)(2,1)}, u32[]{:S(2)}, u32[]{:S(2)}) collective-permute-start(bf16[256,1152]{1,0:T(8,128)(2,1)S(1)} %collective-permute-done.11.refs_5_), channel_id=1, source_target_pairs={{0,1},{1,0},{2,3},{3,2},{4,5},{5,4},{6,7},{7,6},{8,9},{9,8},{10,11... | collective-permute-start | bytes 1769480 | tf_op jit(solution)/shard_map/ppermute | solution.py:582
  103.5 1.1 copy-start.3
  104.5 1.2 copy-start.4
  105.7 1.1 copy-start.6
  106.8 1.1 copy-start.8
  107.9 1.1 copy-start.10
  108.9 1.1 copy-start.12
  110.0 1.2 copy-start.23
  132.7 1.0 copy-start.24
  133.7 8.9 %collective-permute-start.15 = (bf16[2,512,512]{2,1,0:T(8,128)(2,1)}, bf16[2,512,512]{2,1,0:T(8,128)(2,1)}, u32[]{:S(2)}, u32[]{:S(2)}) collective-permute-start(bf16[2,512,512]{2,1,0:T(8,128)(2,1)} %get-tuple-element.86), channel_id=1, source_target_pairs={{0,1},{1,0},{2,3},{3,2},{4,5},{5,4},{6,7},{7,6},{8,9},{9,8},{10,11... | collective-permute-start | bytes 3145736 | tf_op jit(solution)/shard_map/ppermute | solution.py:582
  140.0 5.7 %collective-permute-start.14 = (bf16[2,512,640]{2,1,0:T(8,128)(2,1)}, bf16[2,512,640]{2,1,0:T(8,128)(2,1)}, u32[]{:S(2)}, u32[]{:S(2)}) collective-permute-start(bf16[2,512,640]{2,1,0:T(8,128)(2,1)} %get-tuple-element.81), channel_id=1, source_target_pairs={{0,1},{1,0},{2,3},{3,2},{4,5},{5,4},{6,7},{7,6},{8,9},{9,8},{10,11... | collective-permute-start | bytes 3932168 | tf_op jit(solution)/shard_map/ppermute | solution.py:582
  142.6 5.4 %copy-start.14 = (bf16[1024,1536]{1,0:T(8,128)(2,1)S(1)}, bf16[1024,1536]{1,0:T(8,128)(2,1)}, u32[]{:S(2)}) copy-start(bf16[1024,1536]{1,0:T(8,128)(2,1)} %copy-done.13) | copy-start | bytes 9437188
  142.6 5.4 %copy-start.21 = (bf16[512,1024]{1,0:T(8,128)(2,1)S(1)}, bf16[512,1024]{1,0:T(8,128)(2,1)}, u32[]{:S(2)}) copy-start(bf16[512,1024]{1,0:T(8,128)(2,1)} %copy-done.20) | copy-start | bytes 3145732
  144.6 3.4 %copy-start.19 = (bf16[512,1024]{1,0:T(8,128)(2,1)S(1)}, bf16[512,1024]{1,0:T(8,128)(2,1)}, u32[]{:S(2)}) copy-start(bf16[512,1024]{1,0:T(8,128)(2,1)} %copy-done.18) | copy-start | bytes 3145732
  144.6 18.7 %collective-permute-start.16 = (bf16[4,2,64,512]{3,2,1,0:T(8,128)(2,1)S(1)}, bf16[4,2,64,512]{3,2,1,0:T(8,128)(2,1)S(1)}, u32[]{:S(2)}, u32[]{:S(2)}) collective-permute-start(bf16[4,2,64,512]{3,2,1,0:T(8,128)(2,1)S(1)} %bitcast.126), channel_id=1, source_target_pairs={{0,2},{1,3},{2,0},{3,1},{4,6},{5,7},{6,4},{7,5},{8,10},{9,11},{10,... | collective-permute-start | bytes 1572872 | tf_op jit(solution)/shard_map/ppermute | solution.py:582
  146.9 16.6 %collective-permute-start.17 = (bf16[2,4,64,640]{3,2,1,0:T(8,128)(2,1)S(1)}, bf16[2,4,64,640]{3,2,1,0:T(8,128)(2,1)S(1)}, u32[]{:S(2)}, u32[]{:S(2)}) collective-permute-start(bf16[2,4,64,640]{3,2,1,0:T(8,128)(2,1)S(1)} %fusion.1), channel_id=1, source_target_pairs={{0,4},{4,0},{8,12},{12,8},{16,20},{20,16},{24,28},{28,24},{1,5},{5... | collective-permute-start | bytes 1966088 | tf_op jit(solution)/shard_map/ppermute | solution.py:587
  148.0 1.2 copy-start.25
  163.5 10.3 %collective-permute-start.18 = (bf16[512,384]{1,0:T(8,128)(2,1)S(1)}, bf16[512,384]{1,0:T(8,128)(2,1)S(1)}, u32[]{:S(2)}, u32[]{:S(2)}) collective-permute-start(bf16[512,384]{1,0:T(8,128)(2,1)S(1)} %get-tuple-element.97), channel_id=1, source_target_pairs={{0,1},{1,0},{2,3},{3,2},{4,5},{5,4},{6,7},{7,6},{8,9},{9,8},{10,11... | collective-permute-start | bytes 1179656 | tf_op jit(solution)/shard_map/ppermute | solution.py:582
  164.8 24.5 %collective-permute-start.19 = (bf16[4,64,640]{2,1,0:T(8,128)(2,1)S(1)}, bf16[4,64,640]{2,1,0:T(8,128)(2,1)S(1)}, u32[]{:S(2)}, u32[]{:S(2)}) collective-permute-start(bf16[4,64,640]{2,1,0:T(8,128)(2,1)S(1)} %slice_bitcast_fusion), channel_id=1, source_target_pairs={{0,2},{1,3},{2,0},{3,1},{4,6},{5,7},{6,4},{7,5},{8,10},{9,11},{10,... | collective-permute-start | bytes 983048 | tf_op jit(solution)/shard_map/ppermute | solution.py:582
  167.0 22.3 %collective-permute-start.21 = (bf16[2,64,512]{2,1,0:T(8,128)(2,1)S(1)}, bf16[2,64,512]{2,1,0:T(8,128)(2,1)S(1)}, u32[]{:S(2)}, u32[]{:S(2)}) collective-permute-start(bf16[2,64,512]{2,1,0:T(8,128)(2,1)S(1)} %get-tuple-element.162), channel_id=1, source_target_pairs={{0,8},{4,12},{8,16},{12,20},{16,24},{20,28},{24,0},{28,4},{1,9},{5... | collective-permute-start | bytes 393224 | tf_op jit(solution)/shard_map/ppermute | solution.py:587
  167.4 21.9 %collective-permute-start.22 = (bf16[2,64,512]{2,1,0:T(8,128)(2,1)S(1)}, bf16[2,64,512]{2,1,0:T(8,128)(2,1)S(1)}, u32[]{:S(2)}, u32[]{:S(2)}) collective-permute-start(bf16[2,64,512]{2,1,0:T(8,128)(2,1)S(1)} %get-tuple-element.161), channel_id=1, source_target_pairs={{0,16},{4,20},{8,24},{12,28},{16,0},{20,4},{24,8},{28,12},{1,17},{... | collective-permute-start | bytes 393224 | tf_op jit(solution)/shard_map/ppermute | solution.py:587
  171.7 17.7 %collective-permute-start.23 = (bf16[2,64,512]{2,1,0:T(8,128)(2,1)S(1)}, bf16[2,64,512]{2,1,0:T(8,128)(2,1)S(1)}, u32[]{:S(2)}, u32[]{:S(2)}) collective-permute-start(bf16[2,64,512]{2,1,0:T(8,128)(2,1)S(1)} %get-tuple-element.160), channel_id=1, source_target_pairs={{0,24},{4,28},{8,0},{12,4},{16,8},{20,12},{24,16},{28,20},{1,25},{... | collective-permute-start | bytes 393224 | tf_op jit(solution)/shard_map/ppermute | solution.py:587
  173.9 15.5 %collective-permute-start.20 = (bf16[512,384]{1,0:T(8,128)(2,1)S(1)}, bf16[512,384]{1,0:T(8,128)(2,1)S(1)}, u32[]{:S(2)}, u32[]{:S(2)}) collective-permute-start(bf16[512,384]{1,0:T(8,128)(2,1)S(1)} %add_convert_fusion.3), channel_id=1, source_target_pairs={{0,2},{1,3},{2,0},{3,1},{4,6},{5,7},{6,4},{7,5},{8,10},{9,11},{10,... | collective-permute-start | bytes 1179656 | tf_op jit(solution)/shard_map/ppermute | solution.py:582
  175.1 15.1 %copy-start.15 = (f32[1024,512]{1,0:T(8,128)S(1)}, f32[1024,512]{1,0:T(8,128)}, u32[]{:S(2)}) copy-start(f32[1024,512]{1,0:T(8,128)} %get-tuple-element.107.mg_ref) | copy-start | bytes 6291460
  189.3 1.6 copy-start.17
  189.4 4.9 %copy-start.27 = (bf16[512,384]{1,0:T(8,128)(2,1)}, bf16[512,384]{1,0:T(8,128)(2,1)S(1)}, u32[]{:S(2)}) copy-start(bf16[512,384]{1,0:T(8,128)(2,1)S(1)} %collective-permute-done.20) | copy-start | bytes 1179652
  190.2 4.1 %collective-permute-start.24 = (bf16[512,384]{1,0:T(8,128)(2,1)S(1)}, bf16[512,384]{1,0:T(8,128)(2,1)}, u32[]{:S(2)}, u32[]{:S(2)}) collective-permute-start(bf16[512,384]{1,0:T(8,128)(2,1)S(1)} %get-tuple-element.110), channel_id=1, source_target_pairs={{0,1},{1,0},{2,3},{3,2},{4,5},{5,4},{6,7},{7,6},{8,9},{9,8},{10,11... | collective-permute-start | bytes 1179656 | tf_op jit(solution)/shard_map/ppermute | solution.py:582
  194.4 3.8 %copy-start.28 = (bf16[512,384]{1,0:T(8,128)(2,1)S(1)}, bf16[512,384]{1,0:T(8,128)(2,1)}, u32[]{:S(2)}) copy-start(bf16[512,384]{1,0:T(8,128)(2,1)} %copy-done.27) | copy-start | bytes 1179652
  194.4 45.0 %all-to-all-start.2 = ((bf16[32,136,128]{2,1,0:T(8,128)(2,1)}), bf16[32,136,128]{2,1,0:T(8,128)(2,1)S(1)}, u32[]{:S(2)}, u32[]{:S(2)}) async-start(bf16[32,136,128]{2,1,0:T(8,128)(2,1)} %bitcast.28), calls=%async_computation.2 | async-start | bytes 2228224 | tf_op jit(solution)/shard_map/all_to_all | solution.py:796
  199.1 13.9 %collective-permute-start.25 = (bf16[4,64,384]{2,1,0:T(8,128)(2,1)S(1)}, bf16[4,64,384]{2,1,0:T(8,128)(2,1)S(1)}, u32[]{:S(2)}, u32[]{:S(2)}) collective-permute-start(bf16[4,64,384]{2,1,0:T(8,128)(2,1)S(1)} %fusion.4), channel_id=1, source_target_pairs={{0,4},{4,0},{8,12},{12,8},{16,20},{20,16},{24,28},{28,24},{1,5},{5... | collective-permute-start | bytes 589832 | tf_op jit(solution)/shard_map/ppermute | solution.py:587
  201.4 13.9 %collective-permute-start.32 = (bf16[1,64,512]{2,1,0:T(8,128)(2,1)}, bf16[1,64,512]{2,1,0:T(8,128)(2,1)S(1)}, u32[]{:S(2)}, u32[]{:S(2)}) collective-permute-start(bf16[1,64,512]{2,1,0:T(8,128)(2,1)} %dynamic-slice_convert_fusion), channel_id=1, source_target_pairs={{0,4},{4,0},{8,12},{12,8},{16,20},{20,16},{24,28},{28,24},{1,5},{5... | collective-permute-start | bytes 196616 | tf_op jit(solution)/shard_map/ppermute | solution.py:587
  201.5 20.7 %collective-permute-start.29 = (bf16[64,640]{1,0:T(8,128)(2,1)S(1)}, bf16[64,640]{1,0:T(8,128)(2,1)S(1)}, u32[]{:S(2)}, u32[]{:S(2)}) collective-permute-start(bf16[64,640]{1,0:T(8,128)(2,1)S(1)} %get-tuple-element.166), channel_id=1, source_target_pairs={{0,8},{4,12},{8,16},{12,20},{16,24},{20,28},{24,0},{28,4},{1,9},{5... | collective-permute-start | bytes 245768 | tf_op jit(solution)/shard_map/ppermute | solution.py:587
  203.1 27.7 %collective-permute-start.30 = (bf16[64,640]{1,0:T(8,128)(2,1)S(1)}, bf16[64,640]{1,0:T(8,128)(2,1)S(1)}, u32[]{:S(2)}, u32[]{:S(2)}) collective-permute-start(bf16[64,640]{1,0:T(8,128)(2,1)S(1)} %get-tuple-element.165), channel_id=1, source_target_pairs={{0,16},{4,20},{8,24},{12,28},{16,0},{20,4},{24,8},{28,12},{1,17},{... | collective-permute-start | bytes 245768 | tf_op jit(solution)/shard_map/ppermute | solution.py:587
  205.5 25.3 %collective-permute-start.31 = (bf16[64,640]{1,0:T(8,128)(2,1)S(1)}, bf16[64,640]{1,0:T(8,128)(2,1)S(1)}, u32[]{:S(2)}, u32[]{:S(2)}) collective-permute-start(bf16[64,640]{1,0:T(8,128)(2,1)S(1)} %get-tuple-element.164), channel_id=1, source_target_pairs={{0,24},{4,28},{8,0},{12,4},{16,8},{20,12},{24,16},{28,20},{1,25},{... | collective-permute-start | bytes 245768 | tf_op jit(solution)/shard_map/ppermute | solution.py:587
  230.8 6.3 %collective-permute-start.26 = (bf16[64,384]{1,0:T(8,128)(2,1)S(1)}, bf16[64,384]{1,0:T(8,128)(2,1)S(1)}, u32[]{:S(2)}, u32[]{:S(2)}) collective-permute-start(bf16[64,384]{1,0:T(8,128)(2,1)S(1)} %get-tuple-element.168), channel_id=1, source_target_pairs={{0,8},{4,12},{8,16},{12,20},{16,24},{20,28},{24,0},{28,4},{1,9},{5... | collective-permute-start | bytes 147464 | tf_op jit(solution)/shard_map/ppermute | solution.py:587
  232.7 5.8 %collective-permute-start.27 = (bf16[64,384]{1,0:T(8,128)(2,1)S(1)}, bf16[64,384]{1,0:T(8,128)(2,1)S(1)}, u32[]{:S(2)}, u32[]{:S(2)}) collective-permute-start(bf16[64,384]{1,0:T(8,128)(2,1)S(1)} %get-tuple-element.170), channel_id=1, source_target_pairs={{0,16},{4,20},{8,24},{12,28},{16,0},{20,4},{24,8},{28,12},{1,17},{... | collective-permute-start | bytes 147464 | tf_op jit(solution)/shard_map/ppermute | solution.py:587
  234.2 4.5 %collective-permute-start.28 = (bf16[64,384]{1,0:T(8,128)(2,1)S(1)}, bf16[64,384]{1,0:T(8,128)(2,1)S(1)}, u32[]{:S(2)}, u32[]{:S(2)}) collective-permute-start(bf16[64,384]{1,0:T(8,128)(2,1)S(1)} %get-tuple-element.169), channel_id=1, source_target_pairs={{0,24},{4,28},{8,0},{12,4},{16,8},{20,12},{24,16},{28,20},{1,25},{... | collective-permute-start | bytes 147464 | tf_op jit(solution)/shard_map/ppermute | solution.py:587
  (8 other events, 7.3 us)

commit v6 on v5

--- a/solution.py
+++ b/solution.py
@@ -59,6 +59,10 @@
     mean_scaled = jnp.mean(scaled, axis=-1, keepdims=True)
     mean_along = jnp.mean(scaled * unit, axis=-1, keepdims=True)
     return inverse * (scaled - mean_scaled - unit * mean_along)
+
+
+def in_hbm(value):
+    return pltpu.with_memory_space_constraint(value, pltpu.HBM)
 
 
 def cost(microseconds):
@@ -122,8 +126,8 @@
         ),
         out_shape=[
             jax.ShapeDtypeStruct((length, parts * columns), BF16),
-            jax.ShapeDtypeStruct((features, length), BF16),
-            jax.ShapeDtypeStruct((features, parts * columns), BF16),
+            pltpu.HBM((features, length), BF16),
+            pltpu.HBM((features, parts * columns), BF16),
         ],
         compiler_params=params(20),
         cost_estimate=cost(5),
@@ -211,8 +215,8 @@
             ],
         ),
         out_shape=[
-            jax.ShapeDtypeStruct((length, pairs * PAIR), BF16),
-            jax.ShapeDtypeStruct((pairs * PAIR, length), BF16),
+            pltpu.HBM((length, pairs * PAIR), BF16),
+            pltpu.HBM((pairs * PAIR, length), BF16),
             jax.ShapeDtypeStruct((pairs, 2, length), F32),
         ],
         compiler_params=params(28),
@@ -347,7 +351,7 @@
     length = senders * tokens
     features = feature_parts * width
     parts = len(w_parts)
-    weights = [w for part in w_parts for w in part]
+    weights = [in_hbm(w) for part in w_parts for w in part]
     columns = weights[0].shape[1]
     hidden = (columns - PAIR) // 2
     take = ROWS // tokens
@@ -361,8 +365,8 @@
     grads = lambda first, n: pl.BlockSpec(
         (1, features, n), lambda i, *s: (jnp.clip(i - blocks - first, 0, 1), 0, 0)
     )
-    up_shape = jax.ShapeDtypeStruct((2, features, PAIR + hidden), BF16)
-    down_shape = jax.ShapeDtypeStruct((2, features, hidden), BF16)
+    up_shape = pltpu.HBM((2, features, PAIR + hidden), BF16)
+    down_shape = pltpu.HBM((2, features, hidden), BF16)
     return pl.pallas_call(
         functools.partial(middle_kernel, groups),
         grid_spec=pltpu.PrefetchScalarGridSpec(
@@ -397,15 +401,15 @@
         ),
         out_shape=[
             jax.ShapeDtypeStruct((1, length, features), BF16),
-            jax.ShapeDtypeStruct((length, features), BF16),
-            jax.ShapeDtypeStruct((length, features), F32),
+            pltpu.HBM((length, features), BF16),
+            pltpu.HBM((length, features), F32),
             jax.ShapeDtypeStruct((1, features), F32),
             up_shape, down_shape, up_shape, down_shape,
         ],
-        compiler_params=params(40),
+        compiler_params=params(48),
         cost_estimate=cost(25),
         name="middle",
-    )(limit, place, x_blocks, clock, gain, ctx, out_grad, *weights)
+    )(limit, place, x_blocks, clock, gain, in_hbm(ctx), in_hbm(out_grad), *weights)
 
 
 def attend_back_kernel(
@@ -710,7 +714,7 @@
         qkv_other = across(qkv_rows)
         qkv_parts = collect_columns(jnp.concatenate([qkv_rows, qkv_other], axis=0))
         mine = after(first[:, qkv.shape[1] :], qkv_other)
-        other, far_mine = across(mine), swap(after(mine, qkv_parts[2]), 2)
+        other, far_mine = in_hbm(across(mine)), in_hbm(swap(after(mine, qkv_parts[2]), 2))
     else:
         place, groups = jnp.zeros((1,), jnp.int32), None
         first = collect_rows(qkv)
@@ -737,8 +741,8 @@
     )
     if direct:
         mixed, other = together(mixed, other)
-        near_mine, near_other = swap(after(mine, mixed), 1), swap(other, 1)
-        far_other = swap(other, 2)
+        near_mine, near_other = in_hbm(swap(after(mine, mixed), 1)), in_hbm(swap(other, 1))
+        far_other = in_hbm(swap(other, 2))
     ctx, ctx_turn, lse = attend(limit, mixed, tensor_count)
     if direct:
         ctx, near_mine, near_other, far_mine, far_other = together(

time: 243 us -> 234 us (0.963)
  local copies, waits for them, and re-layouts: 30.8 us -> 15.3 us
  Pallas kernels: 71.1 us -> 84.3 us
  starting transfers between devices: 62.1 us -> 55.7 us
    unnamed x73 -> x45, local copies, waits for them, and re-layouts: 19.3 us -> 3.11 us
    pallas_call x1, Pallas kernels: 20.5 us -> 29.2 us  [middle_block(): pl.pallas_call(functools.partial(middle_kernel, groups), grid_spec=pltpu....]
    ppermute x16, starting transfers between devices: 15.6 us -> 8.96 us  [swap(): return lax.ppermute(value, 'tensor', [(i, i ^ apart) for i in range(count)])]
  transfers between devices with their start and end apart: 36 -> 36, of which waited for: 14 -> 13; matrix products, arithmetic and copies ran while one was open for 6% -> 6% of each run, Pallas kernels for 21% -> 24%
where the time goes in v6:
time: 234 us; the launch traced here: 232 us
  Pallas kernels  84.3 us (36%)
  waiting for transfers between devices  64.6 us (28%)
  starting transfers between devices  55.7 us (24%)
  local copies, waits for them, and re-layouts  15.3 us (7%)
  other arithmetic  8.69 us (4%)
  between operations  3.77 us (2%)
    ppermute x17, waiting for transfers between devices, along_dp(): return lax.ppermute(value, 'dp', [(i, move(i)) for i in range(count)])  57 us
    ppermute x17, starting transfers between devices, along_dp(): return lax.ppermute(value, 'dp', [(i, move(i)) for i in range(count)])  31.7 us
    pallas_call x1, Pallas kernels, middle_block(): pl.pallas_call(functools.partial(middle_kernel, groups), grid_spec=pltpu....  29.2 us
    pallas_call x2, Pallas kernels, attend_back(): pl.pallas_call(attend_back_kernel, grid_spec=pltpu.PrefetchScalarGridSpec...  28.4 us
    pallas_call x1, Pallas kernels, attend(): pl.pallas_call(attend_kernel, grid_spec=pltpu.PrefetchScalarGridSpec(num_...  15.4 us
    ppermute x16, starting transfers between devices, swap(): return lax.ppermute(value, 'tensor', [(i, i ^ apart) for i in range(count)])  8.96 us
    all_to_all x1, starting transfers between devices, on_device(): x_blocks = lax.all_to_all(after(arranged, first), 'dp', 0, 0, tiled=True)  8.09 us
    ppermute x16, waiting for transfers between devices, swap(): return lax.ppermute(value, 'tensor', [(i, i ^ apart) for i in range(count)])  7.55 us
  transfers between devices with their start and end apart: 36, of which 13 were waited for; matrix products, arithmetic and copies ran while one was open for 6% of the time, Pallas kernels for 24%

profile of v6, /device:TPU:0, one launch (start us, length us, event | category | flops | bytes accessed | tf_op | source)
XLA Modules:
  0.0 232.5 jit_solution(13760566302674946607)
XLA Ops:
  0.6 0.8 fusion.12
  1.5 0.7 reshape.155
  2.5 0.7 gather_fusion
  3.3 1.1 pad_maximum_fusion
  4.4 4.4 %all-to-all-start = ((bf16[32,136,128]{2,1,0:T(8,128)(2,1)}), bf16[32,136,128]{2,1,0:T(8,128)(2,1)S(1)}, u32[]{:S(2)}, u32[]{:S(2)}) async-start(bf16[32,136,128]{2,1,0:T(8,128)(2,1)} %pad_maximum_fusion), calls=%async_computation | async-start | bytes 2228224 | tf_op jit(solution)/shard_map/all_to_all | solution.py:730
  8.8 2.4 %collective-permute-start = (bf16[64,1536]{1,0:T(8,128)(2,1)S(1)}, bf16[64,1536]{1,0:T(8,128)(2,1)S(1)}, u32[]{:S(2)}, u32[]{:S(2)}) collective-permute-start(bf16[64,1536]{1,0:T(8,128)(2,1)S(1)} %pad_maximum_fusion.3), channel_id=1, source_target_pairs={{0,8},{4,12},{8,16},{12,20},{16,24},{20,28},{24,0},{28,4},{1,9},{5... | collective-permute-start | bytes 589832 | tf_op jit(solution)/shard_map/ppermute | solution.py:591
  11.2 2.6 %collective-permute-start.1 = (bf16[64,1536]{1,0:T(8,128)(2,1)S(1)}, bf16[64,1536]{1,0:T(8,128)(2,1)S(1)}, u32[]{:S(2)}, u32[]{:S(2)}) collective-permute-start(bf16[64,1536]{1,0:T(8,128)(2,1)S(1)} %pad_maximum_fusion.3), channel_id=1, source_target_pairs={{0,16},{4,20},{8,24},{12,28},{16,0},{20,4},{24,8},{28,12},{1,17},{... | collective-permute-start | bytes 589832 | tf_op jit(solution)/shard_map/ppermute | solution.py:591
  13.8 1.3 collective-permute-start.2
  15.2 4.0 %collective-permute-done = bf16[64,1536]{1,0:T(8,128)(2,1)S(1)} collective-permute-done((bf16[64,1536]{1,0:T(8,128)(2,1)S(1)}, bf16[64,1536]{1,0:T(8,128)(2,1)S(1)}, u32[]{:S(2)}, u32[]{:S(2)}) %collective-permute-start) | collective-permute-done | bytes 196640 | tf_op jit(solution)/shard_map/ppermute | solution.py:591
  19.2 8.2 %collective-permute-done.1 = bf16[64,1536]{1,0:T(8,128)(2,1)S(1)} collective-permute-done((bf16[64,1536]{1,0:T(8,128)(2,1)S(1)}, bf16[64,1536]{1,0:T(8,128)(2,1)S(1)}, u32[]{:S(2)}, u32[]{:S(2)}) %collective-permute-start.1) | collective-permute-done | bytes 196640 | tf_op jit(solution)/shard_map/ppermute | solution.py:591
  27.4 1.2 copy.68
  28.6 8.1 %all-to-all-start.1 = ((bf16[8,4,136,128]{3,2,1,0:T(8,128)(2,1)}), bf16[8,4,136,128]{3,2,1,0:T(8,128)(2,1)S(1)}, u32[]{:S(2)}, u32[]{:S(2)}) async-start(bf16[8,4,136,128]{3,2,1,0:T(8,128)(2,1)} %bitcast.118), calls=%async_computation.1 | async-start | bytes 2228224 | tf_op jit(solution)/shard_map/all_to_all | solution.py:732
  36.8 2.1 collective-permute-start.3
  38.8 13.3 %collective-permute-done.3 = bf16[256,384]{1,0:T(8,128)(2,1)S(1)} collective-permute-done((bf16[256,384]{1,0:T(8,128)(2,1)S(1)}, bf16[256,384]{1,0:T(8,128)(2,1)S(1)}, u32[]{:S(2)}, u32[]{:S(2)}) %collective-permute-start.3) | collective-permute-done | bytes 196640 | tf_op jit(solution)/shard_map/ppermute | solution.py:591
  52.2 1.6 collective-permute-start.5
  56.4 0.6 dynamic-slice.10
  57.8 3.0 %collective-permute-done.5.refs_2_ = bf16[512,384]{1,0:T(8,128)(2,1)S(1)} collective-permute-done((bf16[512,384]{1,0:T(8,128)(2,1)S(1)}, bf16[512,384]{1,0:T(8,128)(2,1)S(1)}, u32[]{:S(2)}, u32[]{:S(2)}) %collective-permute-start.5) | collective-permute-done | bytes 393248 | tf_op jit(solution)/shard_map/ppermute | solution.py:586
  60.9 0.6 dynamic-slice.9.limit_ref
  61.5 1.9 slice.92.refs_0_
  63.4 2.5 %collective-permute-start.7 = (bf16[256,1152]{1,0:T(8,128)(2,1)}, bf16[256,1152]{1,0:T(8,128)(2,1)}, u32[]{:S(2)}, u32[]{:S(2)}) collective-permute-start(bf16[256,1152]{1,0:T(8,128)(2,1)} %slice.92.refs_0_), channel_id=1, source_target_pairs={{0,4},{4,0},{8,12},{12,8},{16,20},{20,16},{24,28},{28,24},{1,5},{5... | collective-permute-start | bytes 1769480 | tf_op jit(solution)/shard_map/ppermute | solution.py:591
  65.9 1.2 collective-permute-start.10
  67.5 6.2 %project.1 = (bf16[1024,1536]{1,0:T(8,128)(2,1)S(1)}, bf16[512,1024]{1,0:T(8,128)(2,1)}, bf16[512,1536]{1,0:T(8,128)(2,1)}) custom-call(s32[1]{0:T(128)} %dynamic-slice.9.limit_ref, s32[8]{0:T(128)S(1)} %pad_add_fusion.place_ref, bf16[8,4,136,128]{3,2,1,0:T(8,128)(2,1)S(1)} %all-to-all-done.1.x_ref, f32[1,512]{1,0:T(1,128)S(1)} %pad_maximum_fusion.4.clock_ref, ...), custom_call_target="tpu_custom_call" | custom-call | flops 5750000128 | bytes 1048576 | tf_op jit(solution)/shard_map/project/pallas_call | solution.py:110
  73.7 6.5 %collective-permute-done.7.refs_1_ = bf16[256,1152]{1,0:T(8,128)(2,1)} collective-permute-done((bf16[256,1152]{1,0:T(8,128)(2,1)}, bf16[256,1152]{1,0:T(8,128)(2,1)}, u32[]{:S(2)}, u32[]{:S(2)}) %collective-permute-start.7) | collective-permute-done | bytes 589856 | tf_op jit(solution)/shard_map/ppermute | solution.py:591
  80.2 1.2 collective-permute-start.11
  82.0 15.4 %attend.1 = (bf16[1024,512]{1,0:T(8,128)(2,1)}, bf16[512,1024]{1,0:T(8,128)(2,1)}, f32[4,2,1024]{2,1,0:T(2,128)S(1)}) custom-call(s32[1]{0:T(128)} %dynamic-slice.9.limit_ref, bf16[1024,1536]{1,0:T(8,128)(2,1)S(1)} %get-tuple-element.67.q_ref.k_ref.v_ref, bf16[1024,1536]{1,0:T(8,128)(2,1)S(1)} %get-tuple-element.67.q_ref.k_ref.v_ref, ...), custom_call_target="tpu_custom_call" | custom-call | flops 17250000896 | bytes 1048576 | tf_op jit(solution)/shard_map/attend/pallas_call | solution.py:199
  98.6 1.3 collective-permute-done.12.refs_6_
  99.9 0.6 collective-permute-done.13.refs_7_
  100.5 29.2 %middle.1 = (bf16[1,1024,512]{2,1,0:T(8,128)(2,1)}, bf16[1024,512]{1,0:T(8,128)(2,1)}, f32[1024,512]{1,0:T(8,128)}, f32[1,512]{1,0:T(1,128)S(1)}, bf16[2,512,640...) custom-call(s32[1]{0:T(128)} %dynamic-slice.9.limit_ref, ...), custom_call_target="tpu_custom_call" | custom-call | flops 28750000128 | bytes 1048576 | tf_op jit(solution)/shard_map/middle/pallas_call | solution.py:370
  130.2 2.6 %collective-permute-done.15 = bf16[2,512,512]{2,1,0:T(8,128)(2,1)} collective-permute-done((bf16[2,512,512]{2,1,0:T(8,128)(2,1)}, bf16[2,512,512]{2,1,0:T(8,128)(2,1)}, u32[]{:S(2)}, u32[]{:S(2)}) %collective-permute-start.15) | collective-permute-done | bytes 1048608 | tf_op jit(solution)/shard_map/ppermute | solution.py:586
  132.8 2.0 convert_add_fusion
  134.8 0.9 collective-permute-start.16
  135.7 1.2 fusion.1
  136.9 2.4 %collective-permute-start.17 = (bf16[2,4,64,640]{3,2,1,0:T(8,128)(2,1)S(1)}, bf16[2,4,64,640]{3,2,1,0:T(8,128)(2,1)S(1)}, u32[]{:S(2)}, u32[]{:S(2)}) collective-permute-start(bf16[2,4,64,640]{3,2,1,0:T(8,128)(2,1)S(1)} %fusion.1), channel_id=1, source_target_pairs={{0,4},{4,0},{8,12},{12,8},{16,20},{20,16},{24,28},{28,24},{1,5},{5... | collective-permute-start | bytes 1966088 | tf_op jit(solution)/shard_map/ppermute | solution.py:591
  139.3 1.2 copy-done.7
  140.6 14.2 %attend_back.2 = (bf16[1024,768]{1,0:T(8,128)(2,1)S(1)}, bf16[512,384]{1,0:T(8,128)(2,1)S(1)}, bf16[512,384]{1,0:T(8,128)(2,1)S(1)}) custom-call(s32[1]{0:T(128)} %dynamic-slice.9.limit_ref, bf16[1024,1536]{1,0:T(8,128)(2,1)S(1)} %copy-done.2, bf16[1024,1536]{1,0:T(8,128)(2,1)S(1)} %copy-done.2, bf16[1024,1536]{1,0:T(8,128)(2,1)S(1)} %copy-done.2, ...), custom_call_target="tpu_custom_call" | custom-call | flops 18400000000 | bytes 1048576 | tf_op jit(solution)/shard_map/attend_back/pallas_call | solution.py:465
  155.2 1.3 collective-permute-start.19
  157.2 3.6 %collective-permute-start.22 = (bf16[2,64,512]{2,1,0:T(8,128)(2,1)S(1)}, bf16[2,64,512]{2,1,0:T(8,128)(2,1)S(1)}, u32[]{:S(2)}, u32[]{:S(2)}) collective-permute-start(bf16[2,64,512]{2,1,0:T(8,128)(2,1)S(1)} %get-tuple-element.161), channel_id=1, source_target_pairs={{0,16},{4,20},{8,24},{12,28},{16,0},{20,4},{24,8},{28,12},{1,17},{... | collective-permute-start | bytes 393224 | tf_op jit(solution)/shard_map/ppermute | solution.py:591
  160.8 2.2 collective-permute-start.23
  163.1 0.9 collective-permute-start.20
  164.0 14.3 %attend_back.3 = (bf16[1024,768]{1,0:T(8,128)(2,1)S(1)}, bf16[512,384]{1,0:T(8,128)(2,1)S(1)}, bf16[512,384]{1,0:T(8,128)(2,1)S(1)}) custom-call(s32[1]{0:T(128)} %dynamic-slice.9.limit_ref, bf16[1024,1536]{1,0:T(8,128)(2,1)S(1)} %copy-done.2, bf16[1024,1536]{1,0:T(8,128)(2,1)S(1)} %copy-done.2, bf16[1024,1536]{1,0:T(8,128)(2,1)S(1)} %copy-done.2, ...), custom_call_target="tpu_custom_call" | custom-call | flops 18400000000 | bytes 1048576 | tf_op jit(solution)/shard_map/attend_back/pallas_call | solution.py:465
  178.5 0.6 dynamic-slice_convert_fusion
  179.7 5.1 %begin_back.1 = bf16[8,4,136,128]{3,2,1,0:T(8,128)(2,1)} custom-call(s32[1]{0:T(128)} %dynamic-slice.9.limit_ref, bf16[8,4,136,128]{3,2,1,0:T(8,128)(2,1)S(1)} %all-to-all-done.1.x_ref, f32[1,512]{1,0:T(1,128)S(1)} %pad_maximum_fusion.4.clock_ref, f32[1,512]{1,0:T(1,128)S(1)} %reshape_squeeze.8.gain_ref, f32[1,512]{1,0:T(1,128)S(1)} %get-tuple-element.78.gg_two_ref, ...), custom_call_target="tpu_custom_call" | custom-call | flops 8049999872 | bytes 1048576 | tf_op jit(solution)/shard_map/begin_back/pallas_call | solution.py:553
  184.8 0.7 copy-done.10
  185.5 2.7 %all-to-all-start.2 = ((bf16[32,136,128]{2,1,0:T(8,128)(2,1)}), bf16[32,136,128]{2,1,0:T(8,128)(2,1)S(1)}, u32[]{:S(2)}, u32[]{:S(2)}) async-start(bf16[32,136,128]{2,1,0:T(8,128)(2,1)} %bitcast.28), calls=%async_computation.2 | async-start | bytes 2228224 | tf_op jit(solution)/shard_map/all_to_all | solution.py:800
  188.2 0.7 scatter_custom_fusion
  188.9 1.1 fusion.4
  190.0 1.7 collective-permute-start.25
  192.1 1.7 collective-permute-start.29
  193.9 2.5 %collective-permute-start.30 = (bf16[64,640]{1,0:T(8,128)(2,1)S(1)}, bf16[64,640]{1,0:T(8,128)(2,1)S(1)}, u32[]{:S(2)}, u32[]{:S(2)}) collective-permute-start(bf16[64,640]{1,0:T(8,128)(2,1)S(1)} %get-tuple-element.165), channel_id=1, source_target_pairs={{0,16},{4,20},{8,24},{12,28},{16,0},{20,4},{24,8},{28,12},{1,17},{... | collective-permute-start | bytes 245768 | tf_op jit(solution)/shard_map/ppermute | solution.py:591
  196.4 1.4 collective-permute-start.31
  197.7 5.8 %collective-permute-done.25 = bf16[4,64,384]{2,1,0:T(8,128)(2,1)S(1)} collective-permute-done((bf16[4,64,384]{2,1,0:T(8,128)(2,1)S(1)}, bf16[4,64,384]{2,1,0:T(8,128)(2,1)S(1)}, u32[]{:S(2)}, u32[]{:S(2)}) %collective-permute-start.25) | collective-permute-done | bytes 196640 | tf_op jit(solution)/shard_map/ppermute | solution.py:591
  203.6 2.3 collective-permute-done.32
  205.9 7.1 %collective-permute-done.29 = bf16[64,640]{1,0:T(8,128)(2,1)S(1)} collective-permute-done((bf16[64,640]{1,0:T(8,128)(2,1)S(1)}, bf16[64,640]{1,0:T(8,128)(2,1)S(1)}, u32[]{:S(2)}, u32[]{:S(2)}) %collective-permute-start.29) | collective-permute-done | bytes 81952 | tf_op jit(solution)/shard_map/ppermute | solution.py:591
  213.0 8.5 %collective-permute-done.30 = bf16[64,640]{1,0:T(8,128)(2,1)S(1)} collective-permute-done((bf16[64,640]{1,0:T(8,128)(2,1)S(1)}, bf16[64,640]{1,0:T(8,128)(2,1)S(1)}, u32[]{:S(2)}, u32[]{:S(2)}) %collective-permute-start.30) | collective-permute-done | bytes 81952 | tf_op jit(solution)/shard_map/ppermute | solution.py:591
  221.6 1.9 collective-permute-start.26
  223.5 1.2 collective-permute-start.27
  224.7 1.3 collective-permute-start.28
  225.9 0.7 add_bitcast_fusion
  226.6 0.6 slice_bitcast_fusion.2
  227.2 0.7 slice.99
  227.9 1.4 collective-permute-done.27
  229.3 0.7 copy_bitcast_fusion.1
  230.0 0.8 gather_fusion.1
  230.7 1.1 slice.97
  (121 shorter events, 7.0 us)
Async XLA Ops:
  0.6 1.8 copy-start
  4.4 4.4 %copy-start.15 = (bf16[64,3,128]{2,0,1:T(8,128)(2,1)S(1)}, bf16[64,3,128]{2,0,1:T(8,128)(2,1)}, u32[]{:S(2)}) copy-start(bf16[64,3,128]{2,0,1:T(8,128)(2,1)} %param.15) | copy-start | bytes 147460
  4.4 4.4 %copy-start.12 = (bf16[512,64]{0,1:T(8,128)(2,1)S(1)}, bf16[512,64]{0,1:T(8,128)(2,1)}, u32[]{:S(2)}) copy-start(bf16[512,64]{0,1:T(8,128)(2,1)} %param.18) | copy-start | bytes 196612
  4.4 4.4 %copy-start.13 = (bf16[64,512]{1,0:T(8,128)(2,1)S(1)}, bf16[64,512]{1,0:T(8,128)(2,1)}, u32[]{:S(2)}) copy-start(bf16[64,512]{1,0:T(8,128)(2,1)} %param.17) | copy-start | bytes 196612
  4.4 4.4 %copy-start.14 = (bf16[128,64]{0,1:T(8,128)(2,1)S(1)}, bf16[128,64]{0,1:T(8,128)(2,1)}, u32[]{:S(2)}) copy-start(bf16[128,64]{0,1:T(8,128)(2,1)} %param.16) | copy-start | bytes 49156
  4.4 23.0 %all-to-all-start = ((bf16[32,136,128]{2,1,0:T(8,128)(2,1)}), bf16[32,136,128]{2,1,0:T(8,128)(2,1)S(1)}, u32[]{:S(2)}, u32[]{:S(2)}) async-start(bf16[32,136,128]{2,1,0:T(8,128)(2,1)} %pad_maximum_fusion), calls=%async_computation | async-start | bytes 2228224 | tf_op jit(solution)/shard_map/all_to_all | solution.py:730
  8.8 10.3 %collective-permute-start = (bf16[64,1536]{1,0:T(8,128)(2,1)S(1)}, bf16[64,1536]{1,0:T(8,128)(2,1)S(1)}, u32[]{:S(2)}, u32[]{:S(2)}) collective-permute-start(bf16[64,1536]{1,0:T(8,128)(2,1)S(1)} %pad_maximum_fusion.3), channel_id=1, source_target_pairs={{0,8},{4,12},{8,16},{12,20},{16,24},{20,28},{24,0},{28,4},{1,9},{5... | collective-permute-start | bytes 589832 | tf_op jit(solution)/shard_map/ppermute | solution.py:591
  11.2 16.1 %collective-permute-start.1 = (bf16[64,1536]{1,0:T(8,128)(2,1)S(1)}, bf16[64,1536]{1,0:T(8,128)(2,1)S(1)}, u32[]{:S(2)}, u32[]{:S(2)}) collective-permute-start(bf16[64,1536]{1,0:T(8,128)(2,1)S(1)} %pad_maximum_fusion.3), channel_id=1, source_target_pairs={{0,16},{4,20},{8,24},{12,28},{16,0},{20,4},{24,8},{28,12},{1,17},{... | collective-permute-start | bytes 589832 | tf_op jit(solution)/shard_map/ppermute | solution.py:591
  13.8 13.5 %collective-permute-start.2 = (bf16[64,1536]{1,0:T(8,128)(2,1)S(1)}, bf16[64,1536]{1,0:T(8,128)(2,1)S(1)}, u32[]{:S(2)}, u32[]{:S(2)}) collective-permute-start(bf16[64,1536]{1,0:T(8,128)(2,1)S(1)} %pad_maximum_fusion.3), channel_id=1, source_target_pairs={{0,24},{4,28},{8,0},{12,4},{16,8},{20,12},{24,16},{28,20},{1,25},{... | collective-permute-start | bytes 589832 | tf_op jit(solution)/shard_map/ppermute | solution.py:591
  27.4 9.3 %copy-start.8 = (bf16[256,1536]{1,0:T(8,128)(2,1)}, bf16[256,1536]{1,0:T(8,128)(2,1)S(1)}, u32[]{:S(2)}) copy-start(bf16[256,1536]{1,0:T(8,128)(2,1)S(1)} %pad_maximum_fusion.1) | copy-start | bytes 2359300
  28.6 25.2 %copy-start.16 = (s32[32]{0:T(128)S(1)}, s32[32]{0:T(128)}, u32[]{:S(2)}) copy-start(s32[32]{0:T(128)} %param.14) | copy-start | bytes 388
  28.6 27.7 %copy-start.20 = (s32[32]{0:T(128)S(1)}, s32[32]{0:T(128)}, u32[]{:S(2)}) copy-start(s32[32]{0:T(128)} %param.12) | copy-start | bytes 388
  28.6 32.3 %copy-start.21 = (s32[32]{0:T(128)S(1)}, s32[32]{0:T(128)}, u32[]{:S(2)}) copy-start(s32[32]{0:T(128)} %param.13) | copy-start | bytes 388
  28.6 38.5 %all-to-all-start.1 = ((bf16[8,4,136,128]{3,2,1,0:T(8,128)(2,1)}), bf16[8,4,136,128]{3,2,1,0:T(8,128)(2,1)S(1)}, u32[]{:S(2)}, u32[]{:S(2)}) async-start(bf16[8,4,136,128]{3,2,1,0:T(8,128)(2,1)} %bitcast.118), calls=%async_computation.1 | async-start | bytes 2228224 | tf_op jit(solution)/shard_map/all_to_all | solution.py:732
  36.8 15.4 %collective-permute-start.3 = (bf16[256,384]{1,0:T(8,128)(2,1)S(1)}, bf16[256,384]{1,0:T(8,128)(2,1)S(1)}, u32[]{:S(2)}, u32[]{:S(2)}) collective-permute-start(bf16[256,384]{1,0:T(8,128)(2,1)S(1)} %slice.91), channel_id=1, source_target_pairs={{0,4},{4,0},{8,12},{12,8},{16,20},{20,16},{24,28},{28,24},{1,5},{5... | collective-permute-start | bytes 589832 | tf_op jit(solution)/shard_map/ppermute | solution.py:591
  52.2 8.6 %collective-permute-start.5 = (bf16[512,384]{1,0:T(8,128)(2,1)S(1)}, bf16[512,384]{1,0:T(8,128)(2,1)S(1)}, u32[]{:S(2)}, u32[]{:S(2)}) collective-permute-start(bf16[512,384]{1,0:T(8,128)(2,1)S(1)} %pad_maximum_fusion.2.refs_0_), channel_id=1, source_target_pairs={{0,2},{1,3},{2,0},{3,1},{4,6},{5,7},{6,4},{7,5},{8,10},{9,11},{10,... | collective-permute-start | bytes 1179656 | tf_op jit(solution)/shard_map/ppermute | solution.py:586
  57.7 9.8 %collective-permute-start.4 = (bf16[512,384]{1,0:T(8,128)(2,1)S(1)}, bf16[512,384]{1,0:T(8,128)(2,1)S(1)}, u32[]{:S(2)}, u32[]{:S(2)}) collective-permute-start(bf16[512,384]{1,0:T(8,128)(2,1)S(1)} %pad_maximum_fusion.2.refs_0_), channel_id=1, source_target_pairs={{0,1},{1,0},{2,3},{3,2},{4,5},{5,4},{6,7},{7,6},{8,9},{9,8},{10,11... | collective-permute-start | bytes 1179656 | tf_op jit(solution)/shard_map/ppermute | solution.py:586
  60.8 6.7 %collective-permute-start.6 = (bf16[512,384]{1,0:T(8,128)(2,1)S(1)}, bf16[512,384]{1,0:T(8,128)(2,1)}, u32[]{:S(2)}, u32[]{:S(2)}) collective-permute-start(bf16[512,384]{1,0:T(8,128)(2,1)S(1)} %collective-permute-done.5.refs_2_), channel_id=1, source_target_pairs={{0,1},{1,0},{2,3},{3,2},{4,5},{5,4},{6,7},{7,6},{8,9},{9,8},{10,11... | collective-permute-start | bytes 1179656 | tf_op jit(solution)/shard_map/ppermute | solution.py:586
  63.4 16.8 %collective-permute-start.7 = (bf16[256,1152]{1,0:T(8,128)(2,1)}, bf16[256,1152]{1,0:T(8,128)(2,1)}, u32[]{:S(2)}, u32[]{:S(2)}) collective-permute-start(bf16[256,1152]{1,0:T(8,128)(2,1)} %slice.92.refs_0_), channel_id=1, source_target_pairs={{0,4},{4,0},{8,12},{12,8},{16,20},{20,16},{24,28},{28,24},{1,5},{5... | collective-permute-start | bytes 1769480 | tf_op jit(solution)/shard_map/ppermute | solution.py:591
  65.9 31.4 %collective-permute-start.10 = (bf16[256,1152]{1,0:T(8,128)(2,1)}, bf16[256,1152]{1,0:T(8,128)(2,1)}, u32[]{:S(2)}, u32[]{:S(2)}) collective-permute-start(bf16[256,1152]{1,0:T(8,128)(2,1)} %slice.92.refs_0_), channel_id=1, source_target_pairs={{0,2},{1,3},{2,0},{3,1},{4,6},{5,7},{6,4},{7,5},{8,10},{9,11},{10,... | collective-permute-start | bytes 1769480 | tf_op jit(solution)/shard_map/ppermute | solution.py:586
  73.7 23.6 %copy-start.1 = (bf16[1024,1536]{1,0:T(8,128)(2,1)}, bf16[1024,1536]{1,0:T(8,128)(2,1)S(1)}, u32[]{:S(2)}) copy-start(bf16[1024,1536]{1,0:T(8,128)(2,1)S(1)} %get-tuple-element.67.q_ref.k_ref.v_ref) | copy-start | bytes 9437188
  80.2 17.1 %collective-permute-start.11 = (bf16[256,1152]{1,0:T(8,128)(2,1)}, bf16[256,1152]{1,0:T(8,128)(2,1)S(1)}, u32[]{:S(2)}, u32[]{:S(2)}) collective-permute-start(bf16[256,1152]{1,0:T(8,128)(2,1)} %collective-permute-done.7.refs_1_), channel_id=1, source_target_pairs={{0,2},{1,3},{2,0},{3,1},{4,6},{5,7},{6,4},{7,5},{8,10},{9,11},{10,... | collective-permute-start | bytes 1769480 | tf_op jit(solution)/shard_map/ppermute | solution.py:586
  81.5 15.9 %collective-permute-start.9 = (bf16[256,1152]{1,0:T(8,128)(2,1)}, bf16[256,1152]{1,0:T(8,128)(2,1)S(1)}, u32[]{:S(2)}, u32[]{:S(2)}) collective-permute-start(bf16[256,1152]{1,0:T(8,128)(2,1)} %collective-permute-done.7.refs_1_), channel_id=1, source_target_pairs={{0,1},{1,0},{2,3},{3,2},{4,5},{5,4},{6,7},{7,6},{8,9},{9,8},{10,11... | collective-permute-start | bytes 1769480 | tf_op jit(solution)/shard_map/ppermute | solution.py:586
  81.5 15.9 %collective-permute-start.8 = (bf16[256,1152]{1,0:T(8,128)(2,1)}, bf16[256,1152]{1,0:T(8,128)(2,1)S(1)}, u32[]{:S(2)}, u32[]{:S(2)}) collective-permute-start(bf16[256,1152]{1,0:T(8,128)(2,1)} %slice.92.refs_0_), channel_id=1, source_target_pairs={{0,1},{1,0},{2,3},{3,2},{4,5},{5,4},{6,7},{7,6},{8,9},{9,8},{10,11... | collective-permute-start | bytes 1769480 | tf_op jit(solution)/shard_map/ppermute | solution.py:586
  97.4 1.0 copy-start.19
  97.4 3.1 %copy-start.17 = (bf16[256,1152]{1,0:T(8,128)(2,1)}, bf16[256,1152]{1,0:T(8,128)(2,1)S(1)}, u32[]{:S(2)}) copy-start(bf16[256,1152]{1,0:T(8,128)(2,1)S(1)} %collective-permute-done.11.refs_5_) | copy-start | bytes 1769476
  97.4 1.0 copy-start.18
  97.4 2.5 %collective-permute-start.12 = (bf16[256,1152]{1,0:T(8,128)(2,1)}, bf16[256,1152]{1,0:T(8,128)(2,1)}, u32[]{:S(2)}, u32[]{:S(2)}) collective-permute-start(bf16[256,1152]{1,0:T(8,128)(2,1)} %collective-permute-done.10.refs_4_), channel_id=1, source_target_pairs={{0,1},{1,0},{2,3},{3,2},{4,5},{5,4},{6,7},{7,6},{8,9},{9,8},{10,11... | collective-permute-start | bytes 1769480 | tf_op jit(solution)/shard_map/ppermute | solution.py:586
  97.5 3.0 %collective-permute-start.13 = (bf16[256,1152]{1,0:T(8,128)(2,1)S(1)}, bf16[256,1152]{1,0:T(8,128)(2,1)}, u32[]{:S(2)}, u32[]{:S(2)}) collective-permute-start(bf16[256,1152]{1,0:T(8,128)(2,1)S(1)} %collective-permute-done.11.refs_5_), channel_id=1, source_target_pairs={{0,1},{1,0},{2,3},{3,2},{4,5},{5,4},{6,7},{7,6},{8,9},{9,8},{10,11... | collective-permute-start | bytes 1769480 | tf_op jit(solution)/shard_map/ppermute | solution.py:586
  129.7 3.2 %collective-permute-start.15 = (bf16[2,512,512]{2,1,0:T(8,128)(2,1)}, bf16[2,512,512]{2,1,0:T(8,128)(2,1)}, u32[]{:S(2)}, u32[]{:S(2)}) collective-permute-start(bf16[2,512,512]{2,1,0:T(8,128)(2,1)} %get-tuple-element.86), channel_id=1, source_target_pairs={{0,1},{1,0},{2,3},{3,2},{4,5},{5,4},{6,7},{7,6},{8,9},{9,8},{10,11... | collective-permute-start | bytes 3145736 | tf_op jit(solution)/shard_map/ppermute | solution.py:586
  129.9 5.8 %collective-permute-start.14 = (bf16[2,512,640]{2,1,0:T(8,128)(2,1)}, bf16[2,512,640]{2,1,0:T(8,128)(2,1)S(1)}, u32[]{:S(2)}, u32[]{:S(2)}) collective-permute-start(bf16[2,512,640]{2,1,0:T(8,128)(2,1)} %get-tuple-element.81), channel_id=1, source_target_pairs={{0,1},{1,0},{2,3},{3,2},{4,5},{5,4},{6,7},{7,6},{8,9},{9,8},{10,11... | collective-permute-start | bytes 3932168 | tf_op jit(solution)/shard_map/ppermute | solution.py:586
  132.8 6.5 %copy-start.2 = (bf16[1024,1536]{1,0:T(8,128)(2,1)S(1)}, bf16[1024,1536]{1,0:T(8,128)(2,1)}, u32[]{:S(2)}) copy-start(bf16[1024,1536]{1,0:T(8,128)(2,1)} %copy-done.1) | copy-start | bytes 9437188
  132.8 6.5 %copy-start.6 = (bf16[512,1024]{1,0:T(8,128)(2,1)S(1)}, bf16[512,1024]{1,0:T(8,128)(2,1)}, u32[]{:S(2)}) copy-start(bf16[512,1024]{1,0:T(8,128)(2,1)} %get-tuple-element.82.turn_ref) | copy-start | bytes 3145732
  134.8 4.5 %copy-start.5 = (bf16[512,1024]{1,0:T(8,128)(2,1)S(1)}, bf16[512,1024]{1,0:T(8,128)(2,1)}, u32[]{:S(2)}) copy-start(bf16[512,1024]{1,0:T(8,128)(2,1)} %get-tuple-element.88.n_turn_ref) | copy-start | bytes 3145732
  134.8 20.0 %collective-permute-start.16 = (bf16[4,2,64,512]{3,2,1,0:T(8,128)(2,1)S(1)}, bf16[4,2,64,512]{3,2,1,0:T(8,128)(2,1)S(1)}, u32[]{:S(2)}, u32[]{:S(2)}) collective-permute-start(bf16[4,2,64,512]{3,2,1,0:T(8,128)(2,1)S(1)} %bitcast.128), channel_id=1, source_target_pairs={{0,2},{1,3},{2,0},{3,1},{4,6},{5,7},{6,4},{7,5},{8,10},{9,11},{10,... | collective-permute-start | bytes 1572872 | tf_op jit(solution)/shard_map/ppermute | solution.py:586
  136.9 17.8 %collective-permute-start.17 = (bf16[2,4,64,640]{3,2,1,0:T(8,128)(2,1)S(1)}, bf16[2,4,64,640]{3,2,1,0:T(8,128)(2,1)S(1)}, u32[]{:S(2)}, u32[]{:S(2)}) collective-permute-start(bf16[2,4,64,640]{3,2,1,0:T(8,128)(2,1)S(1)} %fusion.1), channel_id=1, source_target_pairs={{0,4},{4,0},{8,12},{12,8},{16,20},{20,16},{24,28},{28,24},{1,5},{5... | collective-permute-start | bytes 1966088 | tf_op jit(solution)/shard_map/ppermute | solution.py:591
  139.3 1.2 copy-start.7
  140.6 14.3 %copy-start.9 = (bf16[2,512,640]{2,1,0:T(8,128)(2,1)S(1)}, bf16[2,512,640]{2,1,0:T(8,128)(2,1)}, u32[]{:S(2)}) copy-start(bf16[2,512,640]{2,1,0:T(8,128)(2,1)} %get-tuple-element.80) | copy-start | bytes 3932164
  154.8 8.2 %collective-permute-start.18 = (bf16[512,384]{1,0:T(8,128)(2,1)S(1)}, bf16[512,384]{1,0:T(8,128)(2,1)S(1)}, u32[]{:S(2)}, u32[]{:S(2)}) collective-permute-start(bf16[512,384]{1,0:T(8,128)(2,1)S(1)} %get-tuple-element.97), channel_id=1, source_target_pairs={{0,1},{1,0},{2,3},{3,2},{4,5},{5,4},{6,7},{7,6},{8,9},{9,8},{10,11... | collective-permute-start | bytes 1179656 | tf_op jit(solution)/shard_map/ppermute | solution.py:586
  155.2 23.1 %collective-permute-start.19 = (bf16[4,64,640]{2,1,0:T(8,128)(2,1)S(1)}, bf16[4,64,640]{2,1,0:T(8,128)(2,1)S(1)}, u32[]{:S(2)}, u32[]{:S(2)}) collective-permute-start(bf16[4,64,640]{2,1,0:T(8,128)(2,1)S(1)} %slice_bitcast_fusion), channel_id=1, source_target_pairs={{0,2},{1,3},{2,0},{3,1},{4,6},{5,7},{6,4},{7,5},{8,10},{9,11},{10,... | collective-permute-start | bytes 983048 | tf_op jit(solution)/shard_map/ppermute | solution.py:586
  156.7 21.6 %collective-permute-start.21 = (bf16[2,64,512]{2,1,0:T(8,128)(2,1)S(1)}, bf16[2,64,512]{2,1,0:T(8,128)(2,1)S(1)}, u32[]{:S(2)}, u32[]{:S(2)}) collective-permute-start(bf16[2,64,512]{2,1,0:T(8,128)(2,1)S(1)} %get-tuple-element.162), channel_id=1, source_target_pairs={{0,8},{4,12},{8,16},{12,20},{16,24},{20,28},{24,0},{28,4},{1,9},{5... | collective-permute-start | bytes 393224 | tf_op jit(solution)/shard_map/ppermute | solution.py:591
  157.2 21.1 %collective-permute-start.22 = (bf16[2,64,512]{2,1,0:T(8,128)(2,1)S(1)}, bf16[2,64,512]{2,1,0:T(8,128)(2,1)S(1)}, u32[]{:S(2)}, u32[]{:S(2)}) collective-permute-start(bf16[2,64,512]{2,1,0:T(8,128)(2,1)S(1)} %get-tuple-element.161), channel_id=1, source_target_pairs={{0,16},{4,20},{8,24},{12,28},{16,0},{20,4},{24,8},{28,12},{1,17},{... | collective-permute-start | bytes 393224 | tf_op jit(solution)/shard_map/ppermute | solution.py:591
  160.8 17.5 %collective-permute-start.23 = (bf16[2,64,512]{2,1,0:T(8,128)(2,1)S(1)}, bf16[2,64,512]{2,1,0:T(8,128)(2,1)S(1)}, u32[]{:S(2)}, u32[]{:S(2)}) collective-permute-start(bf16[2,64,512]{2,1,0:T(8,128)(2,1)S(1)} %get-tuple-element.160), channel_id=1, source_target_pairs={{0,24},{4,28},{8,0},{12,4},{16,8},{20,12},{24,16},{28,20},{1,25},{... | collective-permute-start | bytes 393224 | tf_op jit(solution)/shard_map/ppermute | solution.py:591
  163.1 15.2 %collective-permute-start.20 = (bf16[512,384]{1,0:T(8,128)(2,1)S(1)}, bf16[512,384]{1,0:T(8,128)(2,1)S(1)}, u32[]{:S(2)}, u32[]{:S(2)}) collective-permute-start(bf16[512,384]{1,0:T(8,128)(2,1)S(1)} %add_convert_fusion.3), channel_id=1, source_target_pairs={{0,2},{1,3},{2,0},{3,1},{4,6},{5,7},{6,4},{7,5},{8,10},{9,11},{10,... | collective-permute-start | bytes 1179656 | tf_op jit(solution)/shard_map/ppermute | solution.py:586
  164.0 15.1 %copy-start.3 = (f32[1024,512]{1,0:T(8,128)S(1)}, f32[1024,512]{1,0:T(8,128)}, u32[]{:S(2)}) copy-start(f32[1024,512]{1,0:T(8,128)} %get-tuple-element.107.mg_ref) | copy-start | bytes 6291460
  178.2 1.4 copy-start.4
  179.1 5.7 %collective-permute-start.24 = (bf16[512,384]{1,0:T(8,128)(2,1)S(1)}, bf16[512,384]{1,0:T(8,128)(2,1)S(1)}, u32[]{:S(2)}, u32[]{:S(2)}) collective-permute-start(bf16[512,384]{1,0:T(8,128)(2,1)S(1)} %get-tuple-element.110), channel_id=1, source_target_pairs={{0,1},{1,0},{2,3},{3,2},{4,5},{5,4},{6,7},{7,6},{8,9},{9,8},{10,11... | collective-permute-start | bytes 1179656 | tf_op jit(solution)/shard_map/ppermute | solution.py:586
  184.8 0.7 copy-start.10
  185.5 44.4 %all-to-all-start.2 = ((bf16[32,136,128]{2,1,0:T(8,128)(2,1)}), bf16[32,136,128]{2,1,0:T(8,128)(2,1)S(1)}, u32[]{:S(2)}, u32[]{:S(2)}) async-start(bf16[32,136,128]{2,1,0:T(8,128)(2,1)} %bitcast.28), calls=%async_computation.2 | async-start | bytes 2228224 | tf_op jit(solution)/shard_map/all_to_all | solution.py:800
  188.9 14.6 %copy-start.11 = (bf16[512,384]{1,0:T(8,128)(2,1)S(1)}, bf16[512,384]{1,0:T(8,128)(2,1)}, u32[]{:S(2)}) copy-start(bf16[512,384]{1,0:T(8,128)(2,1)} %copy-done.10) | copy-start | bytes 1179652
  190.0 13.5 %collective-permute-start.25 = (bf16[4,64,384]{2,1,0:T(8,128)(2,1)S(1)}, bf16[4,64,384]{2,1,0:T(8,128)(2,1)S(1)}, u32[]{:S(2)}, u32[]{:S(2)}) collective-permute-start(bf16[4,64,384]{2,1,0:T(8,128)(2,1)S(1)} %fusion.4), channel_id=1, source_target_pairs={{0,4},{4,0},{8,12},{12,8},{16,20},{20,16},{24,28},{28,24},{1,5},{5... | collective-permute-start | bytes 589832 | tf_op jit(solution)/shard_map/ppermute | solution.py:591
  191.7 14.2 %collective-permute-start.32 = (bf16[1,64,512]{2,1,0:T(8,128)(2,1)}, bf16[1,64,512]{2,1,0:T(8,128)(2,1)S(1)}, u32[]{:S(2)}, u32[]{:S(2)}) collective-permute-start(bf16[1,64,512]{2,1,0:T(8,128)(2,1)} %dynamic-slice_convert_fusion), channel_id=1, source_target_pairs={{0,4},{4,0},{8,12},{12,8},{16,20},{20,16},{24,28},{28,24},{1,5},{5... | collective-permute-start | bytes 196616 | tf_op jit(solution)/shard_map/ppermute | solution.py:591
  192.1 20.9 %collective-permute-start.29 = (bf16[64,640]{1,0:T(8,128)(2,1)S(1)}, bf16[64,640]{1,0:T(8,128)(2,1)S(1)}, u32[]{:S(2)}, u32[]{:S(2)}) collective-permute-start(bf16[64,640]{1,0:T(8,128)(2,1)S(1)} %get-tuple-element.166), channel_id=1, source_target_pairs={{0,8},{4,12},{8,16},{12,20},{16,24},{20,28},{24,0},{28,4},{1,9},{5... | collective-permute-start | bytes 245768 | tf_op jit(solution)/shard_map/ppermute | solution.py:591
  193.9 27.7 %collective-permute-start.30 = (bf16[64,640]{1,0:T(8,128)(2,1)S(1)}, bf16[64,640]{1,0:T(8,128)(2,1)S(1)}, u32[]{:S(2)}, u32[]{:S(2)}) collective-permute-start(bf16[64,640]{1,0:T(8,128)(2,1)S(1)} %get-tuple-element.165), channel_id=1, source_target_pairs={{0,16},{4,20},{8,24},{12,28},{16,0},{20,4},{24,8},{28,12},{1,17},{... | collective-permute-start | bytes 245768 | tf_op jit(solution)/shard_map/ppermute | solution.py:591
  196.4 25.2 %collective-permute-start.31 = (bf16[64,640]{1,0:T(8,128)(2,1)S(1)}, bf16[64,640]{1,0:T(8,128)(2,1)S(1)}, u32[]{:S(2)}, u32[]{:S(2)}) collective-permute-start(bf16[64,640]{1,0:T(8,128)(2,1)S(1)} %get-tuple-element.164), channel_id=1, source_target_pairs={{0,24},{4,28},{8,0},{12,4},{16,8},{20,12},{24,16},{28,20},{1,25},{... | collective-permute-start | bytes 245768 | tf_op jit(solution)/shard_map/ppermute | solution.py:591
  221.6 6.3 %collective-permute-start.26 = (bf16[64,384]{1,0:T(8,128)(2,1)S(1)}, bf16[64,384]{1,0:T(8,128)(2,1)S(1)}, u32[]{:S(2)}, u32[]{:S(2)}) collective-permute-start(bf16[64,384]{1,0:T(8,128)(2,1)S(1)} %get-tuple-element.168), channel_id=1, source_target_pairs={{0,8},{4,12},{8,16},{12,20},{16,24},{20,28},{24,0},{28,4},{1,9},{5... | collective-permute-start | bytes 147464 | tf_op jit(solution)/shard_map/ppermute | solution.py:591
  223.5 5.8 %collective-permute-start.27 = (bf16[64,384]{1,0:T(8,128)(2,1)S(1)}, bf16[64,384]{1,0:T(8,128)(2,1)S(1)}, u32[]{:S(2)}, u32[]{:S(2)}) collective-permute-start(bf16[64,384]{1,0:T(8,128)(2,1)S(1)} %get-tuple-element.170), channel_id=1, source_target_pairs={{0,16},{4,20},{8,24},{12,28},{16,0},{20,4},{24,8},{28,12},{1,17},{... | collective-permute-start | bytes 147464 | tf_op jit(solution)/shard_map/ppermute | solution.py:591
  224.7 4.6 %collective-permute-start.28 = (bf16[64,384]{1,0:T(8,128)(2,1)S(1)}, bf16[64,384]{1,0:T(8,128)(2,1)S(1)}, u32[]{:S(2)}, u32[]{:S(2)}) collective-permute-start(bf16[64,384]{1,0:T(8,128)(2,1)S(1)} %get-tuple-element.169), channel_id=1, source_target_pairs={{0,24},{4,28},{8,0},{12,4},{16,8},{20,12},{24,16},{28,20},{1,25},{... | collective-permute-start | bytes 147464 | tf_op jit(solution)/shard_map/ppermute | solution.py:591

commit v7 on v6

--- a/solution.py
+++ b/solution.py
@@ -592,12 +592,12 @@
 
 
 def across(value):
-    return along_dp(value, lambda i: i ^ 1)
-
-
-def ahead(value, step):
+    return ahead(value, 0, 1)
+
+
+def ahead(value, step, flip=0):
     count = lax.axis_size("dp") // 2
-    return along_dp(value, lambda i: (i // 2 + step) % count * 2 + i % 2)
+    return along_dp(value, lambda i: (i // 2 + step) % count * 2 + (i + flip) % 2)
 
 
 def places():
@@ -607,9 +607,10 @@
     return jnp.concatenate([coarse * 2 + own % 2, coarse * 2 + 1 - own % 2])
 
 
-def collect_coarse(shard):
+def collect_coarse(shard, flips=(0,)):
     count = lax.axis_size("dp") // 2
-    return jnp.concatenate([shard] + [ahead(shard, step) for step in range(1, count)], axis=0)
+    pieces = [ahead(shard, step, flip) for flip in flips for step in range(count)[1 - flip :]]
+    return jnp.concatenate([shard] + pieces, axis=0)
 
 
 def collect_rows(shard):
@@ -709,16 +710,17 @@
     direct = dp_count <= DIRECT
     if direct:
         place, groups = places(), dp_count
-        first = collect_coarse(jnp.concatenate([qkv, rest], axis=1))
-        qkv_rows = first[:, : qkv.shape[1]]
-        qkv_other = across(qkv_rows)
-        qkv_parts = collect_columns(jnp.concatenate([qkv_rows, qkv_other], axis=0))
-        mine = after(first[:, qkv.shape[1] :], qkv_other)
-        other, far_mine = in_hbm(across(mine)), in_hbm(swap(after(mine, qkv_parts[2]), 2))
+        qkv_rows = collect_coarse(qkv, (0, 1))
+        mine = collect_coarse(rest)
+        first = (qkv_rows, mine)
+        far_rows, other, far_mine = together(
+            swap(qkv_rows, 2), in_hbm(across(mine)), in_hbm(swap(mine, 2))
+        )
+        qkv_parts = (qkv_rows, swap(qkv_rows, 1), far_rows, swap(far_rows, 1))
     else:
         place, groups = jnp.zeros((1,), jnp.int32), None
-        first = collect_rows(qkv)
-        qkv_parts = collect_columns(first)
+        first = (collect_rows(qkv),)
+        qkv_parts = collect_columns(first[0])
         rest_parts = [(part,) for part in collect_columns(collect_rows(rest))]
 
     spare = jnp.stack(three_terms(gain_attn) + three_terms(gain_ffn)).reshape(1, 6 * per)
@@ -729,7 +731,7 @@
     )
     arranged = lax.all_to_all(arranged, "tensor", 0, 0, tiled=True)
     arranged = arranged.reshape(tensor_count, dp_count, tokens + SPARE, width).swapaxes(0, 1)
-    x_blocks = lax.all_to_all(after(arranged, first), "dp", 0, 0, tiled=True)
+    x_blocks = lax.all_to_all(after(arranged, *first), "dp", 0, 0, tiled=True)
     x_blocks = x_blocks.reshape(devices, tokens + SPARE, width)
     gains = jnp.sum(x_blocks[:, tokens, : 6 * per].reshape(devices, 2, 3, per).astype(F32), axis=2)
     gain_one = gains[:, 0].reshape(1, features)
@@ -740,15 +742,14 @@
         limit, place, groups, x_blocks, clock, gain_one, qkv_parts
     )
     if direct:
-        mixed, other = together(mixed, other)
-        near_mine, near_other = in_hbm(swap(after(mine, mixed), 1)), in_hbm(swap(other, 1))
-        far_other = in_hbm(swap(other, 2))
+        near_mine, near_other = in_hbm(swap(mine, 1)), in_hbm(swap(other, 1))
+        last_mine, far_other = in_hbm(swap(far_mine, 1)), in_hbm(swap(other, 2))
     ctx, ctx_turn, lse = attend(limit, mixed, tensor_count)
     if direct:
-        ctx, near_mine, near_other, far_mine, far_other = together(
-            ctx, near_mine, near_other, far_mine, far_other
+        ctx, near_mine, near_other, last_mine, far_other = together(
+            ctx, near_mine, near_other, last_mine, far_other
         )
-        last_mine, last_other = swap(far_mine, 1), swap(far_other, 1)
+        last_other = swap(far_other, 1)
         rest_parts = (
             (mine, other), (near_mine, near_other), (far_mine, far_other), (last_mine, last_other)
         )

time: 234 us -> 230 us (0.983)
  waiting for transfers between devices: 64.6 us -> 58.3 us
  starting transfers between devices: 55.7 us -> 58.1 us
    ppermute x17 -> x23, waiting for transfers between devices: 57 us -> 37.5 us  [along_dp(): return lax.ppermute(value, 'dp', [(i, move(i)) for i in range(count)])]
    ppermute x16, waiting for transfers between devices: 7.55 us -> 20.7 us  [swap(): return lax.ppermute(value, 'tensor', [(i, i ^ apart) for i in range(count)])]
    ppermute x17 -> x23, starting transfers between devices: 31.7 us -> 38 us  [along_dp(): return lax.ppermute(value, 'dp', [(i, move(i)) for i in range(count)])]
  transfers between devices with their start and end apart: 36 -> 42, of which waited for: 13 -> 12; matrix products, arithmetic and copies ran while one was open for 6% -> 7% of each run, Pallas kernels for 24% -> 24%
where the time goes in v7:
time: 230 us; the launch traced here: 229 us
  Pallas kernels  84 us (37%)
  waiting for transfers between devices  58.3 us (25%)
  starting transfers between devices  58.1 us (25%)
  local copies, waits for them, and re-layouts  15.5 us (7%)
  other arithmetic  9.45 us (4%)
  between operations  3.82 us (2%)
    ppermute x23, starting transfers between devices, along_dp(): return lax.ppermute(value, 'dp', [(i, move(i)) for i in range(count)])  38 us
    ppermute x23, waiting for transfers between devices, along_dp(): return lax.ppermute(value, 'dp', [(i, move(i)) for i in range(count)])  37.5 us
    pallas_call x1, Pallas kernels, middle_block(): pl.pallas_call(functools.partial(middle_kernel, groups), grid_spec=pltpu....  29 us
    pallas_call x2, Pallas kernels, attend_back(): pl.pallas_call(attend_back_kernel, grid_spec=pltpu.PrefetchScalarGridSpec...  28.4 us
    ppermute x16, waiting for transfers between devices, swap(): return lax.ppermute(value, 'tensor', [(i, i ^ apart) for i in range(count)])  20.7 us
    pallas_call x1, Pallas kernels, attend(): pl.pallas_call(attend_kernel, grid_spec=pltpu.PrefetchScalarGridSpec(num_...  15.3 us
    ppermute x16, starting transfers between devices, swap(): return lax.ppermute(value, 'tensor', [(i, i ^ apart) for i in range(count)])  7.49 us
    all_to_all x1, starting transfers between devices, on_device(): x_blocks = lax.all_to_all(after(arranged, *first), 'dp', 0, 0, tiled=True)  6.31 us
  transfers between devices with their start and end apart: 42, of which 12 were waited for; matrix products, arithmetic and copies ran while one was open for 7% of the time, Pallas kernels for 24%

profile of v7, /device:TPU:0, one launch (start us, length us, event | category | flops | bytes accessed | tf_op | source)
XLA Modules:
  0.0 229.3 jit_solution(16072973421485548388)
XLA Ops:
  0.6 0.9 copy_bitcast_fusion.2
  1.5 3.0 %collective-permute-start = (bf16[64,384]{1,0:T(8,128)(2,1)S(1)}, bf16[64,384]{1,0:T(8,128)(2,1)S(1)}, u32[]{:S(2)}, u32[]{:S(2)}) collective-permute-start(bf16[64,384]{1,0:T(8,128)(2,1)S(1)} %copy_bitcast_fusion.2), channel_id=1, source_target_pairs={{0,8},{4,12},{8,16},{12,20},{16,24},{20,28},{24,0},{28,4},{1,9},{5... | collective-permute-start | bytes 147464 | tf_op jit(solution)/shard_map/ppermute | solution.py:591
  4.6 2.6 %collective-permute-start.1 = (bf16[64,384]{1,0:T(8,128)(2,1)S(1)}, bf16[64,384]{1,0:T(8,128)(2,1)S(1)}, u32[]{:S(2)}, u32[]{:S(2)}) collective-permute-start(bf16[64,384]{1,0:T(8,128)(2,1)S(1)} %copy_bitcast_fusion.2), channel_id=1, source_target_pairs={{0,16},{4,20},{8,24},{12,28},{16,0},{20,4},{24,8},{28,12},{1,17},{... | collective-permute-start | bytes 147464 | tf_op jit(solution)/shard_map/ppermute | solution.py:591
  7.2 1.3 collective-permute-start.2
  8.5 1.5 collective-permute-start.3
  10.6 0.7 fusion.12
  11.4 0.7 reshape.155
  12.4 0.7 gather_fusion
  13.2 1.1 pad_maximum_fusion
  14.3 3.7 %all-to-all-start = ((bf16[32,136,128]{2,1,0:T(8,128)(2,1)}), bf16[32,136,128]{2,1,0:T(8,128)(2,1)S(1)}, u32[]{:S(2)}, u32[]{:S(2)}) async-start(bf16[32,136,128]{2,1,0:T(8,128)(2,1)} %pad_maximum_fusion), calls=%async_computation | async-start | bytes 2228224 | tf_op jit(solution)/shard_map/all_to_all | solution.py:732
  18.1 1.4 collective-permute-start.5
  19.4 2.9 %collective-permute-start.6 = (bf16[64,384]{1,0:T(8,128)(2,1)S(1)}, bf16[64,384]{1,0:T(8,128)(2,1)S(1)}, u32[]{:S(2)}, u32[]{:S(2)}) collective-permute-start(bf16[64,384]{1,0:T(8,128)(2,1)S(1)} %copy_bitcast_fusion.2), channel_id=1, source_target_pairs={{0,28},{4,24},{8,4},{12,0},{16,12},{20,8},{24,20},{28,16},{1,29},{... | collective-permute-start | bytes 147464 | tf_op jit(solution)/shard_map/ppermute | solution.py:591
  23.0 1.5 collective-permute-start.8
  24.5 3.0 %collective-permute-start.9 = (bf16[64,1152]{1,0:T(8,128)(2,1)S(1)}, bf16[64,1152]{1,0:T(8,128)(2,1)S(1)}, u32[]{:S(2)}, u32[]{:S(2)}) collective-permute-start(bf16[64,1152]{1,0:T(8,128)(2,1)S(1)} %pad_maximum_fusion.2), channel_id=1, source_target_pairs={{0,24},{4,28},{8,0},{12,4},{16,8},{20,12},{24,16},{28,20},{1,25},{... | collective-permute-start | bytes 442376 | tf_op jit(solution)/shard_map/ppermute | solution.py:591
  27.5 3.5 %collective-permute-done.7 = bf16[64,1152]{1,0:T(8,128)(2,1)S(1)} collective-permute-done((bf16[64,1152]{1,0:T(8,128)(2,1)S(1)}, bf16[64,1152]{1,0:T(8,128)(2,1)S(1)}, u32[]{:S(2)}, u32[]{:S(2)}) %collective-permute-start.7) | collective-permute-done | bytes 147488 | tf_op jit(solution)/shard_map/ppermute | solution.py:591
  31.0 5.6 %collective-permute-done.8 = bf16[64,1152]{1,0:T(8,128)(2,1)S(1)} collective-permute-done((bf16[64,1152]{1,0:T(8,128)(2,1)S(1)}, bf16[64,1152]{1,0:T(8,128)(2,1)S(1)}, u32[]{:S(2)}, u32[]{:S(2)}) %collective-permute-start.8) | collective-permute-done | bytes 147488 | tf_op jit(solution)/shard_map/ppermute | solution.py:591
  36.6 0.9 pad_maximum_fusion.1.refs_0_
  37.5 1.1 copy.70
  38.6 6.3 %all-to-all-start.1 = ((bf16[8,4,136,128]{3,2,1,0:T(8,128)(2,1)}), bf16[8,4,136,128]{3,2,1,0:T(8,128)(2,1)S(1)}, u32[]{:S(2)}, u32[]{:S(2)}) async-start(bf16[8,4,136,128]{3,2,1,0:T(8,128)(2,1)} %bitcast.126), calls=%async_computation.1 | async-start | bytes 2228224 | tf_op jit(solution)/shard_map/all_to_all | solution.py:734
  44.9 2.0 collective-permute-start.12
  47.0 1.8 collective-permute-start.13
  53.0 16.2 %collective-permute-done.11.refs_2_ = bf16[512,384]{1,0:T(8,128)(2,1)S(1)} collective-permute-done((bf16[512,384]{1,0:T(8,128)(2,1)S(1)}, bf16[512,384]{1,0:T(8,128)(2,1)S(1)}, u32[]{:S(2)}, u32[]{:S(2)}) %collective-permute-start.11) | collective-permute-done | bytes 393248 | tf_op jit(solution)/shard_map/ppermute | solution.py:586
  69.2 2.1 collective-permute-done.12.refs_1_
  72.5 1.7 collective-permute-start.18
  74.8 6.3 %project.1 = (bf16[1024,1536]{1,0:T(8,128)(2,1)S(1)}, bf16[512,1024]{1,0:T(8,128)(2,1)}, bf16[512,1536]{1,0:T(8,128)(2,1)}) custom-call(s32[1]{0:T(128)} %dynamic-slice.9.limit_ref, s32[8]{0:T(128)S(1)} %pad_add_fusion.place_ref, bf16[8,4,136,128]{3,2,1,0:T(8,128)(2,1)S(1)} %all-to-all-done.1.x_ref, f32[1,512]{1,0:T(1,128)S(1)} %pad_maximum_fusion.3.clock_ref, ...), custom_call_target="tpu_custom_call" | custom-call | flops 5750000128 | bytes 1048576 | tf_op jit(solution)/shard_map/project/pallas_call | solution.py:110
  81.1 15.3 %attend.1 = (bf16[1024,512]{1,0:T(8,128)(2,1)}, bf16[512,1024]{1,0:T(8,128)(2,1)}, f32[4,2,1024]{2,1,0:T(2,128)S(1)}) custom-call(s32[1]{0:T(128)} %dynamic-slice.9.limit_ref, bf16[1024,1536]{1,0:T(8,128)(2,1)S(1)} %get-tuple-element.64.q_ref.k_ref.v_ref, bf16[1024,1536]{1,0:T(8,128)(2,1)S(1)} %get-tuple-element.64.q_ref.k_ref.v_ref, ...), custom_call_target="tpu_custom_call" | custom-call | flops 17250000896 | bytes 1048576 | tf_op jit(solution)/shard_map/attend/pallas_call | solution.py:199
  96.6 0.8 copy-done.16
  97.5 1.3 collective-permute-done.19.refs_7_
  98.8 0.8 copy-done.17
  99.6 29.0 %middle.1 = (bf16[1,1024,512]{2,1,0:T(8,128)(2,1)}, bf16[1024,512]{1,0:T(8,128)(2,1)}, f32[1024,512]{1,0:T(8,128)}, f32[1,512]{1,0:T(1,128)S(1)}, bf16[2,512,640...) custom-call(s32[1]{0:T(128)} %dynamic-slice.9.limit_ref, ...), custom_call_target="tpu_custom_call" | custom-call | flops 28750000128 | bytes 1048576 | tf_op jit(solution)/shard_map/middle/pallas_call | solution.py:370
  129.2 3.2 %collective-permute-done.21 = bf16[2,512,512]{2,1,0:T(8,128)(2,1)} collective-permute-done((bf16[2,512,512]{2,1,0:T(8,128)(2,1)}, bf16[2,512,512]{2,1,0:T(8,128)(2,1)}, u32[]{:S(2)}, u32[]{:S(2)}) %collective-permute-start.21) | collective-permute-done | bytes 1048608 | tf_op jit(solution)/shard_map/ppermute | solution.py:586
  132.4 2.0 convert_add_fusion
  134.4 1.3 fusion.1
  136.0 1.2 copy-done.7
  137.2 14.2 %attend_back.2 = (bf16[1024,768]{1,0:T(8,128)(2,1)S(1)}, bf16[512,384]{1,0:T(8,128)(2,1)S(1)}, bf16[512,384]{1,0:T(8,128)(2,1)S(1)}) custom-call(s32[1]{0:T(128)} %dynamic-slice.9.limit_ref, bf16[1024,1536]{1,0:T(8,128)(2,1)S(1)} %copy-done.2, bf16[1024,1536]{1,0:T(8,128)(2,1)S(1)} %copy-done.2, bf16[1024,1536]{1,0:T(8,128)(2,1)S(1)} %copy-done.2, ...), custom_call_target="tpu_custom_call" | custom-call | flops 18400000000 | bytes 1048576 | tf_op jit(solution)/shard_map/attend_back/pallas_call | solution.py:465
  151.4 1.2 collective-permute-done.23
  152.9 1.7 collective-permute-start.25
  154.9 1.0 collective-permute-start.27
  155.9 1.7 collective-permute-start.28
  157.6 2.8 %collective-permute-start.29 = (bf16[2,64,512]{2,1,0:T(8,128)(2,1)S(1)}, bf16[2,64,512]{2,1,0:T(8,128)(2,1)S(1)}, u32[]{:S(2)}, u32[]{:S(2)}) collective-permute-start(bf16[2,64,512]{2,1,0:T(8,128)(2,1)S(1)} %get-tuple-element.156), channel_id=1, source_target_pairs={{0,24},{4,28},{8,0},{12,4},{16,8},{20,12},{24,16},{28,20},{1,25},{... | collective-permute-start | bytes 393224 | tf_op jit(solution)/shard_map/ppermute | solution.py:591
  160.9 14.2 %attend_back.3 = (bf16[1024,768]{1,0:T(8,128)(2,1)S(1)}, bf16[512,384]{1,0:T(8,128)(2,1)S(1)}, bf16[512,384]{1,0:T(8,128)(2,1)S(1)}) custom-call(s32[1]{0:T(128)} %dynamic-slice.9.limit_ref, bf16[1024,1536]{1,0:T(8,128)(2,1)S(1)} %copy-done.2, bf16[1024,1536]{1,0:T(8,128)(2,1)S(1)} %copy-done.2, bf16[1024,1536]{1,0:T(8,128)(2,1)S(1)} %copy-done.2, ...), custom_call_target="tpu_custom_call" | custom-call | flops 18400000000 | bytes 1048576 | tf_op jit(solution)/shard_map/attend_back/pallas_call | solution.py:465
  175.4 0.6 dynamic-slice_convert_fusion
  176.6 5.0 %begin_back.1 = bf16[8,4,136,128]{3,2,1,0:T(8,128)(2,1)} custom-call(s32[1]{0:T(128)} %dynamic-slice.9.limit_ref, bf16[8,4,136,128]{3,2,1,0:T(8,128)(2,1)S(1)} %all-to-all-done.1.x_ref, f32[1,512]{1,0:T(1,128)S(1)} %pad_maximum_fusion.3.clock_ref, f32[1,512]{1,0:T(1,128)S(1)} %reshape_squeeze.8.gain_ref, f32[1,512]{1,0:T(1,128)S(1)} %get-tuple-element.74.gg_two_ref, ...), custom_call_target="tpu_custom_call" | custom-call | flops 8049999872 | bytes 1048576 | tf_op jit(solution)/shard_map/begin_back/pallas_call | solution.py:553
  181.6 0.7 copy-done.9
  182.3 2.7 %all-to-all-start.2 = ((bf16[32,136,128]{2,1,0:T(8,128)(2,1)}), bf16[32,136,128]{2,1,0:T(8,128)(2,1)S(1)}, u32[]{:S(2)}, u32[]{:S(2)}) async-start(bf16[32,136,128]{2,1,0:T(8,128)(2,1)} %bitcast.28), calls=%async_computation.2 | async-start | bytes 2228224 | tf_op jit(solution)/shard_map/all_to_all | solution.py:801
  185.0 0.7 scatter_custom_fusion
  185.7 1.1 fusion.4
  186.8 1.7 collective-permute-start.31
  188.9 1.7 collective-permute-start.35
  190.7 2.5 %collective-permute-start.36 = (bf16[64,640]{1,0:T(8,128)(2,1)S(1)}, bf16[64,640]{1,0:T(8,128)(2,1)S(1)}, u32[]{:S(2)}, u32[]{:S(2)}) collective-permute-start(bf16[64,640]{1,0:T(8,128)(2,1)S(1)} %get-tuple-element.161), channel_id=1, source_target_pairs={{0,16},{4,20},{8,24},{12,28},{16,0},{20,4},{24,8},{28,12},{1,17},{... | collective-permute-start | bytes 245768 | tf_op jit(solution)/shard_map/ppermute | solution.py:591
  193.2 1.4 collective-permute-start.37
  194.6 5.8 %collective-permute-done.31 = bf16[4,64,384]{2,1,0:T(8,128)(2,1)S(1)} collective-permute-done((bf16[4,64,384]{2,1,0:T(8,128)(2,1)S(1)}, bf16[4,64,384]{2,1,0:T(8,128)(2,1)S(1)}, u32[]{:S(2)}, u32[]{:S(2)}) %collective-permute-start.31) | collective-permute-done | bytes 196640 | tf_op jit(solution)/shard_map/ppermute | solution.py:591
  200.5 2.3 %collective-permute-done.38 = bf16[1,64,512]{2,1,0:T(8,128)(2,1)S(1)} collective-permute-done((bf16[1,64,512]{2,1,0:T(8,128)(2,1)}, bf16[1,64,512]{2,1,0:T(8,128)(2,1)S(1)}, u32[]{:S(2)}, u32[]{:S(2)}) %collective-permute-start.38) | collective-permute-done | bytes 65568 | tf_op jit(solution)/shard_map/ppermute | solution.py:591
  202.8 7.1 %collective-permute-done.35 = bf16[64,640]{1,0:T(8,128)(2,1)S(1)} collective-permute-done((bf16[64,640]{1,0:T(8,128)(2,1)S(1)}, bf16[64,640]{1,0:T(8,128)(2,1)S(1)}, u32[]{:S(2)}, u32[]{:S(2)}) %collective-permute-start.35) | collective-permute-done | bytes 81952 | tf_op jit(solution)/shard_map/ppermute | solution.py:591
  209.9 8.5 %collective-permute-done.36 = bf16[64,640]{1,0:T(8,128)(2,1)S(1)} collective-permute-done((bf16[64,640]{1,0:T(8,128)(2,1)S(1)}, bf16[64,640]{1,0:T(8,128)(2,1)S(1)}, u32[]{:S(2)}, u32[]{:S(2)}) %collective-permute-start.36) | collective-permute-done | bytes 81952 | tf_op jit(solution)/shard_map/ppermute | solution.py:591
  218.4 1.9 collective-permute-start.32
  220.3 1.2 collective-permute-start.33
  221.5 1.3 collective-permute-start.34
  222.7 0.7 add_bitcast_fusion
  224.1 0.7 slice.89
  224.7 1.4 collective-permute-done.33
  226.1 0.7 copy_bitcast_fusion.1
  226.8 0.8 gather_fusion.1
  227.5 1.1 slice.87
  (134 shorter events, 9.7 us)
Async XLA Ops:
  0.6 11.8 %copy-start = (bf16[32,128,128]{2,1,0:T(8,128)(2,1)S(1)}, bf16[32,128,128]{2,1,0:T(8,128)(2,1)}, u32[]{:S(2)}) copy-start(bf16[32,128,128]{2,1,0:T(8,128)(2,1)} %param.11) | copy-start | bytes 3145732
  1.5 16.5 %collective-permute-start = (bf16[64,384]{1,0:T(8,128)(2,1)S(1)}, bf16[64,384]{1,0:T(8,128)(2,1)S(1)}, u32[]{:S(2)}, u32[]{:S(2)}) collective-permute-start(bf16[64,384]{1,0:T(8,128)(2,1)S(1)} %copy_bitcast_fusion.2), channel_id=1, source_target_pairs={{0,8},{4,12},{8,16},{12,20},{16,24},{20,28},{24,0},{28,4},{1,9},{5... | collective-permute-start | bytes 147464 | tf_op jit(solution)/shard_map/ppermute | solution.py:591
  4.6 14.9 %collective-permute-start.1 = (bf16[64,384]{1,0:T(8,128)(2,1)S(1)}, bf16[64,384]{1,0:T(8,128)(2,1)S(1)}, u32[]{:S(2)}, u32[]{:S(2)}) collective-permute-start(bf16[64,384]{1,0:T(8,128)(2,1)S(1)} %copy_bitcast_fusion.2), channel_id=1, source_target_pairs={{0,16},{4,20},{8,24},{12,28},{16,0},{20,4},{24,8},{28,12},{1,17},{... | collective-permute-start | bytes 147464 | tf_op jit(solution)/shard_map/ppermute | solution.py:591
  7.2 15.2 %collective-permute-start.2 = (bf16[64,384]{1,0:T(8,128)(2,1)S(1)}, bf16[64,384]{1,0:T(8,128)(2,1)S(1)}, u32[]{:S(2)}, u32[]{:S(2)}) collective-permute-start(bf16[64,384]{1,0:T(8,128)(2,1)S(1)} %copy_bitcast_fusion.2), channel_id=1, source_target_pairs={{0,24},{4,28},{8,0},{12,4},{16,8},{20,12},{24,16},{28,20},{1,25},{... | collective-permute-start | bytes 147464 | tf_op jit(solution)/shard_map/ppermute | solution.py:591
  8.5 14.5 %collective-permute-start.3 = (bf16[64,384]{1,0:T(8,128)(2,1)S(1)}, bf16[64,384]{1,0:T(8,128)(2,1)S(1)}, u32[]{:S(2)}, u32[]{:S(2)}) collective-permute-start(bf16[64,384]{1,0:T(8,128)(2,1)S(1)} %copy_bitcast_fusion.2), channel_id=1, source_target_pairs={{0,4},{4,0},{8,12},{12,8},{16,20},{20,16},{24,28},{28,24},{1,5},{5... | collective-permute-start | bytes 147464 | tf_op jit(solution)/shard_map/ppermute | solution.py:591
  10.0 14.5 %collective-permute-start.4 = (bf16[64,384]{1,0:T(8,128)(2,1)S(1)}, bf16[64,384]{1,0:T(8,128)(2,1)S(1)}, u32[]{:S(2)}, u32[]{:S(2)}) collective-permute-start(bf16[64,384]{1,0:T(8,128)(2,1)S(1)} %copy_bitcast_fusion.2), channel_id=1, source_target_pairs={{0,12},{4,8},{8,20},{12,16},{16,28},{20,24},{24,4},{28,0},{1,13},{... | collective-permute-start | bytes 147464 | tf_op jit(solution)/shard_map/ppermute | solution.py:591
  14.3 3.7 %copy-start.11 = (bf16[512,64]{0,1:T(8,128)(2,1)S(1)}, bf16[512,64]{0,1:T(8,128)(2,1)}, u32[]{:S(2)}) copy-start(bf16[512,64]{0,1:T(8,128)(2,1)} %param.18) | copy-start | bytes 196612
  14.3 3.7 %copy-start.12 = (bf16[64,512]{1,0:T(8,128)(2,1)S(1)}, bf16[64,512]{1,0:T(8,128)(2,1)}, u32[]{:S(2)}) copy-start(bf16[64,512]{1,0:T(8,128)(2,1)} %param.17) | copy-start | bytes 196612
  14.3 3.7 %copy-start.14 = (bf16[128,64]{0,1:T(8,128)(2,1)S(1)}, bf16[128,64]{0,1:T(8,128)(2,1)}, u32[]{:S(2)}) copy-start(bf16[128,64]{0,1:T(8,128)(2,1)} %param.16) | copy-start | bytes 49156
  14.3 3.7 %copy-start.13 = (bf16[64,3,128]{2,0,1:T(8,128)(2,1)S(1)}, bf16[64,3,128]{2,0,1:T(8,128)(2,1)}, u32[]{:S(2)}) copy-start(bf16[64,3,128]{2,0,1:T(8,128)(2,1)} %param.15) | copy-start | bytes 147460
  14.3 23.2 %all-to-all-start = ((bf16[32,136,128]{2,1,0:T(8,128)(2,1)}), bf16[32,136,128]{2,1,0:T(8,128)(2,1)S(1)}, u32[]{:S(2)}, u32[]{:S(2)}) async-start(bf16[32,136,128]{2,1,0:T(8,128)(2,1)} %pad_maximum_fusion), calls=%async_computation | async-start | bytes 2228224 | tf_op jit(solution)/shard_map/all_to_all | solution.py:732
  18.1 9.4 %collective-permute-start.5 = (bf16[64,384]{1,0:T(8,128)(2,1)S(1)}, bf16[64,384]{1,0:T(8,128)(2,1)S(1)}, u32[]{:S(2)}, u32[]{:S(2)}) collective-permute-start(bf16[64,384]{1,0:T(8,128)(2,1)S(1)} %copy_bitcast_fusion.2), channel_id=1, source_target_pairs={{0,20},{4,16},{8,28},{12,24},{16,4},{20,0},{24,12},{28,8},{1,21},{... | collective-permute-start | bytes 147464 | tf_op jit(solution)/shard_map/ppermute | solution.py:591
  19.4 8.0 %collective-permute-start.6 = (bf16[64,384]{1,0:T(8,128)(2,1)S(1)}, bf16[64,384]{1,0:T(8,128)(2,1)S(1)}, u32[]{:S(2)}, u32[]{:S(2)}) collective-permute-start(bf16[64,384]{1,0:T(8,128)(2,1)S(1)} %copy_bitcast_fusion.2), channel_id=1, source_target_pairs={{0,28},{4,24},{8,4},{12,0},{16,12},{20,8},{24,20},{28,16},{1,29},{... | collective-permute-start | bytes 147464 | tf_op jit(solution)/shard_map/ppermute | solution.py:591
  22.4 8.7 %collective-permute-start.7 = (bf16[64,1152]{1,0:T(8,128)(2,1)S(1)}, bf16[64,1152]{1,0:T(8,128)(2,1)S(1)}, u32[]{:S(2)}, u32[]{:S(2)}) collective-permute-start(bf16[64,1152]{1,0:T(8,128)(2,1)S(1)} %pad_maximum_fusion.2), channel_id=1, source_target_pairs={{0,8},{4,12},{8,16},{12,20},{16,24},{20,28},{24,0},{28,4},{1,9},{5... | collective-permute-start | bytes 442376 | tf_op jit(solution)/shard_map/ppermute | solution.py:591
  23.0 13.6 %collective-permute-start.8 = (bf16[64,1152]{1,0:T(8,128)(2,1)S(1)}, bf16[64,1152]{1,0:T(8,128)(2,1)S(1)}, u32[]{:S(2)}, u32[]{:S(2)}) collective-permute-start(bf16[64,1152]{1,0:T(8,128)(2,1)S(1)} %pad_maximum_fusion.2), channel_id=1, source_target_pairs={{0,16},{4,20},{8,24},{12,28},{16,0},{20,4},{24,8},{28,12},{1,17},{... | collective-permute-start | bytes 442376 | tf_op jit(solution)/shard_map/ppermute | solution.py:591
  24.5 12.1 %collective-permute-start.9 = (bf16[64,1152]{1,0:T(8,128)(2,1)S(1)}, bf16[64,1152]{1,0:T(8,128)(2,1)S(1)}, u32[]{:S(2)}, u32[]{:S(2)}) collective-permute-start(bf16[64,1152]{1,0:T(8,128)(2,1)S(1)} %pad_maximum_fusion.2), channel_id=1, source_target_pairs={{0,24},{4,28},{8,0},{12,4},{16,8},{20,12},{24,16},{28,20},{1,25},{... | collective-permute-start | bytes 442376 | tf_op jit(solution)/shard_map/ppermute | solution.py:591
  38.6 10.4 %copy-start.15 = (s32[32]{0:T(128)S(1)}, s32[32]{0:T(128)}, u32[]{:S(2)}) copy-start(s32[32]{0:T(128)} %param.14) | copy-start | bytes 388
  38.6 12.9 %copy-start.18 = (s32[32]{0:T(128)S(1)}, s32[32]{0:T(128)}, u32[]{:S(2)}) copy-start(s32[32]{0:T(128)} %param.12) | copy-start | bytes 388
  38.6 32.8 %copy-start.19 = (s32[32]{0:T(128)S(1)}, s32[32]{0:T(128)}, u32[]{:S(2)}) copy-start(s32[32]{0:T(128)} %param.13) | copy-start | bytes 388
  38.6 35.6 %all-to-all-start.1 = ((bf16[8,4,136,128]{3,2,1,0:T(8,128)(2,1)}), bf16[8,4,136,128]{3,2,1,0:T(8,128)(2,1)S(1)}, u32[]{:S(2)}, u32[]{:S(2)}) async-start(bf16[8,4,136,128]{3,2,1,0:T(8,128)(2,1)} %bitcast.126), calls=%async_computation.1 | async-start | bytes 2228224 | tf_op jit(solution)/shard_map/all_to_all | solution.py:734
  44.9 26.4 %collective-permute-start.12 = (bf16[256,1152]{1,0:T(8,128)(2,1)}, bf16[256,1152]{1,0:T(8,128)(2,1)}, u32[]{:S(2)}, u32[]{:S(2)}) collective-permute-start(bf16[256,1152]{1,0:T(8,128)(2,1)} %pad_maximum_fusion.1.refs_0_), channel_id=1, source_target_pairs={{0,4},{4,0},{8,12},{12,8},{16,20},{20,16},{24,28},{28,24},{1,5},{5... | collective-permute-start | bytes 1769480 | tf_op jit(solution)/shard_map/ppermute | solution.py:591
  47.0 24.4 %collective-permute-start.13 = (bf16[256,1152]{1,0:T(8,128)(2,1)}, bf16[256,1152]{1,0:T(8,128)(2,1)}, u32[]{:S(2)}, u32[]{:S(2)}) collective-permute-start(bf16[256,1152]{1,0:T(8,128)(2,1)} %pad_maximum_fusion.1.refs_0_), channel_id=1, source_target_pairs={{0,2},{1,3},{2,0},{3,1},{4,6},{5,7},{6,4},{7,5},{8,10},{9,11},{10,... | collective-permute-start | bytes 1769480 | tf_op jit(solution)/shard_map/ppermute | solution.py:586
  48.8 20.4 %collective-permute-start.11 = (bf16[512,384]{1,0:T(8,128)(2,1)S(1)}, bf16[512,384]{1,0:T(8,128)(2,1)S(1)}, u32[]{:S(2)}, u32[]{:S(2)}) collective-permute-start(bf16[512,384]{1,0:T(8,128)(2,1)S(1)} %constant_dynamic-update-slice_fusion.refs_0_), channel_id=1, source_target_pairs={{0,2},{1,3},{2,0},{3,1},{4,6},{5,7},{6,4},{7,5},{8,10},{9,11},{10,... | collective-permute-start | bytes 1179656 | tf_op jit(solution)/shard_map/ppermute | solution.py:586
  52.9 21.7 %collective-permute-start.10 = (bf16[512,384]{1,0:T(8,128)(2,1)S(1)}, bf16[512,384]{1,0:T(8,128)(2,1)S(1)}, u32[]{:S(2)}, u32[]{:S(2)}) collective-permute-start(bf16[512,384]{1,0:T(8,128)(2,1)S(1)} %constant_dynamic-update-slice_fusion.refs_0_), channel_id=1, source_target_pairs={{0,1},{1,0},{2,3},{3,2},{4,5},{5,4},{6,7},{7,6},{8,9},{9,8},{10,11... | collective-permute-start | bytes 1179656 | tf_op jit(solution)/shard_map/ppermute | solution.py:586
  71.3 3.5 %collective-permute-start.14 = (bf16[512,384]{1,0:T(8,128)(2,1)S(1)}, bf16[512,384]{1,0:T(8,128)(2,1)}, u32[]{:S(2)}, u32[]{:S(2)}) collective-permute-start(bf16[512,384]{1,0:T(8,128)(2,1)S(1)} %collective-permute-done.11.refs_2_), channel_id=1, source_target_pairs={{0,1},{1,0},{2,3},{3,2},{4,5},{5,4},{6,7},{7,6},{8,9},{9,8},{10,11... | collective-permute-start | bytes 1179656 | tf_op jit(solution)/shard_map/ppermute | solution.py:586
  72.0 24.4 %collective-permute-start.15 = (bf16[256,1152]{1,0:T(8,128)(2,1)}, bf16[256,1152]{1,0:T(8,128)(2,1)}, u32[]{:S(2)}, u32[]{:S(2)}) collective-permute-start(bf16[256,1152]{1,0:T(8,128)(2,1)} %pad_maximum_fusion.1.refs_0_), channel_id=1, source_target_pairs={{0,1},{1,0},{2,3},{3,2},{4,5},{5,4},{6,7},{7,6},{8,9},{9,8},{10,11... | collective-permute-start | bytes 1769480 | tf_op jit(solution)/shard_map/ppermute | solution.py:586
  72.5 23.9 %collective-permute-start.16 = (bf16[256,1152]{1,0:T(8,128)(2,1)}, bf16[256,1152]{1,0:T(8,128)(2,1)}, u32[]{:S(2)}, u32[]{:S(2)}) collective-permute-start(bf16[256,1152]{1,0:T(8,128)(2,1)} %collective-permute-done.12.refs_1_), channel_id=1, source_target_pairs={{0,1},{1,0},{2,3},{3,2},{4,5},{5,4},{6,7},{7,6},{8,9},{9,8},{10,11... | collective-permute-start | bytes 1769480 | tf_op jit(solution)/shard_map/ppermute | solution.py:586
  72.5 24.0 %collective-permute-start.18 = (bf16[256,1152]{1,0:T(8,128)(2,1)}, bf16[256,1152]{1,0:T(8,128)(2,1)}, u32[]{:S(2)}, u32[]{:S(2)}) collective-permute-start(bf16[256,1152]{1,0:T(8,128)(2,1)} %collective-permute-done.12.refs_1_), channel_id=1, source_target_pairs={{0,2},{1,3},{2,0},{3,1},{4,6},{5,7},{6,4},{7,5},{8,10},{9,11},{10,... | collective-permute-start | bytes 1769480 | tf_op jit(solution)/shard_map/ppermute | solution.py:586
  74.5 21.9 %collective-permute-start.17 = (bf16[256,1152]{1,0:T(8,128)(2,1)}, bf16[256,1152]{1,0:T(8,128)(2,1)S(1)}, u32[]{:S(2)}, u32[]{:S(2)}) collective-permute-start(bf16[256,1152]{1,0:T(8,128)(2,1)} %collective-permute-done.13.refs_4_), channel_id=1, source_target_pairs={{0,1},{1,0},{2,3},{3,2},{4,5},{5,4},{6,7},{7,6},{8,9},{9,8},{10,11... | collective-permute-start | bytes 1769480 | tf_op jit(solution)/shard_map/ppermute | solution.py:586
  81.1 15.3 %copy-start.1 = (bf16[1024,1536]{1,0:T(8,128)(2,1)}, bf16[1024,1536]{1,0:T(8,128)(2,1)S(1)}, u32[]{:S(2)}) copy-start(bf16[1024,1536]{1,0:T(8,128)(2,1)S(1)} %get-tuple-element.64.q_ref.k_ref.v_ref) | copy-start | bytes 9437188
  96.5 0.8 copy-start.16
  96.5 2.3 collective-permute-start.19
  98.8 0.8 copy-start.17
  128.6 3.8 %collective-permute-start.21 = (bf16[2,512,512]{2,1,0:T(8,128)(2,1)}, bf16[2,512,512]{2,1,0:T(8,128)(2,1)}, u32[]{:S(2)}, u32[]{:S(2)}) collective-permute-start(bf16[2,512,512]{2,1,0:T(8,128)(2,1)} %get-tuple-element.82), channel_id=1, source_target_pairs={{0,1},{1,0},{2,3},{3,2},{4,5},{5,4},{6,7},{7,6},{8,9},{9,8},{10,11... | collective-permute-start | bytes 3145736 | tf_op jit(solution)/shard_map/ppermute | solution.py:586
  128.7 5.7 %collective-permute-start.20 = (bf16[2,512,640]{2,1,0:T(8,128)(2,1)}, bf16[2,512,640]{2,1,0:T(8,128)(2,1)S(1)}, u32[]{:S(2)}, u32[]{:S(2)}) collective-permute-start(bf16[2,512,640]{2,1,0:T(8,128)(2,1)} %get-tuple-element.77), channel_id=1, source_target_pairs={{0,1},{1,0},{2,3},{3,2},{4,5},{5,4},{6,7},{7,6},{8,9},{9,8},{10,11... | collective-permute-start | bytes 3932168 | tf_op jit(solution)/shard_map/ppermute | solution.py:586
  132.4 3.5 %copy-start.2 = (bf16[1024,1536]{1,0:T(8,128)(2,1)S(1)}, bf16[1024,1536]{1,0:T(8,128)(2,1)}, u32[]{:S(2)}) copy-start(bf16[1024,1536]{1,0:T(8,128)(2,1)} %copy-done.1) | copy-start | bytes 9437188
  132.4 3.5 %copy-start.6 = (bf16[512,1024]{1,0:T(8,128)(2,1)S(1)}, bf16[512,1024]{1,0:T(8,128)(2,1)}, u32[]{:S(2)}) copy-start(bf16[512,1024]{1,0:T(8,128)(2,1)} %get-tuple-element.78.turn_ref) | copy-start | bytes 3145732
  134.3 1.6 copy-start.5
  134.4 17.0 %collective-permute-start.22 = (bf16[4,2,64,512]{3,2,1,0:T(8,128)(2,1)S(1)}, bf16[4,2,64,512]{3,2,1,0:T(8,128)(2,1)S(1)}, u32[]{:S(2)}, u32[]{:S(2)}) collective-permute-start(bf16[4,2,64,512]{3,2,1,0:T(8,128)(2,1)S(1)} %bitcast.133), channel_id=1, source_target_pairs={{0,2},{1,3},{2,0},{3,1},{4,6},{5,7},{6,4},{7,5},{8,10},{9,11},{10,... | collective-permute-start | bytes 1572872 | tf_op jit(solution)/shard_map/ppermute | solution.py:586
  135.8 16.8 %collective-permute-start.23 = (bf16[2,4,64,640]{3,2,1,0:T(8,128)(2,1)S(1)}, bf16[2,4,64,640]{3,2,1,0:T(8,128)(2,1)S(1)}, u32[]{:S(2)}, u32[]{:S(2)}) collective-permute-start(bf16[2,4,64,640]{3,2,1,0:T(8,128)(2,1)S(1)} %fusion.1), channel_id=1, source_target_pairs={{0,4},{4,0},{8,12},{12,8},{16,20},{20,16},{24,28},{28,24},{1,5},{5... | collective-permute-start | bytes 1966088 | tf_op jit(solution)/shard_map/ppermute | solution.py:591
  136.0 1.2 copy-start.7
  137.2 15.4 %copy-start.8 = (bf16[2,512,640]{2,1,0:T(8,128)(2,1)S(1)}, bf16[2,512,640]{2,1,0:T(8,128)(2,1)}, u32[]{:S(2)}) copy-start(bf16[2,512,640]{2,1,0:T(8,128)(2,1)} %get-tuple-element.76) | copy-start | bytes 3932164
  152.6 7.7 %collective-permute-start.24 = (bf16[512,384]{1,0:T(8,128)(2,1)S(1)}, bf16[512,384]{1,0:T(8,128)(2,1)S(1)}, u32[]{:S(2)}, u32[]{:S(2)}) collective-permute-start(bf16[512,384]{1,0:T(8,128)(2,1)S(1)} %get-tuple-element.93), channel_id=1, source_target_pairs={{0,1},{1,0},{2,3},{3,2},{4,5},{5,4},{6,7},{7,6},{8,9},{9,8},{10,11... | collective-permute-start | bytes 1179656 | tf_op jit(solution)/shard_map/ppermute | solution.py:586
  152.9 22.3 %collective-permute-start.25 = (bf16[4,64,640]{2,1,0:T(8,128)(2,1)S(1)}, bf16[4,64,640]{2,1,0:T(8,128)(2,1)S(1)}, u32[]{:S(2)}, u32[]{:S(2)}) collective-permute-start(bf16[4,64,640]{2,1,0:T(8,128)(2,1)S(1)} %slice_bitcast_fusion), channel_id=1, source_target_pairs={{0,2},{1,3},{2,0},{3,1},{4,6},{5,7},{6,4},{7,5},{8,10},{9,11},{10,... | collective-permute-start | bytes 983048 | tf_op jit(solution)/shard_map/ppermute | solution.py:586
  154.9 20.3 %collective-permute-start.27 = (bf16[2,64,512]{2,1,0:T(8,128)(2,1)S(1)}, bf16[2,64,512]{2,1,0:T(8,128)(2,1)S(1)}, u32[]{:S(2)}, u32[]{:S(2)}) collective-permute-start(bf16[2,64,512]{2,1,0:T(8,128)(2,1)S(1)} %get-tuple-element.158), channel_id=1, source_target_pairs={{0,8},{4,12},{8,16},{12,20},{16,24},{20,28},{24,0},{28,4},{1,9},{5... | collective-permute-start | bytes 393224 | tf_op jit(solution)/shard_map/ppermute | solution.py:591
  155.9 19.3 %collective-permute-start.28 = (bf16[2,64,512]{2,1,0:T(8,128)(2,1)S(1)}, bf16[2,64,512]{2,1,0:T(8,128)(2,1)S(1)}, u32[]{:S(2)}, u32[]{:S(2)}) collective-permute-start(bf16[2,64,512]{2,1,0:T(8,128)(2,1)S(1)} %get-tuple-element.157), channel_id=1, source_target_pairs={{0,16},{4,20},{8,24},{12,28},{16,0},{20,4},{24,8},{28,12},{1,17},{... | collective-permute-start | bytes 393224 | tf_op jit(solution)/shard_map/ppermute | solution.py:591
  157.6 17.6 %collective-permute-start.29 = (bf16[2,64,512]{2,1,0:T(8,128)(2,1)S(1)}, bf16[2,64,512]{2,1,0:T(8,128)(2,1)S(1)}, u32[]{:S(2)}, u32[]{:S(2)}) collective-permute-start(bf16[2,64,512]{2,1,0:T(8,128)(2,1)S(1)} %get-tuple-element.156), channel_id=1, source_target_pairs={{0,24},{4,28},{8,0},{12,4},{16,8},{20,12},{24,16},{28,20},{1,25},{... | collective-permute-start | bytes 393224 | tf_op jit(solution)/shard_map/ppermute | solution.py:591
  160.5 14.8 %collective-permute-start.26 = (bf16[512,384]{1,0:T(8,128)(2,1)S(1)}, bf16[512,384]{1,0:T(8,128)(2,1)S(1)}, u32[]{:S(2)}, u32[]{:S(2)}) collective-permute-start(bf16[512,384]{1,0:T(8,128)(2,1)S(1)} %add_convert_fusion.3), channel_id=1, source_target_pairs={{0,2},{1,3},{2,0},{3,1},{4,6},{5,7},{6,4},{7,5},{8,10},{9,11},{10,... | collective-permute-start | bytes 1179656 | tf_op jit(solution)/shard_map/ppermute | solution.py:586
  160.9 15.1 %copy-start.3 = (f32[1024,512]{1,0:T(8,128)S(1)}, f32[1024,512]{1,0:T(8,128)}, u32[]{:S(2)}) copy-start(f32[1024,512]{1,0:T(8,128)} %get-tuple-element.103.mg_ref) | copy-start | bytes 6291460
  175.2 1.4 copy-start.4
  176.0 5.6 %collective-permute-start.30 = (bf16[512,384]{1,0:T(8,128)(2,1)S(1)}, bf16[512,384]{1,0:T(8,128)(2,1)S(1)}, u32[]{:S(2)}, u32[]{:S(2)}) collective-permute-start(bf16[512,384]{1,0:T(8,128)(2,1)S(1)} %get-tuple-element.106), channel_id=1, source_target_pairs={{0,1},{1,0},{2,3},{3,2},{4,5},{5,4},{6,7},{7,6},{8,9},{9,8},{10,11... | collective-permute-start | bytes 1179656 | tf_op jit(solution)/shard_map/ppermute | solution.py:586
  181.6 0.7 copy-start.9
  182.3 44.4 %all-to-all-start.2 = ((bf16[32,136,128]{2,1,0:T(8,128)(2,1)}), bf16[32,136,128]{2,1,0:T(8,128)(2,1)S(1)}, u32[]{:S(2)}, u32[]{:S(2)}) async-start(bf16[32,136,128]{2,1,0:T(8,128)(2,1)} %bitcast.28), calls=%async_computation.2 | async-start | bytes 2228224 | tf_op jit(solution)/shard_map/all_to_all | solution.py:801
  185.7 14.6 %copy-start.10 = (bf16[512,384]{1,0:T(8,128)(2,1)S(1)}, bf16[512,384]{1,0:T(8,128)(2,1)}, u32[]{:S(2)}) copy-start(bf16[512,384]{1,0:T(8,128)(2,1)} %copy-done.9) | copy-start | bytes 1179652
  186.8 13.5 %collective-permute-start.31 = (bf16[4,64,384]{2,1,0:T(8,128)(2,1)S(1)}, bf16[4,64,384]{2,1,0:T(8,128)(2,1)S(1)}, u32[]{:S(2)}, u32[]{:S(2)}) collective-permute-start(bf16[4,64,384]{2,1,0:T(8,128)(2,1)S(1)} %fusion.4), channel_id=1, source_target_pairs={{0,4},{4,0},{8,12},{12,8},{16,20},{20,16},{24,28},{28,24},{1,5},{5... | collective-permute-start | bytes 589832 | tf_op jit(solution)/shard_map/ppermute | solution.py:591
  188.5 14.2 %collective-permute-start.38 = (bf16[1,64,512]{2,1,0:T(8,128)(2,1)}, bf16[1,64,512]{2,1,0:T(8,128)(2,1)S(1)}, u32[]{:S(2)}, u32[]{:S(2)}) collective-permute-start(bf16[1,64,512]{2,1,0:T(8,128)(2,1)} %dynamic-slice_convert_fusion), channel_id=1, source_target_pairs={{0,4},{4,0},{8,12},{12,8},{16,20},{20,16},{24,28},{28,24},{1,5},{5... | collective-permute-start | bytes 196616 | tf_op jit(solution)/shard_map/ppermute | solution.py:591
  188.9 20.9 %collective-permute-start.35 = (bf16[64,640]{1,0:T(8,128)(2,1)S(1)}, bf16[64,640]{1,0:T(8,128)(2,1)S(1)}, u32[]{:S(2)}, u32[]{:S(2)}) collective-permute-start(bf16[64,640]{1,0:T(8,128)(2,1)S(1)} %get-tuple-element.162), channel_id=1, source_target_pairs={{0,8},{4,12},{8,16},{12,20},{16,24},{20,28},{24,0},{28,4},{1,9},{5... | collective-permute-start | bytes 245768 | tf_op jit(solution)/shard_map/ppermute | solution.py:591
  190.7 27.7 %collective-permute-start.36 = (bf16[64,640]{1,0:T(8,128)(2,1)S(1)}, bf16[64,640]{1,0:T(8,128)(2,1)S(1)}, u32[]{:S(2)}, u32[]{:S(2)}) collective-permute-start(bf16[64,640]{1,0:T(8,128)(2,1)S(1)} %get-tuple-element.161), channel_id=1, source_target_pairs={{0,16},{4,20},{8,24},{12,28},{16,0},{20,4},{24,8},{28,12},{1,17},{... | collective-permute-start | bytes 245768 | tf_op jit(solution)/shard_map/ppermute | solution.py:591
  193.2 25.2 %collective-permute-start.37 = (bf16[64,640]{1,0:T(8,128)(2,1)S(1)}, bf16[64,640]{1,0:T(8,128)(2,1)S(1)}, u32[]{:S(2)}, u32[]{:S(2)}) collective-permute-start(bf16[64,640]{1,0:T(8,128)(2,1)S(1)} %get-tuple-element.160), channel_id=1, source_target_pairs={{0,24},{4,28},{8,0},{12,4},{16,8},{20,12},{24,16},{28,20},{1,25},{... | collective-permute-start | bytes 245768 | tf_op jit(solution)/shard_map/ppermute | solution.py:591
  218.4 6.3 %collective-permute-start.32 = (bf16[64,384]{1,0:T(8,128)(2,1)S(1)}, bf16[64,384]{1,0:T(8,128)(2,1)S(1)}, u32[]{:S(2)}, u32[]{:S(2)}) collective-permute-start(bf16[64,384]{1,0:T(8,128)(2,1)S(1)} %get-tuple-element.164), channel_id=1, source_target_pairs={{0,8},{4,12},{8,16},{12,20},{16,24},{20,28},{24,0},{28,4},{1,9},{5... | collective-permute-start | bytes 147464 | tf_op jit(solution)/shard_map/ppermute | solution.py:591
  220.3 5.8 %collective-permute-start.33 = (bf16[64,384]{1,0:T(8,128)(2,1)S(1)}, bf16[64,384]{1,0:T(8,128)(2,1)S(1)}, u32[]{:S(2)}, u32[]{:S(2)}) collective-permute-start(bf16[64,384]{1,0:T(8,128)(2,1)S(1)} %get-tuple-element.166), channel_id=1, source_target_pairs={{0,16},{4,20},{8,24},{12,28},{16,0},{20,4},{24,8},{28,12},{1,17},{... | collective-permute-start | bytes 147464 | tf_op jit(solution)/shard_map/ppermute | solution.py:591
  221.5 4.6 %collective-permute-start.34 = (bf16[64,384]{1,0:T(8,128)(2,1)S(1)}, bf16[64,384]{1,0:T(8,128)(2,1)S(1)}, u32[]{:S(2)}, u32[]{:S(2)}) collective-permute-start(bf16[64,384]{1,0:T(8,128)(2,1)S(1)} %get-tuple-element.165), channel_id=1, source_target_pairs={{0,24},{4,28},{8,0},{12,4},{16,8},{20,12},{24,16},{28,20},{1,25},{... | collective-permute-start | bytes 147464 | tf_op jit(solution)/shard_map/ppermute | solution.py:591

commit v8 on v7

--- a/solution.py
+++ b/solution.py
@@ -607,10 +607,9 @@
     return jnp.concatenate([coarse * 2 + own % 2, coarse * 2 + 1 - own % 2])
 
 
-def collect_coarse(shard, flips=(0,)):
+def collect_coarse(shard):
     count = lax.axis_size("dp") // 2
-    pieces = [ahead(shard, step, flip) for flip in flips for step in range(count)[1 - flip :]]
-    return jnp.concatenate([shard] + pieces, axis=0)
+    return [shard] + [ahead(shard, step) for step in range(1, count)]
 
 
 def collect_rows(shard):
@@ -710,8 +709,12 @@
     direct = dp_count <= DIRECT
     if direct:
         place, groups = places(), dp_count
-        qkv_rows = collect_coarse(qkv, (0, 1))
-        mine = collect_coarse(rest)
+        wide = qkv.shape[1]
+        pieces = collect_coarse(jnp.concatenate([qkv, across(qkv)], axis=1))
+        qkv_rows = jnp.concatenate(
+            [piece[:, :wide] for piece in pieces] + [piece[:, wide:] for piece in pieces], axis=0
+        )
+        mine = jnp.concatenate(collect_coarse(rest), axis=0)
         first = (qkv_rows, mine)
         far_rows, other, far_mine = together(
             swap(qkv_rows, 2), in_hbm(across(mine)), in_hbm(swap(mine, 2))
@@ -787,7 +790,7 @@
         limit, x_blocks, clock, gain_one, two_grad, qkv_wide, middle_grad, high, low
     )
     if direct:
-        begin_grad, came_one = together(begin_grad, came_one)
+        begin_grad, came_one, up_pieces[2] = together(begin_grad, came_one, up_pieces[2])
         near = [grouped(value[None])[0] for value in (own_part, came_one, came_far)]
         qkv_value, qkv_pieces = fold_coarse(fold_pair(near)[1]())
         *up_pieces, down_came, _ = together(*up_pieces, down_rest()[-1], qkv_value)

time: 230 us -> 225 us (0.978)
  Pallas kernels: 84 us -> 75.4 us
  starting transfers between devices: 58.1 us -> 64.1 us
  waiting for transfers between devices: 58.3 us -> 53.3 us
  other arithmetic: 9.45 us -> 11.9 us
    ppermute x23 -> x20, waiting for transfers between devices: 37.5 us -> 27.7 us  [along_dp(): return lax.ppermute(value, 'dp', [(i, move(i)) for i in range(count)])]
    ppermute x16, starting transfers between devices: 7.49 us -> 15.1 us  [swap(): return lax.ppermute(value, 'tensor', [(i, i ^ apart) for i in range(count)])]
    pallas_call x1, Pallas kernels: 29 us -> 23.1 us  [middle_block(): pl.pallas_call(functools.partial(middle_kernel, groups), grid_spec=pltpu....]
    all_to_all x1, waiting for transfers between devices: 0.01 us -> 5.42 us  [on_device(): arranged = lax.all_to_all(arranged, 'tensor', 0, 0, tiled=True)]
    ppermute x23 -> x20, starting transfers between devices: 38 us -> 36.6 us  [along_dp(): return lax.ppermute(value, 'dp', [(i, move(i)) for i in range(count)])]
  transfers between devices with their start and end apart: 42 -> 39, of which waited for: 12 -> 13; matrix products, arithmetic and copies ran while one was open for 7% -> 9% of each run, Pallas kernels for 24% -> 23%
where the time goes in v8:
time: 225 us
  Pallas kernels  75.4 us (34%)
  starting transfers between devices  64.1 us (28%)
  waiting for transfers between devices  53.3 us (24%)
  local copies, waits for them, and re-layouts  16.2 us (7%)
  other arithmetic  11.9 us (5%)
  between operations  3.72 us (2%)
    ppermute x20, starting transfers between devices, along_dp(): return lax.ppermute(value, 'dp', [(i, move(i)) for i in range(count)])  36.6 us
    pallas_call x2, Pallas kernels, attend_back(): pl.pallas_call(attend_back_kernel, grid_spec=pltpu.PrefetchScalarGridSpec...  28.4 us
    ppermute x20, waiting for transfers between devices, along_dp(): return lax.ppermute(value, 'dp', [(i, move(i)) for i in range(count)])  27.7 us
    pallas_call x1, Pallas kernels, middle_block(): pl.pallas_call(functools.partial(middle_kernel, groups), grid_spec=pltpu....  23.1 us
    ppermute x16, waiting for transfers between devices, swap(): return lax.ppermute(value, 'tensor', [(i, i ^ apart) for i in range(count)])  20.2 us
    pallas_call x1, Pallas kernels, attend(): pl.pallas_call(attend_kernel, grid_spec=pltpu.PrefetchScalarGridSpec(num_...  15.4 us
    ppermute x16, starting transfers between devices, swap(): return lax.ppermute(value, 'tensor', [(i, i ^ apart) for i in range(count)])  15.1 us
    all_to_all x1, waiting for transfers between devices, on_device(): arranged = lax.all_to_all(arranged, 'tensor', 0, 0, tiled=True)  5.42 us
  transfers between devices with their start and end apart: 39, of which 13 were waited for; matrix products, arithmetic and copies ran while one was open for 9% of the time, Pallas kernels for 23%

profile of v8, /device:TPU:0, one launch (start us, length us, event | category | flops | bytes accessed | tf_op | source)
XLA Modules:
  0.0 224.6 jit_solution(10070833221376269422)
XLA Ops:
  0.6 1.0 pad_maximum_fusion.2
  1.6 3.1 %collective-permute-start.4 = (bf16[64,1152]{1,0:T(8,128)(2,1)S(1)}, bf16[64,1152]{1,0:T(8,128)(2,1)S(1)}, u32[]{:S(2)}, u32[]{:S(2)}) collective-permute-start(bf16[64,1152]{1,0:T(8,128)(2,1)S(1)} %pad_maximum_fusion.2), channel_id=1, source_target_pairs={{0,8},{4,12},{8,16},{12,20},{16,24},{20,28},{24,0},{28,4},{1,9},{5... | collective-permute-start | bytes 442376 | tf_op jit(solution)/shard_map/ppermute | solution.py:591
  4.7 2.6 %collective-permute-start.5 = (bf16[64,1152]{1,0:T(8,128)(2,1)S(1)}, bf16[64,1152]{1,0:T(8,128)(2,1)S(1)}, u32[]{:S(2)}, u32[]{:S(2)}) collective-permute-start(bf16[64,1152]{1,0:T(8,128)(2,1)S(1)} %pad_maximum_fusion.2), channel_id=1, source_target_pairs={{0,16},{4,20},{8,24},{12,28},{16,0},{20,4},{24,8},{28,12},{1,17},{... | collective-permute-start | bytes 442376 | tf_op jit(solution)/shard_map/ppermute | solution.py:591
  7.3 1.3 collective-permute-start.6
  8.6 0.8 copy_bitcast_fusion.2
  9.4 1.5 collective-permute-start
  11.0 0.8 constant_dynamic-update-slice_fusion.1
  11.8 0.7 reshape.155
  12.7 0.7 fusion.12
  13.5 0.7 gather_fusion
  14.3 0.7 collective-permute-start.1
  15.1 1.1 pad_maximum_fusion
  16.2 3.7 %all-to-all-start = ((bf16[32,136,128]{2,1,0:T(8,128)(2,1)}), bf16[32,136,128]{2,1,0:T(8,128)(2,1)S(1)}, u32[]{:S(2)}, u32[]{:S(2)}) async-start(bf16[32,136,128]{2,1,0:T(8,128)(2,1)} %pad_maximum_fusion), calls=%async_computation | async-start | bytes 2228224 | tf_op jit(solution)/shard_map/all_to_all | solution.py:735
  20.9 2.3 %collective-permute-start.3 = (bf16[64,768]{1,0:T(8,128)(2,1)S(1)}, bf16[64,768]{1,0:T(8,128)(2,1)S(1)}, u32[]{:S(2)}, u32[]{:S(2)}) collective-permute-start(bf16[64,768]{1,0:T(8,128)(2,1)S(1)} %constant_dynamic-update-slice_fusion), channel_id=1, source_target_pairs={{0,24},{4,28},{8,0},{12,4},{16,8},{20,12},{24,16},{28,20},{1,25},{... | collective-permute-start | bytes 294920 | tf_op jit(solution)/shard_map/ppermute | solution.py:591
  23.2 5.3 %collective-permute-done.2 = bf16[64,768]{1,0:T(8,128)(2,1)S(1)} collective-permute-done((bf16[64,768]{1,0:T(8,128)(2,1)S(1)}, bf16[64,768]{1,0:T(8,128)(2,1)S(1)}, u32[]{:S(2)}, u32[]{:S(2)}) %collective-permute-start.2) | collective-permute-done | bytes 98336 | tf_op jit(solution)/shard_map/ppermute | solution.py:591
  28.7 0.9 pad_maximum_fusion.1.refs_0_
  29.6 5.4 %all-to-all-done = bf16[32,136,128]{2,1,0:T(8,128)(2,1)S(1)} async-done(((bf16[32,136,128]{2,1,0:T(8,128)(2,1)}), bf16[32,136,128]{2,1,0:T(8,128)(2,1)S(1)}, u32[]{:S(2)}, u32[]{:S(2)}) %all-to-all-start) | async-done | bytes 1114144 | tf_op jit(solution)/shard_map/all_to_all | solution.py:735
  35.0 1.1 copy.72
  36.1 4.8 %all-to-all-start.1 = ((bf16[8,4,136,128]{3,2,1,0:T(8,128)(2,1)}), bf16[8,4,136,128]{3,2,1,0:T(8,128)(2,1)S(1)}, u32[]{:S(2)}, u32[]{:S(2)}) async-start(bf16[8,4,136,128]{3,2,1,0:T(8,128)(2,1)} %bitcast.128), calls=%async_computation.1 | async-start | bytes 2228224 | tf_op jit(solution)/shard_map/all_to_all | solution.py:737
  41.2 2.0 collective-permute-start.9
  43.2 1.7 collective-permute-start.8
  48.9 15.2 %collective-permute-done.8.refs_2_ = bf16[512,384]{1,0:T(8,128)(2,1)S(1)} collective-permute-done((bf16[512,384]{1,0:T(8,128)(2,1)S(1)}, bf16[512,384]{1,0:T(8,128)(2,1)S(1)}, u32[]{:S(2)}, u32[]{:S(2)}) %collective-permute-start.8) | collective-permute-done | bytes 393248 | tf_op jit(solution)/shard_map/ppermute | solution.py:586
  64.1 3.6 %collective-permute-done.9.refs_1_ = bf16[256,1152]{1,0:T(8,128)(2,1)} collective-permute-done((bf16[256,1152]{1,0:T(8,128)(2,1)}, bf16[256,1152]{1,0:T(8,128)(2,1)}, u32[]{:S(2)}, u32[]{:S(2)}) %collective-permute-start.9) | collective-permute-done | bytes 589856 | tf_op jit(solution)/shard_map/ppermute | solution.py:591
  70.1 5.1 %project.1 = (bf16[1024,1536]{1,0:T(8,128)(2,1)S(1)}, bf16[512,1024]{1,0:T(8,128)(2,1)}, bf16[512,1536]{1,0:T(8,128)(2,1)}) custom-call(s32[1]{0:T(128)} %dynamic-slice.9.limit_ref, s32[8]{0:T(128)S(1)} %pad_add_fusion.place_ref, bf16[8,4,136,128]{3,2,1,0:T(8,128)(2,1)S(1)} %all-to-all-done.1.x_ref, f32[1,512]{1,0:T(1,128)S(1)} %pad_maximum_fusion.3.clock_ref, ...), custom_call_target="tpu_custom_call" | custom-call | flops 5750000128 | bytes 1048576 | tf_op jit(solution)/shard_map/project/pallas_call | solution.py:110
  75.3 15.4 %attend.1 = (bf16[1024,512]{1,0:T(8,128)(2,1)}, bf16[512,1024]{1,0:T(8,128)(2,1)}, f32[4,2,1024]{2,1,0:T(2,128)S(1)}) custom-call(s32[1]{0:T(128)} %dynamic-slice.9.limit_ref, bf16[1024,1536]{1,0:T(8,128)(2,1)S(1)} %get-tuple-element.65.q_ref.k_ref.v_ref, bf16[1024,1536]{1,0:T(8,128)(2,1)S(1)} %get-tuple-element.65.q_ref.k_ref.v_ref, ...), custom_call_target="tpu_custom_call" | custom-call | flops 17250000896 | bytes 1048576 | tf_op jit(solution)/shard_map/attend/pallas_call | solution.py:199
  90.7 1.5 collective-permute-start.16
  92.3 1.7 collective-permute-done.16.refs_7_
  94.0 0.8 copy-done.17
  94.8 23.1 %middle.1 = (bf16[1,1024,512]{2,1,0:T(8,128)(2,1)}, bf16[1024,512]{1,0:T(8,128)(2,1)}, f32[1024,512]{1,0:T(8,128)}, f32[1,512]{1,0:T(1,128)S(1)}, bf16[2,512,640...) custom-call(s32[1]{0:T(128)} %dynamic-slice.9.limit_ref, ...), custom_call_target="tpu_custom_call" | custom-call | flops 28750000128 | bytes 1048576 | tf_op jit(solution)/shard_map/middle/pallas_call | solution.py:370
  117.9 6.4 %collective-permute-start.18 = (bf16[2,512,512]{2,1,0:T(8,128)(2,1)}, bf16[2,512,512]{2,1,0:T(8,128)(2,1)}, u32[]{:S(2)}, u32[]{:S(2)}) collective-permute-start(bf16[2,512,512]{2,1,0:T(8,128)(2,1)} %get-tuple-element.83), channel_id=1, source_target_pairs={{0,1},{1,0},{2,3},{3,2},{4,5},{5,4},{6,7},{7,6},{8,9},{9,8},{10,11... | collective-permute-start | bytes 3145736 | tf_op jit(solution)/shard_map/ppermute | solution.py:586
  124.4 3.2 %collective-permute-done.18 = bf16[2,512,512]{2,1,0:T(8,128)(2,1)} collective-permute-done((bf16[2,512,512]{2,1,0:T(8,128)(2,1)}, bf16[2,512,512]{2,1,0:T(8,128)(2,1)}, u32[]{:S(2)}, u32[]{:S(2)}) %collective-permute-start.18) | collective-permute-done | bytes 1048608 | tf_op jit(solution)/shard_map/ppermute | solution.py:586
  127.6 2.0 convert_add_fusion
  129.6 0.9 collective-permute-start.19
  130.4 1.3 fusion.1
  131.7 1.0 collective-permute-start.20
  132.7 1.2 copy-done.7
  133.9 14.2 %attend_back.2 = (bf16[1024,768]{1,0:T(8,128)(2,1)S(1)}, bf16[512,384]{1,0:T(8,128)(2,1)S(1)}, bf16[512,384]{1,0:T(8,128)(2,1)S(1)}) custom-call(s32[1]{0:T(128)} %dynamic-slice.9.limit_ref, bf16[1024,1536]{1,0:T(8,128)(2,1)S(1)} %copy-done.2, bf16[1024,1536]{1,0:T(8,128)(2,1)S(1)} %copy-done.2, bf16[1024,1536]{1,0:T(8,128)(2,1)S(1)} %copy-done.2, ...), custom_call_target="tpu_custom_call" | custom-call | flops 18400000000 | bytes 1048576 | tf_op jit(solution)/shard_map/attend_back/pallas_call | solution.py:465
  148.7 1.4 collective-permute-start.22
  150.3 1.5 collective-permute-start.24
  151.9 2.2 collective-permute-start.25
  154.1 1.1 collective-permute-start.26
  155.2 1.3 collective-permute-start.23
  156.6 14.2 %attend_back.3 = (bf16[1024,768]{1,0:T(8,128)(2,1)S(1)}, bf16[512,384]{1,0:T(8,128)(2,1)S(1)}, bf16[512,384]{1,0:T(8,128)(2,1)S(1)}) custom-call(s32[1]{0:T(128)} %dynamic-slice.9.limit_ref, bf16[1024,1536]{1,0:T(8,128)(2,1)S(1)} %copy-done.2, bf16[1024,1536]{1,0:T(8,128)(2,1)S(1)} %copy-done.2, bf16[1024,1536]{1,0:T(8,128)(2,1)S(1)} %copy-done.2, ...), custom_call_target="tpu_custom_call" | custom-call | flops 18400000000 | bytes 1048576 | tf_op jit(solution)/shard_map/attend_back/pallas_call | solution.py:465
  170.9 0.7 dynamic-slice_bitcast_fusion.4
  172.9 3.5 %begin_back.1 = bf16[8,4,136,128]{3,2,1,0:T(8,128)(2,1)} custom-call(s32[1]{0:T(128)} %dynamic-slice.9.limit_ref, bf16[8,4,136,128]{3,2,1,0:T(8,128)(2,1)S(1)} %all-to-all-done.1.x_ref, f32[1,512]{1,0:T(1,128)S(1)} %pad_maximum_fusion.3.clock_ref, f32[1,512]{1,0:T(1,128)S(1)} %reshape_squeeze.8.gain_ref, f32[1,512]{1,0:T(1,128)S(1)} %get-tuple-element.75.gg_two_ref, ...), custom_call_target="tpu_custom_call" | custom-call | flops 8049999872 | bytes 1048576 | tf_op jit(solution)/shard_map/begin_back/pallas_call | solution.py:553
  176.4 1.5 collective-permute-done.28
  178.5 0.7 copy-done.9
  179.2 4.0 %all-to-all-start.2 = ((bf16[32,136,128]{2,1,0:T(8,128)(2,1)}), bf16[32,136,128]{2,1,0:T(8,128)(2,1)S(1)}, u32[]{:S(2)}, u32[]{:S(2)}) async-start(bf16[32,136,128]{2,1,0:T(8,128)(2,1)} %bitcast.29), calls=%async_computation.2 | async-start | bytes 2228224 | tf_op jit(solution)/shard_map/all_to_all | solution.py:804
  183.3 0.7 scatter_custom_fusion
  184.0 1.7 fusion.4
  185.7 1.8 collective-permute-start.29
  187.8 1.8 collective-permute-start.33
  189.5 2.1 collective-permute-start.34
  191.6 7.2 %collective-permute-done.29 = bf16[4,64,384]{2,1,0:T(8,128)(2,1)S(1)} collective-permute-done((bf16[4,64,384]{2,1,0:T(8,128)(2,1)}, bf16[4,64,384]{2,1,0:T(8,128)(2,1)S(1)}, u32[]{:S(2)}, u32[]{:S(2)}) %collective-permute-start.29) | collective-permute-done | bytes 196640 | tf_op jit(solution)/shard_map/ppermute | solution.py:591
  198.8 1.0 fusion.3
  199.8 1.3 collective-permute-done.35
  201.1 7.0 %collective-permute-done.33 = bf16[64,640]{1,0:T(8,128)(2,1)S(1)} collective-permute-done((bf16[64,640]{1,0:T(8,128)(2,1)}, bf16[64,640]{1,0:T(8,128)(2,1)S(1)}, u32[]{:S(2)}, u32[]{:S(2)}) %collective-permute-start.33) | collective-permute-done | bytes 81952 | tf_op jit(solution)/shard_map/ppermute | solution.py:591
  208.1 8.0 %collective-permute-start.30 = (bf16[64,384]{1,0:T(8,128)(2,1)S(1)}, bf16[64,384]{1,0:T(8,128)(2,1)S(1)}, u32[]{:S(2)}, u32[]{:S(2)}) collective-permute-start(bf16[64,384]{1,0:T(8,128)(2,1)S(1)} %get-tuple-element.166), channel_id=1, source_target_pairs={{0,8},{4,12},{8,16},{12,20},{16,24},{20,28},{24,0},{28,4},{1,9},{5... | collective-permute-start | bytes 147464 | tf_op jit(solution)/shard_map/ppermute | solution.py:591
  216.1 2.4 %collective-permute-start.32 = (bf16[64,384]{1,0:T(8,128)(2,1)S(1)}, bf16[64,384]{1,0:T(8,128)(2,1)S(1)}, u32[]{:S(2)}, u32[]{:S(2)}) collective-permute-start(bf16[64,384]{1,0:T(8,128)(2,1)S(1)} %get-tuple-element.167), channel_id=1, source_target_pairs={{0,24},{4,28},{8,0},{12,4},{16,8},{20,12},{24,16},{28,20},{1,25},{... | collective-permute-start | bytes 147464 | tf_op jit(solution)/shard_map/ppermute | solution.py:591
  218.5 0.7 add_bitcast_fusion
  220.6 0.8 collective-permute-done.31
  221.4 0.7 copy_bitcast_fusion.1
  222.1 0.8 gather_fusion.1
  222.8 1.1 slice.117
  (129 shorter events, 11.1 us)
Async XLA Ops:
  0.6 12.9 %copy-start = (bf16[32,128,128]{2,1,0:T(8,128)(2,1)S(1)}, bf16[32,128,128]{2,1,0:T(8,128)(2,1)}, u32[]{:S(2)}) copy-start(bf16[32,128,128]{2,1,0:T(8,128)(2,1)} %param.11) | copy-start | bytes 3145732
  1.6 27.0 %collective-permute-start.4 = (bf16[64,1152]{1,0:T(8,128)(2,1)S(1)}, bf16[64,1152]{1,0:T(8,128)(2,1)S(1)}, u32[]{:S(2)}, u32[]{:S(2)}) collective-permute-start(bf16[64,1152]{1,0:T(8,128)(2,1)S(1)} %pad_maximum_fusion.2), channel_id=1, source_target_pairs={{0,8},{4,12},{8,16},{12,20},{16,24},{20,28},{24,0},{28,4},{1,9},{5... | collective-permute-start | bytes 442376 | tf_op jit(solution)/shard_map/ppermute | solution.py:591
  4.7 23.9 %collective-permute-start.5 = (bf16[64,1152]{1,0:T(8,128)(2,1)S(1)}, bf16[64,1152]{1,0:T(8,128)(2,1)S(1)}, u32[]{:S(2)}, u32[]{:S(2)}) collective-permute-start(bf16[64,1152]{1,0:T(8,128)(2,1)S(1)} %pad_maximum_fusion.2), channel_id=1, source_target_pairs={{0,16},{4,20},{8,24},{12,28},{16,0},{20,4},{24,8},{28,12},{1,17},{... | collective-permute-start | bytes 442376 | tf_op jit(solution)/shard_map/ppermute | solution.py:591
  7.3 21.4 %collective-permute-start.6 = (bf16[64,1152]{1,0:T(8,128)(2,1)S(1)}, bf16[64,1152]{1,0:T(8,128)(2,1)S(1)}, u32[]{:S(2)}, u32[]{:S(2)}) collective-permute-start(bf16[64,1152]{1,0:T(8,128)(2,1)S(1)} %pad_maximum_fusion.2), channel_id=1, source_target_pairs={{0,24},{4,28},{8,0},{12,4},{16,8},{20,12},{24,16},{28,20},{1,25},{... | collective-permute-start | bytes 442376 | tf_op jit(solution)/shard_map/ppermute | solution.py:591
  9.4 4.8 %collective-permute-start = (bf16[64,384]{1,0:T(8,128)(2,1)S(1)}, bf16[64,384]{1,0:T(8,128)(2,1)S(1)}, u32[]{:S(2)}, u32[]{:S(2)}) collective-permute-start(bf16[64,384]{1,0:T(8,128)(2,1)S(1)} %copy_bitcast_fusion.2), channel_id=1, source_target_pairs={{0,4},{4,0},{8,12},{12,8},{16,20},{20,16},{24,28},{28,24},{1,5},{5... | collective-permute-start | bytes 147464 | tf_op jit(solution)/shard_map/ppermute | solution.py:591
  14.3 6.6 %collective-permute-start.1 = (bf16[64,768]{1,0:T(8,128)(2,1)S(1)}, bf16[64,768]{1,0:T(8,128)(2,1)S(1)}, u32[]{:S(2)}, u32[]{:S(2)}) collective-permute-start(bf16[64,768]{1,0:T(8,128)(2,1)S(1)} %constant_dynamic-update-slice_fusion), channel_id=1, source_target_pairs={{0,8},{4,12},{8,16},{12,20},{16,24},{20,28},{24,0},{28,4},{1,9},{5... | collective-permute-start | bytes 294920 | tf_op jit(solution)/shard_map/ppermute | solution.py:591
  16.2 12.5 %copy-start.10 = (bf16[512,64]{0,1:T(8,128)(2,1)S(1)}, bf16[512,64]{0,1:T(8,128)(2,1)}, u32[]{:S(2)}) copy-start(bf16[512,64]{0,1:T(8,128)(2,1)} %param.18) | copy-start | bytes 196612
  16.2 12.5 %copy-start.11 = (bf16[64,512]{1,0:T(8,128)(2,1)S(1)}, bf16[64,512]{1,0:T(8,128)(2,1)}, u32[]{:S(2)}) copy-start(bf16[64,512]{1,0:T(8,128)(2,1)} %param.17) | copy-start | bytes 196612
  16.2 12.5 %copy-start.14 = (bf16[128,64]{0,1:T(8,128)(2,1)S(1)}, bf16[128,64]{0,1:T(8,128)(2,1)}, u32[]{:S(2)}) copy-start(bf16[128,64]{0,1:T(8,128)(2,1)} %param.16) | copy-start | bytes 49156
  16.2 18.8 %all-to-all-start = ((bf16[32,136,128]{2,1,0:T(8,128)(2,1)}), bf16[32,136,128]{2,1,0:T(8,128)(2,1)S(1)}, u32[]{:S(2)}, u32[]{:S(2)}) async-start(bf16[32,136,128]{2,1,0:T(8,128)(2,1)} %pad_maximum_fusion), calls=%async_computation | async-start | bytes 2228224 | tf_op jit(solution)/shard_map/all_to_all | solution.py:735
  19.9 8.7 %collective-permute-start.2 = (bf16[64,768]{1,0:T(8,128)(2,1)S(1)}, bf16[64,768]{1,0:T(8,128)(2,1)S(1)}, u32[]{:S(2)}, u32[]{:S(2)}) collective-permute-start(bf16[64,768]{1,0:T(8,128)(2,1)S(1)} %constant_dynamic-update-slice_fusion), channel_id=1, source_target_pairs={{0,16},{4,20},{8,24},{12,28},{16,0},{20,4},{24,8},{28,12},{1,17},{... | collective-permute-start | bytes 294920 | tf_op jit(solution)/shard_map/ppermute | solution.py:591
  20.9 7.7 %collective-permute-start.3 = (bf16[64,768]{1,0:T(8,128)(2,1)S(1)}, bf16[64,768]{1,0:T(8,128)(2,1)S(1)}, u32[]{:S(2)}, u32[]{:S(2)}) collective-permute-start(bf16[64,768]{1,0:T(8,128)(2,1)S(1)} %constant_dynamic-update-slice_fusion), channel_id=1, source_target_pairs={{0,24},{4,28},{8,0},{12,4},{16,8},{20,12},{24,16},{28,20},{1,25},{... | collective-permute-start | bytes 294920 | tf_op jit(solution)/shard_map/ppermute | solution.py:591
  36.1 8.8 %copy-start.15 = (s32[32]{0:T(128)S(1)}, s32[32]{0:T(128)}, u32[]{:S(2)}) copy-start(s32[32]{0:T(128)} %param.14) | copy-start | bytes 388
  36.1 11.3 %copy-start.18 = (s32[32]{0:T(128)S(1)}, s32[32]{0:T(128)}, u32[]{:S(2)}) copy-start(s32[32]{0:T(128)} %param.12) | copy-start | bytes 388
  36.1 31.7 %copy-start.19 = (s32[32]{0:T(128)S(1)}, s32[32]{0:T(128)}, u32[]{:S(2)}) copy-start(s32[32]{0:T(128)} %param.13) | copy-start | bytes 388
  36.1 33.4 %all-to-all-start.1 = ((bf16[8,4,136,128]{3,2,1,0:T(8,128)(2,1)}), bf16[8,4,136,128]{3,2,1,0:T(8,128)(2,1)S(1)}, u32[]{:S(2)}, u32[]{:S(2)}) async-start(bf16[8,4,136,128]{3,2,1,0:T(8,128)(2,1)} %bitcast.128), calls=%async_computation.1 | async-start | bytes 2228224 | tf_op jit(solution)/shard_map/all_to_all | solution.py:737
  40.9 23.2 %collective-permute-start.10 = (bf16[256,1152]{1,0:T(8,128)(2,1)}, bf16[256,1152]{1,0:T(8,128)(2,1)}, u32[]{:S(2)}, u32[]{:S(2)}) collective-permute-start(bf16[256,1152]{1,0:T(8,128)(2,1)} %pad_maximum_fusion.1.refs_0_), channel_id=1, source_target_pairs={{0,2},{1,3},{2,0},{3,1},{4,6},{5,7},{6,4},{7,5},{8,10},{9,11},{10,... | collective-permute-start | bytes 1769480 | tf_op jit(solution)/shard_map/ppermute | solution.py:586
  41.2 26.5 %collective-permute-start.9 = (bf16[256,1152]{1,0:T(8,128)(2,1)}, bf16[256,1152]{1,0:T(8,128)(2,1)}, u32[]{:S(2)}, u32[]{:S(2)}) collective-permute-start(bf16[256,1152]{1,0:T(8,128)(2,1)} %pad_maximum_fusion.1.refs_0_), channel_id=1, source_target_pairs={{0,4},{4,0},{8,12},{12,8},{16,20},{20,16},{24,28},{28,24},{1,5},{5... | collective-permute-start | bytes 1769480 | tf_op jit(solution)/shard_map/ppermute | solution.py:591
  43.2 20.8 %collective-permute-start.8 = (bf16[512,384]{1,0:T(8,128)(2,1)S(1)}, bf16[512,384]{1,0:T(8,128)(2,1)S(1)}, u32[]{:S(2)}, u32[]{:S(2)}) collective-permute-start(bf16[512,384]{1,0:T(8,128)(2,1)S(1)} %slice_dynamic-update-slice_fusion.refs_0_), channel_id=1, source_target_pairs={{0,2},{1,3},{2,0},{3,1},{4,6},{5,7},{6,4},{7,5},{8,10},{9,11},{10,... | collective-permute-start | bytes 1179656 | tf_op jit(solution)/shard_map/ppermute | solution.py:586
  48.8 21.0 %collective-permute-start.7 = (bf16[512,384]{1,0:T(8,128)(2,1)S(1)}, bf16[512,384]{1,0:T(8,128)(2,1)S(1)}, u32[]{:S(2)}, u32[]{:S(2)}) collective-permute-start(bf16[512,384]{1,0:T(8,128)(2,1)S(1)} %slice_dynamic-update-slice_fusion.refs_0_), channel_id=1, source_target_pairs={{0,1},{1,0},{2,3},{3,2},{4,5},{5,4},{6,7},{7,6},{8,9},{9,8},{10,11... | collective-permute-start | bytes 1179656 | tf_op jit(solution)/shard_map/ppermute | solution.py:586
  67.7 2.4 %collective-permute-start.11 = (bf16[512,384]{1,0:T(8,128)(2,1)S(1)}, bf16[512,384]{1,0:T(8,128)(2,1)}, u32[]{:S(2)}, u32[]{:S(2)}) collective-permute-start(bf16[512,384]{1,0:T(8,128)(2,1)S(1)} %collective-permute-done.8.refs_2_), channel_id=1, source_target_pairs={{0,1},{1,0},{2,3},{3,2},{4,5},{5,4},{6,7},{7,6},{8,9},{9,8},{10,11... | collective-permute-start | bytes 1179656 | tf_op jit(solution)/shard_map/ppermute | solution.py:586
  68.4 22.3 %collective-permute-start.12 = (bf16[256,1152]{1,0:T(8,128)(2,1)}, bf16[256,1152]{1,0:T(8,128)(2,1)}, u32[]{:S(2)}, u32[]{:S(2)}) collective-permute-start(bf16[256,1152]{1,0:T(8,128)(2,1)} %pad_maximum_fusion.1.refs_0_), channel_id=1, source_target_pairs={{0,1},{1,0},{2,3},{3,2},{4,5},{5,4},{6,7},{7,6},{8,9},{9,8},{10,11... | collective-permute-start | bytes 1769480 | tf_op jit(solution)/shard_map/ppermute | solution.py:586
  68.9 21.8 %collective-permute-start.13 = (bf16[256,1152]{1,0:T(8,128)(2,1)}, bf16[256,1152]{1,0:T(8,128)(2,1)}, u32[]{:S(2)}, u32[]{:S(2)}) collective-permute-start(bf16[256,1152]{1,0:T(8,128)(2,1)} %collective-permute-done.9.refs_1_), channel_id=1, source_target_pairs={{0,1},{1,0},{2,3},{3,2},{4,5},{5,4},{6,7},{7,6},{8,9},{9,8},{10,11... | collective-permute-start | bytes 1769480 | tf_op jit(solution)/shard_map/ppermute | solution.py:586
  68.9 21.8 %collective-permute-start.15 = (bf16[256,1152]{1,0:T(8,128)(2,1)}, bf16[256,1152]{1,0:T(8,128)(2,1)}, u32[]{:S(2)}, u32[]{:S(2)}) collective-permute-start(bf16[256,1152]{1,0:T(8,128)(2,1)} %collective-permute-done.9.refs_1_), channel_id=1, source_target_pairs={{0,2},{1,3},{2,0},{3,1},{4,6},{5,7},{6,4},{7,5},{8,10},{9,11},{10,... | collective-permute-start | bytes 1769480 | tf_op jit(solution)/shard_map/ppermute | solution.py:586
  69.8 20.8 %collective-permute-start.14 = (bf16[256,1152]{1,0:T(8,128)(2,1)}, bf16[256,1152]{1,0:T(8,128)(2,1)S(1)}, u32[]{:S(2)}, u32[]{:S(2)}) collective-permute-start(bf16[256,1152]{1,0:T(8,128)(2,1)} %collective-permute-done.10.refs_4_), channel_id=1, source_target_pairs={{0,1},{1,0},{2,3},{3,2},{4,5},{5,4},{6,7},{7,6},{8,9},{9,8},{10,11... | collective-permute-start | bytes 1769480 | tf_op jit(solution)/shard_map/ppermute | solution.py:586
  75.3 15.4 %copy-start.1 = (bf16[1024,1536]{1,0:T(8,128)(2,1)}, bf16[1024,1536]{1,0:T(8,128)(2,1)S(1)}, u32[]{:S(2)}) copy-start(bf16[1024,1536]{1,0:T(8,128)(2,1)S(1)} %get-tuple-element.65.q_ref.k_ref.v_ref) | copy-start | bytes 9437188
  90.7 1.5 copy-start.16
  90.7 3.3 %collective-permute-start.16 = (bf16[256,1152]{1,0:T(8,128)(2,1)}, bf16[256,1152]{1,0:T(8,128)(2,1)S(1)}, u32[]{:S(2)}, u32[]{:S(2)}) collective-permute-start(bf16[256,1152]{1,0:T(8,128)(2,1)} %collective-permute-done.15.refs_5_), channel_id=1, source_target_pairs={{0,1},{1,0},{2,3},{3,2},{4,5},{5,4},{6,7},{7,6},{8,9},{9,8},{10,11... | collective-permute-start | bytes 1769480 | tf_op jit(solution)/shard_map/ppermute | solution.py:586
  94.0 0.8 copy-start.17
  117.9 9.8 %collective-permute-start.18 = (bf16[2,512,512]{2,1,0:T(8,128)(2,1)}, bf16[2,512,512]{2,1,0:T(8,128)(2,1)}, u32[]{:S(2)}, u32[]{:S(2)}) collective-permute-start(bf16[2,512,512]{2,1,0:T(8,128)(2,1)} %get-tuple-element.83), channel_id=1, source_target_pairs={{0,1},{1,0},{2,3},{3,2},{4,5},{5,4},{6,7},{7,6},{8,9},{9,8},{10,11... | collective-permute-start | bytes 3145736 | tf_op jit(solution)/shard_map/ppermute | solution.py:586
  124.3 6.2 %collective-permute-start.17 = (bf16[2,512,640]{2,1,0:T(8,128)(2,1)}, bf16[2,512,640]{2,1,0:T(8,128)(2,1)S(1)}, u32[]{:S(2)}, u32[]{:S(2)}) collective-permute-start(bf16[2,512,640]{2,1,0:T(8,128)(2,1)} %get-tuple-element.78), channel_id=1, source_target_pairs={{0,1},{1,0},{2,3},{3,2},{4,5},{5,4},{6,7},{7,6},{8,9},{9,8},{10,11... | collective-permute-start | bytes 3932168 | tf_op jit(solution)/shard_map/ppermute | solution.py:586
  127.6 5.1 %copy-start.2 = (bf16[1024,1536]{1,0:T(8,128)(2,1)S(1)}, bf16[1024,1536]{1,0:T(8,128)(2,1)}, u32[]{:S(2)}) copy-start(bf16[1024,1536]{1,0:T(8,128)(2,1)} %copy-done.1) | copy-start | bytes 9437188
  127.6 5.1 %copy-start.6 = (bf16[512,1024]{1,0:T(8,128)(2,1)S(1)}, bf16[512,1024]{1,0:T(8,128)(2,1)}, u32[]{:S(2)}) copy-start(bf16[512,1024]{1,0:T(8,128)(2,1)} %get-tuple-element.79.turn_ref) | copy-start | bytes 3145732
  129.6 3.1 %copy-start.5 = (bf16[512,1024]{1,0:T(8,128)(2,1)S(1)}, bf16[512,1024]{1,0:T(8,128)(2,1)}, u32[]{:S(2)}) copy-start(bf16[512,1024]{1,0:T(8,128)(2,1)} %get-tuple-element.85.n_turn_ref) | copy-start | bytes 3145732
  129.6 18.5 %collective-permute-start.19 = (bf16[4,2,64,512]{3,2,1,0:T(8,128)(2,1)S(1)}, bf16[4,2,64,512]{3,2,1,0:T(8,128)(2,1)S(1)}, u32[]{:S(2)}, u32[]{:S(2)}) collective-permute-start(bf16[4,2,64,512]{3,2,1,0:T(8,128)(2,1)S(1)} %bitcast.135), channel_id=1, source_target_pairs={{0,2},{1,3},{2,0},{3,1},{4,6},{5,7},{6,4},{7,5},{8,10},{9,11},{10,... | collective-permute-start | bytes 1572872 | tf_op jit(solution)/shard_map/ppermute | solution.py:586
  131.7 16.7 %collective-permute-start.20 = (bf16[2,4,64,640]{3,2,1,0:T(8,128)(2,1)S(1)}, bf16[2,4,64,640]{3,2,1,0:T(8,128)(2,1)S(1)}, u32[]{:S(2)}, u32[]{:S(2)}) collective-permute-start(bf16[2,4,64,640]{3,2,1,0:T(8,128)(2,1)S(1)} %fusion.1), channel_id=1, source_target_pairs={{0,4},{4,0},{8,12},{12,8},{16,20},{20,16},{24,28},{28,24},{1,5},{5... | collective-permute-start | bytes 1966088 | tf_op jit(solution)/shard_map/ppermute | solution.py:591
  132.7 1.2 copy-start.7
  133.9 14.5 %copy-start.8 = (bf16[2,512,640]{2,1,0:T(8,128)(2,1)S(1)}, bf16[2,512,640]{2,1,0:T(8,128)(2,1)}, u32[]{:S(2)}) copy-start(bf16[2,512,640]{2,1,0:T(8,128)(2,1)} %get-tuple-element.77) | copy-start | bytes 3932164
  148.4 6.7 %collective-permute-start.21 = (bf16[512,384]{1,0:T(8,128)(2,1)S(1)}, bf16[512,384]{1,0:T(8,128)(2,1)S(1)}, u32[]{:S(2)}, u32[]{:S(2)}) collective-permute-start(bf16[512,384]{1,0:T(8,128)(2,1)S(1)} %get-tuple-element.94), channel_id=1, source_target_pairs={{0,1},{1,0},{2,3},{3,2},{4,5},{5,4},{6,7},{7,6},{8,9},{9,8},{10,11... | collective-permute-start | bytes 1179656 | tf_op jit(solution)/shard_map/ppermute | solution.py:586
  148.7 22.1 %collective-permute-start.22 = (bf16[4,64,640]{2,1,0:T(8,128)(2,1)S(1)}, bf16[4,64,640]{2,1,0:T(8,128)(2,1)S(1)}, u32[]{:S(2)}, u32[]{:S(2)}) collective-permute-start(bf16[4,64,640]{2,1,0:T(8,128)(2,1)S(1)} %slice_bitcast_fusion), channel_id=1, source_target_pairs={{0,2},{1,3},{2,0},{3,1},{4,6},{5,7},{6,4},{7,5},{8,10},{9,11},{10,... | collective-permute-start | bytes 983048 | tf_op jit(solution)/shard_map/ppermute | solution.py:586
  150.3 20.4 %collective-permute-start.24 = (bf16[2,64,512]{2,1,0:T(8,128)(2,1)S(1)}, bf16[2,64,512]{2,1,0:T(8,128)(2,1)S(1)}, u32[]{:S(2)}, u32[]{:S(2)}) collective-permute-start(bf16[2,64,512]{2,1,0:T(8,128)(2,1)S(1)} %get-tuple-element.160), channel_id=1, source_target_pairs={{0,8},{4,12},{8,16},{12,20},{16,24},{20,28},{24,0},{28,4},{1,9},{5... | collective-permute-start | bytes 393224 | tf_op jit(solution)/shard_map/ppermute | solution.py:591
  151.9 18.9 %collective-permute-start.25 = (bf16[2,64,512]{2,1,0:T(8,128)(2,1)S(1)}, bf16[2,64,512]{2,1,0:T(8,128)(2,1)S(1)}, u32[]{:S(2)}, u32[]{:S(2)}) collective-permute-start(bf16[2,64,512]{2,1,0:T(8,128)(2,1)S(1)} %get-tuple-element.159), channel_id=1, source_target_pairs={{0,16},{4,20},{8,24},{12,28},{16,0},{20,4},{24,8},{28,12},{1,17},{... | collective-permute-start | bytes 393224 | tf_op jit(solution)/shard_map/ppermute | solution.py:591
  154.1 16.7 %collective-permute-start.26 = (bf16[2,64,512]{2,1,0:T(8,128)(2,1)S(1)}, bf16[2,64,512]{2,1,0:T(8,128)(2,1)S(1)}, u32[]{:S(2)}, u32[]{:S(2)}) collective-permute-start(bf16[2,64,512]{2,1,0:T(8,128)(2,1)S(1)} %get-tuple-element.158), channel_id=1, source_target_pairs={{0,24},{4,28},{8,0},{12,4},{16,8},{20,12},{24,16},{28,20},{1,25},{... | collective-permute-start | bytes 393224 | tf_op jit(solution)/shard_map/ppermute | solution.py:591
  155.2 15.6 %collective-permute-start.23 = (bf16[512,384]{1,0:T(8,128)(2,1)S(1)}, bf16[512,384]{1,0:T(8,128)(2,1)S(1)}, u32[]{:S(2)}, u32[]{:S(2)}) collective-permute-start(bf16[512,384]{1,0:T(8,128)(2,1)S(1)} %add_convert_fusion.3), channel_id=1, source_target_pairs={{0,2},{1,3},{2,0},{3,1},{4,6},{5,7},{6,4},{7,5},{8,10},{9,11},{10,... | collective-permute-start | bytes 1179656 | tf_op jit(solution)/shard_map/ppermute | solution.py:586
  156.6 16.4 %copy-start.4 = (bf16[512,1536]{1,0:T(8,128)(2,1)S(1)}, bf16[512,1536]{1,0:T(8,128)(2,1)}, u32[]{:S(2)}) copy-start(bf16[512,1536]{1,0:T(8,128)(2,1)} %get-tuple-element.105.w_ref) | copy-start | bytes 4718596
  170.8 2.1 copy-start.3
  171.6 6.2 %collective-permute-start.28 = (bf16[64,640]{1,0:T(8,128)(2,1)S(1)}, bf16[64,640]{1,0:T(8,128)(2,1)S(1)}, u32[]{:S(2)}, u32[]{:S(2)}) collective-permute-start(bf16[64,640]{1,0:T(8,128)(2,1)S(1)} %get-tuple-element.165), channel_id=1, source_target_pairs={{0,16},{4,20},{8,24},{12,28},{16,0},{20,4},{24,8},{28,12},{1,17},{... | collective-permute-start | bytes 245768 | tf_op jit(solution)/shard_map/ppermute | solution.py:591
  172.9 5.0 %collective-permute-start.27 = (bf16[512,384]{1,0:T(8,128)(2,1)S(1)}, bf16[512,384]{1,0:T(8,128)(2,1)S(1)}, u32[]{:S(2)}, u32[]{:S(2)}) collective-permute-start(bf16[512,384]{1,0:T(8,128)(2,1)S(1)} %get-tuple-element.107), channel_id=1, source_target_pairs={{0,1},{1,0},{2,3},{3,2},{4,5},{5,4},{6,7},{7,6},{8,9},{9,8},{10,11... | collective-permute-start | bytes 1179656 | tf_op jit(solution)/shard_map/ppermute | solution.py:586
  177.9 0.6 copy-start.12
  178.5 0.7 copy-start.9
  179.2 42.8 %all-to-all-start.2 = ((bf16[32,136,128]{2,1,0:T(8,128)(2,1)}), bf16[32,136,128]{2,1,0:T(8,128)(2,1)S(1)}, u32[]{:S(2)}, u32[]{:S(2)}) async-start(bf16[32,136,128]{2,1,0:T(8,128)(2,1)} %bitcast.29), calls=%async_computation.2 | async-start | bytes 2228224 | tf_op jit(solution)/shard_map/all_to_all | solution.py:804
  185.7 13.1 %collective-permute-start.29 = (bf16[4,64,384]{2,1,0:T(8,128)(2,1)}, bf16[4,64,384]{2,1,0:T(8,128)(2,1)S(1)}, u32[]{:S(2)}, u32[]{:S(2)}) collective-permute-start(bf16[4,64,384]{2,1,0:T(8,128)(2,1)} %fusion.4), channel_id=1, source_target_pairs={{0,4},{4,0},{8,12},{12,8},{16,20},{20,16},{24,28},{28,24},{1,5},{5... | collective-permute-start | bytes 589832 | tf_op jit(solution)/shard_map/ppermute | solution.py:591
  187.4 31.8 %copy-start.13 = (bf16[64,640]{1,0:T(8,128)(2,1)S(1)}, bf16[64,640]{1,0:T(8,128)(2,1)}, u32[]{:S(2)}) copy-start(bf16[64,640]{1,0:T(8,128)(2,1)} %copy-done.12) | copy-start | bytes 245764
  187.4 13.7 %collective-permute-start.35 = (bf16[1,64,512]{2,1,0:T(8,128)(2,1)}, bf16[1,64,512]{2,1,0:T(8,128)(2,1)S(1)}, u32[]{:S(2)}, u32[]{:S(2)}) collective-permute-start(bf16[1,64,512]{2,1,0:T(8,128)(2,1)} %dynamic-slice_convert_fusion), channel_id=1, source_target_pairs={{0,4},{4,0},{8,12},{12,8},{16,20},{20,16},{24,28},{28,24},{1,5},{5... | collective-permute-start | bytes 196616 | tf_op jit(solution)/shard_map/ppermute | solution.py:591
  187.8 20.4 %collective-permute-start.33 = (bf16[64,640]{1,0:T(8,128)(2,1)}, bf16[64,640]{1,0:T(8,128)(2,1)S(1)}, u32[]{:S(2)}, u32[]{:S(2)}) collective-permute-start(bf16[64,640]{1,0:T(8,128)(2,1)} %get-tuple-element.163), channel_id=1, source_target_pairs={{0,8},{4,12},{8,16},{12,20},{16,24},{20,28},{24,0},{28,4},{1,9},{5... | collective-permute-start | bytes 245768 | tf_op jit(solution)/shard_map/ppermute | solution.py:591
  189.5 18.6 %collective-permute-start.34 = (bf16[64,640]{1,0:T(8,128)(2,1)}, bf16[64,640]{1,0:T(8,128)(2,1)S(1)}, u32[]{:S(2)}, u32[]{:S(2)}) collective-permute-start(bf16[64,640]{1,0:T(8,128)(2,1)} %get-tuple-element.162), channel_id=1, source_target_pairs={{0,24},{4,28},{8,0},{12,4},{16,8},{20,12},{24,16},{28,20},{1,25},{... | collective-permute-start | bytes 245768 | tf_op jit(solution)/shard_map/ppermute | solution.py:591
  208.1 12.4 %collective-permute-start.30 = (bf16[64,384]{1,0:T(8,128)(2,1)S(1)}, bf16[64,384]{1,0:T(8,128)(2,1)S(1)}, u32[]{:S(2)}, u32[]{:S(2)}) collective-permute-start(bf16[64,384]{1,0:T(8,128)(2,1)S(1)} %get-tuple-element.166), channel_id=1, source_target_pairs={{0,8},{4,12},{8,16},{12,20},{16,24},{20,28},{24,0},{28,4},{1,9},{5... | collective-permute-start | bytes 147464 | tf_op jit(solution)/shard_map/ppermute | solution.py:591
  216.1 5.3 %collective-permute-start.31 = (bf16[64,384]{1,0:T(8,128)(2,1)S(1)}, bf16[64,384]{1,0:T(8,128)(2,1)S(1)}, u32[]{:S(2)}, u32[]{:S(2)}) collective-permute-start(bf16[64,384]{1,0:T(8,128)(2,1)S(1)} %get-tuple-element.168), channel_id=1, source_target_pairs={{0,16},{4,20},{8,24},{12,28},{16,0},{20,4},{24,8},{28,12},{1,17},{... | collective-permute-start | bytes 147464 | tf_op jit(solution)/shard_map/ppermute | solution.py:591
  216.1 5.3 %collective-permute-start.32 = (bf16[64,384]{1,0:T(8,128)(2,1)S(1)}, bf16[64,384]{1,0:T(8,128)(2,1)S(1)}, u32[]{:S(2)}, u32[]{:S(2)}) collective-permute-start(bf16[64,384]{1,0:T(8,128)(2,1)S(1)} %get-tuple-element.167), channel_id=1, source_target_pairs={{0,24},{4,28},{8,0},{12,4},{16,8},{20,12},{24,16},{28,20},{1,25},{... | collective-permute-start | bytes 147464 | tf_op jit(solution)/shard_map/ppermute | solution.py:591

commit v9 on v8

--- a/solution.py
+++ b/solution.py
@@ -715,27 +715,21 @@
             [piece[:, :wide] for piece in pieces] + [piece[:, wide:] for piece in pieces], axis=0
         )
         mine = jnp.concatenate(collect_coarse(rest), axis=0)
-        first = (qkv_rows, mine)
         far_rows, other, far_mine = together(
             swap(qkv_rows, 2), in_hbm(across(mine)), in_hbm(swap(mine, 2))
         )
         qkv_parts = (qkv_rows, swap(qkv_rows, 1), far_rows, swap(far_rows, 1))
     else:
         place, groups = jnp.zeros((1,), jnp.int32), None
-        first = (collect_rows(qkv),)
-        qkv_parts = collect_columns(first[0])
+        qkv_parts = collect_columns(collect_rows(qkv))
         rest_parts = [(part,) for part in collect_columns(collect_rows(rest))]
 
     spare = jnp.stack(three_terms(gain_attn) + three_terms(gain_ffn)).reshape(1, 6 * per)
     spare = jnp.pad(spare, ((0, SPARE - 1), (0, width - 6 * per)))
-    by_tensor = deal_order.reshape(dp_count, tensor_count).T.reshape(devices)
     arranged = jnp.concatenate(
-        [states[by_tensor], jnp.broadcast_to(spare[None], (devices, SPARE, width))], axis=1
-    )
-    arranged = lax.all_to_all(arranged, "tensor", 0, 0, tiled=True)
-    arranged = arranged.reshape(tensor_count, dp_count, tokens + SPARE, width).swapaxes(0, 1)
-    x_blocks = lax.all_to_all(after(arranged, *first), "dp", 0, 0, tiled=True)
-    x_blocks = x_blocks.reshape(devices, tokens + SPARE, width)
+        [states[deal_order], jnp.broadcast_to(spare[None], (devices, SPARE, width))], axis=1
+    )
+    x_blocks = lax.all_to_all(arranged, both, 0, 0, tiled=True)
     gains = jnp.sum(x_blocks[:, tokens, : 6 * per].reshape(devices, 2, 3, per).astype(F32), axis=2)
     gain_one = gains[:, 0].reshape(1, features)
     gain_two = gains[:, 1].reshape(1, features)

time: 225 us -> 222 us (0.987)
  Pallas kernels: 75.4 us -> 84.1 us
  starting transfers between devices: 64.1 us -> 56.3 us
  waiting for transfers between devices: 53.3 us -> 49.6 us
  local copies, waits for them, and re-layouts: 16.2 us -> 13.9 us
    ppermute x20, waiting for transfers between devices: 27.7 us -> 37.1 us  [along_dp(): return lax.ppermute(value, 'dp', [(i, move(i)) for i in range(count)])]
    ppermute x16, waiting for transfers between devices: 20.2 us -> 12.6 us  [swap(): return lax.ppermute(value, 'tensor', [(i, i ^ apart) for i in range(count)])]
    pallas_call x1, Pallas kernels: 23.1 us -> 29 us  [middle_block(): pl.pallas_call(functools.partial(middle_kernel, groups), grid_spec=pltpu....]
    all_to_all x2 -> x1, starting transfers between devices: 8.41 us -> 2.8 us  [on_device(): x_blocks = lax.all_to_all(arranged, both, 0, 0, tiled=True)]
    all_to_all x2 -> x1, waiting for transfers between devices: 5.42 us -> 0.01 us  [on_device(): x_blocks = lax.all_to_all(arranged, both, 0, 0, tiled=True)]
    ppermute x16, starting transfers between devices: 15.1 us -> 10.4 us  [swap(): return lax.ppermute(value, 'tensor', [(i, i ^ apart) for i in range(count)])]
    ppermute x20, starting transfers between devices: 36.6 us -> 39 us  [along_dp(): return lax.ppermute(value, 'dp', [(i, move(i)) for i in range(count)])]
  transfers between devices with their start and end apart: 39 -> 38, of which waited for: 13 -> 12; matrix products, arithmetic and copies ran while one was open for 9% -> 9% of each run, Pallas kernels for 23% -> 25%
where the time goes in v9:
time: 222 us; the launch traced here: 221 us
  Pallas kernels  84.1 us (38%)
  starting transfers between devices  56.3 us (25%)
  waiting for transfers between devices  49.6 us (22%)
  local copies, waits for them, and re-layouts  13.9 us (6%)
  other arithmetic  13.5 us (6%)
  between operations  3.75 us (2%)
    ppermute x20, starting transfers between devices, along_dp(): return lax.ppermute(value, 'dp', [(i, move(i)) for i in range(count)])  39 us
    ppermute x20, waiting for transfers between devices, along_dp(): return lax.ppermute(value, 'dp', [(i, move(i)) for i in range(count)])  37.1 us
    pallas_call x1, Pallas kernels, middle_block(): pl.pallas_call(functools.partial(middle_kernel, groups), grid_spec=pltpu....  29 us
    pallas_call x2, Pallas kernels, attend_back(): pl.pallas_call(attend_back_kernel, grid_spec=pltpu.PrefetchScalarGridSpec...  28.4 us
    pallas_call x1, Pallas kernels, attend(): pl.pallas_call(attend_kernel, grid_spec=pltpu.PrefetchScalarGridSpec(num_...  15.4 us
    ppermute x16, waiting for transfers between devices, swap(): return lax.ppermute(value, 'tensor', [(i, i ^ apart) for i in range(count)])  12.6 us
    ppermute x16, starting transfers between devices, swap(): return lax.ppermute(value, 'tensor', [(i, i ^ apart) for i in range(count)])  10.4 us
    pallas_call x1, Pallas kernels, project(): pl.pallas_call(functools.partial(project_kernel, groups), grid_spec=pltpu...  6.27 us
  transfers between devices with their start and end apart: 38, of which 12 were waited for; matrix products, arithmetic and copies ran while one was open for 9% of the time, Pallas kernels for 25%

profile of v9, /device:TPU:0, one launch (start us, length us, event | category | flops | bytes accessed | tf_op | source)
XLA Modules:
  0.0 221.1 jit_solution(18429048443207703131)
XLA Ops:
  0.6 1.0 pad_maximum_fusion.2
  1.6 3.1 %collective-permute-start.6 = (bf16[64,1152]{1,0:T(8,128)(2,1)S(1)}, bf16[64,1152]{1,0:T(8,128)(2,1)S(1)}, u32[]{:S(2)}, u32[]{:S(2)}) collective-permute-start(bf16[64,1152]{1,0:T(8,128)(2,1)S(1)} %pad_maximum_fusion.2), channel_id=1, source_target_pairs={{0,8},{4,12},{8,16},{12,20},{16,24},{20,28},{24,0},{28,4},{1,9},{5... | collective-permute-start | bytes 442376 | tf_op jit(solution)/shard_map/ppermute | solution.py:591
  4.7 2.6 %collective-permute-start.7 = (bf16[64,1152]{1,0:T(8,128)(2,1)S(1)}, bf16[64,1152]{1,0:T(8,128)(2,1)S(1)}, u32[]{:S(2)}, u32[]{:S(2)}) collective-permute-start(bf16[64,1152]{1,0:T(8,128)(2,1)S(1)} %pad_maximum_fusion.2), channel_id=1, source_target_pairs={{0,16},{4,20},{8,24},{12,28},{16,0},{20,4},{24,8},{28,12},{1,17},{... | collective-permute-start | bytes 442376 | tf_op jit(solution)/shard_map/ppermute | solution.py:591
  7.3 1.3 collective-permute-start.8
  8.6 0.8 copy_bitcast_fusion.1
  9.4 1.5 collective-permute-start
  11.0 0.7 fusion.12
  11.8 0.7 compare_select_fusion.1
  12.5 0.7 gather_fusion
  13.2 1.1 pad_maximum_fusion
  14.4 2.8 %all-to-all-start = ((bf16[32,136,128]{2,1,0:T(8,128)(2,1)}), bf16[32,136,128]{2,1,0:T(8,128)(2,1)S(1)}, u32[]{:S(2)}, u32[]{:S(2)}) async-start(bf16[32,136,128]{2,1,0:T(8,128)(2,1)} %pad_maximum_fusion), calls=%async_computation | async-start | bytes 2228224 | tf_op jit(solution)/shard_map/all_to_all | solution.py:732
  21.7 1.7 collective-permute-start.1
  23.4 2.5 %collective-permute-start.2 = (bf16[64,768]{1,0:T(8,128)(2,1)S(1)}, bf16[64,768]{1,0:T(8,128)(2,1)S(1)}, u32[]{:S(2)}, u32[]{:S(2)}) collective-permute-start(bf16[64,768]{1,0:T(8,128)(2,1)S(1)} %constant_dynamic-update-slice_fusion), channel_id=1, source_target_pairs={{0,16},{4,20},{8,24},{12,28},{16,0},{20,4},{24,8},{28,12},{1,17},{... | collective-permute-start | bytes 294920 | tf_op jit(solution)/shard_map/ppermute | solution.py:591
  25.9 1.4 collective-permute-start.3
  27.3 0.9 pad_maximum_fusion.1.refs_0_
  28.3 1.5 collective-permute-start.10
  29.7 1.5 collective-permute-start.9
  31.2 11.2 %collective-permute-done.1 = bf16[64,768]{1,0:T(8,128)(2,1)S(1)} collective-permute-done((bf16[64,768]{1,0:T(8,128)(2,1)S(1)}, bf16[64,768]{1,0:T(8,128)(2,1)S(1)}, u32[]{:S(2)}, u32[]{:S(2)}) %collective-permute-start.1) | collective-permute-done | bytes 98336 | tf_op jit(solution)/shard_map/ppermute | solution.py:591
  42.4 9.2 %collective-permute-done.2 = bf16[64,768]{1,0:T(8,128)(2,1)S(1)} collective-permute-done((bf16[64,768]{1,0:T(8,128)(2,1)S(1)}, bf16[64,768]{1,0:T(8,128)(2,1)S(1)}, u32[]{:S(2)}, u32[]{:S(2)}) %collective-permute-start.2) | collective-permute-done | bytes 98336 | tf_op jit(solution)/shard_map/ppermute | solution.py:591
  51.7 1.6 collective-permute-start.5
  54.1 7.9 %collective-permute-done.5.refs_2_ = bf16[512,384]{1,0:T(8,128)(2,1)S(1)} collective-permute-done((bf16[512,384]{1,0:T(8,128)(2,1)S(1)}, bf16[512,384]{1,0:T(8,128)(2,1)S(1)}, u32[]{:S(2)}, u32[]{:S(2)}) %collective-permute-start.5) | collective-permute-done | bytes 393248 | tf_op jit(solution)/shard_map/ppermute | solution.py:586
  62.1 1.6 collective-permute-start.15
  64.6 1.0 collective-permute-done.11.refs_3_
  65.5 6.3 %project.1 = (bf16[1024,1536]{1,0:T(8,128)(2,1)S(1)}, bf16[512,1024]{1,0:T(8,128)(2,1)}, bf16[512,1536]{1,0:T(8,128)(2,1)}) custom-call(s32[1]{0:T(128)} %dynamic-slice.9.limit_ref, s32[8]{0:T(128)S(1)} %pad_add_fusion.place_ref, bf16[8,4,136,128]{3,2,1,0:T(8,128)(2,1)S(1)} %bitcast.117, f32[1,512]{1,0:T(1,128)S(1)} %pad_maximum_fusion.3.clock_ref, ...), custom_call_target="tpu_custom_call" | custom-call | flops 5750000128 | bytes 1048576 | tf_op jit(solution)/shard_map/project/pallas_call | solution.py:110
  71.8 15.4 %attend.1 = (bf16[1024,512]{1,0:T(8,128)(2,1)}, bf16[512,1024]{1,0:T(8,128)(2,1)}, f32[4,2,1024]{2,1,0:T(2,128)S(1)}) custom-call(s32[1]{0:T(128)} %dynamic-slice.9.limit_ref, bf16[1024,1536]{1,0:T(8,128)(2,1)S(1)} %get-tuple-element.63.q_ref.k_ref.v_ref, bf16[1024,1536]{1,0:T(8,128)(2,1)S(1)} %get-tuple-element.63.q_ref.k_ref.v_ref, ...), custom_call_target="tpu_custom_call" | custom-call | flops 17250000896 | bytes 1048576 | tf_op jit(solution)/shard_map/attend/pallas_call | solution.py:199
  88.2 1.3 collective-permute-done.16.refs_7_
  89.5 0.8 copy-done.18
  90.3 29.0 %middle.1 = (bf16[1,1024,512]{2,1,0:T(8,128)(2,1)}, bf16[1024,512]{1,0:T(8,128)(2,1)}, f32[1024,512]{1,0:T(8,128)}, f32[1,512]{1,0:T(1,128)S(1)}, bf16[2,512,640...) custom-call(s32[1]{0:T(128)} %dynamic-slice.9.limit_ref, ...), custom_call_target="tpu_custom_call" | custom-call | flops 28750000128 | bytes 1048576 | tf_op jit(solution)/shard_map/middle/pallas_call | solution.py:370
  119.9 2.4 %collective-permute-done.18 = bf16[2,512,512]{2,1,0:T(8,128)(2,1)S(1)} collective-permute-done((bf16[2,512,512]{2,1,0:T(8,128)(2,1)}, bf16[2,512,512]{2,1,0:T(8,128)(2,1)S(1)}, u32[]{:S(2)}, u32[]{:S(2)}) %collective-permute-start.18) | collective-permute-done | bytes 1048608 | tf_op jit(solution)/shard_map/ppermute | solution.py:586
  122.3 1.6 convert_add_fusion
  123.9 1.6 collective-permute-start.19
  125.5 1.4 fusion.1
  126.9 0.9 collective-permute-start.20
  127.8 1.2 copy-done.7
  129.1 14.2 %attend_back.2 = (bf16[1024,768]{1,0:T(8,128)(2,1)S(1)}, bf16[512,384]{1,0:T(8,128)(2,1)S(1)}, bf16[512,384]{1,0:T(8,128)(2,1)S(1)}) custom-call(s32[1]{0:T(128)} %dynamic-slice.9.limit_ref, bf16[1024,1536]{1,0:T(8,128)(2,1)S(1)} %copy-done.2, bf16[1024,1536]{1,0:T(8,128)(2,1)S(1)} %copy-done.2, bf16[1024,1536]{1,0:T(8,128)(2,1)S(1)} %copy-done.2, ...), custom_call_target="tpu_custom_call" | custom-call | flops 18400000000 | bytes 1048576 | tf_op jit(solution)/shard_map/attend_back/pallas_call | solution.py:465
  143.5 1.3 fusion
  144.9 1.1 collective-permute-start.22
  146.2 3.2 %collective-permute-start.24 = (bf16[2,64,512]{2,1,0:T(8,128)(2,1)S(1)}, bf16[2,64,512]{2,1,0:T(8,128)(2,1)S(1)}, u32[]{:S(2)}, u32[]{:S(2)}) collective-permute-start(bf16[2,64,512]{2,1,0:T(8,128)(2,1)S(1)} %get-tuple-element.182), channel_id=1, source_target_pairs={{0,8},{4,12},{8,16},{12,20},{16,24},{20,28},{24,0},{28,4},{1,9},{5... | collective-permute-start | bytes 393224 | tf_op jit(solution)/shard_map/ppermute | solution.py:591
  149.4 1.3 collective-permute-start.25
  150.7 1.2 collective-permute-start.26
  151.9 1.0 collective-permute-start.23
  153.0 14.2 %attend_back.3 = (bf16[1024,768]{1,0:T(8,128)(2,1)S(1)}, bf16[512,384]{1,0:T(8,128)(2,1)S(1)}, bf16[512,384]{1,0:T(8,128)(2,1)S(1)}) custom-call(s32[1]{0:T(128)} %dynamic-slice.9.limit_ref, bf16[1024,1536]{1,0:T(8,128)(2,1)S(1)} %copy-done.2, bf16[1024,1536]{1,0:T(8,128)(2,1)S(1)} %copy-done.2, bf16[1024,1536]{1,0:T(8,128)(2,1)S(1)} %copy-done.2, ...), custom_call_target="tpu_custom_call" | custom-call | flops 18400000000 | bytes 1048576 | tf_op jit(solution)/shard_map/attend_back/pallas_call | solution.py:465
  167.3 0.7 dynamic-slice_bitcast_fusion.4
  168.6 0.6 dynamic-slice_convert_fusion
  169.3 5.0 %begin_back.1 = bf16[8,4,136,128]{3,2,1,0:T(8,128)(2,1)} custom-call(s32[1]{0:T(128)} %dynamic-slice.9.limit_ref, bf16[8,4,136,128]{3,2,1,0:T(8,128)(2,1)S(1)} %bitcast.119, f32[1,512]{1,0:T(1,128)S(1)} %pad_maximum_fusion.3.clock_ref, f32[1,512]{1,0:T(1,128)S(1)} %reshape_squeeze.8.gain_ref, f32[1,512]{1,0:T(1,128)S(1)} %get-tuple-element.73.gg_two_ref, ...), custom_call_target="tpu_custom_call" | custom-call | flops 8049999872 | bytes 1048576 | tf_op jit(solution)/shard_map/begin_back/pallas_call | solution.py:553
  175.0 0.7 copy-done.9
  175.7 4.1 %all-to-all-start.1 = ((bf16[32,136,128]{2,1,0:T(8,128)(2,1)}), bf16[32,136,128]{2,1,0:T(8,128)(2,1)S(1)}, u32[]{:S(2)}, u32[]{:S(2)}) async-start(bf16[32,136,128]{2,1,0:T(8,128)(2,1)} %bitcast.25), calls=%async_computation.1 | async-start | bytes 2228224 | tf_op jit(solution)/shard_map/all_to_all | solution.py:798
  179.8 0.7 scatter_custom_fusion
  180.5 1.7 fusion.4
  182.2 1.8 collective-permute-start.29
  184.3 1.8 collective-permute-start.33
  186.1 2.1 collective-permute-start.34
  188.1 7.2 %collective-permute-done.29 = bf16[4,64,384]{2,1,0:T(8,128)(2,1)S(1)} collective-permute-done((bf16[4,64,384]{2,1,0:T(8,128)(2,1)}, bf16[4,64,384]{2,1,0:T(8,128)(2,1)S(1)}, u32[]{:S(2)}, u32[]{:S(2)}) %collective-permute-start.29) | collective-permute-done | bytes 196640 | tf_op jit(solution)/shard_map/ppermute | solution.py:591
  195.3 1.0 fusion.3
  196.4 1.3 collective-permute-done.35
  197.7 7.0 %collective-permute-done.33 = bf16[64,640]{1,0:T(8,128)(2,1)S(1)} collective-permute-done((bf16[64,640]{1,0:T(8,128)(2,1)}, bf16[64,640]{1,0:T(8,128)(2,1)S(1)}, u32[]{:S(2)}, u32[]{:S(2)}) %collective-permute-start.33) | collective-permute-done | bytes 81952 | tf_op jit(solution)/shard_map/ppermute | solution.py:591
  204.7 8.0 %collective-permute-start.30 = (bf16[64,384]{1,0:T(8,128)(2,1)S(1)}, bf16[64,384]{1,0:T(8,128)(2,1)S(1)}, u32[]{:S(2)}, u32[]{:S(2)}) collective-permute-start(bf16[64,384]{1,0:T(8,128)(2,1)S(1)} %get-tuple-element.188), channel_id=1, source_target_pairs={{0,8},{4,12},{8,16},{12,20},{16,24},{20,28},{24,0},{28,4},{1,9},{5... | collective-permute-start | bytes 147464 | tf_op jit(solution)/shard_map/ppermute | solution.py:591
  212.7 2.4 %collective-permute-start.32 = (bf16[64,384]{1,0:T(8,128)(2,1)S(1)}, bf16[64,384]{1,0:T(8,128)(2,1)S(1)}, u32[]{:S(2)}, u32[]{:S(2)}) collective-permute-start(bf16[64,384]{1,0:T(8,128)(2,1)S(1)} %get-tuple-element.189), channel_id=1, source_target_pairs={{0,24},{4,28},{8,0},{12,4},{16,8},{20,12},{24,16},{28,20},{1,25},{... | collective-permute-start | bytes 147464 | tf_op jit(solution)/shard_map/ppermute | solution.py:591
  215.1 0.7 add_bitcast_fusion
  216.4 0.7 slice.119
  217.1 0.8 collective-permute-done.31
  217.9 0.7 copy_bitcast_fusion
  218.6 0.8 gather_fusion.1
  219.4 1.1 slice.117
  (127 shorter events, 8.9 us)
Async XLA Ops:
  0.6 11.8 %copy-start = (bf16[32,128,128]{2,1,0:T(8,128)(2,1)S(1)}, bf16[32,128,128]{2,1,0:T(8,128)(2,1)}, u32[]{:S(2)}) copy-start(bf16[32,128,128]{2,1,0:T(8,128)(2,1)} %param.11) | copy-start | bytes 3145732
  1.6 24.3 %collective-permute-start.6 = (bf16[64,1152]{1,0:T(8,128)(2,1)S(1)}, bf16[64,1152]{1,0:T(8,128)(2,1)S(1)}, u32[]{:S(2)}, u32[]{:S(2)}) collective-permute-start(bf16[64,1152]{1,0:T(8,128)(2,1)S(1)} %pad_maximum_fusion.2), channel_id=1, source_target_pairs={{0,8},{4,12},{8,16},{12,20},{16,24},{20,28},{24,0},{28,4},{1,9},{5... | collective-permute-start | bytes 442376 | tf_op jit(solution)/shard_map/ppermute | solution.py:591
  4.7 22.6 %collective-permute-start.7 = (bf16[64,1152]{1,0:T(8,128)(2,1)S(1)}, bf16[64,1152]{1,0:T(8,128)(2,1)S(1)}, u32[]{:S(2)}, u32[]{:S(2)}) collective-permute-start(bf16[64,1152]{1,0:T(8,128)(2,1)S(1)} %pad_maximum_fusion.2), channel_id=1, source_target_pairs={{0,16},{4,20},{8,24},{12,28},{16,0},{20,4},{24,8},{28,12},{1,17},{... | collective-permute-start | bytes 442376 | tf_op jit(solution)/shard_map/ppermute | solution.py:591
  7.3 20.0 %collective-permute-start.8 = (bf16[64,1152]{1,0:T(8,128)(2,1)S(1)}, bf16[64,1152]{1,0:T(8,128)(2,1)S(1)}, u32[]{:S(2)}, u32[]{:S(2)}) collective-permute-start(bf16[64,1152]{1,0:T(8,128)(2,1)S(1)} %pad_maximum_fusion.2), channel_id=1, source_target_pairs={{0,24},{4,28},{8,0},{12,4},{16,8},{20,12},{24,16},{28,20},{1,25},{... | collective-permute-start | bytes 442376 | tf_op jit(solution)/shard_map/ppermute | solution.py:591
  9.4 12.2 %collective-permute-start = (bf16[64,384]{1,0:T(8,128)(2,1)S(1)}, bf16[64,384]{1,0:T(8,128)(2,1)S(1)}, u32[]{:S(2)}, u32[]{:S(2)}) collective-permute-start(bf16[64,384]{1,0:T(8,128)(2,1)S(1)} %copy_bitcast_fusion.1), channel_id=1, source_target_pairs={{0,4},{4,0},{8,12},{12,8},{16,20},{20,16},{24,28},{28,24},{1,5},{5... | collective-permute-start | bytes 147464 | tf_op jit(solution)/shard_map/ppermute | solution.py:591
  14.4 2.9 %copy-start.12 = (bf16[64,3,128]{2,0,1:T(8,128)(2,1)S(1)}, bf16[64,3,128]{2,0,1:T(8,128)(2,1)}, u32[]{:S(2)}) copy-start(bf16[64,3,128]{2,0,1:T(8,128)(2,1)} %param.15) | copy-start | bytes 147460
  14.4 2.9 %copy-start.19 = (s32[32]{0:T(128)S(1)}, s32[32]{0:T(128)}, u32[]{:S(2)}) copy-start(s32[32]{0:T(128)} %param.14) | copy-start | bytes 388
  14.4 5.4 %copy-start.20 = (s32[32]{0:T(128)S(1)}, s32[32]{0:T(128)}, u32[]{:S(2)}) copy-start(s32[32]{0:T(128)} %param.12) | copy-start | bytes 388
  14.4 6.7 %copy-start.21 = (s32[32]{0:T(128)S(1)}, s32[32]{0:T(128)}, u32[]{:S(2)}) copy-start(s32[32]{0:T(128)} %param.13) | copy-start | bytes 388
  14.4 12.9 %copy-start.10 = (bf16[512,64]{0,1:T(8,128)(2,1)S(1)}, bf16[512,64]{0,1:T(8,128)(2,1)}, u32[]{:S(2)}) copy-start(bf16[512,64]{0,1:T(8,128)(2,1)} %param.18) | copy-start | bytes 196612
  14.4 12.9 %copy-start.11 = (bf16[64,512]{1,0:T(8,128)(2,1)S(1)}, bf16[64,512]{1,0:T(8,128)(2,1)}, u32[]{:S(2)}) copy-start(bf16[64,512]{1,0:T(8,128)(2,1)} %param.17) | copy-start | bytes 196612
  14.4 12.9 %copy-start.15 = (bf16[128,64]{0,1:T(8,128)(2,1)S(1)}, bf16[128,64]{0,1:T(8,128)(2,1)}, u32[]{:S(2)}) copy-start(bf16[128,64]{0,1:T(8,128)(2,1)} %param.16) | copy-start | bytes 49156
  14.4 49.4 %all-to-all-start = ((bf16[32,136,128]{2,1,0:T(8,128)(2,1)}), bf16[32,136,128]{2,1,0:T(8,128)(2,1)S(1)}, u32[]{:S(2)}, u32[]{:S(2)}) async-start(bf16[32,136,128]{2,1,0:T(8,128)(2,1)} %pad_maximum_fusion), calls=%async_computation | async-start | bytes 2228224 | tf_op jit(solution)/shard_map/all_to_all | solution.py:732
  21.7 20.7 %collective-permute-start.1 = (bf16[64,768]{1,0:T(8,128)(2,1)S(1)}, bf16[64,768]{1,0:T(8,128)(2,1)S(1)}, u32[]{:S(2)}, u32[]{:S(2)}) collective-permute-start(bf16[64,768]{1,0:T(8,128)(2,1)S(1)} %constant_dynamic-update-slice_fusion), channel_id=1, source_target_pairs={{0,8},{4,12},{8,16},{12,20},{16,24},{20,28},{24,0},{28,4},{1,9},{5... | collective-permute-start | bytes 294920 | tf_op jit(solution)/shard_map/ppermute | solution.py:591
  23.4 28.2 %collective-permute-start.2 = (bf16[64,768]{1,0:T(8,128)(2,1)S(1)}, bf16[64,768]{1,0:T(8,128)(2,1)S(1)}, u32[]{:S(2)}, u32[]{:S(2)}) collective-permute-start(bf16[64,768]{1,0:T(8,128)(2,1)S(1)} %constant_dynamic-update-slice_fusion), channel_id=1, source_target_pairs={{0,16},{4,20},{8,24},{12,28},{16,0},{20,4},{24,8},{28,12},{1,17},{... | collective-permute-start | bytes 294920 | tf_op jit(solution)/shard_map/ppermute | solution.py:591
  25.9 25.7 %collective-permute-start.3 = (bf16[64,768]{1,0:T(8,128)(2,1)S(1)}, bf16[64,768]{1,0:T(8,128)(2,1)S(1)}, u32[]{:S(2)}, u32[]{:S(2)}) collective-permute-start(bf16[64,768]{1,0:T(8,128)(2,1)S(1)} %constant_dynamic-update-slice_fusion), channel_id=1, source_target_pairs={{0,24},{4,28},{8,0},{12,4},{16,8},{20,12},{24,16},{28,20},{1,25},{... | collective-permute-start | bytes 294920 | tf_op jit(solution)/shard_map/ppermute | solution.py:591
  28.3 33.7 %collective-permute-start.10 = (bf16[256,1152]{1,0:T(8,128)(2,1)}, bf16[256,1152]{1,0:T(8,128)(2,1)S(1)}, u32[]{:S(2)}, u32[]{:S(2)}) collective-permute-start(bf16[256,1152]{1,0:T(8,128)(2,1)} %pad_maximum_fusion.1.refs_0_), channel_id=1, source_target_pairs={{0,2},{1,3},{2,0},{3,1},{4,6},{5,7},{6,4},{7,5},{8,10},{9,11},{10,... | collective-permute-start | bytes 1769480 | tf_op jit(solution)/shard_map/ppermute | solution.py:586
  29.7 32.3 %collective-permute-start.9 = (bf16[256,1152]{1,0:T(8,128)(2,1)}, bf16[256,1152]{1,0:T(8,128)(2,1)}, u32[]{:S(2)}, u32[]{:S(2)}) collective-permute-start(bf16[256,1152]{1,0:T(8,128)(2,1)} %pad_maximum_fusion.1.refs_0_), channel_id=1, source_target_pairs={{0,4},{4,0},{8,12},{12,8},{16,20},{20,16},{24,28},{28,24},{1,5},{5... | collective-permute-start | bytes 1769480 | tf_op jit(solution)/shard_map/ppermute | solution.py:591
  51.7 10.3 %collective-permute-start.5 = (bf16[512,384]{1,0:T(8,128)(2,1)S(1)}, bf16[512,384]{1,0:T(8,128)(2,1)S(1)}, u32[]{:S(2)}, u32[]{:S(2)}) collective-permute-start(bf16[512,384]{1,0:T(8,128)(2,1)S(1)} %slice_dynamic-update-slice_fusion.refs_0_), channel_id=1, source_target_pairs={{0,2},{1,3},{2,0},{3,1},{4,6},{5,7},{6,4},{7,5},{8,10},{9,11},{10,... | collective-permute-start | bytes 1179656 | tf_op jit(solution)/shard_map/ppermute | solution.py:586
  53.5 10.6 %collective-permute-start.4 = (bf16[512,384]{1,0:T(8,128)(2,1)S(1)}, bf16[512,384]{1,0:T(8,128)(2,1)S(1)}, u32[]{:S(2)}, u32[]{:S(2)}) collective-permute-start(bf16[512,384]{1,0:T(8,128)(2,1)S(1)} %slice_dynamic-update-slice_fusion.refs_0_), channel_id=1, source_target_pairs={{0,1},{1,0},{2,3},{3,2},{4,5},{5,4},{6,7},{7,6},{8,9},{9,8},{10,11... | collective-permute-start | bytes 1179656 | tf_op jit(solution)/shard_map/ppermute | solution.py:586
  53.6 33.6 %collective-permute-start.12 = (bf16[256,1152]{1,0:T(8,128)(2,1)}, bf16[256,1152]{1,0:T(8,128)(2,1)}, u32[]{:S(2)}, u32[]{:S(2)}) collective-permute-start(bf16[256,1152]{1,0:T(8,128)(2,1)} %pad_maximum_fusion.1.refs_0_), channel_id=1, source_target_pairs={{0,1},{1,0},{2,3},{3,2},{4,5},{5,4},{6,7},{7,6},{8,9},{9,8},{10,11... | collective-permute-start | bytes 1769480 | tf_op jit(solution)/shard_map/ppermute | solution.py:586
  62.0 1.7 copy-start.16
  62.0 25.2 %collective-permute-start.13 = (bf16[256,1152]{1,0:T(8,128)(2,1)}, bf16[256,1152]{1,0:T(8,128)(2,1)}, u32[]{:S(2)}, u32[]{:S(2)}) collective-permute-start(bf16[256,1152]{1,0:T(8,128)(2,1)} %collective-permute-done.9.refs_1_), channel_id=1, source_target_pairs={{0,1},{1,0},{2,3},{3,2},{4,5},{5,4},{6,7},{7,6},{8,9},{9,8},{10,11... | collective-permute-start | bytes 1769480 | tf_op jit(solution)/shard_map/ppermute | solution.py:586
  62.1 25.1 %collective-permute-start.15 = (bf16[256,1152]{1,0:T(8,128)(2,1)}, bf16[256,1152]{1,0:T(8,128)(2,1)}, u32[]{:S(2)}, u32[]{:S(2)}) collective-permute-start(bf16[256,1152]{1,0:T(8,128)(2,1)} %collective-permute-done.9.refs_1_), channel_id=1, source_target_pairs={{0,2},{1,3},{2,0},{3,1},{4,6},{5,7},{6,4},{7,5},{8,10},{9,11},{10,... | collective-permute-start | bytes 1769480 | tf_op jit(solution)/shard_map/ppermute | solution.py:586
  63.7 1.9 collective-permute-start.11
  64.2 23.1 %collective-permute-start.14 = (bf16[256,1152]{1,0:T(8,128)(2,1)}, bf16[256,1152]{1,0:T(8,128)(2,1)S(1)}, u32[]{:S(2)}, u32[]{:S(2)}) collective-permute-start(bf16[256,1152]{1,0:T(8,128)(2,1)} %copy-done.16), channel_id=1, source_target_pairs={{0,1},{1,0},{2,3},{3,2},{4,5},{5,4},{6,7},{7,6},{8,9},{9,8},{10,11... | collective-permute-start | bytes 1769480 | tf_op jit(solution)/shard_map/ppermute | solution.py:586
  71.8 15.4 %copy-start.1 = (bf16[1024,1536]{1,0:T(8,128)(2,1)}, bf16[1024,1536]{1,0:T(8,128)(2,1)S(1)}, u32[]{:S(2)}) copy-start(bf16[1024,1536]{1,0:T(8,128)(2,1)S(1)} %get-tuple-element.63.q_ref.k_ref.v_ref) | copy-start | bytes 9437188
  87.2 0.8 copy-start.17
  87.2 2.3 %collective-permute-start.16 = (bf16[256,1152]{1,0:T(8,128)(2,1)}, bf16[256,1152]{1,0:T(8,128)(2,1)S(1)}, u32[]{:S(2)}, u32[]{:S(2)}) collective-permute-start(bf16[256,1152]{1,0:T(8,128)(2,1)} %collective-permute-done.15.refs_5_), channel_id=1, source_target_pairs={{0,1},{1,0},{2,3},{3,2},{4,5},{5,4},{6,7},{7,6},{8,9},{9,8},{10,11... | collective-permute-start | bytes 1769480 | tf_op jit(solution)/shard_map/ppermute | solution.py:586
  89.5 0.8 copy-start.18
  119.4 2.9 %collective-permute-start.18 = (bf16[2,512,512]{2,1,0:T(8,128)(2,1)}, bf16[2,512,512]{2,1,0:T(8,128)(2,1)S(1)}, u32[]{:S(2)}, u32[]{:S(2)}) collective-permute-start(bf16[2,512,512]{2,1,0:T(8,128)(2,1)} %get-tuple-element.81), channel_id=1, source_target_pairs={{0,1},{1,0},{2,3},{3,2},{4,5},{5,4},{6,7},{7,6},{8,9},{9,8},{10,11... | collective-permute-start | bytes 3145736 | tf_op jit(solution)/shard_map/ppermute | solution.py:586
  119.6 5.9 %collective-permute-start.17 = (bf16[2,512,640]{2,1,0:T(8,128)(2,1)}, bf16[2,512,640]{2,1,0:T(8,128)(2,1)}, u32[]{:S(2)}, u32[]{:S(2)}) collective-permute-start(bf16[2,512,640]{2,1,0:T(8,128)(2,1)} %get-tuple-element.76), channel_id=1, source_target_pairs={{0,1},{1,0},{2,3},{3,2},{4,5},{5,4},{6,7},{7,6},{8,9},{9,8},{10,11... | collective-permute-start | bytes 3932168 | tf_op jit(solution)/shard_map/ppermute | solution.py:586
  122.3 5.5 %copy-start.2 = (bf16[1024,1536]{1,0:T(8,128)(2,1)S(1)}, bf16[1024,1536]{1,0:T(8,128)(2,1)}, u32[]{:S(2)}) copy-start(bf16[1024,1536]{1,0:T(8,128)(2,1)} %copy-done.1) | copy-start | bytes 9437188
  122.3 5.5 %copy-start.6 = (bf16[512,1024]{1,0:T(8,128)(2,1)S(1)}, bf16[512,1024]{1,0:T(8,128)(2,1)}, u32[]{:S(2)}) copy-start(bf16[512,1024]{1,0:T(8,128)(2,1)} %get-tuple-element.77.turn_ref) | copy-start | bytes 3145732
  123.9 3.9 %copy-start.5 = (bf16[512,1024]{1,0:T(8,128)(2,1)S(1)}, bf16[512,1024]{1,0:T(8,128)(2,1)}, u32[]{:S(2)}) copy-start(bf16[512,1024]{1,0:T(8,128)(2,1)} %get-tuple-element.83.n_turn_ref) | copy-start | bytes 3145732
  123.9 19.3 %collective-permute-start.19 = (bf16[4,2,64,512]{3,2,1,0:T(8,128)(2,1)S(1)}, bf16[4,2,64,512]{3,2,1,0:T(8,128)(2,1)S(1)}, u32[]{:S(2)}, u32[]{:S(2)}) collective-permute-start(bf16[4,2,64,512]{3,2,1,0:T(8,128)(2,1)S(1)} %bitcast.125), channel_id=1, source_target_pairs={{0,2},{1,3},{2,0},{3,1},{4,6},{5,7},{6,4},{7,5},{8,10},{9,11},{10,... | collective-permute-start | bytes 1572872 | tf_op jit(solution)/shard_map/ppermute | solution.py:586
  126.9 16.6 %collective-permute-start.20 = (bf16[2,4,64,640]{3,2,1,0:T(8,128)(2,1)S(1)}, bf16[2,4,64,640]{3,2,1,0:T(8,128)(2,1)S(1)}, u32[]{:S(2)}, u32[]{:S(2)}) collective-permute-start(bf16[2,4,64,640]{3,2,1,0:T(8,128)(2,1)S(1)} %fusion.1), channel_id=1, source_target_pairs={{0,4},{4,0},{8,12},{12,8},{16,20},{20,16},{24,28},{28,24},{1,5},{5... | collective-permute-start | bytes 1966088 | tf_op jit(solution)/shard_map/ppermute | solution.py:591
  127.8 1.2 copy-start.7
  129.1 14.4 %copy-start.8 = (bf16[2,512,640]{2,1,0:T(8,128)(2,1)S(1)}, bf16[2,512,640]{2,1,0:T(8,128)(2,1)}, u32[]{:S(2)}) copy-start(bf16[2,512,640]{2,1,0:T(8,128)(2,1)} %get-tuple-element.75) | copy-start | bytes 3932164
  143.5 8.3 %collective-permute-start.21 = (bf16[512,384]{1,0:T(8,128)(2,1)S(1)}, bf16[512,384]{1,0:T(8,128)(2,1)S(1)}, u32[]{:S(2)}, u32[]{:S(2)}) collective-permute-start(bf16[512,384]{1,0:T(8,128)(2,1)S(1)} %get-tuple-element.92), channel_id=1, source_target_pairs={{0,1},{1,0},{2,3},{3,2},{4,5},{5,4},{6,7},{7,6},{8,9},{9,8},{10,11... | collective-permute-start | bytes 1179656 | tf_op jit(solution)/shard_map/ppermute | solution.py:586
  144.9 22.4 %collective-permute-start.22 = (bf16[4,64,640]{2,1,0:T(8,128)(2,1)S(1)}, bf16[4,64,640]{2,1,0:T(8,128)(2,1)S(1)}, u32[]{:S(2)}, u32[]{:S(2)}) collective-permute-start(bf16[4,64,640]{2,1,0:T(8,128)(2,1)S(1)} %slice_bitcast_fusion), channel_id=1, source_target_pairs={{0,2},{1,3},{2,0},{3,1},{4,6},{5,7},{6,4},{7,5},{8,10},{9,11},{10,... | collective-permute-start | bytes 983048 | tf_op jit(solution)/shard_map/ppermute | solution.py:586
  146.2 21.0 %collective-permute-start.24 = (bf16[2,64,512]{2,1,0:T(8,128)(2,1)S(1)}, bf16[2,64,512]{2,1,0:T(8,128)(2,1)S(1)}, u32[]{:S(2)}, u32[]{:S(2)}) collective-permute-start(bf16[2,64,512]{2,1,0:T(8,128)(2,1)S(1)} %get-tuple-element.182), channel_id=1, source_target_pairs={{0,8},{4,12},{8,16},{12,20},{16,24},{20,28},{24,0},{28,4},{1,9},{5... | collective-permute-start | bytes 393224 | tf_op jit(solution)/shard_map/ppermute | solution.py:591
  149.4 17.8 %collective-permute-start.25 = (bf16[2,64,512]{2,1,0:T(8,128)(2,1)S(1)}, bf16[2,64,512]{2,1,0:T(8,128)(2,1)S(1)}, u32[]{:S(2)}, u32[]{:S(2)}) collective-permute-start(bf16[2,64,512]{2,1,0:T(8,128)(2,1)S(1)} %get-tuple-element.181), channel_id=1, source_target_pairs={{0,16},{4,20},{8,24},{12,28},{16,0},{20,4},{24,8},{28,12},{1,17},{... | collective-permute-start | bytes 393224 | tf_op jit(solution)/shard_map/ppermute | solution.py:591
  150.7 16.6 %collective-permute-start.26 = (bf16[2,64,512]{2,1,0:T(8,128)(2,1)S(1)}, bf16[2,64,512]{2,1,0:T(8,128)(2,1)S(1)}, u32[]{:S(2)}, u32[]{:S(2)}) collective-permute-start(bf16[2,64,512]{2,1,0:T(8,128)(2,1)S(1)} %get-tuple-element.180), channel_id=1, source_target_pairs={{0,24},{4,28},{8,0},{12,4},{16,8},{20,12},{24,16},{28,20},{1,25},{... | collective-permute-start | bytes 393224 | tf_op jit(solution)/shard_map/ppermute | solution.py:591
  151.9 15.3 %collective-permute-start.23 = (bf16[512,384]{1,0:T(8,128)(2,1)S(1)}, bf16[512,384]{1,0:T(8,128)(2,1)S(1)}, u32[]{:S(2)}, u32[]{:S(2)}) collective-permute-start(bf16[512,384]{1,0:T(8,128)(2,1)S(1)} %add_convert_fusion.3), channel_id=1, source_target_pairs={{0,2},{1,3},{2,0},{3,1},{4,6},{5,7},{6,4},{7,5},{8,10},{9,11},{10,... | collective-permute-start | bytes 1179656 | tf_op jit(solution)/shard_map/ppermute | solution.py:586
  153.0 16.3 %copy-start.4 = (bf16[512,1536]{1,0:T(8,128)(2,1)S(1)}, bf16[512,1536]{1,0:T(8,128)(2,1)}, u32[]{:S(2)}) copy-start(bf16[512,1536]{1,0:T(8,128)(2,1)} %get-tuple-element.103.w_ref) | copy-start | bytes 4718596
  167.3 2.0 copy-start.3
  168.1 6.3 %collective-permute-start.28 = (bf16[64,640]{1,0:T(8,128)(2,1)S(1)}, bf16[64,640]{1,0:T(8,128)(2,1)S(1)}, u32[]{:S(2)}, u32[]{:S(2)}) collective-permute-start(bf16[64,640]{1,0:T(8,128)(2,1)S(1)} %get-tuple-element.187), channel_id=1, source_target_pairs={{0,16},{4,20},{8,24},{12,28},{16,0},{20,4},{24,8},{28,12},{1,17},{... | collective-permute-start | bytes 245768 | tf_op jit(solution)/shard_map/ppermute | solution.py:591
  169.2 5.1 %collective-permute-start.27 = (bf16[512,384]{1,0:T(8,128)(2,1)S(1)}, bf16[512,384]{1,0:T(8,128)(2,1)S(1)}, u32[]{:S(2)}, u32[]{:S(2)}) collective-permute-start(bf16[512,384]{1,0:T(8,128)(2,1)S(1)} %get-tuple-element.105), channel_id=1, source_target_pairs={{0,1},{1,0},{2,3},{3,2},{4,5},{5,4},{6,7},{7,6},{8,9},{9,8},{10,11... | collective-permute-start | bytes 1179656 | tf_op jit(solution)/shard_map/ppermute | solution.py:586
  174.3 0.6 copy-start.13
  175.0 0.7 copy-start.9
  175.7 42.9 %all-to-all-start.1 = ((bf16[32,136,128]{2,1,0:T(8,128)(2,1)}), bf16[32,136,128]{2,1,0:T(8,128)(2,1)S(1)}, u32[]{:S(2)}, u32[]{:S(2)}) async-start(bf16[32,136,128]{2,1,0:T(8,128)(2,1)} %bitcast.25), calls=%async_computation.1 | async-start | bytes 2228224 | tf_op jit(solution)/shard_map/all_to_all | solution.py:798
  182.2 13.1 %collective-permute-start.29 = (bf16[4,64,384]{2,1,0:T(8,128)(2,1)}, bf16[4,64,384]{2,1,0:T(8,128)(2,1)S(1)}, u32[]{:S(2)}, u32[]{:S(2)}) collective-permute-start(bf16[4,64,384]{2,1,0:T(8,128)(2,1)} %fusion.4), channel_id=1, source_target_pairs={{0,4},{4,0},{8,12},{12,8},{16,20},{20,16},{24,28},{28,24},{1,5},{5... | collective-permute-start | bytes 589832 | tf_op jit(solution)/shard_map/ppermute | solution.py:591
  184.0 31.8 %copy-start.14 = (bf16[64,640]{1,0:T(8,128)(2,1)S(1)}, bf16[64,640]{1,0:T(8,128)(2,1)}, u32[]{:S(2)}) copy-start(bf16[64,640]{1,0:T(8,128)(2,1)} %copy-done.13) | copy-start | bytes 245764
  184.0 13.7 %collective-permute-start.35 = (bf16[1,64,512]{2,1,0:T(8,128)(2,1)}, bf16[1,64,512]{2,1,0:T(8,128)(2,1)S(1)}, u32[]{:S(2)}, u32[]{:S(2)}) collective-permute-start(bf16[1,64,512]{2,1,0:T(8,128)(2,1)} %dynamic-slice_convert_fusion), channel_id=1, source_target_pairs={{0,4},{4,0},{8,12},{12,8},{16,20},{20,16},{24,28},{28,24},{1,5},{5... | collective-permute-start | bytes 196616 | tf_op jit(solution)/shard_map/ppermute | solution.py:591
  184.3 20.4 %collective-permute-start.33 = (bf16[64,640]{1,0:T(8,128)(2,1)}, bf16[64,640]{1,0:T(8,128)(2,1)S(1)}, u32[]{:S(2)}, u32[]{:S(2)}) collective-permute-start(bf16[64,640]{1,0:T(8,128)(2,1)} %get-tuple-element.185), channel_id=1, source_target_pairs={{0,8},{4,12},{8,16},{12,20},{16,24},{20,28},{24,0},{28,4},{1,9},{5... | collective-permute-start | bytes 245768 | tf_op jit(solution)/shard_map/ppermute | solution.py:591
  186.1 18.6 %collective-permute-start.34 = (bf16[64,640]{1,0:T(8,128)(2,1)}, bf16[64,640]{1,0:T(8,128)(2,1)S(1)}, u32[]{:S(2)}, u32[]{:S(2)}) collective-permute-start(bf16[64,640]{1,0:T(8,128)(2,1)} %get-tuple-element.184), channel_id=1, source_target_pairs={{0,24},{4,28},{8,0},{12,4},{16,8},{20,12},{24,16},{28,20},{1,25},{... | collective-permute-start | bytes 245768 | tf_op jit(solution)/shard_map/ppermute | solution.py:591
  204.7 12.4 %collective-permute-start.30 = (bf16[64,384]{1,0:T(8,128)(2,1)S(1)}, bf16[64,384]{1,0:T(8,128)(2,1)S(1)}, u32[]{:S(2)}, u32[]{:S(2)}) collective-permute-start(bf16[64,384]{1,0:T(8,128)(2,1)S(1)} %get-tuple-element.188), channel_id=1, source_target_pairs={{0,8},{4,12},{8,16},{12,20},{16,24},{20,28},{24,0},{28,4},{1,9},{5... | collective-permute-start | bytes 147464 | tf_op jit(solution)/shard_map/ppermute | solution.py:591
  212.7 5.3 %collective-permute-start.31 = (bf16[64,384]{1,0:T(8,128)(2,1)S(1)}, bf16[64,384]{1,0:T(8,128)(2,1)S(1)}, u32[]{:S(2)}, u32[]{:S(2)}) collective-permute-start(bf16[64,384]{1,0:T(8,128)(2,1)S(1)} %get-tuple-element.190), channel_id=1, source_target_pairs={{0,16},{4,20},{8,24},{12,28},{16,0},{20,4},{24,8},{28,12},{1,17},{... | collective-permute-start | bytes 147464 | tf_op jit(solution)/shard_map/ppermute | solution.py:591
  212.7 5.3 %collective-permute-start.32 = (bf16[64,384]{1,0:T(8,128)(2,1)S(1)}, bf16[64,384]{1,0:T(8,128)(2,1)S(1)}, u32[]{:S(2)}, u32[]{:S(2)}) collective-permute-start(bf16[64,384]{1,0:T(8,128)(2,1)S(1)} %get-tuple-element.189), channel_id=1, source_target_pairs={{0,24},{4,28},{8,0},{12,4},{16,8},{20,12},{24,16},{28,20},{1,25},{... | collective-permute-start | bytes 147464 | tf_op jit(solution)/shard_map/ppermute | solution.py:591

commit v10 on v9

--- a/solution.py
+++ b/solution.py
@@ -710,13 +710,13 @@
     if direct:
         place, groups = places(), dp_count
         wide = qkv.shape[1]
-        pieces = collect_coarse(jnp.concatenate([qkv, across(qkv)], axis=1))
-        qkv_rows = jnp.concatenate(
-            [piece[:, :wide] for piece in pieces] + [piece[:, wide:] for piece in pieces], axis=0
-        )
-        mine = jnp.concatenate(collect_coarse(rest), axis=0)
+        pieces = collect_coarse(jnp.concatenate([qkv, rest], axis=1))
+        first = jnp.concatenate(pieces, axis=0)
+        qkv_rows, mine = first[:, :wide], first[:, wide:]
+        qkv_other = across(qkv_rows)
+        qkv_rows = jnp.concatenate([qkv_rows, qkv_other], axis=0)
         far_rows, other, far_mine = together(
-            swap(qkv_rows, 2), in_hbm(across(mine)), in_hbm(swap(mine, 2))
+            swap(qkv_rows, 2), in_hbm(across(after(mine, qkv_other))), in_hbm(swap(mine, 2))
         )
         qkv_parts = (qkv_rows, swap(qkv_rows, 1), far_rows, swap(far_rows, 1))
     else:
@@ -729,6 +729,8 @@
     arranged = jnp.concatenate(
         [states[deal_order], jnp.broadcast_to(spare[None], (devices, SPARE, width))], axis=1
     )
+    if direct:
+        arranged = after(arranged, *pieces[1:])
     x_blocks = lax.all_to_all(arranged, both, 0, 0, tiled=True)
     gains = jnp.sum(x_blocks[:, tokens, : 6 * per].reshape(devices, 2, 3, per).astype(F32), axis=2)
     gain_one = gains[:, 0].reshape(1, features)

time: 222 us -> 224 us (level)
  waiting for transfers between devices: 49.6 us -> 54.8 us
  starting transfers between devices: 56.3 us -> 53.1 us
    ppermute x20 -> x17, starting transfers between devices: 39 us -> 32.4 us  [along_dp(): return lax.ppermute(value, 'dp', [(i, move(i)) for i in range(count)])]
    ppermute x16, waiting for transfers between devices: 12.6 us -> 17.8 us  [swap(): return lax.ppermute(value, 'tensor', [(i, i ^ apart) for i in range(count)])]
    all_to_all x1, starting transfers between devices: 2.8 us -> 7.97 us  [on_device(): x_blocks = lax.all_to_all(arranged, both, 0, 0, tiled=True)]
    ppermute x20 -> x17, waiting for transfers between devices: 37.1 us -> 37 us  [along_dp(): return lax.ppermute(value, 'dp', [(i, move(i)) for i in range(count)])]
  transfers between devices with their start and end apart: 38 -> 35, of which waited for: 12 -> 13; matrix products, arithmetic and copies ran while one was open for 9% -> 8% of each run, Pallas kernels for 25% -> 25%
where the time goes in v10:
time: 224 us; the launch traced here: 223 us
  Pallas kernels  84.3 us (38%)
  waiting for transfers between devices  54.8 us (24%)
  starting transfers between devices  53.1 us (24%)
  local copies, waits for them, and re-layouts  14 us (6%)
  other arithmetic  13.6 us (6%)
  between operations  3.7 us (2%)
    ppermute x17, waiting for transfers between devices, along_dp(): return lax.ppermute(value, 'dp', [(i, move(i)) for i in range(count)])  37 us
    ppermute x17, starting transfers between devices, along_dp(): return lax.ppermute(value, 'dp', [(i, move(i)) for i in range(count)])  32.4 us
    pallas_call x1, Pallas kernels, middle_block(): pl.pallas_call(functools.partial(middle_kernel, groups), grid_spec=pltpu....  29.2 us
    pallas_call x2, Pallas kernels, attend_back(): pl.pallas_call(attend_back_kernel, grid_spec=pltpu.PrefetchScalarGridSpec...  28.4 us
    ppermute x16, waiting for transfers between devices, swap(): return lax.ppermute(value, 'tensor', [(i, i ^ apart) for i in range(count)])  17.8 us
    pallas_call x1, Pallas kernels, attend(): pl.pallas_call(attend_kernel, grid_spec=pltpu.PrefetchScalarGridSpec(num_...  15.3 us
    ppermute x16, starting transfers between devices, swap(): return lax.ppermute(value, 'tensor', [(i, i ^ apart) for i in range(count)])  9.27 us
    all_to_all x1, starting transfers between devices, on_device(): x_blocks = lax.all_to_all(arranged, both, 0, 0, tiled=True)  7.97 us
  transfers between devices with their start and end apart: 35, of which 13 were waited for; matrix products, arithmetic and copies ran while one was open for 8% of the time, Pallas kernels for 25%

profile of v10, /device:TPU:0, one launch (start us, length us, event | category | flops | bytes accessed | tf_op | source)
XLA Modules:
  0.0 223.5 jit_solution(11104285759674283582)
XLA Ops:
  0.6 0.9 copy_bitcast_fusion.1
  1.5 0.9 pad_maximum_fusion.9
  2.4 3.1 %collective-permute-start = (bf16[64,1536]{1,0:T(8,128)(2,1)S(1)}, bf16[64,1536]{1,0:T(8,128)(2,1)S(1)}, u32[]{:S(2)}, u32[]{:S(2)}) collective-permute-start(bf16[64,1536]{1,0:T(8,128)(2,1)S(1)} %pad_maximum_fusion.9), channel_id=1, source_target_pairs={{0,8},{4,12},{8,16},{12,20},{16,24},{20,28},{24,0},{28,4},{1,9},{5... | collective-permute-start | bytes 589832 | tf_op jit(solution)/shard_map/ppermute | solution.py:591
  5.5 2.6 %collective-permute-start.1 = (bf16[64,1536]{1,0:T(8,128)(2,1)S(1)}, bf16[64,1536]{1,0:T(8,128)(2,1)S(1)}, u32[]{:S(2)}, u32[]{:S(2)}) collective-permute-start(bf16[64,1536]{1,0:T(8,128)(2,1)S(1)} %pad_maximum_fusion.9), channel_id=1, source_target_pairs={{0,16},{4,20},{8,24},{12,28},{16,0},{20,4},{24,8},{28,12},{1,17},{... | collective-permute-start | bytes 589832 | tf_op jit(solution)/shard_map/ppermute | solution.py:591
  8.1 1.3 collective-permute-start.2
  9.4 0.7 compare_select_fusion.1
  10.1 0.7 fusion.12
  10.9 0.7 gather_fusion
  11.7 1.1 pad_maximum_fusion
  13.4 7.6 %collective-permute-done.1 = bf16[64,1536]{1,0:T(8,128)(2,1)S(1)} collective-permute-done((bf16[64,1536]{1,0:T(8,128)(2,1)S(1)}, bf16[64,1536]{1,0:T(8,128)(2,1)S(1)}, u32[]{:S(2)}, u32[]{:S(2)}) %collective-permute-start.1) | collective-permute-done | bytes 196640 | tf_op jit(solution)/shard_map/ppermute | solution.py:591
  21.0 8.0 %all-to-all-start = ((bf16[32,136,128]{2,1,0:T(8,128)(2,1)}), bf16[32,136,128]{2,1,0:T(8,128)(2,1)S(1)}, u32[]{:S(2)}, u32[]{:S(2)}) async-start(bf16[32,136,128]{2,1,0:T(8,128)(2,1)} %pad_maximum_fusion), calls=%async_computation | async-start | bytes 2228224 | tf_op jit(solution)/shard_map/all_to_all | solution.py:734
  29.1 1.8 collective-permute-start.3
  30.9 0.9 pad_maximum_fusion.1.refs_0_
  31.8 1.5 collective-permute-start.7
  33.3 11.2 %collective-permute-done.3 = bf16[256,384]{1,0:T(8,128)(2,1)S(1)} collective-permute-done((bf16[256,384]{1,0:T(8,128)(2,1)S(1)}, bf16[256,384]{1,0:T(8,128)(2,1)S(1)}, u32[]{:S(2)}, u32[]{:S(2)}) %collective-permute-start.3) | collective-permute-done | bytes 196640 | tf_op jit(solution)/shard_map/ppermute | solution.py:591
  47.5 0.6 dynamic-slice.10
  48.8 0.6 dynamic-slice.9.limit_ref
  49.4 1.9 collective-permute-start.5
  52.1 12.7 %collective-permute-done.5.refs_2_ = bf16[512,384]{1,0:T(8,128)(2,1)S(1)} collective-permute-done((bf16[512,384]{1,0:T(8,128)(2,1)S(1)}, bf16[512,384]{1,0:T(8,128)(2,1)S(1)}, u32[]{:S(2)}, u32[]{:S(2)}) %collective-permute-start.5) | collective-permute-done | bytes 393248 | tf_op jit(solution)/shard_map/ppermute | solution.py:586
  66.3 1.3 collective-permute-done.8.refs_3_
  67.5 6.3 %project.1 = (bf16[1024,1536]{1,0:T(8,128)(2,1)S(1)}, bf16[512,1024]{1,0:T(8,128)(2,1)}, bf16[512,1536]{1,0:T(8,128)(2,1)}) custom-call(s32[1]{0:T(128)} %dynamic-slice.9.limit_ref, s32[8]{0:T(128)S(1)} %pad_add_fusion.place_ref, bf16[8,4,136,128]{3,2,1,0:T(8,128)(2,1)S(1)} %bitcast.111, f32[1,512]{1,0:T(1,128)S(1)} %pad_maximum_fusion.10.clock_ref, ...), custom_call_target="tpu_custom_call" | custom-call | flops 5750000128 | bytes 1048576 | tf_op jit(solution)/shard_map/project/pallas_call | solution.py:110
  73.8 15.3 %attend.1 = (bf16[1024,512]{1,0:T(8,128)(2,1)}, bf16[512,1024]{1,0:T(8,128)(2,1)}, f32[4,2,1024]{2,1,0:T(2,128)S(1)}) custom-call(s32[1]{0:T(128)} %dynamic-slice.9.limit_ref, bf16[1024,1536]{1,0:T(8,128)(2,1)S(1)} %get-tuple-element.67.q_ref.k_ref.v_ref, bf16[1024,1536]{1,0:T(8,128)(2,1)S(1)} %get-tuple-element.67.q_ref.k_ref.v_ref, ...), custom_call_target="tpu_custom_call" | custom-call | flops 17250000896 | bytes 1048576 | tf_op jit(solution)/shard_map/attend/pallas_call | solution.py:199
  89.4 0.6 copy-done.15
  90.2 1.3 collective-permute-done.13.refs_7_
  91.5 0.8 copy-done.16
  92.3 29.2 %middle.1 = (bf16[1,1024,512]{2,1,0:T(8,128)(2,1)}, bf16[1024,512]{1,0:T(8,128)(2,1)}, f32[1024,512]{1,0:T(8,128)}, f32[1,512]{1,0:T(1,128)S(1)}, bf16[2,512,640...) custom-call(s32[1]{0:T(128)} %dynamic-slice.9.limit_ref, ...), custom_call_target="tpu_custom_call" | custom-call | flops 28750000128 | bytes 1048576 | tf_op jit(solution)/shard_map/middle/pallas_call | solution.py:370
  122.1 2.5 %collective-permute-done.15 = bf16[2,512,512]{2,1,0:T(8,128)(2,1)S(1)} collective-permute-done((bf16[2,512,512]{2,1,0:T(8,128)(2,1)}, bf16[2,512,512]{2,1,0:T(8,128)(2,1)S(1)}, u32[]{:S(2)}, u32[]{:S(2)}) %collective-permute-start.15) | collective-permute-done | bytes 1048608 | tf_op jit(solution)/shard_map/ppermute | solution.py:586
  124.5 1.7 convert_add_fusion
  126.2 1.2 collective-permute-start.16
  127.4 1.4 fusion.1
  129.0 1.2 copy-done.7
  130.2 14.2 %attend_back.2 = (bf16[1024,768]{1,0:T(8,128)(2,1)S(1)}, bf16[512,384]{1,0:T(8,128)(2,1)S(1)}, bf16[512,384]{1,0:T(8,128)(2,1)S(1)}) custom-call(s32[1]{0:T(128)} %dynamic-slice.9.limit_ref, bf16[1024,1536]{1,0:T(8,128)(2,1)S(1)} %copy-done.2, bf16[1024,1536]{1,0:T(8,128)(2,1)S(1)} %copy-done.2, bf16[1024,1536]{1,0:T(8,128)(2,1)S(1)} %copy-done.2, ...), custom_call_target="tpu_custom_call" | custom-call | flops 18400000000 | bytes 1048576 | tf_op jit(solution)/shard_map/attend_back/pallas_call | solution.py:465
  144.4 1.1 collective-permute-done.17
  145.5 1.4 fusion
  146.9 0.9 collective-permute-start.19
  148.1 2.0 collective-permute-start.21
  150.1 2.5 %collective-permute-start.22 = (bf16[2,64,512]{2,1,0:T(8,128)(2,1)S(1)}, bf16[2,64,512]{2,1,0:T(8,128)(2,1)S(1)}, u32[]{:S(2)}, u32[]{:S(2)}) collective-permute-start(bf16[2,64,512]{2,1,0:T(8,128)(2,1)S(1)} %get-tuple-element.185), channel_id=1, source_target_pairs={{0,16},{4,20},{8,24},{12,28},{16,0},{20,4},{24,8},{28,12},{1,17},{... | collective-permute-start | bytes 393224 | tf_op jit(solution)/shard_map/ppermute | solution.py:591
  152.6 2.0 collective-permute-start.23
  154.7 1.3 collective-permute-start.20
  156.0 14.2 %attend_back.3 = (bf16[1024,768]{1,0:T(8,128)(2,1)S(1)}, bf16[512,384]{1,0:T(8,128)(2,1)S(1)}, bf16[512,384]{1,0:T(8,128)(2,1)S(1)}) custom-call(s32[1]{0:T(128)} %dynamic-slice.9.limit_ref, bf16[1024,1536]{1,0:T(8,128)(2,1)S(1)} %copy-done.2, bf16[1024,1536]{1,0:T(8,128)(2,1)S(1)} %copy-done.2, bf16[1024,1536]{1,0:T(8,128)(2,1)S(1)} %copy-done.2, ...), custom_call_target="tpu_custom_call" | custom-call | flops 18400000000 | bytes 1048576 | tf_op jit(solution)/shard_map/attend_back/pallas_call | solution.py:465
  170.4 0.7 dynamic-slice_bitcast_fusion.4
  171.2 0.6 dynamic-slice_convert_fusion
  171.9 5.1 %begin_back.1 = bf16[8,4,136,128]{3,2,1,0:T(8,128)(2,1)} custom-call(s32[1]{0:T(128)} %dynamic-slice.9.limit_ref, bf16[8,4,136,128]{3,2,1,0:T(8,128)(2,1)S(1)} %bitcast.113, f32[1,512]{1,0:T(1,128)S(1)} %pad_maximum_fusion.10.clock_ref, f32[1,512]{1,0:T(1,128)S(1)} %reshape_squeeze.8.gain_ref, f32[1,512]{1,0:T(1,128)S(1)} %get-tuple-element.77.gg_two_ref, ...), custom_call_target="tpu_custom_call" | custom-call | flops 8049999872 | bytes 1048576 | tf_op jit(solution)/shard_map/begin_back/pallas_call | solution.py:553
  177.3 0.6 copy-done.13
  177.9 0.7 copy-done.11
  178.7 3.5 %all-to-all-start.1 = ((bf16[32,136,128]{2,1,0:T(8,128)(2,1)}), bf16[32,136,128]{2,1,0:T(8,128)(2,1)S(1)}, u32[]{:S(2)}, u32[]{:S(2)}) async-start(bf16[32,136,128]{2,1,0:T(8,128)(2,1)} %bitcast.25), calls=%async_computation.1 | async-start | bytes 2228224 | tf_op jit(solution)/shard_map/all_to_all | solution.py:800
  182.2 0.7 scatter_custom_fusion
  182.9 1.7 fusion.4
  184.6 1.8 collective-permute-start.26
  186.7 1.8 collective-permute-start.30
  188.5 2.1 collective-permute-start.31
  190.5 7.2 %collective-permute-done.26 = bf16[4,64,384]{2,1,0:T(8,128)(2,1)S(1)} collective-permute-done((bf16[4,64,384]{2,1,0:T(8,128)(2,1)}, bf16[4,64,384]{2,1,0:T(8,128)(2,1)S(1)}, u32[]{:S(2)}, u32[]{:S(2)}) %collective-permute-start.26) | collective-permute-done | bytes 196640 | tf_op jit(solution)/shard_map/ppermute | solution.py:591
  197.7 1.0 fusion.3
  198.7 1.3 collective-permute-done.32
  200.1 7.0 %collective-permute-done.30 = bf16[64,640]{1,0:T(8,128)(2,1)S(1)} collective-permute-done((bf16[64,640]{1,0:T(8,128)(2,1)}, bf16[64,640]{1,0:T(8,128)(2,1)S(1)}, u32[]{:S(2)}, u32[]{:S(2)}) %collective-permute-start.30) | collective-permute-done | bytes 81952 | tf_op jit(solution)/shard_map/ppermute | solution.py:591
  207.1 8.0 %collective-permute-start.27 = (bf16[64,384]{1,0:T(8,128)(2,1)S(1)}, bf16[64,384]{1,0:T(8,128)(2,1)S(1)}, u32[]{:S(2)}, u32[]{:S(2)}) collective-permute-start(bf16[64,384]{1,0:T(8,128)(2,1)S(1)} %get-tuple-element.192), channel_id=1, source_target_pairs={{0,8},{4,12},{8,16},{12,20},{16,24},{20,28},{24,0},{28,4},{1,9},{5... | collective-permute-start | bytes 147464 | tf_op jit(solution)/shard_map/ppermute | solution.py:591
  215.0 2.4 %collective-permute-start.29 = (bf16[64,384]{1,0:T(8,128)(2,1)S(1)}, bf16[64,384]{1,0:T(8,128)(2,1)S(1)}, u32[]{:S(2)}, u32[]{:S(2)}) collective-permute-start(bf16[64,384]{1,0:T(8,128)(2,1)S(1)} %get-tuple-element.193), channel_id=1, source_target_pairs={{0,24},{4,28},{8,0},{12,4},{16,8},{20,12},{24,16},{28,20},{1,25},{... | collective-permute-start | bytes 147464 | tf_op jit(solution)/shard_map/ppermute | solution.py:591
  217.5 0.7 add_bitcast_fusion
  218.2 0.6 slice_bitcast_fusion.2
  218.8 0.7 slice.97
  219.5 0.8 collective-permute-done.28
  220.3 0.7 copy_bitcast_fusion
  221.0 0.8 gather_fusion.1
  221.8 1.1 slice.95
  (110 shorter events, 7.1 us)
Async XLA Ops:
  0.6 10.3 %copy-start = (bf16[32,128,128]{2,1,0:T(8,128)(2,1)S(1)}, bf16[32,128,128]{2,1,0:T(8,128)(2,1)}, u32[]{:S(2)}) copy-start(bf16[32,128,128]{2,1,0:T(8,128)(2,1)} %param.11) | copy-start | bytes 3145732
  2.4 11.0 %collective-permute-start = (bf16[64,1536]{1,0:T(8,128)(2,1)S(1)}, bf16[64,1536]{1,0:T(8,128)(2,1)S(1)}, u32[]{:S(2)}, u32[]{:S(2)}) collective-permute-start(bf16[64,1536]{1,0:T(8,128)(2,1)S(1)} %pad_maximum_fusion.9), channel_id=1, source_target_pairs={{0,8},{4,12},{8,16},{12,20},{16,24},{20,28},{24,0},{28,4},{1,9},{5... | collective-permute-start | bytes 589832 | tf_op jit(solution)/shard_map/ppermute | solution.py:591
  5.5 15.5 %collective-permute-start.1 = (bf16[64,1536]{1,0:T(8,128)(2,1)S(1)}, bf16[64,1536]{1,0:T(8,128)(2,1)S(1)}, u32[]{:S(2)}, u32[]{:S(2)}) collective-permute-start(bf16[64,1536]{1,0:T(8,128)(2,1)S(1)} %pad_maximum_fusion.9), channel_id=1, source_target_pairs={{0,16},{4,20},{8,24},{12,28},{16,0},{20,4},{24,8},{28,12},{1,17},{... | collective-permute-start | bytes 589832 | tf_op jit(solution)/shard_map/ppermute | solution.py:591
  8.1 12.9 %collective-permute-start.2 = (bf16[64,1536]{1,0:T(8,128)(2,1)S(1)}, bf16[64,1536]{1,0:T(8,128)(2,1)S(1)}, u32[]{:S(2)}, u32[]{:S(2)}) collective-permute-start(bf16[64,1536]{1,0:T(8,128)(2,1)S(1)} %pad_maximum_fusion.9), channel_id=1, source_target_pairs={{0,24},{4,28},{8,0},{12,4},{16,8},{20,12},{24,16},{28,20},{1,25},{... | collective-permute-start | bytes 589832 | tf_op jit(solution)/shard_map/ppermute | solution.py:591
  12.8 16.1 %copy-start.9 = (bf16[512,64]{0,1:T(8,128)(2,1)S(1)}, bf16[512,64]{0,1:T(8,128)(2,1)}, u32[]{:S(2)}) copy-start(bf16[512,64]{0,1:T(8,128)(2,1)} %param.18) | copy-start | bytes 196612
  12.8 16.1 %copy-start.10 = (bf16[64,512]{1,0:T(8,128)(2,1)S(1)}, bf16[64,512]{1,0:T(8,128)(2,1)}, u32[]{:S(2)}) copy-start(bf16[64,512]{1,0:T(8,128)(2,1)} %param.17) | copy-start | bytes 196612
  12.8 16.2 %copy-start.12 = (bf16[128,64]{0,1:T(8,128)(2,1)S(1)}, bf16[128,64]{0,1:T(8,128)(2,1)}, u32[]{:S(2)}) copy-start(bf16[128,64]{0,1:T(8,128)(2,1)} %param.16) | copy-start | bytes 49156
  21.0 44.6 %all-to-all-start = ((bf16[32,136,128]{2,1,0:T(8,128)(2,1)}), bf16[32,136,128]{2,1,0:T(8,128)(2,1)S(1)}, u32[]{:S(2)}, u32[]{:S(2)}) async-start(bf16[32,136,128]{2,1,0:T(8,128)(2,1)} %pad_maximum_fusion), calls=%async_computation | async-start | bytes 2228224 | tf_op jit(solution)/shard_map/all_to_all | solution.py:734
  29.0 16.0 %copy-start.17 = (s32[32]{0:T(128)S(1)}, s32[32]{0:T(128)}, u32[]{:S(2)}) copy-start(s32[32]{0:T(128)} %param.14) | copy-start | bytes 388
  29.0 18.5 %copy-start.18 = (s32[32]{0:T(128)S(1)}, s32[32]{0:T(128)}, u32[]{:S(2)}) copy-start(s32[32]{0:T(128)} %param.12) | copy-start | bytes 388
  29.0 19.7 %copy-start.19 = (s32[32]{0:T(128)S(1)}, s32[32]{0:T(128)}, u32[]{:S(2)}) copy-start(s32[32]{0:T(128)} %param.13) | copy-start | bytes 388
  29.1 15.4 %collective-permute-start.3 = (bf16[256,384]{1,0:T(8,128)(2,1)S(1)}, bf16[256,384]{1,0:T(8,128)(2,1)S(1)}, u32[]{:S(2)}, u32[]{:S(2)}) collective-permute-start(bf16[256,384]{1,0:T(8,128)(2,1)S(1)} %pad_maximum_fusion.8), channel_id=1, source_target_pairs={{0,4},{4,0},{8,12},{12,8},{16,20},{20,16},{24,28},{28,24},{1,5},{5... | collective-permute-start | bytes 589832 | tf_op jit(solution)/shard_map/ppermute | solution.py:591
  31.8 33.0 %collective-permute-start.7 = (bf16[256,1152]{1,0:T(8,128)(2,1)}, bf16[256,1152]{1,0:T(8,128)(2,1)}, u32[]{:S(2)}, u32[]{:S(2)}) collective-permute-start(bf16[256,1152]{1,0:T(8,128)(2,1)} %pad_maximum_fusion.1.refs_0_), channel_id=1, source_target_pairs={{0,2},{1,3},{2,0},{3,1},{4,6},{5,7},{6,4},{7,5},{8,10},{9,11},{10,... | collective-permute-start | bytes 1769480 | tf_op jit(solution)/shard_map/ppermute | solution.py:586
  44.5 20.4 %collective-permute-start.6 = (bf16[256,1152]{1,0:T(8,128)(2,1)}, bf16[256,1152]{1,0:T(8,128)(2,1)}, u32[]{:S(2)}, u32[]{:S(2)}) collective-permute-start(bf16[256,1152]{1,0:T(8,128)(2,1)} %pad_maximum_fusion.1.refs_0_), channel_id=1, source_target_pairs={{0,4},{4,0},{8,12},{12,8},{16,20},{20,16},{24,28},{28,24},{1,5},{5... | collective-permute-start | bytes 1769480 | tf_op jit(solution)/shard_map/ppermute | solution.py:591
  49.4 15.4 %collective-permute-start.5 = (bf16[512,384]{1,0:T(8,128)(2,1)S(1)}, bf16[512,384]{1,0:T(8,128)(2,1)S(1)}, u32[]{:S(2)}, u32[]{:S(2)}) collective-permute-start(bf16[512,384]{1,0:T(8,128)(2,1)S(1)} %pad_maximum_fusion.7.refs_0_), channel_id=1, source_target_pairs={{0,2},{1,3},{2,0},{3,1},{4,6},{5,7},{6,4},{7,5},{8,10},{9,11},{10,... | collective-permute-start | bytes 1179656 | tf_op jit(solution)/shard_map/ppermute | solution.py:586
  51.5 37.7 %collective-permute-start.9 = (bf16[256,1152]{1,0:T(8,128)(2,1)}, bf16[256,1152]{1,0:T(8,128)(2,1)}, u32[]{:S(2)}, u32[]{:S(2)}) collective-permute-start(bf16[256,1152]{1,0:T(8,128)(2,1)} %pad_maximum_fusion.1.refs_0_), channel_id=1, source_target_pairs={{0,1},{1,0},{2,3},{3,2},{4,5},{5,4},{6,7},{7,6},{8,9},{9,8},{10,11... | collective-permute-start | bytes 1769480 | tf_op jit(solution)/shard_map/ppermute | solution.py:586
  51.6 14.3 %collective-permute-start.4 = (bf16[512,384]{1,0:T(8,128)(2,1)S(1)}, bf16[512,384]{1,0:T(8,128)(2,1)S(1)}, u32[]{:S(2)}, u32[]{:S(2)}) collective-permute-start(bf16[512,384]{1,0:T(8,128)(2,1)S(1)} %pad_maximum_fusion.7.refs_0_), channel_id=1, source_target_pairs={{0,1},{1,0},{2,3},{3,2},{4,5},{5,4},{6,7},{7,6},{8,9},{9,8},{10,11... | collective-permute-start | bytes 1179656 | tf_op jit(solution)/shard_map/ppermute | solution.py:586
  64.8 24.3 %collective-permute-start.10 = (bf16[256,1152]{1,0:T(8,128)(2,1)}, bf16[256,1152]{1,0:T(8,128)(2,1)}, u32[]{:S(2)}, u32[]{:S(2)}) collective-permute-start(bf16[256,1152]{1,0:T(8,128)(2,1)} %collective-permute-done.6.refs_1_), channel_id=1, source_target_pairs={{0,1},{1,0},{2,3},{3,2},{4,5},{5,4},{6,7},{7,6},{8,9},{9,8},{10,11... | collective-permute-start | bytes 1769480 | tf_op jit(solution)/shard_map/ppermute | solution.py:586
  64.8 24.3 %collective-permute-start.12 = (bf16[256,1152]{1,0:T(8,128)(2,1)}, bf16[256,1152]{1,0:T(8,128)(2,1)}, u32[]{:S(2)}, u32[]{:S(2)}) collective-permute-start(bf16[256,1152]{1,0:T(8,128)(2,1)} %collective-permute-done.6.refs_1_), channel_id=1, source_target_pairs={{0,2},{1,3},{2,0},{3,1},{4,6},{5,7},{6,4},{7,5},{8,10},{9,11},{10,... | collective-permute-start | bytes 1769480 | tf_op jit(solution)/shard_map/ppermute | solution.py:586
  65.4 2.1 collective-permute-start.8
  65.9 23.3 %collective-permute-start.11 = (bf16[256,1152]{1,0:T(8,128)(2,1)}, bf16[256,1152]{1,0:T(8,128)(2,1)S(1)}, u32[]{:S(2)}, u32[]{:S(2)}) collective-permute-start(bf16[256,1152]{1,0:T(8,128)(2,1)} %collective-permute-done.7.refs_4_), channel_id=1, source_target_pairs={{0,1},{1,0},{2,3},{3,2},{4,5},{5,4},{6,7},{7,6},{8,9},{9,8},{10,11... | collective-permute-start | bytes 1769480 | tf_op jit(solution)/shard_map/ppermute | solution.py:586
  73.8 15.3 %copy-start.1 = (bf16[1024,1536]{1,0:T(8,128)(2,1)}, bf16[1024,1536]{1,0:T(8,128)(2,1)S(1)}, u32[]{:S(2)}) copy-start(bf16[1024,1536]{1,0:T(8,128)(2,1)S(1)} %get-tuple-element.67.q_ref.k_ref.v_ref) | copy-start | bytes 9437188
  89.2 0.8 copy-start.15
  89.2 2.3 %collective-permute-start.13 = (bf16[256,1152]{1,0:T(8,128)(2,1)}, bf16[256,1152]{1,0:T(8,128)(2,1)S(1)}, u32[]{:S(2)}, u32[]{:S(2)}) collective-permute-start(bf16[256,1152]{1,0:T(8,128)(2,1)} %collective-permute-done.12.refs_5_), channel_id=1, source_target_pairs={{0,1},{1,0},{2,3},{3,2},{4,5},{5,4},{6,7},{7,6},{8,9},{9,8},{10,11... | collective-permute-start | bytes 1769480 | tf_op jit(solution)/shard_map/ppermute | solution.py:586
  91.5 0.8 copy-start.16
  121.5 3.0 %collective-permute-start.15 = (bf16[2,512,512]{2,1,0:T(8,128)(2,1)}, bf16[2,512,512]{2,1,0:T(8,128)(2,1)S(1)}, u32[]{:S(2)}, u32[]{:S(2)}) collective-permute-start(bf16[2,512,512]{2,1,0:T(8,128)(2,1)} %get-tuple-element.85), channel_id=1, source_target_pairs={{0,1},{1,0},{2,3},{3,2},{4,5},{5,4},{6,7},{7,6},{8,9},{9,8},{10,11... | collective-permute-start | bytes 3145736 | tf_op jit(solution)/shard_map/ppermute | solution.py:586
  121.7 5.7 %collective-permute-start.14 = (bf16[2,512,640]{2,1,0:T(8,128)(2,1)}, bf16[2,512,640]{2,1,0:T(8,128)(2,1)}, u32[]{:S(2)}, u32[]{:S(2)}) collective-permute-start(bf16[2,512,640]{2,1,0:T(8,128)(2,1)} %get-tuple-element.80), channel_id=1, source_target_pairs={{0,1},{1,0},{2,3},{3,2},{4,5},{5,4},{6,7},{7,6},{8,9},{9,8},{10,11... | collective-permute-start | bytes 3932168 | tf_op jit(solution)/shard_map/ppermute | solution.py:586
  124.5 4.4 %copy-start.2 = (bf16[1024,1536]{1,0:T(8,128)(2,1)S(1)}, bf16[1024,1536]{1,0:T(8,128)(2,1)}, u32[]{:S(2)}) copy-start(bf16[1024,1536]{1,0:T(8,128)(2,1)} %copy-done.1) | copy-start | bytes 9437188
  124.5 4.4 %copy-start.6 = (bf16[512,1024]{1,0:T(8,128)(2,1)S(1)}, bf16[512,1024]{1,0:T(8,128)(2,1)}, u32[]{:S(2)}) copy-start(bf16[512,1024]{1,0:T(8,128)(2,1)} %get-tuple-element.81.turn_ref) | copy-start | bytes 3145732
  126.2 2.8 %copy-start.5 = (bf16[512,1024]{1,0:T(8,128)(2,1)S(1)}, bf16[512,1024]{1,0:T(8,128)(2,1)}, u32[]{:S(2)}) copy-start(bf16[512,1024]{1,0:T(8,128)(2,1)} %get-tuple-element.87.n_turn_ref) | copy-start | bytes 3145732
  126.2 18.2 %collective-permute-start.16 = (bf16[4,2,64,512]{3,2,1,0:T(8,128)(2,1)S(1)}, bf16[4,2,64,512]{3,2,1,0:T(8,128)(2,1)S(1)}, u32[]{:S(2)}, u32[]{:S(2)}) collective-permute-start(bf16[4,2,64,512]{3,2,1,0:T(8,128)(2,1)S(1)} %bitcast.122), channel_id=1, source_target_pairs={{0,2},{1,3},{2,0},{3,1},{4,6},{5,7},{6,4},{7,5},{8,10},{9,11},{10,... | collective-permute-start | bytes 1572872 | tf_op jit(solution)/shard_map/ppermute | solution.py:586
  128.9 16.6 %collective-permute-start.17 = (bf16[2,4,64,640]{3,2,1,0:T(8,128)(2,1)S(1)}, bf16[2,4,64,640]{3,2,1,0:T(8,128)(2,1)S(1)}, u32[]{:S(2)}, u32[]{:S(2)}) collective-permute-start(bf16[2,4,64,640]{3,2,1,0:T(8,128)(2,1)S(1)} %fusion.1), channel_id=1, source_target_pairs={{0,4},{4,0},{8,12},{12,8},{16,20},{20,16},{24,28},{28,24},{1,5},{5... | collective-permute-start | bytes 1966088 | tf_op jit(solution)/shard_map/ppermute | solution.py:591
  129.0 1.2 copy-start.7
  130.2 15.3 %copy-start.8 = (bf16[2,512,640]{2,1,0:T(8,128)(2,1)S(1)}, bf16[2,512,640]{2,1,0:T(8,128)(2,1)}, u32[]{:S(2)}) copy-start(bf16[2,512,640]{2,1,0:T(8,128)(2,1)} %get-tuple-element.79) | copy-start | bytes 3932164
  145.5 9.1 %collective-permute-start.18 = (bf16[512,384]{1,0:T(8,128)(2,1)S(1)}, bf16[512,384]{1,0:T(8,128)(2,1)S(1)}, u32[]{:S(2)}, u32[]{:S(2)}) collective-permute-start(bf16[512,384]{1,0:T(8,128)(2,1)S(1)} %get-tuple-element.96), channel_id=1, source_target_pairs={{0,1},{1,0},{2,3},{3,2},{4,5},{5,4},{6,7},{7,6},{8,9},{9,8},{10,11... | collective-permute-start | bytes 1179656 | tf_op jit(solution)/shard_map/ppermute | solution.py:586
  146.9 23.3 %collective-permute-start.19 = (bf16[4,64,640]{2,1,0:T(8,128)(2,1)S(1)}, bf16[4,64,640]{2,1,0:T(8,128)(2,1)S(1)}, u32[]{:S(2)}, u32[]{:S(2)}) collective-permute-start(bf16[4,64,640]{2,1,0:T(8,128)(2,1)S(1)} %slice_bitcast_fusion), channel_id=1, source_target_pairs={{0,2},{1,3},{2,0},{3,1},{4,6},{5,7},{6,4},{7,5},{8,10},{9,11},{10,... | collective-permute-start | bytes 983048 | tf_op jit(solution)/shard_map/ppermute | solution.py:586
  148.1 22.2 %collective-permute-start.21 = (bf16[2,64,512]{2,1,0:T(8,128)(2,1)S(1)}, bf16[2,64,512]{2,1,0:T(8,128)(2,1)S(1)}, u32[]{:S(2)}, u32[]{:S(2)}) collective-permute-start(bf16[2,64,512]{2,1,0:T(8,128)(2,1)S(1)} %get-tuple-element.186), channel_id=1, source_target_pairs={{0,8},{4,12},{8,16},{12,20},{16,24},{20,28},{24,0},{28,4},{1,9},{5... | collective-permute-start | bytes 393224 | tf_op jit(solution)/shard_map/ppermute | solution.py:591
  150.1 20.1 %collective-permute-start.22 = (bf16[2,64,512]{2,1,0:T(8,128)(2,1)S(1)}, bf16[2,64,512]{2,1,0:T(8,128)(2,1)S(1)}, u32[]{:S(2)}, u32[]{:S(2)}) collective-permute-start(bf16[2,64,512]{2,1,0:T(8,128)(2,1)S(1)} %get-tuple-element.185), channel_id=1, source_target_pairs={{0,16},{4,20},{8,24},{12,28},{16,0},{20,4},{24,8},{28,12},{1,17},{... | collective-permute-start | bytes 393224 | tf_op jit(solution)/shard_map/ppermute | solution.py:591
  152.6 17.7 %collective-permute-start.23 = (bf16[2,64,512]{2,1,0:T(8,128)(2,1)S(1)}, bf16[2,64,512]{2,1,0:T(8,128)(2,1)S(1)}, u32[]{:S(2)}, u32[]{:S(2)}) collective-permute-start(bf16[2,64,512]{2,1,0:T(8,128)(2,1)S(1)} %get-tuple-element.184), channel_id=1, source_target_pairs={{0,24},{4,28},{8,0},{12,4},{16,8},{20,12},{24,16},{28,20},{1,25},{... | collective-permute-start | bytes 393224 | tf_op jit(solution)/shard_map/ppermute | solution.py:591
  154.7 15.6 %collective-permute-start.20 = (bf16[512,384]{1,0:T(8,128)(2,1)S(1)}, bf16[512,384]{1,0:T(8,128)(2,1)S(1)}, u32[]{:S(2)}, u32[]{:S(2)}) collective-permute-start(bf16[512,384]{1,0:T(8,128)(2,1)S(1)} %add_convert_fusion.3), channel_id=1, source_target_pairs={{0,2},{1,3},{2,0},{3,1},{4,6},{5,7},{6,4},{7,5},{8,10},{9,11},{10,... | collective-permute-start | bytes 1179656 | tf_op jit(solution)/shard_map/ppermute | solution.py:586
  156.0 15.9 %copy-start.4 = (bf16[512,1536]{1,0:T(8,128)(2,1)S(1)}, bf16[512,1536]{1,0:T(8,128)(2,1)}, u32[]{:S(2)}) copy-start(bf16[512,1536]{1,0:T(8,128)(2,1)} %get-tuple-element.107.w_ref) | copy-start | bytes 4718596
  170.3 1.7 copy-start.3
  171.1 6.2 %collective-permute-start.25 = (bf16[64,640]{1,0:T(8,128)(2,1)S(1)}, bf16[64,640]{1,0:T(8,128)(2,1)S(1)}, u32[]{:S(2)}, u32[]{:S(2)}) collective-permute-start(bf16[64,640]{1,0:T(8,128)(2,1)S(1)} %get-tuple-element.191), channel_id=1, source_target_pairs={{0,16},{4,20},{8,24},{12,28},{16,0},{20,4},{24,8},{28,12},{1,17},{... | collective-permute-start | bytes 245768 | tf_op jit(solution)/shard_map/ppermute | solution.py:591
  171.9 5.4 %collective-permute-start.24 = (bf16[512,384]{1,0:T(8,128)(2,1)S(1)}, bf16[512,384]{1,0:T(8,128)(2,1)S(1)}, u32[]{:S(2)}, u32[]{:S(2)}) collective-permute-start(bf16[512,384]{1,0:T(8,128)(2,1)S(1)} %get-tuple-element.109), channel_id=1, source_target_pairs={{0,1},{1,0},{2,3},{3,2},{4,5},{5,4},{6,7},{7,6},{8,9},{9,8},{10,11... | collective-permute-start | bytes 1179656 | tf_op jit(solution)/shard_map/ppermute | solution.py:586
  177.3 0.6 copy-start.13
  177.9 0.7 copy-start.11
  178.7 42.3 %all-to-all-start.1 = ((bf16[32,136,128]{2,1,0:T(8,128)(2,1)}), bf16[32,136,128]{2,1,0:T(8,128)(2,1)S(1)}, u32[]{:S(2)}, u32[]{:S(2)}) async-start(bf16[32,136,128]{2,1,0:T(8,128)(2,1)} %bitcast.25), calls=%async_computation.1 | async-start | bytes 2228224 | tf_op jit(solution)/shard_map/all_to_all | solution.py:800
  184.6 13.1 %collective-permute-start.26 = (bf16[4,64,384]{2,1,0:T(8,128)(2,1)}, bf16[4,64,384]{2,1,0:T(8,128)(2,1)S(1)}, u32[]{:S(2)}, u32[]{:S(2)}) collective-permute-start(bf16[4,64,384]{2,1,0:T(8,128)(2,1)} %fusion.4), channel_id=1, source_target_pairs={{0,4},{4,0},{8,12},{12,8},{16,20},{20,16},{24,28},{28,24},{1,5},{5... | collective-permute-start | bytes 589832 | tf_op jit(solution)/shard_map/ppermute | solution.py:591
  186.3 31.8 %copy-start.14 = (bf16[64,640]{1,0:T(8,128)(2,1)S(1)}, bf16[64,640]{1,0:T(8,128)(2,1)}, u32[]{:S(2)}) copy-start(bf16[64,640]{1,0:T(8,128)(2,1)} %copy-done.13) | copy-start | bytes 245764
  186.4 13.7 %collective-permute-start.32 = (bf16[1,64,512]{2,1,0:T(8,128)(2,1)}, bf16[1,64,512]{2,1,0:T(8,128)(2,1)S(1)}, u32[]{:S(2)}, u32[]{:S(2)}) collective-permute-start(bf16[1,64,512]{2,1,0:T(8,128)(2,1)} %dynamic-slice_convert_fusion), channel_id=1, source_target_pairs={{0,4},{4,0},{8,12},{12,8},{16,20},{20,16},{24,28},{28,24},{1,5},{5... | collective-permute-start | bytes 196616 | tf_op jit(solution)/shard_map/ppermute | solution.py:591
  186.7 20.4 %collective-permute-start.30 = (bf16[64,640]{1,0:T(8,128)(2,1)}, bf16[64,640]{1,0:T(8,128)(2,1)S(1)}, u32[]{:S(2)}, u32[]{:S(2)}) collective-permute-start(bf16[64,640]{1,0:T(8,128)(2,1)} %get-tuple-element.189), channel_id=1, source_target_pairs={{0,8},{4,12},{8,16},{12,20},{16,24},{20,28},{24,0},{28,4},{1,9},{5... | collective-permute-start | bytes 245768 | tf_op jit(solution)/shard_map/ppermute | solution.py:591
  188.5 18.6 %collective-permute-start.31 = (bf16[64,640]{1,0:T(8,128)(2,1)}, bf16[64,640]{1,0:T(8,128)(2,1)S(1)}, u32[]{:S(2)}, u32[]{:S(2)}) collective-permute-start(bf16[64,640]{1,0:T(8,128)(2,1)} %get-tuple-element.188), channel_id=1, source_target_pairs={{0,24},{4,28},{8,0},{12,4},{16,8},{20,12},{24,16},{28,20},{1,25},{... | collective-permute-start | bytes 245768 | tf_op jit(solution)/shard_map/ppermute | solution.py:591
  207.1 12.4 %collective-permute-start.27 = (bf16[64,384]{1,0:T(8,128)(2,1)S(1)}, bf16[64,384]{1,0:T(8,128)(2,1)S(1)}, u32[]{:S(2)}, u32[]{:S(2)}) collective-permute-start(bf16[64,384]{1,0:T(8,128)(2,1)S(1)} %get-tuple-element.192), channel_id=1, source_target_pairs={{0,8},{4,12},{8,16},{12,20},{16,24},{20,28},{24,0},{28,4},{1,9},{5... | collective-permute-start | bytes 147464 | tf_op jit(solution)/shard_map/ppermute | solution.py:591
  215.0 5.3 %collective-permute-start.28 = (bf16[64,384]{1,0:T(8,128)(2,1)S(1)}, bf16[64,384]{1,0:T(8,128)(2,1)S(1)}, u32[]{:S(2)}, u32[]{:S(2)}) collective-permute-start(bf16[64,384]{1,0:T(8,128)(2,1)S(1)} %get-tuple-element.194), channel_id=1, source_target_pairs={{0,16},{4,20},{8,24},{12,28},{16,0},{20,4},{24,8},{28,12},{1,17},{... | collective-permute-start | bytes 147464 | tf_op jit(solution)/shard_map/ppermute | solution.py:591
  215.0 5.3 %collective-permute-start.29 = (bf16[64,384]{1,0:T(8,128)(2,1)S(1)}, bf16[64,384]{1,0:T(8,128)(2,1)S(1)}, u32[]{:S(2)}, u32[]{:S(2)}) collective-permute-start(bf16[64,384]{1,0:T(8,128)(2,1)S(1)} %get-tuple-element.193), channel_id=1, source_target_pairs={{0,24},{4,28},{8,0},{12,4},{16,8},{20,12},{24,16},{28,20},{1,25},{... | collective-permute-start | bytes 147464 | tf_op jit(solution)/shard_map/ppermute | solution.py:591

commit v11 on v9

--- a/solution.py
+++ b/solution.py
@@ -760,7 +760,7 @@
         down_sent, down_rest = fold_far([grouped(value) for value in (down_keep, down_came)])
         up_sent, up_rest = fold_pair([grouped(value) for value in (up_keep, up_came)])
         context_grad = after(context_grad, down_sent, up_sent)
-    high, three, two = back(context_grad, n_one_turn, 3)
+    high, three, two = back(in_hbm(context_grad), n_one_turn, 3)
     if direct:
         *down_rest, down_came = down_rest()
         *up_rest, up_came = up_rest()
@@ -787,10 +787,10 @@
         begin_grad, came_one, up_pieces[2] = together(begin_grad, came_one, up_pieces[2])
         near = [grouped(value[None])[0] for value in (own_part, came_one, came_far)]
         qkv_value, qkv_pieces = fold_coarse(fold_pair(near)[1]())
-        *up_pieces, down_came, _ = together(*up_pieces, down_rest()[-1], qkv_value)
-        up_total = add_wide(*up_pieces)
-        down_total = add_wide(*down_rest()[:-1], down_came)[0]
-        qkv_total = add_wide(*qkv_pieces)
+        down_total = add_wide(*down_rest())[0]
+        pieces = together(*up_pieces, *qkv_pieces)
+        up_total = add_wide(*pieces[: len(up_pieces)])
+        qkv_total = add_wide(*pieces[len(up_pieces) :])
     else:
         up_total = exchange_rows(add(*fold_far([up_keep, up_came])[1]()))
         down_total = exchange_rows(add(*fold_far([down_keep, down_came])[1]()))

time: 222 us -> 220 us (level)
  starting transfers between devices: 56.3 us -> 50.6 us
  waiting for transfers between devices: 49.6 us -> 54.2 us
    ppermute x20, starting transfers between devices: 39 us -> 34.3 us  [along_dp(): return lax.ppermute(value, 'dp', [(i, move(i)) for i in range(count)])]
    ppermute x20, waiting for transfers between devices: 37.1 us -> 41 us  [along_dp(): return lax.ppermute(value, 'dp', [(i, move(i)) for i in range(count)])]
  transfers between devices with their start and end apart: 38 -> 38, of which waited for: 12 -> 12; matrix products, arithmetic and copies ran while one was open for 9% -> 8% of each run, Pallas kernels for 25% -> 25%
where the time goes in v11:
time: 220 us
  Pallas kernels  84.8 us (39%)
  waiting for transfers between devices  54.2 us (25%)
  starting transfers between devices  50.6 us (23%)
  other arithmetic  13.5 us (6%)
  local copies, waits for them, and re-layouts  12.9 us (6%)
  between operations  3.79 us (2%)
    ppermute x20, waiting for transfers between devices, along_dp(): return lax.ppermute(value, 'dp', [(i, move(i)) for i in range(count)])  41 us
    ppermute x20, starting transfers between devices, along_dp(): return lax.ppermute(value, 'dp', [(i, move(i)) for i in range(count)])  34.3 us
    pallas_call x2, Pallas kernels, attend_back(): pl.pallas_call(attend_back_kernel, grid_spec=pltpu.PrefetchScalarGridSpec...  29.1 us
    pallas_call x1, Pallas kernels, middle_block(): pl.pallas_call(functools.partial(middle_kernel, groups), grid_spec=pltpu....  29 us
    pallas_call x1, Pallas kernels, attend(): pl.pallas_call(attend_kernel, grid_spec=pltpu.PrefetchScalarGridSpec(num_...  15.4 us
    ppermute x16, waiting for transfers between devices, swap(): return lax.ppermute(value, 'tensor', [(i, i ^ apart) for i in range(count)])  13.3 us
    ppermute x16, starting transfers between devices, swap(): return lax.ppermute(value, 'tensor', [(i, i ^ apart) for i in range(count)])  9.1 us
    pallas_call x1, Pallas kernels, project(): pl.pallas_call(functools.partial(project_kernel, groups), grid_spec=pltpu...  6.27 us
  transfers between devices with their start and end apart: 38, of which 12 were waited for; matrix products, arithmetic and copies ran while one was open for 8% of the time, Pallas kernels for 25%

profile of v11, /device:TPU:0, one launch (start us, length us, event | category | flops | bytes accessed | tf_op | source)
XLA Modules:
  0.0 219.9 jit_solution(9623413097955206235)
XLA Ops:
  0.6 1.0 pad_maximum_fusion.2
  1.6 3.1 %collective-permute-start.6 = (bf16[64,1152]{1,0:T(8,128)(2,1)S(1)}, bf16[64,1152]{1,0:T(8,128)(2,1)S(1)}, u32[]{:S(2)}, u32[]{:S(2)}) collective-permute-start(bf16[64,1152]{1,0:T(8,128)(2,1)S(1)} %pad_maximum_fusion.2), channel_id=1, source_target_pairs={{0,8},{4,12},{8,16},{12,20},{16,24},{20,28},{24,0},{28,4},{1,9},{5... | collective-permute-start | bytes 442376 | tf_op jit(solution)/shard_map/ppermute | solution.py:591
  4.7 2.6 %collective-permute-start.7 = (bf16[64,1152]{1,0:T(8,128)(2,1)S(1)}, bf16[64,1152]{1,0:T(8,128)(2,1)S(1)}, u32[]{:S(2)}, u32[]{:S(2)}) collective-permute-start(bf16[64,1152]{1,0:T(8,128)(2,1)S(1)} %pad_maximum_fusion.2), channel_id=1, source_target_pairs={{0,16},{4,20},{8,24},{12,28},{16,0},{20,4},{24,8},{28,12},{1,17},{... | collective-permute-start | bytes 442376 | tf_op jit(solution)/shard_map/ppermute | solution.py:591
  7.3 1.3 collective-permute-start.8
  8.6 0.8 copy_bitcast_fusion.1
  9.4 1.5 collective-permute-start
  11.0 0.7 fusion.9
  11.8 0.7 compare_select_fusion.1
  12.5 0.7 gather_fusion
  13.2 1.1 pad_maximum_fusion
  14.4 2.8 %all-to-all-start = ((bf16[32,136,128]{2,1,0:T(8,128)(2,1)}), bf16[32,136,128]{2,1,0:T(8,128)(2,1)S(1)}, u32[]{:S(2)}, u32[]{:S(2)}) async-start(bf16[32,136,128]{2,1,0:T(8,128)(2,1)} %pad_maximum_fusion), calls=%async_computation | async-start | bytes 2228224 | tf_op jit(solution)/shard_map/all_to_all | solution.py:732
  21.7 1.7 collective-permute-start.1
  23.4 2.5 %collective-permute-start.2 = (bf16[64,768]{1,0:T(8,128)(2,1)S(1)}, bf16[64,768]{1,0:T(8,128)(2,1)S(1)}, u32[]{:S(2)}, u32[]{:S(2)}) collective-permute-start(bf16[64,768]{1,0:T(8,128)(2,1)S(1)} %constant_dynamic-update-slice_fusion), channel_id=1, source_target_pairs={{0,16},{4,20},{8,24},{12,28},{16,0},{20,4},{24,8},{28,12},{1,17},{... | collective-permute-start | bytes 294920 | tf_op jit(solution)/shard_map/ppermute | solution.py:591
  25.9 1.4 collective-permute-start.3
  27.3 0.9 pad_maximum_fusion.1.refs_0_
  28.2 1.5 collective-permute-start.10
  29.7 1.5 collective-permute-start.9
  31.2 11.2 %collective-permute-done.1 = bf16[64,768]{1,0:T(8,128)(2,1)S(1)} collective-permute-done((bf16[64,768]{1,0:T(8,128)(2,1)S(1)}, bf16[64,768]{1,0:T(8,128)(2,1)S(1)}, u32[]{:S(2)}, u32[]{:S(2)}) %collective-permute-start.1) | collective-permute-done | bytes 98336 | tf_op jit(solution)/shard_map/ppermute | solution.py:591
  42.4 9.2 %collective-permute-done.2 = bf16[64,768]{1,0:T(8,128)(2,1)S(1)} collective-permute-done((bf16[64,768]{1,0:T(8,128)(2,1)S(1)}, bf16[64,768]{1,0:T(8,128)(2,1)S(1)}, u32[]{:S(2)}, u32[]{:S(2)}) %collective-permute-start.2) | collective-permute-done | bytes 98336 | tf_op jit(solution)/shard_map/ppermute | solution.py:591
  51.7 1.6 collective-permute-start.5
  54.1 7.9 %collective-permute-done.5.refs_2_ = bf16[512,384]{1,0:T(8,128)(2,1)S(1)} collective-permute-done((bf16[512,384]{1,0:T(8,128)(2,1)S(1)}, bf16[512,384]{1,0:T(8,128)(2,1)S(1)}, u32[]{:S(2)}, u32[]{:S(2)}) %collective-permute-start.5) | collective-permute-done | bytes 393248 | tf_op jit(solution)/shard_map/ppermute | solution.py:586
  62.1 1.6 collective-permute-start.15
  64.6 1.0 collective-permute-done.11.refs_3_
  65.5 6.3 %project.1 = (bf16[1024,1536]{1,0:T(8,128)(2,1)S(1)}, bf16[512,1024]{1,0:T(8,128)(2,1)}, bf16[512,1536]{1,0:T(8,128)(2,1)}) custom-call(s32[1]{0:T(128)} %dynamic-slice.9.limit_ref, s32[8]{0:T(128)S(1)} %pad_add_fusion.place_ref, bf16[8,4,136,128]{3,2,1,0:T(8,128)(2,1)S(1)} %bitcast.109, f32[1,512]{1,0:T(1,128)S(1)} %pad_maximum_fusion.3.clock_ref, ...), custom_call_target="tpu_custom_call" | custom-call | flops 5750000128 | bytes 1048576 | tf_op jit(solution)/shard_map/project/pallas_call | solution.py:110
  71.8 15.4 %attend.1 = (bf16[1024,512]{1,0:T(8,128)(2,1)}, bf16[512,1024]{1,0:T(8,128)(2,1)}, f32[4,2,1024]{2,1,0:T(2,128)S(1)}) custom-call(s32[1]{0:T(128)} %dynamic-slice.9.limit_ref, bf16[1024,1536]{1,0:T(8,128)(2,1)S(1)} %get-tuple-element.66.q_ref.k_ref.v_ref, bf16[1024,1536]{1,0:T(8,128)(2,1)S(1)} %get-tuple-element.66.q_ref.k_ref.v_ref, ...), custom_call_target="tpu_custom_call" | custom-call | flops 17250000896 | bytes 1048576 | tf_op jit(solution)/shard_map/attend/pallas_call | solution.py:199
  87.3 0.7 copy-done.17
  88.2 1.3 collective-permute-done.16.refs_7_
  89.5 0.8 copy-done.18
  90.3 29.0 %middle.1 = (bf16[1,1024,512]{2,1,0:T(8,128)(2,1)}, bf16[1024,512]{1,0:T(8,128)(2,1)}, f32[1024,512]{1,0:T(8,128)}, f32[1,512]{1,0:T(1,128)S(1)}, bf16[2,512,640...) custom-call(s32[1]{0:T(128)} %dynamic-slice.9.limit_ref, ...), custom_call_target="tpu_custom_call" | custom-call | flops 28750000128 | bytes 1048576 | tf_op jit(solution)/shard_map/middle/pallas_call | solution.py:370
  119.9 3.1 %collective-permute-done.18 = bf16[2,512,512]{2,1,0:T(8,128)(2,1)S(1)} collective-permute-done((bf16[2,512,512]{2,1,0:T(8,128)(2,1)}, bf16[2,512,512]{2,1,0:T(8,128)(2,1)S(1)}, u32[]{:S(2)}, u32[]{:S(2)}) %collective-permute-start.18) | collective-permute-done | bytes 1048608 | tf_op jit(solution)/shard_map/ppermute | solution.py:586
  123.0 1.6 convert_add_fusion
  124.7 1.5 fusion.1
  126.3 1.6 collective-permute-start.20
  127.8 14.9 %attend_back.2 = (bf16[1024,768]{1,0:T(8,128)(2,1)S(1)}, bf16[512,384]{1,0:T(8,128)(2,1)S(1)}, bf16[512,384]{1,0:T(8,128)(2,1)S(1)}) custom-call(s32[1]{0:T(128)} %dynamic-slice.9.limit_ref, bf16[1024,1536]{1,0:T(8,128)(2,1)S(1)} %copy-done.2, bf16[1024,1536]{1,0:T(8,128)(2,1)S(1)} %copy-done.2, bf16[1024,1536]{1,0:T(8,128)(2,1)S(1)} %copy-done.2, ...), custom_call_target="tpu_custom_call" | custom-call | flops 18400000000 | bytes 1048576 | tf_op jit(solution)/shard_map/attend_back/pallas_call | solution.py:465
  143.1 1.3 fusion
  144.5 1.7 collective-permute-start.22
  146.4 2.7 %collective-permute-start.24 = (bf16[2,64,512]{2,1,0:T(8,128)(2,1)S(1)}, bf16[2,64,512]{2,1,0:T(8,128)(2,1)S(1)}, u32[]{:S(2)}, u32[]{:S(2)}) collective-permute-start(bf16[2,64,512]{2,1,0:T(8,128)(2,1)S(1)} %get-tuple-element.188), channel_id=1, source_target_pairs={{0,8},{4,12},{8,16},{12,20},{16,24},{20,28},{24,0},{28,4},{1,9},{5... | collective-permute-start | bytes 393224 | tf_op jit(solution)/shard_map/ppermute | solution.py:591
  149.2 1.5 collective-permute-start.25
  150.7 0.9 collective-permute-start.26
  151.7 0.8 collective-permute-start.23
  152.5 14.2 %attend_back.3 = (bf16[1024,768]{1,0:T(8,128)(2,1)S(1)}, bf16[512,384]{1,0:T(8,128)(2,1)S(1)}, bf16[512,384]{1,0:T(8,128)(2,1)S(1)}) custom-call(s32[1]{0:T(128)} %dynamic-slice.9.limit_ref, bf16[1024,1536]{1,0:T(8,128)(2,1)S(1)} %copy-done.2, bf16[1024,1536]{1,0:T(8,128)(2,1)S(1)} %copy-done.2, bf16[1024,1536]{1,0:T(8,128)(2,1)S(1)} %copy-done.2, ...), custom_call_target="tpu_custom_call" | custom-call | flops 18400000000 | bytes 1048576 | tf_op jit(solution)/shard_map/attend_back/pallas_call | solution.py:465
  166.9 0.6 dynamic-slice_convert_fusion
  167.6 0.7 dynamic-slice_bitcast_fusion.4
  169.0 5.0 %begin_back.1 = bf16[8,4,136,128]{3,2,1,0:T(8,128)(2,1)} custom-call(s32[1]{0:T(128)} %dynamic-slice.9.limit_ref, bf16[8,4,136,128]{3,2,1,0:T(8,128)(2,1)S(1)} %bitcast.111, f32[1,512]{1,0:T(1,128)S(1)} %pad_maximum_fusion.3.clock_ref, f32[1,512]{1,0:T(1,128)S(1)} %reshape_squeeze.8.gain_ref, f32[1,512]{1,0:T(1,128)S(1)} %get-tuple-element.76.gg_two_ref, ...), custom_call_target="tpu_custom_call" | custom-call | flops 8049999872 | bytes 1048576 | tf_op jit(solution)/shard_map/begin_back/pallas_call | solution.py:553
  174.0 0.7 collective-permute-done.28
  175.3 0.7 copy-done.9
  176.1 4.5 %all-to-all-start.1 = ((bf16[32,136,128]{2,1,0:T(8,128)(2,1)}), bf16[32,136,128]{2,1,0:T(8,128)(2,1)S(1)}, u32[]{:S(2)}, u32[]{:S(2)}) async-start(bf16[32,136,128]{2,1,0:T(8,128)(2,1)} %bitcast.25), calls=%async_computation.1 | async-start | bytes 2228224 | tf_op jit(solution)/shard_map/all_to_all | solution.py:798
  180.6 0.7 scatter_custom_fusion
  181.2 1.7 fusion.4
  182.9 1.8 collective-permute-start.31
  185.0 1.8 collective-permute-start.29
  186.8 2.1 collective-permute-start.30
  188.9 7.2 %collective-permute-done.31 = bf16[4,64,384]{2,1,0:T(8,128)(2,1)S(1)} collective-permute-done((bf16[4,64,384]{2,1,0:T(8,128)(2,1)}, bf16[4,64,384]{2,1,0:T(8,128)(2,1)S(1)}, u32[]{:S(2)}, u32[]{:S(2)}) %collective-permute-start.31) | collective-permute-done | bytes 196640 | tf_op jit(solution)/shard_map/ppermute | solution.py:591
  196.1 1.0 fusion.3
  197.1 1.2 collective-permute-start.32
  198.4 3.6 %collective-permute-start.33 = (bf16[64,384]{1,0:T(8,128)(2,1)S(1)}, bf16[64,384]{1,0:T(8,128)(2,1)S(1)}, u32[]{:S(2)}, u32[]{:S(2)}) collective-permute-start(bf16[64,384]{1,0:T(8,128)(2,1)S(1)} %get-tuple-element.195), channel_id=1, source_target_pairs={{0,16},{4,20},{8,24},{12,28},{16,0},{20,4},{24,8},{28,12},{1,17},{... | collective-permute-start | bytes 147464 | tf_op jit(solution)/shard_map/ppermute | solution.py:591
  202.5 0.7 add_bitcast_fusion
  203.1 2.3 %collective-permute-done.29 = bf16[64,640]{1,0:T(8,128)(2,1)S(1)} collective-permute-done((bf16[64,640]{1,0:T(8,128)(2,1)}, bf16[64,640]{1,0:T(8,128)(2,1)S(1)}, u32[]{:S(2)}, u32[]{:S(2)}) %collective-permute-start.29) | collective-permute-done | bytes 81952 | tf_op jit(solution)/shard_map/ppermute | solution.py:591
  205.4 2.9 %collective-permute-done.32 = bf16[64,384]{1,0:T(8,128)(2,1)S(1)} collective-permute-done((bf16[64,384]{1,0:T(8,128)(2,1)S(1)}, bf16[64,384]{1,0:T(8,128)(2,1)S(1)}, u32[]{:S(2)}, u32[]{:S(2)}) %collective-permute-start.32) | collective-permute-done | bytes 49184 | tf_op jit(solution)/shard_map/ppermute | solution.py:591
  208.3 7.1 %collective-permute-done.33 = bf16[64,384]{1,0:T(8,128)(2,1)S(1)} collective-permute-done((bf16[64,384]{1,0:T(8,128)(2,1)S(1)}, bf16[64,384]{1,0:T(8,128)(2,1)S(1)}, u32[]{:S(2)}, u32[]{:S(2)}) %collective-permute-start.33) | collective-permute-done | bytes 49184 | tf_op jit(solution)/shard_map/ppermute | solution.py:591
  215.4 0.7 slice.119
  216.7 0.7 copy_bitcast_fusion
  217.4 0.8 gather_fusion.1
  218.2 1.1 slice.117
  (127 shorter events, 9.0 us)
Async XLA Ops:
  0.6 11.8 %copy-start = (bf16[32,128,128]{2,1,0:T(8,128)(2,1)S(1)}, bf16[32,128,128]{2,1,0:T(8,128)(2,1)}, u32[]{:S(2)}) copy-start(bf16[32,128,128]{2,1,0:T(8,128)(2,1)} %param.11) | copy-start | bytes 3145732
  1.6 24.3 %collective-permute-start.6 = (bf16[64,1152]{1,0:T(8,128)(2,1)S(1)}, bf16[64,1152]{1,0:T(8,128)(2,1)S(1)}, u32[]{:S(2)}, u32[]{:S(2)}) collective-permute-start(bf16[64,1152]{1,0:T(8,128)(2,1)S(1)} %pad_maximum_fusion.2), channel_id=1, source_target_pairs={{0,8},{4,12},{8,16},{12,20},{16,24},{20,28},{24,0},{28,4},{1,9},{5... | collective-permute-start | bytes 442376 | tf_op jit(solution)/shard_map/ppermute | solution.py:591
  4.7 22.6 %collective-permute-start.7 = (bf16[64,1152]{1,0:T(8,128)(2,1)S(1)}, bf16[64,1152]{1,0:T(8,128)(2,1)S(1)}, u32[]{:S(2)}, u32[]{:S(2)}) collective-permute-start(bf16[64,1152]{1,0:T(8,128)(2,1)S(1)} %pad_maximum_fusion.2), channel_id=1, source_target_pairs={{0,16},{4,20},{8,24},{12,28},{16,0},{20,4},{24,8},{28,12},{1,17},{... | collective-permute-start | bytes 442376 | tf_op jit(solution)/shard_map/ppermute | solution.py:591
  7.3 20.0 %collective-permute-start.8 = (bf16[64,1152]{1,0:T(8,128)(2,1)S(1)}, bf16[64,1152]{1,0:T(8,128)(2,1)S(1)}, u32[]{:S(2)}, u32[]{:S(2)}) collective-permute-start(bf16[64,1152]{1,0:T(8,128)(2,1)S(1)} %pad_maximum_fusion.2), channel_id=1, source_target_pairs={{0,24},{4,28},{8,0},{12,4},{16,8},{20,12},{24,16},{28,20},{1,25},{... | collective-permute-start | bytes 442376 | tf_op jit(solution)/shard_map/ppermute | solution.py:591
  9.4 12.2 %collective-permute-start = (bf16[64,384]{1,0:T(8,128)(2,1)S(1)}, bf16[64,384]{1,0:T(8,128)(2,1)S(1)}, u32[]{:S(2)}, u32[]{:S(2)}) collective-permute-start(bf16[64,384]{1,0:T(8,128)(2,1)S(1)} %copy_bitcast_fusion.1), channel_id=1, source_target_pairs={{0,4},{4,0},{8,12},{12,8},{16,20},{20,16},{24,28},{28,24},{1,5},{5... | collective-permute-start | bytes 147464 | tf_op jit(solution)/shard_map/ppermute | solution.py:591
  14.4 2.9 %copy-start.12 = (bf16[64,3,128]{2,0,1:T(8,128)(2,1)S(1)}, bf16[64,3,128]{2,0,1:T(8,128)(2,1)}, u32[]{:S(2)}) copy-start(bf16[64,3,128]{2,0,1:T(8,128)(2,1)} %param.15) | copy-start | bytes 147460
  14.4 2.9 %copy-start.19 = (s32[32]{0:T(128)S(1)}, s32[32]{0:T(128)}, u32[]{:S(2)}) copy-start(s32[32]{0:T(128)} %param.14) | copy-start | bytes 388
  14.4 5.4 %copy-start.20 = (s32[32]{0:T(128)S(1)}, s32[32]{0:T(128)}, u32[]{:S(2)}) copy-start(s32[32]{0:T(128)} %param.12) | copy-start | bytes 388
  14.4 6.7 %copy-start.21 = (s32[32]{0:T(128)S(1)}, s32[32]{0:T(128)}, u32[]{:S(2)}) copy-start(s32[32]{0:T(128)} %param.13) | copy-start | bytes 388
  14.4 12.9 %copy-start.10 = (bf16[512,64]{0,1:T(8,128)(2,1)S(1)}, bf16[512,64]{0,1:T(8,128)(2,1)}, u32[]{:S(2)}) copy-start(bf16[512,64]{0,1:T(8,128)(2,1)} %param.18) | copy-start | bytes 196612
  14.4 12.9 %copy-start.11 = (bf16[64,512]{1,0:T(8,128)(2,1)S(1)}, bf16[64,512]{1,0:T(8,128)(2,1)}, u32[]{:S(2)}) copy-start(bf16[64,512]{1,0:T(8,128)(2,1)} %param.17) | copy-start | bytes 196612
  14.4 12.9 %copy-start.15 = (bf16[128,64]{0,1:T(8,128)(2,1)S(1)}, bf16[128,64]{0,1:T(8,128)(2,1)}, u32[]{:S(2)}) copy-start(bf16[128,64]{0,1:T(8,128)(2,1)} %param.16) | copy-start | bytes 49156
  14.4 49.4 %all-to-all-start = ((bf16[32,136,128]{2,1,0:T(8,128)(2,1)}), bf16[32,136,128]{2,1,0:T(8,128)(2,1)S(1)}, u32[]{:S(2)}, u32[]{:S(2)}) async-start(bf16[32,136,128]{2,1,0:T(8,128)(2,1)} %pad_maximum_fusion), calls=%async_computation | async-start | bytes 2228224 | tf_op jit(solution)/shard_map/all_to_all | solution.py:732
  21.7 20.7 %collective-permute-start.1 = (bf16[64,768]{1,0:T(8,128)(2,1)S(1)}, bf16[64,768]{1,0:T(8,128)(2,1)S(1)}, u32[]{:S(2)}, u32[]{:S(2)}) collective-permute-start(bf16[64,768]{1,0:T(8,128)(2,1)S(1)} %constant_dynamic-update-slice_fusion), channel_id=1, source_target_pairs={{0,8},{4,12},{8,16},{12,20},{16,24},{20,28},{24,0},{28,4},{1,9},{5... | collective-permute-start | bytes 294920 | tf_op jit(solution)/shard_map/ppermute | solution.py:591
  23.4 28.2 %collective-permute-start.2 = (bf16[64,768]{1,0:T(8,128)(2,1)S(1)}, bf16[64,768]{1,0:T(8,128)(2,1)S(1)}, u32[]{:S(2)}, u32[]{:S(2)}) collective-permute-start(bf16[64,768]{1,0:T(8,128)(2,1)S(1)} %constant_dynamic-update-slice_fusion), channel_id=1, source_target_pairs={{0,16},{4,20},{8,24},{12,28},{16,0},{20,4},{24,8},{28,12},{1,17},{... | collective-permute-start | bytes 294920 | tf_op jit(solution)/shard_map/ppermute | solution.py:591
  25.9 25.7 %collective-permute-start.3 = (bf16[64,768]{1,0:T(8,128)(2,1)S(1)}, bf16[64,768]{1,0:T(8,128)(2,1)S(1)}, u32[]{:S(2)}, u32[]{:S(2)}) collective-permute-start(bf16[64,768]{1,0:T(8,128)(2,1)S(1)} %constant_dynamic-update-slice_fusion), channel_id=1, source_target_pairs={{0,24},{4,28},{8,0},{12,4},{16,8},{20,12},{24,16},{28,20},{1,25},{... | collective-permute-start | bytes 294920 | tf_op jit(solution)/shard_map/ppermute | solution.py:591
  28.2 33.8 %collective-permute-start.10 = (bf16[256,1152]{1,0:T(8,128)(2,1)}, bf16[256,1152]{1,0:T(8,128)(2,1)S(1)}, u32[]{:S(2)}, u32[]{:S(2)}) collective-permute-start(bf16[256,1152]{1,0:T(8,128)(2,1)} %pad_maximum_fusion.1.refs_0_), channel_id=1, source_target_pairs={{0,2},{1,3},{2,0},{3,1},{4,6},{5,7},{6,4},{7,5},{8,10},{9,11},{10,... | collective-permute-start | bytes 1769480 | tf_op jit(solution)/shard_map/ppermute | solution.py:586
  29.7 32.3 %collective-permute-start.9 = (bf16[256,1152]{1,0:T(8,128)(2,1)}, bf16[256,1152]{1,0:T(8,128)(2,1)}, u32[]{:S(2)}, u32[]{:S(2)}) collective-permute-start(bf16[256,1152]{1,0:T(8,128)(2,1)} %pad_maximum_fusion.1.refs_0_), channel_id=1, source_target_pairs={{0,4},{4,0},{8,12},{12,8},{16,20},{20,16},{24,28},{28,24},{1,5},{5... | collective-permute-start | bytes 1769480 | tf_op jit(solution)/shard_map/ppermute | solution.py:591
  51.7 10.3 %collective-permute-start.5 = (bf16[512,384]{1,0:T(8,128)(2,1)S(1)}, bf16[512,384]{1,0:T(8,128)(2,1)S(1)}, u32[]{:S(2)}, u32[]{:S(2)}) collective-permute-start(bf16[512,384]{1,0:T(8,128)(2,1)S(1)} %slice_dynamic-update-slice_fusion.refs_0_), channel_id=1, source_target_pairs={{0,2},{1,3},{2,0},{3,1},{4,6},{5,7},{6,4},{7,5},{8,10},{9,11},{10,... | collective-permute-start | bytes 1179656 | tf_op jit(solution)/shard_map/ppermute | solution.py:586
  53.5 10.6 %collective-permute-start.4 = (bf16[512,384]{1,0:T(8,128)(2,1)S(1)}, bf16[512,384]{1,0:T(8,128)(2,1)S(1)}, u32[]{:S(2)}, u32[]{:S(2)}) collective-permute-start(bf16[512,384]{1,0:T(8,128)(2,1)S(1)} %slice_dynamic-update-slice_fusion.refs_0_), channel_id=1, source_target_pairs={{0,1},{1,0},{2,3},{3,2},{4,5},{5,4},{6,7},{7,6},{8,9},{9,8},{10,11... | collective-permute-start | bytes 1179656 | tf_op jit(solution)/shard_map/ppermute | solution.py:586
  53.6 33.6 %collective-permute-start.12 = (bf16[256,1152]{1,0:T(8,128)(2,1)}, bf16[256,1152]{1,0:T(8,128)(2,1)}, u32[]{:S(2)}, u32[]{:S(2)}) collective-permute-start(bf16[256,1152]{1,0:T(8,128)(2,1)} %pad_maximum_fusion.1.refs_0_), channel_id=1, source_target_pairs={{0,1},{1,0},{2,3},{3,2},{4,5},{5,4},{6,7},{7,6},{8,9},{9,8},{10,11... | collective-permute-start | bytes 1769480 | tf_op jit(solution)/shard_map/ppermute | solution.py:586
  62.0 1.7 copy-start.16
  62.0 25.2 %collective-permute-start.13 = (bf16[256,1152]{1,0:T(8,128)(2,1)}, bf16[256,1152]{1,0:T(8,128)(2,1)}, u32[]{:S(2)}, u32[]{:S(2)}) collective-permute-start(bf16[256,1152]{1,0:T(8,128)(2,1)} %collective-permute-done.9.refs_1_), channel_id=1, source_target_pairs={{0,1},{1,0},{2,3},{3,2},{4,5},{5,4},{6,7},{7,6},{8,9},{9,8},{10,11... | collective-permute-start | bytes 1769480 | tf_op jit(solution)/shard_map/ppermute | solution.py:586
  62.1 25.1 %collective-permute-start.15 = (bf16[256,1152]{1,0:T(8,128)(2,1)}, bf16[256,1152]{1,0:T(8,128)(2,1)}, u32[]{:S(2)}, u32[]{:S(2)}) collective-permute-start(bf16[256,1152]{1,0:T(8,128)(2,1)} %collective-permute-done.9.refs_1_), channel_id=1, source_target_pairs={{0,2},{1,3},{2,0},{3,1},{4,6},{5,7},{6,4},{7,5},{8,10},{9,11},{10,... | collective-permute-start | bytes 1769480 | tf_op jit(solution)/shard_map/ppermute | solution.py:586
  63.7 1.9 collective-permute-start.11
  64.2 23.1 %collective-permute-start.14 = (bf16[256,1152]{1,0:T(8,128)(2,1)}, bf16[256,1152]{1,0:T(8,128)(2,1)S(1)}, u32[]{:S(2)}, u32[]{:S(2)}) collective-permute-start(bf16[256,1152]{1,0:T(8,128)(2,1)} %copy-done.16), channel_id=1, source_target_pairs={{0,1},{1,0},{2,3},{3,2},{4,5},{5,4},{6,7},{7,6},{8,9},{9,8},{10,11... | collective-permute-start | bytes 1769480 | tf_op jit(solution)/shard_map/ppermute | solution.py:586
  71.8 15.4 %copy-start.1 = (bf16[1024,1536]{1,0:T(8,128)(2,1)}, bf16[1024,1536]{1,0:T(8,128)(2,1)S(1)}, u32[]{:S(2)}) copy-start(bf16[1024,1536]{1,0:T(8,128)(2,1)S(1)} %get-tuple-element.66.q_ref.k_ref.v_ref) | copy-start | bytes 9437188
  87.2 0.8 copy-start.17
  87.2 2.3 %collective-permute-start.16 = (bf16[256,1152]{1,0:T(8,128)(2,1)}, bf16[256,1152]{1,0:T(8,128)(2,1)S(1)}, u32[]{:S(2)}, u32[]{:S(2)}) collective-permute-start(bf16[256,1152]{1,0:T(8,128)(2,1)} %collective-permute-done.15.refs_5_), channel_id=1, source_target_pairs={{0,1},{1,0},{2,3},{3,2},{4,5},{5,4},{6,7},{7,6},{8,9},{9,8},{10,11... | collective-permute-start | bytes 1769480 | tf_op jit(solution)/shard_map/ppermute | solution.py:586
  89.5 0.8 copy-start.18
  119.4 3.7 %collective-permute-start.18 = (bf16[2,512,512]{2,1,0:T(8,128)(2,1)}, bf16[2,512,512]{2,1,0:T(8,128)(2,1)S(1)}, u32[]{:S(2)}, u32[]{:S(2)}) collective-permute-start(bf16[2,512,512]{2,1,0:T(8,128)(2,1)} %get-tuple-element.84), channel_id=1, source_target_pairs={{0,1},{1,0},{2,3},{3,2},{4,5},{5,4},{6,7},{7,6},{8,9},{9,8},{10,11... | collective-permute-start | bytes 3145736 | tf_op jit(solution)/shard_map/ppermute | solution.py:586
  119.4 5.3 %collective-permute-start.17 = (bf16[2,512,640]{2,1,0:T(8,128)(2,1)}, bf16[2,512,640]{2,1,0:T(8,128)(2,1)}, u32[]{:S(2)}, u32[]{:S(2)}) collective-permute-start(bf16[2,512,640]{2,1,0:T(8,128)(2,1)} %get-tuple-element.79), channel_id=1, source_target_pairs={{0,1},{1,0},{2,3},{3,2},{4,5},{5,4},{6,7},{7,6},{8,9},{9,8},{10,11... | collective-permute-start | bytes 3932168 | tf_op jit(solution)/shard_map/ppermute | solution.py:586
  123.0 4.8 %copy-start.2 = (bf16[1024,1536]{1,0:T(8,128)(2,1)S(1)}, bf16[1024,1536]{1,0:T(8,128)(2,1)}, u32[]{:S(2)}) copy-start(bf16[1024,1536]{1,0:T(8,128)(2,1)} %copy-done.1) | copy-start | bytes 9437188
  123.0 4.8 %copy-start.6 = (bf16[512,1024]{1,0:T(8,128)(2,1)S(1)}, bf16[512,1024]{1,0:T(8,128)(2,1)}, u32[]{:S(2)}) copy-start(bf16[512,1024]{1,0:T(8,128)(2,1)} %get-tuple-element.80.turn_ref) | copy-start | bytes 3145732
  124.6 3.2 %copy-start.5 = (bf16[512,1024]{1,0:T(8,128)(2,1)S(1)}, bf16[512,1024]{1,0:T(8,128)(2,1)}, u32[]{:S(2)}) copy-start(bf16[512,1024]{1,0:T(8,128)(2,1)} %get-tuple-element.86.n_turn_ref) | copy-start | bytes 3145732
  124.6 18.1 %collective-permute-start.19 = (bf16[4,2,64,512]{3,2,1,0:T(8,128)(2,1)S(1)}, bf16[4,2,64,512]{3,2,1,0:T(8,128)(2,1)S(1)}, u32[]{:S(2)}, u32[]{:S(2)}) collective-permute-start(bf16[4,2,64,512]{3,2,1,0:T(8,128)(2,1)S(1)} %bitcast.117), channel_id=1, source_target_pairs={{0,2},{1,3},{2,0},{3,1},{4,6},{5,7},{6,4},{7,5},{8,10},{9,11},{10,... | collective-permute-start | bytes 1572872 | tf_op jit(solution)/shard_map/ppermute | solution.py:586
  126.3 16.8 %collective-permute-start.20 = (bf16[2,4,64,640]{3,2,1,0:T(8,128)(2,1)S(1)}, bf16[2,4,64,640]{3,2,1,0:T(8,128)(2,1)S(1)}, u32[]{:S(2)}, u32[]{:S(2)}) collective-permute-start(bf16[2,4,64,640]{3,2,1,0:T(8,128)(2,1)S(1)} %fusion.1), channel_id=1, source_target_pairs={{0,4},{4,0},{8,12},{12,8},{16,20},{20,16},{24,28},{28,24},{1,5},{5... | collective-permute-start | bytes 1966088 | tf_op jit(solution)/shard_map/ppermute | solution.py:591
  127.8 15.3 %copy-start.8 = (bf16[2,512,640]{2,1,0:T(8,128)(2,1)S(1)}, bf16[2,512,640]{2,1,0:T(8,128)(2,1)}, u32[]{:S(2)}) copy-start(bf16[2,512,640]{2,1,0:T(8,128)(2,1)} %get-tuple-element.78) | copy-start | bytes 3932164
  143.1 8.5 %collective-permute-start.21 = (bf16[512,384]{1,0:T(8,128)(2,1)S(1)}, bf16[512,384]{1,0:T(8,128)(2,1)S(1)}, u32[]{:S(2)}, u32[]{:S(2)}) collective-permute-start(bf16[512,384]{1,0:T(8,128)(2,1)S(1)} %get-tuple-element.95), channel_id=1, source_target_pairs={{0,1},{1,0},{2,3},{3,2},{4,5},{5,4},{6,7},{7,6},{8,9},{9,8},{10,11... | collective-permute-start | bytes 1179656 | tf_op jit(solution)/shard_map/ppermute | solution.py:586
  144.5 22.3 %collective-permute-start.22 = (bf16[4,64,640]{2,1,0:T(8,128)(2,1)S(1)}, bf16[4,64,640]{2,1,0:T(8,128)(2,1)S(1)}, u32[]{:S(2)}, u32[]{:S(2)}) collective-permute-start(bf16[4,64,640]{2,1,0:T(8,128)(2,1)S(1)} %slice_bitcast_fusion), channel_id=1, source_target_pairs={{0,2},{1,3},{2,0},{3,1},{4,6},{5,7},{6,4},{7,5},{8,10},{9,11},{10,... | collective-permute-start | bytes 983048 | tf_op jit(solution)/shard_map/ppermute | solution.py:586
  146.4 6.1 %copy-start.7 = (bf16[1024,512]{1,0:T(8,128)(2,1)S(1)}, bf16[1024,512]{1,0:T(8,128)(2,1)}, u32[]{:S(2)}) copy-start(bf16[1024,512]{1,0:T(8,128)(2,1)} %get-tuple-element.96.cg_ref) | copy-start | bytes 3145732
  146.4 20.3 %collective-permute-start.24 = (bf16[2,64,512]{2,1,0:T(8,128)(2,1)S(1)}, bf16[2,64,512]{2,1,0:T(8,128)(2,1)S(1)}, u32[]{:S(2)}, u32[]{:S(2)}) collective-permute-start(bf16[2,64,512]{2,1,0:T(8,128)(2,1)S(1)} %get-tuple-element.188), channel_id=1, source_target_pairs={{0,8},{4,12},{8,16},{12,20},{16,24},{20,28},{24,0},{28,4},{1,9},{5... | collective-permute-start | bytes 393224 | tf_op jit(solution)/shard_map/ppermute | solution.py:591
  149.2 17.6 %collective-permute-start.25 = (bf16[2,64,512]{2,1,0:T(8,128)(2,1)S(1)}, bf16[2,64,512]{2,1,0:T(8,128)(2,1)S(1)}, u32[]{:S(2)}, u32[]{:S(2)}) collective-permute-start(bf16[2,64,512]{2,1,0:T(8,128)(2,1)S(1)} %get-tuple-element.187), channel_id=1, source_target_pairs={{0,16},{4,20},{8,24},{12,28},{16,0},{20,4},{24,8},{28,12},{1,17},{... | collective-permute-start | bytes 393224 | tf_op jit(solution)/shard_map/ppermute | solution.py:591
  150.7 16.1 %collective-permute-start.26 = (bf16[2,64,512]{2,1,0:T(8,128)(2,1)S(1)}, bf16[2,64,512]{2,1,0:T(8,128)(2,1)S(1)}, u32[]{:S(2)}, u32[]{:S(2)}) collective-permute-start(bf16[2,64,512]{2,1,0:T(8,128)(2,1)S(1)} %get-tuple-element.186), channel_id=1, source_target_pairs={{0,24},{4,28},{8,0},{12,4},{16,8},{20,12},{24,16},{28,20},{1,25},{... | collective-permute-start | bytes 393224 | tf_op jit(solution)/shard_map/ppermute | solution.py:591
  151.7 15.1 %collective-permute-start.23 = (bf16[512,384]{1,0:T(8,128)(2,1)S(1)}, bf16[512,384]{1,0:T(8,128)(2,1)S(1)}, u32[]{:S(2)}, u32[]{:S(2)}) collective-permute-start(bf16[512,384]{1,0:T(8,128)(2,1)S(1)} %add_convert_fusion.3), channel_id=1, source_target_pairs={{0,2},{1,3},{2,0},{3,1},{4,6},{5,7},{6,4},{7,5},{8,10},{9,11},{10,... | collective-permute-start | bytes 1179656 | tf_op jit(solution)/shard_map/ppermute | solution.py:586
  152.5 16.5 %copy-start.4 = (bf16[512,1536]{1,0:T(8,128)(2,1)S(1)}, bf16[512,1536]{1,0:T(8,128)(2,1)}, u32[]{:S(2)}) copy-start(bf16[512,1536]{1,0:T(8,128)(2,1)} %get-tuple-element.106.w_ref) | copy-start | bytes 4718596
  166.8 2.2 copy-start.3
  168.3 6.4 %collective-permute-start.28 = (bf16[64,640]{1,0:T(8,128)(2,1)S(1)}, bf16[64,640]{1,0:T(8,128)(2,1)S(1)}, u32[]{:S(2)}, u32[]{:S(2)}) collective-permute-start(bf16[64,640]{1,0:T(8,128)(2,1)S(1)} %get-tuple-element.193), channel_id=1, source_target_pairs={{0,16},{4,20},{8,24},{12,28},{16,0},{20,4},{24,8},{28,12},{1,17},{... | collective-permute-start | bytes 245768 | tf_op jit(solution)/shard_map/ppermute | solution.py:591
  169.0 5.7 %collective-permute-start.27 = (bf16[512,384]{1,0:T(8,128)(2,1)S(1)}, bf16[512,384]{1,0:T(8,128)(2,1)S(1)}, u32[]{:S(2)}, u32[]{:S(2)}) collective-permute-start(bf16[512,384]{1,0:T(8,128)(2,1)S(1)} %get-tuple-element.108), channel_id=1, source_target_pairs={{0,1},{1,0},{2,3},{3,2},{4,5},{5,4},{6,7},{7,6},{8,9},{9,8},{10,11... | collective-permute-start | bytes 1179656 | tf_op jit(solution)/shard_map/ppermute | solution.py:586
  174.7 0.6 copy-start.13
  175.3 0.7 copy-start.9
  176.1 41.3 %all-to-all-start.1 = ((bf16[32,136,128]{2,1,0:T(8,128)(2,1)}), bf16[32,136,128]{2,1,0:T(8,128)(2,1)S(1)}, u32[]{:S(2)}, u32[]{:S(2)}) async-start(bf16[32,136,128]{2,1,0:T(8,128)(2,1)} %bitcast.25), calls=%async_computation.1 | async-start | bytes 2228224 | tf_op jit(solution)/shard_map/all_to_all | solution.py:798
  182.9 13.1 %collective-permute-start.31 = (bf16[4,64,384]{2,1,0:T(8,128)(2,1)}, bf16[4,64,384]{2,1,0:T(8,128)(2,1)S(1)}, u32[]{:S(2)}, u32[]{:S(2)}) collective-permute-start(bf16[4,64,384]{2,1,0:T(8,128)(2,1)} %fusion.4), channel_id=1, source_target_pairs={{0,4},{4,0},{8,12},{12,8},{16,20},{20,16},{24,28},{28,24},{1,5},{5... | collective-permute-start | bytes 589832 | tf_op jit(solution)/shard_map/ppermute | solution.py:591
  184.7 30.7 %copy-start.14 = (bf16[64,640]{1,0:T(8,128)(2,1)S(1)}, bf16[64,640]{1,0:T(8,128)(2,1)}, u32[]{:S(2)}) copy-start(bf16[64,640]{1,0:T(8,128)(2,1)} %copy-done.13) | copy-start | bytes 245764
  184.7 17.2 %collective-permute-start.35 = (bf16[1,64,512]{2,1,0:T(8,128)(2,1)}, bf16[1,64,512]{2,1,0:T(8,128)(2,1)S(1)}, u32[]{:S(2)}, u32[]{:S(2)}) collective-permute-start(bf16[1,64,512]{2,1,0:T(8,128)(2,1)} %dynamic-slice_convert_fusion), channel_id=1, source_target_pairs={{0,4},{4,0},{8,12},{12,8},{16,20},{20,16},{24,28},{28,24},{1,5},{5... | collective-permute-start | bytes 196616 | tf_op jit(solution)/shard_map/ppermute | solution.py:591
  185.0 20.4 %collective-permute-start.29 = (bf16[64,640]{1,0:T(8,128)(2,1)}, bf16[64,640]{1,0:T(8,128)(2,1)S(1)}, u32[]{:S(2)}, u32[]{:S(2)}) collective-permute-start(bf16[64,640]{1,0:T(8,128)(2,1)} %get-tuple-element.191), channel_id=1, source_target_pairs={{0,8},{4,12},{8,16},{12,20},{16,24},{20,28},{24,0},{28,4},{1,9},{5... | collective-permute-start | bytes 245768 | tf_op jit(solution)/shard_map/ppermute | solution.py:591
  186.8 18.6 %collective-permute-start.30 = (bf16[64,640]{1,0:T(8,128)(2,1)}, bf16[64,640]{1,0:T(8,128)(2,1)S(1)}, u32[]{:S(2)}, u32[]{:S(2)}) collective-permute-start(bf16[64,640]{1,0:T(8,128)(2,1)} %get-tuple-element.190), channel_id=1, source_target_pairs={{0,24},{4,28},{8,0},{12,4},{16,8},{20,12},{24,16},{28,20},{1,25},{... | collective-permute-start | bytes 245768 | tf_op jit(solution)/shard_map/ppermute | solution.py:591
  197.1 11.2 %collective-permute-start.32 = (bf16[64,384]{1,0:T(8,128)(2,1)S(1)}, bf16[64,384]{1,0:T(8,128)(2,1)S(1)}, u32[]{:S(2)}, u32[]{:S(2)}) collective-permute-start(bf16[64,384]{1,0:T(8,128)(2,1)S(1)} %get-tuple-element.196), channel_id=1, source_target_pairs={{0,8},{4,12},{8,16},{12,20},{16,24},{20,28},{24,0},{28,4},{1,9},{5... | collective-permute-start | bytes 147464 | tf_op jit(solution)/shard_map/ppermute | solution.py:591
  198.4 17.0 %collective-permute-start.33 = (bf16[64,384]{1,0:T(8,128)(2,1)S(1)}, bf16[64,384]{1,0:T(8,128)(2,1)S(1)}, u32[]{:S(2)}, u32[]{:S(2)}) collective-permute-start(bf16[64,384]{1,0:T(8,128)(2,1)S(1)} %get-tuple-element.195), channel_id=1, source_target_pairs={{0,16},{4,20},{8,24},{12,28},{16,0},{20,4},{24,8},{28,12},{1,17},{... | collective-permute-start | bytes 147464 | tf_op jit(solution)/shard_map/ppermute | solution.py:591
  201.9 13.4 %collective-permute-start.34 = (bf16[64,384]{1,0:T(8,128)(2,1)S(1)}, bf16[64,384]{1,0:T(8,128)(2,1)S(1)}, u32[]{:S(2)}, u32[]{:S(2)}) collective-permute-start(bf16[64,384]{1,0:T(8,128)(2,1)S(1)} %get-tuple-element.194), channel_id=1, source_target_pairs={{0,24},{4,28},{8,0},{12,4},{16,8},{20,12},{24,16},{28,20},{1,25},{... | collective-permute-start | bytes 147464 | tf_op jit(solution)/shard_map/ppermute | solution.py:591

commit v12 on v11

--- a/solution.py
+++ b/solution.py
@@ -710,7 +710,8 @@
     if direct:
         place, groups = places(), dp_count
         wide = qkv.shape[1]
-        pieces = collect_coarse(jnp.concatenate([qkv, across(qkv)], axis=1))
+        pair = jnp.concatenate([qkv, across(qkv)], axis=1)
+        pieces = collect_coarse(pair)
         qkv_rows = jnp.concatenate(
             [piece[:, :wide] for piece in pieces] + [piece[:, wide:] for piece in pieces], axis=0
         )
@@ -729,6 +730,8 @@
     arranged = jnp.concatenate(
         [states[deal_order], jnp.broadcast_to(spare[None], (devices, SPARE, width))], axis=1
     )
+    if direct:
+        arranged = after(arranged, pair)
     x_blocks = lax.all_to_all(arranged, both, 0, 0, tiled=True)
     gains = jnp.sum(x_blocks[:, tokens, : 6 * per].reshape(devices, 2, 3, per).astype(F32), axis=2)
     gain_one = gains[:, 0].reshape(1, features)

time: 220 us -> 222 us (level)
  starting transfers between devices: 50.6 us -> 54.5 us
  waiting for transfers between devices: 54.2 us -> 50.8 us
    ppermute x20, waiting for transfers between devices: 41 us -> 32.8 us  [along_dp(): return lax.ppermute(value, 'dp', [(i, move(i)) for i in range(count)])]
    ppermute x16, waiting for transfers between devices: 13.3 us -> 18 us  [swap(): return lax.ppermute(value, 'tensor', [(i, i ^ apart) for i in range(count)])]
    ppermute x20, starting transfers between devices: 34.3 us -> 37.6 us  [along_dp(): return lax.ppermute(value, 'dp', [(i, move(i)) for i in range(count)])]
  transfers between devices with their start and end apart: 38 -> 38, of which waited for: 12 -> 9; matrix products, arithmetic and copies ran while one was open for 8% -> 9% of each run, Pallas kernels for 25% -> 25%
where the time goes in v12:
time: 222 us; the launch traced here: 221 us
  Pallas kernels  84.8 us (38%)
  starting transfers between devices  54.5 us (25%)
  waiting for transfers between devices  50.8 us (23%)
  local copies, waits for them, and re-layouts  14.8 us (7%)
  other arithmetic  12.6 us (6%)
  between operations  3.77 us (2%)
    ppermute x20, starting transfers between devices, along_dp(): return lax.ppermute(value, 'dp', [(i, move(i)) for i in range(count)])  37.6 us
    ppermute x20, waiting for transfers between devices, along_dp(): return lax.ppermute(value, 'dp', [(i, move(i)) for i in range(count)])  32.8 us
    pallas_call x2, Pallas kernels, attend_back(): pl.pallas_call(attend_back_kernel, grid_spec=pltpu.PrefetchScalarGridSpec...  29.1 us
    pallas_call x1, Pallas kernels, middle_block(): pl.pallas_call(functools.partial(middle_kernel, groups), grid_spec=pltpu....  29.1 us
    ppermute x16, waiting for transfers between devices, swap(): return lax.ppermute(value, 'tensor', [(i, i ^ apart) for i in range(count)])  18 us
    pallas_call x1, Pallas kernels, attend(): pl.pallas_call(attend_kernel, grid_spec=pltpu.PrefetchScalarGridSpec(num_...  15.3 us
    ppermute x16, starting transfers between devices, swap(): return lax.ppermute(value, 'tensor', [(i, i ^ apart) for i in range(count)])  7.78 us
    pallas_call x1, Pallas kernels, project(): pl.pallas_call(functools.partial(project_kernel, groups), grid_spec=pltpu...  6.24 us
  transfers between devices with their start and end apart: 38, of which 9 were waited for; matrix products, arithmetic and copies ran while one was open for 9% of the time, Pallas kernels for 25%

profile of v12, /device:TPU:0, one launch (start us, length us, event | category | flops | bytes accessed | tf_op | source)
XLA Modules:
  0.0 221.2 jit_solution(11156026482905616071)
XLA Ops:
  0.6 1.0 pad_maximum_fusion.2
  1.6 3.1 %collective-permute-start.6 = (bf16[64,1152]{1,0:T(8,128)(2,1)S(1)}, bf16[64,1152]{1,0:T(8,128)(2,1)S(1)}, u32[]{:S(2)}, u32[]{:S(2)}) collective-permute-start(bf16[64,1152]{1,0:T(8,128)(2,1)S(1)} %pad_maximum_fusion.2), channel_id=1, source_target_pairs={{0,8},{4,12},{8,16},{12,20},{16,24},{20,28},{24,0},{28,4},{1,9},{5... | collective-permute-start | bytes 442376 | tf_op jit(solution)/shard_map/ppermute | solution.py:591
  4.7 2.6 %collective-permute-start.7 = (bf16[64,1152]{1,0:T(8,128)(2,1)S(1)}, bf16[64,1152]{1,0:T(8,128)(2,1)S(1)}, u32[]{:S(2)}, u32[]{:S(2)}) collective-permute-start(bf16[64,1152]{1,0:T(8,128)(2,1)S(1)} %pad_maximum_fusion.2), channel_id=1, source_target_pairs={{0,16},{4,20},{8,24},{12,28},{16,0},{20,4},{24,8},{28,12},{1,17},{... | collective-permute-start | bytes 442376 | tf_op jit(solution)/shard_map/ppermute | solution.py:591
  7.3 1.3 collective-permute-start.8
  8.6 0.8 copy_bitcast_fusion.1
  9.4 1.5 collective-permute-start
  11.0 1.4 constant_dynamic-update-slice_fusion.3
  12.4 0.7 fusion.9
  13.2 0.7 compare_select_fusion.1
  13.9 0.7 gather_fusion
  14.7 1.1 pad_maximum_fusion
  19.6 0.6 dynamic-slice.9.limit_ref
  20.2 0.6 constant_dynamic-update-slice_fusion
  20.9 0.7 collective-permute-start.1
  21.9 4.7 %all-to-all-start = ((bf16[32,136,128]{2,1,0:T(8,128)(2,1)}), bf16[32,136,128]{2,1,0:T(8,128)(2,1)S(1)}, u32[]{:S(2)}, u32[]{:S(2)}) async-start(bf16[32,136,128]{2,1,0:T(8,128)(2,1)} %pad_maximum_fusion), calls=%async_computation | async-start | bytes 2228224 | tf_op jit(solution)/shard_map/all_to_all | solution.py:735
  26.6 3.7 %collective-permute-start.3 = (bf16[64,768]{1,0:T(8,128)(2,1)}, bf16[64,768]{1,0:T(8,128)(2,1)S(1)}, u32[]{:S(2)}, u32[]{:S(2)}) collective-permute-start(bf16[64,768]{1,0:T(8,128)(2,1)} %constant_dynamic-update-slice_fusion), channel_id=1, source_target_pairs={{0,24},{4,28},{8,0},{12,4},{16,8},{20,12},{24,16},{28,20},{1,25},{... | collective-permute-start | bytes 294920 | tf_op jit(solution)/shard_map/ppermute | solution.py:591
  30.3 0.9 pad_maximum_fusion.1.refs_0_
  31.1 1.5 collective-permute-start.10
  32.6 1.5 collective-permute-start.9
  34.1 13.3 %collective-permute-done.3 = bf16[64,768]{1,0:T(8,128)(2,1)S(1)} collective-permute-done((bf16[64,768]{1,0:T(8,128)(2,1)}, bf16[64,768]{1,0:T(8,128)(2,1)S(1)}, u32[]{:S(2)}, u32[]{:S(2)}) %collective-permute-start.3) | collective-permute-done | bytes 98336 | tf_op jit(solution)/shard_map/ppermute | solution.py:591
  47.5 1.7 collective-permute-start.5
  50.0 13.0 %collective-permute-done.5.refs_2_ = bf16[512,384]{1,0:T(8,128)(2,1)S(1)} collective-permute-done((bf16[512,384]{1,0:T(8,128)(2,1)S(1)}, bf16[512,384]{1,0:T(8,128)(2,1)S(1)}, u32[]{:S(2)}, u32[]{:S(2)}) %collective-permute-start.5) | collective-permute-done | bytes 393248 | tf_op jit(solution)/shard_map/ppermute | solution.py:586
  63.1 0.7 collective-permute-start.15
  64.8 1.1 collective-permute-done.11.refs_3_
  65.8 6.2 %project.1 = (bf16[1024,1536]{1,0:T(8,128)(2,1)S(1)}, bf16[512,1024]{1,0:T(8,128)(2,1)}, bf16[512,1536]{1,0:T(8,128)(2,1)}) custom-call(s32[1]{0:T(128)} %dynamic-slice.9.limit_ref, s32[8]{0:T(128)S(1)} %pad_add_fusion.place_ref, bf16[8,4,136,128]{3,2,1,0:T(8,128)(2,1)S(1)} %bitcast.109, f32[1,512]{1,0:T(1,128)S(1)} %pad_maximum_fusion.3.clock_ref, ...), custom_call_target="tpu_custom_call" | custom-call | flops 5750000128 | bytes 1048576 | tf_op jit(solution)/shard_map/project/pallas_call | solution.py:110
  72.1 15.3 %attend.1 = (bf16[1024,512]{1,0:T(8,128)(2,1)}, bf16[512,1024]{1,0:T(8,128)(2,1)}, f32[4,2,1024]{2,1,0:T(2,128)S(1)}) custom-call(s32[1]{0:T(128)} %dynamic-slice.9.limit_ref, bf16[1024,1536]{1,0:T(8,128)(2,1)S(1)} %get-tuple-element.68.q_ref.k_ref.v_ref, bf16[1024,1536]{1,0:T(8,128)(2,1)S(1)} %get-tuple-element.68.q_ref.k_ref.v_ref, ...), custom_call_target="tpu_custom_call" | custom-call | flops 17250000896 | bytes 1048576 | tf_op jit(solution)/shard_map/attend/pallas_call | solution.py:199
  87.7 0.6 copy-done.16
  88.4 1.3 collective-permute-done.16.refs_7_
  89.7 0.8 copy-done.17
  90.5 29.1 %middle.1 = (bf16[1,1024,512]{2,1,0:T(8,128)(2,1)}, bf16[1024,512]{1,0:T(8,128)(2,1)}, f32[1024,512]{1,0:T(8,128)}, f32[1,512]{1,0:T(1,128)S(1)}, bf16[2,512,640...) custom-call(s32[1]{0:T(128)} %dynamic-slice.9.limit_ref, ...), custom_call_target="tpu_custom_call" | custom-call | flops 28750000128 | bytes 1048576 | tf_op jit(solution)/shard_map/middle/pallas_call | solution.py:370
  120.2 2.6 %collective-permute-done.18 = bf16[2,512,512]{2,1,0:T(8,128)(2,1)} collective-permute-done((bf16[2,512,512]{2,1,0:T(8,128)(2,1)}, bf16[2,512,512]{2,1,0:T(8,128)(2,1)}, u32[]{:S(2)}, u32[]{:S(2)}) %collective-permute-start.18) | collective-permute-done | bytes 1048608 | tf_op jit(solution)/shard_map/ppermute | solution.py:586
  122.8 2.0 convert_add_fusion
  124.8 1.3 fusion.1
  126.2 2.7 %collective-permute-start.20 = (bf16[2,4,64,640]{3,2,1,0:T(8,128)(2,1)S(1)}, bf16[2,4,64,640]{3,2,1,0:T(8,128)(2,1)S(1)}, u32[]{:S(2)}, u32[]{:S(2)}) collective-permute-start(bf16[2,4,64,640]{3,2,1,0:T(8,128)(2,1)S(1)} %fusion.1), channel_id=1, source_target_pairs={{0,4},{4,0},{8,12},{12,8},{16,20},{20,16},{24,28},{28,24},{1,5},{5... | collective-permute-start | bytes 1966088 | tf_op jit(solution)/shard_map/ppermute | solution.py:591
  128.8 14.9 %attend_back.2 = (bf16[1024,768]{1,0:T(8,128)(2,1)S(1)}, bf16[512,384]{1,0:T(8,128)(2,1)S(1)}, bf16[512,384]{1,0:T(8,128)(2,1)S(1)}) custom-call(s32[1]{0:T(128)} %dynamic-slice.9.limit_ref, bf16[1024,1536]{1,0:T(8,128)(2,1)S(1)} %copy-done.2, bf16[1024,1536]{1,0:T(8,128)(2,1)S(1)} %copy-done.2, bf16[1024,1536]{1,0:T(8,128)(2,1)S(1)} %copy-done.2, ...), custom_call_target="tpu_custom_call" | custom-call | flops 18400000000 | bytes 1048576 | tf_op jit(solution)/shard_map/attend_back/pallas_call | solution.py:465
  144.2 0.9 collective-permute-start.22
  145.3 6.0 %collective-permute-start.24 = (bf16[2,64,512]{2,1,0:T(8,128)(2,1)S(1)}, bf16[2,64,512]{2,1,0:T(8,128)(2,1)S(1)}, u32[]{:S(2)}, u32[]{:S(2)}) collective-permute-start(bf16[2,64,512]{2,1,0:T(8,128)(2,1)S(1)} %get-tuple-element.190), channel_id=1, source_target_pairs={{0,8},{4,12},{8,16},{12,20},{16,24},{20,28},{24,0},{28,4},{1,9},{5... | collective-permute-start | bytes 393224 | tf_op jit(solution)/shard_map/ppermute | solution.py:591
  151.3 2.4 %collective-permute-start.26 = (bf16[2,64,512]{2,1,0:T(8,128)(2,1)S(1)}, bf16[2,64,512]{2,1,0:T(8,128)(2,1)S(1)}, u32[]{:S(2)}, u32[]{:S(2)}) collective-permute-start(bf16[2,64,512]{2,1,0:T(8,128)(2,1)S(1)} %get-tuple-element.188), channel_id=1, source_target_pairs={{0,24},{4,28},{8,0},{12,4},{16,8},{20,12},{24,16},{28,20},{1,25},{... | collective-permute-start | bytes 393224 | tf_op jit(solution)/shard_map/ppermute | solution.py:591
  153.8 0.8 collective-permute-start.23
  154.7 14.2 %attend_back.3 = (bf16[1024,768]{1,0:T(8,128)(2,1)S(1)}, bf16[512,384]{1,0:T(8,128)(2,1)S(1)}, bf16[512,384]{1,0:T(8,128)(2,1)S(1)}) custom-call(s32[1]{0:T(128)} %dynamic-slice.9.limit_ref, bf16[1024,1536]{1,0:T(8,128)(2,1)S(1)} %copy-done.2, bf16[1024,1536]{1,0:T(8,128)(2,1)S(1)} %copy-done.2, bf16[1024,1536]{1,0:T(8,128)(2,1)S(1)} %copy-done.2, ...), custom_call_target="tpu_custom_call" | custom-call | flops 18400000000 | bytes 1048576 | tf_op jit(solution)/shard_map/attend_back/pallas_call | solution.py:465
  169.0 0.6 dynamic-slice_convert_fusion
  169.8 0.7 dynamic-slice_bitcast_fusion.4
  171.0 5.0 %begin_back.1 = bf16[8,4,136,128]{3,2,1,0:T(8,128)(2,1)} custom-call(s32[1]{0:T(128)} %dynamic-slice.9.limit_ref, bf16[8,4,136,128]{3,2,1,0:T(8,128)(2,1)S(1)} %bitcast.111, f32[1,512]{1,0:T(1,128)S(1)} %pad_maximum_fusion.3.clock_ref, f32[1,512]{1,0:T(1,128)S(1)} %reshape_squeeze.8.gain_ref, f32[1,512]{1,0:T(1,128)S(1)} %get-tuple-element.78.gg_two_ref, ...), custom_call_target="tpu_custom_call" | custom-call | flops 8049999872 | bytes 1048576 | tf_op jit(solution)/shard_map/begin_back/pallas_call | solution.py:553
  176.0 0.6 copy-done.12
  176.6 0.7 copy-done.9
  177.4 4.5 %all-to-all-start.1 = ((bf16[32,136,128]{2,1,0:T(8,128)(2,1)}), bf16[32,136,128]{2,1,0:T(8,128)(2,1)S(1)}, u32[]{:S(2)}, u32[]{:S(2)}) async-start(bf16[32,136,128]{2,1,0:T(8,128)(2,1)} %bitcast.25), calls=%async_computation.1 | async-start | bytes 2228224 | tf_op jit(solution)/shard_map/all_to_all | solution.py:801
  181.9 0.7 scatter_custom_fusion
  182.6 1.7 fusion.4
  184.3 1.8 collective-permute-start.31
  186.4 1.8 collective-permute-start.29
  188.1 2.1 collective-permute-start.30
  190.2 7.2 %collective-permute-done.31 = bf16[4,64,384]{2,1,0:T(8,128)(2,1)S(1)} collective-permute-done((bf16[4,64,384]{2,1,0:T(8,128)(2,1)}, bf16[4,64,384]{2,1,0:T(8,128)(2,1)S(1)}, u32[]{:S(2)}, u32[]{:S(2)}) %collective-permute-start.31) | collective-permute-done | bytes 196640 | tf_op jit(solution)/shard_map/ppermute | solution.py:591
  197.4 1.0 fusion.3
  198.5 1.2 collective-permute-start.32
  199.7 3.6 %collective-permute-start.33 = (bf16[64,384]{1,0:T(8,128)(2,1)S(1)}, bf16[64,384]{1,0:T(8,128)(2,1)S(1)}, u32[]{:S(2)}, u32[]{:S(2)}) collective-permute-start(bf16[64,384]{1,0:T(8,128)(2,1)S(1)} %get-tuple-element.197), channel_id=1, source_target_pairs={{0,16},{4,20},{8,24},{12,28},{16,0},{20,4},{24,8},{28,12},{1,17},{... | collective-permute-start | bytes 147464 | tf_op jit(solution)/shard_map/ppermute | solution.py:591
  203.8 0.7 add_bitcast_fusion
  204.4 2.3 %collective-permute-done.29 = bf16[64,640]{1,0:T(8,128)(2,1)S(1)} collective-permute-done((bf16[64,640]{1,0:T(8,128)(2,1)}, bf16[64,640]{1,0:T(8,128)(2,1)S(1)}, u32[]{:S(2)}, u32[]{:S(2)}) %collective-permute-start.29) | collective-permute-done | bytes 81952 | tf_op jit(solution)/shard_map/ppermute | solution.py:591
  206.7 2.9 %collective-permute-done.32 = bf16[64,384]{1,0:T(8,128)(2,1)S(1)} collective-permute-done((bf16[64,384]{1,0:T(8,128)(2,1)S(1)}, bf16[64,384]{1,0:T(8,128)(2,1)S(1)}, u32[]{:S(2)}, u32[]{:S(2)}) %collective-permute-start.32) | collective-permute-done | bytes 49184 | tf_op jit(solution)/shard_map/ppermute | solution.py:591
  209.6 7.1 %collective-permute-done.33 = bf16[64,384]{1,0:T(8,128)(2,1)S(1)} collective-permute-done((bf16[64,384]{1,0:T(8,128)(2,1)S(1)}, bf16[64,384]{1,0:T(8,128)(2,1)S(1)}, u32[]{:S(2)}, u32[]{:S(2)}) %collective-permute-start.33) | collective-permute-done | bytes 49184 | tf_op jit(solution)/shard_map/ppermute | solution.py:591
  216.7 0.7 slice.119
  217.4 0.6 slice_bitcast_fusion.2
  218.0 0.7 copy_bitcast_fusion
  218.7 0.8 gather_fusion.1
  219.5 1.1 slice.117
  (125 shorter events, 7.4 us)
Async XLA Ops:
  0.6 13.2 %copy-start = (bf16[32,128,128]{2,1,0:T(8,128)(2,1)S(1)}, bf16[32,128,128]{2,1,0:T(8,128)(2,1)}, u32[]{:S(2)}) copy-start(bf16[32,128,128]{2,1,0:T(8,128)(2,1)} %param.11) | copy-start | bytes 3145732
  1.6 24.9 %collective-permute-start.6 = (bf16[64,1152]{1,0:T(8,128)(2,1)S(1)}, bf16[64,1152]{1,0:T(8,128)(2,1)S(1)}, u32[]{:S(2)}, u32[]{:S(2)}) collective-permute-start(bf16[64,1152]{1,0:T(8,128)(2,1)S(1)} %pad_maximum_fusion.2), channel_id=1, source_target_pairs={{0,8},{4,12},{8,16},{12,20},{16,24},{20,28},{24,0},{28,4},{1,9},{5... | collective-permute-start | bytes 442376 | tf_op jit(solution)/shard_map/ppermute | solution.py:591
  4.7 25.5 %collective-permute-start.7 = (bf16[64,1152]{1,0:T(8,128)(2,1)S(1)}, bf16[64,1152]{1,0:T(8,128)(2,1)S(1)}, u32[]{:S(2)}, u32[]{:S(2)}) collective-permute-start(bf16[64,1152]{1,0:T(8,128)(2,1)S(1)} %pad_maximum_fusion.2), channel_id=1, source_target_pairs={{0,16},{4,20},{8,24},{12,28},{16,0},{20,4},{24,8},{28,12},{1,17},{... | collective-permute-start | bytes 442376 | tf_op jit(solution)/shard_map/ppermute | solution.py:591
  7.3 22.9 %collective-permute-start.8 = (bf16[64,1152]{1,0:T(8,128)(2,1)S(1)}, bf16[64,1152]{1,0:T(8,128)(2,1)S(1)}, u32[]{:S(2)}, u32[]{:S(2)}) collective-permute-start(bf16[64,1152]{1,0:T(8,128)(2,1)S(1)} %pad_maximum_fusion.2), channel_id=1, source_target_pairs={{0,24},{4,28},{8,0},{12,4},{16,8},{20,12},{24,16},{28,20},{1,25},{... | collective-permute-start | bytes 442376 | tf_op jit(solution)/shard_map/ppermute | solution.py:591
  9.4 10.8 %collective-permute-start = (bf16[64,384]{1,0:T(8,128)(2,1)S(1)}, bf16[64,384]{1,0:T(8,128)(2,1)S(1)}, u32[]{:S(2)}, u32[]{:S(2)}) collective-permute-start(bf16[64,384]{1,0:T(8,128)(2,1)S(1)} %copy_bitcast_fusion.1), channel_id=1, source_target_pairs={{0,4},{4,0},{8,12},{12,8},{16,20},{20,16},{24,28},{28,24},{1,5},{5... | collective-permute-start | bytes 147464 | tf_op jit(solution)/shard_map/ppermute | solution.py:591
  14.6 1.2 copy-start.18
  14.7 3.7 %copy-start.19 = (s32[32]{0:T(128)S(1)}, s32[32]{0:T(128)}, u32[]{:S(2)}) copy-start(s32[32]{0:T(128)} %param.12) | copy-start | bytes 388
  14.7 5.0 %copy-start.20 = (s32[32]{0:T(128)S(1)}, s32[32]{0:T(128)}, u32[]{:S(2)}) copy-start(s32[32]{0:T(128)} %param.13) | copy-start | bytes 388
  15.8 14.4 %copy-start.10 = (bf16[512,64]{0,1:T(8,128)(2,1)S(1)}, bf16[512,64]{0,1:T(8,128)(2,1)}, u32[]{:S(2)}) copy-start(bf16[512,64]{0,1:T(8,128)(2,1)} %param.18) | copy-start | bytes 196612
  15.8 14.4 %copy-start.11 = (bf16[64,512]{1,0:T(8,128)(2,1)S(1)}, bf16[64,512]{1,0:T(8,128)(2,1)}, u32[]{:S(2)}) copy-start(bf16[64,512]{1,0:T(8,128)(2,1)} %param.17) | copy-start | bytes 196612
  15.8 14.4 %copy-start.14 = (bf16[128,64]{0,1:T(8,128)(2,1)S(1)}, bf16[128,64]{0,1:T(8,128)(2,1)}, u32[]{:S(2)}) copy-start(bf16[128,64]{0,1:T(8,128)(2,1)} %param.16) | copy-start | bytes 49156
  20.9 13.2 %collective-permute-start.1 = (bf16[64,768]{1,0:T(8,128)(2,1)}, bf16[64,768]{1,0:T(8,128)(2,1)S(1)}, u32[]{:S(2)}, u32[]{:S(2)}) collective-permute-start(bf16[64,768]{1,0:T(8,128)(2,1)} %constant_dynamic-update-slice_fusion), channel_id=1, source_target_pairs={{0,8},{4,12},{8,16},{12,20},{16,24},{20,28},{24,0},{28,4},{1,9},{5... | collective-permute-start | bytes 294920 | tf_op jit(solution)/shard_map/ppermute | solution.py:591
  21.5 12.6 %collective-permute-start.2 = (bf16[64,768]{1,0:T(8,128)(2,1)}, bf16[64,768]{1,0:T(8,128)(2,1)S(1)}, u32[]{:S(2)}, u32[]{:S(2)}) collective-permute-start(bf16[64,768]{1,0:T(8,128)(2,1)} %constant_dynamic-update-slice_fusion), channel_id=1, source_target_pairs={{0,16},{4,20},{8,24},{12,28},{16,0},{20,4},{24,8},{28,12},{1,17},{... | collective-permute-start | bytes 294920 | tf_op jit(solution)/shard_map/ppermute | solution.py:591
  21.9 42.2 %all-to-all-start = ((bf16[32,136,128]{2,1,0:T(8,128)(2,1)}), bf16[32,136,128]{2,1,0:T(8,128)(2,1)S(1)}, u32[]{:S(2)}, u32[]{:S(2)}) async-start(bf16[32,136,128]{2,1,0:T(8,128)(2,1)} %pad_maximum_fusion), calls=%async_computation | async-start | bytes 2228224 | tf_op jit(solution)/shard_map/all_to_all | solution.py:735
  26.6 20.9 %collective-permute-start.3 = (bf16[64,768]{1,0:T(8,128)(2,1)}, bf16[64,768]{1,0:T(8,128)(2,1)S(1)}, u32[]{:S(2)}, u32[]{:S(2)}) collective-permute-start(bf16[64,768]{1,0:T(8,128)(2,1)} %constant_dynamic-update-slice_fusion), channel_id=1, source_target_pairs={{0,24},{4,28},{8,0},{12,4},{16,8},{20,12},{24,16},{28,20},{1,25},{... | collective-permute-start | bytes 294920 | tf_op jit(solution)/shard_map/ppermute | solution.py:591
  31.1 31.9 %collective-permute-start.10 = (bf16[256,1152]{1,0:T(8,128)(2,1)}, bf16[256,1152]{1,0:T(8,128)(2,1)S(1)}, u32[]{:S(2)}, u32[]{:S(2)}) collective-permute-start(bf16[256,1152]{1,0:T(8,128)(2,1)} %pad_maximum_fusion.1.refs_0_), channel_id=1, source_target_pairs={{0,2},{1,3},{2,0},{3,1},{4,6},{5,7},{6,4},{7,5},{8,10},{9,11},{10,... | collective-permute-start | bytes 1769480 | tf_op jit(solution)/shard_map/ppermute | solution.py:586
  32.6 30.5 %collective-permute-start.9 = (bf16[256,1152]{1,0:T(8,128)(2,1)}, bf16[256,1152]{1,0:T(8,128)(2,1)}, u32[]{:S(2)}, u32[]{:S(2)}) collective-permute-start(bf16[256,1152]{1,0:T(8,128)(2,1)} %pad_maximum_fusion.1.refs_0_), channel_id=1, source_target_pairs={{0,4},{4,0},{8,12},{12,8},{16,20},{20,16},{24,28},{28,24},{1,5},{5... | collective-permute-start | bytes 1769480 | tf_op jit(solution)/shard_map/ppermute | solution.py:591
  47.5 15.5 %collective-permute-start.5 = (bf16[512,384]{1,0:T(8,128)(2,1)S(1)}, bf16[512,384]{1,0:T(8,128)(2,1)S(1)}, u32[]{:S(2)}, u32[]{:S(2)}) collective-permute-start(bf16[512,384]{1,0:T(8,128)(2,1)S(1)} %slice_dynamic-update-slice_fusion.refs_0_), channel_id=1, source_target_pairs={{0,2},{1,3},{2,0},{3,1},{4,6},{5,7},{6,4},{7,5},{8,10},{9,11},{10,... | collective-permute-start | bytes 1179656 | tf_op jit(solution)/shard_map/ppermute | solution.py:586
  49.4 14.9 %collective-permute-start.4 = (bf16[512,384]{1,0:T(8,128)(2,1)S(1)}, bf16[512,384]{1,0:T(8,128)(2,1)S(1)}, u32[]{:S(2)}, u32[]{:S(2)}) collective-permute-start(bf16[512,384]{1,0:T(8,128)(2,1)S(1)} %slice_dynamic-update-slice_fusion.refs_0_), channel_id=1, source_target_pairs={{0,1},{1,0},{2,3},{3,2},{4,5},{5,4},{6,7},{7,6},{8,9},{9,8},{10,11... | collective-permute-start | bytes 1179656 | tf_op jit(solution)/shard_map/ppermute | solution.py:586
  49.5 37.9 %collective-permute-start.12 = (bf16[256,1152]{1,0:T(8,128)(2,1)}, bf16[256,1152]{1,0:T(8,128)(2,1)}, u32[]{:S(2)}, u32[]{:S(2)}) collective-permute-start(bf16[256,1152]{1,0:T(8,128)(2,1)} %pad_maximum_fusion.1.refs_0_), channel_id=1, source_target_pairs={{0,1},{1,0},{2,3},{3,2},{4,5},{5,4},{6,7},{7,6},{8,9},{9,8},{10,11... | collective-permute-start | bytes 1769480 | tf_op jit(solution)/shard_map/ppermute | solution.py:586
  63.0 0.8 copy-start.15
  63.1 24.4 %collective-permute-start.13 = (bf16[256,1152]{1,0:T(8,128)(2,1)}, bf16[256,1152]{1,0:T(8,128)(2,1)}, u32[]{:S(2)}, u32[]{:S(2)}) collective-permute-start(bf16[256,1152]{1,0:T(8,128)(2,1)} %collective-permute-done.9.refs_1_), channel_id=1, source_target_pairs={{0,1},{1,0},{2,3},{3,2},{4,5},{5,4},{6,7},{7,6},{8,9},{9,8},{10,11... | collective-permute-start | bytes 1769480 | tf_op jit(solution)/shard_map/ppermute | solution.py:586
  63.1 24.3 %collective-permute-start.15 = (bf16[256,1152]{1,0:T(8,128)(2,1)}, bf16[256,1152]{1,0:T(8,128)(2,1)}, u32[]{:S(2)}, u32[]{:S(2)}) collective-permute-start(bf16[256,1152]{1,0:T(8,128)(2,1)} %collective-permute-done.9.refs_1_), channel_id=1, source_target_pairs={{0,2},{1,3},{2,0},{3,1},{4,6},{5,7},{6,4},{7,5},{8,10},{9,11},{10,... | collective-permute-start | bytes 1769480 | tf_op jit(solution)/shard_map/ppermute | solution.py:586
  63.9 1.9 collective-permute-start.11
  64.3 23.1 %collective-permute-start.14 = (bf16[256,1152]{1,0:T(8,128)(2,1)}, bf16[256,1152]{1,0:T(8,128)(2,1)S(1)}, u32[]{:S(2)}, u32[]{:S(2)}) collective-permute-start(bf16[256,1152]{1,0:T(8,128)(2,1)} %copy-done.15), channel_id=1, source_target_pairs={{0,1},{1,0},{2,3},{3,2},{4,5},{5,4},{6,7},{7,6},{8,9},{9,8},{10,11... | collective-permute-start | bytes 1769480 | tf_op jit(solution)/shard_map/ppermute | solution.py:586
  72.1 15.4 %copy-start.1 = (bf16[1024,1536]{1,0:T(8,128)(2,1)}, bf16[1024,1536]{1,0:T(8,128)(2,1)S(1)}, u32[]{:S(2)}) copy-start(bf16[1024,1536]{1,0:T(8,128)(2,1)S(1)} %get-tuple-element.68.q_ref.k_ref.v_ref) | copy-start | bytes 9437188
  87.5 0.8 copy-start.16
  87.5 2.3 %collective-permute-start.16 = (bf16[256,1152]{1,0:T(8,128)(2,1)}, bf16[256,1152]{1,0:T(8,128)(2,1)S(1)}, u32[]{:S(2)}, u32[]{:S(2)}) collective-permute-start(bf16[256,1152]{1,0:T(8,128)(2,1)} %collective-permute-done.15.refs_5_), channel_id=1, source_target_pairs={{0,1},{1,0},{2,3},{3,2},{4,5},{5,4},{6,7},{7,6},{8,9},{9,8},{10,11... | collective-permute-start | bytes 1769480 | tf_op jit(solution)/shard_map/ppermute | solution.py:586
  89.7 0.8 copy-start.17
  119.6 3.2 %collective-permute-start.18 = (bf16[2,512,512]{2,1,0:T(8,128)(2,1)}, bf16[2,512,512]{2,1,0:T(8,128)(2,1)}, u32[]{:S(2)}, u32[]{:S(2)}) collective-permute-start(bf16[2,512,512]{2,1,0:T(8,128)(2,1)} %get-tuple-element.86), channel_id=1, source_target_pairs={{0,1},{1,0},{2,3},{3,2},{4,5},{5,4},{6,7},{7,6},{8,9},{9,8},{10,11... | collective-permute-start | bytes 3145736 | tf_op jit(solution)/shard_map/ppermute | solution.py:586
  119.8 5.0 %collective-permute-start.17 = (bf16[2,512,640]{2,1,0:T(8,128)(2,1)}, bf16[2,512,640]{2,1,0:T(8,128)(2,1)S(1)}, u32[]{:S(2)}, u32[]{:S(2)}) collective-permute-start(bf16[2,512,640]{2,1,0:T(8,128)(2,1)} %get-tuple-element.81), channel_id=1, source_target_pairs={{0,1},{1,0},{2,3},{3,2},{4,5},{5,4},{6,7},{7,6},{8,9},{9,8},{10,11... | collective-permute-start | bytes 3932168 | tf_op jit(solution)/shard_map/ppermute | solution.py:586
  122.8 6.1 %copy-start.2 = (bf16[1024,1536]{1,0:T(8,128)(2,1)S(1)}, bf16[1024,1536]{1,0:T(8,128)(2,1)}, u32[]{:S(2)}) copy-start(bf16[1024,1536]{1,0:T(8,128)(2,1)} %copy-done.1) | copy-start | bytes 9437188
  122.8 6.1 %copy-start.6 = (bf16[512,1024]{1,0:T(8,128)(2,1)S(1)}, bf16[512,1024]{1,0:T(8,128)(2,1)}, u32[]{:S(2)}) copy-start(bf16[512,1024]{1,0:T(8,128)(2,1)} %get-tuple-element.82.turn_ref) | copy-start | bytes 3145732
  124.7 4.1 %copy-start.5 = (bf16[512,1024]{1,0:T(8,128)(2,1)S(1)}, bf16[512,1024]{1,0:T(8,128)(2,1)}, u32[]{:S(2)}) copy-start(bf16[512,1024]{1,0:T(8,128)(2,1)} %get-tuple-element.88.n_turn_ref) | copy-start | bytes 3145732
  124.8 19.0 %collective-permute-start.19 = (bf16[4,2,64,512]{3,2,1,0:T(8,128)(2,1)S(1)}, bf16[4,2,64,512]{3,2,1,0:T(8,128)(2,1)S(1)}, u32[]{:S(2)}, u32[]{:S(2)}) collective-permute-start(bf16[4,2,64,512]{3,2,1,0:T(8,128)(2,1)S(1)} %bitcast.119), channel_id=1, source_target_pairs={{0,2},{1,3},{2,0},{3,1},{4,6},{5,7},{6,4},{7,5},{8,10},{9,11},{10,... | collective-permute-start | bytes 1572872 | tf_op jit(solution)/shard_map/ppermute | solution.py:586
  126.2 17.6 %collective-permute-start.20 = (bf16[2,4,64,640]{3,2,1,0:T(8,128)(2,1)S(1)}, bf16[2,4,64,640]{3,2,1,0:T(8,128)(2,1)S(1)}, u32[]{:S(2)}, u32[]{:S(2)}) collective-permute-start(bf16[2,4,64,640]{3,2,1,0:T(8,128)(2,1)S(1)} %fusion.1), channel_id=1, source_target_pairs={{0,4},{4,0},{8,12},{12,8},{16,20},{20,16},{24,28},{28,24},{1,5},{5... | collective-permute-start | bytes 1966088 | tf_op jit(solution)/shard_map/ppermute | solution.py:591
  128.8 15.0 %copy-start.8 = (bf16[2,512,640]{2,1,0:T(8,128)(2,1)S(1)}, bf16[2,512,640]{2,1,0:T(8,128)(2,1)}, u32[]{:S(2)}) copy-start(bf16[2,512,640]{2,1,0:T(8,128)(2,1)} %get-tuple-element.80) | copy-start | bytes 3932164
  143.8 10.0 %collective-permute-start.21 = (bf16[512,384]{1,0:T(8,128)(2,1)S(1)}, bf16[512,384]{1,0:T(8,128)(2,1)S(1)}, u32[]{:S(2)}, u32[]{:S(2)}) collective-permute-start(bf16[512,384]{1,0:T(8,128)(2,1)S(1)} %get-tuple-element.97), channel_id=1, source_target_pairs={{0,1},{1,0},{2,3},{3,2},{4,5},{5,4},{6,7},{7,6},{8,9},{9,8},{10,11... | collective-permute-start | bytes 1179656 | tf_op jit(solution)/shard_map/ppermute | solution.py:586
  144.2 24.8 %collective-permute-start.22 = (bf16[4,64,640]{2,1,0:T(8,128)(2,1)S(1)}, bf16[4,64,640]{2,1,0:T(8,128)(2,1)S(1)}, u32[]{:S(2)}, u32[]{:S(2)}) collective-permute-start(bf16[4,64,640]{2,1,0:T(8,128)(2,1)S(1)} %slice_bitcast_fusion), channel_id=1, source_target_pairs={{0,2},{1,3},{2,0},{3,1},{4,6},{5,7},{6,4},{7,5},{8,10},{9,11},{10,... | collective-permute-start | bytes 983048 | tf_op jit(solution)/shard_map/ppermute | solution.py:586
  145.2 9.5 %copy-start.7 = (bf16[1024,512]{1,0:T(8,128)(2,1)S(1)}, bf16[1024,512]{1,0:T(8,128)(2,1)}, u32[]{:S(2)}) copy-start(bf16[1024,512]{1,0:T(8,128)(2,1)} %get-tuple-element.98.cg_ref) | copy-start | bytes 3145732
  145.3 23.6 %collective-permute-start.24 = (bf16[2,64,512]{2,1,0:T(8,128)(2,1)S(1)}, bf16[2,64,512]{2,1,0:T(8,128)(2,1)S(1)}, u32[]{:S(2)}, u32[]{:S(2)}) collective-permute-start(bf16[2,64,512]{2,1,0:T(8,128)(2,1)S(1)} %get-tuple-element.190), channel_id=1, source_target_pairs={{0,8},{4,12},{8,16},{12,20},{16,24},{20,28},{24,0},{28,4},{1,9},{5... | collective-permute-start | bytes 393224 | tf_op jit(solution)/shard_map/ppermute | solution.py:591
  151.3 17.6 %collective-permute-start.25 = (bf16[2,64,512]{2,1,0:T(8,128)(2,1)S(1)}, bf16[2,64,512]{2,1,0:T(8,128)(2,1)S(1)}, u32[]{:S(2)}, u32[]{:S(2)}) collective-permute-start(bf16[2,64,512]{2,1,0:T(8,128)(2,1)S(1)} %get-tuple-element.189), channel_id=1, source_target_pairs={{0,16},{4,20},{8,24},{12,28},{16,0},{20,4},{24,8},{28,12},{1,17},{... | collective-permute-start | bytes 393224 | tf_op jit(solution)/shard_map/ppermute | solution.py:591
  151.3 17.6 %collective-permute-start.26 = (bf16[2,64,512]{2,1,0:T(8,128)(2,1)S(1)}, bf16[2,64,512]{2,1,0:T(8,128)(2,1)S(1)}, u32[]{:S(2)}, u32[]{:S(2)}) collective-permute-start(bf16[2,64,512]{2,1,0:T(8,128)(2,1)S(1)} %get-tuple-element.188), channel_id=1, source_target_pairs={{0,24},{4,28},{8,0},{12,4},{16,8},{20,12},{24,16},{28,20},{1,25},{... | collective-permute-start | bytes 393224 | tf_op jit(solution)/shard_map/ppermute | solution.py:591
  153.8 15.1 %collective-permute-start.23 = (bf16[512,384]{1,0:T(8,128)(2,1)S(1)}, bf16[512,384]{1,0:T(8,128)(2,1)S(1)}, u32[]{:S(2)}, u32[]{:S(2)}) collective-permute-start(bf16[512,384]{1,0:T(8,128)(2,1)S(1)} %add_convert_fusion.3), channel_id=1, source_target_pairs={{0,2},{1,3},{2,0},{3,1},{4,6},{5,7},{6,4},{7,5},{8,10},{9,11},{10,... | collective-permute-start | bytes 1179656 | tf_op jit(solution)/shard_map/ppermute | solution.py:586
  154.7 16.3 %copy-start.4 = (bf16[512,1536]{1,0:T(8,128)(2,1)S(1)}, bf16[512,1536]{1,0:T(8,128)(2,1)}, u32[]{:S(2)}) copy-start(bf16[512,1536]{1,0:T(8,128)(2,1)} %get-tuple-element.108.w_ref) | copy-start | bytes 4718596
  168.9 2.0 copy-start.3
  170.5 5.5 %collective-permute-start.28 = (bf16[64,640]{1,0:T(8,128)(2,1)S(1)}, bf16[64,640]{1,0:T(8,128)(2,1)S(1)}, u32[]{:S(2)}, u32[]{:S(2)}) collective-permute-start(bf16[64,640]{1,0:T(8,128)(2,1)S(1)} %get-tuple-element.195), channel_id=1, source_target_pairs={{0,16},{4,20},{8,24},{12,28},{16,0},{20,4},{24,8},{28,12},{1,17},{... | collective-permute-start | bytes 245768 | tf_op jit(solution)/shard_map/ppermute | solution.py:591
  171.0 5.0 %collective-permute-start.27 = (bf16[512,384]{1,0:T(8,128)(2,1)S(1)}, bf16[512,384]{1,0:T(8,128)(2,1)S(1)}, u32[]{:S(2)}, u32[]{:S(2)}) collective-permute-start(bf16[512,384]{1,0:T(8,128)(2,1)S(1)} %get-tuple-element.110), channel_id=1, source_target_pairs={{0,1},{1,0},{2,3},{3,2},{4,5},{5,4},{6,7},{7,6},{8,9},{9,8},{10,11... | collective-permute-start | bytes 1179656 | tf_op jit(solution)/shard_map/ppermute | solution.py:586
  176.0 0.6 copy-start.12
  176.6 0.7 copy-start.9
  177.4 41.3 %all-to-all-start.1 = ((bf16[32,136,128]{2,1,0:T(8,128)(2,1)}), bf16[32,136,128]{2,1,0:T(8,128)(2,1)S(1)}, u32[]{:S(2)}, u32[]{:S(2)}) async-start(bf16[32,136,128]{2,1,0:T(8,128)(2,1)} %bitcast.25), calls=%async_computation.1 | async-start | bytes 2228224 | tf_op jit(solution)/shard_map/all_to_all | solution.py:801
  184.3 13.1 %collective-permute-start.31 = (bf16[4,64,384]{2,1,0:T(8,128)(2,1)}, bf16[4,64,384]{2,1,0:T(8,128)(2,1)S(1)}, u32[]{:S(2)}, u32[]{:S(2)}) collective-permute-start(bf16[4,64,384]{2,1,0:T(8,128)(2,1)} %fusion.4), channel_id=1, source_target_pairs={{0,4},{4,0},{8,12},{12,8},{16,20},{20,16},{24,28},{28,24},{1,5},{5... | collective-permute-start | bytes 589832 | tf_op jit(solution)/shard_map/ppermute | solution.py:591
  186.0 30.7 %copy-start.13 = (bf16[64,640]{1,0:T(8,128)(2,1)S(1)}, bf16[64,640]{1,0:T(8,128)(2,1)}, u32[]{:S(2)}) copy-start(bf16[64,640]{1,0:T(8,128)(2,1)} %copy-done.12) | copy-start | bytes 245764
  186.0 17.2 %collective-permute-start.35 = (bf16[1,64,512]{2,1,0:T(8,128)(2,1)}, bf16[1,64,512]{2,1,0:T(8,128)(2,1)S(1)}, u32[]{:S(2)}, u32[]{:S(2)}) collective-permute-start(bf16[1,64,512]{2,1,0:T(8,128)(2,1)} %dynamic-slice_convert_fusion), channel_id=1, source_target_pairs={{0,4},{4,0},{8,12},{12,8},{16,20},{20,16},{24,28},{28,24},{1,5},{5... | collective-permute-start | bytes 196616 | tf_op jit(solution)/shard_map/ppermute | solution.py:591
  186.4 20.4 %collective-permute-start.29 = (bf16[64,640]{1,0:T(8,128)(2,1)}, bf16[64,640]{1,0:T(8,128)(2,1)S(1)}, u32[]{:S(2)}, u32[]{:S(2)}) collective-permute-start(bf16[64,640]{1,0:T(8,128)(2,1)} %get-tuple-element.193), channel_id=1, source_target_pairs={{0,8},{4,12},{8,16},{12,20},{16,24},{20,28},{24,0},{28,4},{1,9},{5... | collective-permute-start | bytes 245768 | tf_op jit(solution)/shard_map/ppermute | solution.py:591
  188.1 18.6 %collective-permute-start.30 = (bf16[64,640]{1,0:T(8,128)(2,1)}, bf16[64,640]{1,0:T(8,128)(2,1)S(1)}, u32[]{:S(2)}, u32[]{:S(2)}) collective-permute-start(bf16[64,640]{1,0:T(8,128)(2,1)} %get-tuple-element.192), channel_id=1, source_target_pairs={{0,24},{4,28},{8,0},{12,4},{16,8},{20,12},{24,16},{28,20},{1,25},{... | collective-permute-start | bytes 245768 | tf_op jit(solution)/shard_map/ppermute | solution.py:591
  198.5 11.2 %collective-permute-start.32 = (bf16[64,384]{1,0:T(8,128)(2,1)S(1)}, bf16[64,384]{1,0:T(8,128)(2,1)S(1)}, u32[]{:S(2)}, u32[]{:S(2)}) collective-permute-start(bf16[64,384]{1,0:T(8,128)(2,1)S(1)} %get-tuple-element.198), channel_id=1, source_target_pairs={{0,8},{4,12},{8,16},{12,20},{16,24},{20,28},{24,0},{28,4},{1,9},{5... | collective-permute-start | bytes 147464 | tf_op jit(solution)/shard_map/ppermute | solution.py:591
  199.7 17.0 %collective-permute-start.33 = (bf16[64,384]{1,0:T(8,128)(2,1)S(1)}, bf16[64,384]{1,0:T(8,128)(2,1)S(1)}, u32[]{:S(2)}, u32[]{:S(2)}) collective-permute-start(bf16[64,384]{1,0:T(8,128)(2,1)S(1)} %get-tuple-element.197), channel_id=1, source_target_pairs={{0,16},{4,20},{8,24},{12,28},{16,0},{20,4},{24,8},{28,12},{1,17},{... | collective-permute-start | bytes 147464 | tf_op jit(solution)/shard_map/ppermute | solution.py:591
  203.3 13.4 %collective-permute-start.34 = (bf16[64,384]{1,0:T(8,128)(2,1)S(1)}, bf16[64,384]{1,0:T(8,128)(2,1)S(1)}, u32[]{:S(2)}, u32[]{:S(2)}) collective-permute-start(bf16[64,384]{1,0:T(8,128)(2,1)S(1)} %get-tuple-element.196), channel_id=1, source_target_pairs={{0,24},{4,28},{8,0},{12,4},{16,8},{20,12},{24,16},{28,20},{1,25},{... | collective-permute-start | bytes 147464 | tf_op jit(solution)/shard_map/ppermute | solution.py:591

commit v13 on v11

--- a/solution.py
+++ b/solution.py
@@ -697,9 +697,6 @@
     assert tensor_count == 4 and total_seqs == devices
     features = width * tensor_count
     own = lax.axis_index("dp") * tensor_count + lax.axis_index("tensor")
-    own_id = lax.dynamic_slice_in_dim(deal_order, own, 1)
-    limit = lengths[own_id]
-    clock = clock_rows(timesteps[own_id], features)
     per = gain_attn.shape[0]
     rows = w_qkv.shape[0]
     hidden = w_up.shape[1]
@@ -724,6 +721,10 @@
         qkv_parts = collect_columns(collect_rows(qkv))
         rest_parts = [(part,) for part in collect_columns(collect_rows(rest))]
 
+    deal_later = after(deal_order, pieces[1]) if direct else deal_order
+    own_id = lax.dynamic_slice_in_dim(deal_later, own, 1)
+    limit = lengths[own_id]
+    clock = clock_rows(timesteps[own_id], features)
     spare = jnp.stack(three_terms(gain_attn) + three_terms(gain_ffn)).reshape(1, 6 * per)
     spare = jnp.pad(spare, ((0, SPARE - 1), (0, width - 6 * per)))
     arranged = jnp.concatenate(

time: 220 us -> 220 us (level)
    ppermute x16, waiting for transfers between devices: 13.3 us -> 8.96 us  [swap(): return lax.ppermute(value, 'tensor', [(i, i ^ apart) for i in range(count)])]
    ppermute x20, waiting for transfers between devices: 41 us -> 44.7 us  [along_dp(): return lax.ppermute(value, 'dp', [(i, move(i)) for i in range(count)])]
  transfers between devices with their start and end apart: 38 -> 38, of which waited for: 12 -> 11; matrix products, arithmetic and copies ran while one was open for 8% -> 8% of each run, Pallas kernels for 25% -> 25%
where the time goes in v13:
time: 220 us; the launch traced here: 219 us
  Pallas kernels  84.8 us (39%)
  waiting for transfers between devices  53.7 us (24%)
  starting transfers between devices  50.4 us (23%)
  other arithmetic  13.5 us (6%)
  local copies, waits for them, and re-layouts  12.9 us (6%)
  between operations  3.81 us (2%)
    ppermute x20, waiting for transfers between devices, along_dp(): return lax.ppermute(value, 'dp', [(i, move(i)) for i in range(count)])  44.7 us
    ppermute x20, starting transfers between devices, along_dp(): return lax.ppermute(value, 'dp', [(i, move(i)) for i in range(count)])  34.3 us
    pallas_call x2, Pallas kernels, attend_back(): pl.pallas_call(attend_back_kernel, grid_spec=pltpu.PrefetchScalarGridSpec...  29.1 us
    pallas_call x1, Pallas kernels, middle_block(): pl.pallas_call(functools.partial(middle_kernel, groups), grid_spec=pltpu....  29 us
    pallas_call x1, Pallas kernels, attend(): pl.pallas_call(attend_kernel, grid_spec=pltpu.PrefetchScalarGridSpec(num_...  15.3 us
    ppermute x16, starting transfers between devices, swap(): return lax.ppermute(value, 'tensor', [(i, i ^ apart) for i in range(count)])  9.55 us
    ppermute x16, waiting for transfers between devices, swap(): return lax.ppermute(value, 'tensor', [(i, i ^ apart) for i in range(count)])  8.96 us
    pallas_call x1, Pallas kernels, project(): pl.pallas_call(functools.partial(project_kernel, groups), grid_spec=pltpu...  6.26 us
  transfers between devices with their start and end apart: 38, of which 11 were waited for; matrix products, arithmetic and copies ran while one was open for 8% of the time, Pallas kernels for 25%

profile of v13, /device:TPU:0, one launch (start us, length us, event | category | flops | bytes accessed | tf_op | source)
XLA Modules:
  0.0 219.0 jit_solution(17025883134677410566)
XLA Ops:
  0.6 1.0 pad_maximum_fusion.2
  1.6 3.1 %collective-permute-start.6 = (bf16[64,1152]{1,0:T(8,128)(2,1)S(1)}, bf16[64,1152]{1,0:T(8,128)(2,1)S(1)}, u32[]{:S(2)}, u32[]{:S(2)}) collective-permute-start(bf16[64,1152]{1,0:T(8,128)(2,1)S(1)} %pad_maximum_fusion.2), channel_id=1, source_target_pairs={{0,8},{4,12},{8,16},{12,20},{16,24},{20,28},{24,0},{28,4},{1,9},{5... | collective-permute-start | bytes 442376 | tf_op jit(solution)/shard_map/ppermute | solution.py:591
  4.7 2.6 %collective-permute-start.7 = (bf16[64,1152]{1,0:T(8,128)(2,1)S(1)}, bf16[64,1152]{1,0:T(8,128)(2,1)S(1)}, u32[]{:S(2)}, u32[]{:S(2)}) collective-permute-start(bf16[64,1152]{1,0:T(8,128)(2,1)S(1)} %pad_maximum_fusion.2), channel_id=1, source_target_pairs={{0,16},{4,20},{8,24},{12,28},{16,0},{20,4},{24,8},{28,12},{1,17},{... | collective-permute-start | bytes 442376 | tf_op jit(solution)/shard_map/ppermute | solution.py:591
  7.3 1.3 collective-permute-start.8
  8.6 0.8 copy_bitcast_fusion.1
  9.4 1.5 collective-permute-start
  11.0 0.7 fusion.9
  11.8 0.7 compare_select_fusion.1
  12.5 0.7 gather_fusion
  13.2 1.1 pad_maximum_fusion
  14.4 2.8 %all-to-all-start = ((bf16[32,136,128]{2,1,0:T(8,128)(2,1)}), bf16[32,136,128]{2,1,0:T(8,128)(2,1)S(1)}, u32[]{:S(2)}, u32[]{:S(2)}) async-start(bf16[32,136,128]{2,1,0:T(8,128)(2,1)} %pad_maximum_fusion), calls=%async_computation | async-start | bytes 2228224 | tf_op jit(solution)/shard_map/all_to_all | solution.py:733
  17.3 1.7 collective-permute-start.1
  19.0 2.5 %collective-permute-start.2 = (bf16[64,768]{1,0:T(8,128)(2,1)S(1)}, bf16[64,768]{1,0:T(8,128)(2,1)S(1)}, u32[]{:S(2)}, u32[]{:S(2)}) collective-permute-start(bf16[64,768]{1,0:T(8,128)(2,1)S(1)} %constant_dynamic-update-slice_fusion), channel_id=1, source_target_pairs={{0,16},{4,20},{8,24},{12,28},{16,0},{20,4},{24,8},{28,12},{1,17},{... | collective-permute-start | bytes 294920 | tf_op jit(solution)/shard_map/ppermute | solution.py:591
  21.5 1.4 collective-permute-start.3
  23.0 0.9 pad_maximum_fusion.1.refs_0_
  23.8 1.5 collective-permute-start.10
  25.3 1.5 collective-permute-start.9
  26.8 15.6 %collective-permute-done.1 = bf16[64,768]{1,0:T(8,128)(2,1)S(1)} collective-permute-done((bf16[64,768]{1,0:T(8,128)(2,1)S(1)}, bf16[64,768]{1,0:T(8,128)(2,1)S(1)}, u32[]{:S(2)}, u32[]{:S(2)}) %collective-permute-start.1) | collective-permute-done | bytes 98336 | tf_op jit(solution)/shard_map/ppermute | solution.py:591
  42.4 9.2 %collective-permute-done.2 = bf16[64,768]{1,0:T(8,128)(2,1)S(1)} collective-permute-done((bf16[64,768]{1,0:T(8,128)(2,1)S(1)}, bf16[64,768]{1,0:T(8,128)(2,1)S(1)}, u32[]{:S(2)}, u32[]{:S(2)}) %collective-permute-start.2) | collective-permute-done | bytes 98336 | tf_op jit(solution)/shard_map/ppermute | solution.py:591
  51.7 1.6 collective-permute-start.5
  58.4 3.6 %collective-permute-done.5.refs_2_ = bf16[512,384]{1,0:T(8,128)(2,1)S(1)} collective-permute-done((bf16[512,384]{1,0:T(8,128)(2,1)S(1)}, bf16[512,384]{1,0:T(8,128)(2,1)S(1)}, u32[]{:S(2)}, u32[]{:S(2)}) %collective-permute-start.5) | collective-permute-done | bytes 393248 | tf_op jit(solution)/shard_map/ppermute | solution.py:586
  62.0 1.6 collective-permute-start.15
  64.5 1.0 collective-permute-done.11.refs_3_
  65.4 6.3 %project.1 = (bf16[1024,1536]{1,0:T(8,128)(2,1)S(1)}, bf16[512,1024]{1,0:T(8,128)(2,1)}, bf16[512,1536]{1,0:T(8,128)(2,1)}) custom-call(s32[1]{0:T(128)} %dynamic-slice.9.limit_ref, s32[8]{0:T(128)S(1)} %pad_add_fusion.place_ref, bf16[8,4,136,128]{3,2,1,0:T(8,128)(2,1)S(1)} %bitcast.109, f32[1,512]{1,0:T(1,128)S(1)} %pad_maximum_fusion.3.clock_ref, ...), custom_call_target="tpu_custom_call" | custom-call | flops 5750000128 | bytes 1048576 | tf_op jit(solution)/shard_map/project/pallas_call | solution.py:110
  71.7 15.3 %attend.1 = (bf16[1024,512]{1,0:T(8,128)(2,1)}, bf16[512,1024]{1,0:T(8,128)(2,1)}, f32[4,2,1024]{2,1,0:T(2,128)S(1)}) custom-call(s32[1]{0:T(128)} %dynamic-slice.9.limit_ref, bf16[1024,1536]{1,0:T(8,128)(2,1)S(1)} %get-tuple-element.68.q_ref.k_ref.v_ref, bf16[1024,1536]{1,0:T(8,128)(2,1)S(1)} %get-tuple-element.68.q_ref.k_ref.v_ref, ...), custom_call_target="tpu_custom_call" | custom-call | flops 17250000896 | bytes 1048576 | tf_op jit(solution)/shard_map/attend/pallas_call | solution.py:199
  87.2 0.7 copy-done.16
  88.1 1.3 collective-permute-done.16.refs_7_
  89.4 0.8 copy-done.17
  90.2 29.0 %middle.1 = (bf16[1,1024,512]{2,1,0:T(8,128)(2,1)}, bf16[1024,512]{1,0:T(8,128)(2,1)}, f32[1024,512]{1,0:T(8,128)}, f32[1,512]{1,0:T(1,128)S(1)}, bf16[2,512,640...) custom-call(s32[1]{0:T(128)} %dynamic-slice.9.limit_ref, ...), custom_call_target="tpu_custom_call" | custom-call | flops 28750000128 | bytes 1048576 | tf_op jit(solution)/shard_map/middle/pallas_call | solution.py:370
  119.8 3.1 %collective-permute-done.18 = bf16[2,512,512]{2,1,0:T(8,128)(2,1)S(1)} collective-permute-done((bf16[2,512,512]{2,1,0:T(8,128)(2,1)}, bf16[2,512,512]{2,1,0:T(8,128)(2,1)S(1)}, u32[]{:S(2)}, u32[]{:S(2)}) %collective-permute-start.18) | collective-permute-done | bytes 1048608 | tf_op jit(solution)/shard_map/ppermute | solution.py:586
  122.9 1.6 convert_add_fusion
  124.7 1.5 fusion.1
  126.3 2.1 collective-permute-start.20
  128.3 14.9 %attend_back.2 = (bf16[1024,768]{1,0:T(8,128)(2,1)S(1)}, bf16[512,384]{1,0:T(8,128)(2,1)S(1)}, bf16[512,384]{1,0:T(8,128)(2,1)S(1)}) custom-call(s32[1]{0:T(128)} %dynamic-slice.9.limit_ref, bf16[1024,1536]{1,0:T(8,128)(2,1)S(1)} %copy-done.2, bf16[1024,1536]{1,0:T(8,128)(2,1)S(1)} %copy-done.2, bf16[1024,1536]{1,0:T(8,128)(2,1)S(1)} %copy-done.2, ...), custom_call_target="tpu_custom_call" | custom-call | flops 18400000000 | bytes 1048576 | tf_op jit(solution)/shard_map/attend_back/pallas_call | solution.py:465
  143.3 1.3 fusion
  144.7 1.3 collective-permute-start.22
  146.3 2.0 collective-permute-start.24
  148.3 2.2 %collective-permute-start.25 = (bf16[2,64,512]{2,1,0:T(8,128)(2,1)S(1)}, bf16[2,64,512]{2,1,0:T(8,128)(2,1)S(1)}, u32[]{:S(2)}, u32[]{:S(2)}) collective-permute-start(bf16[2,64,512]{2,1,0:T(8,128)(2,1)S(1)} %get-tuple-element.189), channel_id=1, source_target_pairs={{0,16},{4,20},{8,24},{12,28},{16,0},{20,4},{24,8},{28,12},{1,17},{... | collective-permute-start | bytes 393224 | tf_op jit(solution)/shard_map/ppermute | solution.py:591
  150.8 1.5 collective-permute-start.23
  152.4 14.2 %attend_back.3 = (bf16[1024,768]{1,0:T(8,128)(2,1)S(1)}, bf16[512,384]{1,0:T(8,128)(2,1)S(1)}, bf16[512,384]{1,0:T(8,128)(2,1)S(1)}) custom-call(s32[1]{0:T(128)} %dynamic-slice.9.limit_ref, bf16[1024,1536]{1,0:T(8,128)(2,1)S(1)} %copy-done.2, bf16[1024,1536]{1,0:T(8,128)(2,1)S(1)} %copy-done.2, bf16[1024,1536]{1,0:T(8,128)(2,1)S(1)} %copy-done.2, ...), custom_call_target="tpu_custom_call" | custom-call | flops 18400000000 | bytes 1048576 | tf_op jit(solution)/shard_map/attend_back/pallas_call | solution.py:465
  166.7 0.6 dynamic-slice_convert_fusion
  167.5 0.7 dynamic-slice_bitcast_fusion.4
  168.2 0.9 collective-permute-start.28
  169.1 5.0 %begin_back.1 = bf16[8,4,136,128]{3,2,1,0:T(8,128)(2,1)} custom-call(s32[1]{0:T(128)} %dynamic-slice.9.limit_ref, bf16[8,4,136,128]{3,2,1,0:T(8,128)(2,1)S(1)} %bitcast.111, f32[1,512]{1,0:T(1,128)S(1)} %pad_maximum_fusion.3.clock_ref, f32[1,512]{1,0:T(1,128)S(1)} %reshape_squeeze.8.gain_ref, f32[1,512]{1,0:T(1,128)S(1)} %get-tuple-element.78.gg_two_ref, ...), custom_call_target="tpu_custom_call" | custom-call | flops 8049999872 | bytes 1048576 | tf_op jit(solution)/shard_map/begin_back/pallas_call | solution.py:553
  174.6 0.6 copy-done.13
  175.2 0.7 copy-done.9
  175.9 3.7 %all-to-all-start.1 = ((bf16[32,136,128]{2,1,0:T(8,128)(2,1)}), bf16[32,136,128]{2,1,0:T(8,128)(2,1)S(1)}, u32[]{:S(2)}, u32[]{:S(2)}) async-start(bf16[32,136,128]{2,1,0:T(8,128)(2,1)} %bitcast.25), calls=%async_computation.1 | async-start | bytes 2228224 | tf_op jit(solution)/shard_map/all_to_all | solution.py:799
  179.7 0.7 scatter_custom_fusion
  180.4 1.7 fusion.4
  182.1 1.8 collective-permute-start.31
  184.2 1.8 collective-permute-start.29
  185.9 2.1 collective-permute-start.30
  188.0 7.2 %collective-permute-done.31 = bf16[4,64,384]{2,1,0:T(8,128)(2,1)S(1)} collective-permute-done((bf16[4,64,384]{2,1,0:T(8,128)(2,1)}, bf16[4,64,384]{2,1,0:T(8,128)(2,1)S(1)}, u32[]{:S(2)}, u32[]{:S(2)}) %collective-permute-start.31) | collective-permute-done | bytes 196640 | tf_op jit(solution)/shard_map/ppermute | solution.py:591
  195.2 1.0 fusion.3
  196.3 1.2 collective-permute-start.32
  197.5 3.6 %collective-permute-start.33 = (bf16[64,384]{1,0:T(8,128)(2,1)S(1)}, bf16[64,384]{1,0:T(8,128)(2,1)S(1)}, u32[]{:S(2)}, u32[]{:S(2)}) collective-permute-start(bf16[64,384]{1,0:T(8,128)(2,1)S(1)} %get-tuple-element.197), channel_id=1, source_target_pairs={{0,16},{4,20},{8,24},{12,28},{16,0},{20,4},{24,8},{28,12},{1,17},{... | collective-permute-start | bytes 147464 | tf_op jit(solution)/shard_map/ppermute | solution.py:591
  201.6 0.7 add_bitcast_fusion
  202.3 2.3 %collective-permute-done.29 = bf16[64,640]{1,0:T(8,128)(2,1)S(1)} collective-permute-done((bf16[64,640]{1,0:T(8,128)(2,1)}, bf16[64,640]{1,0:T(8,128)(2,1)S(1)}, u32[]{:S(2)}, u32[]{:S(2)}) %collective-permute-start.29) | collective-permute-done | bytes 81952 | tf_op jit(solution)/shard_map/ppermute | solution.py:591
  204.5 2.9 %collective-permute-done.32 = bf16[64,384]{1,0:T(8,128)(2,1)S(1)} collective-permute-done((bf16[64,384]{1,0:T(8,128)(2,1)S(1)}, bf16[64,384]{1,0:T(8,128)(2,1)S(1)}, u32[]{:S(2)}, u32[]{:S(2)}) %collective-permute-start.32) | collective-permute-done | bytes 49184 | tf_op jit(solution)/shard_map/ppermute | solution.py:591
  207.4 7.1 %collective-permute-done.33 = bf16[64,384]{1,0:T(8,128)(2,1)S(1)} collective-permute-done((bf16[64,384]{1,0:T(8,128)(2,1)S(1)}, bf16[64,384]{1,0:T(8,128)(2,1)S(1)}, u32[]{:S(2)}, u32[]{:S(2)}) %collective-permute-start.33) | collective-permute-done | bytes 49184 | tf_op jit(solution)/shard_map/ppermute | solution.py:591
  214.6 0.7 slice.119
  215.8 0.7 copy_bitcast_fusion
  216.5 0.8 gather_fusion.1
  217.3 1.1 slice.117
  (125 shorter events, 8.2 us)
Async XLA Ops:
  0.6 11.8 %copy-start = (bf16[32,128,128]{2,1,0:T(8,128)(2,1)S(1)}, bf16[32,128,128]{2,1,0:T(8,128)(2,1)}, u32[]{:S(2)}) copy-start(bf16[32,128,128]{2,1,0:T(8,128)(2,1)} %param.11) | copy-start | bytes 3145732
  1.6 19.9 %collective-permute-start.6 = (bf16[64,1152]{1,0:T(8,128)(2,1)S(1)}, bf16[64,1152]{1,0:T(8,128)(2,1)S(1)}, u32[]{:S(2)}, u32[]{:S(2)}) collective-permute-start(bf16[64,1152]{1,0:T(8,128)(2,1)S(1)} %pad_maximum_fusion.2), channel_id=1, source_target_pairs={{0,8},{4,12},{8,16},{12,20},{16,24},{20,28},{24,0},{28,4},{1,9},{5... | collective-permute-start | bytes 442376 | tf_op jit(solution)/shard_map/ppermute | solution.py:591
  4.7 18.2 %collective-permute-start.7 = (bf16[64,1152]{1,0:T(8,128)(2,1)S(1)}, bf16[64,1152]{1,0:T(8,128)(2,1)S(1)}, u32[]{:S(2)}, u32[]{:S(2)}) collective-permute-start(bf16[64,1152]{1,0:T(8,128)(2,1)S(1)} %pad_maximum_fusion.2), channel_id=1, source_target_pairs={{0,16},{4,20},{8,24},{12,28},{16,0},{20,4},{24,8},{28,12},{1,17},{... | collective-permute-start | bytes 442376 | tf_op jit(solution)/shard_map/ppermute | solution.py:591
  7.3 15.7 %collective-permute-start.8 = (bf16[64,1152]{1,0:T(8,128)(2,1)S(1)}, bf16[64,1152]{1,0:T(8,128)(2,1)S(1)}, u32[]{:S(2)}, u32[]{:S(2)}) collective-permute-start(bf16[64,1152]{1,0:T(8,128)(2,1)S(1)} %pad_maximum_fusion.2), channel_id=1, source_target_pairs={{0,24},{4,28},{8,0},{12,4},{16,8},{20,12},{24,16},{28,20},{1,25},{... | collective-permute-start | bytes 442376 | tf_op jit(solution)/shard_map/ppermute | solution.py:591
  9.4 7.8 %collective-permute-start = (bf16[64,384]{1,0:T(8,128)(2,1)S(1)}, bf16[64,384]{1,0:T(8,128)(2,1)S(1)}, u32[]{:S(2)}, u32[]{:S(2)}) collective-permute-start(bf16[64,384]{1,0:T(8,128)(2,1)S(1)} %copy_bitcast_fusion.1), channel_id=1, source_target_pairs={{0,4},{4,0},{8,12},{12,8},{16,20},{20,16},{24,28},{28,24},{1,5},{5... | collective-permute-start | bytes 147464 | tf_op jit(solution)/shard_map/ppermute | solution.py:591
  14.4 2.8 %copy-start.12 = (bf16[64,3,128]{2,0,1:T(8,128)(2,1)S(1)}, bf16[64,3,128]{2,0,1:T(8,128)(2,1)}, u32[]{:S(2)}) copy-start(bf16[64,3,128]{2,0,1:T(8,128)(2,1)} %param.15) | copy-start | bytes 147460
  14.4 8.6 %copy-start.10 = (bf16[512,64]{0,1:T(8,128)(2,1)S(1)}, bf16[512,64]{0,1:T(8,128)(2,1)}, u32[]{:S(2)}) copy-start(bf16[512,64]{0,1:T(8,128)(2,1)} %param.18) | copy-start | bytes 196612
  14.4 8.6 %copy-start.11 = (bf16[64,512]{1,0:T(8,128)(2,1)S(1)}, bf16[64,512]{1,0:T(8,128)(2,1)}, u32[]{:S(2)}) copy-start(bf16[64,512]{1,0:T(8,128)(2,1)} %param.17) | copy-start | bytes 196612
  14.4 8.6 %copy-start.15 = (bf16[128,64]{0,1:T(8,128)(2,1)S(1)}, bf16[128,64]{0,1:T(8,128)(2,1)}, u32[]{:S(2)}) copy-start(bf16[128,64]{0,1:T(8,128)(2,1)} %param.16) | copy-start | bytes 49156
  14.4 49.4 %all-to-all-start = ((bf16[32,136,128]{2,1,0:T(8,128)(2,1)}), bf16[32,136,128]{2,1,0:T(8,128)(2,1)S(1)}, u32[]{:S(2)}, u32[]{:S(2)}) async-start(bf16[32,136,128]{2,1,0:T(8,128)(2,1)} %pad_maximum_fusion), calls=%async_computation | async-start | bytes 2228224 | tf_op jit(solution)/shard_map/all_to_all | solution.py:733
  17.2 36.7 %copy-start.18 = (s32[32]{0:T(128)S(1)}, s32[32]{0:T(128)}, u32[]{:S(2)}) copy-start(s32[32]{0:T(128)} %param.14) | copy-start | bytes 388
  17.2 39.2 %copy-start.19 = (s32[32]{0:T(128)S(1)}, s32[32]{0:T(128)}, u32[]{:S(2)}) copy-start(s32[32]{0:T(128)} %param.12) | copy-start | bytes 388
  17.2 40.5 %copy-start.20 = (s32[32]{0:T(128)S(1)}, s32[32]{0:T(128)}, u32[]{:S(2)}) copy-start(s32[32]{0:T(128)} %param.13) | copy-start | bytes 388
  17.3 25.1 %collective-permute-start.1 = (bf16[64,768]{1,0:T(8,128)(2,1)S(1)}, bf16[64,768]{1,0:T(8,128)(2,1)S(1)}, u32[]{:S(2)}, u32[]{:S(2)}) collective-permute-start(bf16[64,768]{1,0:T(8,128)(2,1)S(1)} %constant_dynamic-update-slice_fusion), channel_id=1, source_target_pairs={{0,8},{4,12},{8,16},{12,20},{16,24},{20,28},{24,0},{28,4},{1,9},{5... | collective-permute-start | bytes 294920 | tf_op jit(solution)/shard_map/ppermute | solution.py:591
  19.0 32.6 %collective-permute-start.2 = (bf16[64,768]{1,0:T(8,128)(2,1)S(1)}, bf16[64,768]{1,0:T(8,128)(2,1)S(1)}, u32[]{:S(2)}, u32[]{:S(2)}) collective-permute-start(bf16[64,768]{1,0:T(8,128)(2,1)S(1)} %constant_dynamic-update-slice_fusion), channel_id=1, source_target_pairs={{0,16},{4,20},{8,24},{12,28},{16,0},{20,4},{24,8},{28,12},{1,17},{... | collective-permute-start | bytes 294920 | tf_op jit(solution)/shard_map/ppermute | solution.py:591
  21.5 30.1 %collective-permute-start.3 = (bf16[64,768]{1,0:T(8,128)(2,1)S(1)}, bf16[64,768]{1,0:T(8,128)(2,1)S(1)}, u32[]{:S(2)}, u32[]{:S(2)}) collective-permute-start(bf16[64,768]{1,0:T(8,128)(2,1)S(1)} %constant_dynamic-update-slice_fusion), channel_id=1, source_target_pairs={{0,24},{4,28},{8,0},{12,4},{16,8},{20,12},{24,16},{28,20},{1,25},{... | collective-permute-start | bytes 294920 | tf_op jit(solution)/shard_map/ppermute | solution.py:591
  23.8 38.1 %collective-permute-start.10 = (bf16[256,1152]{1,0:T(8,128)(2,1)}, bf16[256,1152]{1,0:T(8,128)(2,1)}, u32[]{:S(2)}, u32[]{:S(2)}) collective-permute-start(bf16[256,1152]{1,0:T(8,128)(2,1)} %pad_maximum_fusion.1.refs_0_), channel_id=1, source_target_pairs={{0,2},{1,3},{2,0},{3,1},{4,6},{5,7},{6,4},{7,5},{8,10},{9,11},{10,... | collective-permute-start | bytes 1769480 | tf_op jit(solution)/shard_map/ppermute | solution.py:586
  25.3 36.6 %collective-permute-start.9 = (bf16[256,1152]{1,0:T(8,128)(2,1)}, bf16[256,1152]{1,0:T(8,128)(2,1)}, u32[]{:S(2)}, u32[]{:S(2)}) collective-permute-start(bf16[256,1152]{1,0:T(8,128)(2,1)} %pad_maximum_fusion.1.refs_0_), channel_id=1, source_target_pairs={{0,4},{4,0},{8,12},{12,8},{16,20},{20,16},{24,28},{28,24},{1,5},{5... | collective-permute-start | bytes 1769480 | tf_op jit(solution)/shard_map/ppermute | solution.py:591
  51.7 10.3 %collective-permute-start.5 = (bf16[512,384]{1,0:T(8,128)(2,1)S(1)}, bf16[512,384]{1,0:T(8,128)(2,1)S(1)}, u32[]{:S(2)}, u32[]{:S(2)}) collective-permute-start(bf16[512,384]{1,0:T(8,128)(2,1)S(1)} %slice_dynamic-update-slice_fusion.refs_0_), channel_id=1, source_target_pairs={{0,2},{1,3},{2,0},{3,1},{4,6},{5,7},{6,4},{7,5},{8,10},{9,11},{10,... | collective-permute-start | bytes 1179656 | tf_op jit(solution)/shard_map/ppermute | solution.py:586
  53.4 10.6 %collective-permute-start.4 = (bf16[512,384]{1,0:T(8,128)(2,1)S(1)}, bf16[512,384]{1,0:T(8,128)(2,1)S(1)}, u32[]{:S(2)}, u32[]{:S(2)}) collective-permute-start(bf16[512,384]{1,0:T(8,128)(2,1)S(1)} %slice_dynamic-update-slice_fusion.refs_0_), channel_id=1, source_target_pairs={{0,1},{1,0},{2,3},{3,2},{4,5},{5,4},{6,7},{7,6},{8,9},{9,8},{10,11... | collective-permute-start | bytes 1179656 | tf_op jit(solution)/shard_map/ppermute | solution.py:586
  53.4 33.6 %collective-permute-start.12 = (bf16[256,1152]{1,0:T(8,128)(2,1)}, bf16[256,1152]{1,0:T(8,128)(2,1)}, u32[]{:S(2)}, u32[]{:S(2)}) collective-permute-start(bf16[256,1152]{1,0:T(8,128)(2,1)} %pad_maximum_fusion.1.refs_0_), channel_id=1, source_target_pairs={{0,1},{1,0},{2,3},{3,2},{4,5},{5,4},{6,7},{7,6},{8,9},{9,8},{10,11... | collective-permute-start | bytes 1769480 | tf_op jit(solution)/shard_map/ppermute | solution.py:586
  62.0 25.1 %collective-permute-start.13 = (bf16[256,1152]{1,0:T(8,128)(2,1)}, bf16[256,1152]{1,0:T(8,128)(2,1)}, u32[]{:S(2)}, u32[]{:S(2)}) collective-permute-start(bf16[256,1152]{1,0:T(8,128)(2,1)} %collective-permute-done.9.refs_1_), channel_id=1, source_target_pairs={{0,1},{1,0},{2,3},{3,2},{4,5},{5,4},{6,7},{7,6},{8,9},{9,8},{10,11... | collective-permute-start | bytes 1769480 | tf_op jit(solution)/shard_map/ppermute | solution.py:586
  62.0 25.1 %collective-permute-start.15 = (bf16[256,1152]{1,0:T(8,128)(2,1)}, bf16[256,1152]{1,0:T(8,128)(2,1)}, u32[]{:S(2)}, u32[]{:S(2)}) collective-permute-start(bf16[256,1152]{1,0:T(8,128)(2,1)} %collective-permute-done.9.refs_1_), channel_id=1, source_target_pairs={{0,2},{1,3},{2,0},{3,1},{4,6},{5,7},{6,4},{7,5},{8,10},{9,11},{10,... | collective-permute-start | bytes 1769480 | tf_op jit(solution)/shard_map/ppermute | solution.py:586
  63.6 1.9 collective-permute-start.11
  64.0 23.0 %collective-permute-start.14 = (bf16[256,1152]{1,0:T(8,128)(2,1)}, bf16[256,1152]{1,0:T(8,128)(2,1)S(1)}, u32[]{:S(2)}, u32[]{:S(2)}) collective-permute-start(bf16[256,1152]{1,0:T(8,128)(2,1)} %collective-permute-done.10.refs_4_), channel_id=1, source_target_pairs={{0,1},{1,0},{2,3},{3,2},{4,5},{5,4},{6,7},{7,6},{8,9},{9,8},{10,11... | collective-permute-start | bytes 1769480 | tf_op jit(solution)/shard_map/ppermute | solution.py:586
  71.7 15.4 %copy-start.1 = (bf16[1024,1536]{1,0:T(8,128)(2,1)}, bf16[1024,1536]{1,0:T(8,128)(2,1)S(1)}, u32[]{:S(2)}) copy-start(bf16[1024,1536]{1,0:T(8,128)(2,1)S(1)} %get-tuple-element.68.q_ref.k_ref.v_ref) | copy-start | bytes 9437188
  87.1 0.8 copy-start.16
  87.1 2.3 %collective-permute-start.16 = (bf16[256,1152]{1,0:T(8,128)(2,1)}, bf16[256,1152]{1,0:T(8,128)(2,1)S(1)}, u32[]{:S(2)}, u32[]{:S(2)}) collective-permute-start(bf16[256,1152]{1,0:T(8,128)(2,1)} %collective-permute-done.15.refs_5_), channel_id=1, source_target_pairs={{0,1},{1,0},{2,3},{3,2},{4,5},{5,4},{6,7},{7,6},{8,9},{9,8},{10,11... | collective-permute-start | bytes 1769480 | tf_op jit(solution)/shard_map/ppermute | solution.py:586
  89.4 0.8 copy-start.17
  119.2 3.7 %collective-permute-start.18 = (bf16[2,512,512]{2,1,0:T(8,128)(2,1)}, bf16[2,512,512]{2,1,0:T(8,128)(2,1)S(1)}, u32[]{:S(2)}, u32[]{:S(2)}) collective-permute-start(bf16[2,512,512]{2,1,0:T(8,128)(2,1)} %get-tuple-element.86), channel_id=1, source_target_pairs={{0,1},{1,0},{2,3},{3,2},{4,5},{5,4},{6,7},{7,6},{8,9},{9,8},{10,11... | collective-permute-start | bytes 3145736 | tf_op jit(solution)/shard_map/ppermute | solution.py:586
  119.3 5.4 %collective-permute-start.17 = (bf16[2,512,640]{2,1,0:T(8,128)(2,1)}, bf16[2,512,640]{2,1,0:T(8,128)(2,1)}, u32[]{:S(2)}, u32[]{:S(2)}) collective-permute-start(bf16[2,512,640]{2,1,0:T(8,128)(2,1)} %get-tuple-element.81), channel_id=1, source_target_pairs={{0,1},{1,0},{2,3},{3,2},{4,5},{5,4},{6,7},{7,6},{8,9},{9,8},{10,11... | collective-permute-start | bytes 3932168 | tf_op jit(solution)/shard_map/ppermute | solution.py:586
  122.9 5.5 %copy-start.2 = (bf16[1024,1536]{1,0:T(8,128)(2,1)S(1)}, bf16[1024,1536]{1,0:T(8,128)(2,1)}, u32[]{:S(2)}) copy-start(bf16[1024,1536]{1,0:T(8,128)(2,1)} %copy-done.1) | copy-start | bytes 9437188
  122.9 5.5 %copy-start.6 = (bf16[512,1024]{1,0:T(8,128)(2,1)S(1)}, bf16[512,1024]{1,0:T(8,128)(2,1)}, u32[]{:S(2)}) copy-start(bf16[512,1024]{1,0:T(8,128)(2,1)} %get-tuple-element.82.turn_ref) | copy-start | bytes 3145732
  124.5 3.8 %copy-start.5 = (bf16[512,1024]{1,0:T(8,128)(2,1)S(1)}, bf16[512,1024]{1,0:T(8,128)(2,1)}, u32[]{:S(2)}) copy-start(bf16[512,1024]{1,0:T(8,128)(2,1)} %get-tuple-element.88.n_turn_ref) | copy-start | bytes 3145732
  124.5 18.7 %collective-permute-start.19 = (bf16[4,2,64,512]{3,2,1,0:T(8,128)(2,1)S(1)}, bf16[4,2,64,512]{3,2,1,0:T(8,128)(2,1)S(1)}, u32[]{:S(2)}, u32[]{:S(2)}) collective-permute-start(bf16[4,2,64,512]{3,2,1,0:T(8,128)(2,1)S(1)} %bitcast.117), channel_id=1, source_target_pairs={{0,2},{1,3},{2,0},{3,1},{4,6},{5,7},{6,4},{7,5},{8,10},{9,11},{10,... | collective-permute-start | bytes 1572872 | tf_op jit(solution)/shard_map/ppermute | solution.py:586
  126.3 17.0 %collective-permute-start.20 = (bf16[2,4,64,640]{3,2,1,0:T(8,128)(2,1)S(1)}, bf16[2,4,64,640]{3,2,1,0:T(8,128)(2,1)S(1)}, u32[]{:S(2)}, u32[]{:S(2)}) collective-permute-start(bf16[2,4,64,640]{3,2,1,0:T(8,128)(2,1)S(1)} %fusion.1), channel_id=1, source_target_pairs={{0,4},{4,0},{8,12},{12,8},{16,20},{20,16},{24,28},{28,24},{1,5},{5... | collective-permute-start | bytes 1966088 | tf_op jit(solution)/shard_map/ppermute | solution.py:591
  128.3 15.0 %copy-start.8 = (bf16[2,512,640]{2,1,0:T(8,128)(2,1)S(1)}, bf16[2,512,640]{2,1,0:T(8,128)(2,1)}, u32[]{:S(2)}) copy-start(bf16[2,512,640]{2,1,0:T(8,128)(2,1)} %get-tuple-element.80) | copy-start | bytes 3932164
  143.3 7.5 %collective-permute-start.21 = (bf16[512,384]{1,0:T(8,128)(2,1)S(1)}, bf16[512,384]{1,0:T(8,128)(2,1)S(1)}, u32[]{:S(2)}, u32[]{:S(2)}) collective-permute-start(bf16[512,384]{1,0:T(8,128)(2,1)S(1)} %get-tuple-element.97), channel_id=1, source_target_pairs={{0,1},{1,0},{2,3},{3,2},{4,5},{5,4},{6,7},{7,6},{8,9},{9,8},{10,11... | collective-permute-start | bytes 1179656 | tf_op jit(solution)/shard_map/ppermute | solution.py:586
  144.7 21.9 %collective-permute-start.22 = (bf16[4,64,640]{2,1,0:T(8,128)(2,1)S(1)}, bf16[4,64,640]{2,1,0:T(8,128)(2,1)S(1)}, u32[]{:S(2)}, u32[]{:S(2)}) collective-permute-start(bf16[4,64,640]{2,1,0:T(8,128)(2,1)S(1)} %slice_bitcast_fusion), channel_id=1, source_target_pairs={{0,2},{1,3},{2,0},{3,1},{4,6},{5,7},{6,4},{7,5},{8,10},{9,11},{10,... | collective-permute-start | bytes 983048 | tf_op jit(solution)/shard_map/ppermute | solution.py:586
  146.2 6.2 %copy-start.7 = (bf16[1024,512]{1,0:T(8,128)(2,1)S(1)}, bf16[1024,512]{1,0:T(8,128)(2,1)}, u32[]{:S(2)}) copy-start(bf16[1024,512]{1,0:T(8,128)(2,1)} %get-tuple-element.98.cg_ref) | copy-start | bytes 3145732
  146.3 20.3 %collective-permute-start.24 = (bf16[2,64,512]{2,1,0:T(8,128)(2,1)S(1)}, bf16[2,64,512]{2,1,0:T(8,128)(2,1)S(1)}, u32[]{:S(2)}, u32[]{:S(2)}) collective-permute-start(bf16[2,64,512]{2,1,0:T(8,128)(2,1)S(1)} %get-tuple-element.190), channel_id=1, source_target_pairs={{0,8},{4,12},{8,16},{12,20},{16,24},{20,28},{24,0},{28,4},{1,9},{5... | collective-permute-start | bytes 393224 | tf_op jit(solution)/shard_map/ppermute | solution.py:591
  148.3 18.3 %collective-permute-start.25 = (bf16[2,64,512]{2,1,0:T(8,128)(2,1)S(1)}, bf16[2,64,512]{2,1,0:T(8,128)(2,1)S(1)}, u32[]{:S(2)}, u32[]{:S(2)}) collective-permute-start(bf16[2,64,512]{2,1,0:T(8,128)(2,1)S(1)} %get-tuple-element.189), channel_id=1, source_target_pairs={{0,16},{4,20},{8,24},{12,28},{16,0},{20,4},{24,8},{28,12},{1,17},{... | collective-permute-start | bytes 393224 | tf_op jit(solution)/shard_map/ppermute | solution.py:591
  150.5 16.1 %collective-permute-start.26 = (bf16[2,64,512]{2,1,0:T(8,128)(2,1)S(1)}, bf16[2,64,512]{2,1,0:T(8,128)(2,1)S(1)}, u32[]{:S(2)}, u32[]{:S(2)}) collective-permute-start(bf16[2,64,512]{2,1,0:T(8,128)(2,1)S(1)} %get-tuple-element.188), channel_id=1, source_target_pairs={{0,24},{4,28},{8,0},{12,4},{16,8},{20,12},{24,16},{28,20},{1,25},{... | collective-permute-start | bytes 393224 | tf_op jit(solution)/shard_map/ppermute | solution.py:591
  150.8 15.8 %collective-permute-start.23 = (bf16[512,384]{1,0:T(8,128)(2,1)S(1)}, bf16[512,384]{1,0:T(8,128)(2,1)S(1)}, u32[]{:S(2)}, u32[]{:S(2)}) collective-permute-start(bf16[512,384]{1,0:T(8,128)(2,1)S(1)} %add_convert_fusion.3), channel_id=1, source_target_pairs={{0,2},{1,3},{2,0},{3,1},{4,6},{5,7},{6,4},{7,5},{8,10},{9,11},{10,... | collective-permute-start | bytes 1179656 | tf_op jit(solution)/shard_map/ppermute | solution.py:586
  152.4 16.7 %copy-start.4 = (bf16[512,1536]{1,0:T(8,128)(2,1)S(1)}, bf16[512,1536]{1,0:T(8,128)(2,1)}, u32[]{:S(2)}) copy-start(bf16[512,1536]{1,0:T(8,128)(2,1)} %get-tuple-element.108.w_ref) | copy-start | bytes 4718596
  166.7 2.4 %copy-start.3 = (f32[1024,512]{1,0:T(8,128)S(1)}, f32[1024,512]{1,0:T(8,128)}, u32[]{:S(2)}) copy-start(f32[1024,512]{1,0:T(8,128)} %get-tuple-element.107.mg_ref) | copy-start | bytes 6291460
  168.2 6.4 %collective-permute-start.28 = (bf16[64,640]{1,0:T(8,128)(2,1)S(1)}, bf16[64,640]{1,0:T(8,128)(2,1)S(1)}, u32[]{:S(2)}, u32[]{:S(2)}) collective-permute-start(bf16[64,640]{1,0:T(8,128)(2,1)S(1)} %get-tuple-element.195), channel_id=1, source_target_pairs={{0,16},{4,20},{8,24},{12,28},{16,0},{20,4},{24,8},{28,12},{1,17},{... | collective-permute-start | bytes 245768 | tf_op jit(solution)/shard_map/ppermute | solution.py:591
  169.0 5.5 %collective-permute-start.27 = (bf16[512,384]{1,0:T(8,128)(2,1)S(1)}, bf16[512,384]{1,0:T(8,128)(2,1)S(1)}, u32[]{:S(2)}, u32[]{:S(2)}) collective-permute-start(bf16[512,384]{1,0:T(8,128)(2,1)S(1)} %get-tuple-element.110), channel_id=1, source_target_pairs={{0,1},{1,0},{2,3},{3,2},{4,5},{5,4},{6,7},{7,6},{8,9},{9,8},{10,11... | collective-permute-start | bytes 1179656 | tf_op jit(solution)/shard_map/ppermute | solution.py:586
  174.6 0.6 copy-start.13
  175.2 0.7 copy-start.9
  175.9 40.6 %all-to-all-start.1 = ((bf16[32,136,128]{2,1,0:T(8,128)(2,1)}), bf16[32,136,128]{2,1,0:T(8,128)(2,1)S(1)}, u32[]{:S(2)}, u32[]{:S(2)}) async-start(bf16[32,136,128]{2,1,0:T(8,128)(2,1)} %bitcast.25), calls=%async_computation.1 | async-start | bytes 2228224 | tf_op jit(solution)/shard_map/all_to_all | solution.py:799
  182.1 13.1 %collective-permute-start.31 = (bf16[4,64,384]{2,1,0:T(8,128)(2,1)}, bf16[4,64,384]{2,1,0:T(8,128)(2,1)S(1)}, u32[]{:S(2)}, u32[]{:S(2)}) collective-permute-start(bf16[4,64,384]{2,1,0:T(8,128)(2,1)} %fusion.4), channel_id=1, source_target_pairs={{0,4},{4,0},{8,12},{12,8},{16,20},{20,16},{24,28},{28,24},{1,5},{5... | collective-permute-start | bytes 589832 | tf_op jit(solution)/shard_map/ppermute | solution.py:591
  183.8 30.7 %copy-start.14 = (bf16[64,640]{1,0:T(8,128)(2,1)S(1)}, bf16[64,640]{1,0:T(8,128)(2,1)}, u32[]{:S(2)}) copy-start(bf16[64,640]{1,0:T(8,128)(2,1)} %copy-done.13) | copy-start | bytes 245764
  183.8 17.2 %collective-permute-start.35 = (bf16[1,64,512]{2,1,0:T(8,128)(2,1)}, bf16[1,64,512]{2,1,0:T(8,128)(2,1)S(1)}, u32[]{:S(2)}, u32[]{:S(2)}) collective-permute-start(bf16[1,64,512]{2,1,0:T(8,128)(2,1)} %dynamic-slice_convert_fusion), channel_id=1, source_target_pairs={{0,4},{4,0},{8,12},{12,8},{16,20},{20,16},{24,28},{28,24},{1,5},{5... | collective-permute-start | bytes 196616 | tf_op jit(solution)/shard_map/ppermute | solution.py:591
  184.2 20.4 %collective-permute-start.29 = (bf16[64,640]{1,0:T(8,128)(2,1)}, bf16[64,640]{1,0:T(8,128)(2,1)S(1)}, u32[]{:S(2)}, u32[]{:S(2)}) collective-permute-start(bf16[64,640]{1,0:T(8,128)(2,1)} %get-tuple-element.193), channel_id=1, source_target_pairs={{0,8},{4,12},{8,16},{12,20},{16,24},{20,28},{24,0},{28,4},{1,9},{5... | collective-permute-start | bytes 245768 | tf_op jit(solution)/shard_map/ppermute | solution.py:591
  185.9 18.6 %collective-permute-start.30 = (bf16[64,640]{1,0:T(8,128)(2,1)}, bf16[64,640]{1,0:T(8,128)(2,1)S(1)}, u32[]{:S(2)}, u32[]{:S(2)}) collective-permute-start(bf16[64,640]{1,0:T(8,128)(2,1)} %get-tuple-element.192), channel_id=1, source_target_pairs={{0,24},{4,28},{8,0},{12,4},{16,8},{20,12},{24,16},{28,20},{1,25},{... | collective-permute-start | bytes 245768 | tf_op jit(solution)/shard_map/ppermute | solution.py:591
  196.3 11.2 %collective-permute-start.32 = (bf16[64,384]{1,0:T(8,128)(2,1)S(1)}, bf16[64,384]{1,0:T(8,128)(2,1)S(1)}, u32[]{:S(2)}, u32[]{:S(2)}) collective-permute-start(bf16[64,384]{1,0:T(8,128)(2,1)S(1)} %get-tuple-element.198), channel_id=1, source_target_pairs={{0,8},{4,12},{8,16},{12,20},{16,24},{20,28},{24,0},{28,4},{1,9},{5... | collective-permute-start | bytes 147464 | tf_op jit(solution)/shard_map/ppermute | solution.py:591
  197.5 17.0 %collective-permute-start.33 = (bf16[64,384]{1,0:T(8,128)(2,1)S(1)}, bf16[64,384]{1,0:T(8,128)(2,1)S(1)}, u32[]{:S(2)}, u32[]{:S(2)}) collective-permute-start(bf16[64,384]{1,0:T(8,128)(2,1)S(1)} %get-tuple-element.197), channel_id=1, source_target_pairs={{0,16},{4,20},{8,24},{12,28},{16,0},{20,4},{24,8},{28,12},{1,17},{... | collective-permute-start | bytes 147464 | tf_op jit(solution)/shard_map/ppermute | solution.py:591
  201.1 13.4 %collective-permute-start.34 = (bf16[64,384]{1,0:T(8,128)(2,1)S(1)}, bf16[64,384]{1,0:T(8,128)(2,1)S(1)}, u32[]{:S(2)}, u32[]{:S(2)}) collective-permute-start(bf16[64,384]{1,0:T(8,128)(2,1)S(1)} %get-tuple-element.196), channel_id=1, source_target_pairs={{0,24},{4,28},{8,0},{12,4},{16,8},{20,12},{24,16},{28,20},{1,25},{... | collective-permute-start | bytes 147464 | tf_op jit(solution)/shard_map/ppermute | solution.py:591

commit v14 on v13

--- a/solution.py
+++ b/solution.py
@@ -14,6 +14,7 @@
 KEYS = 256
 BACK_KEYS = 512
 SPARE = 8
+UNITS = 2048
 SCORE_SCALE = 1.0 / math.sqrt(HEAD_DIM)
 LOG2E = math.log2(math.e)
 F32 = jnp.float32
@@ -238,20 +239,19 @@
 def middle_kernel(
     groups, limit_ref, place_ref, x_ref, clock_ref, gain_ref, ctx_ref, og_ref, *refs
 ):
-    weight_refs, refs = refs[:-17], refs[-17:]
+    weight_refs, refs = refs[:-18], refs[-18:]
     out_ref, cg_ref, mg_ref, gg_ref, up_send, down_send, up_keep, down_keep = refs[:8]
-    wide, units, active_s, ug_s, n_turn, fg_turn, ag_turn, ctx_s, sems = refs[8:]
+    wide, ups, downs, active_s, ug_s, n_turn, fg_turn, ag_turn, ctx_s, sems = refs[8:]
     step = pl.program_id(0)
-    parts, _, hidden = active_s.shape
+    parts = ctx_s.shape[0]
+    hidden = active_s.shape[1] // parts
     blocks = pl.num_programs(0) - parts
     each = len(weight_refs) // parts
 
     def fetch(part, kind):
-        target, wide_, own = (
-            (wide, PAIR, slice(0, PAIR)),
-            (units, 2 * hidden, slice(PAIR, PAIR + 2 * hidden)),
-        )[kind]
-        columns = slice(part * wide_, (part + 1) * wide_)
+        target, width, first = ((wide, PAIR, 0), (ups, hidden, PAIR), (downs, hidden, PAIR + hidden))[kind]
+        own = slice(first, first + width)
+        columns = slice(part * width, (part + 1) * width)
         copies = []
         for at, w_ref in enumerate(weight_refs[part * each : (part + 1) * each]):
             count = 1 if groups is None else groups // each
@@ -274,10 +274,10 @@
     def _():
         gg_ref[...] = jnp.zeros_like(gg_ref)
         for part in range(parts):
-            for copy in fetch(part, 0) + fetch(part, 1):
+            for copy in fetch(part, 0) + fetch(part, 1) + fetch(part, 2):
                 copy.start()
         for part in range(parts):
-            for copy in fetch(part, 0) + fetch(part, 1):
+            for copy in fetch(part, 0) + fetch(part, 1) + fetch(part, 2):
                 copy.wait()
 
     dead = (step < blocks) & (step * ROWS >= limit_ref[0])
@@ -297,17 +297,15 @@
         fg_turn[:, spot] = feed_grad.T
         feed = jnp.zeros_like(middle)
         two_grad = jnp.zeros_like(middle)
-        for part in range(parts):
-            up = slice(2 * part * hidden, (2 * part + 1) * hidden)
-            down = slice((2 * part + 1) * hidden, (2 * part + 2) * hidden)
-            upper = mul(normed, units[:, up])
-            active, slope = gelu_both(upper)
+        for at in range(0, parts * hidden, UNITS):
+            some = slice(at, at + UNITS)
+            active, slope = gelu_both(mul(normed, ups[:, some]))
             active = active.astype(BF16)
-            active_s[part, spot] = active
-            feed += mul(active, units[:, down], NT)
-            upper_grad = (mul(feed_grad, units[:, down]) * slope).astype(BF16)
-            ug_s[part, spot] = upper_grad
-            two_grad += mul(upper_grad, units[:, up], NT)
+            active_s[spot, some] = active
+            feed += mul(active, downs[:, some], NT)
+            upper_grad = (mul(feed_grad, downs[:, some]) * slope).astype(BF16)
+            ug_s[spot, some] = upper_grad
+            two_grad += mul(upper_grad, ups[:, some], NT)
         out_ref[0] = jnp.where(live, middle + feed, 0.0).astype(BF16)
         gg_ref[...] += jnp.sum(two_grad * unit, axis=0, keepdims=True)
         middle_grad = res_grad + norm_back(two_grad, gain, unit, inverse)
@@ -323,8 +321,9 @@
         spot = pl.ds(pl.multiple_of(step * ROWS, ROWS), ROWS)
         for ref in (out_ref, cg_ref, mg_ref):
             ref[...] = jnp.zeros_like(ref)
-        for ref in (active_s, ug_s, ctx_s):
-            ref[:, spot] = jnp.zeros((ref.shape[0], ROWS, ref.shape[2]), BF16)
+        for ref in (active_s, ug_s):
+            ref[spot] = jnp.zeros((ROWS, ref.shape[1]), BF16)
+        ctx_s[:, spot] = jnp.zeros((parts, ROWS, PAIR), BF16)
         for ref in (n_turn, fg_turn, ag_turn):
             ref[:, spot] = jnp.zeros((ref.shape[0], ROWS), BF16)
 
@@ -332,10 +331,11 @@
     def _():
         turn = step - blocks
         part = jnp.where(turn < 2, 3 - 2 * turn, 6 - 2 * turn)
+        own = pl.ds(pl.multiple_of(part * hidden, hidden), hidden)
         grads = (
             mul(ag_turn[...], ctx_s[part]).astype(BF16),
-            mul(n_turn[...], ug_s[part]).astype(BF16),
-            mul(fg_turn[...], active_s[part]).astype(BF16),
+            mul(n_turn[...], ug_s[:, own]).astype(BF16),
+            mul(fg_turn[...], active_s[:, own]).astype(BF16),
         )
 
         def into(up_ref, down_ref):
@@ -389,14 +389,15 @@
             ],
             scratch_shapes=[
                 pltpu.VMEM((features, parts * PAIR), BF16),
-                pltpu.VMEM((features, parts * 2 * hidden), BF16),
-                pltpu.VMEM((parts, length, hidden), BF16),
-                pltpu.VMEM((parts, length, hidden), BF16),
+                pltpu.VMEM((features, parts * hidden), BF16),
+                pltpu.VMEM((features, parts * hidden), BF16),
+                pltpu.VMEM((length, parts * hidden), BF16),
+                pltpu.VMEM((length, parts * hidden), BF16),
                 pltpu.VMEM((features, length), BF16),
                 pltpu.VMEM((features, length), BF16),
                 pltpu.VMEM((features, length), BF16),
                 pltpu.VMEM((parts, length, PAIR), BF16),
-                pltpu.SemaphoreType.DMA((2, parts, groups or 1)),
+                pltpu.SemaphoreType.DMA((3, parts, groups or 1)),
             ],
         ),
         out_shape=[

time: 220 us -> 219 us (level)
  Pallas kernels: 84.8 us -> 75.9 us
  starting transfers between devices: 50.4 us -> 57.5 us
  waiting for transfers between devices: 53.7 us -> 56.4 us
    ppermute x16, starting transfers between devices: 9.55 us -> 16.1 us  [swap(): return lax.ppermute(value, 'tensor', [(i, i ^ apart) for i in range(count)])]
    pallas_call x1, Pallas kernels: 29 us -> 22.8 us  [middle_block(): pl.pallas_call(functools.partial(middle_kernel, groups), grid_spec=pltpu....]
    ppermute x20, waiting for transfers between devices: 44.7 us -> 47 us  [along_dp(): return lax.ppermute(value, 'dp', [(i, move(i)) for i in range(count)])]
  transfers between devices with their start and end apart: 38 -> 38, of which waited for: 11 -> 12; matrix products, arithmetic and copies ran while one was open for 8% -> 8% of each run, Pallas kernels for 25% -> 24%
where the time goes in v14:
time: 219 us
  Pallas kernels  75.9 us (35%)
  starting transfers between devices  57.5 us (26%)
  waiting for transfers between devices  56.4 us (26%)
  other arithmetic  13.5 us (6%)
  local copies, waits for them, and re-layouts  12.1 us (6%)
  between operations  3.77 us (2%)
    ppermute x20, waiting for transfers between devices, along_dp(): return lax.ppermute(value, 'dp', [(i, move(i)) for i in range(count)])  47 us
    ppermute x20, starting transfers between devices, along_dp(): return lax.ppermute(value, 'dp', [(i, move(i)) for i in range(count)])  34.1 us
    pallas_call x2, Pallas kernels, attend_back(): pl.pallas_call(attend_back_kernel, grid_spec=pltpu.PrefetchScalarGridSpec...  29.1 us
    pallas_call x1, Pallas kernels, middle_block(): pl.pallas_call(functools.partial(middle_kernel, groups), grid_spec=pltpu....  22.8 us
    ppermute x16, starting transfers between devices, swap(): return lax.ppermute(value, 'tensor', [(i, i ^ apart) for i in range(count)])  16.1 us
    pallas_call x1, Pallas kernels, attend(): pl.pallas_call(attend_kernel, grid_spec=pltpu.PrefetchScalarGridSpec(num_...  15.4 us
    ppermute x16, waiting for transfers between devices, swap(): return lax.ppermute(value, 'tensor', [(i, i ^ apart) for i in range(count)])  9.4 us
    convert_element_type x7, other arithmetic, add(): return add_wide(*values).astype(BF16)  5.84 us
  transfers between devices with their start and end apart: 38, of which 12 were waited for; matrix products, arithmetic and copies ran while one was open for 8% of the time, Pallas kernels for 24%

profile of v14, /device:TPU:0, one launch (start us, length us, event | category | flops | bytes accessed | tf_op | source)
XLA Modules:
  0.0 219.1 jit_solution(16053838413229667255)
XLA Ops:
  0.6 1.0 pad_maximum_fusion.2
  1.6 3.1 %collective-permute-start.6 = (bf16[64,1152]{1,0:T(8,128)(2,1)S(1)}, bf16[64,1152]{1,0:T(8,128)(2,1)S(1)}, u32[]{:S(2)}, u32[]{:S(2)}) collective-permute-start(bf16[64,1152]{1,0:T(8,128)(2,1)S(1)} %pad_maximum_fusion.2), channel_id=1, source_target_pairs={{0,8},{4,12},{8,16},{12,20},{16,24},{20,28},{24,0},{28,4},{1,9},{5... | collective-permute-start | bytes 442376 | tf_op jit(solution)/shard_map/ppermute | solution.py:592
  4.7 2.6 %collective-permute-start.7 = (bf16[64,1152]{1,0:T(8,128)(2,1)S(1)}, bf16[64,1152]{1,0:T(8,128)(2,1)S(1)}, u32[]{:S(2)}, u32[]{:S(2)}) collective-permute-start(bf16[64,1152]{1,0:T(8,128)(2,1)S(1)} %pad_maximum_fusion.2), channel_id=1, source_target_pairs={{0,16},{4,20},{8,24},{12,28},{16,0},{20,4},{24,8},{28,12},{1,17},{... | collective-permute-start | bytes 442376 | tf_op jit(solution)/shard_map/ppermute | solution.py:592
  7.3 1.3 collective-permute-start.8
  8.6 0.8 copy_bitcast_fusion.1
  9.4 1.5 collective-permute-start
  11.0 0.7 fusion.9
  11.8 0.7 compare_select_fusion.1
  12.5 0.7 gather_fusion
  13.2 1.1 pad_maximum_fusion
  14.4 2.8 %all-to-all-start = ((bf16[32,136,128]{2,1,0:T(8,128)(2,1)}), bf16[32,136,128]{2,1,0:T(8,128)(2,1)S(1)}, u32[]{:S(2)}, u32[]{:S(2)}) async-start(bf16[32,136,128]{2,1,0:T(8,128)(2,1)} %pad_maximum_fusion), calls=%async_computation | async-start | bytes 2228224 | tf_op jit(solution)/shard_map/all_to_all | solution.py:734
  17.3 1.7 collective-permute-start.1
  19.0 2.5 %collective-permute-start.2 = (bf16[64,768]{1,0:T(8,128)(2,1)S(1)}, bf16[64,768]{1,0:T(8,128)(2,1)S(1)}, u32[]{:S(2)}, u32[]{:S(2)}) collective-permute-start(bf16[64,768]{1,0:T(8,128)(2,1)S(1)} %constant_dynamic-update-slice_fusion), channel_id=1, source_target_pairs={{0,16},{4,20},{8,24},{12,28},{16,0},{20,4},{24,8},{28,12},{1,17},{... | collective-permute-start | bytes 294920 | tf_op jit(solution)/shard_map/ppermute | solution.py:592
  21.5 1.4 collective-permute-start.3
  23.0 0.9 pad_maximum_fusion.1.refs_0_
  23.8 1.5 collective-permute-start.10
  25.3 1.5 collective-permute-start.9
  26.8 15.6 %collective-permute-done.1 = bf16[64,768]{1,0:T(8,128)(2,1)S(1)} collective-permute-done((bf16[64,768]{1,0:T(8,128)(2,1)S(1)}, bf16[64,768]{1,0:T(8,128)(2,1)S(1)}, u32[]{:S(2)}, u32[]{:S(2)}) %collective-permute-start.1) | collective-permute-done | bytes 98336 | tf_op jit(solution)/shard_map/ppermute | solution.py:592
  42.4 9.2 %collective-permute-done.2 = bf16[64,768]{1,0:T(8,128)(2,1)S(1)} collective-permute-done((bf16[64,768]{1,0:T(8,128)(2,1)S(1)}, bf16[64,768]{1,0:T(8,128)(2,1)S(1)}, u32[]{:S(2)}, u32[]{:S(2)}) %collective-permute-start.2) | collective-permute-done | bytes 98336 | tf_op jit(solution)/shard_map/ppermute | solution.py:592
  51.7 1.6 collective-permute-start.5
  58.4 3.6 %collective-permute-done.5.refs_2_ = bf16[512,384]{1,0:T(8,128)(2,1)S(1)} collective-permute-done((bf16[512,384]{1,0:T(8,128)(2,1)S(1)}, bf16[512,384]{1,0:T(8,128)(2,1)S(1)}, u32[]{:S(2)}, u32[]{:S(2)}) %collective-permute-start.5) | collective-permute-done | bytes 393248 | tf_op jit(solution)/shard_map/ppermute | solution.py:587
  62.0 1.6 collective-permute-start.15
  64.5 1.0 collective-permute-done.11.refs_3_
  65.4 5.1 %project.1 = (bf16[1024,1536]{1,0:T(8,128)(2,1)S(1)}, bf16[512,1024]{1,0:T(8,128)(2,1)}, bf16[512,1536]{1,0:T(8,128)(2,1)}) custom-call(s32[1]{0:T(128)} %dynamic-slice.9.limit_ref, s32[8]{0:T(128)S(1)} %pad_add_fusion.place_ref, bf16[8,4,136,128]{3,2,1,0:T(8,128)(2,1)S(1)} %bitcast.109, f32[1,512]{1,0:T(1,128)S(1)} %pad_maximum_fusion.3.clock_ref, ...), custom_call_target="tpu_custom_call" | custom-call | flops 5750000128 | bytes 1048576 | tf_op jit(solution)/shard_map/project/pallas_call | solution.py:111
  70.6 15.4 %attend.1 = (bf16[1024,512]{1,0:T(8,128)(2,1)}, bf16[512,1024]{1,0:T(8,128)(2,1)}, f32[4,2,1024]{2,1,0:T(2,128)S(1)}) custom-call(s32[1]{0:T(128)} %dynamic-slice.9.limit_ref, bf16[1024,1536]{1,0:T(8,128)(2,1)S(1)} %get-tuple-element.68.q_ref.k_ref.v_ref, bf16[1024,1536]{1,0:T(8,128)(2,1)S(1)} %get-tuple-element.68.q_ref.k_ref.v_ref, ...), custom_call_target="tpu_custom_call" | custom-call | flops 17250000896 | bytes 1048576 | tf_op jit(solution)/shard_map/attend/pallas_call | solution.py:200
  86.0 1.3 collective-permute-start.16
  87.5 1.7 collective-permute-done.16.refs_7_
  89.2 0.8 copy-done.17
  90.0 22.8 %middle.1 = (bf16[1,1024,512]{2,1,0:T(8,128)(2,1)}, bf16[1024,512]{1,0:T(8,128)(2,1)}, f32[1024,512]{1,0:T(8,128)}, f32[1,512]{1,0:T(1,128)S(1)}, bf16[2,512,640...) custom-call(s32[1]{0:T(128)} %dynamic-slice.9.limit_ref, ...), custom_call_target="tpu_custom_call" | custom-call | flops 28750000128 | bytes 1048576 | tf_op jit(solution)/shard_map/middle/pallas_call | solution.py:370
  112.8 6.0 %collective-permute-start.18 = (bf16[2,512,512]{2,1,0:T(8,128)(2,1)}, bf16[2,512,512]{2,1,0:T(8,128)(2,1)S(1)}, u32[]{:S(2)}, u32[]{:S(2)}) collective-permute-start(bf16[2,512,512]{2,1,0:T(8,128)(2,1)} %get-tuple-element.86), channel_id=1, source_target_pairs={{0,1},{1,0},{2,3},{3,2},{4,5},{5,4},{6,7},{7,6},{8,9},{9,8},{10,11... | collective-permute-start | bytes 3145736 | tf_op jit(solution)/shard_map/ppermute | solution.py:587
  118.9 3.1 %collective-permute-done.18 = bf16[2,512,512]{2,1,0:T(8,128)(2,1)S(1)} collective-permute-done((bf16[2,512,512]{2,1,0:T(8,128)(2,1)}, bf16[2,512,512]{2,1,0:T(8,128)(2,1)S(1)}, u32[]{:S(2)}, u32[]{:S(2)}) %collective-permute-start.18) | collective-permute-done | bytes 1048608 | tf_op jit(solution)/shard_map/ppermute | solution.py:587
  122.0 1.6 convert_add_fusion
  124.1 1.4 fusion.1
  125.5 1.5 collective-permute-start.20
  127.0 14.9 %attend_back.2 = (bf16[1024,768]{1,0:T(8,128)(2,1)S(1)}, bf16[512,384]{1,0:T(8,128)(2,1)S(1)}, bf16[512,384]{1,0:T(8,128)(2,1)S(1)}) custom-call(s32[1]{0:T(128)} %dynamic-slice.9.limit_ref, bf16[1024,1536]{1,0:T(8,128)(2,1)S(1)} %copy-done.2, bf16[1024,1536]{1,0:T(8,128)(2,1)S(1)} %copy-done.2, bf16[1024,1536]{1,0:T(8,128)(2,1)S(1)} %copy-done.2, ...), custom_call_target="tpu_custom_call" | custom-call | flops 18400000000 | bytes 1048576 | tf_op jit(solution)/shard_map/attend_back/pallas_call | solution.py:466
  142.3 1.3 fusion
  143.7 1.7 collective-permute-start.22
  145.7 2.7 %collective-permute-start.24 = (bf16[2,64,512]{2,1,0:T(8,128)(2,1)S(1)}, bf16[2,64,512]{2,1,0:T(8,128)(2,1)S(1)}, u32[]{:S(2)}, u32[]{:S(2)}) collective-permute-start(bf16[2,64,512]{2,1,0:T(8,128)(2,1)S(1)} %get-tuple-element.190), channel_id=1, source_target_pairs={{0,8},{4,12},{8,16},{12,20},{16,24},{20,28},{24,0},{28,4},{1,9},{5... | collective-permute-start | bytes 393224 | tf_op jit(solution)/shard_map/ppermute | solution.py:592
  148.4 1.5 collective-permute-start.25
  149.9 0.9 collective-permute-start.26
  150.9 0.8 collective-permute-start.23
  151.7 14.2 %attend_back.3 = (bf16[1024,768]{1,0:T(8,128)(2,1)S(1)}, bf16[512,384]{1,0:T(8,128)(2,1)S(1)}, bf16[512,384]{1,0:T(8,128)(2,1)S(1)}) custom-call(s32[1]{0:T(128)} %dynamic-slice.9.limit_ref, bf16[1024,1536]{1,0:T(8,128)(2,1)S(1)} %copy-done.2, bf16[1024,1536]{1,0:T(8,128)(2,1)S(1)} %copy-done.2, bf16[1024,1536]{1,0:T(8,128)(2,1)S(1)} %copy-done.2, ...), custom_call_target="tpu_custom_call" | custom-call | flops 18400000000 | bytes 1048576 | tf_op jit(solution)/shard_map/attend_back/pallas_call | solution.py:466
  166.8 0.7 dynamic-slice_bitcast_fusion.4
  168.2 3.5 %begin_back.1 = bf16[8,4,136,128]{3,2,1,0:T(8,128)(2,1)} custom-call(s32[1]{0:T(128)} %dynamic-slice.9.limit_ref, bf16[8,4,136,128]{3,2,1,0:T(8,128)(2,1)S(1)} %bitcast.111, f32[1,512]{1,0:T(1,128)S(1)} %pad_maximum_fusion.3.clock_ref, f32[1,512]{1,0:T(1,128)S(1)} %reshape_squeeze.8.gain_ref, f32[1,512]{1,0:T(1,128)S(1)} %get-tuple-element.78.gg_two_ref, ...), custom_call_target="tpu_custom_call" | custom-call | flops 8049999872 | bytes 1048576 | tf_op jit(solution)/shard_map/begin_back/pallas_call | solution.py:554
  171.6 2.3 %collective-permute-done.28 = bf16[64,640]{1,0:T(8,128)(2,1)S(1)} collective-permute-done((bf16[64,640]{1,0:T(8,128)(2,1)S(1)}, bf16[64,640]{1,0:T(8,128)(2,1)S(1)}, u32[]{:S(2)}, u32[]{:S(2)}) %collective-permute-start.28) | collective-permute-done | bytes 81952 | tf_op jit(solution)/shard_map/ppermute | solution.py:592
  174.6 0.7 copy-done.9
  175.3 4.4 %all-to-all-start.1 = ((bf16[32,136,128]{2,1,0:T(8,128)(2,1)}), bf16[32,136,128]{2,1,0:T(8,128)(2,1)S(1)}, u32[]{:S(2)}, u32[]{:S(2)}) async-start(bf16[32,136,128]{2,1,0:T(8,128)(2,1)} %bitcast.25), calls=%async_computation.1 | async-start | bytes 2228224 | tf_op jit(solution)/shard_map/all_to_all | solution.py:800
  179.8 0.7 scatter_custom_fusion
  180.4 1.7 fusion.4
  182.1 1.8 collective-permute-start.31
  184.2 1.8 collective-permute-start.29
  186.0 2.1 collective-permute-start.30
  188.1 7.2 %collective-permute-done.31 = bf16[4,64,384]{2,1,0:T(8,128)(2,1)S(1)} collective-permute-done((bf16[4,64,384]{2,1,0:T(8,128)(2,1)}, bf16[4,64,384]{2,1,0:T(8,128)(2,1)S(1)}, u32[]{:S(2)}, u32[]{:S(2)}) %collective-permute-start.31) | collective-permute-done | bytes 196640 | tf_op jit(solution)/shard_map/ppermute | solution.py:592
  195.2 1.0 fusion.3
  196.3 1.2 collective-permute-start.32
  197.5 3.6 %collective-permute-start.33 = (bf16[64,384]{1,0:T(8,128)(2,1)S(1)}, bf16[64,384]{1,0:T(8,128)(2,1)S(1)}, u32[]{:S(2)}, u32[]{:S(2)}) collective-permute-start(bf16[64,384]{1,0:T(8,128)(2,1)S(1)} %get-tuple-element.197), channel_id=1, source_target_pairs={{0,16},{4,20},{8,24},{12,28},{16,0},{20,4},{24,8},{28,12},{1,17},{... | collective-permute-start | bytes 147464 | tf_op jit(solution)/shard_map/ppermute | solution.py:592
  201.6 0.7 add_bitcast_fusion
  202.3 2.3 %collective-permute-done.29 = bf16[64,640]{1,0:T(8,128)(2,1)S(1)} collective-permute-done((bf16[64,640]{1,0:T(8,128)(2,1)}, bf16[64,640]{1,0:T(8,128)(2,1)S(1)}, u32[]{:S(2)}, u32[]{:S(2)}) %collective-permute-start.29) | collective-permute-done | bytes 81952 | tf_op jit(solution)/shard_map/ppermute | solution.py:592
  204.6 2.9 %collective-permute-done.32 = bf16[64,384]{1,0:T(8,128)(2,1)S(1)} collective-permute-done((bf16[64,384]{1,0:T(8,128)(2,1)S(1)}, bf16[64,384]{1,0:T(8,128)(2,1)S(1)}, u32[]{:S(2)}, u32[]{:S(2)}) %collective-permute-start.32) | collective-permute-done | bytes 49184 | tf_op jit(solution)/shard_map/ppermute | solution.py:592
  207.5 7.1 %collective-permute-done.33 = bf16[64,384]{1,0:T(8,128)(2,1)S(1)} collective-permute-done((bf16[64,384]{1,0:T(8,128)(2,1)S(1)}, bf16[64,384]{1,0:T(8,128)(2,1)S(1)}, u32[]{:S(2)}, u32[]{:S(2)}) %collective-permute-start.33) | collective-permute-done | bytes 49184 | tf_op jit(solution)/shard_map/ppermute | solution.py:592
  214.6 0.7 slice.119
  215.9 0.7 copy_bitcast_fusion
  216.6 0.8 gather_fusion.1
  217.3 1.1 slice.117
  (125 shorter events, 9.3 us)
Async XLA Ops:
  0.6 11.8 %copy-start = (bf16[32,128,128]{2,1,0:T(8,128)(2,1)S(1)}, bf16[32,128,128]{2,1,0:T(8,128)(2,1)}, u32[]{:S(2)}) copy-start(bf16[32,128,128]{2,1,0:T(8,128)(2,1)} %param.11) | copy-start | bytes 3145732
  1.6 19.9 %collective-permute-start.6 = (bf16[64,1152]{1,0:T(8,128)(2,1)S(1)}, bf16[64,1152]{1,0:T(8,128)(2,1)S(1)}, u32[]{:S(2)}, u32[]{:S(2)}) collective-permute-start(bf16[64,1152]{1,0:T(8,128)(2,1)S(1)} %pad_maximum_fusion.2), channel_id=1, source_target_pairs={{0,8},{4,12},{8,16},{12,20},{16,24},{20,28},{24,0},{28,4},{1,9},{5... | collective-permute-start | bytes 442376 | tf_op jit(solution)/shard_map/ppermute | solution.py:592
  4.7 18.2 %collective-permute-start.7 = (bf16[64,1152]{1,0:T(8,128)(2,1)S(1)}, bf16[64,1152]{1,0:T(8,128)(2,1)S(1)}, u32[]{:S(2)}, u32[]{:S(2)}) collective-permute-start(bf16[64,1152]{1,0:T(8,128)(2,1)S(1)} %pad_maximum_fusion.2), channel_id=1, source_target_pairs={{0,16},{4,20},{8,24},{12,28},{16,0},{20,4},{24,8},{28,12},{1,17},{... | collective-permute-start | bytes 442376 | tf_op jit(solution)/shard_map/ppermute | solution.py:592
  7.3 15.7 %collective-permute-start.8 = (bf16[64,1152]{1,0:T(8,128)(2,1)S(1)}, bf16[64,1152]{1,0:T(8,128)(2,1)S(1)}, u32[]{:S(2)}, u32[]{:S(2)}) collective-permute-start(bf16[64,1152]{1,0:T(8,128)(2,1)S(1)} %pad_maximum_fusion.2), channel_id=1, source_target_pairs={{0,24},{4,28},{8,0},{12,4},{16,8},{20,12},{24,16},{28,20},{1,25},{... | collective-permute-start | bytes 442376 | tf_op jit(solution)/shard_map/ppermute | solution.py:592
  9.4 7.8 %collective-permute-start = (bf16[64,384]{1,0:T(8,128)(2,1)S(1)}, bf16[64,384]{1,0:T(8,128)(2,1)S(1)}, u32[]{:S(2)}, u32[]{:S(2)}) collective-permute-start(bf16[64,384]{1,0:T(8,128)(2,1)S(1)} %copy_bitcast_fusion.1), channel_id=1, source_target_pairs={{0,4},{4,0},{8,12},{12,8},{16,20},{20,16},{24,28},{28,24},{1,5},{5... | collective-permute-start | bytes 147464 | tf_op jit(solution)/shard_map/ppermute | solution.py:592
  14.4 2.8 %copy-start.12 = (bf16[64,3,128]{2,0,1:T(8,128)(2,1)S(1)}, bf16[64,3,128]{2,0,1:T(8,128)(2,1)}, u32[]{:S(2)}) copy-start(bf16[64,3,128]{2,0,1:T(8,128)(2,1)} %param.15) | copy-start | bytes 147460
  14.4 8.6 %copy-start.10 = (bf16[512,64]{0,1:T(8,128)(2,1)S(1)}, bf16[512,64]{0,1:T(8,128)(2,1)}, u32[]{:S(2)}) copy-start(bf16[512,64]{0,1:T(8,128)(2,1)} %param.18) | copy-start | bytes 196612
  14.4 8.6 %copy-start.11 = (bf16[64,512]{1,0:T(8,128)(2,1)S(1)}, bf16[64,512]{1,0:T(8,128)(2,1)}, u32[]{:S(2)}) copy-start(bf16[64,512]{1,0:T(8,128)(2,1)} %param.17) | copy-start | bytes 196612
  14.4 8.6 %copy-start.15 = (bf16[128,64]{0,1:T(8,128)(2,1)S(1)}, bf16[128,64]{0,1:T(8,128)(2,1)}, u32[]{:S(2)}) copy-start(bf16[128,64]{0,1:T(8,128)(2,1)} %param.16) | copy-start | bytes 49156
  14.4 49.4 %all-to-all-start = ((bf16[32,136,128]{2,1,0:T(8,128)(2,1)}), bf16[32,136,128]{2,1,0:T(8,128)(2,1)S(1)}, u32[]{:S(2)}, u32[]{:S(2)}) async-start(bf16[32,136,128]{2,1,0:T(8,128)(2,1)} %pad_maximum_fusion), calls=%async_computation | async-start | bytes 2228224 | tf_op jit(solution)/shard_map/all_to_all | solution.py:734
  17.2 36.7 %copy-start.18 = (s32[32]{0:T(128)S(1)}, s32[32]{0:T(128)}, u32[]{:S(2)}) copy-start(s32[32]{0:T(128)} %param.14) | copy-start | bytes 388
  17.2 39.2 %copy-start.19 = (s32[32]{0:T(128)S(1)}, s32[32]{0:T(128)}, u32[]{:S(2)}) copy-start(s32[32]{0:T(128)} %param.12) | copy-start | bytes 388
  17.2 40.5 %copy-start.20 = (s32[32]{0:T(128)S(1)}, s32[32]{0:T(128)}, u32[]{:S(2)}) copy-start(s32[32]{0:T(128)} %param.13) | copy-start | bytes 388
  17.3 25.1 %collective-permute-start.1 = (bf16[64,768]{1,0:T(8,128)(2,1)S(1)}, bf16[64,768]{1,0:T(8,128)(2,1)S(1)}, u32[]{:S(2)}, u32[]{:S(2)}) collective-permute-start(bf16[64,768]{1,0:T(8,128)(2,1)S(1)} %constant_dynamic-update-slice_fusion), channel_id=1, source_target_pairs={{0,8},{4,12},{8,16},{12,20},{16,24},{20,28},{24,0},{28,4},{1,9},{5... | collective-permute-start | bytes 294920 | tf_op jit(solution)/shard_map/ppermute | solution.py:592
  19.0 32.6 %collective-permute-start.2 = (bf16[64,768]{1,0:T(8,128)(2,1)S(1)}, bf16[64,768]{1,0:T(8,128)(2,1)S(1)}, u32[]{:S(2)}, u32[]{:S(2)}) collective-permute-start(bf16[64,768]{1,0:T(8,128)(2,1)S(1)} %constant_dynamic-update-slice_fusion), channel_id=1, source_target_pairs={{0,16},{4,20},{8,24},{12,28},{16,0},{20,4},{24,8},{28,12},{1,17},{... | collective-permute-start | bytes 294920 | tf_op jit(solution)/shard_map/ppermute | solution.py:592
  21.5 30.1 %collective-permute-start.3 = (bf16[64,768]{1,0:T(8,128)(2,1)S(1)}, bf16[64,768]{1,0:T(8,128)(2,1)S(1)}, u32[]{:S(2)}, u32[]{:S(2)}) collective-permute-start(bf16[64,768]{1,0:T(8,128)(2,1)S(1)} %constant_dynamic-update-slice_fusion), channel_id=1, source_target_pairs={{0,24},{4,28},{8,0},{12,4},{16,8},{20,12},{24,16},{28,20},{1,25},{... | collective-permute-start | bytes 294920 | tf_op jit(solution)/shard_map/ppermute | solution.py:592
  23.8 38.1 %collective-permute-start.10 = (bf16[256,1152]{1,0:T(8,128)(2,1)}, bf16[256,1152]{1,0:T(8,128)(2,1)}, u32[]{:S(2)}, u32[]{:S(2)}) collective-permute-start(bf16[256,1152]{1,0:T(8,128)(2,1)} %pad_maximum_fusion.1.refs_0_), channel_id=1, source_target_pairs={{0,2},{1,3},{2,0},{3,1},{4,6},{5,7},{6,4},{7,5},{8,10},{9,11},{10,... | collective-permute-start | bytes 1769480 | tf_op jit(solution)/shard_map/ppermute | solution.py:587
  25.3 36.6 %collective-permute-start.9 = (bf16[256,1152]{1,0:T(8,128)(2,1)}, bf16[256,1152]{1,0:T(8,128)(2,1)}, u32[]{:S(2)}, u32[]{:S(2)}) collective-permute-start(bf16[256,1152]{1,0:T(8,128)(2,1)} %pad_maximum_fusion.1.refs_0_), channel_id=1, source_target_pairs={{0,4},{4,0},{8,12},{12,8},{16,20},{20,16},{24,28},{28,24},{1,5},{5... | collective-permute-start | bytes 1769480 | tf_op jit(solution)/shard_map/ppermute | solution.py:592
  51.7 10.3 %collective-permute-start.5 = (bf16[512,384]{1,0:T(8,128)(2,1)S(1)}, bf16[512,384]{1,0:T(8,128)(2,1)S(1)}, u32[]{:S(2)}, u32[]{:S(2)}) collective-permute-start(bf16[512,384]{1,0:T(8,128)(2,1)S(1)} %slice_dynamic-update-slice_fusion.refs_0_), channel_id=1, source_target_pairs={{0,2},{1,3},{2,0},{3,1},{4,6},{5,7},{6,4},{7,5},{8,10},{9,11},{10,... | collective-permute-start | bytes 1179656 | tf_op jit(solution)/shard_map/ppermute | solution.py:587
  53.4 10.6 %collective-permute-start.4 = (bf16[512,384]{1,0:T(8,128)(2,1)S(1)}, bf16[512,384]{1,0:T(8,128)(2,1)S(1)}, u32[]{:S(2)}, u32[]{:S(2)}) collective-permute-start(bf16[512,384]{1,0:T(8,128)(2,1)S(1)} %slice_dynamic-update-slice_fusion.refs_0_), channel_id=1, source_target_pairs={{0,1},{1,0},{2,3},{3,2},{4,5},{5,4},{6,7},{7,6},{8,9},{9,8},{10,11... | collective-permute-start | bytes 1179656 | tf_op jit(solution)/shard_map/ppermute | solution.py:587
  53.4 32.5 %collective-permute-start.12 = (bf16[256,1152]{1,0:T(8,128)(2,1)}, bf16[256,1152]{1,0:T(8,128)(2,1)}, u32[]{:S(2)}, u32[]{:S(2)}) collective-permute-start(bf16[256,1152]{1,0:T(8,128)(2,1)} %pad_maximum_fusion.1.refs_0_), channel_id=1, source_target_pairs={{0,1},{1,0},{2,3},{3,2},{4,5},{5,4},{6,7},{7,6},{8,9},{9,8},{10,11... | collective-permute-start | bytes 1769480 | tf_op jit(solution)/shard_map/ppermute | solution.py:587
  62.0 24.0 %collective-permute-start.13 = (bf16[256,1152]{1,0:T(8,128)(2,1)}, bf16[256,1152]{1,0:T(8,128)(2,1)}, u32[]{:S(2)}, u32[]{:S(2)}) collective-permute-start(bf16[256,1152]{1,0:T(8,128)(2,1)} %collective-permute-done.9.refs_1_), channel_id=1, source_target_pairs={{0,1},{1,0},{2,3},{3,2},{4,5},{5,4},{6,7},{7,6},{8,9},{9,8},{10,11... | collective-permute-start | bytes 1769480 | tf_op jit(solution)/shard_map/ppermute | solution.py:587
  62.0 24.0 %collective-permute-start.15 = (bf16[256,1152]{1,0:T(8,128)(2,1)}, bf16[256,1152]{1,0:T(8,128)(2,1)}, u32[]{:S(2)}, u32[]{:S(2)}) collective-permute-start(bf16[256,1152]{1,0:T(8,128)(2,1)} %collective-permute-done.9.refs_1_), channel_id=1, source_target_pairs={{0,2},{1,3},{2,0},{3,1},{4,6},{5,7},{6,4},{7,5},{8,10},{9,11},{10,... | collective-permute-start | bytes 1769480 | tf_op jit(solution)/shard_map/ppermute | solution.py:587
  63.6 1.9 collective-permute-start.11
  64.0 21.9 %collective-permute-start.14 = (bf16[256,1152]{1,0:T(8,128)(2,1)}, bf16[256,1152]{1,0:T(8,128)(2,1)S(1)}, u32[]{:S(2)}, u32[]{:S(2)}) collective-permute-start(bf16[256,1152]{1,0:T(8,128)(2,1)} %collective-permute-done.10.refs_4_), channel_id=1, source_target_pairs={{0,1},{1,0},{2,3},{3,2},{4,5},{5,4},{6,7},{7,6},{8,9},{9,8},{10,11... | collective-permute-start | bytes 1769480 | tf_op jit(solution)/shard_map/ppermute | solution.py:587
  70.6 15.4 %copy-start.1 = (bf16[1024,1536]{1,0:T(8,128)(2,1)}, bf16[1024,1536]{1,0:T(8,128)(2,1)S(1)}, u32[]{:S(2)}) copy-start(bf16[1024,1536]{1,0:T(8,128)(2,1)S(1)} %get-tuple-element.68.q_ref.k_ref.v_ref) | copy-start | bytes 9437188
  86.0 1.4 copy-start.16
  86.0 3.2 %collective-permute-start.16 = (bf16[256,1152]{1,0:T(8,128)(2,1)}, bf16[256,1152]{1,0:T(8,128)(2,1)S(1)}, u32[]{:S(2)}, u32[]{:S(2)}) collective-permute-start(bf16[256,1152]{1,0:T(8,128)(2,1)} %collective-permute-done.15.refs_5_), channel_id=1, source_target_pairs={{0,1},{1,0},{2,3},{3,2},{4,5},{5,4},{6,7},{7,6},{8,9},{9,8},{10,11... | collective-permute-start | bytes 1769480 | tf_op jit(solution)/shard_map/ppermute | solution.py:587
  89.2 0.8 copy-start.17
  112.8 9.2 %collective-permute-start.18 = (bf16[2,512,512]{2,1,0:T(8,128)(2,1)}, bf16[2,512,512]{2,1,0:T(8,128)(2,1)S(1)}, u32[]{:S(2)}, u32[]{:S(2)}) collective-permute-start(bf16[2,512,512]{2,1,0:T(8,128)(2,1)} %get-tuple-element.86), channel_id=1, source_target_pairs={{0,1},{1,0},{2,3},{3,2},{4,5},{5,4},{6,7},{7,6},{8,9},{9,8},{10,11... | collective-permute-start | bytes 3145736 | tf_op jit(solution)/shard_map/ppermute | solution.py:587
  118.8 5.3 %collective-permute-start.17 = (bf16[2,512,640]{2,1,0:T(8,128)(2,1)}, bf16[2,512,640]{2,1,0:T(8,128)(2,1)}, u32[]{:S(2)}, u32[]{:S(2)}) collective-permute-start(bf16[2,512,640]{2,1,0:T(8,128)(2,1)} %get-tuple-element.81), channel_id=1, source_target_pairs={{0,1},{1,0},{2,3},{3,2},{4,5},{5,4},{6,7},{7,6},{8,9},{9,8},{10,11... | collective-permute-start | bytes 3932168 | tf_op jit(solution)/shard_map/ppermute | solution.py:587
  122.0 5.0 %copy-start.2 = (bf16[1024,1536]{1,0:T(8,128)(2,1)S(1)}, bf16[1024,1536]{1,0:T(8,128)(2,1)}, u32[]{:S(2)}) copy-start(bf16[1024,1536]{1,0:T(8,128)(2,1)} %copy-done.1) | copy-start | bytes 9437188
  122.0 5.0 %copy-start.6 = (bf16[512,1024]{1,0:T(8,128)(2,1)S(1)}, bf16[512,1024]{1,0:T(8,128)(2,1)}, u32[]{:S(2)}) copy-start(bf16[512,1024]{1,0:T(8,128)(2,1)} %get-tuple-element.82.turn_ref) | copy-start | bytes 3145732
  123.6 3.4 %copy-start.5 = (bf16[512,1024]{1,0:T(8,128)(2,1)S(1)}, bf16[512,1024]{1,0:T(8,128)(2,1)}, u32[]{:S(2)}) copy-start(bf16[512,1024]{1,0:T(8,128)(2,1)} %get-tuple-element.88.n_turn_ref) | copy-start | bytes 3145732
  123.6 18.3 %collective-permute-start.19 = (bf16[4,2,64,512]{3,2,1,0:T(8,128)(2,1)S(1)}, bf16[4,2,64,512]{3,2,1,0:T(8,128)(2,1)S(1)}, u32[]{:S(2)}, u32[]{:S(2)}) collective-permute-start(bf16[4,2,64,512]{3,2,1,0:T(8,128)(2,1)S(1)} %bitcast.117), channel_id=1, source_target_pairs={{0,2},{1,3},{2,0},{3,1},{4,6},{5,7},{6,4},{7,5},{8,10},{9,11},{10,... | collective-permute-start | bytes 1572872 | tf_op jit(solution)/shard_map/ppermute | solution.py:587
  125.5 16.8 %collective-permute-start.20 = (bf16[2,4,64,640]{3,2,1,0:T(8,128)(2,1)S(1)}, bf16[2,4,64,640]{3,2,1,0:T(8,128)(2,1)S(1)}, u32[]{:S(2)}, u32[]{:S(2)}) collective-permute-start(bf16[2,4,64,640]{3,2,1,0:T(8,128)(2,1)S(1)} %fusion.1), channel_id=1, source_target_pairs={{0,4},{4,0},{8,12},{12,8},{16,20},{20,16},{24,28},{28,24},{1,5},{5... | collective-permute-start | bytes 1966088 | tf_op jit(solution)/shard_map/ppermute | solution.py:592
  127.0 15.3 %copy-start.8 = (bf16[2,512,640]{2,1,0:T(8,128)(2,1)S(1)}, bf16[2,512,640]{2,1,0:T(8,128)(2,1)}, u32[]{:S(2)}) copy-start(bf16[2,512,640]{2,1,0:T(8,128)(2,1)} %get-tuple-element.80) | copy-start | bytes 3932164
  142.3 8.5 %collective-permute-start.21 = (bf16[512,384]{1,0:T(8,128)(2,1)S(1)}, bf16[512,384]{1,0:T(8,128)(2,1)S(1)}, u32[]{:S(2)}, u32[]{:S(2)}) collective-permute-start(bf16[512,384]{1,0:T(8,128)(2,1)S(1)} %get-tuple-element.97), channel_id=1, source_target_pairs={{0,1},{1,0},{2,3},{3,2},{4,5},{5,4},{6,7},{7,6},{8,9},{9,8},{10,11... | collective-permute-start | bytes 1179656 | tf_op jit(solution)/shard_map/ppermute | solution.py:587
  143.7 22.3 %collective-permute-start.22 = (bf16[4,64,640]{2,1,0:T(8,128)(2,1)S(1)}, bf16[4,64,640]{2,1,0:T(8,128)(2,1)S(1)}, u32[]{:S(2)}, u32[]{:S(2)}) collective-permute-start(bf16[4,64,640]{2,1,0:T(8,128)(2,1)S(1)} %slice_bitcast_fusion), channel_id=1, source_target_pairs={{0,2},{1,3},{2,0},{3,1},{4,6},{5,7},{6,4},{7,5},{8,10},{9,11},{10,... | collective-permute-start | bytes 983048 | tf_op jit(solution)/shard_map/ppermute | solution.py:587
  145.6 6.1 %copy-start.7 = (bf16[1024,512]{1,0:T(8,128)(2,1)S(1)}, bf16[1024,512]{1,0:T(8,128)(2,1)}, u32[]{:S(2)}) copy-start(bf16[1024,512]{1,0:T(8,128)(2,1)} %get-tuple-element.98.cg_ref) | copy-start | bytes 3145732
  145.7 20.3 %collective-permute-start.24 = (bf16[2,64,512]{2,1,0:T(8,128)(2,1)S(1)}, bf16[2,64,512]{2,1,0:T(8,128)(2,1)S(1)}, u32[]{:S(2)}, u32[]{:S(2)}) collective-permute-start(bf16[2,64,512]{2,1,0:T(8,128)(2,1)S(1)} %get-tuple-element.190), channel_id=1, source_target_pairs={{0,8},{4,12},{8,16},{12,20},{16,24},{20,28},{24,0},{28,4},{1,9},{5... | collective-permute-start | bytes 393224 | tf_op jit(solution)/shard_map/ppermute | solution.py:592
  148.4 17.6 %collective-permute-start.25 = (bf16[2,64,512]{2,1,0:T(8,128)(2,1)S(1)}, bf16[2,64,512]{2,1,0:T(8,128)(2,1)S(1)}, u32[]{:S(2)}, u32[]{:S(2)}) collective-permute-start(bf16[2,64,512]{2,1,0:T(8,128)(2,1)S(1)} %get-tuple-element.189), channel_id=1, source_target_pairs={{0,16},{4,20},{8,24},{12,28},{16,0},{20,4},{24,8},{28,12},{1,17},{... | collective-permute-start | bytes 393224 | tf_op jit(solution)/shard_map/ppermute | solution.py:592
  149.9 16.1 %collective-permute-start.26 = (bf16[2,64,512]{2,1,0:T(8,128)(2,1)S(1)}, bf16[2,64,512]{2,1,0:T(8,128)(2,1)S(1)}, u32[]{:S(2)}, u32[]{:S(2)}) collective-permute-start(bf16[2,64,512]{2,1,0:T(8,128)(2,1)S(1)} %get-tuple-element.188), channel_id=1, source_target_pairs={{0,24},{4,28},{8,0},{12,4},{16,8},{20,12},{24,16},{28,20},{1,25},{... | collective-permute-start | bytes 393224 | tf_op jit(solution)/shard_map/ppermute | solution.py:592
  150.9 15.1 %collective-permute-start.23 = (bf16[512,384]{1,0:T(8,128)(2,1)S(1)}, bf16[512,384]{1,0:T(8,128)(2,1)S(1)}, u32[]{:S(2)}, u32[]{:S(2)}) collective-permute-start(bf16[512,384]{1,0:T(8,128)(2,1)S(1)} %add_convert_fusion.3), channel_id=1, source_target_pairs={{0,2},{1,3},{2,0},{3,1},{4,6},{5,7},{6,4},{7,5},{8,10},{9,11},{10,... | collective-permute-start | bytes 1179656 | tf_op jit(solution)/shard_map/ppermute | solution.py:587
  151.7 16.4 %copy-start.4 = (bf16[512,1536]{1,0:T(8,128)(2,1)S(1)}, bf16[512,1536]{1,0:T(8,128)(2,1)}, u32[]{:S(2)}) copy-start(bf16[512,1536]{1,0:T(8,128)(2,1)} %get-tuple-element.108.w_ref) | copy-start | bytes 4718596
  166.0 2.1 copy-start.3
  167.5 6.4 %collective-permute-start.28 = (bf16[64,640]{1,0:T(8,128)(2,1)S(1)}, bf16[64,640]{1,0:T(8,128)(2,1)S(1)}, u32[]{:S(2)}, u32[]{:S(2)}) collective-permute-start(bf16[64,640]{1,0:T(8,128)(2,1)S(1)} %get-tuple-element.195), channel_id=1, source_target_pairs={{0,16},{4,20},{8,24},{12,28},{16,0},{20,4},{24,8},{28,12},{1,17},{... | collective-permute-start | bytes 245768 | tf_op jit(solution)/shard_map/ppermute | solution.py:592
  168.1 5.8 %collective-permute-start.27 = (bf16[512,384]{1,0:T(8,128)(2,1)S(1)}, bf16[512,384]{1,0:T(8,128)(2,1)S(1)}, u32[]{:S(2)}, u32[]{:S(2)}) collective-permute-start(bf16[512,384]{1,0:T(8,128)(2,1)S(1)} %get-tuple-element.110), channel_id=1, source_target_pairs={{0,1},{1,0},{2,3},{3,2},{4,5},{5,4},{6,7},{7,6},{8,9},{9,8},{10,11... | collective-permute-start | bytes 1179656 | tf_op jit(solution)/shard_map/ppermute | solution.py:587
  173.9 0.6 copy-start.13
  174.6 0.7 copy-start.9
  175.3 41.3 %all-to-all-start.1 = ((bf16[32,136,128]{2,1,0:T(8,128)(2,1)}), bf16[32,136,128]{2,1,0:T(8,128)(2,1)S(1)}, u32[]{:S(2)}, u32[]{:S(2)}) async-start(bf16[32,136,128]{2,1,0:T(8,128)(2,1)} %bitcast.25), calls=%async_computation.1 | async-start | bytes 2228224 | tf_op jit(solution)/shard_map/all_to_all | solution.py:800
  182.1 13.1 %collective-permute-start.31 = (bf16[4,64,384]{2,1,0:T(8,128)(2,1)}, bf16[4,64,384]{2,1,0:T(8,128)(2,1)S(1)}, u32[]{:S(2)}, u32[]{:S(2)}) collective-permute-start(bf16[4,64,384]{2,1,0:T(8,128)(2,1)} %fusion.4), channel_id=1, source_target_pairs={{0,4},{4,0},{8,12},{12,8},{16,20},{20,16},{24,28},{28,24},{1,5},{5... | collective-permute-start | bytes 589832 | tf_op jit(solution)/shard_map/ppermute | solution.py:592
  183.9 30.7 %copy-start.14 = (bf16[64,640]{1,0:T(8,128)(2,1)S(1)}, bf16[64,640]{1,0:T(8,128)(2,1)}, u32[]{:S(2)}) copy-start(bf16[64,640]{1,0:T(8,128)(2,1)} %copy-done.13) | copy-start | bytes 245764
  183.9 17.2 %collective-permute-start.35 = (bf16[1,64,512]{2,1,0:T(8,128)(2,1)}, bf16[1,64,512]{2,1,0:T(8,128)(2,1)S(1)}, u32[]{:S(2)}, u32[]{:S(2)}) collective-permute-start(bf16[1,64,512]{2,1,0:T(8,128)(2,1)} %dynamic-slice_convert_fusion), channel_id=1, source_target_pairs={{0,4},{4,0},{8,12},{12,8},{16,20},{20,16},{24,28},{28,24},{1,5},{5... | collective-permute-start | bytes 196616 | tf_op jit(solution)/shard_map/ppermute | solution.py:592
  184.2 20.4 %collective-permute-start.29 = (bf16[64,640]{1,0:T(8,128)(2,1)}, bf16[64,640]{1,0:T(8,128)(2,1)S(1)}, u32[]{:S(2)}, u32[]{:S(2)}) collective-permute-start(bf16[64,640]{1,0:T(8,128)(2,1)} %get-tuple-element.193), channel_id=1, source_target_pairs={{0,8},{4,12},{8,16},{12,20},{16,24},{20,28},{24,0},{28,4},{1,9},{5... | collective-permute-start | bytes 245768 | tf_op jit(solution)/shard_map/ppermute | solution.py:592
  186.0 18.6 %collective-permute-start.30 = (bf16[64,640]{1,0:T(8,128)(2,1)}, bf16[64,640]{1,0:T(8,128)(2,1)S(1)}, u32[]{:S(2)}, u32[]{:S(2)}) collective-permute-start(bf16[64,640]{1,0:T(8,128)(2,1)} %get-tuple-element.192), channel_id=1, source_target_pairs={{0,24},{4,28},{8,0},{12,4},{16,8},{20,12},{24,16},{28,20},{1,25},{... | collective-permute-start | bytes 245768 | tf_op jit(solution)/shard_map/ppermute | solution.py:592
  196.3 11.2 %collective-permute-start.32 = (bf16[64,384]{1,0:T(8,128)(2,1)S(1)}, bf16[64,384]{1,0:T(8,128)(2,1)S(1)}, u32[]{:S(2)}, u32[]{:S(2)}) collective-permute-start(bf16[64,384]{1,0:T(8,128)(2,1)S(1)} %get-tuple-element.198), channel_id=1, source_target_pairs={{0,8},{4,12},{8,16},{12,20},{16,24},{20,28},{24,0},{28,4},{1,9},{5... | collective-permute-start | bytes 147464 | tf_op jit(solution)/shard_map/ppermute | solution.py:592
  197.5 17.0 %collective-permute-start.33 = (bf16[64,384]{1,0:T(8,128)(2,1)S(1)}, bf16[64,384]{1,0:T(8,128)(2,1)S(1)}, u32[]{:S(2)}, u32[]{:S(2)}) collective-permute-start(bf16[64,384]{1,0:T(8,128)(2,1)S(1)} %get-tuple-element.197), channel_id=1, source_target_pairs={{0,16},{4,20},{8,24},{12,28},{16,0},{20,4},{24,8},{28,12},{1,17},{... | collective-permute-start | bytes 147464 | tf_op jit(solution)/shard_map/ppermute | solution.py:592
  201.1 13.4 %collective-permute-start.34 = (bf16[64,384]{1,0:T(8,128)(2,1)S(1)}, bf16[64,384]{1,0:T(8,128)(2,1)S(1)}, u32[]{:S(2)}, u32[]{:S(2)}) collective-permute-start(bf16[64,384]{1,0:T(8,128)(2,1)S(1)} %get-tuple-element.196), channel_id=1, source_target_pairs={{0,24},{4,28},{8,0},{12,4},{16,8},{20,12},{24,16},{28,20},{1,25},{... | collective-permute-start | bytes 147464 | tf_op jit(solution)/shard_map/ppermute | solution.py:592

commit v15 on v14

--- a/solution.py
+++ b/solution.py
@@ -786,7 +786,9 @@
         limit, x_blocks, clock, gain_one, two_grad, qkv_wide, middle_grad, high, low
     )
     if direct:
-        begin_grad, came_one, up_pieces[2] = together(begin_grad, came_one, up_pieces[2])
+        begin_grad, came_one, up_pieces[1], up_pieces[2] = together(
+            begin_grad, came_one, up_pieces[1], up_pieces[2]
+        )
         near = [grouped(value[None])[0] for value in (own_part, came_one, came_far)]
         qkv_value, qkv_pieces = fold_coarse(fold_pair(near)[1]())
         down_total = add_wide(*down_rest())[0]

time: 219 us -> 219 us (level)
  no operation moved by 1% of the time
where the time goes in v15:
time: 219 us; the launch traced here: 218 us
  Pallas kernels  76 us (35%)
  starting transfers between devices  56.6 us (26%)
  waiting for transfers between devices  55.9 us (26%)
  other arithmetic  13.4 us (6%)
  local copies, waits for them, and re-layouts  12.1 us (6%)
  between operations  3.78 us (2%)
    ppermute x20, waiting for transfers between devices, along_dp(): return lax.ppermute(value, 'dp', [(i, move(i)) for i in range(count)])  46.5 us
    ppermute x20, starting transfers between devices, along_dp(): return lax.ppermute(value, 'dp', [(i, move(i)) for i in range(count)])  35 us
    pallas_call x2, Pallas kernels, attend_back(): pl.pallas_call(attend_back_kernel, grid_spec=pltpu.PrefetchScalarGridSpec...  29.1 us
    pallas_call x1, Pallas kernels, middle_block(): pl.pallas_call(functools.partial(middle_kernel, groups), grid_spec=pltpu....  22.9 us
    ppermute x16, starting transfers between devices, swap(): return lax.ppermute(value, 'tensor', [(i, i ^ apart) for i in range(count)])  16.1 us
    pallas_call x1, Pallas kernels, attend(): pl.pallas_call(attend_kernel, grid_spec=pltpu.PrefetchScalarGridSpec(num_...  15.4 us
    ppermute x16, waiting for transfers between devices, swap(): return lax.ppermute(value, 'tensor', [(i, i ^ apart) for i in range(count)])  9.4 us
    convert_element_type x7, other arithmetic, add(): return add_wide(*values).astype(BF16)  5.84 us
  transfers between devices with their start and end apart: 38, of which 12 were waited for; matrix products, arithmetic and copies ran while one was open for 8% of the time, Pallas kernels for 24%

profile of v15, /device:TPU:0, one launch (start us, length us, event | category | flops | bytes accessed | tf_op | source)
XLA Modules:
  0.0 217.8 jit_solution(5456789296924463862)
XLA Ops:
  0.6 1.0 pad_maximum_fusion.2
  1.6 3.1 %collective-permute-start.6 = (bf16[64,1152]{1,0:T(8,128)(2,1)S(1)}, bf16[64,1152]{1,0:T(8,128)(2,1)S(1)}, u32[]{:S(2)}, u32[]{:S(2)}) collective-permute-start(bf16[64,1152]{1,0:T(8,128)(2,1)S(1)} %pad_maximum_fusion.2), channel_id=1, source_target_pairs={{0,8},{4,12},{8,16},{12,20},{16,24},{20,28},{24,0},{28,4},{1,9},{5... | collective-permute-start | bytes 442376 | tf_op jit(solution)/shard_map/ppermute | solution.py:592
  4.7 2.6 %collective-permute-start.7 = (bf16[64,1152]{1,0:T(8,128)(2,1)S(1)}, bf16[64,1152]{1,0:T(8,128)(2,1)S(1)}, u32[]{:S(2)}, u32[]{:S(2)}) collective-permute-start(bf16[64,1152]{1,0:T(8,128)(2,1)S(1)} %pad_maximum_fusion.2), channel_id=1, source_target_pairs={{0,16},{4,20},{8,24},{12,28},{16,0},{20,4},{24,8},{28,12},{1,17},{... | collective-permute-start | bytes 442376 | tf_op jit(solution)/shard_map/ppermute | solution.py:592
  7.3 1.3 collective-permute-start.8
  8.6 0.8 copy_bitcast_fusion.1
  9.4 1.5 collective-permute-start
  11.0 0.7 fusion.9
  12.5 0.7 gather_fusion
  13.2 1.1 pad_maximum_fusion
  14.4 2.8 %all-to-all-start = ((bf16[32,136,128]{2,1,0:T(8,128)(2,1)}), bf16[32,136,128]{2,1,0:T(8,128)(2,1)S(1)}, u32[]{:S(2)}, u32[]{:S(2)}) async-start(bf16[32,136,128]{2,1,0:T(8,128)(2,1)} %pad_maximum_fusion), calls=%async_computation | async-start | bytes 2228224 | tf_op jit(solution)/shard_map/all_to_all | solution.py:734
  17.3 1.7 collective-permute-start.1
  19.0 2.5 %collective-permute-start.2 = (bf16[64,768]{1,0:T(8,128)(2,1)S(1)}, bf16[64,768]{1,0:T(8,128)(2,1)S(1)}, u32[]{:S(2)}, u32[]{:S(2)}) collective-permute-start(bf16[64,768]{1,0:T(8,128)(2,1)S(1)} %constant_dynamic-update-slice_fusion), channel_id=1, source_target_pairs={{0,16},{4,20},{8,24},{12,28},{16,0},{20,4},{24,8},{28,12},{1,17},{... | collective-permute-start | bytes 294920 | tf_op jit(solution)/shard_map/ppermute | solution.py:592
  21.5 1.4 collective-permute-start.3
  23.0 0.9 pad_maximum_fusion.1.refs_0_
  23.8 1.5 collective-permute-start.10
  25.3 1.5 collective-permute-start.9
  26.8 15.6 %collective-permute-done.1 = bf16[64,768]{1,0:T(8,128)(2,1)S(1)} collective-permute-done((bf16[64,768]{1,0:T(8,128)(2,1)S(1)}, bf16[64,768]{1,0:T(8,128)(2,1)S(1)}, u32[]{:S(2)}, u32[]{:S(2)}) %collective-permute-start.1) | collective-permute-done | bytes 98336 | tf_op jit(solution)/shard_map/ppermute | solution.py:592
  42.4 9.2 %collective-permute-done.2 = bf16[64,768]{1,0:T(8,128)(2,1)S(1)} collective-permute-done((bf16[64,768]{1,0:T(8,128)(2,1)S(1)}, bf16[64,768]{1,0:T(8,128)(2,1)S(1)}, u32[]{:S(2)}, u32[]{:S(2)}) %collective-permute-start.2) | collective-permute-done | bytes 98336 | tf_op jit(solution)/shard_map/ppermute | solution.py:592
  51.7 1.6 collective-permute-start.5
  58.4 3.6 %collective-permute-done.5.refs_2_ = bf16[512,384]{1,0:T(8,128)(2,1)S(1)} collective-permute-done((bf16[512,384]{1,0:T(8,128)(2,1)S(1)}, bf16[512,384]{1,0:T(8,128)(2,1)S(1)}, u32[]{:S(2)}, u32[]{:S(2)}) %collective-permute-start.5) | collective-permute-done | bytes 393248 | tf_op jit(solution)/shard_map/ppermute | solution.py:587
  62.0 1.6 collective-permute-start.15
  64.5 1.0 collective-permute-done.11.refs_3_
  65.4 5.2 %project.1 = (bf16[1024,1536]{1,0:T(8,128)(2,1)S(1)}, bf16[512,1024]{1,0:T(8,128)(2,1)}, bf16[512,1536]{1,0:T(8,128)(2,1)}) custom-call(s32[1]{0:T(128)} %dynamic-slice.9.limit_ref, s32[8]{0:T(128)S(1)} %pad_add_fusion.place_ref, bf16[8,4,136,128]{3,2,1,0:T(8,128)(2,1)S(1)} %bitcast.109, f32[1,512]{1,0:T(1,128)S(1)} %pad_maximum_fusion.3.clock_ref, ...), custom_call_target="tpu_custom_call" | custom-call | flops 5750000128 | bytes 1048576 | tf_op jit(solution)/shard_map/project/pallas_call | solution.py:111
  70.6 15.4 %attend.1 = (bf16[1024,512]{1,0:T(8,128)(2,1)}, bf16[512,1024]{1,0:T(8,128)(2,1)}, f32[4,2,1024]{2,1,0:T(2,128)S(1)}) custom-call(s32[1]{0:T(128)} %dynamic-slice.9.limit_ref, bf16[1024,1536]{1,0:T(8,128)(2,1)S(1)} %get-tuple-element.69.q_ref.k_ref.v_ref, bf16[1024,1536]{1,0:T(8,128)(2,1)S(1)} %get-tuple-element.69.q_ref.k_ref.v_ref, ...), custom_call_target="tpu_custom_call" | custom-call | flops 17250000896 | bytes 1048576 | tf_op jit(solution)/shard_map/attend/pallas_call | solution.py:200
  86.0 1.3 collective-permute-start.16
  87.5 1.7 collective-permute-done.16.refs_7_
  89.2 0.8 copy-done.19
  90.0 22.9 %middle.1 = (bf16[1,1024,512]{2,1,0:T(8,128)(2,1)}, bf16[1024,512]{1,0:T(8,128)(2,1)}, f32[1024,512]{1,0:T(8,128)}, f32[1,512]{1,0:T(1,128)S(1)}, bf16[2,512,640...) custom-call(s32[1]{0:T(128)} %dynamic-slice.9.limit_ref, ...), custom_call_target="tpu_custom_call" | custom-call | flops 28750000128 | bytes 1048576 | tf_op jit(solution)/shard_map/middle/pallas_call | solution.py:370
  112.9 6.0 %collective-permute-start.18 = (bf16[2,512,512]{2,1,0:T(8,128)(2,1)}, bf16[2,512,512]{2,1,0:T(8,128)(2,1)S(1)}, u32[]{:S(2)}, u32[]{:S(2)}) collective-permute-start(bf16[2,512,512]{2,1,0:T(8,128)(2,1)} %get-tuple-element.87), channel_id=1, source_target_pairs={{0,1},{1,0},{2,3},{3,2},{4,5},{5,4},{6,7},{7,6},{8,9},{9,8},{10,11... | collective-permute-start | bytes 3145736 | tf_op jit(solution)/shard_map/ppermute | solution.py:587
  118.9 3.1 %collective-permute-done.18 = bf16[2,512,512]{2,1,0:T(8,128)(2,1)S(1)} collective-permute-done((bf16[2,512,512]{2,1,0:T(8,128)(2,1)}, bf16[2,512,512]{2,1,0:T(8,128)(2,1)S(1)}, u32[]{:S(2)}, u32[]{:S(2)}) %collective-permute-start.18) | collective-permute-done | bytes 1048608 | tf_op jit(solution)/shard_map/ppermute | solution.py:587
  122.0 1.6 convert_add_fusion
  123.7 0.8 collective-permute-start.19
  124.5 1.4 fusion.1
  126.0 1.1 collective-permute-start.20
  127.1 14.9 %attend_back.2 = (bf16[1024,768]{1,0:T(8,128)(2,1)S(1)}, bf16[512,384]{1,0:T(8,128)(2,1)S(1)}, bf16[512,384]{1,0:T(8,128)(2,1)S(1)}) custom-call(s32[1]{0:T(128)} %dynamic-slice.9.limit_ref, bf16[1024,1536]{1,0:T(8,128)(2,1)S(1)} %copy-done.2, bf16[1024,1536]{1,0:T(8,128)(2,1)S(1)} %copy-done.2, bf16[1024,1536]{1,0:T(8,128)(2,1)S(1)} %copy-done.2, ...), custom_call_target="tpu_custom_call" | custom-call | flops 18400000000 | bytes 1048576 | tf_op jit(solution)/shard_map/attend_back/pallas_call | solution.py:466
  142.0 0.7 collective-permute-done.20
  142.8 1.3 fusion
  144.1 1.3 collective-permute-start.22
  145.7 2.7 %collective-permute-start.24 = (bf16[2,64,512]{2,1,0:T(8,128)(2,1)S(1)}, bf16[2,64,512]{2,1,0:T(8,128)(2,1)S(1)}, u32[]{:S(2)}, u32[]{:S(2)}) collective-permute-start(bf16[2,64,512]{2,1,0:T(8,128)(2,1)S(1)} %get-tuple-element.192), channel_id=1, source_target_pairs={{0,8},{4,12},{8,16},{12,20},{16,24},{20,28},{24,0},{28,4},{1,9},{5... | collective-permute-start | bytes 393224 | tf_op jit(solution)/shard_map/ppermute | solution.py:592
  148.4 0.8 collective-permute-start.25
  149.2 1.6 collective-permute-start.26
  150.9 0.8 collective-permute-start.23
  151.8 14.2 %attend_back.3 = (bf16[1024,768]{1,0:T(8,128)(2,1)S(1)}, bf16[512,384]{1,0:T(8,128)(2,1)S(1)}, bf16[512,384]{1,0:T(8,128)(2,1)S(1)}) custom-call(s32[1]{0:T(128)} %dynamic-slice.9.limit_ref, bf16[1024,1536]{1,0:T(8,128)(2,1)S(1)} %copy-done.2, bf16[1024,1536]{1,0:T(8,128)(2,1)S(1)} %copy-done.2, bf16[1024,1536]{1,0:T(8,128)(2,1)S(1)} %copy-done.2, ...), custom_call_target="tpu_custom_call" | custom-call | flops 18400000000 | bytes 1048576 | tf_op jit(solution)/shard_map/attend_back/pallas_call | solution.py:466
  166.9 0.7 dynamic-slice_bitcast_fusion.4
  167.5 1.1 collective-permute-start.28
  168.7 1.4 collective-permute-start.29
  170.1 3.5 %begin_back.1 = bf16[8,4,136,128]{3,2,1,0:T(8,128)(2,1)} custom-call(s32[1]{0:T(128)} %dynamic-slice.9.limit_ref, bf16[8,4,136,128]{3,2,1,0:T(8,128)(2,1)S(1)} %bitcast.111, f32[1,512]{1,0:T(1,128)S(1)} %pad_maximum_fusion.3.clock_ref, f32[1,512]{1,0:T(1,128)S(1)} %reshape_squeeze.8.gain_ref, f32[1,512]{1,0:T(1,128)S(1)} %get-tuple-element.79.gg_two_ref, ...), custom_call_target="tpu_custom_call" | custom-call | flops 8049999872 | bytes 1048576 | tf_op jit(solution)/shard_map/begin_back/pallas_call | solution.py:554
  174.1 2.2 collective-permute-done.29
  176.9 0.7 copy-done.9
  177.6 2.6 %all-to-all-start.1 = ((bf16[32,136,128]{2,1,0:T(8,128)(2,1)}), bf16[32,136,128]{2,1,0:T(8,128)(2,1)S(1)}, u32[]{:S(2)}, u32[]{:S(2)}) async-start(bf16[32,136,128]{2,1,0:T(8,128)(2,1)} %bitcast.26), calls=%async_computation.1 | async-start | bytes 2228224 | tf_op jit(solution)/shard_map/all_to_all | solution.py:802
  180.3 0.7 scatter_custom_fusion
  180.9 1.7 fusion.4
  182.6 1.7 collective-permute-start.31
  184.7 3.6 %collective-permute-start.30 = (bf16[64,640]{1,0:T(8,128)(2,1)}, bf16[64,640]{1,0:T(8,128)(2,1)S(1)}, u32[]{:S(2)}, u32[]{:S(2)}) collective-permute-start(bf16[64,640]{1,0:T(8,128)(2,1)} %get-tuple-element.194), channel_id=1, source_target_pairs={{0,24},{4,28},{8,0},{12,4},{16,8},{20,12},{24,16},{28,20},{1,25},{... | collective-permute-start | bytes 245768 | tf_op jit(solution)/shard_map/ppermute | solution.py:592
  188.4 7.3 %collective-permute-done.31 = bf16[4,64,384]{2,1,0:T(8,128)(2,1)S(1)} collective-permute-done((bf16[4,64,384]{2,1,0:T(8,128)(2,1)}, bf16[4,64,384]{2,1,0:T(8,128)(2,1)S(1)}, u32[]{:S(2)}, u32[]{:S(2)}) %collective-permute-start.31) | collective-permute-done | bytes 196640 | tf_op jit(solution)/shard_map/ppermute | solution.py:592
  195.7 1.0 fusion.3
  196.8 1.3 collective-permute-start.32
  198.1 3.5 %collective-permute-start.33 = (bf16[64,384]{1,0:T(8,128)(2,1)S(1)}, bf16[64,384]{1,0:T(8,128)(2,1)S(1)}, u32[]{:S(2)}, u32[]{:S(2)}) collective-permute-start(bf16[64,384]{1,0:T(8,128)(2,1)S(1)} %get-tuple-element.199), channel_id=1, source_target_pairs={{0,16},{4,20},{8,24},{12,28},{16,0},{20,4},{24,8},{28,12},{1,17},{... | collective-permute-start | bytes 147464 | tf_op jit(solution)/shard_map/ppermute | solution.py:592
  201.6 0.7 add_bitcast_fusion
  202.3 4.0 %collective-permute-done.32 = bf16[64,384]{1,0:T(8,128)(2,1)S(1)} collective-permute-done((bf16[64,384]{1,0:T(8,128)(2,1)S(1)}, bf16[64,384]{1,0:T(8,128)(2,1)S(1)}, u32[]{:S(2)}, u32[]{:S(2)}) %collective-permute-start.32) | collective-permute-done | bytes 49184 | tf_op jit(solution)/shard_map/ppermute | solution.py:592
  206.3 7.0 %collective-permute-done.33 = bf16[64,384]{1,0:T(8,128)(2,1)S(1)} collective-permute-done((bf16[64,384]{1,0:T(8,128)(2,1)S(1)}, bf16[64,384]{1,0:T(8,128)(2,1)S(1)}, u32[]{:S(2)}, u32[]{:S(2)}) %collective-permute-start.33) | collective-permute-done | bytes 49184 | tf_op jit(solution)/shard_map/ppermute | solution.py:592
  214.6 0.7 copy_bitcast_fusion
  215.3 0.8 gather_fusion.1
  216.1 1.1 slice.117
  (129 shorter events, 9.3 us)
Async XLA Ops:
  0.6 11.8 %copy-start = (bf16[32,128,128]{2,1,0:T(8,128)(2,1)S(1)}, bf16[32,128,128]{2,1,0:T(8,128)(2,1)}, u32[]{:S(2)}) copy-start(bf16[32,128,128]{2,1,0:T(8,128)(2,1)} %param.11) | copy-start | bytes 3145732
  1.6 19.9 %collective-permute-start.6 = (bf16[64,1152]{1,0:T(8,128)(2,1)S(1)}, bf16[64,1152]{1,0:T(8,128)(2,1)S(1)}, u32[]{:S(2)}, u32[]{:S(2)}) collective-permute-start(bf16[64,1152]{1,0:T(8,128)(2,1)S(1)} %pad_maximum_fusion.2), channel_id=1, source_target_pairs={{0,8},{4,12},{8,16},{12,20},{16,24},{20,28},{24,0},{28,4},{1,9},{5... | collective-permute-start | bytes 442376 | tf_op jit(solution)/shard_map/ppermute | solution.py:592
  4.7 18.2 %collective-permute-start.7 = (bf16[64,1152]{1,0:T(8,128)(2,1)S(1)}, bf16[64,1152]{1,0:T(8,128)(2,1)S(1)}, u32[]{:S(2)}, u32[]{:S(2)}) collective-permute-start(bf16[64,1152]{1,0:T(8,128)(2,1)S(1)} %pad_maximum_fusion.2), channel_id=1, source_target_pairs={{0,16},{4,20},{8,24},{12,28},{16,0},{20,4},{24,8},{28,12},{1,17},{... | collective-permute-start | bytes 442376 | tf_op jit(solution)/shard_map/ppermute | solution.py:592
  7.3 15.6 %collective-permute-start.8 = (bf16[64,1152]{1,0:T(8,128)(2,1)S(1)}, bf16[64,1152]{1,0:T(8,128)(2,1)S(1)}, u32[]{:S(2)}, u32[]{:S(2)}) collective-permute-start(bf16[64,1152]{1,0:T(8,128)(2,1)S(1)} %pad_maximum_fusion.2), channel_id=1, source_target_pairs={{0,24},{4,28},{8,0},{12,4},{16,8},{20,12},{24,16},{28,20},{1,25},{... | collective-permute-start | bytes 442376 | tf_op jit(solution)/shard_map/ppermute | solution.py:592
  9.4 7.8 %collective-permute-start = (bf16[64,384]{1,0:T(8,128)(2,1)S(1)}, bf16[64,384]{1,0:T(8,128)(2,1)S(1)}, u32[]{:S(2)}, u32[]{:S(2)}) collective-permute-start(bf16[64,384]{1,0:T(8,128)(2,1)S(1)} %copy_bitcast_fusion.1), channel_id=1, source_target_pairs={{0,4},{4,0},{8,12},{12,8},{16,20},{20,16},{24,28},{28,24},{1,5},{5... | collective-permute-start | bytes 147464 | tf_op jit(solution)/shard_map/ppermute | solution.py:592
  14.4 2.8 %copy-start.12 = (bf16[64,3,128]{2,0,1:T(8,128)(2,1)S(1)}, bf16[64,3,128]{2,0,1:T(8,128)(2,1)}, u32[]{:S(2)}) copy-start(bf16[64,3,128]{2,0,1:T(8,128)(2,1)} %param.15) | copy-start | bytes 147460
  14.4 8.6 %copy-start.10 = (bf16[512,64]{0,1:T(8,128)(2,1)S(1)}, bf16[512,64]{0,1:T(8,128)(2,1)}, u32[]{:S(2)}) copy-start(bf16[512,64]{0,1:T(8,128)(2,1)} %param.18) | copy-start | bytes 196612
  14.4 8.6 %copy-start.11 = (bf16[64,512]{1,0:T(8,128)(2,1)S(1)}, bf16[64,512]{1,0:T(8,128)(2,1)}, u32[]{:S(2)}) copy-start(bf16[64,512]{1,0:T(8,128)(2,1)} %param.17) | copy-start | bytes 196612
  14.4 8.6 %copy-start.17 = (bf16[128,64]{0,1:T(8,128)(2,1)S(1)}, bf16[128,64]{0,1:T(8,128)(2,1)}, u32[]{:S(2)}) copy-start(bf16[128,64]{0,1:T(8,128)(2,1)} %param.16) | copy-start | bytes 49156
  14.4 49.4 %all-to-all-start = ((bf16[32,136,128]{2,1,0:T(8,128)(2,1)}), bf16[32,136,128]{2,1,0:T(8,128)(2,1)S(1)}, u32[]{:S(2)}, u32[]{:S(2)}) async-start(bf16[32,136,128]{2,1,0:T(8,128)(2,1)} %pad_maximum_fusion), calls=%async_computation | async-start | bytes 2228224 | tf_op jit(solution)/shard_map/all_to_all | solution.py:734
  17.2 36.7 %copy-start.20 = (s32[32]{0:T(128)S(1)}, s32[32]{0:T(128)}, u32[]{:S(2)}) copy-start(s32[32]{0:T(128)} %param.14) | copy-start | bytes 388
  17.2 39.2 %copy-start.21 = (s32[32]{0:T(128)S(1)}, s32[32]{0:T(128)}, u32[]{:S(2)}) copy-start(s32[32]{0:T(128)} %param.12) | copy-start | bytes 388
  17.2 40.5 %copy-start.22 = (s32[32]{0:T(128)S(1)}, s32[32]{0:T(128)}, u32[]{:S(2)}) copy-start(s32[32]{0:T(128)} %param.13) | copy-start | bytes 388
  17.3 25.1 %collective-permute-start.1 = (bf16[64,768]{1,0:T(8,128)(2,1)S(1)}, bf16[64,768]{1,0:T(8,128)(2,1)S(1)}, u32[]{:S(2)}, u32[]{:S(2)}) collective-permute-start(bf16[64,768]{1,0:T(8,128)(2,1)S(1)} %constant_dynamic-update-slice_fusion), channel_id=1, source_target_pairs={{0,8},{4,12},{8,16},{12,20},{16,24},{20,28},{24,0},{28,4},{1,9},{5... | collective-permute-start | bytes 294920 | tf_op jit(solution)/shard_map/ppermute | solution.py:592
  19.0 32.6 %collective-permute-start.2 = (bf16[64,768]{1,0:T(8,128)(2,1)S(1)}, bf16[64,768]{1,0:T(8,128)(2,1)S(1)}, u32[]{:S(2)}, u32[]{:S(2)}) collective-permute-start(bf16[64,768]{1,0:T(8,128)(2,1)S(1)} %constant_dynamic-update-slice_fusion), channel_id=1, source_target_pairs={{0,16},{4,20},{8,24},{12,28},{16,0},{20,4},{24,8},{28,12},{1,17},{... | collective-permute-start | bytes 294920 | tf_op jit(solution)/shard_map/ppermute | solution.py:592
  21.5 30.1 %collective-permute-start.3 = (bf16[64,768]{1,0:T(8,128)(2,1)S(1)}, bf16[64,768]{1,0:T(8,128)(2,1)S(1)}, u32[]{:S(2)}, u32[]{:S(2)}) collective-permute-start(bf16[64,768]{1,0:T(8,128)(2,1)S(1)} %constant_dynamic-update-slice_fusion), channel_id=1, source_target_pairs={{0,24},{4,28},{8,0},{12,4},{16,8},{20,12},{24,16},{28,20},{1,25},{... | collective-permute-start | bytes 294920 | tf_op jit(solution)/shard_map/ppermute | solution.py:592
  23.8 38.1 %collective-permute-start.10 = (bf16[256,1152]{1,0:T(8,128)(2,1)}, bf16[256,1152]{1,0:T(8,128)(2,1)}, u32[]{:S(2)}, u32[]{:S(2)}) collective-permute-start(bf16[256,1152]{1,0:T(8,128)(2,1)} %pad_maximum_fusion.1.refs_0_), channel_id=1, source_target_pairs={{0,2},{1,3},{2,0},{3,1},{4,6},{5,7},{6,4},{7,5},{8,10},{9,11},{10,... | collective-permute-start | bytes 1769480 | tf_op jit(solution)/shard_map/ppermute | solution.py:587
  25.3 36.6 %collective-permute-start.9 = (bf16[256,1152]{1,0:T(8,128)(2,1)}, bf16[256,1152]{1,0:T(8,128)(2,1)}, u32[]{:S(2)}, u32[]{:S(2)}) collective-permute-start(bf16[256,1152]{1,0:T(8,128)(2,1)} %pad_maximum_fusion.1.refs_0_), channel_id=1, source_target_pairs={{0,4},{4,0},{8,12},{12,8},{16,20},{20,16},{24,28},{28,24},{1,5},{5... | collective-permute-start | bytes 1769480 | tf_op jit(solution)/shard_map/ppermute | solution.py:592
  51.7 10.3 %collective-permute-start.5 = (bf16[512,384]{1,0:T(8,128)(2,1)S(1)}, bf16[512,384]{1,0:T(8,128)(2,1)S(1)}, u32[]{:S(2)}, u32[]{:S(2)}) collective-permute-start(bf16[512,384]{1,0:T(8,128)(2,1)S(1)} %slice_dynamic-update-slice_fusion.refs_0_), channel_id=1, source_target_pairs={{0,2},{1,3},{2,0},{3,1},{4,6},{5,7},{6,4},{7,5},{8,10},{9,11},{10,... | collective-permute-start | bytes 1179656 | tf_op jit(solution)/shard_map/ppermute | solution.py:587
  53.4 10.6 %collective-permute-start.4 = (bf16[512,384]{1,0:T(8,128)(2,1)S(1)}, bf16[512,384]{1,0:T(8,128)(2,1)S(1)}, u32[]{:S(2)}, u32[]{:S(2)}) collective-permute-start(bf16[512,384]{1,0:T(8,128)(2,1)S(1)} %slice_dynamic-update-slice_fusion.refs_0_), channel_id=1, source_target_pairs={{0,1},{1,0},{2,3},{3,2},{4,5},{5,4},{6,7},{7,6},{8,9},{9,8},{10,11... | collective-permute-start | bytes 1179656 | tf_op jit(solution)/shard_map/ppermute | solution.py:587
  53.4 32.5 %collective-permute-start.12 = (bf16[256,1152]{1,0:T(8,128)(2,1)}, bf16[256,1152]{1,0:T(8,128)(2,1)}, u32[]{:S(2)}, u32[]{:S(2)}) collective-permute-start(bf16[256,1152]{1,0:T(8,128)(2,1)} %pad_maximum_fusion.1.refs_0_), channel_id=1, source_target_pairs={{0,1},{1,0},{2,3},{3,2},{4,5},{5,4},{6,7},{7,6},{8,9},{9,8},{10,11... | collective-permute-start | bytes 1769480 | tf_op jit(solution)/shard_map/ppermute | solution.py:587
  62.0 24.0 %collective-permute-start.13 = (bf16[256,1152]{1,0:T(8,128)(2,1)}, bf16[256,1152]{1,0:T(8,128)(2,1)}, u32[]{:S(2)}, u32[]{:S(2)}) collective-permute-start(bf16[256,1152]{1,0:T(8,128)(2,1)} %collective-permute-done.9.refs_1_), channel_id=1, source_target_pairs={{0,1},{1,0},{2,3},{3,2},{4,5},{5,4},{6,7},{7,6},{8,9},{9,8},{10,11... | collective-permute-start | bytes 1769480 | tf_op jit(solution)/shard_map/ppermute | solution.py:587
  62.0 24.0 %collective-permute-start.15 = (bf16[256,1152]{1,0:T(8,128)(2,1)}, bf16[256,1152]{1,0:T(8,128)(2,1)}, u32[]{:S(2)}, u32[]{:S(2)}) collective-permute-start(bf16[256,1152]{1,0:T(8,128)(2,1)} %collective-permute-done.9.refs_1_), channel_id=1, source_target_pairs={{0,2},{1,3},{2,0},{3,1},{4,6},{5,7},{6,4},{7,5},{8,10},{9,11},{10,... | collective-permute-start | bytes 1769480 | tf_op jit(solution)/shard_map/ppermute | solution.py:587
  63.6 1.9 collective-permute-start.11
  64.0 22.0 %collective-permute-start.14 = (bf16[256,1152]{1,0:T(8,128)(2,1)}, bf16[256,1152]{1,0:T(8,128)(2,1)S(1)}, u32[]{:S(2)}, u32[]{:S(2)}) collective-permute-start(bf16[256,1152]{1,0:T(8,128)(2,1)} %collective-permute-done.10.refs_4_), channel_id=1, source_target_pairs={{0,1},{1,0},{2,3},{3,2},{4,5},{5,4},{6,7},{7,6},{8,9},{9,8},{10,11... | collective-permute-start | bytes 1769480 | tf_op jit(solution)/shard_map/ppermute | solution.py:587
  70.6 15.4 %copy-start.1 = (bf16[1024,1536]{1,0:T(8,128)(2,1)}, bf16[1024,1536]{1,0:T(8,128)(2,1)S(1)}, u32[]{:S(2)}) copy-start(bf16[1024,1536]{1,0:T(8,128)(2,1)S(1)} %get-tuple-element.69.q_ref.k_ref.v_ref) | copy-start | bytes 9437188
  86.0 1.4 copy-start.18
  86.0 3.2 %collective-permute-start.16 = (bf16[256,1152]{1,0:T(8,128)(2,1)}, bf16[256,1152]{1,0:T(8,128)(2,1)S(1)}, u32[]{:S(2)}, u32[]{:S(2)}) collective-permute-start(bf16[256,1152]{1,0:T(8,128)(2,1)} %collective-permute-done.15.refs_5_), channel_id=1, source_target_pairs={{0,1},{1,0},{2,3},{3,2},{4,5},{5,4},{6,7},{7,6},{8,9},{9,8},{10,11... | collective-permute-start | bytes 1769480 | tf_op jit(solution)/shard_map/ppermute | solution.py:587
  89.2 0.8 copy-start.19
  112.9 9.2 %collective-permute-start.18 = (bf16[2,512,512]{2,1,0:T(8,128)(2,1)}, bf16[2,512,512]{2,1,0:T(8,128)(2,1)S(1)}, u32[]{:S(2)}, u32[]{:S(2)}) collective-permute-start(bf16[2,512,512]{2,1,0:T(8,128)(2,1)} %get-tuple-element.87), channel_id=1, source_target_pairs={{0,1},{1,0},{2,3},{3,2},{4,5},{5,4},{6,7},{7,6},{8,9},{9,8},{10,11... | collective-permute-start | bytes 3145736 | tf_op jit(solution)/shard_map/ppermute | solution.py:587
  118.8 5.7 %collective-permute-start.17 = (bf16[2,512,640]{2,1,0:T(8,128)(2,1)}, bf16[2,512,640]{2,1,0:T(8,128)(2,1)}, u32[]{:S(2)}, u32[]{:S(2)}) collective-permute-start(bf16[2,512,640]{2,1,0:T(8,128)(2,1)} %get-tuple-element.82), channel_id=1, source_target_pairs={{0,1},{1,0},{2,3},{3,2},{4,5},{5,4},{6,7},{7,6},{8,9},{9,8},{10,11... | collective-permute-start | bytes 3932168 | tf_op jit(solution)/shard_map/ppermute | solution.py:587
  122.0 5.0 %copy-start.2 = (bf16[1024,1536]{1,0:T(8,128)(2,1)S(1)}, bf16[1024,1536]{1,0:T(8,128)(2,1)}, u32[]{:S(2)}) copy-start(bf16[1024,1536]{1,0:T(8,128)(2,1)} %copy-done.1) | copy-start | bytes 9437188
  122.0 5.0 %copy-start.6 = (bf16[512,1024]{1,0:T(8,128)(2,1)S(1)}, bf16[512,1024]{1,0:T(8,128)(2,1)}, u32[]{:S(2)}) copy-start(bf16[512,1024]{1,0:T(8,128)(2,1)} %get-tuple-element.83.turn_ref) | copy-start | bytes 3145732
  123.7 3.4 %copy-start.5 = (bf16[512,1024]{1,0:T(8,128)(2,1)S(1)}, bf16[512,1024]{1,0:T(8,128)(2,1)}, u32[]{:S(2)}) copy-start(bf16[512,1024]{1,0:T(8,128)(2,1)} %get-tuple-element.89.n_turn_ref) | copy-start | bytes 3145732
  123.7 18.3 %collective-permute-start.19 = (bf16[4,2,64,512]{3,2,1,0:T(8,128)(2,1)S(1)}, bf16[4,2,64,512]{3,2,1,0:T(8,128)(2,1)S(1)}, u32[]{:S(2)}, u32[]{:S(2)}) collective-permute-start(bf16[4,2,64,512]{3,2,1,0:T(8,128)(2,1)S(1)} %bitcast.117), channel_id=1, source_target_pairs={{0,2},{1,3},{2,0},{3,1},{4,6},{5,7},{6,4},{7,5},{8,10},{9,11},{10,... | collective-permute-start | bytes 1572872 | tf_op jit(solution)/shard_map/ppermute | solution.py:587
  126.0 16.8 %collective-permute-start.20 = (bf16[2,4,64,640]{3,2,1,0:T(8,128)(2,1)S(1)}, bf16[2,4,64,640]{3,2,1,0:T(8,128)(2,1)S(1)}, u32[]{:S(2)}, u32[]{:S(2)}) collective-permute-start(bf16[2,4,64,640]{3,2,1,0:T(8,128)(2,1)S(1)} %fusion.1), channel_id=1, source_target_pairs={{0,4},{4,0},{8,12},{12,8},{16,20},{20,16},{24,28},{28,24},{1,5},{5... | collective-permute-start | bytes 1966088 | tf_op jit(solution)/shard_map/ppermute | solution.py:592
  127.1 15.7 %copy-start.8 = (bf16[2,512,640]{2,1,0:T(8,128)(2,1)S(1)}, bf16[2,512,640]{2,1,0:T(8,128)(2,1)}, u32[]{:S(2)}) copy-start(bf16[2,512,640]{2,1,0:T(8,128)(2,1)} %get-tuple-element.81) | copy-start | bytes 3932164
  142.7 8.1 %collective-permute-start.21 = (bf16[512,384]{1,0:T(8,128)(2,1)S(1)}, bf16[512,384]{1,0:T(8,128)(2,1)S(1)}, u32[]{:S(2)}, u32[]{:S(2)}) collective-permute-start(bf16[512,384]{1,0:T(8,128)(2,1)S(1)} %get-tuple-element.98), channel_id=1, source_target_pairs={{0,1},{1,0},{2,3},{3,2},{4,5},{5,4},{6,7},{7,6},{8,9},{9,8},{10,11... | collective-permute-start | bytes 1179656 | tf_op jit(solution)/shard_map/ppermute | solution.py:587
  144.1 21.9 %collective-permute-start.22 = (bf16[4,64,640]{2,1,0:T(8,128)(2,1)S(1)}, bf16[4,64,640]{2,1,0:T(8,128)(2,1)S(1)}, u32[]{:S(2)}, u32[]{:S(2)}) collective-permute-start(bf16[4,64,640]{2,1,0:T(8,128)(2,1)S(1)} %slice_bitcast_fusion), channel_id=1, source_target_pairs={{0,2},{1,3},{2,0},{3,1},{4,6},{5,7},{6,4},{7,5},{8,10},{9,11},{10,... | collective-permute-start | bytes 983048 | tf_op jit(solution)/shard_map/ppermute | solution.py:587
  145.6 6.1 %copy-start.7 = (bf16[1024,512]{1,0:T(8,128)(2,1)S(1)}, bf16[1024,512]{1,0:T(8,128)(2,1)}, u32[]{:S(2)}) copy-start(bf16[1024,512]{1,0:T(8,128)(2,1)} %get-tuple-element.99.cg_ref) | copy-start | bytes 3145732
  145.7 20.3 %collective-permute-start.24 = (bf16[2,64,512]{2,1,0:T(8,128)(2,1)S(1)}, bf16[2,64,512]{2,1,0:T(8,128)(2,1)S(1)}, u32[]{:S(2)}, u32[]{:S(2)}) collective-permute-start(bf16[2,64,512]{2,1,0:T(8,128)(2,1)S(1)} %get-tuple-element.192), channel_id=1, source_target_pairs={{0,8},{4,12},{8,16},{12,20},{16,24},{20,28},{24,0},{28,4},{1,9},{5... | collective-permute-start | bytes 393224 | tf_op jit(solution)/shard_map/ppermute | solution.py:592
  148.4 17.6 %collective-permute-start.25 = (bf16[2,64,512]{2,1,0:T(8,128)(2,1)S(1)}, bf16[2,64,512]{2,1,0:T(8,128)(2,1)S(1)}, u32[]{:S(2)}, u32[]{:S(2)}) collective-permute-start(bf16[2,64,512]{2,1,0:T(8,128)(2,1)S(1)} %get-tuple-element.191), channel_id=1, source_target_pairs={{0,16},{4,20},{8,24},{12,28},{16,0},{20,4},{24,8},{28,12},{1,17},{... | collective-permute-start | bytes 393224 | tf_op jit(solution)/shard_map/ppermute | solution.py:592
  149.2 16.8 %collective-permute-start.26 = (bf16[2,64,512]{2,1,0:T(8,128)(2,1)S(1)}, bf16[2,64,512]{2,1,0:T(8,128)(2,1)S(1)}, u32[]{:S(2)}, u32[]{:S(2)}) collective-permute-start(bf16[2,64,512]{2,1,0:T(8,128)(2,1)S(1)} %get-tuple-element.190), channel_id=1, source_target_pairs={{0,24},{4,28},{8,0},{12,4},{16,8},{20,12},{24,16},{28,20},{1,25},{... | collective-permute-start | bytes 393224 | tf_op jit(solution)/shard_map/ppermute | solution.py:592
  150.9 15.1 %collective-permute-start.23 = (bf16[512,384]{1,0:T(8,128)(2,1)S(1)}, bf16[512,384]{1,0:T(8,128)(2,1)S(1)}, u32[]{:S(2)}, u32[]{:S(2)}) collective-permute-start(bf16[512,384]{1,0:T(8,128)(2,1)S(1)} %add_convert_fusion.3), channel_id=1, source_target_pairs={{0,2},{1,3},{2,0},{3,1},{4,6},{5,7},{6,4},{7,5},{8,10},{9,11},{10,... | collective-permute-start | bytes 1179656 | tf_op jit(solution)/shard_map/ppermute | solution.py:587
  151.8 18.3 %copy-start.4 = (bf16[512,1536]{1,0:T(8,128)(2,1)S(1)}, bf16[512,1536]{1,0:T(8,128)(2,1)}, u32[]{:S(2)}) copy-start(bf16[512,1536]{1,0:T(8,128)(2,1)} %get-tuple-element.109.w_ref) | copy-start | bytes 4718596
  166.0 4.0 %copy-start.3 = (f32[1024,512]{1,0:T(8,128)S(1)}, f32[1024,512]{1,0:T(8,128)}, u32[]{:S(2)}) copy-start(f32[1024,512]{1,0:T(8,128)} %get-tuple-element.108.mg_ref) | copy-start | bytes 6291460
  167.5 6.5 %collective-permute-start.28 = (bf16[64,640]{1,0:T(8,128)(2,1)S(1)}, bf16[64,640]{1,0:T(8,128)(2,1)S(1)}, u32[]{:S(2)}, u32[]{:S(2)}) collective-permute-start(bf16[64,640]{1,0:T(8,128)(2,1)S(1)} %get-tuple-element.197), channel_id=1, source_target_pairs={{0,8},{4,12},{8,16},{12,20},{16,24},{20,28},{24,0},{28,4},{1,9},{5... | collective-permute-start | bytes 245768 | tf_op jit(solution)/shard_map/ppermute | solution.py:592
  168.7 7.6 %collective-permute-start.29 = (bf16[64,640]{1,0:T(8,128)(2,1)S(1)}, bf16[64,640]{1,0:T(8,128)(2,1)S(1)}, u32[]{:S(2)}, u32[]{:S(2)}) collective-permute-start(bf16[64,640]{1,0:T(8,128)(2,1)S(1)} %get-tuple-element.196), channel_id=1, source_target_pairs={{0,16},{4,20},{8,24},{12,28},{16,0},{20,4},{24,8},{28,12},{1,17},{... | collective-permute-start | bytes 245768 | tf_op jit(solution)/shard_map/ppermute | solution.py:592
  170.0 6.2 %collective-permute-start.27 = (bf16[512,384]{1,0:T(8,128)(2,1)S(1)}, bf16[512,384]{1,0:T(8,128)(2,1)S(1)}, u32[]{:S(2)}, u32[]{:S(2)}) collective-permute-start(bf16[512,384]{1,0:T(8,128)(2,1)S(1)} %get-tuple-element.111), channel_id=1, source_target_pairs={{0,1},{1,0},{2,3},{3,2},{4,5},{5,4},{6,7},{7,6},{8,9},{9,8},{10,11... | collective-permute-start | bytes 1179656 | tf_op jit(solution)/shard_map/ppermute | solution.py:587
  174.1 2.2 copy-start.13
  176.2 0.6 copy-start.15
  176.9 0.7 copy-start.9
  177.6 37.7 %all-to-all-start.1 = ((bf16[32,136,128]{2,1,0:T(8,128)(2,1)}), bf16[32,136,128]{2,1,0:T(8,128)(2,1)S(1)}, u32[]{:S(2)}, u32[]{:S(2)}) async-start(bf16[32,136,128]{2,1,0:T(8,128)(2,1)} %bitcast.26), calls=%async_computation.1 | async-start | bytes 2228224 | tf_op jit(solution)/shard_map/all_to_all | solution.py:802
  182.6 13.1 %collective-permute-start.31 = (bf16[4,64,384]{2,1,0:T(8,128)(2,1)}, bf16[4,64,384]{2,1,0:T(8,128)(2,1)S(1)}, u32[]{:S(2)}, u32[]{:S(2)}) collective-permute-start(bf16[4,64,384]{2,1,0:T(8,128)(2,1)} %fusion.4), channel_id=1, source_target_pairs={{0,4},{4,0},{8,12},{12,8},{16,20},{20,16},{24,28},{28,24},{1,5},{5... | collective-permute-start | bytes 589832 | tf_op jit(solution)/shard_map/ppermute | solution.py:592
  184.3 29.0 %copy-start.14 = (bf16[64,640]{1,0:T(8,128)(2,1)S(1)}, bf16[64,640]{1,0:T(8,128)(2,1)}, u32[]{:S(2)}) copy-start(bf16[64,640]{1,0:T(8,128)(2,1)} %copy-done.13) | copy-start | bytes 245764
  184.3 29.0 %copy-start.16 = (bf16[64,640]{1,0:T(8,128)(2,1)S(1)}, bf16[64,640]{1,0:T(8,128)(2,1)}, u32[]{:S(2)}) copy-start(bf16[64,640]{1,0:T(8,128)(2,1)} %copy-done.15) | copy-start | bytes 245764
  184.3 17.3 %collective-permute-start.35 = (bf16[1,64,512]{2,1,0:T(8,128)(2,1)}, bf16[1,64,512]{2,1,0:T(8,128)(2,1)S(1)}, u32[]{:S(2)}, u32[]{:S(2)}) collective-permute-start(bf16[1,64,512]{2,1,0:T(8,128)(2,1)} %dynamic-slice_convert_fusion), channel_id=1, source_target_pairs={{0,4},{4,0},{8,12},{12,8},{16,20},{20,16},{24,28},{28,24},{1,5},{5... | collective-permute-start | bytes 196616 | tf_op jit(solution)/shard_map/ppermute | solution.py:592
  184.7 17.6 %collective-permute-start.30 = (bf16[64,640]{1,0:T(8,128)(2,1)}, bf16[64,640]{1,0:T(8,128)(2,1)S(1)}, u32[]{:S(2)}, u32[]{:S(2)}) collective-permute-start(bf16[64,640]{1,0:T(8,128)(2,1)} %get-tuple-element.194), channel_id=1, source_target_pairs={{0,24},{4,28},{8,0},{12,4},{16,8},{20,12},{24,16},{28,20},{1,25},{... | collective-permute-start | bytes 245768 | tf_op jit(solution)/shard_map/ppermute | solution.py:592
  196.8 9.5 %collective-permute-start.32 = (bf16[64,384]{1,0:T(8,128)(2,1)S(1)}, bf16[64,384]{1,0:T(8,128)(2,1)S(1)}, u32[]{:S(2)}, u32[]{:S(2)}) collective-permute-start(bf16[64,384]{1,0:T(8,128)(2,1)S(1)} %get-tuple-element.200), channel_id=1, source_target_pairs={{0,8},{4,12},{8,16},{12,20},{16,24},{20,28},{24,0},{28,4},{1,9},{5... | collective-permute-start | bytes 147464 | tf_op jit(solution)/shard_map/ppermute | solution.py:592
  198.1 15.2 %collective-permute-start.33 = (bf16[64,384]{1,0:T(8,128)(2,1)S(1)}, bf16[64,384]{1,0:T(8,128)(2,1)S(1)}, u32[]{:S(2)}, u32[]{:S(2)}) collective-permute-start(bf16[64,384]{1,0:T(8,128)(2,1)S(1)} %get-tuple-element.199), channel_id=1, source_target_pairs={{0,16},{4,20},{8,24},{12,28},{16,0},{20,4},{24,8},{28,12},{1,17},{... | collective-permute-start | bytes 147464 | tf_op jit(solution)/shard_map/ppermute | solution.py:592
  201.6 11.7 %collective-permute-start.34 = (bf16[64,384]{1,0:T(8,128)(2,1)S(1)}, bf16[64,384]{1,0:T(8,128)(2,1)S(1)}, u32[]{:S(2)}, u32[]{:S(2)}) collective-permute-start(bf16[64,384]{1,0:T(8,128)(2,1)S(1)} %get-tuple-element.198), channel_id=1, source_target_pairs={{0,24},{4,28},{8,0},{12,4},{16,8},{20,12},{24,16},{28,20},{1,25},{... | collective-permute-start | bytes 147464 | tf_op jit(solution)/shard_map/ppermute | solution.py:592

commit v16 on v14

--- a/solution.py
+++ b/solution.py
@@ -790,9 +790,8 @@
         near = [grouped(value[None])[0] for value in (own_part, came_one, came_far)]
         qkv_value, qkv_pieces = fold_coarse(fold_pair(near)[1]())
         down_total = add_wide(*down_rest())[0]
-        pieces = together(*up_pieces, *qkv_pieces)
-        up_total = add_wide(*pieces[: len(up_pieces)])
-        qkv_total = add_wide(*pieces[len(up_pieces) :])
+        *up_pieces, qkv_pieces[1] = together(*up_pieces, qkv_pieces[1])
+        up_total = add_wide(*up_pieces)
     else:
         up_total = exchange_rows(add(*fold_far([up_keep, up_came])[1]()))
         down_total = exchange_rows(add(*fold_far([down_keep, down_came])[1]()))
@@ -806,6 +805,9 @@
         .set(jnp.arange(total_seqs, dtype=jnp.int32))
     )
     states_grad = returned[inverse][:, :tokens]
+    if direct:
+        *qkv_pieces, states_grad = together(*qkv_pieces, states_grad)
+        qkv_total = add_wide(*qkv_pieces)
     gain_grads = jnp.sum(returned[:, tokens:].astype(F32), axis=0).reshape(2, devices, per)
     gain_grads = lax.dynamic_index_in_dim(gain_grads, own, 1, keepdims=False)
     return (

time: 219 us -> 217 us (level)
  Pallas kernels: 75.9 us -> 84.2 us
  waiting for transfers between devices: 56.4 us -> 48.6 us
  starting transfers between devices: 57.5 us -> 51.2 us
    ppermute x20, waiting for transfers between devices: 47 us -> 38.8 us  [along_dp(): return lax.ppermute(value, 'dp', [(i, move(i)) for i in range(count)])]
    ppermute x16, starting transfers between devices: 16.1 us -> 9.16 us  [swap(): return lax.ppermute(value, 'tensor', [(i, i ^ apart) for i in range(count)])]
    pallas_call x1, Pallas kernels: 22.8 us -> 28.4 us  [middle_block(): pl.pallas_call(functools.partial(middle_kernel, groups), grid_spec=pltpu....]
    all_to_all x1, waiting for transfers between devices: 0.01 us -> 2.89 us  [on_device(): lax.all_to_all(begin_grad.reshape(devices, tokens + SPARE, width), both,...]
    ppermute x16, waiting for transfers between devices: 9.4 us -> 6.96 us  [swap(): return lax.ppermute(value, 'tensor', [(i, i ^ apart) for i in range(count)])]
  transfers between devices with their start and end apart: 38 -> 38, of which waited for: 12 -> 14; matrix products, arithmetic and copies ran while one was open for 8% -> 10% of each run, Pallas kernels for 24% -> 26%
where the time goes in v16:
time: 217 us; the launch traced here: 216 us
  Pallas kernels  84.2 us (39%)
  starting transfers between devices  51.2 us (24%)
  waiting for transfers between devices  48.6 us (22%)
  other arithmetic  14.3 us (7%)
  local copies, waits for them, and re-layouts  14 us (6%)
  between operations  3.75 us (2%)
    ppermute x20, waiting for transfers between devices, along_dp(): return lax.ppermute(value, 'dp', [(i, move(i)) for i in range(count)])  38.8 us
    ppermute x20, starting transfers between devices, along_dp(): return lax.ppermute(value, 'dp', [(i, move(i)) for i in range(count)])  35.5 us
    pallas_call x2, Pallas kernels, attend_back(): pl.pallas_call(attend_back_kernel, grid_spec=pltpu.PrefetchScalarGridSpec...  29.1 us
    pallas_call x1, Pallas kernels, middle_block(): pl.pallas_call(functools.partial(middle_kernel, groups), grid_spec=pltpu....  28.4 us
    pallas_call x1, Pallas kernels, attend(): pl.pallas_call(attend_kernel, grid_spec=pltpu.PrefetchScalarGridSpec(num_...  15.4 us
    ppermute x16, starting transfers between devices, swap(): return lax.ppermute(value, 'tensor', [(i, i ^ apart) for i in range(count)])  9.16 us
    ppermute x16, waiting for transfers between devices, swap(): return lax.ppermute(value, 'tensor', [(i, i ^ apart) for i in range(count)])  6.96 us
    pallas_call x1, Pallas kernels, project(): pl.pallas_call(functools.partial(project_kernel, groups), grid_spec=pltpu...  6.29 us
  transfers between devices with their start and end apart: 38, of which 14 were waited for; matrix products, arithmetic and copies ran while one was open for 10% of the time, Pallas kernels for 26%

profile of v16, /device:TPU:0, one launch (start us, length us, event | category | flops | bytes accessed | tf_op | source)
XLA Modules:
  0.0 216.1 jit_solution(910142324228876535)
XLA Ops:
  0.6 1.0 pad_maximum_fusion.2
  1.6 3.1 %collective-permute-start.6 = (bf16[64,1152]{1,0:T(8,128)(2,1)S(1)}, bf16[64,1152]{1,0:T(8,128)(2,1)S(1)}, u32[]{:S(2)}, u32[]{:S(2)}) collective-permute-start(bf16[64,1152]{1,0:T(8,128)(2,1)S(1)} %pad_maximum_fusion.2), channel_id=1, source_target_pairs={{0,8},{4,12},{8,16},{12,20},{16,24},{20,28},{24,0},{28,4},{1,9},{5... | collective-permute-start | bytes 442376 | tf_op jit(solution)/shard_map/ppermute | solution.py:592
  4.7 2.6 %collective-permute-start.7 = (bf16[64,1152]{1,0:T(8,128)(2,1)S(1)}, bf16[64,1152]{1,0:T(8,128)(2,1)S(1)}, u32[]{:S(2)}, u32[]{:S(2)}) collective-permute-start(bf16[64,1152]{1,0:T(8,128)(2,1)S(1)} %pad_maximum_fusion.2), channel_id=1, source_target_pairs={{0,16},{4,20},{8,24},{12,28},{16,0},{20,4},{24,8},{28,12},{1,17},{... | collective-permute-start | bytes 442376 | tf_op jit(solution)/shard_map/ppermute | solution.py:592
  7.3 1.3 collective-permute-start.8
  8.6 0.8 copy_bitcast_fusion.1
  9.4 1.5 collective-permute-start
  11.0 0.7 fusion.9
  12.5 0.7 gather_fusion
  13.2 1.2 pad_maximum_fusion
  14.4 2.8 %all-to-all-start = ((bf16[32,136,128]{2,1,0:T(8,128)(2,1)}), bf16[32,136,128]{2,1,0:T(8,128)(2,1)S(1)}, u32[]{:S(2)}, u32[]{:S(2)}) async-start(bf16[32,136,128]{2,1,0:T(8,128)(2,1)} %pad_maximum_fusion), calls=%async_computation | async-start | bytes 2228224 | tf_op jit(solution)/shard_map/all_to_all | solution.py:734
  17.3 1.7 collective-permute-start.1
  19.0 2.5 %collective-permute-start.2 = (bf16[64,768]{1,0:T(8,128)(2,1)S(1)}, bf16[64,768]{1,0:T(8,128)(2,1)S(1)}, u32[]{:S(2)}, u32[]{:S(2)}) collective-permute-start(bf16[64,768]{1,0:T(8,128)(2,1)S(1)} %constant_dynamic-update-slice_fusion), channel_id=1, source_target_pairs={{0,16},{4,20},{8,24},{12,28},{16,0},{20,4},{24,8},{28,12},{1,17},{... | collective-permute-start | bytes 294920 | tf_op jit(solution)/shard_map/ppermute | solution.py:592
  21.5 1.4 collective-permute-start.3
  23.0 0.9 pad_maximum_fusion.1.refs_0_
  23.8 1.5 collective-permute-start.10
  25.3 1.5 collective-permute-start.9
  26.8 15.6 %collective-permute-done.1 = bf16[64,768]{1,0:T(8,128)(2,1)S(1)} collective-permute-done((bf16[64,768]{1,0:T(8,128)(2,1)S(1)}, bf16[64,768]{1,0:T(8,128)(2,1)S(1)}, u32[]{:S(2)}, u32[]{:S(2)}) %collective-permute-start.1) | collective-permute-done | bytes 98336 | tf_op jit(solution)/shard_map/ppermute | solution.py:592
  42.4 9.2 %collective-permute-done.2 = bf16[64,768]{1,0:T(8,128)(2,1)S(1)} collective-permute-done((bf16[64,768]{1,0:T(8,128)(2,1)S(1)}, bf16[64,768]{1,0:T(8,128)(2,1)S(1)}, u32[]{:S(2)}, u32[]{:S(2)}) %collective-permute-start.2) | collective-permute-done | bytes 98336 | tf_op jit(solution)/shard_map/ppermute | solution.py:592
  51.7 1.6 collective-permute-start.5
  56.5 1.2 dynamic-slice.10
  58.4 1.2 dynamic-slice.9.limit_ref
  59.7 2.3 %collective-permute-done.5.refs_2_ = bf16[512,384]{1,0:T(8,128)(2,1)S(1)} collective-permute-done((bf16[512,384]{1,0:T(8,128)(2,1)S(1)}, bf16[512,384]{1,0:T(8,128)(2,1)S(1)}, u32[]{:S(2)}, u32[]{:S(2)}) %collective-permute-start.5) | collective-permute-done | bytes 393248 | tf_op jit(solution)/shard_map/ppermute | solution.py:587
  62.0 1.6 collective-permute-start.15
  64.5 1.0 collective-permute-done.11.refs_3_
  65.4 6.3 %project.1 = (bf16[1024,1536]{1,0:T(8,128)(2,1)S(1)}, bf16[512,1024]{1,0:T(8,128)(2,1)}, bf16[512,1536]{1,0:T(8,128)(2,1)}) custom-call(s32[1]{0:T(128)} %dynamic-slice.9.limit_ref, s32[8]{0:T(128)S(1)} %pad_add_fusion.place_ref, bf16[8,4,136,128]{3,2,1,0:T(8,128)(2,1)S(1)} %bitcast.109, f32[1,512]{1,0:T(1,128)S(1)} %pad_maximum_fusion.3.clock_ref, ...), custom_call_target="tpu_custom_call" | custom-call | flops 5750000128 | bytes 1048576 | tf_op jit(solution)/shard_map/project/pallas_call | solution.py:111
  71.7 15.4 %attend.1 = (bf16[1024,512]{1,0:T(8,128)(2,1)}, bf16[512,1024]{1,0:T(8,128)(2,1)}, f32[4,2,1024]{2,1,0:T(2,128)S(1)}) custom-call(s32[1]{0:T(128)} %dynamic-slice.9.limit_ref, bf16[1024,1536]{1,0:T(8,128)(2,1)S(1)} %get-tuple-element.70.q_ref.k_ref.v_ref, bf16[1024,1536]{1,0:T(8,128)(2,1)S(1)} %get-tuple-element.70.q_ref.k_ref.v_ref, ...), custom_call_target="tpu_custom_call" | custom-call | flops 17250000896 | bytes 1048576 | tf_op jit(solution)/shard_map/attend/pallas_call | solution.py:200
  88.1 1.3 collective-permute-done.16.refs_7_
  89.4 0.8 copy-done.17
  90.2 28.4 %middle.1 = (bf16[1,1024,512]{2,1,0:T(8,128)(2,1)}, bf16[1024,512]{1,0:T(8,128)(2,1)}, f32[1024,512]{1,0:T(8,128)}, f32[1,512]{1,0:T(1,128)S(1)}, bf16[2,512,640...) custom-call(s32[1]{0:T(128)} %dynamic-slice.9.limit_ref, ...), custom_call_target="tpu_custom_call" | custom-call | flops 28750000128 | bytes 1048576 | tf_op jit(solution)/shard_map/middle/pallas_call | solution.py:370
  119.2 2.4 %collective-permute-done.17 = bf16[2,512,512]{2,1,0:T(8,128)(2,1)S(1)} collective-permute-done((bf16[2,512,512]{2,1,0:T(8,128)(2,1)}, bf16[2,512,512]{2,1,0:T(8,128)(2,1)S(1)}, u32[]{:S(2)}, u32[]{:S(2)}) %collective-permute-start.17) | collective-permute-done | bytes 1048608 | tf_op jit(solution)/shard_map/ppermute | solution.py:587
  121.6 1.6 convert_add_fusion
  123.2 0.9 collective-permute-start.19
  124.1 1.4 fusion.1
  125.6 1.9 collective-permute-start.20
  127.5 14.9 %attend_back.2 = (bf16[1024,768]{1,0:T(8,128)(2,1)S(1)}, bf16[512,384]{1,0:T(8,128)(2,1)S(1)}, bf16[512,384]{1,0:T(8,128)(2,1)S(1)}) custom-call(s32[1]{0:T(128)} %dynamic-slice.9.limit_ref, bf16[1024,1536]{1,0:T(8,128)(2,1)S(1)} %copy-done.2, bf16[1024,1536]{1,0:T(8,128)(2,1)S(1)} %copy-done.2, bf16[1024,1536]{1,0:T(8,128)(2,1)S(1)} %copy-done.2, ...), custom_call_target="tpu_custom_call" | custom-call | flops 18400000000 | bytes 1048576 | tf_op jit(solution)/shard_map/attend_back/pallas_call | solution.py:466
  142.5 1.3 fusion
  143.9 0.9 collective-permute-start.22
  145.0 3.4 %collective-permute-start.24 = (bf16[2,64,512]{2,1,0:T(8,128)(2,1)S(1)}, bf16[2,64,512]{2,1,0:T(8,128)(2,1)S(1)}, u32[]{:S(2)}, u32[]{:S(2)}) collective-permute-start(bf16[2,64,512]{2,1,0:T(8,128)(2,1)S(1)} %get-tuple-element.194), channel_id=1, source_target_pairs={{0,8},{4,12},{8,16},{12,20},{16,24},{20,28},{24,0},{28,4},{1,9},{5... | collective-permute-start | bytes 393224 | tf_op jit(solution)/shard_map/ppermute | solution.py:592
  148.4 1.0 collective-permute-start.25
  149.4 1.4 collective-permute-start.26
  150.9 0.8 collective-permute-start.23
  151.7 14.2 %attend_back.3 = (bf16[1024,768]{1,0:T(8,128)(2,1)S(1)}, bf16[512,384]{1,0:T(8,128)(2,1)S(1)}, bf16[512,384]{1,0:T(8,128)(2,1)S(1)}) custom-call(s32[1]{0:T(128)} %dynamic-slice.9.limit_ref, bf16[1024,1536]{1,0:T(8,128)(2,1)S(1)} %copy-done.2, bf16[1024,1536]{1,0:T(8,128)(2,1)S(1)} %copy-done.2, bf16[1024,1536]{1,0:T(8,128)(2,1)S(1)} %copy-done.2, ...), custom_call_target="tpu_custom_call" | custom-call | flops 18400000000 | bytes 1048576 | tf_op jit(solution)/shard_map/attend_back/pallas_call | solution.py:466
  166.8 0.7 dynamic-slice_bitcast_fusion.4
  167.5 0.9 collective-permute-start.28
  168.5 5.0 %begin_back.1 = bf16[8,4,136,128]{3,2,1,0:T(8,128)(2,1)} custom-call(s32[1]{0:T(128)} %dynamic-slice.9.limit_ref, bf16[8,4,136,128]{3,2,1,0:T(8,128)(2,1)S(1)} %bitcast.111, f32[1,512]{1,0:T(1,128)S(1)} %pad_maximum_fusion.3.clock_ref, f32[1,512]{1,0:T(1,128)S(1)} %reshape_squeeze.8.gain_ref, f32[1,512]{1,0:T(1,128)S(1)} %get-tuple-element.103.gg_two_ref, ...), custom_call_target="tpu_custom_call" | custom-call | flops 8049999872 | bytes 1048576 | tf_op jit(solution)/shard_map/begin_back/pallas_call | solution.py:554
  174.5 0.7 copy-done.9
  175.3 3.8 %all-to-all-start.1 = ((bf16[32,136,128]{2,1,0:T(8,128)(2,1)}), bf16[32,136,128]{2,1,0:T(8,128)(2,1)S(1)}, u32[]{:S(2)}, u32[]{:S(2)}) async-start(bf16[32,136,128]{2,1,0:T(8,128)(2,1)} %bitcast.37), calls=%async_computation.1 | async-start | bytes 2228224 | tf_op jit(solution)/shard_map/all_to_all | solution.py:799
  179.1 0.7 scatter_custom_fusion
  179.8 1.7 fusion.4
  181.5 1.8 collective-permute-start.29
  183.6 1.8 collective-permute-start.30
  185.3 2.1 collective-permute-start.31
  187.4 7.2 %collective-permute-done.29 = bf16[4,64,384]{2,1,0:T(8,128)(2,1)S(1)} collective-permute-done((bf16[4,64,384]{2,1,0:T(8,128)(2,1)}, bf16[4,64,384]{2,1,0:T(8,128)(2,1)S(1)}, u32[]{:S(2)}, u32[]{:S(2)}) %collective-permute-start.29) | collective-permute-done | bytes 196640 | tf_op jit(solution)/shard_map/ppermute | solution.py:592
  194.6 1.0 fusion.3
  195.7 1.2 collective-permute-start.32
  197.0 0.7 add_bitcast_fusion
  197.6 3.5 %collective-permute-start.33 = (bf16[64,384]{1,0:T(8,128)(2,1)S(1)}, bf16[64,384]{1,0:T(8,128)(2,1)}, u32[]{:S(2)}, u32[]{:S(2)}) collective-permute-start(bf16[64,384]{1,0:T(8,128)(2,1)S(1)} %get-tuple-element.201), channel_id=1, source_target_pairs={{0,16},{4,20},{8,24},{12,28},{16,0},{20,4},{24,8},{28,12},{1,17},{... | collective-permute-start | bytes 147464 | tf_op jit(solution)/shard_map/ppermute | solution.py:592
  201.7 2.3 %collective-permute-done.30 = bf16[64,640]{1,0:T(8,128)(2,1)S(1)} collective-permute-done((bf16[64,640]{1,0:T(8,128)(2,1)}, bf16[64,640]{1,0:T(8,128)(2,1)S(1)}, u32[]{:S(2)}, u32[]{:S(2)}) %collective-permute-start.30) | collective-permute-done | bytes 81952 | tf_op jit(solution)/shard_map/ppermute | solution.py:592
  203.9 2.9 %collective-permute-done.32 = bf16[64,384]{1,0:T(8,128)(2,1)S(1)} collective-permute-done((bf16[64,384]{1,0:T(8,128)(2,1)S(1)}, bf16[64,384]{1,0:T(8,128)(2,1)S(1)}, u32[]{:S(2)}, u32[]{:S(2)}) %collective-permute-start.32) | collective-permute-done | bytes 49184 | tf_op jit(solution)/shard_map/ppermute | solution.py:592
  208.2 2.9 %all-to-all-done.1 = bf16[32,136,128]{2,1,0:T(8,128)(2,1)S(1)} async-done(((bf16[32,136,128]{2,1,0:T(8,128)(2,1)}), bf16[32,136,128]{2,1,0:T(8,128)(2,1)S(1)}, u32[]{:S(2)}, u32[]{:S(2)}) %all-to-all-start.1) | async-done | bytes 1114144 | tf_op jit(solution)/shard_map/all_to_all | solution.py:799
  211.1 0.8 gather_fusion.1
  211.8 1.1 slice.117
  212.9 1.0 collective-permute-done.33
  214.6 1.5 copy_bitcast_fusion
  (121 shorter events, 9.9 us)
Async XLA Ops:
  0.6 11.8 %copy-start = (bf16[32,128,128]{2,1,0:T(8,128)(2,1)S(1)}, bf16[32,128,128]{2,1,0:T(8,128)(2,1)}, u32[]{:S(2)}) copy-start(bf16[32,128,128]{2,1,0:T(8,128)(2,1)} %param.11) | copy-start | bytes 3145732
  1.6 19.9 %collective-permute-start.6 = (bf16[64,1152]{1,0:T(8,128)(2,1)S(1)}, bf16[64,1152]{1,0:T(8,128)(2,1)S(1)}, u32[]{:S(2)}, u32[]{:S(2)}) collective-permute-start(bf16[64,1152]{1,0:T(8,128)(2,1)S(1)} %pad_maximum_fusion.2), channel_id=1, source_target_pairs={{0,8},{4,12},{8,16},{12,20},{16,24},{20,28},{24,0},{28,4},{1,9},{5... | collective-permute-start | bytes 442376 | tf_op jit(solution)/shard_map/ppermute | solution.py:592
  4.7 18.2 %collective-permute-start.7 = (bf16[64,1152]{1,0:T(8,128)(2,1)S(1)}, bf16[64,1152]{1,0:T(8,128)(2,1)S(1)}, u32[]{:S(2)}, u32[]{:S(2)}) collective-permute-start(bf16[64,1152]{1,0:T(8,128)(2,1)S(1)} %pad_maximum_fusion.2), channel_id=1, source_target_pairs={{0,16},{4,20},{8,24},{12,28},{16,0},{20,4},{24,8},{28,12},{1,17},{... | collective-permute-start | bytes 442376 | tf_op jit(solution)/shard_map/ppermute | solution.py:592
  7.3 15.6 %collective-permute-start.8 = (bf16[64,1152]{1,0:T(8,128)(2,1)S(1)}, bf16[64,1152]{1,0:T(8,128)(2,1)S(1)}, u32[]{:S(2)}, u32[]{:S(2)}) collective-permute-start(bf16[64,1152]{1,0:T(8,128)(2,1)S(1)} %pad_maximum_fusion.2), channel_id=1, source_target_pairs={{0,24},{4,28},{8,0},{12,4},{16,8},{20,12},{24,16},{28,20},{1,25},{... | collective-permute-start | bytes 442376 | tf_op jit(solution)/shard_map/ppermute | solution.py:592
  9.4 7.8 %collective-permute-start = (bf16[64,384]{1,0:T(8,128)(2,1)S(1)}, bf16[64,384]{1,0:T(8,128)(2,1)S(1)}, u32[]{:S(2)}, u32[]{:S(2)}) collective-permute-start(bf16[64,384]{1,0:T(8,128)(2,1)S(1)} %copy_bitcast_fusion.1), channel_id=1, source_target_pairs={{0,4},{4,0},{8,12},{12,8},{16,20},{20,16},{24,28},{28,24},{1,5},{5... | collective-permute-start | bytes 147464 | tf_op jit(solution)/shard_map/ppermute | solution.py:592
  14.4 2.8 %copy-start.12 = (bf16[64,3,128]{2,0,1:T(8,128)(2,1)S(1)}, bf16[64,3,128]{2,0,1:T(8,128)(2,1)}, u32[]{:S(2)}) copy-start(bf16[64,3,128]{2,0,1:T(8,128)(2,1)} %param.15) | copy-start | bytes 147460
  14.4 8.6 %copy-start.10 = (bf16[512,64]{0,1:T(8,128)(2,1)S(1)}, bf16[512,64]{0,1:T(8,128)(2,1)}, u32[]{:S(2)}) copy-start(bf16[512,64]{0,1:T(8,128)(2,1)} %param.18) | copy-start | bytes 196612
  14.4 8.6 %copy-start.11 = (bf16[64,512]{1,0:T(8,128)(2,1)S(1)}, bf16[64,512]{1,0:T(8,128)(2,1)}, u32[]{:S(2)}) copy-start(bf16[64,512]{1,0:T(8,128)(2,1)} %param.17) | copy-start | bytes 196612
  14.4 8.6 %copy-start.15 = (bf16[128,64]{0,1:T(8,128)(2,1)S(1)}, bf16[128,64]{0,1:T(8,128)(2,1)}, u32[]{:S(2)}) copy-start(bf16[128,64]{0,1:T(8,128)(2,1)} %param.16) | copy-start | bytes 49156
  14.4 49.4 %all-to-all-start = ((bf16[32,136,128]{2,1,0:T(8,128)(2,1)}), bf16[32,136,128]{2,1,0:T(8,128)(2,1)S(1)}, u32[]{:S(2)}, u32[]{:S(2)}) async-start(bf16[32,136,128]{2,1,0:T(8,128)(2,1)} %pad_maximum_fusion), calls=%async_computation | async-start | bytes 2228224 | tf_op jit(solution)/shard_map/all_to_all | solution.py:734
  17.2 36.7 %copy-start.18 = (s32[32]{0:T(128)S(1)}, s32[32]{0:T(128)}, u32[]{:S(2)}) copy-start(s32[32]{0:T(128)} %param.14) | copy-start | bytes 388
  17.3 25.1 %collective-permute-start.1 = (bf16[64,768]{1,0:T(8,128)(2,1)S(1)}, bf16[64,768]{1,0:T(8,128)(2,1)S(1)}, u32[]{:S(2)}, u32[]{:S(2)}) collective-permute-start(bf16[64,768]{1,0:T(8,128)(2,1)S(1)} %constant_dynamic-update-slice_fusion), channel_id=1, source_target_pairs={{0,8},{4,12},{8,16},{12,20},{16,24},{20,28},{24,0},{28,4},{1,9},{5... | collective-permute-start | bytes 294920 | tf_op jit(solution)/shard_map/ppermute | solution.py:592
  19.0 32.6 %collective-permute-start.2 = (bf16[64,768]{1,0:T(8,128)(2,1)S(1)}, bf16[64,768]{1,0:T(8,128)(2,1)S(1)}, u32[]{:S(2)}, u32[]{:S(2)}) collective-permute-start(bf16[64,768]{1,0:T(8,128)(2,1)S(1)} %constant_dynamic-update-slice_fusion), channel_id=1, source_target_pairs={{0,16},{4,20},{8,24},{12,28},{16,0},{20,4},{24,8},{28,12},{1,17},{... | collective-permute-start | bytes 294920 | tf_op jit(solution)/shard_map/ppermute | solution.py:592
  21.5 30.1 %collective-permute-start.3 = (bf16[64,768]{1,0:T(8,128)(2,1)S(1)}, bf16[64,768]{1,0:T(8,128)(2,1)S(1)}, u32[]{:S(2)}, u32[]{:S(2)}) collective-permute-start(bf16[64,768]{1,0:T(8,128)(2,1)S(1)} %constant_dynamic-update-slice_fusion), channel_id=1, source_target_pairs={{0,24},{4,28},{8,0},{12,4},{16,8},{20,12},{24,16},{28,20},{1,25},{... | collective-permute-start | bytes 294920 | tf_op jit(solution)/shard_map/ppermute | solution.py:592
  23.8 38.1 %collective-permute-start.10 = (bf16[256,1152]{1,0:T(8,128)(2,1)}, bf16[256,1152]{1,0:T(8,128)(2,1)}, u32[]{:S(2)}, u32[]{:S(2)}) collective-permute-start(bf16[256,1152]{1,0:T(8,128)(2,1)} %pad_maximum_fusion.1.refs_0_), channel_id=1, source_target_pairs={{0,2},{1,3},{2,0},{3,1},{4,6},{5,7},{6,4},{7,5},{8,10},{9,11},{10,... | collective-permute-start | bytes 1769480 | tf_op jit(solution)/shard_map/ppermute | solution.py:587
  25.3 36.7 %collective-permute-start.9 = (bf16[256,1152]{1,0:T(8,128)(2,1)}, bf16[256,1152]{1,0:T(8,128)(2,1)}, u32[]{:S(2)}, u32[]{:S(2)}) collective-permute-start(bf16[256,1152]{1,0:T(8,128)(2,1)} %pad_maximum_fusion.1.refs_0_), channel_id=1, source_target_pairs={{0,4},{4,0},{8,12},{12,8},{16,20},{20,16},{24,28},{28,24},{1,5},{5... | collective-permute-start | bytes 1769480 | tf_op jit(solution)/shard_map/ppermute | solution.py:592
  51.7 10.3 %collective-permute-start.5 = (bf16[512,384]{1,0:T(8,128)(2,1)S(1)}, bf16[512,384]{1,0:T(8,128)(2,1)S(1)}, u32[]{:S(2)}, u32[]{:S(2)}) collective-permute-start(bf16[512,384]{1,0:T(8,128)(2,1)S(1)} %slice_dynamic-update-slice_fusion.refs_0_), channel_id=1, source_target_pairs={{0,2},{1,3},{2,0},{3,1},{4,6},{5,7},{6,4},{7,5},{8,10},{9,11},{10,... | collective-permute-start | bytes 1179656 | tf_op jit(solution)/shard_map/ppermute | solution.py:587
  53.4 10.6 %collective-permute-start.4 = (bf16[512,384]{1,0:T(8,128)(2,1)S(1)}, bf16[512,384]{1,0:T(8,128)(2,1)S(1)}, u32[]{:S(2)}, u32[]{:S(2)}) collective-permute-start(bf16[512,384]{1,0:T(8,128)(2,1)S(1)} %slice_dynamic-update-slice_fusion.refs_0_), channel_id=1, source_target_pairs={{0,1},{1,0},{2,3},{3,2},{4,5},{5,4},{6,7},{7,6},{8,9},{9,8},{10,11... | collective-permute-start | bytes 1179656 | tf_op jit(solution)/shard_map/ppermute | solution.py:587
  53.4 33.7 %collective-permute-start.12 = (bf16[256,1152]{1,0:T(8,128)(2,1)}, bf16[256,1152]{1,0:T(8,128)(2,1)}, u32[]{:S(2)}, u32[]{:S(2)}) collective-permute-start(bf16[256,1152]{1,0:T(8,128)(2,1)} %pad_maximum_fusion.1.refs_0_), channel_id=1, source_target_pairs={{0,1},{1,0},{2,3},{3,2},{4,5},{5,4},{6,7},{7,6},{8,9},{9,8},{10,11... | collective-permute-start | bytes 1769480 | tf_op jit(solution)/shard_map/ppermute | solution.py:587
  62.0 25.1 %collective-permute-start.13 = (bf16[256,1152]{1,0:T(8,128)(2,1)}, bf16[256,1152]{1,0:T(8,128)(2,1)}, u32[]{:S(2)}, u32[]{:S(2)}) collective-permute-start(bf16[256,1152]{1,0:T(8,128)(2,1)} %collective-permute-done.9.refs_1_), channel_id=1, source_target_pairs={{0,1},{1,0},{2,3},{3,2},{4,5},{5,4},{6,7},{7,6},{8,9},{9,8},{10,11... | collective-permute-start | bytes 1769480 | tf_op jit(solution)/shard_map/ppermute | solution.py:587
  62.0 25.1 %collective-permute-start.15 = (bf16[256,1152]{1,0:T(8,128)(2,1)}, bf16[256,1152]{1,0:T(8,128)(2,1)}, u32[]{:S(2)}, u32[]{:S(2)}) collective-permute-start(bf16[256,1152]{1,0:T(8,128)(2,1)} %collective-permute-done.9.refs_1_), channel_id=1, source_target_pairs={{0,2},{1,3},{2,0},{3,1},{4,6},{5,7},{6,4},{7,5},{8,10},{9,11},{10,... | collective-permute-start | bytes 1769480 | tf_op jit(solution)/shard_map/ppermute | solution.py:587
  63.6 1.9 collective-permute-start.11
  64.1 23.1 %collective-permute-start.14 = (bf16[256,1152]{1,0:T(8,128)(2,1)}, bf16[256,1152]{1,0:T(8,128)(2,1)S(1)}, u32[]{:S(2)}, u32[]{:S(2)}) collective-permute-start(bf16[256,1152]{1,0:T(8,128)(2,1)} %collective-permute-done.10.refs_4_), channel_id=1, source_target_pairs={{0,1},{1,0},{2,3},{3,2},{4,5},{5,4},{6,7},{7,6},{8,9},{9,8},{10,11... | collective-permute-start | bytes 1769480 | tf_op jit(solution)/shard_map/ppermute | solution.py:587
  71.7 15.4 %copy-start.1 = (bf16[1024,1536]{1,0:T(8,128)(2,1)}, bf16[1024,1536]{1,0:T(8,128)(2,1)S(1)}, u32[]{:S(2)}) copy-start(bf16[1024,1536]{1,0:T(8,128)(2,1)S(1)} %get-tuple-element.70.q_ref.k_ref.v_ref) | copy-start | bytes 9437188
  87.1 0.8 copy-start.16
  87.1 2.3 %collective-permute-start.16 = (bf16[256,1152]{1,0:T(8,128)(2,1)}, bf16[256,1152]{1,0:T(8,128)(2,1)S(1)}, u32[]{:S(2)}, u32[]{:S(2)}) collective-permute-start(bf16[256,1152]{1,0:T(8,128)(2,1)} %collective-permute-done.15.refs_5_), channel_id=1, source_target_pairs={{0,1},{1,0},{2,3},{3,2},{4,5},{5,4},{6,7},{7,6},{8,9},{9,8},{10,11... | collective-permute-start | bytes 1769480 | tf_op jit(solution)/shard_map/ppermute | solution.py:587
  89.4 0.8 copy-start.17
  118.6 3.0 %collective-permute-start.17 = (bf16[2,512,512]{2,1,0:T(8,128)(2,1)}, bf16[2,512,512]{2,1,0:T(8,128)(2,1)S(1)}, u32[]{:S(2)}, u32[]{:S(2)}) collective-permute-start(bf16[2,512,512]{2,1,0:T(8,128)(2,1)} %get-tuple-element.84), channel_id=1, source_target_pairs={{0,1},{1,0},{2,3},{3,2},{4,5},{5,4},{6,7},{7,6},{8,9},{9,8},{10,11... | collective-permute-start | bytes 3145736 | tf_op jit(solution)/shard_map/ppermute | solution.py:587
  118.8 5.3 %collective-permute-start.18 = (bf16[2,512,640]{2,1,0:T(8,128)(2,1)}, bf16[2,512,640]{2,1,0:T(8,128)(2,1)}, u32[]{:S(2)}, u32[]{:S(2)}) collective-permute-start(bf16[2,512,640]{2,1,0:T(8,128)(2,1)} %get-tuple-element.86), channel_id=1, source_target_pairs={{0,1},{1,0},{2,3},{3,2},{4,5},{5,4},{6,7},{7,6},{8,9},{9,8},{10,11... | collective-permute-start | bytes 3932168 | tf_op jit(solution)/shard_map/ppermute | solution.py:587
  121.6 5.9 %copy-start.2 = (bf16[1024,1536]{1,0:T(8,128)(2,1)S(1)}, bf16[1024,1536]{1,0:T(8,128)(2,1)}, u32[]{:S(2)}) copy-start(bf16[1024,1536]{1,0:T(8,128)(2,1)} %copy-done.1) | copy-start | bytes 9437188
  121.6 5.9 %copy-start.6 = (bf16[512,1024]{1,0:T(8,128)(2,1)S(1)}, bf16[512,1024]{1,0:T(8,128)(2,1)}, u32[]{:S(2)}) copy-start(bf16[512,1024]{1,0:T(8,128)(2,1)} %get-tuple-element.80.turn_ref) | copy-start | bytes 3145732
  123.2 4.3 %copy-start.5 = (bf16[512,1024]{1,0:T(8,128)(2,1)S(1)}, bf16[512,1024]{1,0:T(8,128)(2,1)}, u32[]{:S(2)}) copy-start(bf16[512,1024]{1,0:T(8,128)(2,1)} %get-tuple-element.88.n_turn_ref) | copy-start | bytes 3145732
  123.2 19.2 %collective-permute-start.19 = (bf16[4,2,64,512]{3,2,1,0:T(8,128)(2,1)S(1)}, bf16[4,2,64,512]{3,2,1,0:T(8,128)(2,1)S(1)}, u32[]{:S(2)}, u32[]{:S(2)}) collective-permute-start(bf16[4,2,64,512]{3,2,1,0:T(8,128)(2,1)S(1)} %bitcast.117), channel_id=1, source_target_pairs={{0,2},{1,3},{2,0},{3,1},{4,6},{5,7},{6,4},{7,5},{8,10},{9,11},{10,... | collective-permute-start | bytes 1572872 | tf_op jit(solution)/shard_map/ppermute | solution.py:587
  125.6 16.9 %collective-permute-start.20 = (bf16[2,4,64,640]{3,2,1,0:T(8,128)(2,1)S(1)}, bf16[2,4,64,640]{3,2,1,0:T(8,128)(2,1)S(1)}, u32[]{:S(2)}, u32[]{:S(2)}) collective-permute-start(bf16[2,4,64,640]{3,2,1,0:T(8,128)(2,1)S(1)} %fusion.1), channel_id=1, source_target_pairs={{0,4},{4,0},{8,12},{12,8},{16,20},{20,16},{24,28},{28,24},{1,5},{5... | collective-permute-start | bytes 1966088 | tf_op jit(solution)/shard_map/ppermute | solution.py:592
  127.5 15.0 %copy-start.8 = (bf16[2,512,640]{2,1,0:T(8,128)(2,1)S(1)}, bf16[2,512,640]{2,1,0:T(8,128)(2,1)}, u32[]{:S(2)}) copy-start(bf16[2,512,640]{2,1,0:T(8,128)(2,1)} %get-tuple-element.85) | copy-start | bytes 3932164
  142.4 8.4 %collective-permute-start.21 = (bf16[512,384]{1,0:T(8,128)(2,1)S(1)}, bf16[512,384]{1,0:T(8,128)(2,1)S(1)}, u32[]{:S(2)}, u32[]{:S(2)}) collective-permute-start(bf16[512,384]{1,0:T(8,128)(2,1)S(1)} %get-tuple-element.97), channel_id=1, source_target_pairs={{0,1},{1,0},{2,3},{3,2},{4,5},{5,4},{6,7},{7,6},{8,9},{9,8},{10,11... | collective-permute-start | bytes 1179656 | tf_op jit(solution)/shard_map/ppermute | solution.py:587
  143.9 22.1 %collective-permute-start.22 = (bf16[4,64,640]{2,1,0:T(8,128)(2,1)S(1)}, bf16[4,64,640]{2,1,0:T(8,128)(2,1)S(1)}, u32[]{:S(2)}, u32[]{:S(2)}) collective-permute-start(bf16[4,64,640]{2,1,0:T(8,128)(2,1)S(1)} %slice_bitcast_fusion.1), channel_id=1, source_target_pairs={{0,2},{1,3},{2,0},{3,1},{4,6},{5,7},{6,4},{7,5},{8,10},{9,11},{10,... | collective-permute-start | bytes 983048 | tf_op jit(solution)/shard_map/ppermute | solution.py:587
  144.9 6.8 %copy-start.7 = (bf16[1024,512]{1,0:T(8,128)(2,1)S(1)}, bf16[1024,512]{1,0:T(8,128)(2,1)}, u32[]{:S(2)}) copy-start(bf16[1024,512]{1,0:T(8,128)(2,1)} %get-tuple-element.98.cg_ref) | copy-start | bytes 3145732
  145.0 21.0 %collective-permute-start.24 = (bf16[2,64,512]{2,1,0:T(8,128)(2,1)S(1)}, bf16[2,64,512]{2,1,0:T(8,128)(2,1)S(1)}, u32[]{:S(2)}, u32[]{:S(2)}) collective-permute-start(bf16[2,64,512]{2,1,0:T(8,128)(2,1)S(1)} %get-tuple-element.194), channel_id=1, source_target_pairs={{0,8},{4,12},{8,16},{12,20},{16,24},{20,28},{24,0},{28,4},{1,9},{5... | collective-permute-start | bytes 393224 | tf_op jit(solution)/shard_map/ppermute | solution.py:592
  148.4 17.6 %collective-permute-start.25 = (bf16[2,64,512]{2,1,0:T(8,128)(2,1)S(1)}, bf16[2,64,512]{2,1,0:T(8,128)(2,1)S(1)}, u32[]{:S(2)}, u32[]{:S(2)}) collective-permute-start(bf16[2,64,512]{2,1,0:T(8,128)(2,1)S(1)} %get-tuple-element.193), channel_id=1, source_target_pairs={{0,16},{4,20},{8,24},{12,28},{16,0},{20,4},{24,8},{28,12},{1,17},{... | collective-permute-start | bytes 393224 | tf_op jit(solution)/shard_map/ppermute | solution.py:592
  149.4 16.6 %collective-permute-start.26 = (bf16[2,64,512]{2,1,0:T(8,128)(2,1)S(1)}, bf16[2,64,512]{2,1,0:T(8,128)(2,1)S(1)}, u32[]{:S(2)}, u32[]{:S(2)}) collective-permute-start(bf16[2,64,512]{2,1,0:T(8,128)(2,1)S(1)} %get-tuple-element.192), channel_id=1, source_target_pairs={{0,24},{4,28},{8,0},{12,4},{16,8},{20,12},{24,16},{28,20},{1,25},{... | collective-permute-start | bytes 393224 | tf_op jit(solution)/shard_map/ppermute | solution.py:592
  150.9 15.1 %collective-permute-start.23 = (bf16[512,384]{1,0:T(8,128)(2,1)S(1)}, bf16[512,384]{1,0:T(8,128)(2,1)S(1)}, u32[]{:S(2)}, u32[]{:S(2)}) collective-permute-start(bf16[512,384]{1,0:T(8,128)(2,1)S(1)} %add_convert_fusion.3), channel_id=1, source_target_pairs={{0,2},{1,3},{2,0},{3,1},{4,6},{5,7},{6,4},{7,5},{8,10},{9,11},{10,... | collective-permute-start | bytes 1179656 | tf_op jit(solution)/shard_map/ppermute | solution.py:587
  151.7 16.7 %copy-start.4 = (bf16[512,1536]{1,0:T(8,128)(2,1)S(1)}, bf16[512,1536]{1,0:T(8,128)(2,1)}, u32[]{:S(2)}) copy-start(bf16[512,1536]{1,0:T(8,128)(2,1)} %get-tuple-element.111.w_ref) | copy-start | bytes 4718596
  166.0 2.4 %copy-start.3 = (f32[1024,512]{1,0:T(8,128)S(1)}, f32[1024,512]{1,0:T(8,128)}, u32[]{:S(2)}) copy-start(f32[1024,512]{1,0:T(8,128)} %get-tuple-element.110.mg_ref) | copy-start | bytes 6291460
  167.5 6.4 %collective-permute-start.28 = (bf16[64,640]{1,0:T(8,128)(2,1)S(1)}, bf16[64,640]{1,0:T(8,128)(2,1)S(1)}, u32[]{:S(2)}, u32[]{:S(2)}) collective-permute-start(bf16[64,640]{1,0:T(8,128)(2,1)S(1)} %get-tuple-element.199), channel_id=1, source_target_pairs={{0,16},{4,20},{8,24},{12,28},{16,0},{20,4},{24,8},{28,12},{1,17},{... | collective-permute-start | bytes 245768 | tf_op jit(solution)/shard_map/ppermute | solution.py:592
  168.4 5.5 %collective-permute-start.27 = (bf16[512,384]{1,0:T(8,128)(2,1)S(1)}, bf16[512,384]{1,0:T(8,128)(2,1)S(1)}, u32[]{:S(2)}, u32[]{:S(2)}) collective-permute-start(bf16[512,384]{1,0:T(8,128)(2,1)S(1)} %get-tuple-element.113), channel_id=1, source_target_pairs={{0,1},{1,0},{2,3},{3,2},{4,5},{5,4},{6,7},{7,6},{8,9},{9,8},{10,11... | collective-permute-start | bytes 1179656 | tf_op jit(solution)/shard_map/ppermute | solution.py:587
  173.9 0.6 copy-start.13
  174.5 0.7 copy-start.9
  175.3 35.8 %all-to-all-start.1 = ((bf16[32,136,128]{2,1,0:T(8,128)(2,1)}), bf16[32,136,128]{2,1,0:T(8,128)(2,1)S(1)}, u32[]{:S(2)}, u32[]{:S(2)}) async-start(bf16[32,136,128]{2,1,0:T(8,128)(2,1)} %bitcast.37), calls=%async_computation.1 | async-start | bytes 2228224 | tf_op jit(solution)/shard_map/all_to_all | solution.py:799
  181.5 13.1 %collective-permute-start.29 = (bf16[4,64,384]{2,1,0:T(8,128)(2,1)}, bf16[4,64,384]{2,1,0:T(8,128)(2,1)S(1)}, u32[]{:S(2)}, u32[]{:S(2)}) collective-permute-start(bf16[4,64,384]{2,1,0:T(8,128)(2,1)} %fusion.4), channel_id=1, source_target_pairs={{0,4},{4,0},{8,12},{12,8},{16,20},{20,16},{24,28},{28,24},{1,5},{5... | collective-permute-start | bytes 589832 | tf_op jit(solution)/shard_map/ppermute | solution.py:592
  183.2 23.6 %copy-start.14 = (bf16[64,640]{1,0:T(8,128)(2,1)S(1)}, bf16[64,640]{1,0:T(8,128)(2,1)}, u32[]{:S(2)}) copy-start(bf16[64,640]{1,0:T(8,128)(2,1)} %copy-done.13) | copy-start | bytes 245764
  183.3 13.7 %collective-permute-start.35 = (bf16[1,64,512]{2,1,0:T(8,128)(2,1)}, bf16[1,64,512]{2,1,0:T(8,128)(2,1)S(1)}, u32[]{:S(2)}, u32[]{:S(2)}) collective-permute-start(bf16[1,64,512]{2,1,0:T(8,128)(2,1)} %dynamic-slice_convert_fusion), channel_id=1, source_target_pairs={{0,4},{4,0},{8,12},{12,8},{16,20},{20,16},{24,28},{28,24},{1,5},{5... | collective-permute-start | bytes 196616 | tf_op jit(solution)/shard_map/ppermute | solution.py:592
  183.6 20.4 %collective-permute-start.30 = (bf16[64,640]{1,0:T(8,128)(2,1)}, bf16[64,640]{1,0:T(8,128)(2,1)S(1)}, u32[]{:S(2)}, u32[]{:S(2)}) collective-permute-start(bf16[64,640]{1,0:T(8,128)(2,1)} %get-tuple-element.197), channel_id=1, source_target_pairs={{0,8},{4,12},{8,16},{12,20},{16,24},{20,28},{24,0},{28,4},{1,9},{5... | collective-permute-start | bytes 245768 | tf_op jit(solution)/shard_map/ppermute | solution.py:592
  185.3 18.6 %collective-permute-start.31 = (bf16[64,640]{1,0:T(8,128)(2,1)}, bf16[64,640]{1,0:T(8,128)(2,1)S(1)}, u32[]{:S(2)}, u32[]{:S(2)}) collective-permute-start(bf16[64,640]{1,0:T(8,128)(2,1)} %get-tuple-element.196), channel_id=1, source_target_pairs={{0,24},{4,28},{8,0},{12,4},{16,8},{20,12},{24,16},{28,20},{1,25},{... | collective-permute-start | bytes 245768 | tf_op jit(solution)/shard_map/ppermute | solution.py:592
  195.7 11.2 %collective-permute-start.32 = (bf16[64,384]{1,0:T(8,128)(2,1)S(1)}, bf16[64,384]{1,0:T(8,128)(2,1)S(1)}, u32[]{:S(2)}, u32[]{:S(2)}) collective-permute-start(bf16[64,384]{1,0:T(8,128)(2,1)S(1)} %get-tuple-element.202), channel_id=1, source_target_pairs={{0,8},{4,12},{8,16},{12,20},{16,24},{20,28},{24,0},{28,4},{1,9},{5... | collective-permute-start | bytes 147464 | tf_op jit(solution)/shard_map/ppermute | solution.py:592
  197.6 16.3 %collective-permute-start.33 = (bf16[64,384]{1,0:T(8,128)(2,1)S(1)}, bf16[64,384]{1,0:T(8,128)(2,1)}, u32[]{:S(2)}, u32[]{:S(2)}) collective-permute-start(bf16[64,384]{1,0:T(8,128)(2,1)S(1)} %get-tuple-element.201), channel_id=1, source_target_pairs={{0,16},{4,20},{8,24},{12,28},{16,0},{20,4},{24,8},{28,12},{1,17},{... | collective-permute-start | bytes 147464 | tf_op jit(solution)/shard_map/ppermute | solution.py:592
  201.2 12.8 %collective-permute-start.34 = (bf16[64,384]{1,0:T(8,128)(2,1)S(1)}, bf16[64,384]{1,0:T(8,128)(2,1)}, u32[]{:S(2)}, u32[]{:S(2)}) collective-permute-start(bf16[64,384]{1,0:T(8,128)(2,1)S(1)} %get-tuple-element.200), channel_id=1, source_target_pairs={{0,24},{4,28},{8,0},{12,4},{16,8},{20,12},{24,16},{28,20},{1,25},{... | collective-permute-start | bytes 147464 | tf_op jit(solution)/shard_map/ppermute | solution.py:592

commit v17 on v14

--- a/solution.py
+++ b/solution.py
@@ -748,7 +748,7 @@
         ctx, near_mine, near_other, last_mine, far_other = together(
             ctx, near_mine, near_other, last_mine, far_other
         )
-        last_other = swap(far_other, 1)
+        last_other = in_hbm(swap(far_other, 1))
         rest_parts = (
             (mine, other), (near_mine, near_other), (far_mine, far_other), (last_mine, last_other)
         )

time: 219 us -> 219 us (level)
  Pallas kernels: 75.9 us -> 84.1 us
  starting transfers between devices: 57.5 us -> 50.3 us
    ppermute x16, starting transfers between devices: 16.1 us -> 9.61 us  [swap(): return lax.ppermute(value, 'tensor', [(i, i ^ apart) for i in range(count)])]
    pallas_call x1, Pallas kernels: 22.8 us -> 28.4 us  [middle_block(): pl.pallas_call(functools.partial(middle_kernel, groups), grid_spec=pltpu....]
  transfers between devices with their start and end apart: 38 -> 38, of which waited for: 12 -> 12; matrix products, arithmetic and copies ran while one was open for 8% -> 8% of each run, Pallas kernels for 24% -> 25%
where the time goes in v17:
time: 219 us
  Pallas kernels  84.1 us (38%)
  waiting for transfers between devices  54.5 us (25%)
  starting transfers between devices  50.3 us (23%)
  other arithmetic  13.5 us (6%)
  local copies, waits for them, and re-layouts  12.9 us (6%)
  between operations  3.78 us (2%)
    ppermute x20, waiting for transfers between devices, along_dp(): return lax.ppermute(value, 'dp', [(i, move(i)) for i in range(count)])  45.6 us
    ppermute x20, starting transfers between devices, along_dp(): return lax.ppermute(value, 'dp', [(i, move(i)) for i in range(count)])  33.5 us
    pallas_call x2, Pallas kernels, attend_back(): pl.pallas_call(attend_back_kernel, grid_spec=pltpu.PrefetchScalarGridSpec...  29.1 us
    pallas_call x1, Pallas kernels, middle_block(): pl.pallas_call(functools.partial(middle_kernel, groups), grid_spec=pltpu....  28.4 us
    pallas_call x1, Pallas kernels, attend(): pl.pallas_call(attend_kernel, grid_spec=pltpu.PrefetchScalarGridSpec(num_...  15.3 us
    ppermute x16, starting transfers between devices, swap(): return lax.ppermute(value, 'tensor', [(i, i ^ apart) for i in range(count)])  9.61 us
    ppermute x16, waiting for transfers between devices, swap(): return lax.ppermute(value, 'tensor', [(i, i ^ apart) for i in range(count)])  8.96 us
    pallas_call x1, Pallas kernels, project(): pl.pallas_call(functools.partial(project_kernel, groups), grid_spec=pltpu...  6.26 us
  transfers between devices with their start and end apart: 38, of which 12 were waited for; matrix products, arithmetic and copies ran while one was open for 8% of the time, Pallas kernels for 25%

profile of v17, /device:TPU:0, one launch (start us, length us, event | category | flops | bytes accessed | tf_op | source)
XLA Modules:
  0.0 219.1 jit_solution(16053838413229667255)
XLA Ops:
  0.6 1.0 pad_maximum_fusion.2
  1.6 3.1 %collective-permute-start.6 = (bf16[64,1152]{1,0:T(8,128)(2,1)S(1)}, bf16[64,1152]{1,0:T(8,128)(2,1)S(1)}, u32[]{:S(2)}, u32[]{:S(2)}) collective-permute-start(bf16[64,1152]{1,0:T(8,128)(2,1)S(1)} %pad_maximum_fusion.2), channel_id=1, source_target_pairs={{0,8},{4,12},{8,16},{12,20},{16,24},{20,28},{24,0},{28,4},{1,9},{5... | collective-permute-start | bytes 442376 | tf_op jit(solution)/shard_map/ppermute | solution.py:592
  4.7 2.6 %collective-permute-start.7 = (bf16[64,1152]{1,0:T(8,128)(2,1)S(1)}, bf16[64,1152]{1,0:T(8,128)(2,1)S(1)}, u32[]{:S(2)}, u32[]{:S(2)}) collective-permute-start(bf16[64,1152]{1,0:T(8,128)(2,1)S(1)} %pad_maximum_fusion.2), channel_id=1, source_target_pairs={{0,16},{4,20},{8,24},{12,28},{16,0},{20,4},{24,8},{28,12},{1,17},{... | collective-permute-start | bytes 442376 | tf_op jit(solution)/shard_map/ppermute | solution.py:592
  7.3 1.3 collective-permute-start.8
  8.6 0.8 copy_bitcast_fusion.1
  9.4 1.5 collective-permute-start
  11.0 0.7 fusion.9
  11.8 0.7 compare_select_fusion.1
  12.5 0.7 gather_fusion
  13.2 1.1 pad_maximum_fusion
  14.4 2.8 %all-to-all-start = ((bf16[32,136,128]{2,1,0:T(8,128)(2,1)}), bf16[32,136,128]{2,1,0:T(8,128)(2,1)S(1)}, u32[]{:S(2)}, u32[]{:S(2)}) async-start(bf16[32,136,128]{2,1,0:T(8,128)(2,1)} %pad_maximum_fusion), calls=%async_computation | async-start | bytes 2228224 | tf_op jit(solution)/shard_map/all_to_all | solution.py:734
  17.3 1.7 collective-permute-start.1
  19.0 2.5 %collective-permute-start.2 = (bf16[64,768]{1,0:T(8,128)(2,1)S(1)}, bf16[64,768]{1,0:T(8,128)(2,1)S(1)}, u32[]{:S(2)}, u32[]{:S(2)}) collective-permute-start(bf16[64,768]{1,0:T(8,128)(2,1)S(1)} %constant_dynamic-update-slice_fusion), channel_id=1, source_target_pairs={{0,16},{4,20},{8,24},{12,28},{16,0},{20,4},{24,8},{28,12},{1,17},{... | collective-permute-start | bytes 294920 | tf_op jit(solution)/shard_map/ppermute | solution.py:592
  21.5 1.4 collective-permute-start.3
  23.0 0.9 pad_maximum_fusion.1.refs_0_
  23.8 1.5 collective-permute-start.10
  25.3 1.5 collective-permute-start.9
  26.8 15.6 %collective-permute-done.1 = bf16[64,768]{1,0:T(8,128)(2,1)S(1)} collective-permute-done((bf16[64,768]{1,0:T(8,128)(2,1)S(1)}, bf16[64,768]{1,0:T(8,128)(2,1)S(1)}, u32[]{:S(2)}, u32[]{:S(2)}) %collective-permute-start.1) | collective-permute-done | bytes 98336 | tf_op jit(solution)/shard_map/ppermute | solution.py:592
  42.4 9.2 %collective-permute-done.2 = bf16[64,768]{1,0:T(8,128)(2,1)S(1)} collective-permute-done((bf16[64,768]{1,0:T(8,128)(2,1)S(1)}, bf16[64,768]{1,0:T(8,128)(2,1)S(1)}, u32[]{:S(2)}, u32[]{:S(2)}) %collective-permute-start.2) | collective-permute-done | bytes 98336 | tf_op jit(solution)/shard_map/ppermute | solution.py:592
  51.7 1.6 collective-permute-start.5
  58.4 3.6 %collective-permute-done.5.refs_2_ = bf16[512,384]{1,0:T(8,128)(2,1)S(1)} collective-permute-done((bf16[512,384]{1,0:T(8,128)(2,1)S(1)}, bf16[512,384]{1,0:T(8,128)(2,1)S(1)}, u32[]{:S(2)}, u32[]{:S(2)}) %collective-permute-start.5) | collective-permute-done | bytes 393248 | tf_op jit(solution)/shard_map/ppermute | solution.py:587
  62.0 1.6 collective-permute-start.15
  64.5 1.0 collective-permute-done.11.refs_3_
  65.4 6.3 %project.1 = (bf16[1024,1536]{1,0:T(8,128)(2,1)S(1)}, bf16[512,1024]{1,0:T(8,128)(2,1)}, bf16[512,1536]{1,0:T(8,128)(2,1)}) custom-call(s32[1]{0:T(128)} %dynamic-slice.9.limit_ref, s32[8]{0:T(128)S(1)} %pad_add_fusion.place_ref, bf16[8,4,136,128]{3,2,1,0:T(8,128)(2,1)S(1)} %bitcast.109, f32[1,512]{1,0:T(1,128)S(1)} %pad_maximum_fusion.3.clock_ref, ...), custom_call_target="tpu_custom_call" | custom-call | flops 5750000128 | bytes 1048576 | tf_op jit(solution)/shard_map/project/pallas_call | solution.py:111
  71.7 15.3 %attend.1 = (bf16[1024,512]{1,0:T(8,128)(2,1)}, bf16[512,1024]{1,0:T(8,128)(2,1)}, f32[4,2,1024]{2,1,0:T(2,128)S(1)}) custom-call(s32[1]{0:T(128)} %dynamic-slice.9.limit_ref, bf16[1024,1536]{1,0:T(8,128)(2,1)S(1)} %get-tuple-element.68.q_ref.k_ref.v_ref, bf16[1024,1536]{1,0:T(8,128)(2,1)S(1)} %get-tuple-element.68.q_ref.k_ref.v_ref, ...), custom_call_target="tpu_custom_call" | custom-call | flops 17250000896 | bytes 1048576 | tf_op jit(solution)/shard_map/attend/pallas_call | solution.py:200
  87.2 0.7 copy-done.16
  88.1 1.3 collective-permute-done.16.refs_7_
  89.4 0.8 copy-done.17
  90.2 28.4 %middle.1 = (bf16[1,1024,512]{2,1,0:T(8,128)(2,1)}, bf16[1024,512]{1,0:T(8,128)(2,1)}, f32[1024,512]{1,0:T(8,128)}, f32[1,512]{1,0:T(1,128)S(1)}, bf16[2,512,640...) custom-call(s32[1]{0:T(128)} %dynamic-slice.9.limit_ref, ...), custom_call_target="tpu_custom_call" | custom-call | flops 28750000128 | bytes 1048576 | tf_op jit(solution)/shard_map/middle/pallas_call | solution.py:370
  119.1 3.1 %collective-permute-done.18 = bf16[2,512,512]{2,1,0:T(8,128)(2,1)S(1)} collective-permute-done((bf16[2,512,512]{2,1,0:T(8,128)(2,1)}, bf16[2,512,512]{2,1,0:T(8,128)(2,1)S(1)}, u32[]{:S(2)}, u32[]{:S(2)}) %collective-permute-start.18) | collective-permute-done | bytes 1048608 | tf_op jit(solution)/shard_map/ppermute | solution.py:587
  122.2 1.6 convert_add_fusion
  123.9 0.8 collective-permute-start.19
  124.7 1.4 fusion.1
  126.2 0.9 collective-permute-start.20
  127.1 14.9 %attend_back.2 = (bf16[1024,768]{1,0:T(8,128)(2,1)S(1)}, bf16[512,384]{1,0:T(8,128)(2,1)S(1)}, bf16[512,384]{1,0:T(8,128)(2,1)S(1)}) custom-call(s32[1]{0:T(128)} %dynamic-slice.9.limit_ref, bf16[1024,1536]{1,0:T(8,128)(2,1)S(1)} %copy-done.2, bf16[1024,1536]{1,0:T(8,128)(2,1)S(1)} %copy-done.2, bf16[1024,1536]{1,0:T(8,128)(2,1)S(1)} %copy-done.2, ...), custom_call_target="tpu_custom_call" | custom-call | flops 18400000000 | bytes 1048576 | tf_op jit(solution)/shard_map/attend_back/pallas_call | solution.py:466
  142.0 0.7 collective-permute-done.20
  142.7 1.3 fusion
  144.1 1.3 collective-permute-start.22
  145.6 2.5 %collective-permute-start.24 = (bf16[2,64,512]{2,1,0:T(8,128)(2,1)S(1)}, bf16[2,64,512]{2,1,0:T(8,128)(2,1)S(1)}, u32[]{:S(2)}, u32[]{:S(2)}) collective-permute-start(bf16[2,64,512]{2,1,0:T(8,128)(2,1)S(1)} %get-tuple-element.190), channel_id=1, source_target_pairs={{0,8},{4,12},{8,16},{12,20},{16,24},{20,28},{24,0},{28,4},{1,9},{5... | collective-permute-start | bytes 393224 | tf_op jit(solution)/shard_map/ppermute | solution.py:592
  148.1 2.0 collective-permute-start.25
  150.7 1.1 collective-permute-start.23
  151.7 14.2 %attend_back.3 = (bf16[1024,768]{1,0:T(8,128)(2,1)S(1)}, bf16[512,384]{1,0:T(8,128)(2,1)S(1)}, bf16[512,384]{1,0:T(8,128)(2,1)S(1)}) custom-call(s32[1]{0:T(128)} %dynamic-slice.9.limit_ref, bf16[1024,1536]{1,0:T(8,128)(2,1)S(1)} %copy-done.2, bf16[1024,1536]{1,0:T(8,128)(2,1)S(1)} %copy-done.2, bf16[1024,1536]{1,0:T(8,128)(2,1)S(1)} %copy-done.2, ...), custom_call_target="tpu_custom_call" | custom-call | flops 18400000000 | bytes 1048576 | tf_op jit(solution)/shard_map/attend_back/pallas_call | solution.py:466
  166.8 0.7 dynamic-slice_bitcast_fusion.4
  167.5 0.8 collective-permute-start.28
  168.3 5.0 %begin_back.1 = bf16[8,4,136,128]{3,2,1,0:T(8,128)(2,1)} custom-call(s32[1]{0:T(128)} %dynamic-slice.9.limit_ref, bf16[8,4,136,128]{3,2,1,0:T(8,128)(2,1)S(1)} %bitcast.111, f32[1,512]{1,0:T(1,128)S(1)} %pad_maximum_fusion.3.clock_ref, f32[1,512]{1,0:T(1,128)S(1)} %reshape_squeeze.8.gain_ref, f32[1,512]{1,0:T(1,128)S(1)} %get-tuple-element.78.gg_two_ref, ...), custom_call_target="tpu_custom_call" | custom-call | flops 8049999872 | bytes 1048576 | tf_op jit(solution)/shard_map/begin_back/pallas_call | solution.py:554
  174.5 0.7 copy-done.9
  175.3 4.4 %all-to-all-start.1 = ((bf16[32,136,128]{2,1,0:T(8,128)(2,1)}), bf16[32,136,128]{2,1,0:T(8,128)(2,1)S(1)}, u32[]{:S(2)}, u32[]{:S(2)}) async-start(bf16[32,136,128]{2,1,0:T(8,128)(2,1)} %bitcast.25), calls=%async_computation.1 | async-start | bytes 2228224 | tf_op jit(solution)/shard_map/all_to_all | solution.py:800
  179.7 0.7 scatter_custom_fusion
  180.4 1.7 fusion.4
  182.1 1.8 collective-permute-start.31
  184.2 1.8 collective-permute-start.29
  186.0 2.1 collective-permute-start.30
  188.0 7.2 %collective-permute-done.31 = bf16[4,64,384]{2,1,0:T(8,128)(2,1)S(1)} collective-permute-done((bf16[4,64,384]{2,1,0:T(8,128)(2,1)}, bf16[4,64,384]{2,1,0:T(8,128)(2,1)S(1)}, u32[]{:S(2)}, u32[]{:S(2)}) %collective-permute-start.31) | collective-permute-done | bytes 196640 | tf_op jit(solution)/shard_map/ppermute | solution.py:592
  195.2 1.0 fusion.3
  196.3 1.2 collective-permute-start.32
  197.5 3.6 %collective-permute-start.33 = (bf16[64,384]{1,0:T(8,128)(2,1)S(1)}, bf16[64,384]{1,0:T(8,128)(2,1)S(1)}, u32[]{:S(2)}, u32[]{:S(2)}) collective-permute-start(bf16[64,384]{1,0:T(8,128)(2,1)S(1)} %get-tuple-element.197), channel_id=1, source_target_pairs={{0,16},{4,20},{8,24},{12,28},{16,0},{20,4},{24,8},{28,12},{1,17},{... | collective-permute-start | bytes 147464 | tf_op jit(solution)/shard_map/ppermute | solution.py:592
  201.6 0.7 add_bitcast_fusion
  202.3 2.3 %collective-permute-done.29 = bf16[64,640]{1,0:T(8,128)(2,1)S(1)} collective-permute-done((bf16[64,640]{1,0:T(8,128)(2,1)}, bf16[64,640]{1,0:T(8,128)(2,1)S(1)}, u32[]{:S(2)}, u32[]{:S(2)}) %collective-permute-start.29) | collective-permute-done | bytes 81952 | tf_op jit(solution)/shard_map/ppermute | solution.py:592
  204.6 2.9 %collective-permute-done.32 = bf16[64,384]{1,0:T(8,128)(2,1)S(1)} collective-permute-done((bf16[64,384]{1,0:T(8,128)(2,1)S(1)}, bf16[64,384]{1,0:T(8,128)(2,1)S(1)}, u32[]{:S(2)}, u32[]{:S(2)}) %collective-permute-start.32) | collective-permute-done | bytes 49184 | tf_op jit(solution)/shard_map/ppermute | solution.py:592
  207.5 7.1 %collective-permute-done.33 = bf16[64,384]{1,0:T(8,128)(2,1)S(1)} collective-permute-done((bf16[64,384]{1,0:T(8,128)(2,1)S(1)}, bf16[64,384]{1,0:T(8,128)(2,1)S(1)}, u32[]{:S(2)}, u32[]{:S(2)}) %collective-permute-start.33) | collective-permute-done | bytes 49184 | tf_op jit(solution)/shard_map/ppermute | solution.py:592
  214.6 0.7 slice.119
  215.9 0.7 copy_bitcast_fusion
  216.6 0.8 gather_fusion.1
  217.3 1.1 slice.117
  (125 shorter events, 9.4 us)
Async XLA Ops:
  0.6 11.8 %copy-start = (bf16[32,128,128]{2,1,0:T(8,128)(2,1)S(1)}, bf16[32,128,128]{2,1,0:T(8,128)(2,1)}, u32[]{:S(2)}) copy-start(bf16[32,128,128]{2,1,0:T(8,128)(2,1)} %param.11) | copy-start | bytes 3145732
  1.6 19.9 %collective-permute-start.6 = (bf16[64,1152]{1,0:T(8,128)(2,1)S(1)}, bf16[64,1152]{1,0:T(8,128)(2,1)S(1)}, u32[]{:S(2)}, u32[]{:S(2)}) collective-permute-start(bf16[64,1152]{1,0:T(8,128)(2,1)S(1)} %pad_maximum_fusion.2), channel_id=1, source_target_pairs={{0,8},{4,12},{8,16},{12,20},{16,24},{20,28},{24,0},{28,4},{1,9},{5... | collective-permute-start | bytes 442376 | tf_op jit(solution)/shard_map/ppermute | solution.py:592
  4.7 18.2 %collective-permute-start.7 = (bf16[64,1152]{1,0:T(8,128)(2,1)S(1)}, bf16[64,1152]{1,0:T(8,128)(2,1)S(1)}, u32[]{:S(2)}, u32[]{:S(2)}) collective-permute-start(bf16[64,1152]{1,0:T(8,128)(2,1)S(1)} %pad_maximum_fusion.2), channel_id=1, source_target_pairs={{0,16},{4,20},{8,24},{12,28},{16,0},{20,4},{24,8},{28,12},{1,17},{... | collective-permute-start | bytes 442376 | tf_op jit(solution)/shard_map/ppermute | solution.py:592
  7.3 15.7 %collective-permute-start.8 = (bf16[64,1152]{1,0:T(8,128)(2,1)S(1)}, bf16[64,1152]{1,0:T(8,128)(2,1)S(1)}, u32[]{:S(2)}, u32[]{:S(2)}) collective-permute-start(bf16[64,1152]{1,0:T(8,128)(2,1)S(1)} %pad_maximum_fusion.2), channel_id=1, source_target_pairs={{0,24},{4,28},{8,0},{12,4},{16,8},{20,12},{24,16},{28,20},{1,25},{... | collective-permute-start | bytes 442376 | tf_op jit(solution)/shard_map/ppermute | solution.py:592
  9.4 7.8 %collective-permute-start = (bf16[64,384]{1,0:T(8,128)(2,1)S(1)}, bf16[64,384]{1,0:T(8,128)(2,1)S(1)}, u32[]{:S(2)}, u32[]{:S(2)}) collective-permute-start(bf16[64,384]{1,0:T(8,128)(2,1)S(1)} %copy_bitcast_fusion.1), channel_id=1, source_target_pairs={{0,4},{4,0},{8,12},{12,8},{16,20},{20,16},{24,28},{28,24},{1,5},{5... | collective-permute-start | bytes 147464 | tf_op jit(solution)/shard_map/ppermute | solution.py:592
  14.4 2.8 %copy-start.12 = (bf16[64,3,128]{2,0,1:T(8,128)(2,1)S(1)}, bf16[64,3,128]{2,0,1:T(8,128)(2,1)}, u32[]{:S(2)}) copy-start(bf16[64,3,128]{2,0,1:T(8,128)(2,1)} %param.15) | copy-start | bytes 147460
  14.4 8.6 %copy-start.10 = (bf16[512,64]{0,1:T(8,128)(2,1)S(1)}, bf16[512,64]{0,1:T(8,128)(2,1)}, u32[]{:S(2)}) copy-start(bf16[512,64]{0,1:T(8,128)(2,1)} %param.18) | copy-start | bytes 196612
  14.4 8.6 %copy-start.11 = (bf16[64,512]{1,0:T(8,128)(2,1)S(1)}, bf16[64,512]{1,0:T(8,128)(2,1)}, u32[]{:S(2)}) copy-start(bf16[64,512]{1,0:T(8,128)(2,1)} %param.17) | copy-start | bytes 196612
  14.4 8.6 %copy-start.15 = (bf16[128,64]{0,1:T(8,128)(2,1)S(1)}, bf16[128,64]{0,1:T(8,128)(2,1)}, u32[]{:S(2)}) copy-start(bf16[128,64]{0,1:T(8,128)(2,1)} %param.16) | copy-start | bytes 49156
  14.4 49.4 %all-to-all-start = ((bf16[32,136,128]{2,1,0:T(8,128)(2,1)}), bf16[32,136,128]{2,1,0:T(8,128)(2,1)S(1)}, u32[]{:S(2)}, u32[]{:S(2)}) async-start(bf16[32,136,128]{2,1,0:T(8,128)(2,1)} %pad_maximum_fusion), calls=%async_computation | async-start | bytes 2228224 | tf_op jit(solution)/shard_map/all_to_all | solution.py:734
  17.2 36.7 %copy-start.18 = (s32[32]{0:T(128)S(1)}, s32[32]{0:T(128)}, u32[]{:S(2)}) copy-start(s32[32]{0:T(128)} %param.14) | copy-start | bytes 388
  17.2 39.2 %copy-start.19 = (s32[32]{0:T(128)S(1)}, s32[32]{0:T(128)}, u32[]{:S(2)}) copy-start(s32[32]{0:T(128)} %param.12) | copy-start | bytes 388
  17.2 40.5 %copy-start.20 = (s32[32]{0:T(128)S(1)}, s32[32]{0:T(128)}, u32[]{:S(2)}) copy-start(s32[32]{0:T(128)} %param.13) | copy-start | bytes 388
  17.3 25.1 %collective-permute-start.1 = (bf16[64,768]{1,0:T(8,128)(2,1)S(1)}, bf16[64,768]{1,0:T(8,128)(2,1)S(1)}, u32[]{:S(2)}, u32[]{:S(2)}) collective-permute-start(bf16[64,768]{1,0:T(8,128)(2,1)S(1)} %constant_dynamic-update-slice_fusion), channel_id=1, source_target_pairs={{0,8},{4,12},{8,16},{12,20},{16,24},{20,28},{24,0},{28,4},{1,9},{5... | collective-permute-start | bytes 294920 | tf_op jit(solution)/shard_map/ppermute | solution.py:592
  19.0 32.6 %collective-permute-start.2 = (bf16[64,768]{1,0:T(8,128)(2,1)S(1)}, bf16[64,768]{1,0:T(8,128)(2,1)S(1)}, u32[]{:S(2)}, u32[]{:S(2)}) collective-permute-start(bf16[64,768]{1,0:T(8,128)(2,1)S(1)} %constant_dynamic-update-slice_fusion), channel_id=1, source_target_pairs={{0,16},{4,20},{8,24},{12,28},{16,0},{20,4},{24,8},{28,12},{1,17},{... | collective-permute-start | bytes 294920 | tf_op jit(solution)/shard_map/ppermute | solution.py:592
  21.5 30.1 %collective-permute-start.3 = (bf16[64,768]{1,0:T(8,128)(2,1)S(1)}, bf16[64,768]{1,0:T(8,128)(2,1)S(1)}, u32[]{:S(2)}, u32[]{:S(2)}) collective-permute-start(bf16[64,768]{1,0:T(8,128)(2,1)S(1)} %constant_dynamic-update-slice_fusion), channel_id=1, source_target_pairs={{0,24},{4,28},{8,0},{12,4},{16,8},{20,12},{24,16},{28,20},{1,25},{... | collective-permute-start | bytes 294920 | tf_op jit(solution)/shard_map/ppermute | solution.py:592
  23.8 38.1 %collective-permute-start.10 = (bf16[256,1152]{1,0:T(8,128)(2,1)}, bf16[256,1152]{1,0:T(8,128)(2,1)}, u32[]{:S(2)}, u32[]{:S(2)}) collective-permute-start(bf16[256,1152]{1,0:T(8,128)(2,1)} %pad_maximum_fusion.1.refs_0_), channel_id=1, source_target_pairs={{0,2},{1,3},{2,0},{3,1},{4,6},{5,7},{6,4},{7,5},{8,10},{9,11},{10,... | collective-permute-start | bytes 1769480 | tf_op jit(solution)/shard_map/ppermute | solution.py:587
  25.3 36.6 %collective-permute-start.9 = (bf16[256,1152]{1,0:T(8,128)(2,1)}, bf16[256,1152]{1,0:T(8,128)(2,1)}, u32[]{:S(2)}, u32[]{:S(2)}) collective-permute-start(bf16[256,1152]{1,0:T(8,128)(2,1)} %pad_maximum_fusion.1.refs_0_), channel_id=1, source_target_pairs={{0,4},{4,0},{8,12},{12,8},{16,20},{20,16},{24,28},{28,24},{1,5},{5... | collective-permute-start | bytes 1769480 | tf_op jit(solution)/shard_map/ppermute | solution.py:592
  51.7 10.3 %collective-permute-start.5 = (bf16[512,384]{1,0:T(8,128)(2,1)S(1)}, bf16[512,384]{1,0:T(8,128)(2,1)S(1)}, u32[]{:S(2)}, u32[]{:S(2)}) collective-permute-start(bf16[512,384]{1,0:T(8,128)(2,1)S(1)} %slice_dynamic-update-slice_fusion.refs_0_), channel_id=1, source_target_pairs={{0,2},{1,3},{2,0},{3,1},{4,6},{5,7},{6,4},{7,5},{8,10},{9,11},{10,... | collective-permute-start | bytes 1179656 | tf_op jit(solution)/shard_map/ppermute | solution.py:587
  53.4 10.6 %collective-permute-start.4 = (bf16[512,384]{1,0:T(8,128)(2,1)S(1)}, bf16[512,384]{1,0:T(8,128)(2,1)S(1)}, u32[]{:S(2)}, u32[]{:S(2)}) collective-permute-start(bf16[512,384]{1,0:T(8,128)(2,1)S(1)} %slice_dynamic-update-slice_fusion.refs_0_), channel_id=1, source_target_pairs={{0,1},{1,0},{2,3},{3,2},{4,5},{5,4},{6,7},{7,6},{8,9},{9,8},{10,11... | collective-permute-start | bytes 1179656 | tf_op jit(solution)/shard_map/ppermute | solution.py:587
  53.4 33.6 %collective-permute-start.12 = (bf16[256,1152]{1,0:T(8,128)(2,1)}, bf16[256,1152]{1,0:T(8,128)(2,1)}, u32[]{:S(2)}, u32[]{:S(2)}) collective-permute-start(bf16[256,1152]{1,0:T(8,128)(2,1)} %pad_maximum_fusion.1.refs_0_), channel_id=1, source_target_pairs={{0,1},{1,0},{2,3},{3,2},{4,5},{5,4},{6,7},{7,6},{8,9},{9,8},{10,11... | collective-permute-start | bytes 1769480 | tf_op jit(solution)/shard_map/ppermute | solution.py:587
  62.0 25.1 %collective-permute-start.13 = (bf16[256,1152]{1,0:T(8,128)(2,1)}, bf16[256,1152]{1,0:T(8,128)(2,1)}, u32[]{:S(2)}, u32[]{:S(2)}) collective-permute-start(bf16[256,1152]{1,0:T(8,128)(2,1)} %collective-permute-done.9.refs_1_), channel_id=1, source_target_pairs={{0,1},{1,0},{2,3},{3,2},{4,5},{5,4},{6,7},{7,6},{8,9},{9,8},{10,11... | collective-permute-start | bytes 1769480 | tf_op jit(solution)/shard_map/ppermute | solution.py:587
  62.0 25.1 %collective-permute-start.15 = (bf16[256,1152]{1,0:T(8,128)(2,1)}, bf16[256,1152]{1,0:T(8,128)(2,1)}, u32[]{:S(2)}, u32[]{:S(2)}) collective-permute-start(bf16[256,1152]{1,0:T(8,128)(2,1)} %collective-permute-done.9.refs_1_), channel_id=1, source_target_pairs={{0,2},{1,3},{2,0},{3,1},{4,6},{5,7},{6,4},{7,5},{8,10},{9,11},{10,... | collective-permute-start | bytes 1769480 | tf_op jit(solution)/shard_map/ppermute | solution.py:587
  63.6 1.9 collective-permute-start.11
  64.0 23.0 %collective-permute-start.14 = (bf16[256,1152]{1,0:T(8,128)(2,1)}, bf16[256,1152]{1,0:T(8,128)(2,1)S(1)}, u32[]{:S(2)}, u32[]{:S(2)}) collective-permute-start(bf16[256,1152]{1,0:T(8,128)(2,1)} %collective-permute-done.10.refs_4_), channel_id=1, source_target_pairs={{0,1},{1,0},{2,3},{3,2},{4,5},{5,4},{6,7},{7,6},{8,9},{9,8},{10,11... | collective-permute-start | bytes 1769480 | tf_op jit(solution)/shard_map/ppermute | solution.py:587
  71.7 15.4 %copy-start.1 = (bf16[1024,1536]{1,0:T(8,128)(2,1)}, bf16[1024,1536]{1,0:T(8,128)(2,1)S(1)}, u32[]{:S(2)}) copy-start(bf16[1024,1536]{1,0:T(8,128)(2,1)S(1)} %get-tuple-element.68.q_ref.k_ref.v_ref) | copy-start | bytes 9437188
  87.1 0.8 copy-start.16
  87.1 2.3 %collective-permute-start.16 = (bf16[256,1152]{1,0:T(8,128)(2,1)}, bf16[256,1152]{1,0:T(8,128)(2,1)S(1)}, u32[]{:S(2)}, u32[]{:S(2)}) collective-permute-start(bf16[256,1152]{1,0:T(8,128)(2,1)} %collective-permute-done.15.refs_5_), channel_id=1, source_target_pairs={{0,1},{1,0},{2,3},{3,2},{4,5},{5,4},{6,7},{7,6},{8,9},{9,8},{10,11... | collective-permute-start | bytes 1769480 | tf_op jit(solution)/shard_map/ppermute | solution.py:587
  89.4 0.8 copy-start.17
  118.6 3.7 %collective-permute-start.18 = (bf16[2,512,512]{2,1,0:T(8,128)(2,1)}, bf16[2,512,512]{2,1,0:T(8,128)(2,1)S(1)}, u32[]{:S(2)}, u32[]{:S(2)}) collective-permute-start(bf16[2,512,512]{2,1,0:T(8,128)(2,1)} %get-tuple-element.86), channel_id=1, source_target_pairs={{0,1},{1,0},{2,3},{3,2},{4,5},{5,4},{6,7},{7,6},{8,9},{9,8},{10,11... | collective-permute-start | bytes 3145736 | tf_op jit(solution)/shard_map/ppermute | solution.py:587
  118.6 6.1 %collective-permute-start.17 = (bf16[2,512,640]{2,1,0:T(8,128)(2,1)}, bf16[2,512,640]{2,1,0:T(8,128)(2,1)}, u32[]{:S(2)}, u32[]{:S(2)}) collective-permute-start(bf16[2,512,640]{2,1,0:T(8,128)(2,1)} %get-tuple-element.81), channel_id=1, source_target_pairs={{0,1},{1,0},{2,3},{3,2},{4,5},{5,4},{6,7},{7,6},{8,9},{9,8},{10,11... | collective-permute-start | bytes 3932168 | tf_op jit(solution)/shard_map/ppermute | solution.py:587
  122.2 4.8 %copy-start.2 = (bf16[1024,1536]{1,0:T(8,128)(2,1)S(1)}, bf16[1024,1536]{1,0:T(8,128)(2,1)}, u32[]{:S(2)}) copy-start(bf16[1024,1536]{1,0:T(8,128)(2,1)} %copy-done.1) | copy-start | bytes 9437188
  122.2 4.8 %copy-start.6 = (bf16[512,1024]{1,0:T(8,128)(2,1)S(1)}, bf16[512,1024]{1,0:T(8,128)(2,1)}, u32[]{:S(2)}) copy-start(bf16[512,1024]{1,0:T(8,128)(2,1)} %get-tuple-element.82.turn_ref) | copy-start | bytes 3145732
  123.8 3.2 %copy-start.5 = (bf16[512,1024]{1,0:T(8,128)(2,1)S(1)}, bf16[512,1024]{1,0:T(8,128)(2,1)}, u32[]{:S(2)}) copy-start(bf16[512,1024]{1,0:T(8,128)(2,1)} %get-tuple-element.88.n_turn_ref) | copy-start | bytes 3145732
  123.9 18.1 %collective-permute-start.19 = (bf16[4,2,64,512]{3,2,1,0:T(8,128)(2,1)S(1)}, bf16[4,2,64,512]{3,2,1,0:T(8,128)(2,1)S(1)}, u32[]{:S(2)}, u32[]{:S(2)}) collective-permute-start(bf16[4,2,64,512]{3,2,1,0:T(8,128)(2,1)S(1)} %bitcast.117), channel_id=1, source_target_pairs={{0,2},{1,3},{2,0},{3,1},{4,6},{5,7},{6,4},{7,5},{8,10},{9,11},{10,... | collective-permute-start | bytes 1572872 | tf_op jit(solution)/shard_map/ppermute | solution.py:587
  126.2 16.6 %collective-permute-start.20 = (bf16[2,4,64,640]{3,2,1,0:T(8,128)(2,1)S(1)}, bf16[2,4,64,640]{3,2,1,0:T(8,128)(2,1)S(1)}, u32[]{:S(2)}, u32[]{:S(2)}) collective-permute-start(bf16[2,4,64,640]{3,2,1,0:T(8,128)(2,1)S(1)} %fusion.1), channel_id=1, source_target_pairs={{0,4},{4,0},{8,12},{12,8},{16,20},{20,16},{24,28},{28,24},{1,5},{5... | collective-permute-start | bytes 1966088 | tf_op jit(solution)/shard_map/ppermute | solution.py:592
  127.1 15.7 %copy-start.8 = (bf16[2,512,640]{2,1,0:T(8,128)(2,1)S(1)}, bf16[2,512,640]{2,1,0:T(8,128)(2,1)}, u32[]{:S(2)}) copy-start(bf16[2,512,640]{2,1,0:T(8,128)(2,1)} %get-tuple-element.80) | copy-start | bytes 3932164
  142.7 7.8 %collective-permute-start.21 = (bf16[512,384]{1,0:T(8,128)(2,1)S(1)}, bf16[512,384]{1,0:T(8,128)(2,1)S(1)}, u32[]{:S(2)}, u32[]{:S(2)}) collective-permute-start(bf16[512,384]{1,0:T(8,128)(2,1)S(1)} %get-tuple-element.97), channel_id=1, source_target_pairs={{0,1},{1,0},{2,3},{3,2},{4,5},{5,4},{6,7},{7,6},{8,9},{9,8},{10,11... | collective-permute-start | bytes 1179656 | tf_op jit(solution)/shard_map/ppermute | solution.py:587
  144.1 21.9 %collective-permute-start.22 = (bf16[4,64,640]{2,1,0:T(8,128)(2,1)S(1)}, bf16[4,64,640]{2,1,0:T(8,128)(2,1)S(1)}, u32[]{:S(2)}, u32[]{:S(2)}) collective-permute-start(bf16[4,64,640]{2,1,0:T(8,128)(2,1)S(1)} %slice_bitcast_fusion), channel_id=1, source_target_pairs={{0,2},{1,3},{2,0},{3,1},{4,6},{5,7},{6,4},{7,5},{8,10},{9,11},{10,... | collective-permute-start | bytes 983048 | tf_op jit(solution)/shard_map/ppermute | solution.py:587
  145.6 6.2 %copy-start.7 = (bf16[1024,512]{1,0:T(8,128)(2,1)S(1)}, bf16[1024,512]{1,0:T(8,128)(2,1)}, u32[]{:S(2)}) copy-start(bf16[1024,512]{1,0:T(8,128)(2,1)} %get-tuple-element.98.cg_ref) | copy-start | bytes 3145732
  145.6 20.3 %collective-permute-start.24 = (bf16[2,64,512]{2,1,0:T(8,128)(2,1)S(1)}, bf16[2,64,512]{2,1,0:T(8,128)(2,1)S(1)}, u32[]{:S(2)}, u32[]{:S(2)}) collective-permute-start(bf16[2,64,512]{2,1,0:T(8,128)(2,1)S(1)} %get-tuple-element.190), channel_id=1, source_target_pairs={{0,8},{4,12},{8,16},{12,20},{16,24},{20,28},{24,0},{28,4},{1,9},{5... | collective-permute-start | bytes 393224 | tf_op jit(solution)/shard_map/ppermute | solution.py:592
  148.1 17.9 %collective-permute-start.25 = (bf16[2,64,512]{2,1,0:T(8,128)(2,1)S(1)}, bf16[2,64,512]{2,1,0:T(8,128)(2,1)S(1)}, u32[]{:S(2)}, u32[]{:S(2)}) collective-permute-start(bf16[2,64,512]{2,1,0:T(8,128)(2,1)S(1)} %get-tuple-element.189), channel_id=1, source_target_pairs={{0,16},{4,20},{8,24},{12,28},{16,0},{20,4},{24,8},{28,12},{1,17},{... | collective-permute-start | bytes 393224 | tf_op jit(solution)/shard_map/ppermute | solution.py:592
  150.1 15.9 %collective-permute-start.26 = (bf16[2,64,512]{2,1,0:T(8,128)(2,1)S(1)}, bf16[2,64,512]{2,1,0:T(8,128)(2,1)S(1)}, u32[]{:S(2)}, u32[]{:S(2)}) collective-permute-start(bf16[2,64,512]{2,1,0:T(8,128)(2,1)S(1)} %get-tuple-element.188), channel_id=1, source_target_pairs={{0,24},{4,28},{8,0},{12,4},{16,8},{20,12},{24,16},{28,20},{1,25},{... | collective-permute-start | bytes 393224 | tf_op jit(solution)/shard_map/ppermute | solution.py:592
  150.7 15.3 %collective-permute-start.23 = (bf16[512,384]{1,0:T(8,128)(2,1)S(1)}, bf16[512,384]{1,0:T(8,128)(2,1)S(1)}, u32[]{:S(2)}, u32[]{:S(2)}) collective-permute-start(bf16[512,384]{1,0:T(8,128)(2,1)S(1)} %add_convert_fusion.3), channel_id=1, source_target_pairs={{0,2},{1,3},{2,0},{3,1},{4,6},{5,7},{6,4},{7,5},{8,10},{9,11},{10,... | collective-permute-start | bytes 1179656 | tf_op jit(solution)/shard_map/ppermute | solution.py:587
  151.7 16.6 %copy-start.4 = (bf16[512,1536]{1,0:T(8,128)(2,1)S(1)}, bf16[512,1536]{1,0:T(8,128)(2,1)}, u32[]{:S(2)}) copy-start(bf16[512,1536]{1,0:T(8,128)(2,1)} %get-tuple-element.108.w_ref) | copy-start | bytes 4718596
  166.0 2.3 %copy-start.3 = (f32[1024,512]{1,0:T(8,128)S(1)}, f32[1024,512]{1,0:T(8,128)}, u32[]{:S(2)}) copy-start(f32[1024,512]{1,0:T(8,128)} %get-tuple-element.107.mg_ref) | copy-start | bytes 6291460
  167.5 6.4 %collective-permute-start.28 = (bf16[64,640]{1,0:T(8,128)(2,1)S(1)}, bf16[64,640]{1,0:T(8,128)(2,1)S(1)}, u32[]{:S(2)}, u32[]{:S(2)}) collective-permute-start(bf16[64,640]{1,0:T(8,128)(2,1)S(1)} %get-tuple-element.195), channel_id=1, source_target_pairs={{0,16},{4,20},{8,24},{12,28},{16,0},{20,4},{24,8},{28,12},{1,17},{... | collective-permute-start | bytes 245768 | tf_op jit(solution)/shard_map/ppermute | solution.py:592
  168.3 5.6 %collective-permute-start.27 = (bf16[512,384]{1,0:T(8,128)(2,1)S(1)}, bf16[512,384]{1,0:T(8,128)(2,1)S(1)}, u32[]{:S(2)}, u32[]{:S(2)}) collective-permute-start(bf16[512,384]{1,0:T(8,128)(2,1)S(1)} %get-tuple-element.110), channel_id=1, source_target_pairs={{0,1},{1,0},{2,3},{3,2},{4,5},{5,4},{6,7},{7,6},{8,9},{9,8},{10,11... | collective-permute-start | bytes 1179656 | tf_op jit(solution)/shard_map/ppermute | solution.py:587
  173.9 0.6 copy-start.13
  174.5 0.7 copy-start.9
  175.3 41.3 %all-to-all-start.1 = ((bf16[32,136,128]{2,1,0:T(8,128)(2,1)}), bf16[32,136,128]{2,1,0:T(8,128)(2,1)S(1)}, u32[]{:S(2)}, u32[]{:S(2)}) async-start(bf16[32,136,128]{2,1,0:T(8,128)(2,1)} %bitcast.25), calls=%async_computation.1 | async-start | bytes 2228224 | tf_op jit(solution)/shard_map/all_to_all | solution.py:800
  182.1 13.1 %collective-permute-start.31 = (bf16[4,64,384]{2,1,0:T(8,128)(2,1)}, bf16[4,64,384]{2,1,0:T(8,128)(2,1)S(1)}, u32[]{:S(2)}, u32[]{:S(2)}) collective-permute-start(bf16[4,64,384]{2,1,0:T(8,128)(2,1)} %fusion.4), channel_id=1, source_target_pairs={{0,4},{4,0},{8,12},{12,8},{16,20},{20,16},{24,28},{28,24},{1,5},{5... | collective-permute-start | bytes 589832 | tf_op jit(solution)/shard_map/ppermute | solution.py:592
  183.9 30.7 %copy-start.14 = (bf16[64,640]{1,0:T(8,128)(2,1)S(1)}, bf16[64,640]{1,0:T(8,128)(2,1)}, u32[]{:S(2)}) copy-start(bf16[64,640]{1,0:T(8,128)(2,1)} %copy-done.13) | copy-start | bytes 245764
  183.9 17.2 %collective-permute-start.35 = (bf16[1,64,512]{2,1,0:T(8,128)(2,1)}, bf16[1,64,512]{2,1,0:T(8,128)(2,1)S(1)}, u32[]{:S(2)}, u32[]{:S(2)}) collective-permute-start(bf16[1,64,512]{2,1,0:T(8,128)(2,1)} %dynamic-slice_convert_fusion), channel_id=1, source_target_pairs={{0,4},{4,0},{8,12},{12,8},{16,20},{20,16},{24,28},{28,24},{1,5},{5... | collective-permute-start | bytes 196616 | tf_op jit(solution)/shard_map/ppermute | solution.py:592
  184.2 20.4 %collective-permute-start.29 = (bf16[64,640]{1,0:T(8,128)(2,1)}, bf16[64,640]{1,0:T(8,128)(2,1)S(1)}, u32[]{:S(2)}, u32[]{:S(2)}) collective-permute-start(bf16[64,640]{1,0:T(8,128)(2,1)} %get-tuple-element.193), channel_id=1, source_target_pairs={{0,8},{4,12},{8,16},{12,20},{16,24},{20,28},{24,0},{28,4},{1,9},{5... | collective-permute-start | bytes 245768 | tf_op jit(solution)/shard_map/ppermute | solution.py:592
  186.0 18.6 %collective-permute-start.30 = (bf16[64,640]{1,0:T(8,128)(2,1)}, bf16[64,640]{1,0:T(8,128)(2,1)S(1)}, u32[]{:S(2)}, u32[]{:S(2)}) collective-permute-start(bf16[64,640]{1,0:T(8,128)(2,1)} %get-tuple-element.192), channel_id=1, source_target_pairs={{0,24},{4,28},{8,0},{12,4},{16,8},{20,12},{24,16},{28,20},{1,25},{... | collective-permute-start | bytes 245768 | tf_op jit(solution)/shard_map/ppermute | solution.py:592
  196.3 11.2 %collective-permute-start.32 = (bf16[64,384]{1,0:T(8,128)(2,1)S(1)}, bf16[64,384]{1,0:T(8,128)(2,1)S(1)}, u32[]{:S(2)}, u32[]{:S(2)}) collective-permute-start(bf16[64,384]{1,0:T(8,128)(2,1)S(1)} %get-tuple-element.198), channel_id=1, source_target_pairs={{0,8},{4,12},{8,16},{12,20},{16,24},{20,28},{24,0},{28,4},{1,9},{5... | collective-permute-start | bytes 147464 | tf_op jit(solution)/shard_map/ppermute | solution.py:592
  197.5 17.0 %collective-permute-start.33 = (bf16[64,384]{1,0:T(8,128)(2,1)S(1)}, bf16[64,384]{1,0:T(8,128)(2,1)S(1)}, u32[]{:S(2)}, u32[]{:S(2)}) collective-permute-start(bf16[64,384]{1,0:T(8,128)(2,1)S(1)} %get-tuple-element.197), channel_id=1, source_target_pairs={{0,16},{4,20},{8,24},{12,28},{16,0},{20,4},{24,8},{28,12},{1,17},{... | collective-permute-start | bytes 147464 | tf_op jit(solution)/shard_map/ppermute | solution.py:592
  201.1 13.4 %collective-permute-start.34 = (bf16[64,384]{1,0:T(8,128)(2,1)S(1)}, bf16[64,384]{1,0:T(8,128)(2,1)S(1)}, u32[]{:S(2)}, u32[]{:S(2)}) collective-permute-start(bf16[64,384]{1,0:T(8,128)(2,1)S(1)} %get-tuple-element.196), channel_id=1, source_target_pairs={{0,24},{4,28},{8,0},{12,4},{16,8},{20,12},{24,16},{28,20},{1,25},{... | collective-permute-start | bytes 147464 | tf_op jit(solution)/shard_map/ppermute | solution.py:592
